TPU v7x, 128 devices: a whole 4x4x4 slice. The times are simulated.
128 devices in a mesh: dp: 32 (over z, y_hi, x), tensor: 4 (over y_lo, core).
Axes of the slice: x: 4, y: 4 (y_hi: 2, y_lo: 2; y = y_hi * 2 + y_lo), z: 4, core: 2. Of those that a mesh axis runs over, the one named last changes fastest.
Arguments:
- tokens: bfloat16 [32, 4, 128, 2048], P('dp', 'tensor'), may hold values from -6 to 6
- doc_ids: int32 [32, 4, 128], P('dp'), may hold values from 0 to 3, never falling along the last dimension, each value on 1 to 64 neighbouring positions
- attn_gain: float32 [2048], P(('dp', 'tensor')), may hold values from 0.5 to 1.5
- forget_floor: float32 [2048], P(('dp', 'tensor')), may hold values from 0.5 to 0.98
- w_query: bfloat16 [2048, 2048], P('dp', 'tensor'), may hold values from -0.125 to 0.125
- w_forget: bfloat16 [2048, 2048], P('dp', 'tensor'), may hold values from -0.125 to 0.125
- w_value: bfloat16 [2048, 2048], P('dp', 'tensor'), may hold values from -0.125 to 0.125
- w_outgate: bfloat16 [2048, 2048], P('dp', 'tensor'), may hold values from -0.125 to 0.125
- w_output: bfloat16 [2048, 2048], P('tensor', 'dp'), may hold values from -0.125 to 0.125
- mlp_gain: float32 [2048], P(('dp', 'tensor')), may hold values from 0.5 to 1.5
- w_gate: bfloat16 [2048, 5632], P('dp', 'tensor'), may hold values from -0.125 to 0.125
- w_up: bfloat16 [2048, 5632], P('dp', 'tensor'), may hold values from -0.125 to 0.125
- w_down: bfloat16 [5632, 2048], P('tensor', 'dp'), may hold values from -0.078125 to 0.078125
- cotangent: bfloat16 [32, 4, 128, 2048], P('dp', 'tensor'), may hold values from -6 to 6
Outputs:
- layer_out: bfloat16 [32, 4, 128, 2048], P('dp', 'tensor')
- grad_tokens: float32 [32, 4, 128, 2048], P('dp', 'tensor')
- grad_attn_gain: float32 [2048], P(('dp', 'tensor'))
- grad_floor: float32 [2048], P(('dp', 'tensor'))
- grad_query: float32 [2048, 2048], P('dp', 'tensor')
- grad_forget: float32 [2048, 2048], P('dp', 'tensor')
- grad_value: float32 [2048, 2048], P('dp', 'tensor')
- grad_outgate: float32 [2048, 2048], P('dp', 'tensor')
- grad_output: float32 [2048, 2048], P('tensor', 'dp')
- grad_mlp_gain: float32 [2048], P(('dp', 'tensor'))
- grad_gate: float32 [2048, 5632], P('dp', 'tensor')
- grad_up: float32 [2048, 5632], P('dp', 'tensor')
- grad_down: float32 [5632, 2048], P('tensor', 'dp')
Inputs may be any that keep to these rules, and one draw needn't show every extreme that they name: `doc_ids`: within each row of 128 tokens the sequence numbers never fall; each sequence has 1 to 64 tokens, and the longest has exactly 64.
All inputs are finite; a program needn't handle non-finite values.
Results may differ from a plain program's by a relative error of at most 0.025.
Values may be sent and summed in bfloat16 or wider, within the bound.
No kernel may reach another device: no remote copies, remote signals or barrier semaphores. Data moves between devices by JAX's collectives and lax.ppermute only.
A program may use at most 192 MiB of HBM per device.

v0:
```python
import jax
import jax.numpy as jnp
from jax import lax
from jax.sharding import PartitionSpec as P

HK = 128
BLOCK = 64


epsilon = 1e-06


def row_scale(values):
    return lax.rsqrt(jnp.mean(values * values, axis=-1, keepdims=True) + epsilon)


def silu_slope(values):
    sigmoid_val = jax.nn.sigmoid(values)
    return sigmoid_val * (1.0 + values * (1.0 - sigmoid_val))


def matmul_plain(left, right):
    return jnp.dot(left, right, preferred_element_type=jnp.float32)


def times_trans(left, right):
    return lax.dot_general(
        left, right, (((1,), (1,)), ((), ())), preferred_element_type=jnp.float32
    )


def trans_times(left, right):
    return lax.dot_general(
        left, right, (((0,), (0,)), ((), ())), preferred_element_type=jnp.float32
    )


def recurrence(query, forget_raw, value, floor_vec, doc_row):
    length, heads_n, chan = query.shape
    forget = floor_vec + (1.0 - floor_vec) * jax.nn.sigmoid(forget_raw)
    log_forget = jnp.log(forget)
    keyed = 1.0 - forget
    block_count = length // BLOCK

    def split_blocks(arr):
        return arr.reshape(block_count, BLOCK, heads_n, chan)

    doc_blocks = doc_row.reshape(block_count, BLOCK)
    before = jnp.concatenate([jnp.full((1,), -1, jnp.int32), doc_blocks[:-1, -1]])
    position = jnp.arange(BLOCK)
    causal = position[:, None] >= position[None, :]

    @jax.checkpoint
    def block_step(recurrent_state, pieces):
        query_block, log_b, key_b, value_block, doc_b, prev_doc = pieces
        running_total = jnp.cumsum(log_b, axis=0)
        same_doc = (causal & (doc_b[:, None] == doc_b[None, :]))[:, :, None, None]
        log_gap = running_total[:, None] - running_total[None, :]
        decay = jnp.where(same_doc, jnp.exp(jnp.where(same_doc, log_gap, 0.0)), 0.0)
        scores = jnp.einsum(
            "ihk,jhk,ijhk->ijh", query_block, key_b, decay, precision=lax.Precision.HIGHEST
        )
        intra = jnp.einsum("ijh,jhv->ihv", scores, value_block, precision=lax.Precision.HIGHEST)
        carried_over = (doc_b == prev_doc).astype(jnp.float32)[:, None, None]
        across_blocks = (
            jnp.einsum(
                "bma,maf->bmf",
                query_block * jnp.exp(running_total),
                recurrent_state,
                precision=lax.Precision.HIGHEST,
            )
            * carried_over
        )
        block_finish = running_total[-1]
        end_flag = (doc_b == doc_b[-1]).astype(jnp.float32)[:, None, None]
        weighted_values = key_b * jnp.exp(block_finish[None] - running_total) * end_flag
        carry_marker = (doc_b[-1] == prev_doc).astype(jnp.float32)
        recurrent_state = recurrent_state * (
            jnp.exp(block_finish)[:, :, None] * carry_marker
        ) + jnp.einsum(
            "dmf,dmb->mfb", weighted_values, value_block, precision=lax.Precision.HIGHEST
        )
        return (recurrent_state, intra + across_blocks)

    start_state = jnp.zeros((heads_n, chan, chan), jnp.float32)
    final_state, results = lax.scan(
        block_step,
        start_state,
        (
            split_blocks(query),
            split_blocks(log_forget),
            split_blocks(keyed),
            split_blocks(value),
            doc_blocks,
            before,
        ),
    )
    return results.reshape(length, heads_n, chan)


def row_gather(values):
    return lax.all_gather(values, "tensor", axis=0, tiled=True)


def row_sum(values):
    return lax.psum_scatter(values, "tensor", scatter_dimension=0, tiled=True)


def fetch_weights(inputs, outputs):
    gathered_in = (
        lax.all_gather(inputs[0], "dp", axis=0, tiled=True),
        lax.all_gather(inputs[1], "dp", axis=0, tiled=True),
        lax.all_gather(inputs[2], "dp", axis=0, tiled=True),
        lax.all_gather(inputs[3], "dp", axis=0, tiled=True),
        lax.all_gather(inputs[4], "dp", axis=0, tiled=True),
        lax.all_gather(inputs[5], "dp", axis=0, tiled=True),
    )
    gathered_out = (
        lax.all_gather(outputs[0], "dp", axis=1, tiled=True),
        lax.all_gather(outputs[1], "dp", axis=1, tiled=True),
    )
    return (gathered_in, gathered_out)


def shards(
    tokens,
    doc_ids,
    attn_gain,
    forget_floor,
    w_query,
    w_forget,
    w_value,
    w_outgate,
    w_output,
    mlp_gain,
    w_gate,
    w_up,
    w_down,
    cotangent,
):
    attn_full, floor_full, mlp_full = (
        lax.all_gather(attn_gain, ("dp", "tensor"), axis=0, tiled=True),
        lax.all_gather(forget_floor, ("dp", "tensor"), axis=0, tiled=True),
        lax.all_gather(mlp_gain, ("dp", "tensor"), axis=0, tiled=True),
    )
    part_index = lax.axis_index("tensor")
    local_width = w_query.shape[1]
    local_heads = local_width // HK
    floor_local = lax.dynamic_slice_in_dim(
        floor_full, part_index * local_width, local_width
    ).reshape(local_heads, HK)
    inputs = (w_query, w_forget, w_value, w_outgate, w_gate, w_up)
    outputs = (w_output, w_down)
    model_width = attn_full.shape[0]
    doc_all = doc_ids[0]
    row_count = doc_all.shape[0]
    resid_in = tokens[0].reshape(-1, model_width).astype(jnp.float32)
    cot_local = cotangent[0].reshape(-1, model_width)
    weights = fetch_weights(inputs, outputs)
    (wq_all, wf_all, wv_all, wg_all, wgate_all, wup_all), (wo_all, wdown_all) = weights
    scale_one = row_scale(resid_in)
    normed = row_gather((resid_in * scale_one * attn_full).astype(jnp.bfloat16))
    query = matmul_plain(normed, wq_all)
    forget_raw = matmul_plain(normed, wf_all)
    value = matmul_plain(normed, wv_all)
    out_gate = matmul_plain(normed, wg_all)

    def mixer(query_in, forget_in, value_in, floor_in):

        def shaped(arr):
            return arr.reshape(row_count, -1, local_heads, HK)

        mixed_rows = jax.vmap(recurrence, in_axes=(0, 0, 0, None, 0))(
            shaped(query_in), shaped(forget_in), shaped(value_in), floor_in, doc_all
        )
        return mixed_rows.reshape(query_in.shape[0], local_width)

    mixed, pullback = jax.vjp(mixer, query, forget_raw, value, floor_local)
    gate_act = jax.nn.silu(out_gate)
    gated = (mixed * gate_act).astype(jnp.bfloat16)
    branch = row_sum(matmul_plain(gated, wo_all))
    resid = resid_in + branch
    scale_two = row_scale(resid)
    normed2 = row_gather((resid * scale_two * mlp_full).astype(jnp.bfloat16))
    gate_proj = matmul_plain(normed2, wgate_all)
    up_proj = matmul_plain(normed2, wup_all)
    gate_silu = jax.nn.silu(gate_proj)
    hidden = (gate_silu * up_proj).astype(jnp.bfloat16)
    ffn_out = row_sum(matmul_plain(hidden, wdown_all))
    layer_out = (resid + ffn_out).astype(jnp.bfloat16).reshape(tokens.shape)
    weights = fetch_weights(inputs, outputs)
    (wq_all, wf_all, wv_all, wg_all, wgate_all, wup_all), (wo_all, wdown_all) = weights
    cot_full = row_gather(cot_local)
    d_hidden = times_trans(cot_full, wdown_all)
    grad_down = trans_times(hidden, cot_full)
    d_gate = (d_hidden * up_proj * silu_slope(gate_proj)).astype(jnp.bfloat16)
    d_up = (d_hidden * gate_silu).astype(jnp.bfloat16)
    grad_gate = trans_times(normed2, d_gate)
    grad_up = trans_times(normed2, d_up)
    d_normed2 = row_sum(times_trans(d_gate, wgate_all) + times_trans(d_up, wup_all))
    grad_mlp = jnp.sum(d_normed2 * resid * scale_two, axis=0)
    inner_two = jnp.mean(d_normed2 * mlp_full * resid, axis=-1, keepdims=True)
    d_resid = (
        cot_local.astype(jnp.float32)
        + d_normed2 * mlp_full * scale_two
        - resid * scale_two**3 * inner_two
    )
    d_branch = row_gather(d_resid.astype(jnp.bfloat16))
    d_gated = times_trans(d_branch, wo_all)
    grad_output = trans_times(gated, d_branch)
    d_mixed = d_gated * gate_act
    d_outgate = (d_gated * mixed * silu_slope(out_gate)).astype(jnp.bfloat16)
    d_query, d_forget, d_value, d_floor = pullback(d_mixed)
    d_query = d_query.astype(jnp.bfloat16)
    d_forget = d_forget.astype(jnp.bfloat16)
    d_value = d_value.astype(jnp.bfloat16)
    grad_query = trans_times(normed, d_query)
    grad_forget = trans_times(normed, d_forget)
    grad_value = trans_times(normed, d_value)
    grad_outgate = trans_times(normed, d_outgate)
    d_normed = row_sum(
        times_trans(d_query, wq_all)
        + times_trans(d_forget, wf_all)
        + times_trans(d_value, wv_all)
        + times_trans(d_outgate, wg_all)
    )
    grad_attn = jnp.sum(d_normed * resid_in * scale_one, axis=0)
    inner_one = jnp.mean(d_normed * attn_full * resid_in, axis=-1, keepdims=True)
    grad_tokens = (
        d_resid + d_normed * attn_full * scale_one - resid_in * scale_one**3 * inner_one
    ).reshape(tokens.shape)
    reduced_in = (
        lax.psum_scatter(
            grad_query.astype(jnp.bfloat16), "dp", scatter_dimension=0, tiled=True
        ).astype(jnp.float32),
        lax.psum_scatter(
            grad_forget.astype(jnp.bfloat16), "dp", scatter_dimension=0, tiled=True
        ).astype(jnp.float32),
        lax.psum_scatter(
            grad_value.astype(jnp.bfloat16), "dp", scatter_dimension=0, tiled=True
        ).astype(jnp.float32),
        lax.psum_scatter(
            grad_outgate.astype(jnp.bfloat16), "dp", scatter_dimension=0, tiled=True
        ).astype(jnp.float32),
        lax.psum_scatter(
            grad_gate.astype(jnp.bfloat16), "dp", scatter_dimension=0, tiled=True
        ).astype(jnp.float32),
        lax.psum_scatter(
            grad_up.astype(jnp.bfloat16), "dp", scatter_dimension=0, tiled=True
        ).astype(jnp.float32),
    )
    reduced_out = (
        lax.psum_scatter(
            grad_output.astype(jnp.bfloat16), "dp", scatter_dimension=1, tiled=True
        ).astype(jnp.float32),
        lax.psum_scatter(
            grad_down.astype(jnp.bfloat16), "dp", scatter_dimension=1, tiled=True
        ).astype(jnp.float32),
    )
    floor_vector = lax.dynamic_update_slice(
        jnp.zeros((model_width,), jnp.float32), d_floor.reshape(-1), (part_index * local_width,)
    )
    reduced_small = (
        lax.psum_scatter(grad_attn, ("dp", "tensor"), scatter_dimension=0, tiled=True),
        lax.psum_scatter(floor_vector, ("dp", "tensor"), scatter_dimension=0, tiled=True),
        lax.psum_scatter(grad_mlp, ("dp", "tensor"), scatter_dimension=0, tiled=True),
    )
    return (
        layer_out,
        grad_tokens,
        reduced_small[0],
        reduced_small[1],
        reduced_in[0],
        reduced_in[1],
        reduced_in[2],
        reduced_in[3],
        reduced_out[0],
        reduced_small[2],
        reduced_in[4],
        reduced_in[5],
        reduced_out[1],
    )


def solution(mesh):
    return jax.shard_map(
        shards,
        mesh=mesh,
        in_specs=(
            P("dp", "tensor", None, None),
            P("dp", None, None),
            P(("dp", "tensor")),
            P(("dp", "tensor")),
            P("dp", "tensor"),
            P("dp", "tensor"),
            P("dp", "tensor"),
            P("dp", "tensor"),
            P("tensor", "dp"),
            P(("dp", "tensor")),
            P("dp", "tensor"),
            P("dp", "tensor"),
            P("tensor", "dp"),
            P("dp", "tensor", None, None),
        ),
        out_specs=(
            P("dp", "tensor", None, None),
            P("dp", "tensor", None, None),
            P(("dp", "tensor")),
            P(("dp", "tensor")),
            P("dp", "tensor"),
            P("dp", "tensor"),
            P("dp", "tensor"),
            P("dp", "tensor"),
            P("tensor", "dp"),
            P(("dp", "tensor")),
            P("dp", "tensor"),
            P("dp", "tensor"),
            P("tensor", "dp"),
        ),
        check_vma=False,
    )
```

profile of v0, /device:TPU:0, one launch (start us, length us, event | category | flops | bytes accessed | tf_op | source)
XLA Modules:
  0.0 2645.1 jit_solution(10890282832894742384)
XLA Ops:
  11.6 68.5 %all-reduce.9 = (f32[2048]{0:T(1024)S(1)}, f32[2048]{0:T(1024)S(1)}, f32[2048]{0:T(1024)S(1)}) all-reduce(f32[2048]{0:T(1024)S(1)} %dynamic-update-slice.1, f32[2048]{0:T(1024)S(1)} %dynamic-update-slice, f32[2048]{0:T(1024)S(1)} %dynamic-update-slice.2), channel_id=1, replica_groups=mesh['dp'=32,'tensor'=4] {'dp','tensor'}, use_global_device_ids=true, to_apply=%add.3 | all-reduce | flops 6144 | bytes 49152
  87.0 20.4 all-gather.14.cloned.1.call-done
  107.4 75.0 %all-gather.16.cloned.1.call-done = bf16[2048,512]{1,0:T(8,128)(2,1)} async-done(((bf16[64,512]{1,0:T(8,128)(2,1)}), bf16[2048,512]{1,0:T(8,128)(2,1)}) %all-gather.16.cloned.1.call-update) | async-done | bytes 2097168 | tf_op jit(solution)/shard_map/all_gather | solution.py:112
  182.4 3.6 fusion.70
  189.3 63.8 %all-gather.18.cloned.1.call-done = bf16[2048,512]{1,0:T(8,128)(2,1)} async-done(((bf16[64,512]{1,0:T(8,128)(2,1)}), bf16[2048,512]{1,0:T(8,128)(2,1)}) %all-gather.18.cloned.1.call-update) | async-done | bytes 2097168 | tf_op jit(solution)/shard_map/all_gather | solution.py:113
  253.1 4.4 fusion.106
  259.1 64.6 %all-gather.20.cloned.1.call-done = bf16[2048,512]{1,0:T(8,128)(2,1)} async-done(((bf16[64,512]{1,0:T(8,128)(2,1)}), bf16[2048,512]{1,0:T(8,128)(2,1)}) %all-gather.20.cloned.1.call-update) | async-done | bytes 2097168 | tf_op jit(solution)/shard_map/all_gather | solution.py:111
  323.7 3.5 fusion.107
  332.1 142.7 %while.40 = (s32[]{:T(128)}, f32[4,4,128,128]{3,2,1,0:T(8,128)S(1)}, f32[2,4,64,4,128]{4,2,3,1,0:T(8,128)}, f32[2,4,4,128,128]{4,3,2,1,0:T(8,128)}, f32[2,4,64,4...) while((s32[]{:T(128)}, ...), condition=%wide.region_3.4_spmd.clone, body=%wide.region_1.3_spmd.clone.sunk | while | flops 563977216 | bytes 90539864 | solution.py:86
  333.7 21.6 exponential_select_fusion.2
  357.4 36.4 %fusion.209 = f32[4,64,64,4]{1,2,3,0:T(8,128)S(1)} fusion(f32[4,64,64,4,128]{4,3,2,1,0:T(4,128)} %exponential_select_fusion.2, f32[4,4,128,64]{2,3,1,0:T(8,128)S(1)} %copy.387, f32[4,4,128,64]{2,3,1,0:T(8,128)S(1)} %copy.389), kind=kLoop, calls=%fused_computation.75.clone.1 | loop fusion | flops 25100288 | bytes 34865152 | tf_op jit(solution)/shard_map/jvp(vmap())/while/body/eval_jaxpr/ihk,jhk,ijhk->ijh/dot_general | solution.py:60
  396.9 2.9 fusion.210
  404.7 21.6 exponential_select_fusion.2
  428.4 36.4 %fusion.209 = f32[4,64,64,4]{1,2,3,0:T(8,128)S(1)} fusion(f32[4,64,64,4,128]{4,3,2,1,0:T(4,128)} %exponential_select_fusion.2, f32[4,4,128,64]{2,3,1,0:T(8,128)S(1)} %copy.387, f32[4,4,128,64]{2,3,1,0:T(8,128)S(1)} %copy.389), kind=kLoop, calls=%fused_computation.75.clone.1 | loop fusion | flops 25100288 | bytes 34865152 | tf_op jit(solution)/shard_map/jvp(vmap())/while/body/eval_jaxpr/ihk,jhk,ijhk->ijh/dot_general | solution.py:60
  468.0 2.9 fusion.210
  476.7 4.9 fusion.84
  481.6 5.1 fusion.108
  487.6 41.5 %reduce-scatter.13.cloned.1.call-done = f32[128,2048]{1,0:T(8,128)} async-done(((f32[512,2048]{1,0:T(8,128)}), f32[128,2048]{1,0:T(8,128)}) %reduce-scatter.13.cloned.1.call-update) | async-done | bytes 1048592 | tf_op jit(solution)/shard_map/reduce_scatter | solution.py:106
  533.5 89.1 %all-gather.28.cloned.1.call-done = bf16[2048,1408]{1,0:T(8,128)(2,1)} async-done(((bf16[64,1408]{1,0:T(8,128)(2,1)}), bf16[2048,1408]{1,0:T(8,128)(2,1)}) %all-gather.28.cloned.1.call-update) | async-done | bytes 5767184 | tf_op jit(solution)/shard_map/all_gather | solution.py:115
  622.6 29.0 %all-gather.26.cloned.1.call-done = bf16[512,2048]{1,0:T(8,128)(2,1)} async-done(((bf16[128,2048]{1,0:T(8,128)(2,1)}), bf16[512,2048]{1,0:T(8,128)(2,1)}) %all-gather.26.cloned.1.call-update) | async-done | bytes 2097168 | tf_op jit(solution)/shard_map/all_gather | solution.py:102
  651.6 8.2 fusion.109
  659.8 85.2 %all-gather.30.cloned.1.call-done = bf16[2048,1408]{1,0:T(8,128)(2,1)} async-done(((bf16[64,1408]{1,0:T(8,128)(2,1)}), bf16[2048,1408]{1,0:T(8,128)(2,1)}) %all-gather.30.cloned.1.call-update) | async-done | bytes 5767184 | tf_op jit(solution)/shard_map/all_gather | solution.py:116
  745.0 8.3 fusion.110
  753.3 20.2 all-gather.36.cloned.1.call-done
  773.5 93.4 %all-gather.32.cloned.1.call-done = bf16[1408,2048]{0,1:T(8,128)(2,1)} async-done(((bf16[1408,64]{0,1:T(8,128)(2,1)}), bf16[1408,2048]{0,1:T(8,128)(2,1)}) %all-gather.32.cloned.1.call-update) | async-done | bytes 5767184 | tf_op jit(solution)/shard_map/all_gather | solution.py:120
  866.9 10.3 multiply_convert_fusion
  877.2 6.8 fusion.112
  884.0 5.1 convolution_add_fusion.3
  889.2 8.5 fusion.111
  897.7 34.6 %reduce-scatter.17.cloned.1.call-done = f32[128,2048]{1,0:T(8,128)} async-done(((f32[512,2048]{1,0:T(8,128)}), f32[128,2048]{1,0:T(8,128)}) %reduce-scatter.17.cloned.1.call-update) | async-done | bytes 1048592 | tf_op jit(solution)/shard_map/reduce_scatter | solution.py:106
  934.4 46.5 %reduce-scatter.15.cloned.1.call-done = f32[128,2048]{1,0:T(8,128)} async-done(((f32[512,2048]{1,0:T(8,128)}), f32[128,2048]{1,0:T(8,128)}) %reduce-scatter.15.cloned.1.call-update) | async-done | bytes 1048592 | tf_op jit(solution)/shard_map/reduce_scatter | solution.py:106
  980.9 3.3 fusion.102
  984.3 8.0 convolution_convert_fusion.2
  993.8 6.7 convolution_convert_fusion.1
  1002.3 6.6 convolution_convert_fusion
  1009.1 5.2 all-gather.34.cloned.1.call-done
  1014.3 4.9 fusion.86
  1024.1 167.7 %while.41 = (s32[]{:T(128)}, f32[4,4,128,128]{3,2,1,0:T(8,128)}, bf16[2,4,64,4,128]{4,2,3,1,0:T(8,128)(2,1)}, f32[2,4,64,4,128]{4,2,3,1,0:T(8,128)}, f32[2,4,64,...) while((s32[]{:T(128)}, f32[4,4,128,128]{3,2,1,0:T(8,128)}, ...), condition=%wide.region_16.17_spmd.clone, body=%wide.region_9.16_spmd.clone.sunk | while | flops 1228907520 | bytes 113469472 | solution.py:86
  1033.8 27.5 %fusion.229 = (f32[4,64,4,128]{3,1,2,0:T(8,128)}, f32[4,64,4,128]{3,2,1,0:T(4,128)}, f32[4,64,64,4]{2,3,1,0:T(4,128)S(1)}) fusion(f32[4,4,128,64]{2,3,1,0:T(8,128)S(1)} %bitcast.402, f32[4,4,128,64]{2,1,3,0:T(4,128)S(1)} %copy.401, f32[4,64,4,128]{3,1,2,0:T(8,128)S(1)} %copy.399, f32[4,64,4,128]{3,2,1,0:T(4,128)S(1)} %fusion.226, ...), kind=kLoop, calls=%fused_computation.16.clone.1 | loop fusion | flops 100335616 | bytes 3686400 | tf_op jit(solution)/shard_map/transpose(jvp(vmap()))/while/body/eval_jaxpr/checkpoint/reduce_sum | solution.py:58
  1064.0 3.0 fusion.234
  1069.4 15.5 fusion.228
  1084.9 12.5 fusion.227
  1104.3 3.0 convolution_add_fusion.7
  1107.4 2.7 dynamic-slice_bitcast_fusion.15
  1118.0 27.5 %fusion.229 = (f32[4,64,4,128]{3,1,2,0:T(8,128)}, f32[4,64,4,128]{3,2,1,0:T(4,128)}, f32[4,64,64,4]{2,3,1,0:T(4,128)S(1)}) fusion(f32[4,4,128,64]{2,3,1,0:T(8,128)S(1)} %bitcast.402, f32[4,4,128,64]{2,1,3,0:T(4,128)S(1)} %copy.401, f32[4,64,4,128]{3,1,2,0:T(8,128)S(1)} %copy.399, f32[4,64,4,128]{3,2,1,0:T(4,128)S(1)} %fusion.226, ...), kind=kLoop, calls=%fused_computation.16.clone.1 | loop fusion | flops 100335616 | bytes 3686400 | tf_op jit(solution)/shard_map/transpose(jvp(vmap()))/while/body/eval_jaxpr/checkpoint/reduce_sum | solution.py:58
  1148.2 3.0 fusion.234
  1153.5 15.5 fusion.228
  1169.1 12.5 fusion.227
  1188.5 3.0 convolution_add_fusion.7
  1198.3 4.4 convolution_convert_fusion.3
  1203.2 4.3 convolution_convert_fusion.7
  1207.9 4.4 convolution_convert_fusion.5
  1212.4 4.3 convolution_convert_fusion.4
  1216.9 3.0 fusion.113
  1223.2 3.4 add_add_fusion
  1228.4 179.0 %reduce-scatter.33.cloned.1.call-done = bf16[64,1408]{1,0:T(8,128)(2,1)} async-done(((bf16[2048,1408]{1,0:T(8,128)(2,1)}), bf16[64,1408]{1,0:T(8,128)(2,1)}) %reduce-scatter.33.cloned.1.call-update) | async-done | bytes 180240 | tf_op jit(solution)/shard_map/reduce_scatter | solution.py:248
  1409.1 191.7 %reduce-scatter.35.cloned.1.call-done = bf16[1408,64]{0,1:T(8,128)(2,1)} async-done(((bf16[1408,2048]{0,1:T(8,128)(2,1)}), bf16[1408,64]{0,1:T(8,128)(2,1)}) %reduce-scatter.35.cloned.1.call-update) | async-done | bytes 180240 | tf_op jit(solution)/shard_map/reduce_scatter | solution.py:256
  1604.2 181.2 %reduce-scatter.23.cloned.1.call-done = bf16[64,512]{1,0:T(8,128)(2,1)} async-done(((bf16[2048,512]{1,0:T(8,128)(2,1)}), bf16[64,512]{1,0:T(8,128)(2,1)}) %reduce-scatter.23.cloned.1.call-update) | async-done | bytes 65552 | tf_op jit(solution)/shard_map/reduce_scatter | solution.py:236
  1786.9 182.8 %reduce-scatter.29.cloned.1.call-done = bf16[512,64]{0,1:T(8,128)(2,1)} async-done(((bf16[512,2048]{0,1:T(8,128)(2,1)}), bf16[512,64]{0,1:T(8,128)(2,1)}) %reduce-scatter.29.cloned.1.call-update) | async-done | bytes 65552 | tf_op jit(solution)/shard_map/reduce_scatter | solution.py:253
  1971.2 183.1 %reduce-scatter.21.cloned.1.call-done = bf16[64,512]{1,0:T(8,128)(2,1)} async-done(((bf16[2048,512]{1,0:T(8,128)(2,1)}), bf16[64,512]{1,0:T(8,128)(2,1)}) %reduce-scatter.21.cloned.1.call-update) | async-done | bytes 65552 | tf_op jit(solution)/shard_map/reduce_scatter | solution.py:233
  2155.7 183.1 %reduce-scatter.25.cloned.1.call-done = bf16[64,512]{1,0:T(8,128)(2,1)} async-done(((bf16[2048,512]{1,0:T(8,128)(2,1)}), bf16[64,512]{1,0:T(8,128)(2,1)}) %reduce-scatter.25.cloned.1.call-update) | async-done | bytes 65552 | tf_op jit(solution)/shard_map/reduce_scatter | solution.py:239
  2340.3 182.9 %reduce-scatter.27.cloned.1.call-done = bf16[64,512]{1,0:T(8,128)(2,1)} async-done(((bf16[2048,512]{1,0:T(8,128)(2,1)}), bf16[64,512]{1,0:T(8,128)(2,1)}) %reduce-scatter.27.cloned.1.call-update) | async-done | bytes 65552 | tf_op jit(solution)/shard_map/reduce_scatter | solution.py:242
  2524.7 40.8 %reduce-scatter.19.cloned.1.call-done = f32[128,2048]{1,0:T(8,128)} async-done(((f32[512,2048]{1,0:T(8,128)}), f32[128,2048]{1,0:T(8,128)}) %reduce-scatter.19.cloned.1.call-update) | async-done | bytes 1048592 | tf_op jit(solution)/shard_map/reduce_scatter | solution.py:106
  2567.0 66.7 %all-reduce.8 = (f32[2048]{0:T(1024)S(1)}, f32[2048]{0:T(1024)S(1)}, f32[2048]{0:T(1024)S(1)}) all-reduce(f32[2048]{0:T(1024)S(1)} %get-tuple-element.694, f32[2048]{0:T(1024)S(1)} %bitcast_dynamic-update-slice_fusion.3, f32[2048]{0:T(1024)S(1)} %copy-done.50), channel_id=7, replica_groups=mesh['dp'=32,'tensor'=4] {'dp','tensor'}, use_global_device_ids=true, to_apply=%region_20.21.clone | all-reduce | flops 6144 | bytes 49152
  (387 shorter events, 130.4 us)
Async XLA Ops:
  7.2 100.2 %all-gather.14.cloned.1.call-start = ((), (), s32[]{:S(2)}) async-start(), calls=%async_computation.12 | async-start | bytes 2621440 | tf_op jit(solution)/shard_map/all_gather | solution.py:102
  9.1 77.0 %copy-start.54 = (f32[128]{0:T(128)}, f32[128]{0:T(128)S(1)}, u32[]{:S(2)}) copy-start(f32[128]{0:T(128)S(1)} %get-tuple-element.782) | copy-start | bytes 1540
  80.1 6.0 copy-start.46
  82.1 100.2 %all-gather.16.cloned.1.call-start = ((), (), s32[]{:S(2)}) async-start(), calls=%async_computation.13 | async-start | bytes 2162688 | tf_op jit(solution)/shard_map/all_gather | solution.py:112
  82.9 170.2 %all-gather.18.cloned.1.call-start = ((), (), s32[]{:S(2)}) async-start(), calls=%async_computation.14 | async-start | bytes 2162688 | tf_op jit(solution)/shard_map/all_gather | solution.py:113
  83.6 240.1 %all-gather.20.cloned.1.call-start = ((), (), s32[]{:S(2)}) async-start(), calls=%async_computation.15 | async-start | bytes 2162688 | tf_op jit(solution)/shard_map/all_gather | solution.py:111
  84.2 392.5 %all-gather.22.cloned.1.call-start = ((), (), s32[]{:S(2)}) async-start(), calls=%async_computation.16 | async-start | bytes 2162688 | tf_op jit(solution)/shard_map/all_gather | solution.py:114
  84.8 396.8 %all-gather.24.cloned.1.call-start = ((), (), s32[]{:S(2)}) async-start(), calls=%async_computation.17 | async-start | bytes 2162688 | tf_op jit(solution)/shard_map/all_gather | solution.py:119
  85.3 443.8 %reduce-scatter.13.cloned.1.call-start = ((), (), s32[]{:S(2)}) async-start(), calls=%async_computation.18 | async-start | bytes 5242880 | tf_op jit(solution)/shard_map/reduce_scatter | solution.py:106
  86.1 100.3 %copy-start.48 = (f32[512]{0:T(512)}, f32[512]{0:T(512)S(1)}, u32[]{:S(2)}) copy-start(f32[512]{0:T(512)S(1)} %get-tuple-element.753) | copy-start | bytes 6148
  86.1 100.3 %copy-start.51 = (f32[4,128]{1,0:T(4,128)}, f32[4,128]{1,0:T(4,128)S(1)}, u32[]{:S(2)}) copy-start(f32[4,128]{1,0:T(4,128)S(1)} %broadcast_subtract_fusion.1) | copy-start | bytes 6148
  86.9 95.5 %copy-start.40 = (s32[1,4,128]{1,2,0:T(8,128)}, s32[1,4,128]{1,2,0:T(8,128)S(1)}, u32[]{:S(2)}) copy-start(s32[1,4,128]{1,2,0:T(8,128)S(1)} %copy.227) | copy-start | bytes 6148
  186.4 71.2 %copy-start.20 = (f32[4,2,64,4,128]{4,3,2,1,0:T(4,128)}, f32[4,2,64,4,128]{4,3,2,1,0:T(4,128)S(1)}, u32[]{:S(2)}) copy-start(f32[4,2,64,4,128]{4,3,2,1,0:T(4,128)S(1)} %div.43) | copy-start | bytes 3145732
  486.7 42.4 %copy-start.16 = (bf16[1,1,128,2048]{3,2,1,0:T(8,128)(2,1)S(1)}, bf16[1,1,128,2048]{3,2,1,0:T(8,128)(2,1)}, u32[]{:S(2)}) copy-start(bf16[1,1,128,2048]{3,2,1,0:T(8,128)(2,1)} %param.18) | copy-start | bytes 1572868
  486.8 135.8 %all-gather.28.cloned.1.call-start = ((), (), s32[]{:S(2)}) async-start(), calls=%async_computation.20 | async-start | bytes 5947392 | tf_op jit(solution)/shard_map/all_gather | solution.py:115
  487.5 164.1 %all-gather.26.cloned.1.call-start = ((), (), s32[]{:S(2)}) async-start(), calls=%async_computation.19 | async-start | bytes 2621440 | tf_op jit(solution)/shard_map/all_gather | solution.py:102
  531.5 213.5 %all-gather.30.cloned.1.call-start = ((), (), s32[]{:S(2)}) async-start(), calls=%async_computation.21 | async-start | bytes 5947392 | tf_op jit(solution)/shard_map/all_gather | solution.py:116
  532.1 241.3 %all-gather.36.cloned.1.call-start = ((), (), s32[]{:S(2)}) async-start(), calls=%async_computation.35 | async-start | bytes 2621440 | tf_op jit(solution)/shard_map/all_gather | solution.py:102
  532.9 334.0 %all-gather.32.cloned.1.call-start = ((), (), s32[]{:S(2)}) async-start(), calls=%async_computation.22 | async-start | bytes 5947392 | tf_op jit(solution)/shard_map/all_gather | solution.py:120
  533.4 398.9 %reduce-scatter.17.cloned.1.call-start = ((), (), s32[]{:S(2)}) async-start(), calls=%async_computation.24 | async-start | bytes 5242880 | tf_op jit(solution)/shard_map/reduce_scatter | solution.py:106
  877.2 6.8 copy-start.62
  877.2 6.8 copy-start.61
  877.2 6.8 copy-start.57
  889.1 91.8 %reduce-scatter.15.cloned.1.call-start = ((), (), s32[]{:S(2)}) async-start(), calls=%async_computation.23 | async-start | bytes 5242880 | tf_op jit(solution)/shard_map/reduce_scatter | solution.py:106
  897.7 83.3 %copy-start.35 = (bf16[1,1,128,2048]{3,2,1,0:T(8,128)(2,1)S(1)}, bf16[1,1,128,2048]{3,2,1,0:T(8,128)(2,1)}, u32[]{:S(2)}) copy-start(bf16[1,1,128,2048]{3,2,1,0:T(8,128)(2,1)} %param.31) | copy-start | bytes 1572868
  897.7 116.6 %all-gather.34.cloned.1.call-start = ((), (), s32[]{:S(2)}) async-start(), calls=%async_computation.25 | async-start | bytes 2621440 | tf_op jit(solution)/shard_map/all_gather | solution.py:102
  984.2 242.4 %reduce-scatter.31.cloned.1.call-start = ((), (), s32[]{:S(2)}) async-start(), calls=%async_computation.32 | async-start | bytes 5947392 | tf_op jit(solution)/shard_map/reduce_scatter | solution.py:245
  992.3 415.1 %reduce-scatter.33.cloned.1.call-start = ((), (), s32[]{:S(2)}) async-start(), calls=%async_computation.33 | async-start | bytes 5947392 | tf_op jit(solution)/shard_map/reduce_scatter | solution.py:248
  1000.5 600.2 %reduce-scatter.35.cloned.1.call-start = ((), (), s32[]{:S(2)}) async-start(), calls=%async_computation.34 | async-start | bytes 5947392 | tf_op jit(solution)/shard_map/reduce_scatter | solution.py:256
  1009.0 5.3 copy-start.39
  1009.0 776.4 %reduce-scatter.23.cloned.1.call-start = ((), (), s32[]{:S(2)}) async-start(), calls=%async_computation.28 | async-start | bytes 2162688 | tf_op jit(solution)/shard_map/reduce_scatter | solution.py:236
  1032.0 29.3 %copy-start.12 = (f32[4,64,64,4]{2,3,1,0:T(4,128)}, f32[4,64,64,4]{2,3,1,0:T(4,128)S(1)}, u32[]{:S(2)}) copy-start(f32[4,64,64,4]{2,3,1,0:T(4,128)S(1)} %copy.402) | copy-start | bytes 786436 | tf_op jit(solution)/shard_map/transpose(jvp(vmap()))/while
  1032.2 29.1 %copy-start.9 = (f32[4,64,4,128]{3,1,2,0:T(8,128)}, f32[4,64,4,128]{3,1,2,0:T(8,128)S(1)}, u32[]{:S(2)}) copy-start(f32[4,64,4,128]{3,1,2,0:T(8,128)S(1)} %copy.399) | copy-start | bytes 1572868 | tf_op jit(solution)/shard_map/transpose(jvp(vmap()))/while
  1033.8 27.5 %copy-start.14 = (f32[4,4,128,64]{2,1,3,0:T(4,128)}, f32[4,4,128,64]{2,1,3,0:T(4,128)S(1)}, u32[]{:S(2)}) copy-start(f32[4,4,128,64]{2,1,3,0:T(4,128)S(1)} %copy.401) | copy-start | bytes 1572868 | tf_op jit(solution)/shard_map/transpose(jvp(vmap()))/while
  1069.3 15.5 copy-start.10
  1069.3 15.5 copy-start.13
  1069.3 15.5 copy-start.15
  1084.9 12.5 copy-start.4
  1084.9 12.5 copy-start.25
  1084.9 12.5 copy-start.28
  1101.9 5.5 copy-start.6
  1116.2 29.3 %copy-start.12 = (f32[4,64,64,4]{2,3,1,0:T(4,128)}, f32[4,64,64,4]{2,3,1,0:T(4,128)S(1)}, u32[]{:S(2)}) copy-start(f32[4,64,64,4]{2,3,1,0:T(4,128)S(1)} %copy.402) | copy-start | bytes 786436 | tf_op jit(solution)/shard_map/transpose(jvp(vmap()))/while
  1116.4 29.1 %copy-start.9 = (f32[4,64,4,128]{3,1,2,0:T(8,128)}, f32[4,64,4,128]{3,1,2,0:T(8,128)S(1)}, u32[]{:S(2)}) copy-start(f32[4,64,4,128]{3,1,2,0:T(8,128)S(1)} %copy.399) | copy-start | bytes 1572868 | tf_op jit(solution)/shard_map/transpose(jvp(vmap()))/while
  1117.9 27.5 %copy-start.14 = (f32[4,4,128,64]{2,1,3,0:T(4,128)}, f32[4,4,128,64]{2,1,3,0:T(4,128)S(1)}, u32[]{:S(2)}) copy-start(f32[4,4,128,64]{2,1,3,0:T(4,128)S(1)} %copy.401) | copy-start | bytes 1572868 | tf_op jit(solution)/shard_map/transpose(jvp(vmap()))/while
  1153.5 15.5 copy-start.10
  1153.5 15.5 copy-start.13
  1153.5 15.5 copy-start.15
  1169.0 12.5 copy-start.4
  1169.0 12.5 copy-start.25
  1169.1 12.5 copy-start.28
  1186.1 5.5 copy-start.6
  1198.2 771.4 %reduce-scatter.29.cloned.1.call-start = ((), (), s32[]{:S(2)}) async-start(), calls=%async_computation.31 | async-start | bytes 2162688 | tf_op jit(solution)/shard_map/reduce_scatter | solution.py:253
  1202.7 951.5 %reduce-scatter.21.cloned.1.call-start = ((), (), s32[]{:S(2)}) async-start(), calls=%async_computation.27 | async-start | bytes 2162688 | tf_op jit(solution)/shard_map/reduce_scatter | solution.py:233
  1207.4 1131.3 %reduce-scatter.25.cloned.1.call-start = ((), (), s32[]{:S(2)}) async-start(), calls=%async_computation.29 | async-start | bytes 2162688 | tf_op jit(solution)/shard_map/reduce_scatter | solution.py:239
  1212.3 1310.8 %reduce-scatter.27.cloned.1.call-start = ((), (), s32[]{:S(2)}) async-start(), calls=%async_computation.30 | async-start | bytes 2162688 | tf_op jit(solution)/shard_map/reduce_scatter | solution.py:242
  1216.7 1348.8 %reduce-scatter.19.cloned.1.call-start = ((), (), s32[]{:S(2)}) async-start(), calls=%async_computation.26 | async-start | bytes 5242880 | tf_op jit(solution)/shard_map/reduce_scatter | solution.py:106
  1226.5 375.9 %copy-start.21 = (f32[4,2,64,4,128]{4,3,2,1,0:T(4,128)S(1)}, f32[4,2,64,4,128]{4,3,2,1,0:T(4,128)}, u32[]{:S(2)}) copy-start(f32[4,2,64,4,128]{4,3,2,1,0:T(4,128)} %copy-done.20) | copy-start | bytes 3145732
  1226.5 375.9 %copy-start.52 = (f32[4,128]{1,0:T(4,128)S(1)}, f32[4,128]{1,0:T(4,128)}, u32[]{:S(2)}) copy-start(f32[4,128]{1,0:T(4,128)} %copy-done.51) | copy-start | bytes 6148
  1226.6 1338.9 %copy-start.17 = (bf16[1,1,128,2048]{3,2,1,0:T(8,128)(2,1)S(1)}, bf16[1,1,128,2048]{3,2,1,0:T(8,128)(2,1)}, u32[]{:S(2)}) copy-start(bf16[1,1,128,2048]{3,2,1,0:T(8,128)(2,1)} %param.18) | copy-start | bytes 1572868
  1226.6 1338.9 %copy-start.47 = (f32[2048]{0:T(1024)S(1)}, f32[2048]{0:T(1024)}, u32[]{:S(2)}) copy-start(f32[2048]{0:T(1024)} %copy-done.46) | copy-start | bytes 24580
  1226.6 1338.9 %copy-start.55 = (f32[128]{0:T(128)S(1)}, f32[128]{0:T(128)}, u32[]{:S(2)}) copy-start(f32[128]{0:T(128)} %copy-done.54) | copy-start | bytes 1540
  1602.5 964.6 %copy-start.50 = (f32[2048]{0:T(1024)S(1)}, f32[2048]{0:T(1024)}, u32[]{:S(2)}) copy-start(f32[2048]{0:T(1024)} %get-tuple-element.692) | copy-start | bytes 24580
  1602.5 1033.0 %copy-start.56 = (f32[128]{0:T(128)S(1)}, f32[128]{0:T(128)}, u32[]{:S(2)}) copy-start(f32[128]{0:T(128)} %get-tuple-element.781) | copy-start | bytes 1540
  1604.0 1031.5 %copy-start.31 = (f32[128,2048]{1,0:T(8,128)S(1)}, f32[128,2048]{1,0:T(8,128)}, u32[]{:S(2)}) copy-start(f32[128,2048]{1,0:T(8,128)} %get-tuple-element.755) | copy-start | bytes 3145732
  (47 other events, 135.0 us)
Sparse Core Ops, SparseCore 0:
  82.2 25.0 all-gather.13
  110.4 71.9 all-gather.15
  185.4 67.6 all-gather.17
  256.0 67.6 all-gather.19
  326.5 67.6 all-gather.21
  397.1 67.6 all-gather.23
  486.9 42.1 reduce-scatter.12
  532.6 89.9 all-gather.27
  624.9 26.6 all-gather.25
  655.0 90.0 all-gather.29
  746.8 26.6 all-gather.35
  776.8 90.0 all-gather.31
  889.2 43.0 reduce-scatter.16
  934.6 46.3 reduce-scatter.14
  984.4 29.8 all-gather.33
  1016.7 197.3 reduce-scatter.30
  1216.4 190.9 reduce-scatter.32
  1409.8 190.9 reduce-scatter.34
  1603.3 182.0 reduce-scatter.22
  1787.6 182.0 reduce-scatter.28
  1972.2 182.0 reduce-scatter.20
  2156.6 182.1 reduce-scatter.24
  2341.3 181.8 reduce-scatter.26
  2525.4 40.0 reduce-scatter.18
where the time goes:
time: 2650 us
  waiting for transfers between devices  2000 us (75%)
  other arithmetic  276 us (10%)
  matrix products  162 us (6%)
  blocking collectives  135 us (5%)
  local copies, waits for them, and re-layouts  54.2 us (2%)
    reduce_scatter x1, waiting for transfers between devices, shards(): lax.psum_scatter(grad_down.astype(jnp.bfloat16), 'dp', scatter_dimension=...  192 us
    reduce_scatter x1, waiting for transfers between devices, shards(): lax.psum_scatter(grad_query.astype(jnp.bfloat16), 'dp', scatter_dimension...  183 us
    reduce_scatter x1, waiting for transfers between devices, shards(): lax.psum_scatter(grad_value.astype(jnp.bfloat16), 'dp', scatter_dimension...  183 us
    reduce_scatter x1, waiting for transfers between devices, shards(): lax.psum_scatter(grad_outgate.astype(jnp.bfloat16), 'dp', scatter_dimensi...  183 us
    reduce_scatter x1, waiting for transfers between devices, shards(): lax.psum_scatter(grad_output.astype(jnp.bfloat16), 'dp', scatter_dimensio...  183 us
    reduce_scatter x1, waiting for transfers between devices, shards(): lax.psum_scatter(grad_forget.astype(jnp.bfloat16), 'dp', scatter_dimensio...  181 us
    reduce_scatter x1, waiting for transfers between devices, shards(): lax.psum_scatter(grad_up.astype(jnp.bfloat16), 'dp', scatter_dimension=0,...  179 us
    reduce_scatter x4, waiting for transfers between devices, row_sum(): return lax.psum_scatter(values, 'tensor', scatter_dimension=0, tiled=True)  163 us
  transfers between devices with their start and end apart: 24, of which 21 were waited for; matrix products, arithmetic and copies ran while one was open for 17% of the time, Pallas kernels for 0%

commit v1 on v0

--- a/solution.py
+++ b/solution.py
@@ -99,27 +99,31 @@
 
 
 def row_gather(values):
-    return lax.all_gather(values, "tensor", axis=0, tiled=True)
+    count = 4
+    spread = jnp.broadcast_to(values[None], (count,) + values.shape)
+    got = lax.all_to_all(spread, "tensor", 0, 0, tiled=False)
+    return got.reshape((-1,) + values.shape[1:])
 
 
 def row_sum(values):
-    return lax.psum_scatter(values, "tensor", scatter_dimension=0, tiled=True)
-
-
-def fetch_weights(inputs, outputs):
-    gathered_in = (
-        lax.all_gather(inputs[0], "dp", axis=0, tiled=True),
-        lax.all_gather(inputs[1], "dp", axis=0, tiled=True),
-        lax.all_gather(inputs[2], "dp", axis=0, tiled=True),
-        lax.all_gather(inputs[3], "dp", axis=0, tiled=True),
-        lax.all_gather(inputs[4], "dp", axis=0, tiled=True),
-        lax.all_gather(inputs[5], "dp", axis=0, tiled=True),
-    )
-    gathered_out = (
-        lax.all_gather(outputs[0], "dp", axis=1, tiled=True),
-        lax.all_gather(outputs[1], "dp", axis=1, tiled=True),
-    )
-    return (gathered_in, gathered_out)
+    count = 4
+    blocks = values.reshape((count, -1) + values.shape[1:])
+    got = lax.all_to_all(blocks, "tensor", 0, 0, tiled=False)
+    return got.sum(axis=0)
+
+
+def small_gather(vectors):
+    count = 128
+    spread = jnp.broadcast_to(vectors[None], (count,) + vectors.shape)
+    got = lax.all_to_all(spread, ("dp", "tensor"), 0, 0, tiled=False)
+    return jnp.swapaxes(got, 0, 1).reshape(vectors.shape[0], -1)
+
+
+def small_sum(vectors):
+    count = 128
+    blocks = vectors.reshape(vectors.shape[0], count, -1)
+    got = lax.all_to_all(jnp.swapaxes(blocks, 0, 1), ("dp", "tensor"), 0, 0, tiled=False)
+    return got.sum(axis=0)
 
 
 def shards(
@@ -138,26 +142,32 @@
     w_down,
     cotangent,
 ):
-    attn_full, floor_full, mlp_full = (
-        lax.all_gather(attn_gain, ("dp", "tensor"), axis=0, tiled=True),
-        lax.all_gather(forget_floor, ("dp", "tensor"), axis=0, tiled=True),
-        lax.all_gather(mlp_gain, ("dp", "tensor"), axis=0, tiled=True),
-    )
+    gains = small_gather(jnp.stack([attn_gain, forget_floor, mlp_gain]))
+    attn_full, floor_full, mlp_full = gains[0], gains[1], gains[2]
     part_index = lax.axis_index("tensor")
     local_width = w_query.shape[1]
     local_heads = local_width // HK
+    hidden_width = w_gate.shape[1]
     floor_local = lax.dynamic_slice_in_dim(
         floor_full, part_index * local_width, local_width
     ).reshape(local_heads, HK)
-    inputs = (w_query, w_forget, w_value, w_outgate, w_gate, w_up)
-    outputs = (w_output, w_down)
     model_width = attn_full.shape[0]
     doc_all = doc_ids[0]
     row_count = doc_all.shape[0]
     resid_in = tokens[0].reshape(-1, model_width).astype(jnp.float32)
     cot_local = cotangent[0].reshape(-1, model_width)
-    weights = fetch_weights(inputs, outputs)
-    (wq_all, wf_all, wv_all, wg_all, wgate_all, wup_all), (wo_all, wdown_all) = weights
+    attn_pack = jnp.concatenate([w_query, w_forget, w_value, w_outgate, w_output.T], axis=1)
+    mlp_pack = jnp.concatenate([w_gate, w_up, w_down.T], axis=1)
+    attn_all = lax.all_gather(attn_pack, "dp", axis=0, tiled=True)
+    mlp_all = lax.all_gather(mlp_pack, "dp", axis=0, tiled=True)
+    wq_all = attn_all[:, 0 * local_width : 1 * local_width]
+    wf_all = attn_all[:, 1 * local_width : 2 * local_width]
+    wv_all = attn_all[:, 2 * local_width : 3 * local_width]
+    wg_all = attn_all[:, 3 * local_width : 4 * local_width]
+    wo_t = attn_all[:, 4 * local_width : 5 * local_width]
+    wgate_all = mlp_all[:, 0:hidden_width]
+    wup_all = mlp_all[:, hidden_width : 2 * hidden_width]
+    wdown_t = mlp_all[:, 2 * hidden_width : 3 * hidden_width]
     scale_one = row_scale(resid_in)
     normed = row_gather((resid_in * scale_one * attn_full).astype(jnp.bfloat16))
     query = matmul_plain(normed, wq_all)
@@ -178,7 +188,7 @@
     mixed, pullback = jax.vjp(mixer, query, forget_raw, value, floor_local)
     gate_act = jax.nn.silu(out_gate)
     gated = (mixed * gate_act).astype(jnp.bfloat16)
-    branch = row_sum(matmul_plain(gated, wo_all))
+    branch = row_sum(times_trans(gated, wo_t))
     resid = resid_in + branch
     scale_two = row_scale(resid)
     normed2 = row_gather((resid * scale_two * mlp_full).astype(jnp.bfloat16))
@@ -186,17 +196,20 @@
     up_proj = matmul_plain(normed2, wup_all)
     gate_silu = jax.nn.silu(gate_proj)
     hidden = (gate_silu * up_proj).astype(jnp.bfloat16)
-    ffn_out = row_sum(matmul_plain(hidden, wdown_all))
+    ffn_out = row_sum(times_trans(hidden, wdown_t))
     layer_out = (resid + ffn_out).astype(jnp.bfloat16).reshape(tokens.shape)
-    weights = fetch_weights(inputs, outputs)
-    (wq_all, wf_all, wv_all, wg_all, wgate_all, wup_all), (wo_all, wdown_all) = weights
     cot_full = row_gather(cot_local)
-    d_hidden = times_trans(cot_full, wdown_all)
-    grad_down = trans_times(hidden, cot_full)
+    d_hidden = matmul_plain(cot_full, wdown_t)
+    grad_down_t = trans_times(cot_full, hidden)
     d_gate = (d_hidden * up_proj * silu_slope(gate_proj)).astype(jnp.bfloat16)
     d_up = (d_hidden * gate_silu).astype(jnp.bfloat16)
     grad_gate = trans_times(normed2, d_gate)
     grad_up = trans_times(normed2, d_up)
+    mlp_grads = jnp.concatenate(
+        [grad_gate.astype(jnp.bfloat16), grad_up.astype(jnp.bfloat16), grad_down_t.astype(jnp.bfloat16)],
+        axis=1,
+    )
+    mlp_red = lax.psum_scatter(mlp_grads, "dp", scatter_dimension=0, tiled=True).astype(jnp.float32)
     d_normed2 = row_sum(times_trans(d_gate, wgate_all) + times_trans(d_up, wup_all))
     grad_mlp = jnp.sum(d_normed2 * resid * scale_two, axis=0)
     inner_two = jnp.mean(d_normed2 * mlp_full * resid, axis=-1, keepdims=True)
@@ -206,8 +219,8 @@
         - resid * scale_two**3 * inner_two
     )
     d_branch = row_gather(d_resid.astype(jnp.bfloat16))
-    d_gated = times_trans(d_branch, wo_all)
-    grad_output = trans_times(gated, d_branch)
+    d_gated = matmul_plain(d_branch, wo_t)
+    grad_output_t = trans_times(d_branch, gated)
     d_mixed = d_gated * gate_act
     d_outgate = (d_gated * mixed * silu_slope(out_gate)).astype(jnp.bfloat16)
     d_query, d_forget, d_value, d_floor = pullback(d_mixed)
@@ -218,6 +231,17 @@
     grad_forget = trans_times(normed, d_forget)
     grad_value = trans_times(normed, d_value)
     grad_outgate = trans_times(normed, d_outgate)
+    attn_grads = jnp.concatenate(
+        [
+            grad_query.astype(jnp.bfloat16),
+            grad_forget.astype(jnp.bfloat16),
+            grad_value.astype(jnp.bfloat16),
+            grad_outgate.astype(jnp.bfloat16),
+            grad_output_t.astype(jnp.bfloat16),
+        ],
+        axis=1,
+    )
+    attn_red = lax.psum_scatter(attn_grads, "dp", scatter_dimension=0, tiled=True).astype(jnp.float32)
     d_normed = row_sum(
         times_trans(d_query, wq_all)
         + times_trans(d_forget, wf_all)
@@ -229,56 +253,24 @@
     grad_tokens = (
         d_resid + d_normed * attn_full * scale_one - resid_in * scale_one**3 * inner_one
     ).reshape(tokens.shape)
-    reduced_in = (
-        lax.psum_scatter(
-            grad_query.astype(jnp.bfloat16), "dp", scatter_dimension=0, tiled=True
-        ).astype(jnp.float32),
-        lax.psum_scatter(
-            grad_forget.astype(jnp.bfloat16), "dp", scatter_dimension=0, tiled=True
-        ).astype(jnp.float32),
-        lax.psum_scatter(
-            grad_value.astype(jnp.bfloat16), "dp", scatter_dimension=0, tiled=True
-        ).astype(jnp.float32),
-        lax.psum_scatter(
-            grad_outgate.astype(jnp.bfloat16), "dp", scatter_dimension=0, tiled=True
-        ).astype(jnp.float32),
-        lax.psum_scatter(
-            grad_gate.astype(jnp.bfloat16), "dp", scatter_dimension=0, tiled=True
-        ).astype(jnp.float32),
-        lax.psum_scatter(
-            grad_up.astype(jnp.bfloat16), "dp", scatter_dimension=0, tiled=True
-        ).astype(jnp.float32),
-    )
-    reduced_out = (
-        lax.psum_scatter(
-            grad_output.astype(jnp.bfloat16), "dp", scatter_dimension=1, tiled=True
-        ).astype(jnp.float32),
-        lax.psum_scatter(
-            grad_down.astype(jnp.bfloat16), "dp", scatter_dimension=1, tiled=True
-        ).astype(jnp.float32),
-    )
     floor_vector = lax.dynamic_update_slice(
         jnp.zeros((model_width,), jnp.float32), d_floor.reshape(-1), (part_index * local_width,)
     )
-    reduced_small = (
-        lax.psum_scatter(grad_attn, ("dp", "tensor"), scatter_dimension=0, tiled=True),
-        lax.psum_scatter(floor_vector, ("dp", "tensor"), scatter_dimension=0, tiled=True),
-        lax.psum_scatter(grad_mlp, ("dp", "tensor"), scatter_dimension=0, tiled=True),
-    )
+    reduced_small = small_sum(jnp.stack([grad_attn, floor_vector, grad_mlp]))
     return (
         layer_out,
         grad_tokens,
         reduced_small[0],
         reduced_small[1],
-        reduced_in[0],
-        reduced_in[1],
-        reduced_in[2],
-        reduced_in[3],
-        reduced_out[0],
+        attn_red[:, 0 * local_width : 1 * local_width],
+        attn_red[:, 1 * local_width : 2 * local_width],
+        attn_red[:, 2 * local_width : 3 * local_width],
+        attn_red[:, 3 * local_width : 4 * local_width],
+        attn_red[:, 4 * local_width : 5 * local_width].T,
         reduced_small[2],
-        reduced_in[4],
-        reduced_in[5],
-        reduced_out[1],
+        mlp_red[:, 0:hidden_width],
+        mlp_red[:, hidden_width : 2 * hidden_width],
+        mlp_red[:, 2 * hidden_width : 3 * hidden_width].T,
     )
 
 

time: 2650 us -> 1300 us (0.49)
  waiting for transfers between devices: 2000 us -> 552 us
  local copies, waits for them, and re-layouts: 54.2 us -> 130 us
  starting transfers between devices: 1.18 us -> 47.8 us
  blocking collectives: 135 us -> 103 us
    reduce_scatter x12 -> x0, waiting for transfers between devices: 1450 us -> none  [the longest x1 192 us: shards(): lax.psum_scatter(grad_down.astype(jnp.bfloat16), 'dp', scatter_dimension=...]
    all_gather x12 -> x2, waiting for transfers between devices: 546 us -> 96.4 us  [the longest x1 96.4 us: shards(): attn_all = lax.all_gather(attn_pack, 'dp', axis=0, tiled=True)]
    all_to_all x0 -> x8, waiting for transfers between devices: none -> 234 us  [the longest x2 151 us: row_sum(): got = lax.all_to_all(blocks, 'tensor', 0, 0, tiled=False)]
    unnamed x24 -> x6, waiting for transfers between devices: 5.63 us -> 222 us
    unnamed x2 -> x0, blocking collectives: 135 us -> none
    all_to_all x0 -> x2, blocking collectives: none -> 103 us  [row_sum(): got = lax.all_to_all(blocks, 'tensor', 0, 0, tiled=False)]
    all_to_all x0 -> x8, starting transfers between devices: none -> 47.4 us  [the longest x4 17.1 us: row_gather(): got = lax.all_to_all(spread, 'tensor', 0, 0, tiled=False)]
    unnamed x92 -> x118, local copies, waits for them, and re-layouts: 11.1 us -> 56.3 us
  transfers between devices with their start and end apart: 24 -> 12, of which waited for: 21 -> 9; matrix products, arithmetic and copies ran while one was open for 17% -> 23% of each run, Pallas kernels for 0% -> 0%
where the time goes in v1:
time: 1300 us; the launch traced here: 1290 us
  waiting for transfers between devices  552 us (42%)
  other arithmetic  280 us (22%)
  matrix products  161 us (12%)
  local copies, waits for them, and re-layouts  130 us (10%)
  blocking collectives  103 us (8%)
  starting transfers between devices  47.8 us (4%)
  between operations  14.8 us (1%)
    unnamed x6, waiting for transfers between devices  222 us
    all_to_all x2, waiting for transfers between devices, row_sum(): got = lax.all_to_all(blocks, 'tensor', 0, 0, tiled=False)  151 us
    all_to_all x2, blocking collectives, row_sum(): got = lax.all_to_all(blocks, 'tensor', 0, 0, tiled=False)  103 us
    dot_general x4, other arithmetic, block_step(): jnp.einsum('ihk,jhk,ijhk->ijh', query_block, key_b, decay, precision=lax....  102 us
    all_gather x1, waiting for transfers between devices, shards(): attn_all = lax.all_gather(attn_pack, 'dp', axis=0, tiled=True)  96.4 us
    all_to_all x4, waiting for transfers between devices, row_gather(): got = lax.all_to_all(spread, 'tensor', 0, 0, tiled=False)  64 us
    unnamed x118, local copies, waits for them, and re-layouts  56.3 us
    reduce_sum x2, other arithmetic, block_step(): log_gap = running_total[:, None] - running_total[None, :]  54.8 us
  transfers between devices with their start and end apart: 12, of which 9 were waited for; matrix products, arithmetic and copies ran while one was open for 23% of the time, Pallas kernels for 0%

profile of v1, /device:TPU:0, one launch (start us, length us, event | category | flops | bytes accessed | tf_op | source)
XLA Modules:
  0.0 1291.5 jit_solution(5244657009365066844)
XLA Ops:
  15.7 11.1 all-to-all-start
  28.6 10.2 all-to-all-done
  41.7 4.5 all-to-all-start.1
  47.0 96.4 %all-gather.3.cloned.1.call-done = bf16[2048,2560]{1,0:T(8,128)(2,1)} async-done(((bf16[64,2560]{1,0:T(8,128)(2,1)}), bf16[2048,2560]{1,0:T(8,128)(2,1)}) %all-gather.3.cloned.1.call-update) | async-done | bytes 10485776 | tf_op jit(solution)/shard_map/all_gather | solution.py:161
  143.4 5.4 slice_bitcast_fusion.2
  151.2 4.8 fusion.142
  157.6 4.0 copy.290
  161.6 3.5 convolution_bitcast_fusion.4
  166.2 3.9 copy.291
  170.2 4.5 convolution_bitcast_fusion.3
  174.7 140.9 %while.40 = (s32[]{:T(128)}, f32[4,4,128,128]{3,2,1,0:T(8,128)S(1)}, f32[2,4,64,4,128]{4,2,3,1,0:T(8,128)S(1)}, f32[2,4,4,128,128]{4,3,2,1,0:T(8,128)}, f32[2,4,...) while((s32[]{:T(128)}, ...), condition=%wide.region_3.4_spmd.clone, body=%wide.region_1.3_spmd.clone.sunk | while | flops 563977216 | bytes 88180056 | solution.py:86
  177.3 21.6 %exponential_select_fusion.2 = f32[4,64,64,4,128]{4,3,2,1,0:T(4,128)} fusion(f32[4,64,4,128]{3,2,1,0:T(4,128)S(1)} %fusion.238, pred[4,64,64]{2,1,0:T(8,128)(4,1)S(1)} %compare_and_fusion.4), kind=kLoop, calls=%fused_computation.76.clone.1 | loop fusion | flops 25165824 | bytes 34095104 | tf_op jit(solution)/shard_map/jvp(vmap())/while/body/eval_jaxpr/jit(_where)/select_n | solution.py:59
  200.9 36.4 %fusion.241 = f32[4,64,64,4]{1,2,3,0:T(8,128)S(1)} fusion(f32[4,64,64,4,128]{4,3,2,1,0:T(4,128)} %exponential_select_fusion.2, f32[4,4,128,64]{2,3,1,0:T(8,128)S(1)} %copy.466, f32[4,4,128,64]{2,3,1,0:T(8,128)S(1)} %copy.468), kind=kLoop, calls=%fused_computation.75.clone.1 | loop fusion | flops 25100288 | bytes 34865152 | tf_op jit(solution)/shard_map/jvp(vmap())/while/body/eval_jaxpr/ihk,jhk,ijhk->ijh/dot_general | solution.py:60
  247.5 21.6 %exponential_select_fusion.2 = f32[4,64,64,4,128]{4,3,2,1,0:T(4,128)} fusion(f32[4,64,4,128]{3,2,1,0:T(4,128)S(1)} %fusion.238, pred[4,64,64]{2,1,0:T(8,128)(4,1)S(1)} %compare_and_fusion.4), kind=kLoop, calls=%fused_computation.76.clone.1 | loop fusion | flops 25165824 | bytes 34095104 | tf_op jit(solution)/shard_map/jvp(vmap())/while/body/eval_jaxpr/jit(_where)/select_n | solution.py:59
  271.1 36.4 %fusion.241 = f32[4,64,64,4]{1,2,3,0:T(8,128)S(1)} fusion(f32[4,64,64,4,128]{4,3,2,1,0:T(4,128)} %exponential_select_fusion.2, f32[4,4,128,64]{2,3,1,0:T(8,128)S(1)} %copy.466, f32[4,4,128,64]{2,3,1,0:T(8,128)S(1)} %copy.468), kind=kLoop, calls=%fused_computation.75.clone.1 | loop fusion | flops 25100288 | bytes 34865152 | tf_op jit(solution)/shard_map/jvp(vmap())/while/body/eval_jaxpr/ihk,jhk,ijhk->ijh/dot_general | solution.py:60
  311.9 3.3 convolution_add_fusion.5
  316.3 4.9 fusion.131
  324.3 51.7 %all_to_all.50 = f32[4,128,2048]{2,1,0:T(8,128)} all-to-all(f32[4,128,2048]{2,1,0:T(8,128)S(1)} %bitcast.501), channel_id=1, replica_groups=mesh['dp'=32,'tensor'=4] {'tensor'}, dimensions={0} | all-to-all | bytes 8388608 | tf_op jit(solution)/shard_map/all_to_all | solution.py:111
  377.6 4.6 all-to-all-start.5
  385.4 22.6 %all-to-all-done.5 = bf16[4,128,2048]{2,1,0:T(8,128)(2,1)} async-done(((bf16[4,128,2048]{2,1,0:T(8,128)(2,1)}), bf16[4,128,2048]{2,1,0:T(8,128)(2,1)}, u32[]{:S(2)}, u32[]{:S(2)}) %all-to-all-start.5) | async-done | bytes 2097184 | tf_op jit(solution)/shard_map/all_to_all | solution.py:104
  409.5 4.4 all-to-all-start.3
  414.0 8.3 fusion.77
  422.3 17.5 %all-to-all-done.3 = bf16[4,128,2048]{2,1,0:T(8,128)(2,1)} async-done(((bf16[4,128,2048]{2,1,0:T(8,128)(2,1)}), bf16[4,128,2048]{2,1,0:T(8,128)(2,1)}, u32[]{:S(2)}, u32[]{:S(2)}) %all-to-all-start.3) | async-done | bytes 2097184 | tf_op jit(solution)/shard_map/all_to_all | solution.py:104
  439.7 8.4 fusion.71
  449.8 7.8 multiply_convert_fusion.1
  457.6 5.1 fusion.69
  462.7 5.3 fusion.80
  468.0 51.6 %all_to_all.51 = f32[4,128,2048]{2,1,0:T(8,128)} all-to-all(f32[4,128,2048]{2,1,0:T(8,128)S(1)} %bitcast.513), channel_id=1, replica_groups=mesh['dp'=32,'tensor'=4] {'tensor'}, dimensions={0} | all-to-all | bytes 8388608 | tf_op jit(solution)/shard_map/all_to_all | solution.py:111
  525.2 3.6 all-to-all-start.7
  530.6 23.9 %all-to-all-done.7 = bf16[4,128,2048]{2,1,0:T(8,128)(2,1)S(1)} async-done(((bf16[4,128,2048]{2,1,0:T(8,128)(2,1)}), bf16[4,128,2048]{2,1,0:T(8,128)(2,1)S(1)}, u32[]{:S(2)}, u32[]{:S(2)}) %all-to-all-start.7) | async-done | bytes 2097184 | tf_op jit(solution)/shard_map/all_to_all | solution.py:104
  554.4 5.7 fusion.133
  565.6 183.3 %while.41 = (s32[]{:T(128)}, f32[4,4,128,128]{3,2,1,0:T(8,128)}, bf16[2,4,64,4,128]{4,2,3,1,0:T(8,128)(2,1)}, f32[2,4,64,4,128]{4,3,2,1,0:T(4,128)}, f32[2,4,64,...) while((s32[]{:T(128)}, f32[4,4,128,128]{3,2,1,0:T(8,128)}, ...), condition=%wide.region_16.17_spmd.clone, body=%wide.region_9.16_spmd.clone.sunk | while | flops 1228907520 | bytes 80963376 | solution.py:86
  577.1 4.2 convolution_add_fusion.6
  585.8 14.8 %fusion.258 = f32[4,4,128,64]{2,3,1,0:T(8,128)} fusion(f32[4,4,128,64]{2,1,3,0:T(4,128)} %copy.479, f32[4,64,4,128]{3,1,2,0:T(8,128)} %copy-done.12, f32[4,64,4,128]{3,2,1,0:T(4,128)S(1)} %fusion.257, f32[4,64,64,4]{2,3,1,0:T(4,128)} %copy.480, pred[4,64,64]{2,1,0:T(8,128)(4,1)S(1)} %compare_and_fusion.5), kind=kLoop, calls=%fused_computation.3.clone.1 | loop fusion | flops 50200576 | bytes 2375680 | tf_op jit(solution)/shard_map/transpose(jvp(vmap()))/while/body/eval_jaxpr/checkpoint/ihk,jhk,ijhk->ijh/dot_general | solution.py:60
  600.6 14.3 %fusion.259 = f32[4,4,128,64]{2,1,3,0:T(4,128)} fusion(f32[4,4,128,64]{2,3,1,0:T(8,128)S(1)} %bitcast.496, f32[4,64,4,128]{3,1,2,0:T(8,128)S(1)} %copy-done.13, f32[4,64,4,128]{3,2,1,0:T(4,128)S(1)} %fusion.257, f32[4,64,64,4]{2,3,1,0:T(4,128)S(1)} %copy-done.16, pred[4,64,64]{2,1,0:T(8,128)(4,1)S(1)} %compare_and_fusion.5), kind=kLoop, calls=%fused_computation.11.clone.1 | loop fusion | flops 50200576 | bytes 2375680 | tf_op jit(solution)/shard_map/transpose(jvp(vmap()))/while
  618.0 4.6 bitcast_dynamic-update-slice_fusion.7
  622.6 27.4 %fusion.260 = (f32[4,64,4,128]{3,1,2,0:T(8,128)S(1)}, f32[4,64,4,128]{3,2,1,0:T(4,128)}, f32[4,64,64,4]{2,3,1,0:T(4,128)S(1)}) fusion(f32[4,4,128,64]{2,3,1,0:T(8,128)S(1)} %bitcast.497, f32[4,4,128,64]{2,1,3,0:T(4,128)S(1)} %copy-done.15, f32[4,64,4,128]{3,1,2,0:T(8,128)S(1)} %copy-done.14, f32[4,64,4,128]{3,2,1,0:T(4,128)S(1)} %fusion.257, ...), kind=kLoop, calls=%fused_computation.16.clone.1 | loop fusion | flops 100335616 | bytes 3686400 | tf_op jit(solution)/shard_map/transpose(jvp(vmap()))/while/body/eval_jaxpr/checkpoint/reduce_sum | solution.py:58
  669.1 4.2 convolution_add_fusion.6
  677.8 14.8 %fusion.258 = f32[4,4,128,64]{2,3,1,0:T(8,128)} fusion(f32[4,4,128,64]{2,1,3,0:T(4,128)} %copy.479, f32[4,64,4,128]{3,1,2,0:T(8,128)} %copy-done.12, f32[4,64,4,128]{3,2,1,0:T(4,128)S(1)} %fusion.257, f32[4,64,64,4]{2,3,1,0:T(4,128)} %copy.480, pred[4,64,64]{2,1,0:T(8,128)(4,1)S(1)} %compare_and_fusion.5), kind=kLoop, calls=%fused_computation.3.clone.1 | loop fusion | flops 50200576 | bytes 2375680 | tf_op jit(solution)/shard_map/transpose(jvp(vmap()))/while/body/eval_jaxpr/checkpoint/ihk,jhk,ijhk->ijh/dot_general | solution.py:60
  692.6 14.3 %fusion.259 = f32[4,4,128,64]{2,1,3,0:T(4,128)} fusion(f32[4,4,128,64]{2,3,1,0:T(8,128)S(1)} %bitcast.496, f32[4,64,4,128]{3,1,2,0:T(8,128)S(1)} %copy-done.13, f32[4,64,4,128]{3,2,1,0:T(4,128)S(1)} %fusion.257, f32[4,64,64,4]{2,3,1,0:T(4,128)S(1)} %copy-done.16, pred[4,64,64]{2,1,0:T(8,128)(4,1)S(1)} %compare_and_fusion.5), kind=kLoop, calls=%fused_computation.11.clone.1 | loop fusion | flops 50200576 | bytes 2375680 | tf_op jit(solution)/shard_map/transpose(jvp(vmap()))/while
  709.9 4.7 bitcast_dynamic-update-slice_fusion.7
  714.6 27.4 %fusion.260 = (f32[4,64,4,128]{3,1,2,0:T(8,128)S(1)}, f32[4,64,4,128]{3,2,1,0:T(4,128)}, f32[4,64,64,4]{2,3,1,0:T(4,128)S(1)}) fusion(f32[4,4,128,64]{2,3,1,0:T(8,128)S(1)} %bitcast.497, f32[4,4,128,64]{2,1,3,0:T(4,128)S(1)} %copy-done.15, f32[4,64,4,128]{3,1,2,0:T(8,128)S(1)} %copy-done.14, f32[4,64,4,128]{3,2,1,0:T(4,128)S(1)} %fusion.257, ...), kind=kLoop, calls=%fused_computation.16.clone.1 | loop fusion | flops 100335616 | bytes 3686400 | tf_op jit(solution)/shard_map/transpose(jvp(vmap()))/while/body/eval_jaxpr/checkpoint/reduce_sum | solution.py:58
  754.5 4.2 fusion.87
  758.7 4.2 fusion.86
  762.9 4.3 fusion.85
  767.2 4.4 fusion.84
  774.3 13.8 %copy.349 = bf16[2048,2560]{1,0:T(8,128)(2,1)} copy(bf16[2048,2560]{0,1:T(8,128)(2,1)} %fusion.83) | data formatting | bytes 20971520
  788.4 5.3 convolution_convert_fusion.1
  793.7 5.0 convolution_convert_fusion.2
  798.7 4.8 fusion.64
  803.5 7.7 pad_maximum_fusion
  811.2 21.2 %copy.351 = bf16[2048,4224]{1,0:T(8,128)(2,1)} copy(bf16[2048,4224]{0,1:T(8,128)(2,1)} %pad_maximum_fusion) | data formatting | bytes 34603008
  832.4 8.7 fusion.67
  841.1 5.0 all-to-all-start.4
  854.8 5.0 add_add_fusion
  859.8 100.0 %all-to-all-done.4 = f32[4,128,2048]{2,1,0:T(8,128)} async-done(((f32[4,128,2048]{2,1,0:T(8,128)}), f32[4,128,2048]{2,1,0:T(8,128)}, u32[]{:S(2)}, u32[]{:S(2)}) %all-to-all-start.4) | async-done | bytes 4194336 | tf_op jit(solution)/shard_map/all_to_all | solution.py:111
  959.7 5.0 all-to-all-start.8
  964.9 3.6 reduce_sum.223
  970.1 51.1 %all-to-all-done.8 = f32[4,128,2048]{2,1,0:T(8,128)} async-done(((f32[4,128,2048]{2,1,0:T(8,128)}), f32[4,128,2048]{2,1,0:T(8,128)}, u32[]{:S(2)}, u32[]{:S(2)}) %all-to-all-start.8) | async-done | bytes 4194336 | tf_op jit(solution)/shard_map/all_to_all | solution.py:111
  1021.2 3.6 reduce_sum.228
  1027.4 9.2 all-to-all-start.9
  1036.6 3.5 fusion.128
  1040.1 8.6 all-to-all-done.9
  1054.7 221.6 %reduce-scatter.9.cloned.1.call-done = bf16[64,4224]{1,0:T(8,128)(2,1)} async-done(((bf16[2048,4224]{1,0:T(8,128)(2,1)}), bf16[64,4224]{1,0:T(8,128)(2,1)}) %reduce-scatter.9.cloned.1.call-update) | async-done | bytes 540688
  (361 shorter events, 151.8 us)
Async XLA Ops:
  7.2 32.8 %copy-start.7 = (bf16[1,1,128,2048]{3,2,1,0:T(8,128)(2,1)S(1)}, bf16[1,1,128,2048]{3,2,1,0:T(8,128)(2,1)}, u32[]{:S(2)}) copy-start(bf16[1,1,128,2048]{3,2,1,0:T(8,128)(2,1)} %param.18) | copy-start | bytes 1572868
  7.2 136.2 %all-gather.3.cloned.1.call-start = ((), (), s32[]{:S(2)}) async-start(), calls=%async_computation.12 | async-start | bytes 10813440 | tf_op jit(solution)/shard_map/all_gather | solution.py:161
  12.3 401.7 %all-gather.5.cloned.1.call-start = ((), (), s32[]{:S(2)}) async-start(), calls=%async_computation.13 | async-start | bytes 17842176 | tf_op jit(solution)/shard_map/all_gather | solution.py:162
  15.7 23.1 %all-to-all-start = ((f32[128,3,16]{2,1,0:T(4,128)}), f32[128,3,16]{2,1,0:T(4,128)S(1)}, u32[]{:S(2)}, u32[]{:S(2)}) async-start(f32[128,3,16]{2,1,0:T(4,128)} %broadcast_in_dim.179), calls=%async_computation | async-start | bytes 524288 | tf_op jit(solution)/shard_map/all_to_all | solution.py:118
  28.1 18.1 %copy-start.52 = (s32[1,4,128]{2,1,0:T(4,128)S(1)}, s32[1,4,128]{2,1,0:T(4,128)}, u32[]{:S(2)}) copy-start(s32[1,4,128]{2,1,0:T(4,128)} %param.19) | copy-start | bytes 6148
  28.6 13.1 %copy-start.50 = (f32[128]{0:T(128)}, f32[128]{0:T(128)S(1)}, u32[]{:S(2)}) copy-start(f32[128]{0:T(128)S(1)} %get-tuple-element.863) | copy-start | bytes 1540
  41.7 109.5 %all-to-all-start.1 = ((bf16[4,128,2048]{2,1,0:T(8,128)(2,1)}), bf16[4,128,2048]{2,1,0:T(8,128)(2,1)}, u32[]{:S(2)}, u32[]{:S(2)}) async-start(bf16[4,128,2048]{2,1,0:T(8,128)(2,1)} %broadcast_in_dim.180), calls=%async_computation.1 | async-start | bytes 4194304 | tf_op jit(solution)/shard_map/all_to_all | solution.py:104
  47.0 104.2 %copy-start.44 = (f32[4,128]{1,0:T(4,128)}, f32[4,128]{1,0:T(4,128)S(1)}, u32[]{:S(2)}) copy-start(f32[4,128]{1,0:T(4,128)S(1)} %get-tuple-element.828) | copy-start | bytes 6148
  47.0 104.2 %copy-start.46 = (f32[4,128]{1,0:T(4,128)}, f32[4,128]{1,0:T(4,128)S(1)}, u32[]{:S(2)}) copy-start(f32[4,128]{1,0:T(4,128)S(1)} %get-tuple-element.829) | copy-start | bytes 6148
  315.6 5.6 copy-start.18
  316.3 4.9 copy-start.35
  324.3 51.7 %copy-start.21 = (bf16[1,1,128,2048]{3,2,1,0:T(8,128)(2,1)S(1)}, bf16[1,1,128,2048]{3,2,1,0:T(8,128)(2,1)}, u32[]{:S(2)}) copy-start(bf16[1,1,128,2048]{3,2,1,0:T(8,128)(2,1)} %param.31) | copy-start | bytes 1572868
  376.1 6.2 copy-start.38
  377.6 7.3 copy-start.8
  377.6 30.3 %all-to-all-start.5 = ((bf16[4,128,2048]{2,1,0:T(8,128)(2,1)}), bf16[4,128,2048]{2,1,0:T(8,128)(2,1)}, u32[]{:S(2)}, u32[]{:S(2)}) async-start(bf16[4,128,2048]{2,1,0:T(8,128)(2,1)} %broadcast_in_dim.183), calls=%async_computation.5 | async-start | bytes 4194304 | tf_op jit(solution)/shard_map/all_to_all | solution.py:104
  382.3 140.8 %copy-start.39 = (f32[2048]{0:T(1024)}, f32[2048]{0:T(1024)S(1)}, u32[]{:S(2)}) copy-start(f32[2048]{0:T(1024)S(1)} %mul.610) | copy-start | bytes 24580
  384.9 138.2 %copy-start.5 = (f32[128,2048]{1,0:T(8,128)}, f32[128,2048]{1,0:T(8,128)S(1)}, u32[]{:S(2)}) copy-start(f32[128,2048]{1,0:T(8,128)S(1)} %reduce_sum.220) | copy-start | bytes 3145732
  385.2 138.0 %copy-start.48 = (f32[128]{0:T(128)}, f32[128]{0:T(128)S(1)}, u32[]{:S(2)}) copy-start(f32[128]{0:T(128)S(1)} %get-tuple-element.865) | copy-start | bytes 1540
  385.2 138.0 %copy-start.53 = (f32[128]{0:T(128)}, f32[128]{0:T(128)S(1)}, u32[]{:S(2)}) copy-start(f32[128]{0:T(128)S(1)} %get-tuple-element.864) | copy-start | bytes 1540
  409.5 30.2 %all-to-all-start.3 = ((bf16[4,128,2048]{2,1,0:T(8,128)(2,1)}), bf16[4,128,2048]{2,1,0:T(8,128)(2,1)}, u32[]{:S(2)}, u32[]{:S(2)}) async-start(bf16[4,128,2048]{2,1,0:T(8,128)(2,1)} %broadcast_in_dim.181), calls=%async_computation.3 | async-start | bytes 4194304 | tf_op jit(solution)/shard_map/all_to_all | solution.py:104
  439.7 9.1 copy-start.58
  439.7 10.1 copy-start.63
  457.6 5.1 copy-start.62
  457.6 5.1 copy-start.59
  525.2 29.3 %all-to-all-start.7 = ((bf16[4,128,2048]{2,1,0:T(8,128)(2,1)}), bf16[4,128,2048]{2,1,0:T(8,128)(2,1)S(1)}, u32[]{:S(2)}, u32[]{:S(2)}) async-start(bf16[4,128,2048]{2,1,0:T(8,128)(2,1)} %broadcast_in_dim.184), calls=%async_computation.7 | async-start | bytes 4194304 | tf_op jit(solution)/shard_map/all_to_all | solution.py:104
  528.8 520.6 %reduce-scatter.7.cloned.1.call-start = ((), (), s32[]{:S(2)}) async-start(), calls=%async_computation.14 | async-start | bytes 10813440
  554.4 5.7 copy-start.27
  554.4 7.3 copy-start.19
  560.1 5.4 copy-start.32
  577.1 6.3 copy-start.3
  585.8 14.8 %copy-start = (f32[4,64,4,128]{3,1,2,0:T(8,128)S(1)}, f32[4,64,4,128]{3,1,2,0:T(8,128)}, u32[]{:S(2)}) copy-start(f32[4,64,4,128]{3,1,2,0:T(8,128)} %dynamic-slice_bitcast_fusion.20) | copy-start | bytes 1572868 | tf_op jit(solution)/shard_map/transpose(jvp(vmap()))/while
  585.8 14.8 %copy-start.13 = (f32[4,64,4,128]{3,1,2,0:T(8,128)S(1)}, f32[4,64,4,128]{3,1,2,0:T(8,128)}, u32[]{:S(2)}) copy-start(f32[4,64,4,128]{3,1,2,0:T(8,128)} %copy-done.12) | copy-start | bytes 1572868 | tf_op jit(solution)/shard_map/transpose(jvp(vmap()))/while
  585.8 14.8 %copy-start.16 = (f32[4,64,64,4]{2,3,1,0:T(4,128)S(1)}, f32[4,64,64,4]{2,3,1,0:T(4,128)}, u32[]{:S(2)}) copy-start(f32[4,64,64,4]{2,3,1,0:T(4,128)} %copy.480) | copy-start | bytes 786436 | tf_op jit(solution)/shard_map/transpose(jvp(vmap()))/while
  622.6 28.1 %copy-start.2 = (f32[4,64,4,128]{3,1,2,0:T(8,128)S(1)}, f32[4,64,4,128]{3,1,2,0:T(8,128)}, u32[]{:S(2)}) copy-start(f32[4,64,4,128]{3,1,2,0:T(8,128)} %dynamic-slice_bitcast_fusion.18) | copy-start | bytes 1572868 | tf_op jit(solution)/shard_map/transpose(jvp(vmap()))/while
  622.6 28.1 %copy-start.4 = (f32[4,64,4,128]{3,1,2,0:T(8,128)S(1)}, f32[4,64,4,128]{3,1,2,0:T(8,128)}, u32[]{:S(2)}) copy-start(f32[4,64,4,128]{3,1,2,0:T(8,128)} %convolution_bitcast_fusion.10) | copy-start | bytes 1572868 | tf_op jit(solution)/shard_map/transpose(jvp(vmap()))/while
  669.1 6.3 copy-start.3
  677.7 14.8 %copy-start = (f32[4,64,4,128]{3,1,2,0:T(8,128)S(1)}, f32[4,64,4,128]{3,1,2,0:T(8,128)}, u32[]{:S(2)}) copy-start(f32[4,64,4,128]{3,1,2,0:T(8,128)} %dynamic-slice_bitcast_fusion.20) | copy-start | bytes 1572868 | tf_op jit(solution)/shard_map/transpose(jvp(vmap()))/while
  677.7 14.8 %copy-start.13 = (f32[4,64,4,128]{3,1,2,0:T(8,128)S(1)}, f32[4,64,4,128]{3,1,2,0:T(8,128)}, u32[]{:S(2)}) copy-start(f32[4,64,4,128]{3,1,2,0:T(8,128)} %copy-done.12) | copy-start | bytes 1572868 | tf_op jit(solution)/shard_map/transpose(jvp(vmap()))/while
  677.7 14.8 %copy-start.16 = (f32[4,64,64,4]{2,3,1,0:T(4,128)S(1)}, f32[4,64,64,4]{2,3,1,0:T(4,128)}, u32[]{:S(2)}) copy-start(f32[4,64,64,4]{2,3,1,0:T(4,128)} %copy.480) | copy-start | bytes 786436 | tf_op jit(solution)/shard_map/transpose(jvp(vmap()))/while
  709.9 4.7 copy-start.1
  709.9 4.7 copy-start.14
  709.9 4.7 copy-start.15
  709.9 4.7 copy-start.17
  714.6 28.1 %copy-start.2 = (f32[4,64,4,128]{3,1,2,0:T(8,128)S(1)}, f32[4,64,4,128]{3,1,2,0:T(8,128)}, u32[]{:S(2)}) copy-start(f32[4,64,4,128]{3,1,2,0:T(8,128)} %dynamic-slice_bitcast_fusion.18) | copy-start | bytes 1572868 | tf_op jit(solution)/shard_map/transpose(jvp(vmap()))/while
  714.6 28.1 %copy-start.4 = (f32[4,64,4,128]{3,1,2,0:T(8,128)S(1)}, f32[4,64,4,128]{3,1,2,0:T(8,128)}, u32[]{:S(2)}) copy-start(f32[4,64,4,128]{3,1,2,0:T(8,128)} %convolution_bitcast_fusion.10) | copy-start | bytes 1572868 | tf_op jit(solution)/shard_map/transpose(jvp(vmap()))/while
  748.8 4.7 copy-start.26
  788.1 488.2 %reduce-scatter.9.cloned.1.call-start = ((), (), s32[]{:S(2)}) async-start(), calls=%async_computation.15 | async-start | bytes 17842176
  788.3 5.3 copy-start.60
  793.7 5.0 copy-start.61
  841.1 118.7 %all-to-all-start.4 = ((f32[4,128,2048]{2,1,0:T(8,128)}), f32[4,128,2048]{2,1,0:T(8,128)}, u32[]{:S(2)}, u32[]{:S(2)}) async-start(f32[4,128,2048]{2,1,0:T(8,128)} %bitcast.512), calls=%async_computation.4 | async-start | bytes 8388608 | tf_op jit(solution)/shard_map/all_to_all | solution.py:111
  959.7 5.0 copy-start.43
  959.7 61.5 %all-to-all-start.8 = ((f32[4,128,2048]{2,1,0:T(8,128)}), f32[4,128,2048]{2,1,0:T(8,128)}, u32[]{:S(2)}, u32[]{:S(2)}) async-start(f32[4,128,2048]{2,1,0:T(8,128)} %bitcast.502), calls=%async_computation.8 | async-start | bytes 8388608 | tf_op jit(solution)/shard_map/all_to_all | solution.py:111
  964.8 60.0 %copy-start.9 = (bf16[1,1,128,2048]{3,2,1,0:T(8,128)(2,1)S(1)}, bf16[1,1,128,2048]{3,2,1,0:T(8,128)(2,1)}, u32[]{:S(2)}) copy-start(bf16[1,1,128,2048]{3,2,1,0:T(8,128)(2,1)} %param.18) | copy-start | bytes 1572868
  964.9 60.0 %copy-start.42 = (f32[2048]{0:T(1024)S(1)}, f32[2048]{0:T(1024)}, u32[]{:S(2)}) copy-start(f32[2048]{0:T(1024)} %copy-done.41) | copy-start | bytes 24580
  964.9 60.0 %copy-start.51 = (f32[128]{0:T(128)S(1)}, f32[128]{0:T(128)}, u32[]{:S(2)}) copy-start(f32[128]{0:T(128)} %copy-done.50) | copy-start | bytes 1540
  968.5 68.0 %copy-start.6 = (f32[128,2048]{1,0:T(8,128)S(1)}, f32[128,2048]{1,0:T(8,128)}, u32[]{:S(2)}) copy-start(f32[128,2048]{1,0:T(8,128)} %copy-done.5) | copy-start | bytes 3145732
  968.5 68.0 %copy-start.11 = (f32[128,2048]{1,0:T(8,128)S(1)}, f32[128,2048]{1,0:T(8,128)}, u32[]{:S(2)}) copy-start(f32[128,2048]{1,0:T(8,128)} %copy-done.10) | copy-start | bytes 3145732
  968.5 68.0 %copy-start.22 = (bf16[1,1,128,2048]{3,2,1,0:T(8,128)(2,1)S(1)}, bf16[1,1,128,2048]{3,2,1,0:T(8,128)(2,1)}, u32[]{:S(2)}) copy-start(bf16[1,1,128,2048]{3,2,1,0:T(8,128)(2,1)} %param.31) | copy-start | bytes 1572868
  968.6 68.0 %copy-start.40 = (f32[2048]{0:T(1024)S(1)}, f32[2048]{0:T(1024)}, u32[]{:S(2)}) copy-start(f32[2048]{0:T(1024)} %copy-done.39) | copy-start | bytes 24580
  968.6 68.0 %copy-start.49 = (f32[128]{0:T(128)S(1)}, f32[128]{0:T(128)}, u32[]{:S(2)}) copy-start(f32[128]{0:T(128)} %copy-done.48) | copy-start | bytes 1540
  968.6 68.0 %copy-start.54 = (f32[128]{0:T(128)S(1)}, f32[128]{0:T(128)}, u32[]{:S(2)}) copy-start(f32[128]{0:T(128)} %copy-done.53) | copy-start | bytes 1540
  968.6 68.0 %copy-start.56 = (f32[128]{0:T(128)S(1)}, f32[128]{0:T(128)}, u32[]{:S(2)}) copy-start(f32[128]{0:T(128)} %copy-done.55) | copy-start | bytes 1540
  968.6 68.0 %copy-start.57 = (f32[128]{0:T(128)S(1)}, f32[128]{0:T(128)}, u32[]{:S(2)}) copy-start(f32[128]{0:T(128)} %get-tuple-element.862) | copy-start | bytes 1540
  1027.4 21.3 %all-to-all-start.9 = ((f32[128,3,16]{2,1,0:T(4,128)}), f32[128,3,16]{2,1,0:T(4,128)S(1)}, u32[]{:S(2)}, u32[]{:S(2)}) async-start(f32[128,3,16]{2,1,0:T(4,128)} %copy.307), calls=%async_computation.9 | async-start | bytes 524288 | tf_op jit(solution)/shard_map/all_to_all | solution.py:125
  (27 other events, 77.6 us)
Sparse Core Ops, SparseCore 0:
  12.4 130.9 all-gather.2
  147.0 156.2 all-gather.4
  788.2 207.1 reduce-scatter.6
  1001.1 275.1 reduce-scatter.8

commit v2 on v1

--- a/solution.py
+++ b/solution.py
@@ -4,7 +4,7 @@
 from jax.sharding import PartitionSpec as P
 
 HK = 128
-BLOCK = 64
+HIGHEST = lax.Precision.HIGHEST
 
 
 epsilon = 1e-06
@@ -35,67 +35,24 @@
     )
 
 
-def recurrence(query, forget_raw, value, floor_vec, doc_row):
-    length, heads_n, chan = query.shape
+def recurrence(query, forget_raw, value, floor_vec, doc_rows):
+    length = query.shape[1]
     forget = floor_vec + (1.0 - floor_vec) * jax.nn.sigmoid(forget_raw)
     log_forget = jnp.log(forget)
     keyed = 1.0 - forget
-    block_count = length // BLOCK
-
-    def split_blocks(arr):
-        return arr.reshape(block_count, BLOCK, heads_n, chan)
-
-    doc_blocks = doc_row.reshape(block_count, BLOCK)
-    before = jnp.concatenate([jnp.full((1,), -1, jnp.int32), doc_blocks[:-1, -1]])
-    position = jnp.arange(BLOCK)
-    causal = position[:, None] >= position[None, :]
-
-    @jax.checkpoint
-    def block_step(recurrent_state, pieces):
-        query_block, log_b, key_b, value_block, doc_b, prev_doc = pieces
-        running_total = jnp.cumsum(log_b, axis=0)
-        same_doc = (causal & (doc_b[:, None] == doc_b[None, :]))[:, :, None, None]
-        log_gap = running_total[:, None] - running_total[None, :]
-        decay = jnp.where(same_doc, jnp.exp(jnp.where(same_doc, log_gap, 0.0)), 0.0)
-        scores = jnp.einsum(
-            "ihk,jhk,ijhk->ijh", query_block, key_b, decay, precision=lax.Precision.HIGHEST
-        )
-        intra = jnp.einsum("ijh,jhv->ihv", scores, value_block, precision=lax.Precision.HIGHEST)
-        carried_over = (doc_b == prev_doc).astype(jnp.float32)[:, None, None]
-        across_blocks = (
-            jnp.einsum(
-                "bma,maf->bmf",
-                query_block * jnp.exp(running_total),
-                recurrent_state,
-                precision=lax.Precision.HIGHEST,
-            )
-            * carried_over
-        )
-        block_finish = running_total[-1]
-        end_flag = (doc_b == doc_b[-1]).astype(jnp.float32)[:, None, None]
-        weighted_values = key_b * jnp.exp(block_finish[None] - running_total) * end_flag
-        carry_marker = (doc_b[-1] == prev_doc).astype(jnp.float32)
-        recurrent_state = recurrent_state * (
-            jnp.exp(block_finish)[:, :, None] * carry_marker
-        ) + jnp.einsum(
-            "dmf,dmb->mfb", weighted_values, value_block, precision=lax.Precision.HIGHEST
-        )
-        return (recurrent_state, intra + across_blocks)
-
-    start_state = jnp.zeros((heads_n, chan, chan), jnp.float32)
-    final_state, results = lax.scan(
-        block_step,
-        start_state,
-        (
-            split_blocks(query),
-            split_blocks(log_forget),
-            split_blocks(keyed),
-            split_blocks(value),
-            doc_blocks,
-            before,
-        ),
-    )
-    return results.reshape(length, heads_n, chan)
+    position = jnp.arange(length)
+    same_doc = doc_rows[:, :, None] == doc_rows[:, None, :]
+    causal = same_doc & (position[:, None] >= position[None, :])
+    starts = jnp.concatenate(
+        [jnp.zeros_like(doc_rows[:, :1], dtype=bool), doc_rows[:, 1:] == doc_rows[:, :-1]], axis=1
+    )
+    summing = (causal & starts[:, None, :]).astype(jnp.float32)
+    running = jnp.einsum("rij,rjhk->rihk", summing, log_forget, precision=HIGHEST)
+    query_t = query * jnp.exp(running)
+    key_t = keyed * jnp.exp(-running)
+    scores = jnp.einsum("rihk,rjhk->rhij", query_t, key_t, precision=HIGHEST)
+    scores = jnp.where(causal[:, None], scores, 0.0)
+    return jnp.einsum("rhij,rjhv->rihv", scores, value, precision=HIGHEST)
 
 
 def row_gather(values):
@@ -180,7 +137,7 @@
         def shaped(arr):
             return arr.reshape(row_count, -1, local_heads, HK)
 
-        mixed_rows = jax.vmap(recurrence, in_axes=(0, 0, 0, None, 0))(
+        mixed_rows = recurrence(
             shaped(query_in), shaped(forget_in), shaped(value_in), floor_in, doc_all
         )
         return mixed_rows.reshape(query_in.shape[0], local_width)

time: 1300 us -> 1040 us (0.80)
  other arithmetic: 280 us -> 35.6 us
  blocking collectives: 103 us -> 150 us
  local copies, waits for them, and re-layouts: 130 us -> 92 us
  matrix products: 161 us -> 138 us
    dot_general x4 -> x0, other arithmetic: 102 us -> none  [block_step(): jnp.einsum('ihk,jhk,ijhk->ijh', query_block, key_b, decay, precision=lax....]
    reduce_sum x7 -> x0, other arithmetic: 56.2 us -> none  [the longest x2 54.8 us: block_step(): log_gap = running_total[:, None] - running_total[None, :]]
    select_n x2 -> x0, other arithmetic: 43.2 us -> none  [block_step(): decay = jnp.where(same_doc, jnp.exp(jnp.where(same_doc, log_gap, 0.0)), 0.0)]
    all_gather x1, waiting for transfers between devices: 0.02 us -> 30.7 us  [shards(): mlp_all = lax.all_gather(mlp_pack, 'dp', axis=0, tiled=True)]
    while x2 -> x0, other arithmetic: 28.6 us -> none
    all_to_all x0 -> x1, blocking collectives: none -> 28.3 us  [row_gather(): got = lax.all_to_all(spread, 'tensor', 0, 0, tiled=False)]
    dot_general x18 -> x8, matrix products: 42.7 us -> 22 us  [the longest x3 8.43 us: recurrence(): return jnp.einsum('rhij,rjhv->rihv', scores, value, precision=HIGHEST)]
    all_to_all x4 -> x3, waiting for transfers between devices: 64 us -> 44.7 us  [row_gather(): got = lax.all_to_all(spread, 'tensor', 0, 0, tiled=False)]
  transfers between devices with their start and end apart: 12 -> 11, of which waited for: 9 -> 8; matrix products, arithmetic and copies ran while one was open for 23% -> 15% of each run, Pallas kernels for 0% -> 0%
where the time goes in v2:
time: 1040 us
  waiting for transfers between devices  564 us (54%)
  blocking collectives  150 us (14%)
  matrix products  138 us (13%)
  local copies, waits for them, and re-layouts  92 us (9%)
  starting transfers between devices  44.4 us (4%)
  other arithmetic  35.6 us (3%)
  between operations  14.6 us (1%)
    unnamed x6, waiting for transfers between devices  222 us
    all_to_all x2, waiting for transfers between devices, row_sum(): got = lax.all_to_all(blocks, 'tensor', 0, 0, tiled=False)  150 us
    all_to_all x2, blocking collectives, row_sum(): got = lax.all_to_all(blocks, 'tensor', 0, 0, tiled=False)  122 us
    all_gather x1, waiting for transfers between devices, shards(): attn_all = lax.all_gather(attn_pack, 'dp', axis=0, tiled=True)  96.8 us
    unnamed x94, local copies, waits for them, and re-layouts  52.3 us
    all_to_all x3, waiting for transfers between devices, row_gather(): got = lax.all_to_all(spread, 'tensor', 0, 0, tiled=False)  44.7 us
    dot_general x8, matrix products, matmul_plain(): return jnp.dot(left, right, preferred_element_type=jnp.float32)  44.2 us
    dot_general x8, matrix products, times_trans(): lax.dot_general(left, right, (((1,), (1,)), ((), ())), preferred_element_...  36 us
  transfers between devices with their start and end apart: 11, of which 8 were waited for; matrix products, arithmetic and copies ran while one was open for 15% of the time, Pallas kernels for 0%

profile of v2, /device:TPU:0, one launch (start us, length us, event | category | flops | bytes accessed | tf_op | source)
XLA Modules:
  0.0 1038.4 jit_solution(17702758190825516779)
XLA Ops:
  15.7 11.1 %all-to-all-start = ((f32[128,3,16]{2,1,0:T(4,128)}), f32[128,3,16]{2,1,0:T(4,128)S(1)}, u32[]{:S(2)}, u32[]{:S(2)}) async-start(f32[128,3,16]{2,1,0:T(4,128)} %broadcast_in_dim.27), calls=%async_computation | async-start | bytes 524288 | tf_op jit(solution)/shard_map/all_to_all | solution.py:75
  27.6 11.2 %all-to-all-done = f32[128,3,16]{2,1,0:T(4,128)S(1)} async-done(((f32[128,3,16]{2,1,0:T(4,128)}), f32[128,3,16]{2,1,0:T(4,128)S(1)}, u32[]{:S(2)}, u32[]{:S(2)}) %all-to-all-start) | async-done | bytes 24608 | tf_op jit(solution)/shard_map/all_to_all | solution.py:75
  41.3 4.7 all-to-all-start.1
  46.7 96.8 %all-gather.3.cloned.1.call-done = bf16[2048,2560]{1,0:T(8,128)(2,1)} async-done(((bf16[64,2560]{1,0:T(8,128)(2,1)}), bf16[2048,2560]{1,0:T(8,128)(2,1)}) %all-gather.3.cloned.1.call-update) | async-done | bytes 10485776 | tf_op jit(solution)/shard_map/all_gather | solution.py:118
  143.5 5.3 slice_bitcast_fusion
  148.8 4.0 copy.96
  152.8 4.0 copy.95
  156.8 2.5 copy.93
  159.3 3.8 fusion.59
  164.0 2.9 fusion.27
  167.0 2.5 convolution_select_fusion.1
  169.5 3.3 fusion.29
  173.7 2.9 convolution_bitcast_fusion.2
  176.6 2.6 copy.99
  179.2 4.8 fusion.73
  184.1 3.1 fusion.33
  187.2 70.3 %all_to_all.50 = f32[4,128,2048]{2,1,0:T(8,128)} all-to-all(f32[4,128,2048]{2,1,0:T(8,128)S(1)} %bitcast.225), channel_id=1, replica_groups=mesh['dp'=32,'tensor'=4] {'tensor'}, dimensions={0} | all-to-all | bytes 8388608 | tf_op jit(solution)/shard_map/all_to_all | solution.py:68
  259.1 4.4 all-to-all-start.5
  263.6 2.6 reduce_sum.134
  267.4 44.7 %all-to-all-done.5 = bf16[4,128,2048]{2,1,0:T(8,128)(2,1)} async-done(((bf16[4,128,2048]{2,1,0:T(8,128)(2,1)}), bf16[4,128,2048]{2,1,0:T(8,128)(2,1)}, u32[]{:S(2)}, u32[]{:S(2)}) %all-to-all-start.5) | async-done | bytes 2097184 | tf_op jit(solution)/shard_map/all_to_all | solution.py:61
  312.1 2.6 broadcast_in_dim.31
  314.7 4.5 all-to-all-start.3
  319.2 30.7 %all-gather.5.cloned.1.call-done = bf16[2048,4224]{1,0:T(8,128)(2,1)} async-done(((bf16[64,4224]{1,0:T(8,128)(2,1)}), bf16[2048,4224]{1,0:T(8,128)(2,1)}) %all-gather.5.cloned.1.call-update) | async-done | bytes 17301520 | tf_op jit(solution)/shard_map/all_gather | solution.py:119
  350.0 8.2 fusion.13
  358.2 8.4 fusion.7
  368.3 7.7 multiply_convert_fusion.1
  376.0 5.0 fusion.5
  381.1 5.3 fusion.16
  386.4 51.6 %all_to_all.51 = f32[4,128,2048]{2,1,0:T(8,128)} all-to-all(f32[4,128,2048]{2,1,0:T(8,128)S(1)} %bitcast.229), channel_id=1, replica_groups=mesh['dp'=32,'tensor'=4] {'tensor'}, dimensions={0} | all-to-all | bytes 8388608 | tf_op jit(solution)/shard_map/all_to_all | solution.py:68
  438.0 3.6 reduce_sum.139
  444.0 28.3 %all_to_all.52 = bf16[4,128,2048]{2,1,0:T(8,128)(2,1)S(1)} all-to-all(bf16[4,128,2048]{2,1,0:T(8,128)(2,1)S(1)} %broadcast_in_dim.34), channel_id=1, replica_groups=mesh['dp'=32,'tensor'=4] {'tensor'}, dimensions={0} | all-to-all | bytes 4194304 | tf_op jit(solution)/shard_map/all_to_all | solution.py:61
  472.3 5.0 fusion.75
  477.3 2.6 reshape.481
  479.9 2.6 copy.126
  482.5 3.6 fusion.62
  488.1 2.9 convolution_bitcast_fusion
  491.0 2.6 multiply_convert_fusion.3
  497.1 4.7 multiply_reduce_fusion.1
  502.2 4.9 fusion.23
  507.1 4.3 fusion.22
  511.4 4.3 fusion.21
  515.7 4.4 fusion.20
  520.1 2.7 fusion.19
  522.8 13.7 %copy.127 = bf16[2048,2560]{1,0:T(8,128)(2,1)} copy(bf16[2048,2560]{0,1:T(8,128)(2,1)} %fusion.19) | data formatting | bytes 20971520
  536.6 5.3 convolution_convert_fusion.2
  541.9 5.1 convolution_convert_fusion.1
  547.0 4.8 fusion
  551.8 7.6 pad_maximum_fusion
  559.4 21.7 %copy.129 = bf16[2048,4224]{1,0:T(8,128)(2,1)} copy(bf16[2048,4224]{0,1:T(8,128)(2,1)} %pad_maximum_fusion) | data formatting | bytes 34603008
  581.1 8.6 fusion.3
  589.8 5.0 all-to-all-start.4
  594.8 3.1 fusion.38
  598.0 2.9 fusion.40
  600.9 2.9 fusion.42
  603.8 5.0 add_add_fusion
  608.8 98.3 %all-to-all-done.4 = f32[4,128,2048]{2,1,0:T(8,128)} async-done(((f32[4,128,2048]{2,1,0:T(8,128)}), f32[4,128,2048]{2,1,0:T(8,128)}, u32[]{:S(2)}, u32[]{:S(2)}) %all-to-all-start.4) | async-done | bytes 4194336 | tf_op jit(solution)/shard_map/all_to_all | solution.py:68
  707.1 4.9 all-to-all-start.8
  712.1 3.6 reduce_sum.137
  717.0 51.9 %all-to-all-done.8 = f32[4,128,2048]{2,1,0:T(8,128)} async-done(((f32[4,128,2048]{2,1,0:T(8,128)}), f32[4,128,2048]{2,1,0:T(8,128)}, u32[]{:S(2)}, u32[]{:S(2)}) %all-to-all-start.8) | async-done | bytes 4194336 | tf_op jit(solution)/shard_map/all_to_all | solution.py:68
  769.0 3.6 reduce_sum.142
  775.1 9.5 all-to-all-start.9
  784.6 3.4 fusion.70
  788.1 8.4 all-to-all-done.9
  802.5 221.6 %reduce-scatter.9.cloned.1.call-done = bf16[64,4224]{1,0:T(8,128)(2,1)} async-done(((bf16[2048,4224]{1,0:T(8,128)(2,1)}), bf16[64,4224]{1,0:T(8,128)(2,1)}) %reduce-scatter.9.cloned.1.call-update) | async-done | bytes 540688
  (154 shorter events, 44.6 us)
Async XLA Ops:
  7.2 19.7 %copy-start = (bf16[1,1,128,2048]{3,2,1,0:T(8,128)(2,1)S(1)}, bf16[1,1,128,2048]{3,2,1,0:T(8,128)(2,1)}, u32[]{:S(2)}) copy-start(bf16[1,1,128,2048]{3,2,1,0:T(8,128)(2,1)} %param.14) | copy-start | bytes 1572868
  7.2 136.3 %all-gather.3.cloned.1.call-start = ((), (), s32[]{:S(2)}) async-start(), calls=%async_computation.12 | async-start | bytes 10813440 | tf_op jit(solution)/shard_map/all_gather | solution.py:118
  11.5 0.7 copy-start.25
  12.3 337.7 %all-gather.5.cloned.1.call-start = ((), (), s32[]{:S(2)}) async-start(), calls=%async_computation.13 | async-start | bytes 17842176 | tf_op jit(solution)/shard_map/all_gather | solution.py:119
  15.7 23.1 %all-to-all-start = ((f32[128,3,16]{2,1,0:T(4,128)}), f32[128,3,16]{2,1,0:T(4,128)S(1)}, u32[]{:S(2)}, u32[]{:S(2)}) async-start(f32[128,3,16]{2,1,0:T(4,128)} %broadcast_in_dim.27), calls=%async_computation | async-start | bytes 524288 | tf_op jit(solution)/shard_map/all_to_all | solution.py:75
  27.6 13.7 %copy-start.29 = (f32[128]{0:T(128)}, f32[128]{0:T(128)S(1)}, u32[]{:S(2)}) copy-start(f32[128]{0:T(128)S(1)} %get-tuple-element.97) | copy-start | bytes 1540
  39.4 1.8 copy-start.26
  39.6 6.4 copy-start.28
  41.3 118.0 %all-to-all-start.1 = ((bf16[4,128,2048]{2,1,0:T(8,128)(2,1)}), bf16[4,128,2048]{2,1,0:T(8,128)(2,1)}, u32[]{:S(2)}, u32[]{:S(2)}) async-start(bf16[4,128,2048]{2,1,0:T(8,128)(2,1)} %broadcast_in_dim.28), calls=%async_computation.1 | async-start | bytes 4194304 | tf_op jit(solution)/shard_map/all_to_all | solution.py:61
  159.3 4.8 copy-start.18
  163.1 3.9 copy-start.5
  166.9 5.8 copy-start.10
  166.9 2.5 copy-start.19
  169.4 3.3 copy-start.4
  172.8 1.0 copy-start.8
  184.1 3.1 copy-start.20
  187.1 70.3 %copy-start.7 = (bf16[1,1,128,2048]{3,2,1,0:T(8,128)(2,1)S(1)}, bf16[1,1,128,2048]{3,2,1,0:T(8,128)(2,1)}, u32[]{:S(2)}) copy-start(bf16[1,1,128,2048]{3,2,1,0:T(8,128)(2,1)} %param.27) | copy-start | bytes 1572868
  259.1 53.0 %all-to-all-start.5 = ((bf16[4,128,2048]{2,1,0:T(8,128)(2,1)}), bf16[4,128,2048]{2,1,0:T(8,128)(2,1)}, u32[]{:S(2)}, u32[]{:S(2)}) async-start(bf16[4,128,2048]{2,1,0:T(8,128)(2,1)} %broadcast_in_dim.33), calls=%async_computation.5 | async-start | bytes 4194304 | tf_op jit(solution)/shard_map/all_to_all | solution.py:61
  314.7 43.5 %all-to-all-start.3 = ((bf16[4,128,2048]{2,1,0:T(8,128)(2,1)}), bf16[4,128,2048]{2,1,0:T(8,128)(2,1)}, u32[]{:S(2)}, u32[]{:S(2)}) async-start(bf16[4,128,2048]{2,1,0:T(8,128)(2,1)} %broadcast_in_dim.31), calls=%async_computation.3 | async-start | bytes 4194304 | tf_op jit(solution)/shard_map/all_to_all | solution.py:61
  319.2 478.0 %reduce-scatter.7.cloned.1.call-start = ((), (), s32[]{:S(2)}) async-start(), calls=%async_computation.14 | async-start | bytes 10813440
  358.2 9.1 copy-start.32
  358.2 10.1 copy-start.38
  376.0 5.1 copy-start.36
  376.0 5.1 copy-start.33
  441.6 1.6 copy-start.1
  443.7 28.6 %copy-start.22 = (f32[4,128,4,128]{3,2,1,0:T(4,128)S(1)}, f32[4,128,4,128]{3,2,1,0:T(4,128)}, u32[]{:S(2)}) copy-start(f32[4,128,4,128]{3,2,1,0:T(4,128)} %copy.99) | copy-start | bytes 3145732
  443.7 28.6 %copy-start.34 = (f32[512,512]{1,0:T(8,128)S(1)}, f32[512,512]{1,0:T(8,128)}, u32[]{:S(2)}) copy-start(f32[512,512]{1,0:T(8,128)} %get-tuple-element.101) | copy-start | bytes 3145732
  472.3 5.1 copy-start.16
  482.5 3.6 copy-start.3
  482.5 3.6 copy-start.9
  482.5 5.6 copy-start.11
  488.0 3.0 copy-start.6
  497.1 5.1 copy-start.13
  502.2 4.9 copy-start.15
  507.1 4.3 copy-start.12
  511.4 4.3 copy-start.23
  515.7 4.4 copy-start.17
  515.7 4.4 copy-start.21
  536.6 487.6 %reduce-scatter.9.cloned.1.call-start = ((), (), s32[]{:S(2)}) async-start(), calls=%async_computation.15 | async-start | bytes 17842176
  536.6 5.3 copy-start.37
  541.9 5.1 copy-start.35
  589.8 117.3 %all-to-all-start.4 = ((f32[4,128,2048]{2,1,0:T(8,128)}), f32[4,128,2048]{2,1,0:T(8,128)}, u32[]{:S(2)}, u32[]{:S(2)}) async-start(f32[4,128,2048]{2,1,0:T(8,128)} %bitcast.228), calls=%async_computation.4 | async-start | bytes 8388608 | tf_op jit(solution)/shard_map/all_to_all | solution.py:68
  594.8 3.1 copy-start.14
  600.9 3.0 copy-start.24
  707.1 61.8 %all-to-all-start.8 = ((f32[4,128,2048]{2,1,0:T(8,128)}), f32[4,128,2048]{2,1,0:T(8,128)}, u32[]{:S(2)}, u32[]{:S(2)}) async-start(f32[4,128,2048]{2,1,0:T(8,128)} %bitcast.226), calls=%async_computation.8 | async-start | bytes 8388608 | tf_op jit(solution)/shard_map/all_to_all | solution.py:68
  715.7 56.9 %copy-start.27 = (f32[2048]{0:T(1024)S(1)}, f32[2048]{0:T(1024)}, u32[]{:S(2)}) copy-start(f32[2048]{0:T(1024)} %copy-done.26) | copy-start | bytes 24580
  715.7 56.9 %copy-start.30 = (f32[128]{0:T(128)S(1)}, f32[128]{0:T(128)}, u32[]{:S(2)}) copy-start(f32[128]{0:T(128)} %copy-done.29) | copy-start | bytes 1540
  717.0 67.6 %copy-start.2 = (f32[128,2048]{1,0:T(8,128)S(1)}, f32[128,2048]{1,0:T(8,128)}, u32[]{:S(2)}) copy-start(f32[128,2048]{1,0:T(8,128)} %reduce_sum.139) | copy-start | bytes 3145732
  717.0 67.6 %copy-start.31 = (f32[128]{0:T(128)S(1)}, f32[128]{0:T(128)}, u32[]{:S(2)}) copy-start(f32[128]{0:T(128)} %get-tuple-element.96) | copy-start | bytes 1540
  775.1 21.4 %all-to-all-start.9 = ((f32[128,3,16]{2,1,0:T(4,128)}), f32[128,3,16]{2,1,0:T(4,128)S(1)}, u32[]{:S(2)}, u32[]{:S(2)}) async-start(f32[128,3,16]{2,1,0:T(4,128)} %copy.107), calls=%async_computation.9 | async-start | bytes 524288 | tf_op jit(solution)/shard_map/all_to_all | solution.py:82
Sparse Core Ops, SparseCore 0:
  12.4 131.0 all-gather.2
  146.5 203.3 all-gather.4
  536.7 206.7 reduce-scatter.6
  749.1 274.9 reduce-scatter.8

commit v3 on v2

--- a/solution.py
+++ b/solution.py
@@ -55,18 +55,24 @@
     return jnp.einsum("rhij,rjhv->rihv", scores, value, precision=HIGHEST)
 
 
+ON_CHIP = [(0, 1), (1, 0), (2, 3), (3, 2)]
+ACROSS = [(0, 2), (2, 0), (1, 3), (3, 1)]
+SLOT_XOR = (0, 2, 1, 3)
+
+
 def row_gather(values):
-    count = 4
-    spread = jnp.broadcast_to(values[None], (count,) + values.shape)
-    got = lax.all_to_all(spread, "tensor", 0, 0, tiled=False)
-    return got.reshape((-1,) + values.shape[1:])
+    across = lax.ppermute(values, "tensor", ACROSS)
+    pair = jnp.stack([values, across])
+    other = lax.ppermute(pair, "tensor", ON_CHIP)
+    return jnp.concatenate([pair, other]).reshape((-1,) + values.shape[1:])
 
 
 def row_sum(values):
-    count = 4
-    blocks = values.reshape((count, -1) + values.shape[1:])
-    got = lax.all_to_all(blocks, "tensor", 0, 0, tiled=False)
-    return got.sum(axis=0)
+    blocks = values.reshape((4, -1) + values.shape[1:])
+    got = lax.ppermute(blocks[2:], "tensor", ON_CHIP)
+    mine = blocks[0] + got[0]
+    theirs = blocks[1] + got[1]
+    return mine + lax.ppermute(theirs, "tensor", ACROSS)
 
 
 def small_gather(vectors):
@@ -109,7 +115,8 @@
         floor_full, part_index * local_width, local_width
     ).reshape(local_heads, HK)
     model_width = attn_full.shape[0]
-    doc_all = doc_ids[0]
+    slot_rows = jnp.bitwise_xor(part_index, jnp.array(SLOT_XOR, jnp.int32))
+    doc_all = jnp.take(doc_ids[0], slot_rows, axis=0)
     row_count = doc_all.shape[0]
     resid_in = tokens[0].reshape(-1, model_width).astype(jnp.float32)
     cot_local = cotangent[0].reshape(-1, model_width)

time: 1040 us -> 972 us (0.935)
  blocking collectives: 150 us -> 0 us
  waiting for transfers between devices: 564 us -> 679 us
  matrix products: 138 us -> 112 us
    ppermute x0 -> x16, waiting for transfers between devices: none -> 201 us  [the longest x4 123 us: row_sum(): return mine + lax.ppermute(theirs, 'tensor', ACROSS)]
    all_to_all x5 -> x0, waiting for transfers between devices: 195 us -> none  [the longest x2 150 us: row_sum(): got = lax.all_to_all(blocks, 'tensor', 0, 0, tiled=False)]
    all_to_all x3 -> x0, blocking collectives: 150 us -> none  [the longest x2 122 us: row_sum(): got = lax.all_to_all(blocks, 'tensor', 0, 0, tiled=False)]
    unnamed x6, waiting for transfers between devices: 222 us -> 320 us
    all_gather x1, waiting for transfers between devices: 30.7 us -> 62 us  [shards(): mlp_all = lax.all_gather(mlp_pack, 'dp', axis=0, tiled=True)]
    all_gather x1, waiting for transfers between devices: 96.8 us -> 72.4 us  [shards(): attn_all = lax.all_gather(attn_pack, 'dp', axis=0, tiled=True)]
    all_to_all x5 -> x0, starting transfers between devices: 23.6 us -> none  [the longest x3 13.6 us: row_gather(): got = lax.all_to_all(spread, 'tensor', 0, 0, tiled=False)]
    all_to_all x1, starting transfers between devices: 9.49 us -> 23.7 us  [small_sum(): lax.all_to_all(jnp.swapaxes(blocks, 0, 1), ('dp', 'tensor'), 0, 0, tiled=...]
  transfers between devices with their start and end apart: 11 -> 22, of which waited for: 8 -> 20; matrix products, arithmetic and copies ran while one was open for 15% -> 13% of each run, Pallas kernels for 0% -> 0%
where the time goes in v3:
time: 972 us; the launch traced here: 967 us
  waiting for transfers between devices  679 us (70%)
  matrix products  112 us (12%)
  local copies, waits for them, and re-layouts  87.8 us (9%)
  starting transfers between devices  43.8 us (5%)
  other arithmetic  29.6 us (3%)
  between operations  15.2 us (2%)
    unnamed x6, waiting for transfers between devices  320 us
    ppermute x4, waiting for transfers between devices, row_sum(): return mine + lax.ppermute(theirs, 'tensor', ACROSS)  123 us
    all_gather x1, waiting for transfers between devices, shards(): attn_all = lax.all_gather(attn_pack, 'dp', axis=0, tiled=True)  72.4 us
    ppermute x4, waiting for transfers between devices, row_gather(): across = lax.ppermute(values, 'tensor', ACROSS)  63.1 us
    all_gather x1, waiting for transfers between devices, shards(): mlp_all = lax.all_gather(mlp_pack, 'dp', axis=0, tiled=True)  62 us
    unnamed x108, local copies, waits for them, and re-layouts  56.6 us
    dot_general x8, matrix products, matmul_plain(): return jnp.dot(left, right, preferred_element_type=jnp.float32)  37.5 us
    dot_general x8, matrix products, times_trans(): lax.dot_general(left, right, (((1,), (1,)), ((), ())), preferred_element_...  27.9 us
  transfers between devices with their start and end apart: 22, of which 20 were waited for; matrix products, arithmetic and copies ran while one was open for 13% of the time, Pallas kernels for 0%

profile of v3, /device:TPU:0, one launch (start us, length us, event | category | flops | bytes accessed | tf_op | source)
XLA Modules:
  0.0 966.7 jit_solution(16642316750731490610)
XLA Ops:
  15.1 11.1 %all-to-all-start = ((f32[128,3,16]{2,1,0:T(4,128)}), f32[128,3,16]{2,1,0:T(4,128)S(1)}, u32[]{:S(2)}, u32[]{:S(2)}) async-start(f32[128,3,16]{2,1,0:T(4,128)} %broadcast_in_dim.29), calls=%async_computation | async-start | bytes 524288 | tf_op jit(solution)/shard_map/all_to_all | solution.py:81
  27.0 11.5 %all-to-all-done = f32[128,3,16]{2,1,0:T(4,128)S(1)} async-done(((f32[128,3,16]{2,1,0:T(4,128)}), f32[128,3,16]{2,1,0:T(4,128)S(1)}, u32[]{:S(2)}, u32[]{:S(2)}) %all-to-all-start) | async-done | bytes 24608 | tf_op jit(solution)/shard_map/all_to_all | solution.py:81
  40.2 15.5 %collective-permute-done = bf16[128,2048]{1,0:T(8,128)(2,1)S(1)} collective-permute-done((bf16[128,2048]{1,0:T(8,128)(2,1)S(1)}, bf16[128,2048]{1,0:T(8,128)(2,1)S(1)}, u32[]{:S(2)}, u32[]{:S(2)}) %collective-permute-start) | collective-permute-done | bytes 524320 | tf_op jit(solution)/shard_map/ppermute | solution.py:64
  58.7 2.8 pad_maximum_fusion.1
  61.5 72.4 %all-gather.3.cloned.1.call-done = bf16[2048,2560]{1,0:T(8,128)(2,1)} async-done(((bf16[64,2560]{1,0:T(8,128)(2,1)}), bf16[2048,2560]{1,0:T(8,128)(2,1)}) %all-gather.3.cloned.1.call-update) | async-done | bytes 10485776 | tf_op jit(solution)/shard_map/all_gather | solution.py:125
  133.9 5.5 slice_bitcast_fusion
  139.3 4.2 copy.91
  143.5 4.1 copy.93
  147.6 2.5 copy.94
  150.0 3.6 fusion.56
  155.6 2.5 fusion.23
  158.2 2.5 convolution_select_fusion.1
  160.7 2.9 fusion.25
  163.6 2.9 convolution_bitcast_fusion.2
  166.5 2.5 copy.97
  169.0 4.9 fusion.74
  173.9 3.1 fusion.29
  177.4 4.1 collective-permute-done.2
  184.3 24.8 %collective-permute-done.3 = f32[128,2048]{1,0:T(8,128)} collective-permute-done((f32[128,2048]{1,0:T(8,128)S(1)}, f32[128,2048]{1,0:T(8,128)}, u32[]{:S(2)}, u32[]{:S(2)}) %collective-permute-start.3) | collective-permute-done | bytes 1048608 | tf_op jit(solution)/shard_map/ppermute | solution.py:75
  209.1 2.3 multiply_reduce_fusion.3
  212.0 14.5 %collective-permute-done.8 = bf16[128,2048]{1,0:T(8,128)(2,1)} collective-permute-done((bf16[128,2048]{1,0:T(8,128)(2,1)S(1)}, bf16[128,2048]{1,0:T(8,128)(2,1)}, u32[]{:S(2)}, u32[]{:S(2)}) %collective-permute-start.8) | collective-permute-done | bytes 524320 | tf_op jit(solution)/shard_map/ppermute | solution.py:64
  227.9 20.7 %collective-permute-done.4 = bf16[128,2048]{1,0:T(8,128)(2,1)S(1)} collective-permute-done((bf16[128,2048]{1,0:T(8,128)(2,1)S(1)}, bf16[128,2048]{1,0:T(8,128)(2,1)S(1)}, u32[]{:S(2)}, u32[]{:S(2)}) %collective-permute-start.4) | collective-permute-done | bytes 524320 | tf_op jit(solution)/shard_map/ppermute | solution.py:64
  248.8 2.6 pad_maximum_fusion.3
  253.0 62.0 %all-gather.5.cloned.1.call-done = bf16[2048,4224]{1,0:T(8,128)(2,1)} async-done(((bf16[64,4224]{1,0:T(8,128)(2,1)}), bf16[2048,4224]{1,0:T(8,128)(2,1)}) %all-gather.5.cloned.1.call-update) | async-done | bytes 17301520 | tf_op jit(solution)/shard_map/all_gather | solution.py:126
  315.0 6.5 fusion
  321.5 2.3 copy-done.41
  323.9 5.0 fusion.6
  328.8 7.3 multiply_convert_fusion.1
  336.1 3.4 fusion.4
  339.6 4.8 fusion.12
  344.8 4.8 fusion.2
  351.1 3.0 collective-permute-done.6
  354.9 21.6 %collective-permute-done.11 = f32[128,2048]{1,0:T(8,128)S(1)} collective-permute-done((f32[128,2048]{1,0:T(8,128)S(1)}, f32[128,2048]{1,0:T(8,128)S(1)}, u32[]{:S(2)}, u32[]{:S(2)}) %collective-permute-start.11) | collective-permute-done | bytes 1048608 | tf_op jit(solution)/shard_map/ppermute | solution.py:75
  377.0 21.1 %collective-permute-done.7 = f32[128,2048]{1,0:T(8,128)S(1)} collective-permute-done((f32[128,2048]{1,0:T(8,128)S(1)}, f32[128,2048]{1,0:T(8,128)S(1)}, u32[]{:S(2)}, u32[]{:S(2)}) %collective-permute-start.7) | collective-permute-done | bytes 1048608 | tf_op jit(solution)/shard_map/ppermute | solution.py:75
  400.4 12.4 %collective-permute-done.12 = bf16[128,2048]{1,0:T(8,128)(2,1)S(1)} collective-permute-done((bf16[128,2048]{1,0:T(8,128)(2,1)S(1)}, bf16[128,2048]{1,0:T(8,128)(2,1)S(1)}, u32[]{:S(2)}, u32[]{:S(2)}) %collective-permute-start.12) | collective-permute-done | bytes 524320 | tf_op jit(solution)/shard_map/ppermute | solution.py:64
  413.2 2.6 collective-permute-done.13
  416.1 4.8 fusion.76
  423.7 2.4 fusion.59
  428.1 2.7 multiply_convert_fusion.3
  430.8 2.9 convolution_bitcast_fusion
  435.5 4.0 multiply_reduce_fusion.1
  440.0 2.9 fusion.19
  442.9 2.7 fusion.18
  445.6 2.7 fusion.17
  448.3 2.7 fusion.16
  451.0 2.6 fusion.15
  453.7 13.8 %copy.123 = bf16[2048,2560]{1,0:T(8,128)(2,1)} copy(bf16[2048,2560]{0,1:T(8,128)(2,1)} %fusion.15) | data formatting | bytes 20971520
  467.6 5.3 convolution_convert_fusion
  472.9 3.5 convolution_convert_fusion.1
  476.4 3.5 convolution_convert_fusion.2
  479.9 7.7 pad_maximum_fusion
  487.6 21.8 %copy.125 = bf16[2048,4224]{1,0:T(8,128)(2,1)} copy(bf16[2048,4224]{0,1:T(8,128)(2,1)} %pad_maximum_fusion) | data formatting | bytes 34603008
  509.4 2.9 fusion.38
  512.3 2.9 fusion.36
  515.2 2.9 fusion.34
  518.1 3.0 add_add_fusion
  522.5 3.8 collective-permute-done.14
  529.9 55.5 %collective-permute-done.15 = f32[128,2048]{1,0:T(8,128)} collective-permute-done((f32[128,2048]{1,0:T(8,128)S(1)}, f32[128,2048]{1,0:T(8,128)}, u32[]{:S(2)}, u32[]{:S(2)}) %collective-permute-start.15) | collective-permute-done | bytes 1048608 | tf_op jit(solution)/shard_map/ppermute | solution.py:75
  585.5 2.3 fusion.68
  588.7 23.7 %all-to-all-start.1 = ((f32[128,3,16]{2,1,0:T(4,128)}), f32[128,3,16]{2,1,0:T(4,128)S(1)}, u32[]{:S(2)}, u32[]{:S(2)}) async-start(f32[128,3,16]{2,1,0:T(4,128)} %copy.104), calls=%async_computation.1 | async-start | bytes 524288 | tf_op jit(solution)/shard_map/all_to_all | solution.py:88
  613.8 11.2 %all-to-all-done.1 = f32[128,3,16]{2,1,0:T(4,128)S(1)} async-done(((f32[128,3,16]{2,1,0:T(4,128)}), f32[128,3,16]{2,1,0:T(4,128)S(1)}, u32[]{:S(2)}, u32[]{:S(2)}) %all-to-all-start.1) | async-done | bytes 24608 | tf_op jit(solution)/shard_map/all_to_all | solution.py:88
  625.7 50.8 %reduce-scatter.7.cloned.1.call-done = bf16[64,2560]{1,0:T(8,128)(2,1)} async-done(((bf16[2048,2560]{1,0:T(8,128)(2,1)}), bf16[64,2560]{1,0:T(8,128)(2,1)}) %reduce-scatter.7.cloned.1.call-update) | async-done | bytes 327696
  681.8 269.4 %reduce-scatter.9.cloned.1.call-done = bf16[64,4224]{1,0:T(8,128)(2,1)} async-done(((bf16[2048,4224]{1,0:T(8,128)(2,1)}), bf16[64,4224]{1,0:T(8,128)(2,1)}) %reduce-scatter.9.cloned.1.call-update) | async-done | bytes 540688
  954.4 2.1 copy.110
  (201 shorter events, 54.6 us)
Async XLA Ops:
  7.2 48.8 %copy-start = (s32[1,4,128]{2,1,0:T(4,128)S(1)}, s32[1,4,128]{2,1,0:T(4,128)}, u32[]{:S(2)}) copy-start(s32[1,4,128]{2,1,0:T(4,128)} %param.16) | copy-start | bytes 6148
  7.2 7.1 copy-start.37
  7.2 7.1 copy-start.38
  7.2 7.1 copy-start.39
  7.2 19.1 %copy-start.3 = (bf16[1,1,128,2048]{3,2,1,0:T(8,128)(2,1)S(1)}, bf16[1,1,128,2048]{3,2,1,0:T(8,128)(2,1)}, u32[]{:S(2)}) copy-start(bf16[1,1,128,2048]{3,2,1,0:T(8,128)(2,1)} %param.15) | copy-start | bytes 1572868
  7.2 126.6 %all-gather.3.cloned.1.call-start = ((), (), s32[]{:S(2)}) async-start(), calls=%async_computation.4 | async-start | bytes 10813440 | tf_op jit(solution)/shard_map/all_gather | solution.py:125
  12.3 302.6 %all-gather.5.cloned.1.call-start = ((), (), s32[]{:S(2)}) async-start(), calls=%async_computation.5 | async-start | bytes 17842176 | tf_op jit(solution)/shard_map/all_gather | solution.py:126
  15.1 23.5 %all-to-all-start = ((f32[128,3,16]{2,1,0:T(4,128)}), f32[128,3,16]{2,1,0:T(4,128)S(1)}, u32[]{:S(2)}, u32[]{:S(2)}) async-start(f32[128,3,16]{2,1,0:T(4,128)} %broadcast_in_dim.29), calls=%async_computation | async-start | bytes 524288 | tf_op jit(solution)/shard_map/all_to_all | solution.py:81
  26.3 650.2 %reduce-scatter.7.cloned.1.call-start = ((), (), s32[]{:S(2)}) async-start(), calls=%async_computation.6 | async-start | bytes 10813440
  27.0 28.8 %copy-start.34 = (f32[128]{0:T(128)}, f32[128]{0:T(128)S(1)}, u32[]{:S(2)}) copy-start(f32[128]{0:T(128)S(1)} %get-tuple-element.104) | copy-start | bytes 1540
  39.2 16.6 %copy-start.32 = (f32[2048]{0:T(1024)}, f32[2048]{0:T(1024)S(1)}, u32[]{:S(2)}) copy-start(f32[2048]{0:T(1024)S(1)} %mul.250) | copy-start | bytes 24580
  39.2 16.7 %copy-start.40 = (s32[4]{0:T(128)S(1)}, s32[4]{0:T(128)}, u32[]{:S(2)}) copy-start(s32[4]{0:T(128)} %constant.52.clone) | copy-start | bytes 52
  39.4 16.3 %collective-permute-start = (bf16[128,2048]{1,0:T(8,128)(2,1)S(1)}, bf16[128,2048]{1,0:T(8,128)(2,1)S(1)}, u32[]{:S(2)}, u32[]{:S(2)}) collective-permute-start(bf16[128,2048]{1,0:T(8,128)(2,1)S(1)} %fusion.62), channel_id=1, source_target_pairs={{0,2},{2,0},{1,3},{3,1},{4,6},{6,4},{5,7},{7,5},{8,10},{10,8},{9,1... | collective-permute-start | bytes 1572872 | tf_op jit(solution)/shard_map/ppermute | solution.py:64
  55.7 5.8 copy-start.25
  55.9 2.9 collective-permute-start.1
  150.0 4.5 copy-start.26
  153.6 4.5 copy-start.7
  153.6 2.0 copy-start.24
  158.1 2.5 copy-start.14
  158.1 2.5 copy-start.23
  160.6 2.9 copy-start.6
  163.6 5.4 copy-start.12
  173.9 3.1 copy-start.27
  177.0 4.5 copy-start.2
  177.3 6.0 copy-start.10
  177.3 4.2 collective-permute-start.2
  181.7 27.5 %collective-permute-start.3 = (f32[128,2048]{1,0:T(8,128)S(1)}, f32[128,2048]{1,0:T(8,128)}, u32[]{:S(2)}, u32[]{:S(2)}) collective-permute-start(f32[128,2048]{1,0:T(8,128)S(1)} %fusion.88), channel_id=1, source_target_pairs={{0,2},{2,0},{1,3},{3,1},{4,6},{6,4},{5,7},{7,5},{8,10},{10,8},{9,1... | collective-permute-start | bytes 3145736 | tf_op jit(solution)/shard_map/ppermute | solution.py:75
  183.2 43.3 %collective-permute-start.8 = (bf16[128,2048]{1,0:T(8,128)(2,1)S(1)}, bf16[128,2048]{1,0:T(8,128)(2,1)}, u32[]{:S(2)}, u32[]{:S(2)}) collective-permute-start(bf16[128,2048]{1,0:T(8,128)(2,1)S(1)} %bitcast.265), channel_id=1, source_target_pairs={{0,2},{2,0},{1,3},{3,1},{4,6},{6,4},{5,7},{7,5},{8,10},{10,8},{9,1... | collective-permute-start | bytes 1572872 | tf_op jit(solution)/shard_map/ppermute | solution.py:64
  211.6 37.0 %collective-permute-start.4 = (bf16[128,2048]{1,0:T(8,128)(2,1)S(1)}, bf16[128,2048]{1,0:T(8,128)(2,1)S(1)}, u32[]{:S(2)}, u32[]{:S(2)}) collective-permute-start(bf16[128,2048]{1,0:T(8,128)(2,1)S(1)} %multiply_convert_fusion.4), channel_id=1, source_target_pairs={{0,2},{2,0},{1,3},{3,1},{4,6},{6,4},{5,7},{7,5},{8,10},{10,8},{9,1... | collective-permute-start | bytes 1572872 | tf_op jit(solution)/shard_map/ppermute | solution.py:64
  227.6 21.1 %collective-permute-start.9 = (bf16[2,128,2048]{2,1,0:T(8,128)(2,1)S(1)}, bf16[2,128,2048]{2,1,0:T(8,128)(2,1)S(1)}, u32[]{:S(2)}, u32[]{:S(2)}) collective-permute-start(bf16[2,128,2048]{2,1,0:T(8,128)(2,1)S(1)} %pad_maximum_fusion.7), channel_id=1, source_target_pairs={{0,1},{1,0},{2,3},{3,2},{4,5},{5,4},{6,7},{7,6},{8,9},{9,8},{10,11... | collective-permute-start | bytes 3145736 | tf_op jit(solution)/shard_map/ppermute | solution.py:66
  248.7 2.7 collective-permute-start.5
  315.0 6.6 copy-start.18
  315.0 8.9 copy-start.41
  336.1 3.5 copy-start.44
  344.7 5.6 collective-permute-start.10
  349.7 4.4 collective-permute-start.6
  350.4 26.1 %collective-permute-start.11 = (f32[128,2048]{1,0:T(8,128)S(1)}, f32[128,2048]{1,0:T(8,128)S(1)}, u32[]{:S(2)}, u32[]{:S(2)}) collective-permute-start(f32[128,2048]{1,0:T(8,128)S(1)} %fusion.80), channel_id=1, source_target_pairs={{0,2},{2,0},{1,3},{3,1},{4,6},{6,4},{5,7},{7,5},{8,10},{10,8},{9,1... | collective-permute-start | bytes 3145736 | tf_op jit(solution)/shard_map/ppermute | solution.py:75
  354.2 43.8 %collective-permute-start.7 = (f32[128,2048]{1,0:T(8,128)S(1)}, f32[128,2048]{1,0:T(8,128)S(1)}, u32[]{:S(2)}, u32[]{:S(2)}) collective-permute-start(f32[128,2048]{1,0:T(8,128)S(1)} %fusion.83), channel_id=1, source_target_pairs={{0,2},{2,0},{1,3},{3,1},{4,6},{6,4},{5,7},{7,5},{8,10},{10,8},{9,1... | collective-permute-start | bytes 3145736 | tf_op jit(solution)/shard_map/ppermute | solution.py:75
  399.8 13.0 %collective-permute-start.12 = (bf16[128,2048]{1,0:T(8,128)(2,1)S(1)}, bf16[128,2048]{1,0:T(8,128)(2,1)S(1)}, u32[]{:S(2)}, u32[]{:S(2)}) collective-permute-start(bf16[128,2048]{1,0:T(8,128)(2,1)S(1)} %get-tuple-element.75), channel_id=1, source_target_pairs={{0,2},{2,0},{1,3},{3,1},{4,6},{6,4},{5,7},{7,5},{8,10},{10,8},{9,1... | collective-permute-start | bytes 1572872 | tf_op jit(solution)/shard_map/ppermute | solution.py:64
  412.9 3.2 copy-start.29
  412.9 3.2 copy-start.43
  412.9 2.9 collective-permute-start.13
  416.0 4.8 copy-start.20
  423.7 2.5 copy-start.13
  426.2 2.0 copy-start.8
  428.1 2.7 copy-start.15
  435.5 4.5 copy-start.17
  445.6 2.7 copy-start.30
  448.3 2.7 copy-start.21
  448.3 2.7 copy-start.28
  467.5 483.8 %reduce-scatter.9.cloned.1.call-start = ((), (), s32[]{:S(2)}) async-start(), calls=%async_computation.7 | async-start | bytes 17842176
  467.6 5.4 copy-start.19
  467.6 5.4 copy-start.45
  472.9 3.5 copy-start.42
  521.1 5.2 copy-start.5
  521.3 64.1 %copy-start.4 = (bf16[1,1,128,2048]{3,2,1,0:T(8,128)(2,1)S(1)}, bf16[1,1,128,2048]{3,2,1,0:T(8,128)(2,1)}, u32[]{:S(2)}) copy-start(bf16[1,1,128,2048]{3,2,1,0:T(8,128)(2,1)} %param.15) | copy-start | bytes 1572868
  521.4 64.1 %copy-start.33 = (f32[2048]{0:T(1024)S(1)}, f32[2048]{0:T(1024)}, u32[]{:S(2)}) copy-start(f32[2048]{0:T(1024)} %copy-done.32) | copy-start | bytes 24580
  521.4 64.1 %copy-start.35 = (f32[128]{0:T(128)S(1)}, f32[128]{0:T(128)}, u32[]{:S(2)}) copy-start(f32[128]{0:T(128)} %copy-done.34) | copy-start | bytes 1540
  521.4 4.9 collective-permute-start.14
  527.7 57.8 %collective-permute-start.15 = (f32[128,2048]{1,0:T(8,128)S(1)}, f32[128,2048]{1,0:T(8,128)}, u32[]{:S(2)}, u32[]{:S(2)}) collective-permute-start(f32[128,2048]{1,0:T(8,128)S(1)} %fusion.77), channel_id=1, source_target_pairs={{0,2},{2,0},{1,3},{3,1},{4,6},{6,4},{5,7},{7,5},{8,10},{10,8},{9,1... | collective-permute-start | bytes 3145736 | tf_op jit(solution)/shard_map/ppermute | solution.py:75
  529.9 82.6 %copy-start.11 = (f32[128,2048]{1,0:T(8,128)S(1)}, f32[128,2048]{1,0:T(8,128)}, u32[]{:S(2)}) copy-start(f32[128,2048]{1,0:T(8,128)} %get-tuple-element.76) | copy-start | bytes 3145732
  529.9 82.6 %copy-start.36 = (f32[128]{0:T(128)S(1)}, f32[128]{0:T(128)}, u32[]{:S(2)}) copy-start(f32[128]{0:T(128)} %get-tuple-element.103) | copy-start | bytes 1540
  588.7 36.3 %all-to-all-start.1 = ((f32[128,3,16]{2,1,0:T(4,128)}), f32[128,3,16]{2,1,0:T(4,128)S(1)}, u32[]{:S(2)}, u32[]{:S(2)}) async-start(f32[128,3,16]{2,1,0:T(4,128)} %copy.104), calls=%async_computation.1 | async-start | bytes 524288 | tf_op jit(solution)/shard_map/all_to_all | solution.py:88
  954.4 5.3 copy-start.1
  (4 other events, 5.6 us)
Sparse Core Ops, SparseCore 0:
  12.4 121.3 all-gather.2
  136.9 177.9 all-gather.4
  467.6 208.8 reduce-scatter.6
  682.1 269.1 reduce-scatter.8

commit v4 on v3

--- a/solution.py
+++ b/solution.py
@@ -73,6 +73,12 @@
     mine = blocks[0] + got[0]
     theirs = blocks[1] + got[1]
     return mine + lax.ppermute(theirs, "tensor", ACROSS)
+
+
+def spread_sum(values, axis, count):
+    blocks = values.reshape((count, -1) + values.shape[1:])
+    got = lax.all_to_all(blocks, axis, 0, 0, tiled=False)
+    return got.astype(jnp.float32).sum(axis=0)
 
 
 def small_gather(vectors):
@@ -205,7 +211,7 @@
         ],
         axis=1,
     )
-    attn_red = lax.psum_scatter(attn_grads, "dp", scatter_dimension=0, tiled=True).astype(jnp.float32)
+    attn_red = spread_sum(attn_grads, "dp", 32)
     d_normed = row_sum(
         times_trans(d_query, wq_all)
         + times_trans(d_forget, wf_all)

time: 972 us -> 813 us (0.84)
  waiting for transfers between devices: 679 us -> 527 us
  starting transfers between devices: 43.8 us -> 34 us
    unnamed x6 -> x4, waiting for transfers between devices: 320 us -> 31.9 us
    all_to_all x0 -> x1, waiting for transfers between devices: none -> 164 us  [spread_sum(): got = lax.all_to_all(blocks, axis, 0, 0, tiled=False)]
    ppermute x4, waiting for transfers between devices: 123 us -> 106 us  [row_sum(): return mine + lax.ppermute(theirs, 'tensor', ACROSS)]
    all_to_all x1, starting transfers between devices: 23.7 us -> 7.17 us  [small_sum(): lax.all_to_all(jnp.swapaxes(blocks, 0, 1), ('dp', 'tensor'), 0, 0, tiled=...]
    unnamed x108 -> x101, local copies, waits for them, and re-layouts: 56.6 us -> 40.4 us
    concatenate x0 -> x1, local copies, waits for them, and re-layouts: none -> 13.9 us  [shards(): jnp.concatenate([grad_query.astype(jnp.bfloat16), grad_forget.astype(jnp....]
    all_to_all x1, waiting for transfers between devices: 11.2 us -> 0.01 us  [small_sum(): lax.all_to_all(jnp.swapaxes(blocks, 0, 1), ('dp', 'tensor'), 0, 0, tiled=...]
    all_to_all x0 -> x1, starting transfers between devices: none -> 9.76 us  [spread_sum(): got = lax.all_to_all(blocks, axis, 0, 0, tiled=False)]
  transfers between devices with their start and end apart: 22 -> 22, of which waited for: 20 -> 19; matrix products, arithmetic and copies ran while one was open for 13% -> 19% of each run, Pallas kernels for 0% -> 0%
where the time goes in v4:
time: 813 us; the launch traced here: 808 us
  waiting for transfers between devices  527 us (65%)
  matrix products  108 us (13%)
  local copies, waits for them, and re-layouts  86.1 us (11%)
  other arithmetic  37 us (5%)
  starting transfers between devices  34 us (4%)
  between operations  15.3 us (2%)
    all_to_all x1, waiting for transfers between devices, spread_sum(): got = lax.all_to_all(blocks, axis, 0, 0, tiled=False)  164 us
    ppermute x4, waiting for transfers between devices, row_sum(): return mine + lax.ppermute(theirs, 'tensor', ACROSS)  106 us
    all_gather x1, waiting for transfers between devices, shards(): attn_all = lax.all_gather(attn_pack, 'dp', axis=0, tiled=True)  72.5 us
    ppermute x4, waiting for transfers between devices, row_gather(): across = lax.ppermute(values, 'tensor', ACROSS)  66.2 us
    all_gather x1, waiting for transfers between devices, shards(): mlp_all = lax.all_gather(mlp_pack, 'dp', axis=0, tiled=True)  63.5 us
    unnamed x101, local copies, waits for them, and re-layouts  40.4 us
    dot_general x8, matrix products, matmul_plain(): return jnp.dot(left, right, preferred_element_type=jnp.float32)  36.9 us
    unnamed x4, waiting for transfers between devices  31.9 us
  transfers between devices with their start and end apart: 22, of which 19 were waited for; matrix products, arithmetic and copies ran while one was open for 19% of the time, Pallas kernels for 0%

profile of v4, /device:TPU:0, one launch (start us, length us, event | category | flops | bytes accessed | tf_op | source)
XLA Modules:
  0.0 807.6 jit_solution(461497468060412222)
XLA Ops:
  12.4 2.0 pad_maximum_fusion.9
  15.1 11.1 %all-to-all-start = ((f32[128,3,16]{2,1,0:T(4,128)}), f32[128,3,16]{2,1,0:T(4,128)S(1)}, u32[]{:S(2)}, u32[]{:S(2)}) async-start(f32[128,3,16]{2,1,0:T(4,128)} %broadcast_in_dim.29), calls=%async_computation | async-start | bytes 524288 | tf_op jit(solution)/shard_map/all_to_all | solution.py:87
  27.1 11.5 %all-to-all-done = f32[128,3,16]{2,1,0:T(4,128)S(1)} async-done(((f32[128,3,16]{2,1,0:T(4,128)}), f32[128,3,16]{2,1,0:T(4,128)S(1)}, u32[]{:S(2)}, u32[]{:S(2)}) %all-to-all-start) | async-done | bytes 24608 | tf_op jit(solution)/shard_map/all_to_all | solution.py:87
  40.2 15.4 %collective-permute-done = bf16[128,2048]{1,0:T(8,128)(2,1)S(1)} collective-permute-done((bf16[128,2048]{1,0:T(8,128)(2,1)S(1)}, bf16[128,2048]{1,0:T(8,128)(2,1)S(1)}, u32[]{:S(2)}, u32[]{:S(2)}) %collective-permute-start) | collective-permute-done | bytes 524320 | tf_op jit(solution)/shard_map/ppermute | solution.py:64
  58.6 2.8 pad_maximum_fusion.1
  61.4 72.5 %all-gather.3.cloned.1.call-done = bf16[2048,2560]{1,0:T(8,128)(2,1)} async-done(((bf16[64,2560]{1,0:T(8,128)(2,1)}), bf16[2048,2560]{1,0:T(8,128)(2,1)}) %all-gather.3.cloned.1.call-update) | async-done | bytes 10485776 | tf_op jit(solution)/shard_map/all_gather | solution.py:131
  133.9 5.3 slice_bitcast_fusion
  139.2 4.1 copy.78
  143.3 4.1 copy.80
  147.4 2.4 copy.81
  149.8 3.6 fusion.56
  155.4 2.5 fusion.23
  157.9 2.5 convolution_select_fusion.1
  160.5 2.9 fusion.25
  164.3 1.9 convolution_bitcast_fusion.2
  167.5 5.4 fusion.74
  172.9 3.1 fusion.29
  176.4 4.1 collective-permute-done.2
  182.8 26.3 %collective-permute-done.3 = f32[128,2048]{1,0:T(8,128)} collective-permute-done((f32[128,2048]{1,0:T(8,128)S(1)}, f32[128,2048]{1,0:T(8,128)}, u32[]{:S(2)}, u32[]{:S(2)}) %collective-permute-start.3) | collective-permute-done | bytes 1048608 | tf_op jit(solution)/shard_map/ppermute | solution.py:75
  209.1 2.3 multiply_reduce_fusion.3
  211.9 13.1 %collective-permute-done.8 = bf16[128,2048]{1,0:T(8,128)(2,1)} collective-permute-done((bf16[128,2048]{1,0:T(8,128)(2,1)S(1)}, bf16[128,2048]{1,0:T(8,128)(2,1)}, u32[]{:S(2)}, u32[]{:S(2)}) %collective-permute-start.8) | collective-permute-done | bytes 524320 | tf_op jit(solution)/shard_map/ppermute | solution.py:64
  226.3 20.7 %collective-permute-done.4 = bf16[128,2048]{1,0:T(8,128)(2,1)S(1)} collective-permute-done((bf16[128,2048]{1,0:T(8,128)(2,1)S(1)}, bf16[128,2048]{1,0:T(8,128)(2,1)S(1)}, u32[]{:S(2)}, u32[]{:S(2)}) %collective-permute-start.4) | collective-permute-done | bytes 524320 | tf_op jit(solution)/shard_map/ppermute | solution.py:64
  247.2 2.5 pad_maximum_fusion.3
  251.4 63.5 %all-gather.5.cloned.1.call-done = bf16[2048,4224]{1,0:T(8,128)(2,1)} async-done(((bf16[64,4224]{1,0:T(8,128)(2,1)}), bf16[2048,4224]{1,0:T(8,128)(2,1)}) %all-gather.5.cloned.1.call-update) | async-done | bytes 17301520 | tf_op jit(solution)/shard_map/all_gather | solution.py:132
  315.0 7.0 fusion
  322.0 1.9 copy-done.36
  323.9 3.4 fusion.6
  327.3 7.3 multiply_convert_fusion.1
  334.7 3.5 convolution_convert_fusion
  338.2 3.5 convolution_convert_fusion.1
  341.6 3.5 convolution_convert_fusion.2
  345.1 7.9 pad_maximum_fusion
  353.0 21.9 %copy.106 = bf16[2048,4224]{1,0:T(8,128)(2,1)} copy(bf16[2048,4224]{0,1:T(8,128)(2,1)} %pad_maximum_fusion) | data formatting | bytes 34603008
  374.9 6.0 fusion.4
  381.0 5.6 fusion.12
  387.9 5.5 fusion.2
  394.5 3.4 collective-permute-done.6
  398.6 29.0 %collective-permute-done.11 = f32[128,2048]{1,0:T(8,128)S(1)} collective-permute-done((f32[128,2048]{1,0:T(8,128)S(1)}, f32[128,2048]{1,0:T(8,128)S(1)}, u32[]{:S(2)}, u32[]{:S(2)}) %collective-permute-start.11) | collective-permute-done | bytes 1048608 | tf_op jit(solution)/shard_map/ppermute | solution.py:75
  428.1 29.3 %collective-permute-done.7 = f32[128,2048]{1,0:T(8,128)S(1)} collective-permute-done((f32[128,2048]{1,0:T(8,128)S(1)}, f32[128,2048]{1,0:T(8,128)S(1)}, u32[]{:S(2)}, u32[]{:S(2)}) %collective-permute-start.7) | collective-permute-done | bytes 1048608 | tf_op jit(solution)/shard_map/ppermute | solution.py:75
  457.4 1.7 fusion.133
  459.6 17.0 %collective-permute-done.12 = bf16[128,2048]{1,0:T(8,128)(2,1)S(1)} collective-permute-done((bf16[128,2048]{1,0:T(8,128)(2,1)S(1)}, bf16[128,2048]{1,0:T(8,128)(2,1)S(1)}, u32[]{:S(2)}, u32[]{:S(2)}) %collective-permute-start.12) | collective-permute-done | bytes 524320 | tf_op jit(solution)/shard_map/ppermute | solution.py:64
  477.1 2.6 collective-permute-done.13
  480.0 4.7 fusion.76
  487.6 3.2 fusion.59
  492.1 3.3 convolution_select_fusion
  497.4 1.9 convolution_bitcast_fusion
  499.3 2.1 multiply_reduce_fusion.1
  510.0 4.2 fusion.19
  514.4 1.7 fusion.77
  518.6 4.4 fusion.18
  523.0 2.7 fusion.17
  525.7 2.7 fusion.16
  528.4 21.0 %collective-permute-done.15 = f32[128,2048]{1,0:T(8,128)} collective-permute-done((f32[128,2048]{1,0:T(8,128)S(1)}, f32[128,2048]{1,0:T(8,128)}, u32[]{:S(2)}, u32[]{:S(2)}) %collective-permute-start.15) | collective-permute-done | bytes 1048608 | tf_op jit(solution)/shard_map/ppermute | solution.py:75
  549.4 2.3 fusion.68
  552.6 7.2 all-to-all-start.1
  559.8 4.2 fusion.15
  564.0 13.9 %copy.92 = bf16[2048,2560]{1,0:T(8,128)(2,1)} copy(bf16[2048,2560]{0,1:T(8,128)(2,1)} %fusion.15) | data formatting | bytes 20971520 | tf_op jit(solution)/shard_map/concatenate | solution.py:204
  578.0 9.8 %all-to-all-start.2 = ((bf16[32,64,2560]{2,1,0:T(8,128)(2,1)}), bf16[32,64,2560]{2,1,0:T(8,128)(2,1)}, u32[]{:S(2)}, u32[]{:S(2)}) async-start(bf16[32,64,2560]{2,1,0:T(8,128)(2,1)} %bitcast.265), calls=%async_computation.2 | async-start | bytes 20971520 | tf_op jit(solution)/shard_map/all_to_all | solution.py:80
  589.7 163.9 %all-to-all-done.2 = bf16[32,64,2560]{2,1,0:T(8,128)(2,1)} async-done(((bf16[32,64,2560]{2,1,0:T(8,128)(2,1)}), bf16[32,64,2560]{2,1,0:T(8,128)(2,1)}, u32[]{:S(2)}, u32[]{:S(2)}) %all-to-all-start.2) | async-done | bytes 10485792 | tf_op jit(solution)/shard_map/all_to_all | solution.py:80
  753.7 5.8 convert_reduce_fusion
  760.3 31.9 %reduce-scatter.4.cloned.1.call-done = bf16[64,4224]{1,0:T(8,128)(2,1)} async-done(((bf16[2048,4224]{1,0:T(8,128)(2,1)}), bf16[64,4224]{1,0:T(8,128)(2,1)}) %reduce-scatter.4.cloned.1.call-update) | async-done | bytes 540688
  792.2 1.8 copy.107
  795.3 2.1 copy.93
  797.4 2.1 copy.94
  (194 shorter events, 49.9 us)
Async XLA Ops:
  7.2 48.7 %copy-start = (s32[1,4,128]{2,1,0:T(4,128)S(1)}, s32[1,4,128]{2,1,0:T(4,128)}, u32[]{:S(2)}) copy-start(s32[1,4,128]{2,1,0:T(4,128)} %param.16) | copy-start | bytes 6148
  7.2 7.2 copy-start.32
  7.2 7.2 copy-start.33
  7.2 7.2 copy-start.34
  7.2 19.1 %copy-start.3 = (bf16[1,1,128,2048]{3,2,1,0:T(8,128)(2,1)S(1)}, bf16[1,1,128,2048]{3,2,1,0:T(8,128)(2,1)}, u32[]{:S(2)}) copy-start(bf16[1,1,128,2048]{3,2,1,0:T(8,128)(2,1)} %param.15) | copy-start | bytes 1572868
  7.2 126.6 %all-gather.3.cloned.1.call-start = ((), (), s32[]{:S(2)}) async-start(), calls=%async_computation.4 | async-start | bytes 10813440 | tf_op jit(solution)/shard_map/all_gather | solution.py:131
  12.3 302.7 %all-gather.5.cloned.1.call-start = ((), (), s32[]{:S(2)}) async-start(), calls=%async_computation.5 | async-start | bytes 17842176 | tf_op jit(solution)/shard_map/all_gather | solution.py:132
  15.1 23.4 %all-to-all-start = ((f32[128,3,16]{2,1,0:T(4,128)}), f32[128,3,16]{2,1,0:T(4,128)S(1)}, u32[]{:S(2)}, u32[]{:S(2)}) async-start(f32[128,3,16]{2,1,0:T(4,128)} %broadcast_in_dim.29), calls=%async_computation | async-start | bytes 524288 | tf_op jit(solution)/shard_map/all_to_all | solution.py:87
  26.3 765.9 %reduce-scatter.4.cloned.1.call-start = ((), (), s32[]{:S(2)}) async-start(), calls=%async_computation.6 | async-start | bytes 17842176
  27.1 28.7 %copy-start.29 = (f32[128]{0:T(128)}, f32[128]{0:T(128)S(1)}, u32[]{:S(2)}) copy-start(f32[128]{0:T(128)S(1)} %get-tuple-element.105) | copy-start | bytes 1540
  39.2 16.6 %copy-start.27 = (f32[2048]{0:T(1024)}, f32[2048]{0:T(1024)S(1)}, u32[]{:S(2)}) copy-start(f32[2048]{0:T(1024)S(1)} %mul.250) | copy-start | bytes 24580
  39.2 16.7 %copy-start.35 = (s32[4]{0:T(128)S(1)}, s32[4]{0:T(128)}, u32[]{:S(2)}) copy-start(s32[4]{0:T(128)} %constant.52.clone) | copy-start | bytes 52
  39.4 16.3 %collective-permute-start = (bf16[128,2048]{1,0:T(8,128)(2,1)S(1)}, bf16[128,2048]{1,0:T(8,128)(2,1)S(1)}, u32[]{:S(2)}, u32[]{:S(2)}) collective-permute-start(bf16[128,2048]{1,0:T(8,128)(2,1)S(1)} %fusion.62), channel_id=1, source_target_pairs={{0,2},{2,0},{1,3},{3,1},{4,6},{6,4},{5,7},{7,5},{8,10},{10,8},{9,1... | collective-permute-start | bytes 1572872 | tf_op jit(solution)/shard_map/ppermute | solution.py:64
  55.7 5.8 copy-start.20
  55.8 2.9 collective-permute-start.1
  149.8 4.5 copy-start.21
  153.4 4.6 copy-start.6
  153.4 2.0 copy-start.19
  157.9 2.5 copy-start.11
  157.9 2.5 copy-start.18
  160.4 2.9 copy-start.5
  172.9 3.1 copy-start.22
  176.0 4.5 copy-start.2
  176.3 5.6 copy-start.8
  176.3 4.2 collective-permute-start.2
  180.7 28.5 %collective-permute-start.3 = (f32[128,2048]{1,0:T(8,128)S(1)}, f32[128,2048]{1,0:T(8,128)}, u32[]{:S(2)}, u32[]{:S(2)}) collective-permute-start(f32[128,2048]{1,0:T(8,128)S(1)} %fusion.88), channel_id=1, source_target_pairs={{0,2},{2,0},{1,3},{3,1},{4,6},{6,4},{5,7},{7,5},{8,10},{10,8},{9,1... | collective-permute-start | bytes 3145736 | tf_op jit(solution)/shard_map/ppermute | solution.py:75
  181.9 43.1 %collective-permute-start.8 = (bf16[128,2048]{1,0:T(8,128)(2,1)S(1)}, bf16[128,2048]{1,0:T(8,128)(2,1)}, u32[]{:S(2)}, u32[]{:S(2)}) collective-permute-start(bf16[128,2048]{1,0:T(8,128)(2,1)S(1)} %bitcast.268), channel_id=1, source_target_pairs={{0,2},{2,0},{1,3},{3,1},{4,6},{6,4},{5,7},{7,5},{8,10},{10,8},{9,1... | collective-permute-start | bytes 1572872 | tf_op jit(solution)/shard_map/ppermute | solution.py:64
  211.6 35.5 %collective-permute-start.4 = (bf16[128,2048]{1,0:T(8,128)(2,1)S(1)}, bf16[128,2048]{1,0:T(8,128)(2,1)S(1)}, u32[]{:S(2)}, u32[]{:S(2)}) collective-permute-start(bf16[128,2048]{1,0:T(8,128)(2,1)S(1)} %multiply_convert_fusion.4), channel_id=1, source_target_pairs={{0,2},{2,0},{1,3},{3,1},{4,6},{6,4},{5,7},{7,5},{8,10},{10,8},{9,1... | collective-permute-start | bytes 1572872 | tf_op jit(solution)/shard_map/ppermute | solution.py:64
  226.1 21.1 %collective-permute-start.9 = (bf16[2,128,2048]{2,1,0:T(8,128)(2,1)S(1)}, bf16[2,128,2048]{2,1,0:T(8,128)(2,1)S(1)}, u32[]{:S(2)}, u32[]{:S(2)}) collective-permute-start(bf16[2,128,2048]{2,1,0:T(8,128)(2,1)S(1)} %pad_maximum_fusion.7), channel_id=1, source_target_pairs={{0,1},{1,0},{2,3},{3,2},{4,5},{5,4},{6,7},{7,6},{8,9},{9,8},{10,11... | collective-permute-start | bytes 3145736 | tf_op jit(solution)/shard_map/ppermute | solution.py:66
  247.1 2.7 collective-permute-start.5
  315.0 7.0 copy-start.17
  315.0 8.9 %copy-start.36 = (bf16[2048,4224]{1,0:T(8,128)(2,1)S(1)}, bf16[2048,4224]{1,0:T(8,128)(2,1)}, u32[]{:S(2)}) copy-start(bf16[2048,4224]{1,0:T(8,128)(2,1)} %all-gather.5.cloned.1.call-done) | copy-start | bytes 51904516
  327.3 7.4 copy-start.16
  334.7 3.5 copy-start.40
  334.7 3.5 copy-start.42
  334.7 7.0 copy-start.37
  374.9 6.0 copy-start.38
  386.6 1.4 copy-start.41
  386.8 6.9 collective-permute-start.10
  393.6 4.2 collective-permute-start.6
  393.8 33.8 %collective-permute-start.11 = (f32[128,2048]{1,0:T(8,128)S(1)}, f32[128,2048]{1,0:T(8,128)S(1)}, u32[]{:S(2)}, u32[]{:S(2)}) collective-permute-start(f32[128,2048]{1,0:T(8,128)S(1)} %fusion.80), channel_id=1, source_target_pairs={{0,2},{2,0},{1,3},{3,1},{4,6},{6,4},{5,7},{7,5},{8,10},{10,8},{9,1... | collective-permute-start | bytes 3145736 | tf_op jit(solution)/shard_map/ppermute | solution.py:75
  398.0 59.4 %collective-permute-start.7 = (f32[128,2048]{1,0:T(8,128)S(1)}, f32[128,2048]{1,0:T(8,128)S(1)}, u32[]{:S(2)}, u32[]{:S(2)}) collective-permute-start(f32[128,2048]{1,0:T(8,128)S(1)} %fusion.83), channel_id=1, source_target_pairs={{0,2},{2,0},{1,3},{3,1},{4,6},{6,4},{5,7},{7,5},{8,10},{10,8},{9,1... | collective-permute-start | bytes 3145736 | tf_op jit(solution)/shard_map/ppermute | solution.py:75
  459.1 17.6 %collective-permute-start.12 = (bf16[128,2048]{1,0:T(8,128)(2,1)S(1)}, bf16[128,2048]{1,0:T(8,128)(2,1)S(1)}, u32[]{:S(2)}, u32[]{:S(2)}) collective-permute-start(bf16[128,2048]{1,0:T(8,128)(2,1)S(1)} %get-tuple-element.75), channel_id=1, source_target_pairs={{0,2},{2,0},{1,3},{3,1},{4,6},{6,4},{5,7},{7,5},{8,10},{10,8},{9,1... | collective-permute-start | bytes 1572872 | tf_op jit(solution)/shard_map/ppermute | solution.py:64
  476.7 3.2 copy-start.24
  476.8 3.2 copy-start.39
  476.8 3.0 collective-permute-start.13
  479.9 4.8 copy-start.15
  492.1 3.3 copy-start.7
  495.4 1.9 copy-start.12
  495.5 6.5 slice-start
  497.4 4.5 slice-start.1
  499.3 2.6 slice-start.2
  507.2 2.7 copy-start.4
  509.9 4.5 collective-permute-start.14
  516.1 33.3 %collective-permute-start.15 = (f32[128,2048]{1,0:T(8,128)S(1)}, f32[128,2048]{1,0:T(8,128)}, u32[]{:S(2)}, u32[]{:S(2)}) collective-permute-start(f32[128,2048]{1,0:T(8,128)S(1)} %fusion.77), channel_id=1, source_target_pairs={{0,2},{2,0},{1,3},{3,1},{4,6},{6,4},{5,7},{7,5},{8,10},{10,8},{9,1... | collective-permute-start | bytes 3145736 | tf_op jit(solution)/shard_map/ppermute | solution.py:75
  518.5 4.4 copy-start.14
  525.7 23.7 %copy-start.28 = (f32[2048]{0:T(1024)S(1)}, f32[2048]{0:T(1024)}, u32[]{:S(2)}) copy-start(f32[2048]{0:T(1024)} %copy-done.27) | copy-start | bytes 24580
  525.7 23.7 %copy-start.30 = (f32[128]{0:T(128)S(1)}, f32[128]{0:T(128)}, u32[]{:S(2)}) copy-start(f32[128]{0:T(128)} %copy-done.29) | copy-start | bytes 1540
  528.4 31.4 %copy-start.23 = (bf16[512,512]{1,0:T(8,128)(2,1)S(1)}, bf16[512,512]{1,0:T(8,128)(2,1)}, u32[]{:S(2)}) copy-start(bf16[512,512]{1,0:T(8,128)(2,1)} %copy-done.22) | copy-start | bytes 1572868
  552.6 25.4 %all-to-all-start.1 = ((f32[128,3,16]{2,1,0:T(4,128)}), f32[128,3,16]{2,1,0:T(4,128)S(1)}, u32[]{:S(2)}, u32[]{:S(2)}) async-start(f32[128,3,16]{2,1,0:T(4,128)} %copy.91), calls=%async_computation.1 | async-start | bytes 524288 | tf_op jit(solution)/shard_map/all_to_all | solution.py:94
  577.9 9.8 %copy-start.10 = (f32[128,2048]{1,0:T(8,128)S(1)}, f32[128,2048]{1,0:T(8,128)}, u32[]{:S(2)}) copy-start(f32[128,2048]{1,0:T(8,128)} %get-tuple-element.76) | copy-start | bytes 3145732
  578.0 9.8 %copy-start.31 = (f32[128]{0:T(128)S(1)}, f32[128]{0:T(128)}, u32[]{:S(2)}) copy-start(f32[128]{0:T(128)} %get-tuple-element.104) | copy-start | bytes 1540
  578.0 175.7 %all-to-all-start.2 = ((bf16[32,64,2560]{2,1,0:T(8,128)(2,1)}), bf16[32,64,2560]{2,1,0:T(8,128)(2,1)}, u32[]{:S(2)}, u32[]{:S(2)}) async-start(bf16[32,64,2560]{2,1,0:T(8,128)(2,1)} %bitcast.265), calls=%async_computation.2 | async-start | bytes 20971520 | tf_op jit(solution)/shard_map/all_to_all | solution.py:80
  795.3 5.3 copy-start.1
  (4 other events, 4.3 us)
Sparse Core Ops, SparseCore 0:
  12.4 121.4 all-gather.2
  136.9 177.9 all-gather.4
  375.0 417.0 reduce-scatter.3

commit v5 on v4

--- a/solution.py
+++ b/solution.py
@@ -1,6 +1,10 @@
+import functools
+
 import jax
 import jax.numpy as jnp
 from jax import lax
+from jax.experimental import pallas as pl
+from jax.experimental.pallas import tpu as pltpu
 from jax.sharding import PartitionSpec as P
 
 HK = 128
@@ -33,6 +37,46 @@
     return lax.dot_general(
         left, right, (((0,), (0,)), ((), ())), preferred_element_type=jnp.float32
     )
+
+
+def pack_kernel(per, first_ref, second_ref, right_ref, out_ref):
+    col = pl.program_id(1)
+
+    @pl.when(col < per)
+    def _():
+        out_ref[...] = jnp.dot(
+            first_ref[...].T, right_ref[...], preferred_element_type=jnp.float32
+        ).astype(out_ref.dtype)
+
+    @pl.when(col >= per)
+    def _():
+        out_ref[...] = jnp.dot(
+            second_ref[...].T, right_ref[...], preferred_element_type=jnp.float32
+        ).astype(out_ref.dtype)
+
+
+def grad_pack(first, second, right, width):
+    depth, rows_out = first.shape
+    cols = right.shape[1]
+    blocks = cols // width
+    per = blocks - 1
+    tile = 512
+    return pl.pallas_call(
+        functools.partial(pack_kernel, per),
+        grid=(rows_out // tile, blocks),
+        in_specs=[
+            pl.BlockSpec((depth, tile), lambda i, j: (0, i)),
+            pl.BlockSpec((depth, tile), lambda i, j: (0, i)),
+            pl.BlockSpec((depth, width), lambda i, j: (0, j)),
+        ],
+        out_specs=pl.BlockSpec((tile, width), lambda i, j: (i, j)),
+        out_shape=jax.ShapeDtypeStruct((rows_out, cols), jnp.bfloat16),
+        cost_estimate=pl.CostEstimate(
+            flops=2 * depth * rows_out * cols,
+            transcendentals=0,
+            bytes_accessed=2 * (2 * depth * rows_out + depth * cols + rows_out * cols),
+        ),
+    )(first, second, right)
 
 
 def recurrence(query, forget_raw, value, floor_vec, doc_rows):
@@ -170,14 +214,10 @@
     layer_out = (resid + ffn_out).astype(jnp.bfloat16).reshape(tokens.shape)
     cot_full = row_gather(cot_local)
     d_hidden = matmul_plain(cot_full, wdown_t)
-    grad_down_t = trans_times(cot_full, hidden)
     d_gate = (d_hidden * up_proj * silu_slope(gate_proj)).astype(jnp.bfloat16)
     d_up = (d_hidden * gate_silu).astype(jnp.bfloat16)
-    grad_gate = trans_times(normed2, d_gate)
-    grad_up = trans_times(normed2, d_up)
-    mlp_grads = jnp.concatenate(
-        [grad_gate.astype(jnp.bfloat16), grad_up.astype(jnp.bfloat16), grad_down_t.astype(jnp.bfloat16)],
-        axis=1,
+    mlp_grads = grad_pack(
+        normed2, cot_full, jnp.concatenate([d_gate, d_up, hidden], axis=1), hidden_width
     )
     mlp_red = lax.psum_scatter(mlp_grads, "dp", scatter_dimension=0, tiled=True).astype(jnp.float32)
     d_normed2 = row_sum(times_trans(d_gate, wgate_all) + times_trans(d_up, wup_all))
@@ -190,26 +230,17 @@
     )
     d_branch = row_gather(d_resid.astype(jnp.bfloat16))
     d_gated = matmul_plain(d_branch, wo_t)
-    grad_output_t = trans_times(d_branch, gated)
     d_mixed = d_gated * gate_act
     d_outgate = (d_gated * mixed * silu_slope(out_gate)).astype(jnp.bfloat16)
     d_query, d_forget, d_value, d_floor = pullback(d_mixed)
     d_query = d_query.astype(jnp.bfloat16)
     d_forget = d_forget.astype(jnp.bfloat16)
     d_value = d_value.astype(jnp.bfloat16)
-    grad_query = trans_times(normed, d_query)
-    grad_forget = trans_times(normed, d_forget)
-    grad_value = trans_times(normed, d_value)
-    grad_outgate = trans_times(normed, d_outgate)
-    attn_grads = jnp.concatenate(
-        [
-            grad_query.astype(jnp.bfloat16),
-            grad_forget.astype(jnp.bfloat16),
-            grad_value.astype(jnp.bfloat16),
-            grad_outgate.astype(jnp.bfloat16),
-            grad_output_t.astype(jnp.bfloat16),
-        ],
-        axis=1,
+    attn_grads = grad_pack(
+        normed,
+        d_branch,
+        jnp.concatenate([d_query, d_forget, d_value, d_outgate, gated], axis=1),
+        local_width,
     )
     attn_red = spread_sum(attn_grads, "dp", 32)
     d_normed = row_sum(

time: 813 us -> 800 us (0.984)
  Pallas kernels: 0 us -> 40.7 us
  local copies, waits for them, and re-layouts: 86.1 us -> 45.4 us
  matrix products: 108 us -> 82.9 us
  waiting for transfers between devices: 527 us -> 543 us
    pallas_call x0 -> x2, Pallas kernels: none -> 40.7 us  [grad_pack(): pl.pallas_call(functools.partial(pack_kernel, per), grid=(rows_out // til...]
    reduce_scatter x0 -> x1, waiting for transfers between devices: none -> 37.9 us  [shards(): lax.psum_scatter(mlp_grads, 'dp', scatter_dimension=0, tiled=True)]
    unnamed x4 -> x3, waiting for transfers between devices: 31.9 us -> 0.05 us
    dot_general x8 -> x0, matrix products: 28.6 us -> none  [trans_times(): lax.dot_general(left, right, (((0,), (0,)), ((), ())), preferred_element_...]
    unnamed x101 -> x85, local copies, waits for them, and re-layouts: 40.4 us -> 12.1 us
    concatenate x1, local copies, waits for them, and re-layouts: 13.9 us -> 0.85 us  [shards(): jnp.concatenate([d_query, d_forget, d_value, d_outgate, gated], axis=1)]
    ppermute x4, waiting for transfers between devices: 106 us -> 114 us  [row_sum(): return mine + lax.ppermute(theirs, 'tensor', ACROSS)]
  transfers between devices with their start and end apart: 22 -> 22, of which waited for: 19 -> 18; matrix products, arithmetic and copies ran while one was open for 19% -> 16% of each run, Pallas kernels for 0% -> 3%
where the time goes in v5:
time: 800 us; the launch traced here: 795 us
  waiting for transfers between devices  543 us (68%)
  matrix products  82.9 us (10%)
  local copies, waits for them, and re-layouts  45.4 us (6%)
  Pallas kernels  40.7 us (5%)
  starting transfers between devices  35 us (4%)
  other arithmetic  32.7 us (4%)
  between operations  14.9 us (2%)
    all_to_all x1, waiting for transfers between devices, spread_sum(): got = lax.all_to_all(blocks, axis, 0, 0, tiled=False)  162 us
    ppermute x4, waiting for transfers between devices, row_sum(): return mine + lax.ppermute(theirs, 'tensor', ACROSS)  114 us
    all_gather x1, waiting for transfers between devices, shards(): attn_all = lax.all_gather(attn_pack, 'dp', axis=0, tiled=True)  71.8 us
    ppermute x4, waiting for transfers between devices, row_gather(): across = lax.ppermute(values, 'tensor', ACROSS)  67.2 us
    all_gather x1, waiting for transfers between devices, shards(): mlp_all = lax.all_gather(mlp_pack, 'dp', axis=0, tiled=True)  62.8 us
    pallas_call x2, Pallas kernels, grad_pack(): pl.pallas_call(functools.partial(pack_kernel, per), grid=(rows_out // til...  40.7 us
    dot_general x8, matrix products, matmul_plain(): return jnp.dot(left, right, preferred_element_type=jnp.float32)  39.1 us
    reduce_scatter x1, waiting for transfers between devices, shards(): lax.psum_scatter(mlp_grads, 'dp', scatter_dimension=0, tiled=True)  37.9 us
  transfers between devices with their start and end apart: 22, of which 18 were waited for; matrix products, arithmetic and copies ran while one was open for 16% of the time, Pallas kernels for 3%

profile of v5, /device:TPU:0, one launch (start us, length us, event | category | flops | bytes accessed | tf_op | source)
XLA Modules:
  0.0 794.5 jit_solution(1963365905374166089)
XLA Ops:
  12.3 1.9 pad_maximum_fusion.9
  15.7 11.1 %all-to-all-start = ((f32[128,3,16]{2,1,0:T(4,128)}), f32[128,3,16]{2,1,0:T(4,128)S(1)}, u32[]{:S(2)}, u32[]{:S(2)}) async-start(f32[128,3,16]{2,1,0:T(4,128)} %broadcast_in_dim.29), calls=%async_computation | async-start | bytes 524288 | tf_op jit(solution)/shard_map/all_to_all | solution.py:131
  27.7 11.2 %all-to-all-done = f32[128,3,16]{2,1,0:T(4,128)S(1)} async-done(((f32[128,3,16]{2,1,0:T(4,128)}), f32[128,3,16]{2,1,0:T(4,128)S(1)}, u32[]{:S(2)}, u32[]{:S(2)}) %all-to-all-start) | async-done | bytes 24608 | tf_op jit(solution)/shard_map/all_to_all | solution.py:131
  40.5 15.8 %collective-permute-done = bf16[128,2048]{1,0:T(8,128)(2,1)S(1)} collective-permute-done((bf16[128,2048]{1,0:T(8,128)(2,1)S(1)}, bf16[128,2048]{1,0:T(8,128)(2,1)S(1)}, u32[]{:S(2)}, u32[]{:S(2)}) %collective-permute-start) | collective-permute-done | bytes 524320 | tf_op jit(solution)/shard_map/ppermute | solution.py:108
  57.8 1.4 collective-permute-done.1
  59.2 2.8 pad_maximum_fusion.1
  62.0 71.8 %all-gather.3.cloned.1.call-done = bf16[2048,2560]{1,0:T(8,128)(2,1)} async-done(((bf16[64,2560]{1,0:T(8,128)(2,1)}), bf16[2048,2560]{1,0:T(8,128)(2,1)}) %all-gather.3.cloned.1.call-update) | async-done | bytes 10485776 | tf_op jit(solution)/shard_map/all_gather | solution.py:175
  133.8 5.3 slice_bitcast_fusion
  139.1 4.1 copy.86
  143.2 4.0 copy.88
  147.2 2.5 copy.89
  149.7 3.7 fusion.51
  154.3 2.5 fusion.18
  156.9 2.5 convolution_select_fusion.1
  159.4 2.9 fusion.20
  162.4 2.9 convolution_bitcast_fusion.2
  165.3 2.6 copy.92
  167.8 5.4 fusion.69
  173.2 3.1 fusion.24
  176.6 4.1 collective-permute-done.2
  182.1 1.3 collective-permute-start.8
  183.5 25.5 %collective-permute-done.3 = f32[128,2048]{1,0:T(8,128)} collective-permute-done((f32[128,2048]{1,0:T(8,128)S(1)}, f32[128,2048]{1,0:T(8,128)}, u32[]{:S(2)}, u32[]{:S(2)}) %collective-permute-start.3) | collective-permute-done | bytes 1048608 | tf_op jit(solution)/shard_map/ppermute | solution.py:119
  209.1 2.3 multiply_reduce_fusion.3
  211.9 13.8 %collective-permute-done.8 = bf16[128,2048]{1,0:T(8,128)(2,1)} collective-permute-done((bf16[128,2048]{1,0:T(8,128)(2,1)S(1)}, bf16[128,2048]{1,0:T(8,128)(2,1)}, u32[]{:S(2)}, u32[]{:S(2)}) %collective-permute-start.8) | collective-permute-done | bytes 524320 | tf_op jit(solution)/shard_map/ppermute | solution.py:108
  227.0 20.7 %collective-permute-done.4 = bf16[128,2048]{1,0:T(8,128)(2,1)S(1)} collective-permute-done((bf16[128,2048]{1,0:T(8,128)(2,1)S(1)}, bf16[128,2048]{1,0:T(8,128)(2,1)S(1)}, u32[]{:S(2)}, u32[]{:S(2)}) %collective-permute-start.4) | collective-permute-done | bytes 524320 | tf_op jit(solution)/shard_map/ppermute | solution.py:108
  247.9 2.6 pad_maximum_fusion.3
  250.6 1.5 pad_maximum_fusion.2
  252.1 62.8 %all-gather.5.cloned.1.call-done = bf16[2048,4224]{1,0:T(8,128)(2,1)} async-done(((bf16[64,4224]{1,0:T(8,128)(2,1)}), bf16[2048,4224]{1,0:T(8,128)(2,1)}) %all-gather.5.cloned.1.call-update) | async-done | bytes 17301520 | tf_op jit(solution)/shard_map/all_gather | solution.py:176
  314.9 8.4 %fusion = f32[512,1408]{1,0:T(8,128)} fusion(bf16[512,2048]{1,0:T(8,128)(2,1)} %bitcast.269, bf16[2048,4224]{1,0:T(8,128)(2,1)} %all-gather.5.cloned.1.call-done), kind=kOutput, calls=%fused_computation.2 | convolution fusion | flops 2952790016 | bytes 10747904 | tf_op jit(solution)/shard_map/dot_general | solution.py:27
  323.3 1.5 copy-done.35
  324.8 5.0 fusion.6
  329.8 6.6 multiply_convert_fusion.1
  338.5 2.1 pad_maximum_fusion.right_ref
  340.6 20.8 %shard_map.247 = bf16[2048,4224]{1,0:T(8,128)(2,1)} custom-call(bf16[512,2048]{1,0:T(8,128)(2,1)} %bitcast.271, bf16[512,2048]{1,0:T(8,128)(2,1)} %bitcast.270, bf16[512,4224]{1,0:T(8,128)(2,1)} %pad_maximum_fusion.right_ref), custom_call_target="tpu_custom_call" | custom-call | flops 8858370048 | bytes 25821184 | tf_op jit(solution)/shard_map/pallas_call | solution.py:64
  361.4 6.0 fusion.4
  367.5 5.6 fusion.12
  374.4 5.5 fusion.2
  381.0 3.4 collective-permute-done.6
  385.1 29.0 %collective-permute-done.11 = f32[128,2048]{1,0:T(8,128)S(1)} collective-permute-done((f32[128,2048]{1,0:T(8,128)S(1)}, f32[128,2048]{1,0:T(8,128)S(1)}, u32[]{:S(2)}, u32[]{:S(2)}) %collective-permute-start.11) | collective-permute-done | bytes 1048608 | tf_op jit(solution)/shard_map/ppermute | solution.py:119
  414.6 29.3 %collective-permute-done.7 = f32[128,2048]{1,0:T(8,128)S(1)} collective-permute-done((f32[128,2048]{1,0:T(8,128)S(1)}, f32[128,2048]{1,0:T(8,128)S(1)}, u32[]{:S(2)}, u32[]{:S(2)}) %collective-permute-start.7) | collective-permute-done | bytes 1048608 | tf_op jit(solution)/shard_map/ppermute | solution.py:119
  443.9 1.7 fusion.123
  446.1 16.9 %collective-permute-done.12 = bf16[128,2048]{1,0:T(8,128)(2,1)S(1)} collective-permute-done((bf16[128,2048]{1,0:T(8,128)(2,1)S(1)}, bf16[128,2048]{1,0:T(8,128)(2,1)S(1)}, u32[]{:S(2)}, u32[]{:S(2)}) %collective-permute-start.12) | collective-permute-done | bytes 524320 | tf_op jit(solution)/shard_map/ppermute | solution.py:108
  463.5 2.6 collective-permute-done.13
  466.3 4.6 fusion.115
  472.3 1.6 copy.116
  473.9 3.2 fusion.54
  477.0 1.4 copy.101
  478.4 3.3 convolution_select_fusion
  481.8 1.5 multiply_convert_fusion.3
  483.7 1.9 convolution_bitcast_fusion
  485.6 2.1 multiply_reduce_fusion.1
  490.9 1.4 constant_dynamic-update-slice_fusion.5
  496.2 1.3 add_add_fusion
  497.9 4.1 collective-permute-done.14
  505.7 30.1 %collective-permute-done.15 = f32[128,2048]{1,0:T(8,128)} collective-permute-done((f32[128,2048]{1,0:T(8,128)S(1)}, f32[128,2048]{1,0:T(8,128)}, u32[]{:S(2)}, u32[]{:S(2)}) %collective-permute-start.15) | collective-permute-done | bytes 1048608 | tf_op jit(solution)/shard_map/ppermute | solution.py:119
  535.8 2.3 fusion.63
  539.0 6.7 all-to-all-start.1
  545.8 19.9 %shard_map.246 = bf16[2048,2560]{1,0:T(8,128)(2,1)} custom-call(bf16[512,2048]{1,0:T(8,128)(2,1)} %bitcast.266, bf16[512,2048]{1,0:T(8,128)(2,1)} %bitcast.268, bf16[512,2560]{1,0:T(8,128)(2,1)} %constant_dynamic-update-slice_fusion.4.right_ref), custom_call_target="tpu_custom_call" | custom-call | flops 5368709120 | bytes 17301504 | tf_op jit(solution)/shard_map/pallas_call | solution.py:64
  565.7 10.1 %all-to-all-start.2 = ((bf16[32,64,2560]{2,1,0:T(8,128)(2,1)}), bf16[32,64,2560]{2,1,0:T(8,128)(2,1)}, u32[]{:S(2)}, u32[]{:S(2)}) async-start(bf16[32,64,2560]{2,1,0:T(8,128)(2,1)} %bitcast.251), calls=%async_computation.2 | async-start | bytes 20971520 | tf_op jit(solution)/shard_map/all_to_all | solution.py:124
  575.8 1.3 fusion.60
  577.8 162.3 %all-to-all-done.2 = bf16[32,64,2560]{2,1,0:T(8,128)(2,1)} async-done(((bf16[32,64,2560]{2,1,0:T(8,128)(2,1)}), bf16[32,64,2560]{2,1,0:T(8,128)(2,1)}, u32[]{:S(2)}, u32[]{:S(2)}) %all-to-all-start.2) | async-done | bytes 10485792 | tf_op jit(solution)/shard_map/all_to_all | solution.py:124
  740.1 5.7 convert_reduce_fusion
  746.7 37.9 %reduce-scatter.2.cloned.1.call-done = bf16[64,4224]{1,0:T(8,128)(2,1)} async-done(((bf16[2048,4224]{1,0:T(8,128)(2,1)}), bf16[64,4224]{1,0:T(8,128)(2,1)}) %reduce-scatter.2.cloned.1.call-update) | async-done | bytes 540688 | tf_op jit(solution)/shard_map/reduce_scatter | solution.py:222
  785.7 2.0 fusion.126
  (172 shorter events, 38.2 us)
Async XLA Ops:
  7.2 49.3 %copy-start = (s32[1,4,128]{2,1,0:T(4,128)S(1)}, s32[1,4,128]{2,1,0:T(4,128)}, u32[]{:S(2)}) copy-start(s32[1,4,128]{2,1,0:T(4,128)} %param.16) | copy-start | bytes 6148
  7.2 19.7 %copy-start.3 = (bf16[1,1,128,2048]{3,2,1,0:T(8,128)(2,1)S(1)}, bf16[1,1,128,2048]{3,2,1,0:T(8,128)(2,1)}, u32[]{:S(2)}) copy-start(bf16[1,1,128,2048]{3,2,1,0:T(8,128)(2,1)} %param.15) | copy-start | bytes 1572868
  7.2 126.6 %all-gather.3.cloned.1.call-start = ((), (), s32[]{:S(2)}) async-start(), calls=%async_computation.4 | async-start | bytes 10813440 | tf_op jit(solution)/shard_map/all_gather | solution.py:175
  11.5 0.7 copy-start.32
  12.3 302.6 %all-gather.5.cloned.1.call-start = ((), (), s32[]{:S(2)}) async-start(), calls=%async_computation.5 | async-start | bytes 17842176 | tf_op jit(solution)/shard_map/all_gather | solution.py:176
  15.7 23.1 %all-to-all-start = ((f32[128,3,16]{2,1,0:T(4,128)}), f32[128,3,16]{2,1,0:T(4,128)S(1)}, u32[]{:S(2)}, u32[]{:S(2)}) async-start(f32[128,3,16]{2,1,0:T(4,128)} %broadcast_in_dim.29), calls=%async_computation | async-start | bytes 524288 | tf_op jit(solution)/shard_map/all_to_all | solution.py:131
  26.9 29.6 %copy-start.34 = (s32[4]{0:T(128)S(1)}, s32[4]{0:T(128)}, u32[]{:S(2)}) copy-start(s32[4]{0:T(128)} %constant.52.clone) | copy-start | bytes 52
  26.9 757.7 %reduce-scatter.2.cloned.1.call-start = ((), (), s32[]{:S(2)}) async-start(), calls=%async_computation.6 | async-start | bytes 17842176 | tf_op jit(solution)/shard_map/reduce_scatter | solution.py:222
  39.7 16.6 %collective-permute-start = (bf16[128,2048]{1,0:T(8,128)(2,1)S(1)}, bf16[128,2048]{1,0:T(8,128)(2,1)S(1)}, u32[]{:S(2)}, u32[]{:S(2)}) collective-permute-start(bf16[128,2048]{1,0:T(8,128)(2,1)S(1)} %fusion.57), channel_id=1, source_target_pairs={{0,2},{2,0},{1,3},{3,1},{4,6},{6,4},{5,7},{7,5},{8,10},{10,8},{9,1... | collective-permute-start | bytes 1572872 | tf_op jit(solution)/shard_map/ppermute | solution.py:108
  56.3 5.7 copy-start.22
  56.4 2.9 collective-permute-start.1
  149.7 4.6 copy-start.21
  149.7 4.6 copy-start.23
  153.4 3.5 copy-start.6
  156.9 2.5 copy-start.12
  156.9 2.5 copy-start.20
  159.4 2.9 copy-start.5
  162.4 5.5 copy-start.9
  173.2 3.1 copy-start.14
  176.3 4.6 copy-start.2
  176.5 5.6 copy-start.8
  176.6 4.2 collective-permute-start.2
  180.8 1.3 copy-start.16
  180.9 28.1 %collective-permute-start.3 = (f32[128,2048]{1,0:T(8,128)S(1)}, f32[128,2048]{1,0:T(8,128)}, u32[]{:S(2)}, u32[]{:S(2)}) collective-permute-start(f32[128,2048]{1,0:T(8,128)S(1)} %fusion.83), channel_id=1, source_target_pairs={{0,2},{2,0},{1,3},{3,1},{4,6},{6,4},{5,7},{7,5},{8,10},{10,8},{9,1... | collective-permute-start | bytes 3145736 | tf_op jit(solution)/shard_map/ppermute | solution.py:119
  182.1 43.5 %collective-permute-start.8 = (bf16[128,2048]{1,0:T(8,128)(2,1)S(1)}, bf16[128,2048]{1,0:T(8,128)(2,1)}, u32[]{:S(2)}, u32[]{:S(2)}) collective-permute-start(bf16[128,2048]{1,0:T(8,128)(2,1)S(1)} %bitcast.258), channel_id=1, source_target_pairs={{0,2},{2,0},{1,3},{3,1},{4,6},{6,4},{5,7},{7,5},{8,10},{10,8},{9,1... | collective-permute-start | bytes 1572872 | tf_op jit(solution)/shard_map/ppermute | solution.py:108
  211.5 36.2 %collective-permute-start.4 = (bf16[128,2048]{1,0:T(8,128)(2,1)S(1)}, bf16[128,2048]{1,0:T(8,128)(2,1)S(1)}, u32[]{:S(2)}, u32[]{:S(2)}) collective-permute-start(bf16[128,2048]{1,0:T(8,128)(2,1)S(1)} %multiply_convert_fusion.4), channel_id=1, source_target_pairs={{0,2},{2,0},{1,3},{3,1},{4,6},{6,4},{5,7},{7,5},{8,10},{10,8},{9,1... | collective-permute-start | bytes 1572872 | tf_op jit(solution)/shard_map/ppermute | solution.py:108
  226.8 21.1 %collective-permute-start.9 = (bf16[2,128,2048]{2,1,0:T(8,128)(2,1)S(1)}, bf16[2,128,2048]{2,1,0:T(8,128)(2,1)S(1)}, u32[]{:S(2)}, u32[]{:S(2)}) collective-permute-start(bf16[2,128,2048]{2,1,0:T(8,128)(2,1)S(1)} %pad_maximum_fusion.7), channel_id=1, source_target_pairs={{0,1},{1,0},{2,3},{3,2},{4,5},{5,4},{6,7},{7,6},{8,9},{9,8},{10,11... | collective-permute-start | bytes 3145736 | tf_op jit(solution)/shard_map/ppermute | solution.py:110
  247.8 2.7 collective-permute-start.5
  314.9 8.4 %copy-start.19 = (bf16[4,128,2048]{2,1,0:T(8,128)(2,1)S(1)}, bf16[4,128,2048]{2,1,0:T(8,128)(2,1)}, u32[]{:S(2)}) copy-start(bf16[4,128,2048]{2,1,0:T(8,128)(2,1)} %pad_maximum_fusion.2) | copy-start | bytes 6291460
  314.9 9.9 %copy-start.35 = (bf16[2048,4224]{1,0:T(8,128)(2,1)S(1)}, bf16[2048,4224]{1,0:T(8,128)(2,1)}, u32[]{:S(2)}) copy-start(bf16[2048,4224]{1,0:T(8,128)(2,1)} %all-gather.5.cloned.1.call-done) | copy-start | bytes 51904516
  336.5 1.1 copy-start.24
  336.5 1.6 copy-start.26
  336.5 2.0 copy-start.28
  361.4 6.0 copy-start.27
  373.1 1.4 copy-start.25
  373.3 6.9 collective-permute-start.10
  380.1 4.2 collective-permute-start.6
  380.3 33.8 %collective-permute-start.11 = (f32[128,2048]{1,0:T(8,128)S(1)}, f32[128,2048]{1,0:T(8,128)S(1)}, u32[]{:S(2)}, u32[]{:S(2)}) collective-permute-start(f32[128,2048]{1,0:T(8,128)S(1)} %fusion.75), channel_id=1, source_target_pairs={{0,2},{2,0},{1,3},{3,1},{4,6},{6,4},{5,7},{7,5},{8,10},{10,8},{9,1... | collective-permute-start | bytes 3145736 | tf_op jit(solution)/shard_map/ppermute | solution.py:119
  384.5 59.4 %collective-permute-start.7 = (f32[128,2048]{1,0:T(8,128)S(1)}, f32[128,2048]{1,0:T(8,128)S(1)}, u32[]{:S(2)}, u32[]{:S(2)}) collective-permute-start(f32[128,2048]{1,0:T(8,128)S(1)} %fusion.78), channel_id=1, source_target_pairs={{0,2},{2,0},{1,3},{3,1},{4,6},{6,4},{5,7},{7,5},{8,10},{10,8},{9,1... | collective-permute-start | bytes 3145736 | tf_op jit(solution)/shard_map/ppermute | solution.py:119
  445.6 17.5 %collective-permute-start.12 = (bf16[128,2048]{1,0:T(8,128)(2,1)S(1)}, bf16[128,2048]{1,0:T(8,128)(2,1)S(1)}, u32[]{:S(2)}, u32[]{:S(2)}) collective-permute-start(bf16[128,2048]{1,0:T(8,128)(2,1)S(1)} %get-tuple-element.25), channel_id=1, source_target_pairs={{0,2},{2,0},{1,3},{3,1},{4,6},{6,4},{5,7},{7,5},{8,10},{10,8},{9,1... | collective-permute-start | bytes 1572872 | tf_op jit(solution)/shard_map/ppermute | solution.py:108
  463.2 3.1 copy-start.29
  463.2 2.9 collective-permute-start.13
  466.3 4.6 copy-start.17
  478.4 3.3 copy-start.7
  481.7 1.9 copy-start.13
  483.3 9.1 %slice-start = ((s8[10485760]{0:T(1024)(128)(4,1)}), s8[4194304]{0:T(1024)(128)(4,1)S(1)}, s32[]{:S(2)}) async-start(s8[10485760]{0:T(1024)(128)(4,1)} %bitcast.249), calls=%async_computation.7 | async-start | bytes 8388608
  485.6 6.7 slice-start.1
  487.7 3.2 copy-start.11
  487.8 3.2 copy-start.30
  487.8 3.1 copy-start.31
  487.8 4.5 slice-start.2
  497.6 4.6 copy-start.4
  497.8 7.1 copy-start.15
  497.8 4.2 collective-permute-start.14
  502.0 1.4 copy-start.18
  502.2 33.6 %collective-permute-start.15 = (f32[128,2048]{1,0:T(8,128)S(1)}, f32[128,2048]{1,0:T(8,128)}, u32[]{:S(2)}, u32[]{:S(2)}) collective-permute-start(f32[128,2048]{1,0:T(8,128)S(1)} %fusion.72), channel_id=1, source_target_pairs={{0,2},{2,0},{1,3},{3,1},{4,6},{6,4},{5,7},{7,5},{8,10},{10,8},{9,1... | collective-permute-start | bytes 3145736 | tf_op jit(solution)/shard_map/ppermute | solution.py:119
  539.0 26.7 %all-to-all-start.1 = ((f32[128,3,16]{2,1,0:T(4,128)}), f32[128,3,16]{2,1,0:T(4,128)S(1)}, u32[]{:S(2)}, u32[]{:S(2)}) async-start(f32[128,3,16]{2,1,0:T(4,128)} %copy.104), calls=%async_computation.1 | async-start | bytes 524288 | tf_op jit(solution)/shard_map/all_to_all | solution.py:138
  565.7 10.1 %copy-start.10 = (f32[128,2048]{1,0:T(8,128)S(1)}, f32[128,2048]{1,0:T(8,128)}, u32[]{:S(2)}) copy-start(f32[128,2048]{1,0:T(8,128)} %get-tuple-element.26) | copy-start | bytes 3145732
  565.7 10.1 %copy-start.33 = (f32[128]{0:T(128)S(1)}, f32[128]{0:T(128)}, u32[]{:S(2)}) copy-start(f32[128]{0:T(128)} %get-tuple-element.52) | copy-start | bytes 1540
  565.7 174.4 %all-to-all-start.2 = ((bf16[32,64,2560]{2,1,0:T(8,128)(2,1)}), bf16[32,64,2560]{2,1,0:T(8,128)(2,1)}, u32[]{:S(2)}, u32[]{:S(2)}) async-start(bf16[32,64,2560]{2,1,0:T(8,128)(2,1)} %bitcast.251), calls=%async_computation.2 | async-start | bytes 20971520 | tf_op jit(solution)/shard_map/all_to_all | solution.py:124
  740.1 47.6 %copy-start.1 = (s32[1,4,128]{2,1,0:T(4,128)S(1)}, s32[1,4,128]{2,1,0:T(4,128)}, u32[]{:S(2)}) copy-start(s32[1,4,128]{2,1,0:T(4,128)} %param.16) | copy-start | bytes 6148
Sparse Core Ops, SparseCore 0:
  12.4 121.3 all-gather.2
  136.9 177.9 all-gather.4
  361.5 423.0 reduce-scatter.1

commit v6 on v5

--- a/solution.py
+++ b/solution.py
@@ -219,7 +219,7 @@
     mlp_grads = grad_pack(
         normed2, cot_full, jnp.concatenate([d_gate, d_up, hidden], axis=1), hidden_width
     )
-    mlp_red = lax.psum_scatter(mlp_grads, "dp", scatter_dimension=0, tiled=True).astype(jnp.float32)
+    mlp_red = spread_sum(mlp_grads, "dp", 32)
     d_normed2 = row_sum(times_trans(d_gate, wgate_all) + times_trans(d_up, wup_all))
     grad_mlp = jnp.sum(d_normed2 * resid * scale_two, axis=0)
     inner_two = jnp.mean(d_normed2 * mlp_full * resid, axis=-1, keepdims=True)

time: 800 us -> 1010 us (1.26)
  the two profiles are of different devices: /device:TPU:0 before, /device:TPU:58 now
where the time goes in v6:
time: 1010 us; the launch traced here: 1000 us
  waiting for transfers between devices  731 us (72%)
  matrix products  81.4 us (8%)
  starting transfers between devices  49.3 us (5%)
  local copies, waits for them, and re-layouts  46.5 us (5%)
  Pallas kernels  40.7 us (4%)
  other arithmetic  39.2 us (4%)
  between operations  15.2 us (2%)
    all_to_all x2, waiting for transfers between devices, spread_sum(): got = lax.all_to_all(blocks, axis, 0, 0, tiled=False)  420 us
    ppermute x4, waiting for transfers between devices, row_sum(): return mine + lax.ppermute(theirs, 'tensor', ACROSS)  93.7 us
    all_gather x1, waiting for transfers between devices, shards(): attn_all = lax.all_gather(attn_pack, 'dp', axis=0, tiled=True)  75.5 us
    all_gather x1, waiting for transfers between devices, shards(): mlp_all = lax.all_gather(mlp_pack, 'dp', axis=0, tiled=True)  60.3 us
    ppermute x4, waiting for transfers between devices, row_gather(): across = lax.ppermute(values, 'tensor', ACROSS)  58.8 us
    pallas_call x2, Pallas kernels, grad_pack(): pl.pallas_call(functools.partial(pack_kernel, per), grid=(rows_out // til...  40.7 us
    dot_general x8, matrix products, matmul_plain(): return jnp.dot(left, right, preferred_element_type=jnp.float32)  35.4 us
    dot_general x8, matrix products, times_trans(): lax.dot_general(left, right, (((1,), (1,)), ((), ())), preferred_element_...  26.6 us
  transfers between devices with their start and end apart: 22, of which 18 were waited for; matrix products, arithmetic and copies ran while one was open for 8% of the time, Pallas kernels for 4%

profile of v6, /device:TPU:58, one launch (start us, length us, event | category | flops | bytes accessed | tf_op | source)
XLA Modules:
  0.0 1003.7 jit_solution(10217436753001942477)
XLA Ops:
  12.3 2.0 pad_maximum_fusion.9
  15.8 10.1 %all-to-all-start = ((f32[128,3,16]{2,1,0:T(4,128)}), f32[128,3,16]{2,1,0:T(4,128)S(1)}, u32[]{:S(2)}, u32[]{:S(2)}) async-start(f32[128,3,16]{2,1,0:T(4,128)} %broadcast_in_dim.29), calls=%async_computation | async-start | bytes 524288 | tf_op jit(solution)/shard_map/all_to_all | solution.py:131
  26.6 7.5 all-to-all-done
  34.9 1.6 collective-permute-start
  36.7 12.2 %collective-permute-done = bf16[128,2048]{1,0:T(8,128)(2,1)S(1)} collective-permute-done((bf16[128,2048]{1,0:T(8,128)(2,1)S(1)}, bf16[128,2048]{1,0:T(8,128)(2,1)S(1)}, u32[]{:S(2)}, u32[]{:S(2)}) %collective-permute-start) | collective-permute-done | bytes 524320 | tf_op jit(solution)/shard_map/ppermute | solution.py:108
  50.5 1.4 collective-permute-done.1
  51.9 2.7 pad_maximum_fusion.1
  54.6 75.5 %all-gather.3.cloned.1.call-done = bf16[2048,2560]{1,0:T(8,128)(2,1)} async-done(((bf16[64,2560]{1,0:T(8,128)(2,1)}), bf16[2048,2560]{1,0:T(8,128)(2,1)}) %all-gather.3.cloned.1.call-update) | async-done | bytes 10485776 | tf_op jit(solution)/shard_map/all_gather | solution.py:175
  130.1 5.7 slice_bitcast_fusion
  135.8 4.1 copy.86
  139.9 4.0 copy.88
  143.8 4.1 copy.89
  147.9 3.5 fusion.51
  152.4 2.5 fusion.18
  154.9 2.5 convolution_select_fusion.1
  157.5 2.9 fusion.20
  161.4 1.9 convolution_bitcast_fusion.2
  164.6 4.8 fusion.69
  169.4 3.1 fusion.24
  172.8 4.1 collective-permute-done.2
  178.3 1.4 collective-permute-start.8
  179.7 28.0 %collective-permute-done.3 = f32[128,2048]{1,0:T(8,128)} collective-permute-done((f32[128,2048]{1,0:T(8,128)S(1)}, f32[128,2048]{1,0:T(8,128)}, u32[]{:S(2)}, u32[]{:S(2)}) %collective-permute-start.3) | collective-permute-done | bytes 1048608 | tf_op jit(solution)/shard_map/ppermute | solution.py:119
  207.7 2.3 multiply_reduce_fusion.3
  211.3 13.1 %collective-permute-done.8 = bf16[128,2048]{1,0:T(8,128)(2,1)} collective-permute-done((bf16[128,2048]{1,0:T(8,128)(2,1)S(1)}, bf16[128,2048]{1,0:T(8,128)(2,1)}, u32[]{:S(2)}, u32[]{:S(2)}) %collective-permute-start.8) | collective-permute-done | bytes 524320 | tf_op jit(solution)/shard_map/ppermute | solution.py:108
  225.8 20.7 %collective-permute-done.4 = bf16[128,2048]{1,0:T(8,128)(2,1)S(1)} collective-permute-done((bf16[128,2048]{1,0:T(8,128)(2,1)S(1)}, bf16[128,2048]{1,0:T(8,128)(2,1)S(1)}, u32[]{:S(2)}, u32[]{:S(2)}) %collective-permute-start.4) | collective-permute-done | bytes 524320 | tf_op jit(solution)/shard_map/ppermute | solution.py:108
  246.7 2.6 pad_maximum_fusion.3
  249.4 1.5 pad_maximum_fusion.2
  250.9 60.3 %all-gather.5.cloned.1.call-done = bf16[2048,4224]{1,0:T(8,128)(2,1)} async-done(((bf16[64,4224]{1,0:T(8,128)(2,1)}), bf16[2048,4224]{1,0:T(8,128)(2,1)}) %all-gather.5.cloned.1.call-update) | async-done | bytes 17301520 | tf_op jit(solution)/shard_map/all_gather | solution.py:176
  311.2 6.5 fusion
  317.8 2.3 copy-done.36
  320.1 3.4 fusion.6
  323.5 7.2 multiply_convert_fusion.1
  330.7 7.1 fusion.4
  337.8 5.5 fusion.12
  343.9 5.5 fusion.2
  350.3 3.6 collective-permute-done.6
  354.1 22.2 %collective-permute-done.11 = f32[128,2048]{1,0:T(8,128)S(1)} collective-permute-done((f32[128,2048]{1,0:T(8,128)S(1)}, f32[128,2048]{1,0:T(8,128)S(1)}, u32[]{:S(2)}, u32[]{:S(2)}) %collective-permute-start.11) | collective-permute-done | bytes 1048608 | tf_op jit(solution)/shard_map/ppermute | solution.py:119
  376.8 21.1 %collective-permute-done.7 = f32[128,2048]{1,0:T(8,128)S(1)} collective-permute-done((f32[128,2048]{1,0:T(8,128)S(1)}, f32[128,2048]{1,0:T(8,128)S(1)}, u32[]{:S(2)}, u32[]{:S(2)}) %collective-permute-start.7) | collective-permute-done | bytes 1048608 | tf_op jit(solution)/shard_map/ppermute | solution.py:119
  397.9 1.7 fusion.123
  399.8 12.7 %collective-permute-done.12 = bf16[128,2048]{1,0:T(8,128)(2,1)S(1)} collective-permute-done((bf16[128,2048]{1,0:T(8,128)(2,1)S(1)}, bf16[128,2048]{1,0:T(8,128)(2,1)S(1)}, u32[]{:S(2)}, u32[]{:S(2)}) %collective-permute-start.12) | collective-permute-done | bytes 524320 | tf_op jit(solution)/shard_map/ppermute | solution.py:108
  412.7 2.6 collective-permute-done.13
  415.6 4.6 fusion.115
  421.5 1.5 copy.116
  423.1 2.0 fusion.54
  425.1 1.9 convolution_select_fusion
  427.0 2.7 multiply_convert_fusion.3
  429.7 2.9 convolution_bitcast_fusion
  432.6 2.1 copy.101
  434.7 1.4 copy.98
  436.2 4.6 multiply_reduce_fusion.1
  444.1 1.5 fusion.33
  450.1 4.0 collective-permute-done.14
  458.3 22.4 %collective-permute-done.15 = f32[128,2048]{1,0:T(8,128)} collective-permute-done((f32[128,2048]{1,0:T(8,128)S(1)}, f32[128,2048]{1,0:T(8,128)}, u32[]{:S(2)}, u32[]{:S(2)}) %collective-permute-start.15) | collective-permute-done | bytes 1048608 | tf_op jit(solution)/shard_map/ppermute | solution.py:119
  480.7 2.3 fusion.63
  483.9 9.1 all-to-all-start.1
  493.0 19.9 %shard_map.246 = bf16[2048,2560]{1,0:T(8,128)(2,1)} custom-call(bf16[512,2048]{1,0:T(8,128)(2,1)} %bitcast.268, bf16[512,2048]{1,0:T(8,128)(2,1)} %bitcast.275, bf16[512,2560]{1,0:T(8,128)(2,1)} %constant_dynamic-update-slice_fusion.4.right_ref), custom_call_target="tpu_custom_call" | custom-call | flops 5368709120 | bytes 17301504 | tf_op jit(solution)/shard_map/pallas_call | solution.py:64
  512.9 10.1 %all-to-all-start.2 = ((bf16[32,64,2560]{2,1,0:T(8,128)(2,1)}), bf16[32,64,2560]{2,1,0:T(8,128)(2,1)}, u32[]{:S(2)}, u32[]{:S(2)}) async-start(bf16[32,64,2560]{2,1,0:T(8,128)(2,1)} %bitcast.253), calls=%async_computation.2 | async-start | bytes 20971520 | tf_op jit(solution)/shard_map/all_to_all | solution.py:124
  523.1 3.8 pad_maximum_fusion.right_ref
  526.8 20.8 %shard_map.247 = bf16[2048,4224]{1,0:T(8,128)(2,1)} custom-call(bf16[512,2048]{1,0:T(8,128)(2,1)} %bitcast.271, bf16[512,2048]{1,0:T(8,128)(2,1)} %bitcast.270, bf16[512,4224]{1,0:T(8,128)(2,1)} %pad_maximum_fusion.right_ref), custom_call_target="tpu_custom_call" | custom-call | flops 8858370048 | bytes 25821184 | tf_op jit(solution)/shard_map/pallas_call | solution.py:64
  547.6 134.4 %all-to-all-done.2 = bf16[32,64,2560]{2,1,0:T(8,128)(2,1)} async-done(((bf16[32,64,2560]{2,1,0:T(8,128)(2,1)}), bf16[32,64,2560]{2,1,0:T(8,128)(2,1)}, u32[]{:S(2)}, u32[]{:S(2)}) %all-to-all-start.2) | async-done | bytes 10485792 | tf_op jit(solution)/shard_map/all_to_all | solution.py:124
  682.1 12.8 %all-to-all-start.3 = ((bf16[32,64,4224]{2,1,0:T(8,128)(2,1)}), bf16[32,64,4224]{2,1,0:T(8,128)(2,1)}, u32[]{:S(2)}, u32[]{:S(2)}) async-start(bf16[32,64,4224]{2,1,0:T(8,128)(2,1)} %bitcast.252), calls=%async_computation.3 | async-start | bytes 34603008 | tf_op jit(solution)/shard_map/all_to_all | solution.py:124
  696.9 5.7 convert_reduce_fusion.1
  703.5 285.2 %all-to-all-done.3 = bf16[32,64,4224]{2,1,0:T(8,128)(2,1)} async-done(((bf16[32,64,4224]{2,1,0:T(8,128)(2,1)}), bf16[32,64,4224]{2,1,0:T(8,128)(2,1)}, u32[]{:S(2)}, u32[]{:S(2)}) %all-to-all-start.3) | async-done | bytes 17301536 | tf_op jit(solution)/shard_map/all_to_all | solution.py:124
  988.7 6.9 convert_reduce_fusion
  (173 shorter events, 38.2 us)
Async XLA Ops:
  7.2 42.0 %copy-start = (s32[1,4,128]{2,1,0:T(4,128)S(1)}, s32[1,4,128]{2,1,0:T(4,128)}, u32[]{:S(2)}) copy-start(s32[1,4,128]{2,1,0:T(4,128)} %param.16) | copy-start | bytes 6148
  7.2 18.7 %copy-start.3 = (bf16[1,1,128,2048]{3,2,1,0:T(8,128)(2,1)S(1)}, bf16[1,1,128,2048]{3,2,1,0:T(8,128)(2,1)}, u32[]{:S(2)}) copy-start(bf16[1,1,128,2048]{3,2,1,0:T(8,128)(2,1)} %param.15) | copy-start | bytes 1572868
  7.2 122.9 %all-gather.3.cloned.1.call-start = ((), (), s32[]{:S(2)}) async-start(), calls=%async_computation.4 | async-start | bytes 10813440 | tf_op jit(solution)/shard_map/all_gather | solution.py:175
  11.5 0.7 copy-start.32
  12.3 298.9 %all-gather.5.cloned.1.call-start = ((), (), s32[]{:S(2)}) async-start(), calls=%async_computation.5 | async-start | bytes 17842176 | tf_op jit(solution)/shard_map/all_gather | solution.py:176
  15.8 18.3 %all-to-all-start = ((f32[128,3,16]{2,1,0:T(4,128)}), f32[128,3,16]{2,1,0:T(4,128)S(1)}, u32[]{:S(2)}, u32[]{:S(2)}) async-start(f32[128,3,16]{2,1,0:T(4,128)} %broadcast_in_dim.29), calls=%async_computation | async-start | bytes 524288 | tf_op jit(solution)/shard_map/all_to_all | solution.py:131
  25.9 23.3 %copy-start.35 = (s32[4]{0:T(128)S(1)}, s32[4]{0:T(128)}, u32[]{:S(2)}) copy-start(s32[4]{0:T(128)} %constant.52.clone) | copy-start | bytes 52
  34.9 14.0 %collective-permute-start = (bf16[128,2048]{1,0:T(8,128)(2,1)S(1)}, bf16[128,2048]{1,0:T(8,128)(2,1)S(1)}, u32[]{:S(2)}, u32[]{:S(2)}) collective-permute-start(bf16[128,2048]{1,0:T(8,128)(2,1)S(1)} %fusion.57), channel_id=1, source_target_pairs={{0,2},{2,0},{1,3},{3,1},{4,6},{6,4},{5,7},{7,5},{8,10},{10,8},{9,1... | collective-permute-start | bytes 1572872 | tf_op jit(solution)/shard_map/ppermute | solution.py:108
  49.0 2.9 collective-permute-start.1
  147.9 4.5 copy-start.25
  151.4 3.5 copy-start.8
  154.9 2.5 copy-start.16
  154.9 2.5 copy-start.24
  157.4 2.9 copy-start.6
  160.4 1.0 copy-start.13
  169.4 3.1 copy-start.18
  172.4 4.6 copy-start.2
  172.7 5.6 copy-start.11
  172.7 4.2 collective-permute-start.2
  176.9 1.3 copy-start.20
  177.1 30.6 %collective-permute-start.3 = (f32[128,2048]{1,0:T(8,128)S(1)}, f32[128,2048]{1,0:T(8,128)}, u32[]{:S(2)}, u32[]{:S(2)}) collective-permute-start(f32[128,2048]{1,0:T(8,128)S(1)} %fusion.83), channel_id=1, source_target_pairs={{0,2},{2,0},{1,3},{3,1},{4,6},{6,4},{5,7},{7,5},{8,10},{10,8},{9,1... | collective-permute-start | bytes 3145736 | tf_op jit(solution)/shard_map/ppermute | solution.py:119
  178.3 46.2 %collective-permute-start.8 = (bf16[128,2048]{1,0:T(8,128)(2,1)S(1)}, bf16[128,2048]{1,0:T(8,128)(2,1)}, u32[]{:S(2)}, u32[]{:S(2)}) collective-permute-start(bf16[128,2048]{1,0:T(8,128)(2,1)S(1)} %bitcast.260), channel_id=1, source_target_pairs={{0,2},{2,0},{1,3},{3,1},{4,6},{6,4},{5,7},{7,5},{8,10},{10,8},{9,1... | collective-permute-start | bytes 1572872 | tf_op jit(solution)/shard_map/ppermute | solution.py:108
  210.1 36.4 %collective-permute-start.4 = (bf16[128,2048]{1,0:T(8,128)(2,1)S(1)}, bf16[128,2048]{1,0:T(8,128)(2,1)S(1)}, u32[]{:S(2)}, u32[]{:S(2)}) collective-permute-start(bf16[128,2048]{1,0:T(8,128)(2,1)S(1)} %multiply_convert_fusion.4), channel_id=1, source_target_pairs={{0,2},{2,0},{1,3},{3,1},{4,6},{6,4},{5,7},{7,5},{8,10},{10,8},{9,1... | collective-permute-start | bytes 1572872 | tf_op jit(solution)/shard_map/ppermute | solution.py:108
  225.6 21.1 %collective-permute-start.9 = (bf16[2,128,2048]{2,1,0:T(8,128)(2,1)S(1)}, bf16[2,128,2048]{2,1,0:T(8,128)(2,1)S(1)}, u32[]{:S(2)}, u32[]{:S(2)}) collective-permute-start(bf16[2,128,2048]{2,1,0:T(8,128)(2,1)S(1)} %pad_maximum_fusion.7), channel_id=1, source_target_pairs={{0,1},{1,0},{2,3},{3,2},{4,5},{5,4},{6,7},{7,6},{8,9},{9,8},{10,11... | collective-permute-start | bytes 3145736 | tf_op jit(solution)/shard_map/ppermute | solution.py:110
  246.6 2.7 collective-permute-start.5
  311.2 6.6 copy-start.21
  311.2 8.9 copy-start.36
  330.7 7.1 copy-start.27
  330.7 7.1 copy-start.26
  330.7 13.1 %copy-start.28 = (bf16[512,1408]{1,0:T(8,128)(2,1)}, bf16[512,1408]{1,0:T(8,128)(2,1)S(1)}, u32[]{:S(2)}) copy-start(bf16[512,1408]{1,0:T(8,128)(2,1)S(1)} %get-tuple-element.39) | copy-start | bytes 4325380
  343.6 6.5 collective-permute-start.10
  349.5 4.3 collective-permute-start.6
  350.2 26.1 %collective-permute-start.11 = (f32[128,2048]{1,0:T(8,128)S(1)}, f32[128,2048]{1,0:T(8,128)S(1)}, u32[]{:S(2)}, u32[]{:S(2)}) collective-permute-start(f32[128,2048]{1,0:T(8,128)S(1)} %fusion.75), channel_id=1, source_target_pairs={{0,2},{2,0},{1,3},{3,1},{4,6},{6,4},{5,7},{7,5},{8,10},{10,8},{9,1... | collective-permute-start | bytes 3145736 | tf_op jit(solution)/shard_map/ppermute | solution.py:119
  354.0 43.8 %collective-permute-start.7 = (f32[128,2048]{1,0:T(8,128)S(1)}, f32[128,2048]{1,0:T(8,128)S(1)}, u32[]{:S(2)}, u32[]{:S(2)}) collective-permute-start(f32[128,2048]{1,0:T(8,128)S(1)} %fusion.78), channel_id=1, source_target_pairs={{0,2},{2,0},{1,3},{3,1},{4,6},{6,4},{5,7},{7,5},{8,10},{10,8},{9,1... | collective-permute-start | bytes 3145736 | tf_op jit(solution)/shard_map/ppermute | solution.py:119
  399.5 13.0 %collective-permute-start.12 = (bf16[128,2048]{1,0:T(8,128)(2,1)S(1)}, bf16[128,2048]{1,0:T(8,128)(2,1)S(1)}, u32[]{:S(2)}, u32[]{:S(2)}) collective-permute-start(bf16[128,2048]{1,0:T(8,128)(2,1)S(1)} %get-tuple-element.25), channel_id=1, source_target_pairs={{0,2},{2,0},{1,3},{3,1},{4,6},{6,4},{5,7},{7,5},{8,10},{10,8},{9,1... | collective-permute-start | bytes 1572872 | tf_op jit(solution)/shard_map/ppermute | solution.py:108
  412.6 3.0 copy-start.29
  412.7 2.7 collective-permute-start.13
  415.6 4.6 copy-start.22
  420.2 2.9 copy-start.7
  423.1 2.0 copy-start.14
  423.1 3.9 copy-start.9
  427.0 2.7 copy-start.17
  429.7 13.7 %slice-start = ((s8[10485760]{0:T(1024)(128)(4,1)}), s8[2097152]{0:T(1024)(128)(4,1)S(1)}, s32[]{:S(2)}) async-start(s8[10485760]{0:T(1024)(128)(4,1)} %bitcast.250), calls=%async_computation.6 | async-start | bytes 4194304
  436.2 7.2 slice-start.1
  440.8 1.0 copy-start.10
  440.8 1.4 copy-start.15
  440.8 1.7 copy-start.30
  440.9 2.0 copy-start.31
  440.9 3.3 slice-start.2
  444.1 1.5 copy-start.33
  449.6 4.5 copy-start.5
  449.8 7.6 copy-start.19
  449.8 30.9 %copy-start.4 = (bf16[1,1,128,2048]{3,2,1,0:T(8,128)(2,1)S(1)}, bf16[1,1,128,2048]{3,2,1,0:T(8,128)(2,1)}, u32[]{:S(2)}) copy-start(bf16[1,1,128,2048]{3,2,1,0:T(8,128)(2,1)} %param.15) | copy-start | bytes 1572868
  449.8 4.2 collective-permute-start.14
  454.1 1.3 copy-start.23
  455.4 25.3 %collective-permute-start.15 = (f32[128,2048]{1,0:T(8,128)S(1)}, f32[128,2048]{1,0:T(8,128)}, u32[]{:S(2)}, u32[]{:S(2)}) collective-permute-start(f32[128,2048]{1,0:T(8,128)S(1)} %fusion.72), channel_id=1, source_target_pairs={{0,2},{2,0},{1,3},{3,1},{4,6},{6,4},{5,7},{7,5},{8,10},{10,8},{9,1... | collective-permute-start | bytes 3145736 | tf_op jit(solution)/shard_map/ppermute | solution.py:119
  483.9 29.0 %all-to-all-start.1 = ((f32[128,3,16]{2,1,0:T(4,128)}), f32[128,3,16]{2,1,0:T(4,128)S(1)}, u32[]{:S(2)}, u32[]{:S(2)}) async-start(f32[128,3,16]{2,1,0:T(4,128)} %copy.104), calls=%async_computation.1 | async-start | bytes 524288 | tf_op jit(solution)/shard_map/all_to_all | solution.py:138
  512.9 169.1 %all-to-all-start.2 = ((bf16[32,64,2560]{2,1,0:T(8,128)(2,1)}), bf16[32,64,2560]{2,1,0:T(8,128)(2,1)}, u32[]{:S(2)}, u32[]{:S(2)}) async-start(bf16[32,64,2560]{2,1,0:T(8,128)(2,1)} %bitcast.253), calls=%async_computation.2 | async-start | bytes 20971520 | tf_op jit(solution)/shard_map/all_to_all | solution.py:124
  682.1 12.8 %copy-start.12 = (f32[128,2048]{1,0:T(8,128)S(1)}, f32[128,2048]{1,0:T(8,128)}, u32[]{:S(2)}) copy-start(f32[128,2048]{1,0:T(8,128)} %get-tuple-element.26) | copy-start | bytes 3145732
  682.1 12.8 %copy-start.34 = (f32[128]{0:T(128)S(1)}, f32[128]{0:T(128)}, u32[]{:S(2)}) copy-start(f32[128]{0:T(128)} %get-tuple-element.53) | copy-start | bytes 1540
  682.1 306.6 %all-to-all-start.3 = ((bf16[32,64,4224]{2,1,0:T(8,128)(2,1)}), bf16[32,64,4224]{2,1,0:T(8,128)(2,1)}, u32[]{:S(2)}, u32[]{:S(2)}) async-start(bf16[32,64,4224]{2,1,0:T(8,128)(2,1)} %bitcast.252), calls=%async_computation.3 | async-start | bytes 34603008 | tf_op jit(solution)/shard_map/all_to_all | solution.py:124
  988.7 7.9 copy-start.1
Sparse Core Ops, SparseCore 0:
  12.4 117.6 all-gather.2
  133.2 177.9 all-gather.4

commit v7 on v5

--- a/solution.py
+++ b/solution.py
@@ -116,7 +116,7 @@
     got = lax.ppermute(blocks[2:], "tensor", ON_CHIP)
     mine = blocks[0] + got[0]
     theirs = blocks[1] + got[1]
-    return mine + lax.ppermute(theirs, "tensor", ACROSS)
+    return mine + lax.ppermute(theirs.astype(jnp.bfloat16), "tensor", ACROSS).astype(jnp.float32)
 
 
 def spread_sum(values, axis, count):

time: 800 us -> 761 us (0.951)
  waiting for transfers between devices: 543 us -> 502 us
    ppermute x4, waiting for transfers between devices: 114 us -> 57.1 us  [row_sum(): lax.ppermute(theirs.astype(jnp.bfloat16), 'tensor', ACROSS)]
    reduce_scatter x1, waiting for transfers between devices: 37.9 us -> 60.4 us  [shards(): lax.psum_scatter(mlp_grads, 'dp', scatter_dimension=0, tiled=True)]
    all_gather x1, waiting for transfers between devices: 62.8 us -> 74.1 us  [shards(): mlp_all = lax.all_gather(mlp_pack, 'dp', axis=0, tiled=True)]
    ppermute x4, waiting for transfers between devices: 67.2 us -> 56.1 us  [row_gather(): across = lax.ppermute(values, 'tensor', ACROSS)]
  transfers between devices with their start and end apart: 22 -> 22, of which waited for: 18 -> 18; matrix products, arithmetic and copies ran while one was open for 16% -> 17% of each run, Pallas kernels for 3% -> 3%
where the time goes in v7:
time: 761 us; the launch traced here: 755 us
  waiting for transfers between devices  502 us (66%)
  matrix products  82.8 us (11%)
  local copies, waits for them, and re-layouts  45.5 us (6%)
  Pallas kernels  40.7 us (5%)
  starting transfers between devices  36.5 us (5%)
  other arithmetic  33 us (4%)
  between operations  14.9 us (2%)
    all_to_all x1, waiting for transfers between devices, spread_sum(): got = lax.all_to_all(blocks, axis, 0, 0, tiled=False)  156 us
    all_gather x1, waiting for transfers between devices, shards(): mlp_all = lax.all_gather(mlp_pack, 'dp', axis=0, tiled=True)  74.1 us
    all_gather x1, waiting for transfers between devices, shards(): attn_all = lax.all_gather(attn_pack, 'dp', axis=0, tiled=True)  71.8 us
    reduce_scatter x1, waiting for transfers between devices, shards(): lax.psum_scatter(mlp_grads, 'dp', scatter_dimension=0, tiled=True)  60.4 us
    ppermute x4, waiting for transfers between devices, row_sum(): lax.ppermute(theirs.astype(jnp.bfloat16), 'tensor', ACROSS)  57.1 us
    ppermute x4, waiting for transfers between devices, row_gather(): across = lax.ppermute(values, 'tensor', ACROSS)  56.1 us
    pallas_call x2, Pallas kernels, grad_pack(): pl.pallas_call(functools.partial(pack_kernel, per), grid=(rows_out // til...  40.7 us
    dot_general x8, matrix products, matmul_plain(): return jnp.dot(left, right, preferred_element_type=jnp.float32)  39.1 us
  transfers between devices with their start and end apart: 22, of which 18 were waited for; matrix products, arithmetic and copies ran while one was open for 17% of the time, Pallas kernels for 3%

profile of v7, /device:TPU:0, one launch (start us, length us, event | category | flops | bytes accessed | tf_op | source)
XLA Modules:
  0.0 755.4 jit_solution(1822014292151853645)
XLA Ops:
  12.3 1.9 pad_maximum_fusion.9
  15.7 11.1 %all-to-all-start = ((f32[128,3,16]{2,1,0:T(4,128)}), f32[128,3,16]{2,1,0:T(4,128)S(1)}, u32[]{:S(2)}, u32[]{:S(2)}) async-start(f32[128,3,16]{2,1,0:T(4,128)} %broadcast_in_dim.29), calls=%async_computation | async-start | bytes 524288 | tf_op jit(solution)/shard_map/all_to_all | solution.py:131
  27.7 11.2 %all-to-all-done = f32[128,3,16]{2,1,0:T(4,128)S(1)} async-done(((f32[128,3,16]{2,1,0:T(4,128)}), f32[128,3,16]{2,1,0:T(4,128)S(1)}, u32[]{:S(2)}, u32[]{:S(2)}) %all-to-all-start) | async-done | bytes 24608 | tf_op jit(solution)/shard_map/all_to_all | solution.py:131
  40.5 15.8 %collective-permute-done = bf16[128,2048]{1,0:T(8,128)(2,1)S(1)} collective-permute-done((bf16[128,2048]{1,0:T(8,128)(2,1)S(1)}, bf16[128,2048]{1,0:T(8,128)(2,1)S(1)}, u32[]{:S(2)}, u32[]{:S(2)}) %collective-permute-start) | collective-permute-done | bytes 524320 | tf_op jit(solution)/shard_map/ppermute | solution.py:108
  57.8 1.4 collective-permute-done.1
  59.2 2.8 pad_maximum_fusion.1
  62.0 71.8 %all-gather.3.cloned.1.call-done = bf16[2048,2560]{1,0:T(8,128)(2,1)} async-done(((bf16[64,2560]{1,0:T(8,128)(2,1)}), bf16[2048,2560]{1,0:T(8,128)(2,1)}) %all-gather.3.cloned.1.call-update) | async-done | bytes 10485776 | tf_op jit(solution)/shard_map/all_gather | solution.py:175
  133.8 5.3 slice_bitcast_fusion
  139.1 4.1 copy.86
  143.2 4.0 copy.88
  147.2 2.5 copy.89
  149.7 3.7 fusion.51
  154.3 2.5 fusion.18
  156.9 2.5 convolution_select_fusion.1
  159.4 2.9 fusion.20
  162.4 2.9 convolution_bitcast_fusion.2
  165.3 2.6 copy.92
  167.8 5.4 fusion.69
  173.2 3.1 fusion.24
  176.6 4.1 collective-permute-done.2
  182.1 1.3 collective-permute-start.8
  183.5 14.3 %collective-permute-done.3 = bf16[128,2048]{1,0:T(8,128)(2,1)} collective-permute-done((bf16[128,2048]{1,0:T(8,128)(2,1)S(1)}, bf16[128,2048]{1,0:T(8,128)(2,1)}, u32[]{:S(2)}, u32[]{:S(2)}) %collective-permute-start.3) | collective-permute-done | bytes 524320 | tf_op jit(solution)/shard_map/ppermute | solution.py:119
  197.8 2.1 multiply_reduce_fusion.3
  200.4 8.6 %collective-permute-done.8 = bf16[128,2048]{1,0:T(8,128)(2,1)} collective-permute-done((bf16[128,2048]{1,0:T(8,128)(2,1)S(1)}, bf16[128,2048]{1,0:T(8,128)(2,1)}, u32[]{:S(2)}, u32[]{:S(2)}) %collective-permute-start.8) | collective-permute-done | bytes 524320 | tf_op jit(solution)/shard_map/ppermute | solution.py:108
  210.5 14.8 %collective-permute-done.4 = bf16[128,2048]{1,0:T(8,128)(2,1)S(1)} collective-permute-done((bf16[128,2048]{1,0:T(8,128)(2,1)S(1)}, bf16[128,2048]{1,0:T(8,128)(2,1)S(1)}, u32[]{:S(2)}, u32[]{:S(2)}) %collective-permute-start.4) | collective-permute-done | bytes 524320 | tf_op jit(solution)/shard_map/ppermute | solution.py:108
  225.5 2.6 pad_maximum_fusion.3
  228.1 1.5 pad_maximum_fusion.2
  229.6 74.1 %all-gather.5.cloned.1.call-done = bf16[2048,4224]{1,0:T(8,128)(2,1)} async-done(((bf16[64,4224]{1,0:T(8,128)(2,1)}), bf16[2048,4224]{1,0:T(8,128)(2,1)}) %all-gather.5.cloned.1.call-update) | async-done | bytes 17301520 | tf_op jit(solution)/shard_map/all_gather | solution.py:176
  303.7 8.4 %fusion = f32[512,1408]{1,0:T(8,128)} fusion(bf16[512,2048]{1,0:T(8,128)(2,1)} %bitcast.277, bf16[2048,4224]{1,0:T(8,128)(2,1)} %all-gather.5.cloned.1.call-done), kind=kOutput, calls=%fused_computation.2 | convolution fusion | flops 2952790016 | bytes 10747904 | tf_op jit(solution)/shard_map/dot_general | solution.py:27
  312.0 1.5 copy-done.35
  313.6 5.0 fusion.6
  318.6 6.6 multiply_convert_fusion.1
  327.3 2.1 pad_maximum_fusion.right_ref
  329.4 20.8 %shard_map.247 = bf16[2048,4224]{1,0:T(8,128)(2,1)} custom-call(bf16[512,2048]{1,0:T(8,128)(2,1)} %bitcast.279, bf16[512,2048]{1,0:T(8,128)(2,1)} %bitcast.278, bf16[512,4224]{1,0:T(8,128)(2,1)} %pad_maximum_fusion.right_ref), custom_call_target="tpu_custom_call" | custom-call | flops 8858370048 | bytes 25821184 | tf_op jit(solution)/shard_map/pallas_call | solution.py:64
  350.2 6.0 fusion.4
  356.3 5.6 fusion.12
  363.2 5.5 fusion.2
  369.8 3.4 collective-permute-done.6
  374.0 13.9 %collective-permute-done.11 = bf16[128,2048]{1,0:T(8,128)(2,1)S(1)} collective-permute-done((bf16[128,2048]{1,0:T(8,128)(2,1)S(1)}, bf16[128,2048]{1,0:T(8,128)(2,1)S(1)}, u32[]{:S(2)}, u32[]{:S(2)}) %collective-permute-start.11) | collective-permute-done | bytes 524320 | tf_op jit(solution)/shard_map/ppermute | solution.py:119
  388.3 14.2 %collective-permute-done.7 = bf16[128,2048]{1,0:T(8,128)(2,1)S(1)} collective-permute-done((bf16[128,2048]{1,0:T(8,128)(2,1)S(1)}, bf16[128,2048]{1,0:T(8,128)(2,1)S(1)}, u32[]{:S(2)}, u32[]{:S(2)}) %collective-permute-start.7) | collective-permute-done | bytes 524320 | tf_op jit(solution)/shard_map/ppermute | solution.py:119
  402.5 1.7 fusion.127
  404.8 16.8 %collective-permute-done.12 = bf16[128,2048]{1,0:T(8,128)(2,1)S(1)} collective-permute-done((bf16[128,2048]{1,0:T(8,128)(2,1)S(1)}, bf16[128,2048]{1,0:T(8,128)(2,1)S(1)}, u32[]{:S(2)}, u32[]{:S(2)}) %collective-permute-start.12) | collective-permute-done | bytes 524320 | tf_op jit(solution)/shard_map/ppermute | solution.py:108
  422.0 2.6 collective-permute-done.13
  424.9 4.6 fusion.119
  430.8 1.6 copy.116
  432.4 3.2 fusion.54
  435.6 1.4 copy.101
  437.0 3.3 convolution_select_fusion
  440.2 1.5 multiply_convert_fusion.3
  442.2 1.9 convolution_bitcast_fusion
  444.1 2.1 multiply_reduce_fusion.1
  449.4 1.4 constant_dynamic-update-slice_fusion.5
  454.7 1.3 add_add_fusion
  456.5 4.0 collective-permute-done.14
  460.7 2.5 collective-permute-start.15
  465.5 14.7 %collective-permute-done.15 = bf16[128,2048]{1,0:T(8,128)(2,1)S(1)} collective-permute-done((bf16[128,2048]{1,0:T(8,128)(2,1)S(1)}, bf16[128,2048]{1,0:T(8,128)(2,1)S(1)}, u32[]{:S(2)}, u32[]{:S(2)}) %collective-permute-start.15) | collective-permute-done | bytes 524320 | tf_op jit(solution)/shard_map/ppermute | solution.py:119
  480.1 2.0 fusion.63
  483.1 7.0 all-to-all-start.1
  490.1 19.9 %shard_map.246 = bf16[2048,2560]{1,0:T(8,128)(2,1)} custom-call(bf16[512,2048]{1,0:T(8,128)(2,1)} %bitcast.274, bf16[512,2048]{1,0:T(8,128)(2,1)} %bitcast.276, bf16[512,2560]{1,0:T(8,128)(2,1)} %constant_dynamic-update-slice_fusion.4.right_ref), custom_call_target="tpu_custom_call" | custom-call | flops 5368709120 | bytes 17301504 | tf_op jit(solution)/shard_map/pallas_call | solution.py:64
  510.1 10.0 %all-to-all-start.2 = ((bf16[32,64,2560]{2,1,0:T(8,128)(2,1)}), bf16[32,64,2560]{2,1,0:T(8,128)(2,1)}, u32[]{:S(2)}, u32[]{:S(2)}) async-start(bf16[32,64,2560]{2,1,0:T(8,128)(2,1)} %bitcast.259), calls=%async_computation.2 | async-start | bytes 20971520 | tf_op jit(solution)/shard_map/all_to_all | solution.py:124
  522.1 155.7 %all-to-all-done.2 = bf16[32,64,2560]{2,1,0:T(8,128)(2,1)} async-done(((bf16[32,64,2560]{2,1,0:T(8,128)(2,1)}), bf16[32,64,2560]{2,1,0:T(8,128)(2,1)}, u32[]{:S(2)}, u32[]{:S(2)}) %all-to-all-start.2) | async-done | bytes 10485792 | tf_op jit(solution)/shard_map/all_to_all | solution.py:124
  677.8 6.4 convert_reduce_fusion
  685.1 60.4 %reduce-scatter.2.cloned.1.call-done = bf16[64,4224]{1,0:T(8,128)(2,1)} async-done(((bf16[2048,4224]{1,0:T(8,128)(2,1)}), bf16[64,4224]{1,0:T(8,128)(2,1)}) %reduce-scatter.2.cloned.1.call-update) | async-done | bytes 540688 | tf_op jit(solution)/shard_map/reduce_scatter | solution.py:222
  746.6 2.0 fusion.130
  (172 shorter events, 38.4 us)
Async XLA Ops:
  7.2 49.3 %copy-start = (s32[1,4,128]{2,1,0:T(4,128)S(1)}, s32[1,4,128]{2,1,0:T(4,128)}, u32[]{:S(2)}) copy-start(s32[1,4,128]{2,1,0:T(4,128)} %param.16) | copy-start | bytes 6148
  7.2 19.7 %copy-start.3 = (bf16[1,1,128,2048]{3,2,1,0:T(8,128)(2,1)S(1)}, bf16[1,1,128,2048]{3,2,1,0:T(8,128)(2,1)}, u32[]{:S(2)}) copy-start(bf16[1,1,128,2048]{3,2,1,0:T(8,128)(2,1)} %param.15) | copy-start | bytes 1572868
  7.2 126.6 %all-gather.3.cloned.1.call-start = ((), (), s32[]{:S(2)}) async-start(), calls=%async_computation.4 | async-start | bytes 10813440 | tf_op jit(solution)/shard_map/all_gather | solution.py:175
  11.5 0.7 copy-start.32
  12.3 291.4 %all-gather.5.cloned.1.call-start = ((), (), s32[]{:S(2)}) async-start(), calls=%async_computation.5 | async-start | bytes 17842176 | tf_op jit(solution)/shard_map/all_gather | solution.py:176
  15.7 23.1 %all-to-all-start = ((f32[128,3,16]{2,1,0:T(4,128)}), f32[128,3,16]{2,1,0:T(4,128)S(1)}, u32[]{:S(2)}, u32[]{:S(2)}) async-start(f32[128,3,16]{2,1,0:T(4,128)} %broadcast_in_dim.29), calls=%async_computation | async-start | bytes 524288 | tf_op jit(solution)/shard_map/all_to_all | solution.py:131
  26.9 29.6 %copy-start.34 = (s32[4]{0:T(128)S(1)}, s32[4]{0:T(128)}, u32[]{:S(2)}) copy-start(s32[4]{0:T(128)} %constant.52.clone) | copy-start | bytes 52
  26.9 718.6 %reduce-scatter.2.cloned.1.call-start = ((), (), s32[]{:S(2)}) async-start(), calls=%async_computation.6 | async-start | bytes 17842176 | tf_op jit(solution)/shard_map/reduce_scatter | solution.py:222
  39.7 16.6 %collective-permute-start = (bf16[128,2048]{1,0:T(8,128)(2,1)S(1)}, bf16[128,2048]{1,0:T(8,128)(2,1)S(1)}, u32[]{:S(2)}, u32[]{:S(2)}) collective-permute-start(bf16[128,2048]{1,0:T(8,128)(2,1)S(1)} %fusion.57), channel_id=1, source_target_pairs={{0,2},{2,0},{1,3},{3,1},{4,6},{6,4},{5,7},{7,5},{8,10},{10,8},{9,1... | collective-permute-start | bytes 1572872 | tf_op jit(solution)/shard_map/ppermute | solution.py:108
  56.3 5.7 copy-start.22
  56.4 2.9 collective-permute-start.1
  149.7 4.6 copy-start.21
  149.7 4.6 copy-start.23
  153.4 3.5 copy-start.6
  156.9 2.5 copy-start.12
  156.9 2.5 copy-start.20
  159.4 2.9 copy-start.5
  162.4 5.5 copy-start.9
  173.2 3.1 copy-start.14
  176.3 4.6 copy-start.2
  176.3 5.8 copy-start.8
  176.6 4.2 collective-permute-start.2
  180.8 1.3 copy-start.17
  181.0 16.9 %collective-permute-start.3 = (bf16[128,2048]{1,0:T(8,128)(2,1)S(1)}, bf16[128,2048]{1,0:T(8,128)(2,1)}, u32[]{:S(2)}, u32[]{:S(2)}) collective-permute-start(bf16[128,2048]{1,0:T(8,128)(2,1)S(1)} %fusion.87), channel_id=1, source_target_pairs={{0,2},{2,0},{1,3},{3,1},{4,6},{6,4},{5,7},{7,5},{8,10},{10,8},{9,1... | collective-permute-start | bytes 1572872 | tf_op jit(solution)/shard_map/ppermute | solution.py:119
  182.1 26.9 %collective-permute-start.8 = (bf16[128,2048]{1,0:T(8,128)(2,1)S(1)}, bf16[128,2048]{1,0:T(8,128)(2,1)}, u32[]{:S(2)}, u32[]{:S(2)}) collective-permute-start(bf16[128,2048]{1,0:T(8,128)(2,1)S(1)} %bitcast.266), channel_id=1, source_target_pairs={{0,2},{2,0},{1,3},{3,1},{4,6},{6,4},{5,7},{7,5},{8,10},{10,8},{9,1... | collective-permute-start | bytes 1572872 | tf_op jit(solution)/shard_map/ppermute | solution.py:108
  200.2 25.1 %collective-permute-start.4 = (bf16[128,2048]{1,0:T(8,128)(2,1)S(1)}, bf16[128,2048]{1,0:T(8,128)(2,1)S(1)}, u32[]{:S(2)}, u32[]{:S(2)}) collective-permute-start(bf16[128,2048]{1,0:T(8,128)(2,1)S(1)} %multiply_convert_fusion.4), channel_id=1, source_target_pairs={{0,2},{2,0},{1,3},{3,1},{4,6},{6,4},{5,7},{7,5},{8,10},{10,8},{9,1... | collective-permute-start | bytes 1572872 | tf_op jit(solution)/shard_map/ppermute | solution.py:108
  210.2 15.2 %collective-permute-start.9 = (bf16[2,128,2048]{2,1,0:T(8,128)(2,1)S(1)}, bf16[2,128,2048]{2,1,0:T(8,128)(2,1)S(1)}, u32[]{:S(2)}, u32[]{:S(2)}) collective-permute-start(bf16[2,128,2048]{2,1,0:T(8,128)(2,1)S(1)} %pad_maximum_fusion.7), channel_id=1, source_target_pairs={{0,1},{1,0},{2,3},{3,2},{4,5},{5,4},{6,7},{7,6},{8,9},{9,8},{10,11... | collective-permute-start | bytes 3145736 | tf_op jit(solution)/shard_map/ppermute | solution.py:110
  225.4 2.7 collective-permute-start.5
  303.7 8.4 %copy-start.19 = (bf16[4,128,2048]{2,1,0:T(8,128)(2,1)S(1)}, bf16[4,128,2048]{2,1,0:T(8,128)(2,1)}, u32[]{:S(2)}) copy-start(bf16[4,128,2048]{2,1,0:T(8,128)(2,1)} %pad_maximum_fusion.2) | copy-start | bytes 6291460
  303.7 9.9 %copy-start.35 = (bf16[2048,4224]{1,0:T(8,128)(2,1)S(1)}, bf16[2048,4224]{1,0:T(8,128)(2,1)}, u32[]{:S(2)}) copy-start(bf16[2048,4224]{1,0:T(8,128)(2,1)} %all-gather.5.cloned.1.call-done) | copy-start | bytes 51904516
  325.2 1.1 copy-start.24
  325.2 1.6 copy-start.26
  325.3 2.0 copy-start.28
  350.2 6.0 copy-start.27
  361.8 1.4 copy-start.25
  362.1 7.0 collective-permute-start.10
  368.9 4.2 collective-permute-start.6
  369.2 18.7 %collective-permute-start.11 = (bf16[128,2048]{1,0:T(8,128)(2,1)S(1)}, bf16[128,2048]{1,0:T(8,128)(2,1)S(1)}, u32[]{:S(2)}, u32[]{:S(2)}) collective-permute-start(bf16[128,2048]{1,0:T(8,128)(2,1)S(1)} %fusion.77), channel_id=1, source_target_pairs={{0,2},{2,0},{1,3},{3,1},{4,6},{6,4},{5,7},{7,5},{8,10},{10,8},{9,1... | collective-permute-start | bytes 1572872 | tf_op jit(solution)/shard_map/ppermute | solution.py:119
  373.3 29.2 %collective-permute-start.7 = (bf16[128,2048]{1,0:T(8,128)(2,1)S(1)}, bf16[128,2048]{1,0:T(8,128)(2,1)S(1)}, u32[]{:S(2)}, u32[]{:S(2)}) collective-permute-start(bf16[128,2048]{1,0:T(8,128)(2,1)S(1)} %fusion.81), channel_id=1, source_target_pairs={{0,2},{2,0},{1,3},{3,1},{4,6},{6,4},{5,7},{7,5},{8,10},{10,8},{9,1... | collective-permute-start | bytes 1572872 | tf_op jit(solution)/shard_map/ppermute | solution.py:119
  404.3 17.4 %collective-permute-start.12 = (bf16[128,2048]{1,0:T(8,128)(2,1)S(1)}, bf16[128,2048]{1,0:T(8,128)(2,1)S(1)}, u32[]{:S(2)}, u32[]{:S(2)}) collective-permute-start(bf16[128,2048]{1,0:T(8,128)(2,1)S(1)} %get-tuple-element.25), channel_id=1, source_target_pairs={{0,2},{2,0},{1,3},{3,1},{4,6},{6,4},{5,7},{7,5},{8,10},{10,8},{9,1... | collective-permute-start | bytes 1572872 | tf_op jit(solution)/shard_map/ppermute | solution.py:108
  421.8 3.1 copy-start.29
  421.8 2.9 collective-permute-start.13
  424.9 4.6 copy-start.18
  437.0 3.3 copy-start.7
  440.2 1.9 copy-start.13
  441.8 9.1 %slice-start = ((s8[10485760]{0:T(1024)(128)(4,1)}), s8[4194304]{0:T(1024)(128)(4,1)S(1)}, s32[]{:S(2)}) async-start(s8[10485760]{0:T(1024)(128)(4,1)} %bitcast.257), calls=%async_computation.7 | async-start | bytes 8388608
  444.1 6.7 slice-start.1
  446.2 3.2 copy-start.11
  446.2 3.2 copy-start.30
  446.3 3.1 copy-start.31
  446.3 4.5 slice-start.2
  456.1 4.6 copy-start.4
  456.1 8.5 %copy-start.15 = (bf16[512,512]{1,0:T(8,128)(2,1)S(1)}, bf16[512,512]{1,0:T(8,128)(2,1)}, u32[]{:S(2)}) copy-start(bf16[512,512]{1,0:T(8,128)(2,1)} %copy-done.14) | copy-start | bytes 1572868
  456.3 4.2 collective-permute-start.14
  460.5 2.7 copy-start.16
  460.7 19.5 %collective-permute-start.15 = (bf16[128,2048]{1,0:T(8,128)(2,1)S(1)}, bf16[128,2048]{1,0:T(8,128)(2,1)S(1)}, u32[]{:S(2)}, u32[]{:S(2)}) collective-permute-start(bf16[128,2048]{1,0:T(8,128)(2,1)S(1)} %fusion.73), channel_id=1, source_target_pairs={{0,2},{2,0},{1,3},{3,1},{4,6},{6,4},{5,7},{7,5},{8,10},{10,8},{9,1... | collective-permute-start | bytes 1572872 | tf_op jit(solution)/shard_map/ppermute | solution.py:119
  483.1 27.0 %all-to-all-start.1 = ((f32[128,3,16]{2,1,0:T(4,128)}), f32[128,3,16]{2,1,0:T(4,128)S(1)}, u32[]{:S(2)}, u32[]{:S(2)}) async-start(f32[128,3,16]{2,1,0:T(4,128)} %copy.104), calls=%async_computation.1 | async-start | bytes 524288 | tf_op jit(solution)/shard_map/all_to_all | solution.py:138
  510.1 10.0 %copy-start.10 = (f32[128,2048]{1,0:T(8,128)S(1)}, f32[128,2048]{1,0:T(8,128)}, u32[]{:S(2)}) copy-start(f32[128,2048]{1,0:T(8,128)} %get-tuple-element.26) | copy-start | bytes 3145732
  510.1 10.0 %copy-start.33 = (f32[128]{0:T(128)S(1)}, f32[128]{0:T(128)}, u32[]{:S(2)}) copy-start(f32[128]{0:T(128)} %get-tuple-element.52) | copy-start | bytes 1540
  510.1 167.7 %all-to-all-start.2 = ((bf16[32,64,2560]{2,1,0:T(8,128)(2,1)}), bf16[32,64,2560]{2,1,0:T(8,128)(2,1)}, u32[]{:S(2)}, u32[]{:S(2)}) async-start(bf16[32,64,2560]{2,1,0:T(8,128)(2,1)} %bitcast.259), calls=%async_computation.2 | async-start | bytes 20971520 | tf_op jit(solution)/shard_map/all_to_all | solution.py:124
  677.8 70.8 %copy-start.1 = (s32[1,4,128]{2,1,0:T(4,128)S(1)}, s32[1,4,128]{2,1,0:T(4,128)}, u32[]{:S(2)}) copy-start(s32[1,4,128]{2,1,0:T(4,128)} %param.16) | copy-start | bytes 6148
Sparse Core Ops, SparseCore 0:
  12.4 121.3 all-gather.2
  136.9 166.7 all-gather.4
  350.3 395.1 reduce-scatter.1

commit v8 on v7

--- a/solution.py
+++ b/solution.py
@@ -242,6 +242,7 @@
         jnp.concatenate([d_query, d_forget, d_value, d_outgate, gated], axis=1),
         local_width,
     )
+    attn_grads, mlp_red = lax.optimization_barrier((attn_grads, mlp_red))
     attn_red = spread_sum(attn_grads, "dp", 32)
     d_normed = row_sum(
         times_trans(d_query, wq_all)

time: 761 us -> 820 us (1.078)
  waiting for transfers between devices: 502 us -> 558 us
    reduce_scatter x1, waiting for transfers between devices: 60.4 us -> 123 us  [shards(): lax.psum_scatter(mlp_grads, 'dp', scatter_dimension=0, tiled=True)]
  transfers between devices with their start and end apart: 22 -> 22, of which waited for: 18 -> 19; matrix products, arithmetic and copies ran while one was open for 17% -> 15% of each run, Pallas kernels for 3% -> 2%
where the time goes in v8:
time: 820 us; the launch traced here: 807 us
  waiting for transfers between devices  558 us (68%)
  matrix products  82.8 us (10%)
  local copies, waits for them, and re-layouts  44.4 us (5%)
  Pallas kernels  40.7 us (5%)
  other arithmetic  35.1 us (4%)
  starting transfers between devices  32 us (4%)
  between operations  14.9 us (2%)
    all_to_all x1, waiting for transfers between devices, spread_sum(): got = lax.all_to_all(blocks, axis, 0, 0, tiled=False)  148 us
    reduce_scatter x1, waiting for transfers between devices, shards(): lax.psum_scatter(mlp_grads, 'dp', scatter_dimension=0, tiled=True)  123 us
    all_gather x1, waiting for transfers between devices, shards(): mlp_all = lax.all_gather(mlp_pack, 'dp', axis=0, tiled=True)  74.1 us
    all_gather x1, waiting for transfers between devices, shards(): attn_all = lax.all_gather(attn_pack, 'dp', axis=0, tiled=True)  71.8 us
    ppermute x4, waiting for transfers between devices, row_sum(): lax.ppermute(theirs.astype(jnp.bfloat16), 'tensor', ACROSS)  57.8 us
    ppermute x4, waiting for transfers between devices, row_gather(): across = lax.ppermute(values, 'tensor', ACROSS)  56.1 us
    pallas_call x2, Pallas kernels, grad_pack(): pl.pallas_call(functools.partial(pack_kernel, per), grid=(rows_out // til...  40.7 us
    dot_general x8, matrix products, matmul_plain(): return jnp.dot(left, right, preferred_element_type=jnp.float32)  39.1 us
  transfers between devices with their start and end apart: 22, of which 19 were waited for; matrix products, arithmetic and copies ran while one was open for 15% of the time, Pallas kernels for 2%

profile of v8, /device:TPU:0, one launch (start us, length us, event | category | flops | bytes accessed | tf_op | source)
XLA Modules:
  0.0 807.4 jit_solution(15485117485764021158)
XLA Ops:
  12.3 1.9 pad_maximum_fusion.9
  15.7 11.1 %all-to-all-start = ((f32[128,3,16]{2,1,0:T(4,128)}), f32[128,3,16]{2,1,0:T(4,128)S(1)}, u32[]{:S(2)}, u32[]{:S(2)}) async-start(f32[128,3,16]{2,1,0:T(4,128)} %broadcast_in_dim.29), calls=%async_computation | async-start | bytes 524288 | tf_op jit(solution)/shard_map/all_to_all | solution.py:131
  27.7 11.2 %all-to-all-done = f32[128,3,16]{2,1,0:T(4,128)S(1)} async-done(((f32[128,3,16]{2,1,0:T(4,128)}), f32[128,3,16]{2,1,0:T(4,128)S(1)}, u32[]{:S(2)}, u32[]{:S(2)}) %all-to-all-start) | async-done | bytes 24608 | tf_op jit(solution)/shard_map/all_to_all | solution.py:131
  40.5 15.8 %collective-permute-done = bf16[128,2048]{1,0:T(8,128)(2,1)S(1)} collective-permute-done((bf16[128,2048]{1,0:T(8,128)(2,1)S(1)}, bf16[128,2048]{1,0:T(8,128)(2,1)S(1)}, u32[]{:S(2)}, u32[]{:S(2)}) %collective-permute-start) | collective-permute-done | bytes 524320 | tf_op jit(solution)/shard_map/ppermute | solution.py:108
  57.8 1.4 collective-permute-done.1
  59.2 2.8 pad_maximum_fusion.1
  62.0 71.8 %all-gather.3.cloned.1.call-done = bf16[2048,2560]{1,0:T(8,128)(2,1)} async-done(((bf16[64,2560]{1,0:T(8,128)(2,1)}), bf16[2048,2560]{1,0:T(8,128)(2,1)}) %all-gather.3.cloned.1.call-update) | async-done | bytes 10485776 | tf_op jit(solution)/shard_map/all_gather | solution.py:175
  133.8 5.3 slice_bitcast_fusion
  139.1 4.1 copy.86
  143.2 4.0 copy.88
  147.2 2.5 copy.89
  149.7 3.7 fusion.51
  154.3 2.5 fusion.18
  156.9 2.5 convolution_select_fusion.1
  159.4 2.9 fusion.20
  162.4 2.9 convolution_bitcast_fusion.2
  165.3 2.5 copy.92
  167.8 5.4 fusion.69
  173.2 3.1 fusion.24
  176.6 4.1 collective-permute-done.2
  182.1 1.3 collective-permute-start.8
  183.5 14.3 %collective-permute-done.3 = bf16[128,2048]{1,0:T(8,128)(2,1)} collective-permute-done((bf16[128,2048]{1,0:T(8,128)(2,1)S(1)}, bf16[128,2048]{1,0:T(8,128)(2,1)}, u32[]{:S(2)}, u32[]{:S(2)}) %collective-permute-start.3) | collective-permute-done | bytes 524320 | tf_op jit(solution)/shard_map/ppermute | solution.py:119
  197.8 2.1 multiply_reduce_fusion.3
  200.5 8.6 %collective-permute-done.8 = bf16[128,2048]{1,0:T(8,128)(2,1)} collective-permute-done((bf16[128,2048]{1,0:T(8,128)(2,1)S(1)}, bf16[128,2048]{1,0:T(8,128)(2,1)}, u32[]{:S(2)}, u32[]{:S(2)}) %collective-permute-start.8) | collective-permute-done | bytes 524320 | tf_op jit(solution)/shard_map/ppermute | solution.py:108
  210.5 14.8 %collective-permute-done.4 = bf16[128,2048]{1,0:T(8,128)(2,1)S(1)} collective-permute-done((bf16[128,2048]{1,0:T(8,128)(2,1)S(1)}, bf16[128,2048]{1,0:T(8,128)(2,1)S(1)}, u32[]{:S(2)}, u32[]{:S(2)}) %collective-permute-start.4) | collective-permute-done | bytes 524320 | tf_op jit(solution)/shard_map/ppermute | solution.py:108
  225.5 2.6 pad_maximum_fusion.3
  228.1 1.5 pad_maximum_fusion.2
  229.6 74.1 %all-gather.5.cloned.1.call-done = bf16[2048,4224]{1,0:T(8,128)(2,1)} async-done(((bf16[64,4224]{1,0:T(8,128)(2,1)}), bf16[2048,4224]{1,0:T(8,128)(2,1)}) %all-gather.5.cloned.1.call-update) | async-done | bytes 17301520 | tf_op jit(solution)/shard_map/all_gather | solution.py:176
  303.7 8.4 %fusion = f32[512,1408]{1,0:T(8,128)} fusion(bf16[512,2048]{1,0:T(8,128)(2,1)} %bitcast.277, bf16[2048,4224]{1,0:T(8,128)(2,1)} %all-gather.5.cloned.1.call-done), kind=kOutput, calls=%fused_computation.2 | convolution fusion | flops 2952790016 | bytes 10747904 | tf_op jit(solution)/shard_map/dot_general | solution.py:27
  312.0 1.5 copy-done.34
  313.6 5.0 fusion.6
  318.6 6.6 multiply_convert_fusion.1
  327.3 2.1 pad_maximum_fusion.right_ref
  329.4 20.7 %shard_map.247 = bf16[2048,4224]{1,0:T(8,128)(2,1)} custom-call(bf16[512,2048]{1,0:T(8,128)(2,1)} %bitcast.279, bf16[512,2048]{1,0:T(8,128)(2,1)} %bitcast.278, bf16[512,4224]{1,0:T(8,128)(2,1)} %pad_maximum_fusion.right_ref), custom_call_target="tpu_custom_call" | custom-call | flops 8858370048 | bytes 25821184 | tf_op jit(solution)/shard_map/pallas_call | solution.py:64
  350.2 6.0 fusion.4
  356.2 5.6 fusion.12
  363.2 5.5 fusion.2
  369.8 3.4 collective-permute-done.6
  373.9 13.9 %collective-permute-done.11 = bf16[128,2048]{1,0:T(8,128)(2,1)S(1)} collective-permute-done((bf16[128,2048]{1,0:T(8,128)(2,1)S(1)}, bf16[128,2048]{1,0:T(8,128)(2,1)S(1)}, u32[]{:S(2)}, u32[]{:S(2)}) %collective-permute-start.11) | collective-permute-done | bytes 524320 | tf_op jit(solution)/shard_map/ppermute | solution.py:119
  388.3 14.2 %collective-permute-done.7 = bf16[128,2048]{1,0:T(8,128)(2,1)S(1)} collective-permute-done((bf16[128,2048]{1,0:T(8,128)(2,1)S(1)}, bf16[128,2048]{1,0:T(8,128)(2,1)S(1)}, u32[]{:S(2)}, u32[]{:S(2)}) %collective-permute-start.7) | collective-permute-done | bytes 524320 | tf_op jit(solution)/shard_map/ppermute | solution.py:119
  402.5 1.7 fusion.127
  404.8 16.9 %collective-permute-done.12 = bf16[128,2048]{1,0:T(8,128)(2,1)S(1)} collective-permute-done((bf16[128,2048]{1,0:T(8,128)(2,1)S(1)}, bf16[128,2048]{1,0:T(8,128)(2,1)S(1)}, u32[]{:S(2)}, u32[]{:S(2)}) %collective-permute-start.12) | collective-permute-done | bytes 524320 | tf_op jit(solution)/shard_map/ppermute | solution.py:108
  422.0 2.6 collective-permute-done.13
  424.9 4.6 fusion.119
  430.8 1.6 copy.116
  432.4 3.2 fusion.54
  435.5 1.4 copy.101
  436.9 3.3 convolution_select_fusion
  440.2 1.5 multiply_convert_fusion.3
  442.2 1.9 convolution_bitcast_fusion
  444.1 2.1 multiply_reduce_fusion.1
  449.4 1.4 constant_dynamic-update-slice_fusion.5
  454.7 1.3 add_add_fusion
  456.5 4.0 collective-permute-done.14
  461.4 2.5 collective-permute-start.15
  466.2 15.3 %collective-permute-done.15 = bf16[128,2048]{1,0:T(8,128)(2,1)} collective-permute-done((bf16[128,2048]{1,0:T(8,128)(2,1)}, bf16[128,2048]{1,0:T(8,128)(2,1)}, u32[]{:S(2)}, u32[]{:S(2)}) %collective-permute-start.15) | collective-permute-done | bytes 524320 | tf_op jit(solution)/shard_map/ppermute | solution.py:119
  481.5 2.7 fusion.63
  485.2 7.2 all-to-all-start.1
  492.4 20.0 %shard_map.246 = bf16[2048,2560]{1,0:T(8,128)(2,1)} custom-call(bf16[512,2048]{1,0:T(8,128)(2,1)} %bitcast.274, bf16[512,2048]{1,0:T(8,128)(2,1)} %bitcast.276, bf16[512,2560]{1,0:T(8,128)(2,1)} %constant_dynamic-update-slice_fusion.4.right_ref), custom_call_target="tpu_custom_call" | custom-call | flops 5368709120 | bytes 17301504 | tf_op jit(solution)/shard_map/pallas_call | solution.py:64
  512.4 122.9 %reduce-scatter.2.cloned.1.call-done = bf16[64,4224]{1,0:T(8,128)(2,1)} async-done(((bf16[2048,4224]{1,0:T(8,128)(2,1)}), bf16[64,4224]{1,0:T(8,128)(2,1)}) %reduce-scatter.2.cloned.1.call-update) | async-done | bytes 540688 | tf_op jit(solution)/shard_map/reduce_scatter | solution.py:222
  636.5 5.4 all-to-all-start.2
  641.9 2.5 fusion.60
  646.1 147.9 %all-to-all-done.2 = bf16[32,64,2560]{2,1,0:T(8,128)(2,1)} async-done(((bf16[32,64,2560]{2,1,0:T(8,128)(2,1)}), bf16[32,64,2560]{2,1,0:T(8,128)(2,1)}, u32[]{:S(2)}, u32[]{:S(2)}) %all-to-all-start.2) | async-done | bytes 10485792 | tf_op jit(solution)/shard_map/all_to_all | solution.py:124
  794.0 5.7 convert_reduce_fusion
  (170 shorter events, 38.8 us)
Async XLA Ops:
  7.2 49.3 %copy-start = (s32[1,4,128]{2,1,0:T(4,128)S(1)}, s32[1,4,128]{2,1,0:T(4,128)}, u32[]{:S(2)}) copy-start(s32[1,4,128]{2,1,0:T(4,128)} %param.16) | copy-start | bytes 6148
  7.2 19.7 %copy-start.3 = (bf16[1,1,128,2048]{3,2,1,0:T(8,128)(2,1)S(1)}, bf16[1,1,128,2048]{3,2,1,0:T(8,128)(2,1)}, u32[]{:S(2)}) copy-start(bf16[1,1,128,2048]{3,2,1,0:T(8,128)(2,1)} %param.15) | copy-start | bytes 1572868
  7.2 126.6 %all-gather.3.cloned.1.call-start = ((), (), s32[]{:S(2)}) async-start(), calls=%async_computation.4 | async-start | bytes 10813440 | tf_op jit(solution)/shard_map/all_gather | solution.py:175
  11.5 0.7 copy-start.31
  12.3 291.4 %all-gather.5.cloned.1.call-start = ((), (), s32[]{:S(2)}) async-start(), calls=%async_computation.5 | async-start | bytes 17842176 | tf_op jit(solution)/shard_map/all_gather | solution.py:176
  15.7 23.1 %all-to-all-start = ((f32[128,3,16]{2,1,0:T(4,128)}), f32[128,3,16]{2,1,0:T(4,128)S(1)}, u32[]{:S(2)}, u32[]{:S(2)}) async-start(f32[128,3,16]{2,1,0:T(4,128)} %broadcast_in_dim.29), calls=%async_computation | async-start | bytes 524288 | tf_op jit(solution)/shard_map/all_to_all | solution.py:131
  26.9 29.6 %copy-start.33 = (s32[4]{0:T(128)S(1)}, s32[4]{0:T(128)}, u32[]{:S(2)}) copy-start(s32[4]{0:T(128)} %constant.52.clone) | copy-start | bytes 52
  26.9 608.4 %reduce-scatter.2.cloned.1.call-start = ((), (), s32[]{:S(2)}) async-start(), calls=%async_computation.6 | async-start | bytes 17842176 | tf_op jit(solution)/shard_map/reduce_scatter | solution.py:222
  39.7 16.6 %collective-permute-start = (bf16[128,2048]{1,0:T(8,128)(2,1)S(1)}, bf16[128,2048]{1,0:T(8,128)(2,1)S(1)}, u32[]{:S(2)}, u32[]{:S(2)}) collective-permute-start(bf16[128,2048]{1,0:T(8,128)(2,1)S(1)} %fusion.57), channel_id=1, source_target_pairs={{0,2},{2,0},{1,3},{3,1},{4,6},{6,4},{5,7},{7,5},{8,10},{10,8},{9,1... | collective-permute-start | bytes 1572872 | tf_op jit(solution)/shard_map/ppermute | solution.py:108
  56.3 5.7 copy-start.21
  56.4 2.9 collective-permute-start.1
  149.7 4.6 copy-start.20
  149.7 4.6 copy-start.22
  153.4 3.5 copy-start.6
  156.9 2.5 copy-start.12
  156.9 2.5 copy-start.19
  159.4 2.9 copy-start.5
  162.4 5.5 copy-start.9
  173.2 3.1 copy-start.14
  176.3 4.6 copy-start.2
  176.3 5.8 copy-start.8
  176.5 4.2 collective-permute-start.2
  180.8 1.3 copy-start.16
  180.9 16.9 %collective-permute-start.3 = (bf16[128,2048]{1,0:T(8,128)(2,1)S(1)}, bf16[128,2048]{1,0:T(8,128)(2,1)}, u32[]{:S(2)}, u32[]{:S(2)}) collective-permute-start(bf16[128,2048]{1,0:T(8,128)(2,1)S(1)} %fusion.87), channel_id=1, source_target_pairs={{0,2},{2,0},{1,3},{3,1},{4,6},{6,4},{5,7},{7,5},{8,10},{10,8},{9,1... | collective-permute-start | bytes 1572872 | tf_op jit(solution)/shard_map/ppermute | solution.py:119
  182.1 26.9 %collective-permute-start.8 = (bf16[128,2048]{1,0:T(8,128)(2,1)S(1)}, bf16[128,2048]{1,0:T(8,128)(2,1)}, u32[]{:S(2)}, u32[]{:S(2)}) collective-permute-start(bf16[128,2048]{1,0:T(8,128)(2,1)S(1)} %bitcast.266), channel_id=1, source_target_pairs={{0,2},{2,0},{1,3},{3,1},{4,6},{6,4},{5,7},{7,5},{8,10},{10,8},{9,1... | collective-permute-start | bytes 1572872 | tf_op jit(solution)/shard_map/ppermute | solution.py:108
  200.1 25.1 %collective-permute-start.4 = (bf16[128,2048]{1,0:T(8,128)(2,1)S(1)}, bf16[128,2048]{1,0:T(8,128)(2,1)S(1)}, u32[]{:S(2)}, u32[]{:S(2)}) collective-permute-start(bf16[128,2048]{1,0:T(8,128)(2,1)S(1)} %multiply_convert_fusion.4), channel_id=1, source_target_pairs={{0,2},{2,0},{1,3},{3,1},{4,6},{6,4},{5,7},{7,5},{8,10},{10,8},{9,1... | collective-permute-start | bytes 1572872 | tf_op jit(solution)/shard_map/ppermute | solution.py:108
  210.2 15.2 %collective-permute-start.9 = (bf16[2,128,2048]{2,1,0:T(8,128)(2,1)S(1)}, bf16[2,128,2048]{2,1,0:T(8,128)(2,1)S(1)}, u32[]{:S(2)}, u32[]{:S(2)}) collective-permute-start(bf16[2,128,2048]{2,1,0:T(8,128)(2,1)S(1)} %pad_maximum_fusion.7), channel_id=1, source_target_pairs={{0,1},{1,0},{2,3},{3,2},{4,5},{5,4},{6,7},{7,6},{8,9},{9,8},{10,11... | collective-permute-start | bytes 3145736 | tf_op jit(solution)/shard_map/ppermute | solution.py:110
  225.4 2.7 collective-permute-start.5
  303.7 8.4 %copy-start.18 = (bf16[4,128,2048]{2,1,0:T(8,128)(2,1)S(1)}, bf16[4,128,2048]{2,1,0:T(8,128)(2,1)}, u32[]{:S(2)}) copy-start(bf16[4,128,2048]{2,1,0:T(8,128)(2,1)} %pad_maximum_fusion.2) | copy-start | bytes 6291460
  303.7 9.9 %copy-start.34 = (bf16[2048,4224]{1,0:T(8,128)(2,1)S(1)}, bf16[2048,4224]{1,0:T(8,128)(2,1)}, u32[]{:S(2)}) copy-start(bf16[2048,4224]{1,0:T(8,128)(2,1)} %all-gather.5.cloned.1.call-done) | copy-start | bytes 51904516
  325.2 1.1 copy-start.23
  325.2 1.6 copy-start.25
  325.3 2.0 copy-start.27
  350.2 6.0 copy-start.26
  361.8 1.4 copy-start.24
  362.0 7.0 collective-permute-start.10
  368.9 4.2 collective-permute-start.6
  369.2 18.7 %collective-permute-start.11 = (bf16[128,2048]{1,0:T(8,128)(2,1)S(1)}, bf16[128,2048]{1,0:T(8,128)(2,1)S(1)}, u32[]{:S(2)}, u32[]{:S(2)}) collective-permute-start(bf16[128,2048]{1,0:T(8,128)(2,1)S(1)} %fusion.77), channel_id=1, source_target_pairs={{0,2},{2,0},{1,3},{3,1},{4,6},{6,4},{5,7},{7,5},{8,10},{10,8},{9,1... | collective-permute-start | bytes 1572872 | tf_op jit(solution)/shard_map/ppermute | solution.py:119
  373.3 29.2 %collective-permute-start.7 = (bf16[128,2048]{1,0:T(8,128)(2,1)S(1)}, bf16[128,2048]{1,0:T(8,128)(2,1)S(1)}, u32[]{:S(2)}, u32[]{:S(2)}) collective-permute-start(bf16[128,2048]{1,0:T(8,128)(2,1)S(1)} %fusion.81), channel_id=1, source_target_pairs={{0,2},{2,0},{1,3},{3,1},{4,6},{6,4},{5,7},{7,5},{8,10},{10,8},{9,1... | collective-permute-start | bytes 1572872 | tf_op jit(solution)/shard_map/ppermute | solution.py:119
  404.2 17.4 %collective-permute-start.12 = (bf16[128,2048]{1,0:T(8,128)(2,1)S(1)}, bf16[128,2048]{1,0:T(8,128)(2,1)S(1)}, u32[]{:S(2)}, u32[]{:S(2)}) collective-permute-start(bf16[128,2048]{1,0:T(8,128)(2,1)S(1)} %get-tuple-element.29), channel_id=1, source_target_pairs={{0,2},{2,0},{1,3},{3,1},{4,6},{6,4},{5,7},{7,5},{8,10},{10,8},{9,1... | collective-permute-start | bytes 1572872 | tf_op jit(solution)/shard_map/ppermute | solution.py:108
  421.7 3.1 copy-start.28
  421.7 2.9 collective-permute-start.13
  424.9 4.6 copy-start.17
  436.9 3.3 copy-start.7
  440.2 1.9 copy-start.13
  441.7 9.0 %slice-start = ((s8[10485760]{0:T(1024)(128)(4,1)}), s8[4194304]{0:T(1024)(128)(4,1)S(1)}, s32[]{:S(2)}) async-start(s8[10485760]{0:T(1024)(128)(4,1)} %bitcast.257), calls=%async_computation.7 | async-start | bytes 8388608
  444.1 6.7 slice-start.1
  446.2 3.2 copy-start.11
  446.2 3.2 copy-start.29
  446.2 3.1 copy-start.30
  446.2 4.5 slice-start.2
  456.0 5.4 copy-start.4
  456.0 9.3 %copy-start.15 = (bf16[512,512]{1,0:T(8,128)(2,1)S(1)}, bf16[512,512]{1,0:T(8,128)(2,1)}, u32[]{:S(2)}) copy-start(bf16[512,512]{1,0:T(8,128)(2,1)} %copy-done.14) | copy-start | bytes 1572868
  456.3 4.2 collective-permute-start.14
  461.4 20.1 %collective-permute-start.15 = (bf16[128,2048]{1,0:T(8,128)(2,1)}, bf16[128,2048]{1,0:T(8,128)(2,1)}, u32[]{:S(2)}, u32[]{:S(2)}) collective-permute-start(bf16[128,2048]{1,0:T(8,128)(2,1)} %fusion.73), channel_id=1, source_target_pairs={{0,2},{2,0},{1,3},{3,1},{4,6},{6,4},{5,7},{7,5},{8,10},{10,8},{9,1... | collective-permute-start | bytes 1572872 | tf_op jit(solution)/shard_map/ppermute | solution.py:119
  485.2 151.2 %all-to-all-start.1 = ((f32[128,3,16]{2,1,0:T(4,128)}), f32[128,3,16]{2,1,0:T(4,128)S(1)}, u32[]{:S(2)}, u32[]{:S(2)}) async-start(f32[128,3,16]{2,1,0:T(4,128)} %copy.104), calls=%async_computation.1 | async-start | bytes 524288 | tf_op jit(solution)/shard_map/all_to_all | solution.py:138
  636.5 5.4 copy-start.10
  636.5 5.4 copy-start.32
  636.5 157.6 %all-to-all-start.2 = ((bf16[32,64,2560]{2,1,0:T(8,128)(2,1)}), bf16[32,64,2560]{2,1,0:T(8,128)(2,1)}, u32[]{:S(2)}, u32[]{:S(2)}) async-start(bf16[32,64,2560]{2,1,0:T(8,128)(2,1)} %bitcast.259), calls=%async_computation.3 | async-start | bytes 20971520 | tf_op jit(solution)/shard_map/all_to_all | solution.py:124
  794.0 6.5 copy-start.1
Sparse Core Ops, SparseCore 0:
  12.4 121.3 all-gather.2
  136.9 166.7 all-gather.4
  350.3 284.9 reduce-scatter.1

commit v9 on v7

--- a/solution.py
+++ b/solution.py
@@ -60,7 +60,7 @@
     cols = right.shape[1]
     blocks = cols // width
     per = blocks - 1
-    tile = 512
+    tile = rows_out
     return pl.pallas_call(
         functools.partial(pack_kernel, per),
         grid=(rows_out // tile, blocks),

time: 761 us -> 758 us (level)
  Pallas kernels: 40.7 us -> 26.4 us
  waiting for transfers between devices: 502 us -> 513 us
    pallas_call x2, Pallas kernels: 40.7 us -> 26.4 us  [grad_pack(): pl.pallas_call(functools.partial(pack_kernel, per), grid=(rows_out // til...]
    all_to_all x1, waiting for transfers between devices: 156 us -> 169 us  [spread_sum(): got = lax.all_to_all(blocks, axis, 0, 0, tiled=False)]
  transfers between devices with their start and end apart: 22 -> 22, of which waited for: 18 -> 19; matrix products, arithmetic and copies ran while one was open for 17% -> 17% of each run, Pallas kernels for 3% -> 1%
where the time goes in v9:
time: 758 us; the launch traced here: 753 us
  waiting for transfers between devices  513 us (68%)
  matrix products  82.8 us (11%)
  local copies, waits for them, and re-layouts  45.4 us (6%)
  starting transfers between devices  36.9 us (5%)
  other arithmetic  33.1 us (4%)
  Pallas kernels  26.4 us (3%)
  between operations  14.9 us (2%)
    all_to_all x1, waiting for transfers between devices, spread_sum(): got = lax.all_to_all(blocks, axis, 0, 0, tiled=False)  169 us
    all_gather x1, waiting for transfers between devices, shards(): mlp_all = lax.all_gather(mlp_pack, 'dp', axis=0, tiled=True)  74.1 us
    all_gather x1, waiting for transfers between devices, shards(): attn_all = lax.all_gather(attn_pack, 'dp', axis=0, tiled=True)  71.8 us
    reduce_scatter x1, waiting for transfers between devices, shards(): lax.psum_scatter(mlp_grads, 'dp', scatter_dimension=0, tiled=True)  58.3 us
    ppermute x4, waiting for transfers between devices, row_sum(): lax.ppermute(theirs.astype(jnp.bfloat16), 'tensor', ACROSS)  57.3 us
    ppermute x4, waiting for transfers between devices, row_gather(): across = lax.ppermute(values, 'tensor', ACROSS)  56.2 us
    dot_general x8, matrix products, matmul_plain(): return jnp.dot(left, right, preferred_element_type=jnp.float32)  39.1 us
    pallas_call x2, Pallas kernels, grad_pack(): pl.pallas_call(functools.partial(pack_kernel, per), grid=(rows_out // til...  26.4 us
  transfers between devices with their start and end apart: 22, of which 19 were waited for; matrix products, arithmetic and copies ran while one was open for 17% of the time, Pallas kernels for 1%

profile of v9, /device:TPU:0, one launch (start us, length us, event | category | flops | bytes accessed | tf_op | source)
XLA Modules:
  0.0 752.9 jit_solution(3557098458939328357)
XLA Ops:
  12.3 1.9 pad_maximum_fusion.9
  15.7 11.1 %all-to-all-start = ((f32[128,3,16]{2,1,0:T(4,128)}), f32[128,3,16]{2,1,0:T(4,128)S(1)}, u32[]{:S(2)}, u32[]{:S(2)}) async-start(f32[128,3,16]{2,1,0:T(4,128)} %broadcast_in_dim.29), calls=%async_computation | async-start | bytes 524288 | tf_op jit(solution)/shard_map/all_to_all | solution.py:131
  27.7 11.2 %all-to-all-done = f32[128,3,16]{2,1,0:T(4,128)S(1)} async-done(((f32[128,3,16]{2,1,0:T(4,128)}), f32[128,3,16]{2,1,0:T(4,128)S(1)}, u32[]{:S(2)}, u32[]{:S(2)}) %all-to-all-start) | async-done | bytes 24608 | tf_op jit(solution)/shard_map/all_to_all | solution.py:131
  40.5 15.8 %collective-permute-done = bf16[128,2048]{1,0:T(8,128)(2,1)S(1)} collective-permute-done((bf16[128,2048]{1,0:T(8,128)(2,1)S(1)}, bf16[128,2048]{1,0:T(8,128)(2,1)S(1)}, u32[]{:S(2)}, u32[]{:S(2)}) %collective-permute-start) | collective-permute-done | bytes 524320 | tf_op jit(solution)/shard_map/ppermute | solution.py:108
  57.8 1.4 collective-permute-done.1
  59.2 2.8 pad_maximum_fusion.1
  62.0 71.8 %all-gather.3.cloned.1.call-done = bf16[2048,2560]{1,0:T(8,128)(2,1)} async-done(((bf16[64,2560]{1,0:T(8,128)(2,1)}), bf16[2048,2560]{1,0:T(8,128)(2,1)}) %all-gather.3.cloned.1.call-update) | async-done | bytes 10485776 | tf_op jit(solution)/shard_map/all_gather | solution.py:175
  133.8 5.3 slice_bitcast_fusion
  139.1 4.1 copy.86
  143.2 4.0 copy.88
  147.2 2.5 copy.89
  149.7 3.7 fusion.51
  154.3 2.5 fusion.18
  156.9 2.5 convolution_select_fusion.1
  159.4 2.9 fusion.20
  162.4 2.9 convolution_bitcast_fusion.2
  165.3 2.6 copy.92
  167.8 5.4 fusion.69
  173.2 3.1 fusion.24
  176.6 4.1 collective-permute-done.2
  182.1 1.3 collective-permute-start.8
  183.5 14.3 %collective-permute-done.3 = bf16[128,2048]{1,0:T(8,128)(2,1)} collective-permute-done((bf16[128,2048]{1,0:T(8,128)(2,1)S(1)}, bf16[128,2048]{1,0:T(8,128)(2,1)}, u32[]{:S(2)}, u32[]{:S(2)}) %collective-permute-start.3) | collective-permute-done | bytes 524320 | tf_op jit(solution)/shard_map/ppermute | solution.py:119
  197.8 2.1 multiply_reduce_fusion.3
  200.4 8.6 %collective-permute-done.8 = bf16[128,2048]{1,0:T(8,128)(2,1)} collective-permute-done((bf16[128,2048]{1,0:T(8,128)(2,1)S(1)}, bf16[128,2048]{1,0:T(8,128)(2,1)}, u32[]{:S(2)}, u32[]{:S(2)}) %collective-permute-start.8) | collective-permute-done | bytes 524320 | tf_op jit(solution)/shard_map/ppermute | solution.py:108
  210.5 14.8 %collective-permute-done.4 = bf16[128,2048]{1,0:T(8,128)(2,1)S(1)} collective-permute-done((bf16[128,2048]{1,0:T(8,128)(2,1)S(1)}, bf16[128,2048]{1,0:T(8,128)(2,1)S(1)}, u32[]{:S(2)}, u32[]{:S(2)}) %collective-permute-start.4) | collective-permute-done | bytes 524320 | tf_op jit(solution)/shard_map/ppermute | solution.py:108
  225.5 2.6 pad_maximum_fusion.3
  228.1 1.5 pad_maximum_fusion.2
  229.6 74.1 %all-gather.5.cloned.1.call-done = bf16[2048,4224]{1,0:T(8,128)(2,1)} async-done(((bf16[64,4224]{1,0:T(8,128)(2,1)}), bf16[2048,4224]{1,0:T(8,128)(2,1)}) %all-gather.5.cloned.1.call-update) | async-done | bytes 17301520 | tf_op jit(solution)/shard_map/all_gather | solution.py:176
  303.7 8.4 %fusion = f32[512,1408]{1,0:T(8,128)} fusion(bf16[512,2048]{1,0:T(8,128)(2,1)} %bitcast.277, bf16[2048,4224]{1,0:T(8,128)(2,1)} %all-gather.5.cloned.1.call-done), kind=kOutput, calls=%fused_computation.2 | convolution fusion | flops 2952790016 | bytes 10747904 | tf_op jit(solution)/shard_map/dot_general | solution.py:27
  312.0 1.5 copy-done.35
  313.6 5.0 fusion.6
  318.6 6.6 multiply_convert_fusion.1
  327.3 2.1 pad_maximum_fusion.right_ref
  329.4 15.7 %shard_map.247 = bf16[2048,4224]{1,0:T(8,128)(2,1)} custom-call(bf16[512,2048]{1,0:T(8,128)(2,1)} %bitcast.279, bf16[512,2048]{1,0:T(8,128)(2,1)} %bitcast.278, bf16[512,4224]{1,0:T(8,128)(2,1)} %pad_maximum_fusion.right_ref), custom_call_target="tpu_custom_call" | custom-call | flops 8858370048 | bytes 25821184 | tf_op jit(solution)/shard_map/pallas_call | solution.py:64
  345.1 6.0 fusion.4
  351.2 5.6 fusion.12
  358.1 5.5 fusion.2
  364.9 3.2 collective-permute-done.6
  368.9 14.0 %collective-permute-done.11 = bf16[128,2048]{1,0:T(8,128)(2,1)S(1)} collective-permute-done((bf16[128,2048]{1,0:T(8,128)(2,1)S(1)}, bf16[128,2048]{1,0:T(8,128)(2,1)S(1)}, u32[]{:S(2)}, u32[]{:S(2)}) %collective-permute-start.11) | collective-permute-done | bytes 524320 | tf_op jit(solution)/shard_map/ppermute | solution.py:119
  383.4 14.2 %collective-permute-done.7 = bf16[128,2048]{1,0:T(8,128)(2,1)S(1)} collective-permute-done((bf16[128,2048]{1,0:T(8,128)(2,1)S(1)}, bf16[128,2048]{1,0:T(8,128)(2,1)S(1)}, u32[]{:S(2)}, u32[]{:S(2)}) %collective-permute-start.7) | collective-permute-done | bytes 524320 | tf_op jit(solution)/shard_map/ppermute | solution.py:119
  397.6 1.7 fusion.127
  399.9 17.0 %collective-permute-done.12 = bf16[128,2048]{1,0:T(8,128)(2,1)S(1)} collective-permute-done((bf16[128,2048]{1,0:T(8,128)(2,1)S(1)}, bf16[128,2048]{1,0:T(8,128)(2,1)S(1)}, u32[]{:S(2)}, u32[]{:S(2)}) %collective-permute-start.12) | collective-permute-done | bytes 524320 | tf_op jit(solution)/shard_map/ppermute | solution.py:108
  417.1 2.6 collective-permute-done.13
  420.0 4.6 fusion.119
  425.9 1.6 copy.116
  427.5 3.2 fusion.54
  430.7 1.4 copy.101
  432.0 3.2 convolution_select_fusion
  435.3 1.5 multiply_convert_fusion.3
  437.2 1.9 convolution_bitcast_fusion
  439.2 2.1 multiply_reduce_fusion.1
  444.5 1.4 constant_dynamic-update-slice_fusion.5
  449.7 1.3 add_add_fusion
  451.6 4.0 collective-permute-done.14
  455.7 2.3 collective-permute-start.15
  460.3 14.7 %collective-permute-done.15 = bf16[128,2048]{1,0:T(8,128)(2,1)S(1)} collective-permute-done((bf16[128,2048]{1,0:T(8,128)(2,1)S(1)}, bf16[128,2048]{1,0:T(8,128)(2,1)S(1)}, u32[]{:S(2)}, u32[]{:S(2)}) %collective-permute-start.15) | collective-permute-done | bytes 524320 | tf_op jit(solution)/shard_map/ppermute | solution.py:119
  475.0 2.0 fusion.63
  478.0 7.5 %all-to-all-start.1 = ((f32[128,3,16]{2,1,0:T(4,128)}), f32[128,3,16]{2,1,0:T(4,128)S(1)}, u32[]{:S(2)}, u32[]{:S(2)}) async-start(f32[128,3,16]{2,1,0:T(4,128)} %copy.104), calls=%async_computation.1 | async-start | bytes 524288 | tf_op jit(solution)/shard_map/all_to_all | solution.py:138
  485.5 10.7 %shard_map.246 = bf16[2048,2560]{1,0:T(8,128)(2,1)} custom-call(bf16[512,2048]{1,0:T(8,128)(2,1)} %bitcast.274, bf16[512,2048]{1,0:T(8,128)(2,1)} %bitcast.276, bf16[512,2560]{1,0:T(8,128)(2,1)} %constant_dynamic-update-slice_fusion.4.right_ref), custom_call_target="tpu_custom_call" | custom-call | flops 5368709120 | bytes 17301504 | tf_op jit(solution)/shard_map/pallas_call | solution.py:64
  496.3 10.0 %all-to-all-start.2 = ((bf16[32,64,2560]{2,1,0:T(8,128)(2,1)}), bf16[32,64,2560]{2,1,0:T(8,128)(2,1)}, u32[]{:S(2)}, u32[]{:S(2)}) async-start(bf16[32,64,2560]{2,1,0:T(8,128)(2,1)} %bitcast.259), calls=%async_computation.2 | async-start | bytes 20971520 | tf_op jit(solution)/shard_map/all_to_all | solution.py:124
  508.4 169.0 %all-to-all-done.2 = bf16[32,64,2560]{2,1,0:T(8,128)(2,1)} async-done(((bf16[32,64,2560]{2,1,0:T(8,128)(2,1)}), bf16[32,64,2560]{2,1,0:T(8,128)(2,1)}, u32[]{:S(2)}, u32[]{:S(2)}) %all-to-all-start.2) | async-done | bytes 10485792 | tf_op jit(solution)/shard_map/all_to_all | solution.py:124
  677.3 6.5 convert_reduce_fusion
  684.7 58.3 %reduce-scatter.2.cloned.1.call-done = bf16[64,4224]{1,0:T(8,128)(2,1)} async-done(((bf16[2048,4224]{1,0:T(8,128)(2,1)}), bf16[64,4224]{1,0:T(8,128)(2,1)}) %reduce-scatter.2.cloned.1.call-update) | async-done | bytes 540688 | tf_op jit(solution)/shard_map/reduce_scatter | solution.py:222
  744.1 2.0 fusion.130
  (172 shorter events, 38.5 us)
Async XLA Ops:
  7.2 49.3 %copy-start = (s32[1,4,128]{2,1,0:T(4,128)S(1)}, s32[1,4,128]{2,1,0:T(4,128)}, u32[]{:S(2)}) copy-start(s32[1,4,128]{2,1,0:T(4,128)} %param.16) | copy-start | bytes 6148
  7.2 19.7 %copy-start.3 = (bf16[1,1,128,2048]{3,2,1,0:T(8,128)(2,1)S(1)}, bf16[1,1,128,2048]{3,2,1,0:T(8,128)(2,1)}, u32[]{:S(2)}) copy-start(bf16[1,1,128,2048]{3,2,1,0:T(8,128)(2,1)} %param.15) | copy-start | bytes 1572868
  7.2 126.6 %all-gather.3.cloned.1.call-start = ((), (), s32[]{:S(2)}) async-start(), calls=%async_computation.4 | async-start | bytes 10813440 | tf_op jit(solution)/shard_map/all_gather | solution.py:175
  11.5 0.7 copy-start.32
  12.3 291.4 %all-gather.5.cloned.1.call-start = ((), (), s32[]{:S(2)}) async-start(), calls=%async_computation.5 | async-start | bytes 17842176 | tf_op jit(solution)/shard_map/all_gather | solution.py:176
  15.7 23.1 %all-to-all-start = ((f32[128,3,16]{2,1,0:T(4,128)}), f32[128,3,16]{2,1,0:T(4,128)S(1)}, u32[]{:S(2)}, u32[]{:S(2)}) async-start(f32[128,3,16]{2,1,0:T(4,128)} %broadcast_in_dim.29), calls=%async_computation | async-start | bytes 524288 | tf_op jit(solution)/shard_map/all_to_all | solution.py:131
  26.9 29.6 %copy-start.34 = (s32[4]{0:T(128)S(1)}, s32[4]{0:T(128)}, u32[]{:S(2)}) copy-start(s32[4]{0:T(128)} %constant.52.clone) | copy-start | bytes 52
  26.9 716.1 %reduce-scatter.2.cloned.1.call-start = ((), (), s32[]{:S(2)}) async-start(), calls=%async_computation.6 | async-start | bytes 17842176 | tf_op jit(solution)/shard_map/reduce_scatter | solution.py:222
  39.7 16.6 %collective-permute-start = (bf16[128,2048]{1,0:T(8,128)(2,1)S(1)}, bf16[128,2048]{1,0:T(8,128)(2,1)S(1)}, u32[]{:S(2)}, u32[]{:S(2)}) collective-permute-start(bf16[128,2048]{1,0:T(8,128)(2,1)S(1)} %fusion.57), channel_id=1, source_target_pairs={{0,2},{2,0},{1,3},{3,1},{4,6},{6,4},{5,7},{7,5},{8,10},{10,8},{9,1... | collective-permute-start | bytes 1572872 | tf_op jit(solution)/shard_map/ppermute | solution.py:108
  56.3 5.7 copy-start.22
  56.4 2.9 collective-permute-start.1
  149.7 4.6 copy-start.21
  149.7 4.6 copy-start.23
  153.4 3.5 copy-start.6
  156.9 2.5 copy-start.12
  156.9 2.5 copy-start.20
  159.4 2.9 copy-start.5
  162.4 5.5 copy-start.9
  173.2 3.1 copy-start.14
  176.3 4.6 copy-start.2
  176.3 5.8 copy-start.8
  176.6 4.2 collective-permute-start.2
  180.8 1.3 copy-start.17
  181.0 16.9 %collective-permute-start.3 = (bf16[128,2048]{1,0:T(8,128)(2,1)S(1)}, bf16[128,2048]{1,0:T(8,128)(2,1)}, u32[]{:S(2)}, u32[]{:S(2)}) collective-permute-start(bf16[128,2048]{1,0:T(8,128)(2,1)S(1)} %fusion.87), channel_id=1, source_target_pairs={{0,2},{2,0},{1,3},{3,1},{4,6},{6,4},{5,7},{7,5},{8,10},{10,8},{9,1... | collective-permute-start | bytes 1572872 | tf_op jit(solution)/shard_map/ppermute | solution.py:119
  182.1 26.9 %collective-permute-start.8 = (bf16[128,2048]{1,0:T(8,128)(2,1)S(1)}, bf16[128,2048]{1,0:T(8,128)(2,1)}, u32[]{:S(2)}, u32[]{:S(2)}) collective-permute-start(bf16[128,2048]{1,0:T(8,128)(2,1)S(1)} %bitcast.266), channel_id=1, source_target_pairs={{0,2},{2,0},{1,3},{3,1},{4,6},{6,4},{5,7},{7,5},{8,10},{10,8},{9,1... | collective-permute-start | bytes 1572872 | tf_op jit(solution)/shard_map/ppermute | solution.py:108
  200.2 25.1 %collective-permute-start.4 = (bf16[128,2048]{1,0:T(8,128)(2,1)S(1)}, bf16[128,2048]{1,0:T(8,128)(2,1)S(1)}, u32[]{:S(2)}, u32[]{:S(2)}) collective-permute-start(bf16[128,2048]{1,0:T(8,128)(2,1)S(1)} %multiply_convert_fusion.4), channel_id=1, source_target_pairs={{0,2},{2,0},{1,3},{3,1},{4,6},{6,4},{5,7},{7,5},{8,10},{10,8},{9,1... | collective-permute-start | bytes 1572872 | tf_op jit(solution)/shard_map/ppermute | solution.py:108
  210.2 15.2 %collective-permute-start.9 = (bf16[2,128,2048]{2,1,0:T(8,128)(2,1)S(1)}, bf16[2,128,2048]{2,1,0:T(8,128)(2,1)S(1)}, u32[]{:S(2)}, u32[]{:S(2)}) collective-permute-start(bf16[2,128,2048]{2,1,0:T(8,128)(2,1)S(1)} %pad_maximum_fusion.7), channel_id=1, source_target_pairs={{0,1},{1,0},{2,3},{3,2},{4,5},{5,4},{6,7},{7,6},{8,9},{9,8},{10,11... | collective-permute-start | bytes 3145736 | tf_op jit(solution)/shard_map/ppermute | solution.py:110
  225.4 2.7 collective-permute-start.5
  303.7 8.4 %copy-start.19 = (bf16[4,128,2048]{2,1,0:T(8,128)(2,1)S(1)}, bf16[4,128,2048]{2,1,0:T(8,128)(2,1)}, u32[]{:S(2)}) copy-start(bf16[4,128,2048]{2,1,0:T(8,128)(2,1)} %pad_maximum_fusion.2) | copy-start | bytes 6291460
  303.7 9.9 %copy-start.35 = (bf16[2048,4224]{1,0:T(8,128)(2,1)S(1)}, bf16[2048,4224]{1,0:T(8,128)(2,1)}, u32[]{:S(2)}) copy-start(bf16[2048,4224]{1,0:T(8,128)(2,1)} %all-gather.5.cloned.1.call-done) | copy-start | bytes 51904516
  325.2 1.1 copy-start.24
  325.2 1.6 copy-start.26
  325.3 2.0 copy-start.28
  345.1 6.0 copy-start.27
  356.7 1.4 copy-start.25
  357.0 7.0 collective-permute-start.10
  363.9 4.2 collective-permute-start.6
  364.1 18.8 %collective-permute-start.11 = (bf16[128,2048]{1,0:T(8,128)(2,1)S(1)}, bf16[128,2048]{1,0:T(8,128)(2,1)S(1)}, u32[]{:S(2)}, u32[]{:S(2)}) collective-permute-start(bf16[128,2048]{1,0:T(8,128)(2,1)S(1)} %fusion.77), channel_id=1, source_target_pairs={{0,2},{2,0},{1,3},{3,1},{4,6},{6,4},{5,7},{7,5},{8,10},{10,8},{9,1... | collective-permute-start | bytes 1572872 | tf_op jit(solution)/shard_map/ppermute | solution.py:119
  368.2 29.4 %collective-permute-start.7 = (bf16[128,2048]{1,0:T(8,128)(2,1)S(1)}, bf16[128,2048]{1,0:T(8,128)(2,1)S(1)}, u32[]{:S(2)}, u32[]{:S(2)}) collective-permute-start(bf16[128,2048]{1,0:T(8,128)(2,1)S(1)} %fusion.81), channel_id=1, source_target_pairs={{0,2},{2,0},{1,3},{3,1},{4,6},{6,4},{5,7},{7,5},{8,10},{10,8},{9,1... | collective-permute-start | bytes 1572872 | tf_op jit(solution)/shard_map/ppermute | solution.py:119
  399.4 17.5 %collective-permute-start.12 = (bf16[128,2048]{1,0:T(8,128)(2,1)S(1)}, bf16[128,2048]{1,0:T(8,128)(2,1)S(1)}, u32[]{:S(2)}, u32[]{:S(2)}) collective-permute-start(bf16[128,2048]{1,0:T(8,128)(2,1)S(1)} %get-tuple-element.25), channel_id=1, source_target_pairs={{0,2},{2,0},{1,3},{3,1},{4,6},{6,4},{5,7},{7,5},{8,10},{10,8},{9,1... | collective-permute-start | bytes 1572872 | tf_op jit(solution)/shard_map/ppermute | solution.py:108
  417.0 3.0 copy-start.29
  417.0 2.7 collective-permute-start.13
  420.0 4.6 copy-start.18
  432.0 3.3 copy-start.7
  435.3 1.9 copy-start.13
  436.8 9.1 %slice-start = ((s8[10485760]{0:T(1024)(128)(4,1)}), s8[4194304]{0:T(1024)(128)(4,1)S(1)}, s32[]{:S(2)}) async-start(s8[10485760]{0:T(1024)(128)(4,1)} %bitcast.257), calls=%async_computation.7 | async-start | bytes 8388608
  439.2 6.7 slice-start.1
  441.3 3.2 copy-start.11
  441.3 3.2 copy-start.30
  441.3 3.1 copy-start.31
  441.3 4.5 slice-start.2
  451.1 4.6 copy-start.4
  451.1 8.3 %copy-start.15 = (bf16[512,512]{1,0:T(8,128)(2,1)S(1)}, bf16[512,512]{1,0:T(8,128)(2,1)}, u32[]{:S(2)}) copy-start(bf16[512,512]{1,0:T(8,128)(2,1)} %copy-done.14) | copy-start | bytes 1572868
  451.3 4.2 collective-permute-start.14
  455.6 2.5 copy-start.16
  455.7 19.3 %collective-permute-start.15 = (bf16[128,2048]{1,0:T(8,128)(2,1)S(1)}, bf16[128,2048]{1,0:T(8,128)(2,1)S(1)}, u32[]{:S(2)}, u32[]{:S(2)}) collective-permute-start(bf16[128,2048]{1,0:T(8,128)(2,1)S(1)} %fusion.73), channel_id=1, source_target_pairs={{0,2},{2,0},{1,3},{3,1},{4,6},{6,4},{5,7},{7,5},{8,10},{10,8},{9,1... | collective-permute-start | bytes 1572872 | tf_op jit(solution)/shard_map/ppermute | solution.py:119
  478.0 18.4 %all-to-all-start.1 = ((f32[128,3,16]{2,1,0:T(4,128)}), f32[128,3,16]{2,1,0:T(4,128)S(1)}, u32[]{:S(2)}, u32[]{:S(2)}) async-start(f32[128,3,16]{2,1,0:T(4,128)} %copy.104), calls=%async_computation.1 | async-start | bytes 524288 | tf_op jit(solution)/shard_map/all_to_all | solution.py:138
  496.3 10.0 %copy-start.10 = (f32[128,2048]{1,0:T(8,128)S(1)}, f32[128,2048]{1,0:T(8,128)}, u32[]{:S(2)}) copy-start(f32[128,2048]{1,0:T(8,128)} %get-tuple-element.26) | copy-start | bytes 3145732
  496.3 10.0 %copy-start.33 = (f32[128]{0:T(128)S(1)}, f32[128]{0:T(128)}, u32[]{:S(2)}) copy-start(f32[128]{0:T(128)} %get-tuple-element.52) | copy-start | bytes 1540
  496.3 181.0 %all-to-all-start.2 = ((bf16[32,64,2560]{2,1,0:T(8,128)(2,1)}), bf16[32,64,2560]{2,1,0:T(8,128)(2,1)}, u32[]{:S(2)}, u32[]{:S(2)}) async-start(bf16[32,64,2560]{2,1,0:T(8,128)(2,1)} %bitcast.259), calls=%async_computation.2 | async-start | bytes 20971520 | tf_op jit(solution)/shard_map/all_to_all | solution.py:124
  677.3 68.8 %copy-start.1 = (s32[1,4,128]{2,1,0:T(4,128)S(1)}, s32[1,4,128]{2,1,0:T(4,128)}, u32[]{:S(2)}) copy-start(s32[1,4,128]{2,1,0:T(4,128)} %param.16) | copy-start | bytes 6148
Sparse Core Ops, SparseCore 0:
  12.4 121.3 all-gather.2
  136.9 166.7 all-gather.4
  345.2 397.7 reduce-scatter.1

commit v10 on v9

--- a/solution.py
+++ b/solution.py
@@ -123,6 +123,44 @@
     blocks = values.reshape((count, -1) + values.shape[1:])
     got = lax.all_to_all(blocks, axis, 0, 0, tiled=False)
     return got.astype(jnp.float32).sum(axis=0)
+
+
+def ring_pairs(step, stride, size):
+    pairs = []
+    for i in range(32):
+        pos = (i // stride) % size
+        pairs.append((i, i + (((pos + step) % size) - pos) * stride))
+    return pairs
+
+
+def ring_stage(chunks, pos, stride, size):
+    half = chunks.shape[-1] // 2
+    result = []
+    for step, cols in ((1, slice(0, half)), (size - 1, slice(half, None))):
+        own = chunks[..., cols]
+        pairs = ring_pairs(step, stride, size)
+
+        def pick(k):
+            return lax.dynamic_index_in_dim(own, (pos - k * step) % size, 0, keepdims=False)
+
+        acc = pick(1).astype(jnp.float32)
+        for k in range(2, size + 1):
+            got = lax.ppermute(acc.astype(jnp.bfloat16), "dp", pairs)
+            acc = pick(k % size).astype(jnp.float32) + got.astype(jnp.float32)
+        result.append(acc)
+    return jnp.concatenate(result, axis=-1)
+
+
+def ring_sum(values):
+    index = lax.axis_index("dp")
+    x_pos, y_pos, z_pos = index % 4, (index // 4) % 2, index // 8
+    blocks = values.reshape((4, 2, 4, -1) + values.shape[1:])
+    along_x = ring_stage(jnp.moveaxis(blocks, 2, 0), x_pos, 1, 4)
+    along_z = ring_stage(along_x.astype(jnp.bfloat16), z_pos, 8, 4)
+    keep = lax.dynamic_index_in_dim(along_z, y_pos, 0, keepdims=False)
+    give = lax.dynamic_index_in_dim(along_z, 1 - y_pos, 0, keepdims=False)
+    pair = [(i, i ^ 4) for i in range(32)]
+    return keep + lax.ppermute(give.astype(jnp.bfloat16), "dp", pair).astype(jnp.float32)
 
 
 def small_gather(vectors):
@@ -242,7 +280,7 @@
         jnp.concatenate([d_query, d_forget, d_value, d_outgate, gated], axis=1),
         local_width,
     )
-    attn_red = spread_sum(attn_grads, "dp", 32)
+    attn_red = ring_sum(attn_grads)
     d_normed = row_sum(
         times_trans(d_query, wq_all)
         + times_trans(d_forget, wf_all)

time: 758 us -> 659 us (0.87)
  waiting for transfers between devices: 513 us -> 355 us
  local copies, waits for them, and re-layouts: 45.4 us -> 70 us
  starting transfers between devices: 36.9 us -> 51 us
  other arithmetic: 33.1 us -> 46.8 us
    all_to_all x1 -> x0, waiting for transfers between devices: 169 us -> none  [spread_sum(): got = lax.all_to_all(blocks, axis, 0, 0, tiled=False)]
    ppermute x0 -> x13, waiting for transfers between devices: none -> 82 us  [the longest x12 78.1 us: ring_stage(): got = lax.ppermute(acc.astype(jnp.bfloat16), 'dp', pairs)]
    reduce_scatter x1, waiting for transfers between devices: 58.3 us -> 0.01 us  [shards(): lax.psum_scatter(mlp_grads, 'dp', scatter_dimension=0, tiled=True)]
    ppermute x0 -> x13, starting transfers between devices: none -> 22.8 us  [the longest x12 20.1 us: ring_stage(): got = lax.ppermute(acc.astype(jnp.bfloat16), 'dp', pairs)]
    convert_element_type x0 -> x9, other arithmetic: none -> 12.4 us  [the longest x8 12.3 us: ring_stage(): got = lax.ppermute(acc.astype(jnp.bfloat16), 'dp', pairs)]
    ppermute x4, waiting for transfers between devices: 57.3 us -> 47 us  [row_sum(): lax.ppermute(theirs.astype(jnp.bfloat16), 'tensor', ACROSS)]
    all_to_all x1 -> x0, starting transfers between devices: 10 us -> none  [spread_sum(): got = lax.all_to_all(blocks, axis, 0, 0, tiled=False)]
    slice x0 -> x1, local copies, waits for them, and re-layouts: none -> 9.37 us  [ring_stage(): own = chunks[..., cols]]
  transfers between devices with their start and end apart: 22 -> 34, of which waited for: 19 -> 25; matrix products, arithmetic and copies ran while one was open for 17% -> 26% of each run, Pallas kernels for 1% -> 2%
where the time goes in v10:
time: 659 us; the launch traced here: 653 us
  waiting for transfers between devices  355 us (54%)
  matrix products  88.8 us (13%)
  local copies, waits for them, and re-layouts  70 us (11%)
  starting transfers between devices  51 us (8%)
  other arithmetic  46.8 us (7%)
  Pallas kernels  26.4 us (4%)
  between operations  15.4 us (2%)
    ppermute x12, waiting for transfers between devices, ring_stage(): got = lax.ppermute(acc.astype(jnp.bfloat16), 'dp', pairs)  78.1 us
    all_gather x1, waiting for transfers between devices, shards(): mlp_all = lax.all_gather(mlp_pack, 'dp', axis=0, tiled=True)  73.2 us
    all_gather x1, waiting for transfers between devices, shards(): attn_all = lax.all_gather(attn_pack, 'dp', axis=0, tiled=True)  72.5 us
    ppermute x4, waiting for transfers between devices, row_gather(): across = lax.ppermute(values, 'tensor', ACROSS)  56.6 us
    ppermute x4, waiting for transfers between devices, row_sum(): lax.ppermute(theirs.astype(jnp.bfloat16), 'tensor', ACROSS)  47 us
    dot_general x8, matrix products, matmul_plain(): return jnp.dot(left, right, preferred_element_type=jnp.float32)  38.5 us
    dot_general x8, matrix products, times_trans(): lax.dot_general(left, right, (((1,), (1,)), ((), ())), preferred_element_...  31.9 us
    pallas_call x2, Pallas kernels, grad_pack(): pl.pallas_call(functools.partial(pack_kernel, per), grid=(rows_out // til...  26.4 us
  transfers between devices with their start and end apart: 34, of which 25 were waited for; matrix products, arithmetic and copies ran while one was open for 26% of the time, Pallas kernels for 2%

profile of v10, /device:TPU:0, one launch (start us, length us, event | category | flops | bytes accessed | tf_op | source)
XLA Modules:
  0.0 653.1 jit_solution(16532576953574524784)
XLA Ops:
  15.1 11.1 %all-to-all-start = ((f32[128,3,16]{2,1,0:T(4,128)}), f32[128,3,16]{2,1,0:T(4,128)S(1)}, u32[]{:S(2)}, u32[]{:S(2)}) async-start(f32[128,3,16]{2,1,0:T(4,128)} %broadcast_in_dim.29), calls=%async_computation | async-start | bytes 524288 | tf_op jit(solution)/shard_map/all_to_all | solution.py:169
  27.1 11.5 %all-to-all-done = f32[128,3,16]{2,1,0:T(4,128)S(1)} async-done(((f32[128,3,16]{2,1,0:T(4,128)}), f32[128,3,16]{2,1,0:T(4,128)S(1)}, u32[]{:S(2)}, u32[]{:S(2)}) %all-to-all-start) | async-done | bytes 24608 | tf_op jit(solution)/shard_map/all_to_all | solution.py:169
  40.2 15.4 %collective-permute-done = bf16[128,2048]{1,0:T(8,128)(2,1)S(1)} collective-permute-done((bf16[128,2048]{1,0:T(8,128)(2,1)S(1)}, bf16[128,2048]{1,0:T(8,128)(2,1)S(1)}, u32[]{:S(2)}, u32[]{:S(2)}) %collective-permute-start) | collective-permute-done | bytes 524320 | tf_op jit(solution)/shard_map/ppermute | solution.py:108
  58.6 2.8 pad_maximum_fusion.1
  61.4 72.5 %all-gather.3.cloned.1.call-done = bf16[2048,2560]{1,0:T(8,128)(2,1)} async-done(((bf16[64,2560]{1,0:T(8,128)(2,1)}), bf16[2048,2560]{1,0:T(8,128)(2,1)}) %all-gather.3.cloned.1.call-update) | async-done | bytes 10485776 | tf_op jit(solution)/shard_map/all_gather | solution.py:213
  133.9 5.3 slice_bitcast_fusion
  139.2 4.2 copy.89
  143.3 4.0 copy.91
  149.8 3.6 fusion.57
  155.4 2.5 fusion.24
  157.9 2.5 convolution_select_fusion.1
  160.4 2.9 fusion.26
  164.3 2.9 convolution_bitcast_fusion.2
  168.9 4.9 fusion.75
  173.8 3.1 fusion.30
  177.2 4.1 collective-permute-done.2
  184.2 13.7 %collective-permute-done.3 = bf16[128,2048]{1,0:T(8,128)(2,1)} collective-permute-done((bf16[128,2048]{1,0:T(8,128)(2,1)S(1)}, bf16[128,2048]{1,0:T(8,128)(2,1)}, u32[]{:S(2)}, u32[]{:S(2)}) %collective-permute-start.3) | collective-permute-done | bytes 524320 | tf_op jit(solution)/shard_map/ppermute | solution.py:119
  200.6 8.5 %collective-permute-done.8 = bf16[128,2048]{1,0:T(8,128)(2,1)} collective-permute-done((bf16[128,2048]{1,0:T(8,128)(2,1)S(1)}, bf16[128,2048]{1,0:T(8,128)(2,1)}, u32[]{:S(2)}, u32[]{:S(2)}) %collective-permute-start.8) | collective-permute-done | bytes 524320 | tf_op jit(solution)/shard_map/ppermute | solution.py:108
  210.5 15.7 %collective-permute-done.4 = bf16[128,2048]{1,0:T(8,128)(2,1)S(1)} collective-permute-done((bf16[128,2048]{1,0:T(8,128)(2,1)S(1)}, bf16[128,2048]{1,0:T(8,128)(2,1)S(1)}, u32[]{:S(2)}, u32[]{:S(2)}) %collective-permute-start.4) | collective-permute-done | bytes 524320 | tf_op jit(solution)/shard_map/ppermute | solution.py:108
  226.4 2.6 pad_maximum_fusion.3
  230.5 73.2 %all-gather.5.cloned.1.call-done = bf16[2048,4224]{1,0:T(8,128)(2,1)} async-done(((bf16[64,4224]{1,0:T(8,128)(2,1)}), bf16[2048,4224]{1,0:T(8,128)(2,1)}) %all-gather.5.cloned.1.call-update) | async-done | bytes 17301520 | tf_op jit(solution)/shard_map/all_gather | solution.py:214
  303.7 8.4 %fusion = f32[512,1408]{1,0:T(8,128)} fusion(bf16[512,2048]{1,0:T(8,128)(2,1)} %bitcast.329, bf16[2048,4224]{1,0:T(8,128)(2,1)} %all-gather.5.cloned.1.call-done), kind=kOutput, calls=%fused_computation.2 | convolution fusion | flops 2952790016 | bytes 10747904 | tf_op jit(solution)/shard_map/dot_general | solution.py:27
  313.6 5.0 fusion.6
  318.6 6.6 %multiply_convert_fusion.1 = (bf16[512,1408]{1,0:T(8,128)(2,1)S(1)}, bf16[512,1408]{1,0:T(8,128)(2,1)S(1)}, bf16[512,1408]{1,0:T(8,128)(2,1)S(1)}) fusion(f32[512,1408]{1,0:T(8,128)} %fusion, f32[512,1408]{1,0:T(8,128)} %fusion.6, bf16[512,2048]{1,0:T(8,128)(2,1)S(1)} %bitcast.333, bf16[2048,4224]{1,0:T(8,128)(2,1)S(1)} %copy-done.45), kind=kOutput, calls=%fused_computation.18 | convolution fusion | flops 2963603456 | bytes 17956864 | tf_op jit(solution)/shard_map/dot_general | solution.py:27
  329.5 15.7 %shard_map.247 = bf16[2048,4224]{1,0:T(8,128)(2,1)} custom-call(bf16[512,2048]{1,0:T(8,128)(2,1)} %bitcast.331, bf16[512,2048]{1,0:T(8,128)(2,1)} %bitcast.330, bf16[512,4224]{1,0:T(8,128)(2,1)} %pad_maximum_fusion.right_ref), custom_call_target="tpu_custom_call" | custom-call | flops 8858370048 | bytes 25821184 | tf_op jit(solution)/shard_map/pallas_call | solution.py:64
  345.1 6.0 fusion.4
  351.2 5.6 fusion.12
  358.1 5.5 fusion.2
  364.9 3.2 collective-permute-done.6
  368.9 14.0 %collective-permute-done.11 = bf16[128,2048]{1,0:T(8,128)(2,1)S(1)} collective-permute-done((bf16[128,2048]{1,0:T(8,128)(2,1)S(1)}, bf16[128,2048]{1,0:T(8,128)(2,1)S(1)}, u32[]{:S(2)}, u32[]{:S(2)}) %collective-permute-start.11) | collective-permute-done | bytes 524320 | tf_op jit(solution)/shard_map/ppermute | solution.py:119
  383.4 14.2 %collective-permute-done.7 = bf16[128,2048]{1,0:T(8,128)(2,1)S(1)} collective-permute-done((bf16[128,2048]{1,0:T(8,128)(2,1)S(1)}, bf16[128,2048]{1,0:T(8,128)(2,1)S(1)}, u32[]{:S(2)}, u32[]{:S(2)}) %collective-permute-start.7) | collective-permute-done | bytes 524320 | tf_op jit(solution)/shard_map/ppermute | solution.py:119
  399.9 17.0 %collective-permute-done.12 = bf16[128,2048]{1,0:T(8,128)(2,1)S(1)} collective-permute-done((bf16[128,2048]{1,0:T(8,128)(2,1)S(1)}, bf16[128,2048]{1,0:T(8,128)(2,1)S(1)}, u32[]{:S(2)}, u32[]{:S(2)}) %collective-permute-start.12) | collective-permute-done | bytes 524320 | tf_op jit(solution)/shard_map/ppermute | solution.py:108
  418.1 3.0 collective-permute-done.13
  422.7 4.6 fusion.135
  430.2 3.2 fusion.60
  434.8 3.3 convolution_select_fusion
  449.5 10.8 %shard_map.246 = bf16[2048,2560]{1,0:T(8,128)(2,1)} custom-call(bf16[512,2048]{1,0:T(8,128)(2,1)} %bitcast.326, bf16[512,2048]{1,0:T(8,128)(2,1)} %bitcast.328, bf16[512,2560]{1,0:T(8,128)(2,1)} %constant_dynamic-update-slice_fusion.4.right_ref), custom_call_target="tpu_custom_call" | custom-call | flops 5368709120 | bytes 17301504 | tf_op jit(solution)/shard_map/pallas_call | solution.py:64
  460.3 9.1 %copy.144 = bf16[4,2,4,64,2560]{4,3,1,0,2:T(8,128)(2,1)} copy(bf16[4,2,4,64,2560]{4,3,2,1,0:T(8,128)(2,1)} %bitcast.311) | data formatting | bytes 20971520 | tf_op jit(solution)/shard_map/reshape | solution.py:157
  469.4 9.4 %fusion.146 = (bf16[4,4,2,64,1280]{4,3,2,1,0:T(8,128)(2,1)}, bf16[4,4,2,64,1280]{4,3,2,1,0:T(8,128)(2,1)}) fusion(bf16[4,4,2,64,2560]{4,3,2,1,0:T(8,128)(2,1)} %bitcast.310), kind=kLoop, calls=%fused_computation.241 | loop fusion | bytes 20971520 | tf_op jit(solution)/shard_map/slice | solution.py:140
  485.9 2.9 fusion.39
  488.8 2.9 fusion.37
  491.8 2.9 fusion.35
  494.6 3.0 add_add_fusion
  500.4 11.8 %collective-permute-done.16 = bf16[4,2,64,1280]{3,2,1,0:T(8,128)(2,1)S(1)} collective-permute-done((bf16[4,2,64,1280]{3,2,1,0:T(8,128)(2,1)S(1)}, bf16[4,2,64,1280]{3,2,1,0:T(8,128)(2,1)S(1)}, u32[]{:S(2)}, u32[]{:S(2)}) %collective-permute-start.16) | collective-permute-done | bytes 1310752 | tf_op jit(solution)/shard_map/ppermute | solution.py:148
  512.1 2.7 fusion.19
  515.4 3.1 fusion.16
  518.5 3.0 collective-permute-start.23
  522.8 23.7 %collective-permute-done.17 = bf16[4,2,64,1280]{3,2,1,0:T(8,128)(2,1)} collective-permute-done((bf16[4,2,64,1280]{3,2,1,0:T(8,128)(2,1)}, bf16[4,2,64,1280]{3,2,1,0:T(8,128)(2,1)}, u32[]{:S(2)}, u32[]{:S(2)}) %collective-permute-start.17) | collective-permute-done | bytes 1310752 | tf_op jit(solution)/shard_map/ppermute | solution.py:148
  546.5 3.1 fusion.20
  553.2 3.1 fusion.17
  556.3 3.2 collective-permute-start.24
  559.5 5.0 collective-permute-done.15
  564.5 2.6 fusion.69
  568.0 8.5 %all-to-all-start.1 = ((f32[128,3,16]{2,1,0:T(4,128)}), f32[128,3,16]{2,1,0:T(4,128)S(1)}, u32[]{:S(2)}, u32[]{:S(2)}) async-start(f32[128,3,16]{2,1,0:T(4,128)} %copy.107), calls=%async_computation.1 | async-start | bytes 524288 | tf_op jit(solution)/shard_map/all_to_all | solution.py:176
  576.5 17.2 %collective-permute-done.18 = bf16[4,2,64,1280]{3,2,1,0:T(8,128)(2,1)} collective-permute-done((bf16[4,2,64,1280]{3,2,1,0:T(8,128)(2,1)}, bf16[4,2,64,1280]{3,2,1,0:T(8,128)(2,1)}, u32[]{:S(2)}, u32[]{:S(2)}) %collective-permute-start.18) | collective-permute-done | bytes 1310752 | tf_op jit(solution)/shard_map/ppermute | solution.py:148
  596.4 3.1 collective-permute-done.24
  601.6 2.6 collective-permute-start.25
  604.1 7.6 %collective-permute-done.19 = bf16[2,64,1280]{2,1,0:T(8,128)(2,1)S(1)} collective-permute-done((bf16[2,64,1280]{2,1,0:T(8,128)(2,1)S(1)}, bf16[2,64,1280]{2,1,0:T(8,128)(2,1)S(1)}, u32[]{:S(2)}, u32[]{:S(2)}) %collective-permute-start.19) | collective-permute-done | bytes 327712 | tf_op jit(solution)/shard_map/ppermute | solution.py:148
  612.0 3.3 collective-permute-start.26
  615.2 8.5 %collective-permute-done.20 = bf16[2,64,1280]{2,1,0:T(8,128)(2,1)S(1)} collective-permute-done((bf16[2,64,1280]{2,1,0:T(8,128)(2,1)S(1)}, bf16[2,64,1280]{2,1,0:T(8,128)(2,1)S(1)}, u32[]{:S(2)}, u32[]{:S(2)}) %collective-permute-start.20) | collective-permute-done | bytes 327712 | tf_op jit(solution)/shard_map/ppermute | solution.py:148
  625.8 3.8 collective-permute-start.27
  629.6 4.4 collective-permute-done.21
  634.3 2.7 collective-permute-start.28
  639.0 3.9 collective-permute-done.28
  (228 shorter events, 87.6 us)
Async XLA Ops:
  7.2 48.7 %copy-start = (s32[1,4,128]{2,1,0:T(4,128)S(1)}, s32[1,4,128]{2,1,0:T(4,128)}, u32[]{:S(2)}) copy-start(s32[1,4,128]{2,1,0:T(4,128)} %param.16) | copy-start | bytes 6148
  7.2 7.2 %copy-start.41 = (f32[16]{0:T(128)S(1)}, f32[16]{0:T(128)}, u32[]{:S(2)}) copy-start(f32[16]{0:T(128)} %param.24) | copy-start | bytes 196
  7.2 7.2 %copy-start.42 = (f32[16]{0:T(128)S(1)}, f32[16]{0:T(128)}, u32[]{:S(2)}) copy-start(f32[16]{0:T(128)} %param.18) | copy-start | bytes 196
  7.2 7.2 %copy-start.43 = (f32[16]{0:T(128)S(1)}, f32[16]{0:T(128)}, u32[]{:S(2)}) copy-start(f32[16]{0:T(128)} %param.17) | copy-start | bytes 196
  7.2 19.1 %copy-start.3 = (bf16[1,1,128,2048]{3,2,1,0:T(8,128)(2,1)S(1)}, bf16[1,1,128,2048]{3,2,1,0:T(8,128)(2,1)}, u32[]{:S(2)}) copy-start(bf16[1,1,128,2048]{3,2,1,0:T(8,128)(2,1)} %param.15) | copy-start | bytes 1572868
  7.2 126.6 %all-gather.3.cloned.1.call-start = ((), (), s32[]{:S(2)}) async-start(), calls=%async_computation.3 | async-start | bytes 10813440 | tf_op jit(solution)/shard_map/all_gather | solution.py:213
  12.3 291.4 %all-gather.5.cloned.1.call-start = ((), (), s32[]{:S(2)}) async-start(), calls=%async_computation.4 | async-start | bytes 17842176 | tf_op jit(solution)/shard_map/all_gather | solution.py:214
  15.1 23.4 %all-to-all-start = ((f32[128,3,16]{2,1,0:T(4,128)}), f32[128,3,16]{2,1,0:T(4,128)S(1)}, u32[]{:S(2)}, u32[]{:S(2)}) async-start(f32[128,3,16]{2,1,0:T(4,128)} %broadcast_in_dim.29), calls=%async_computation | async-start | bytes 524288 | tf_op jit(solution)/shard_map/all_to_all | solution.py:169
  26.3 617.6 %reduce-scatter.2.cloned.1.call-start = ((), (), s32[]{:S(2)}) async-start(), calls=%async_computation.5 | async-start | bytes 17842176 | tf_op jit(solution)/shard_map/reduce_scatter | solution.py:260
  27.1 28.7 %copy-start.38 = (f32[128]{0:T(128)}, f32[128]{0:T(128)S(1)}, u32[]{:S(2)}) copy-start(f32[128]{0:T(128)S(1)} %get-tuple-element.55) | copy-start | bytes 1540
  39.2 16.6 %copy-start.36 = (f32[2048]{0:T(1024)}, f32[2048]{0:T(1024)S(1)}, u32[]{:S(2)}) copy-start(f32[2048]{0:T(1024)S(1)} %mul.250) | copy-start | bytes 24580
  39.2 16.7 %copy-start.44 = (s32[4]{0:T(128)S(1)}, s32[4]{0:T(128)}, u32[]{:S(2)}) copy-start(s32[4]{0:T(128)} %constant.215.clone) | copy-start | bytes 52
  39.4 16.3 %collective-permute-start = (bf16[128,2048]{1,0:T(8,128)(2,1)S(1)}, bf16[128,2048]{1,0:T(8,128)(2,1)S(1)}, u32[]{:S(2)}, u32[]{:S(2)}) collective-permute-start(bf16[128,2048]{1,0:T(8,128)(2,1)S(1)} %fusion.63), channel_id=1, source_target_pairs={{0,2},{2,0},{1,3},{3,1},{4,6},{6,4},{5,7},{7,5},{8,10},{10,8},{9,1... | collective-permute-start | bytes 1572872 | tf_op jit(solution)/shard_map/ppermute | solution.py:108
  55.6 5.8 copy-start.25
  55.8 2.9 collective-permute-start.1
  149.8 4.6 copy-start.26
  153.3 4.6 copy-start.6
  168.9 4.9 copy-start.13
  173.8 3.1 copy-start.17
  176.9 4.5 copy-start.2
  177.1 6.0 copy-start.8
  177.1 4.2 collective-permute-start.2
  181.5 16.4 %collective-permute-start.3 = (bf16[128,2048]{1,0:T(8,128)(2,1)S(1)}, bf16[128,2048]{1,0:T(8,128)(2,1)}, u32[]{:S(2)}, u32[]{:S(2)}) collective-permute-start(bf16[128,2048]{1,0:T(8,128)(2,1)S(1)} %fusion.93), channel_id=1, source_target_pairs={{0,2},{2,0},{1,3},{3,1},{4,6},{6,4},{5,7},{7,5},{8,10},{10,8},{9,1... | collective-permute-start | bytes 1572872 | tf_op jit(solution)/shard_map/ppermute | solution.py:119
  183.1 26.0 %collective-permute-start.8 = (bf16[128,2048]{1,0:T(8,128)(2,1)S(1)}, bf16[128,2048]{1,0:T(8,128)(2,1)}, u32[]{:S(2)}, u32[]{:S(2)}) collective-permute-start(bf16[128,2048]{1,0:T(8,128)(2,1)S(1)} %bitcast.318), channel_id=1, source_target_pairs={{0,2},{2,0},{1,3},{3,1},{4,6},{6,4},{5,7},{7,5},{8,10},{10,8},{9,1... | collective-permute-start | bytes 1572872 | tf_op jit(solution)/shard_map/ppermute | solution.py:108
  200.1 26.0 %collective-permute-start.4 = (bf16[128,2048]{1,0:T(8,128)(2,1)S(1)}, bf16[128,2048]{1,0:T(8,128)(2,1)S(1)}, u32[]{:S(2)}, u32[]{:S(2)}) collective-permute-start(bf16[128,2048]{1,0:T(8,128)(2,1)S(1)} %multiply_convert_fusion.4), channel_id=1, source_target_pairs={{0,2},{2,0},{1,3},{3,1},{4,6},{6,4},{5,7},{7,5},{8,10},{10,8},{9,1... | collective-permute-start | bytes 1572872 | tf_op jit(solution)/shard_map/ppermute | solution.py:108
  210.2 16.1 %collective-permute-start.9 = (bf16[2,128,2048]{2,1,0:T(8,128)(2,1)S(1)}, bf16[2,128,2048]{2,1,0:T(8,128)(2,1)S(1)}, u32[]{:S(2)}, u32[]{:S(2)}) collective-permute-start(bf16[2,128,2048]{2,1,0:T(8,128)(2,1)S(1)} %pad_maximum_fusion.7), channel_id=1, source_target_pairs={{0,1},{1,0},{2,3},{3,2},{4,5},{5,4},{6,7},{7,6},{8,9},{9,8},{10,11... | collective-permute-start | bytes 3145736 | tf_op jit(solution)/shard_map/ppermute | solution.py:110
  226.3 2.7 collective-permute-start.5
  303.7 8.4 %copy-start.22 = (bf16[4,128,2048]{2,1,0:T(8,128)(2,1)S(1)}, bf16[4,128,2048]{2,1,0:T(8,128)(2,1)}, u32[]{:S(2)}) copy-start(bf16[4,128,2048]{2,1,0:T(8,128)(2,1)} %pad_maximum_fusion.2) | copy-start | bytes 6291460
  303.7 9.9 %copy-start.45 = (bf16[2048,4224]{1,0:T(8,128)(2,1)S(1)}, bf16[2048,4224]{1,0:T(8,128)(2,1)}, u32[]{:S(2)}) copy-start(bf16[2048,4224]{1,0:T(8,128)(2,1)} %all-gather.5.cloned.1.call-done) | copy-start | bytes 51904516
  345.1 6.0 copy-start.30
  357.0 7.0 %collective-permute-start.10 = (f32[2,128,2048]{2,1,0:T(8,128)S(1)}, f32[2,128,2048]{2,1,0:T(8,128)S(1)}, u32[]{:S(2)}, u32[]{:S(2)}) collective-permute-start(f32[2,128,2048]{2,1,0:T(8,128)S(1)} %bitcast.336), channel_id=1, source_target_pairs={{0,1},{1,0},{2,3},{3,2},{4,5},{5,4},{6,7},{7,6},{8,9},{9,8},{10,11... | collective-permute-start | bytes 6291464 | tf_op jit(solution)/shard_map/ppermute | solution.py:116
  363.9 4.2 collective-permute-start.6
  364.1 18.8 %collective-permute-start.11 = (bf16[128,2048]{1,0:T(8,128)(2,1)S(1)}, bf16[128,2048]{1,0:T(8,128)(2,1)S(1)}, u32[]{:S(2)}, u32[]{:S(2)}) collective-permute-start(bf16[128,2048]{1,0:T(8,128)(2,1)S(1)} %fusion.83), channel_id=1, source_target_pairs={{0,2},{2,0},{1,3},{3,1},{4,6},{6,4},{5,7},{7,5},{8,10},{10,8},{9,1... | collective-permute-start | bytes 1572872 | tf_op jit(solution)/shard_map/ppermute | solution.py:119
  368.3 29.4 %collective-permute-start.7 = (bf16[128,2048]{1,0:T(8,128)(2,1)S(1)}, bf16[128,2048]{1,0:T(8,128)(2,1)S(1)}, u32[]{:S(2)}, u32[]{:S(2)}) collective-permute-start(bf16[128,2048]{1,0:T(8,128)(2,1)S(1)} %fusion.87), channel_id=1, source_target_pairs={{0,2},{2,0},{1,3},{3,1},{4,6},{6,4},{5,7},{7,5},{8,10},{10,8},{9,1... | collective-permute-start | bytes 1572872 | tf_op jit(solution)/shard_map/ppermute | solution.py:119
  399.4 17.6 %copy-start.9 = (bf16[128,2048]{1,0:T(8,128)(2,1)}, bf16[128,2048]{1,0:T(8,128)(2,1)S(1)}, u32[]{:S(2)}) copy-start(bf16[128,2048]{1,0:T(8,128)(2,1)S(1)} %get-tuple-element.25) | copy-start | bytes 1572868
  399.4 17.6 %collective-permute-start.12 = (bf16[128,2048]{1,0:T(8,128)(2,1)S(1)}, bf16[128,2048]{1,0:T(8,128)(2,1)S(1)}, u32[]{:S(2)}, u32[]{:S(2)}) collective-permute-start(bf16[128,2048]{1,0:T(8,128)(2,1)S(1)} %get-tuple-element.25), channel_id=1, source_target_pairs={{0,2},{2,0},{1,3},{3,1},{4,6},{6,4},{5,7},{7,5},{8,10},{10,8},{9,1... | collective-permute-start | bytes 1572872 | tf_op jit(solution)/shard_map/ppermute | solution.py:108
  418.0 3.0 collective-permute-start.13
  418.1 4.6 copy-start.32
  422.6 4.6 copy-start.21
  434.8 3.3 copy-start.7
  444.0 3.1 copy-start.14
  444.0 3.1 copy-start.33
  444.1 3.1 copy-start.34
  480.2 32.0 %collective-permute-start.16 = (bf16[4,2,64,1280]{3,2,1,0:T(8,128)(2,1)S(1)}, bf16[4,2,64,1280]{3,2,1,0:T(8,128)(2,1)S(1)}, u32[]{:S(2)}, u32[]{:S(2)}) collective-permute-start(bf16[4,2,64,1280]{3,2,1,0:T(8,128)(2,1)S(1)} %dynamic-slice_bitcast_fusion.1), channel_id=1, source_target_pairs={{0,4},{4,8},{8,12},{12,0},{16,20},{20,24},{24,28},{28,16},{32,36},... | collective-permute-start | bytes 3932168 | tf_op jit(solution)/shard_map/ppermute | solution.py:148
  483.6 31.8 %collective-permute-start.22 = (bf16[4,2,64,1280]{3,2,1,0:T(8,128)(2,1)}, bf16[4,2,64,1280]{3,2,1,0:T(8,128)(2,1)}, u32[]{:S(2)}, u32[]{:S(2)}) collective-permute-start(bf16[4,2,64,1280]{3,2,1,0:T(8,128)(2,1)} %dynamic-slice_bitcast_fusion), channel_id=1, source_target_pairs={{0,12},{4,0},{8,4},{12,8},{16,28},{20,16},{24,20},{28,24},{32,44},... | collective-permute-start | bytes 3932168 | tf_op jit(solution)/shard_map/ppermute | solution.py:148
  500.3 49.2 %collective-permute-start.14 = (f32[2,128,2048]{2,1,0:T(8,128)}, f32[2,128,2048]{2,1,0:T(8,128)S(1)}, u32[]{:S(2)}, u32[]{:S(2)}) collective-permute-start(f32[2,128,2048]{2,1,0:T(8,128)} %bitcast.54), channel_id=1, source_target_pairs={{0,1},{1,0},{2,3},{3,2},{4,5},{5,4},{6,7},{7,6},{8,9},{9,8},{10,11... | collective-permute-start | bytes 6291464 | tf_op jit(solution)/shard_map/ppermute | solution.py:116
  514.8 31.6 %collective-permute-start.17 = (bf16[4,2,64,1280]{3,2,1,0:T(8,128)(2,1)}, bf16[4,2,64,1280]{3,2,1,0:T(8,128)(2,1)}, u32[]{:S(2)}, u32[]{:S(2)}) collective-permute-start(bf16[4,2,64,1280]{3,2,1,0:T(8,128)(2,1)} %fusion.19), channel_id=1, source_target_pairs={{0,4},{4,8},{8,12},{12,0},{16,20},{20,24},{24,28},{28,16},{32,36},... | collective-permute-start | bytes 3932168 | tf_op jit(solution)/shard_map/ppermute | solution.py:148
  518.5 34.6 %collective-permute-start.23 = (bf16[4,2,64,1280]{3,2,1,0:T(8,128)(2,1)}, bf16[4,2,64,1280]{3,2,1,0:T(8,128)(2,1)}, u32[]{:S(2)}, u32[]{:S(2)}) collective-permute-start(bf16[4,2,64,1280]{3,2,1,0:T(8,128)(2,1)} %fusion.16), channel_id=1, source_target_pairs={{0,12},{4,0},{8,4},{12,8},{16,28},{20,16},{24,20},{28,24},{32,44},... | collective-permute-start | bytes 3932168 | tf_op jit(solution)/shard_map/ppermute | solution.py:148
  549.5 44.2 %collective-permute-start.18 = (bf16[4,2,64,1280]{3,2,1,0:T(8,128)(2,1)}, bf16[4,2,64,1280]{3,2,1,0:T(8,128)(2,1)}, u32[]{:S(2)}, u32[]{:S(2)}) collective-permute-start(bf16[4,2,64,1280]{3,2,1,0:T(8,128)(2,1)} %fusion.20), channel_id=1, source_target_pairs={{0,4},{4,8},{8,12},{12,0},{16,20},{20,24},{24,28},{28,16},{32,36},... | collective-permute-start | bytes 3932168 | tf_op jit(solution)/shard_map/ppermute | solution.py:148
  550.9 13.5 %copy-start.37 = (f32[2048]{0:T(1024)S(1)}, f32[2048]{0:T(1024)}, u32[]{:S(2)}) copy-start(f32[2048]{0:T(1024)} %copy-done.36) | copy-start | bytes 24580
  551.0 13.5 %copy-start.39 = (f32[128]{0:T(128)S(1)}, f32[128]{0:T(128)}, u32[]{:S(2)}) copy-start(f32[128]{0:T(128)} %copy-done.38) | copy-start | bytes 1540
  551.0 13.5 %collective-permute-start.15 = (bf16[128,2048]{1,0:T(8,128)(2,1)S(1)}, bf16[128,2048]{1,0:T(8,128)(2,1)S(1)}, u32[]{:S(2)}, u32[]{:S(2)}) collective-permute-start(bf16[128,2048]{1,0:T(8,128)(2,1)S(1)} %fusion.79), channel_id=1, source_target_pairs={{0,2},{2,0},{1,3},{3,1},{4,6},{6,4},{5,7},{7,5},{8,10},{10,8},{9,1... | collective-permute-start | bytes 1572872 | tf_op jit(solution)/shard_map/ppermute | solution.py:119
  556.3 43.2 %collective-permute-start.24 = (bf16[4,2,64,1280]{3,2,1,0:T(8,128)(2,1)}, bf16[4,2,64,1280]{3,2,1,0:T(8,128)(2,1)}, u32[]{:S(2)}, u32[]{:S(2)}) collective-permute-start(bf16[4,2,64,1280]{3,2,1,0:T(8,128)(2,1)} %fusion.17), channel_id=1, source_target_pairs={{0,12},{4,0},{8,4},{12,8},{16,28},{20,16},{24,20},{28,24},{32,44},... | collective-permute-start | bytes 3932168 | tf_op jit(solution)/shard_map/ppermute | solution.py:148
  568.0 70.3 %all-to-all-start.1 = ((f32[128,3,16]{2,1,0:T(4,128)}), f32[128,3,16]{2,1,0:T(4,128)S(1)}, u32[]{:S(2)}, u32[]{:S(2)}) async-start(f32[128,3,16]{2,1,0:T(4,128)} %copy.107), calls=%async_computation.1 | async-start | bytes 524288 | tf_op jit(solution)/shard_map/all_to_all | solution.py:176
  595.8 15.9 %collective-permute-start.19 = (bf16[2,64,1280]{2,1,0:T(8,128)(2,1)S(1)}, bf16[2,64,1280]{2,1,0:T(8,128)(2,1)S(1)}, u32[]{:S(2)}, u32[]{:S(2)}) collective-permute-start(bf16[2,64,1280]{2,1,0:T(8,128)(2,1)S(1)} %dynamic-slice_bitcast_fusion.3), channel_id=1, source_target_pairs={{0,32},{4,36},{8,40},{12,44},{16,48},{20,52},{24,56},{28,60},{32,6... | collective-permute-start | bytes 983048 | tf_op jit(solution)/shard_map/ppermute | solution.py:148
  601.6 10.3 %collective-permute-start.25 = (bf16[2,64,1280]{2,1,0:T(8,128)(2,1)S(1)}, bf16[2,64,1280]{2,1,0:T(8,128)(2,1)S(1)}, u32[]{:S(2)}, u32[]{:S(2)}) collective-permute-start(bf16[2,64,1280]{2,1,0:T(8,128)(2,1)S(1)} %dynamic-slice_bitcast_fusion.2), channel_id=1, source_target_pairs={{0,96},{4,100},{8,104},{12,108},{16,112},{20,116},{24,120},{28,124... | collective-permute-start | bytes 983048 | tf_op jit(solution)/shard_map/ppermute | solution.py:148
  611.8 12.0 %collective-permute-start.20 = (bf16[2,64,1280]{2,1,0:T(8,128)(2,1)S(1)}, bf16[2,64,1280]{2,1,0:T(8,128)(2,1)S(1)}, u32[]{:S(2)}, u32[]{:S(2)}) collective-permute-start(bf16[2,64,1280]{2,1,0:T(8,128)(2,1)S(1)} %fusion.116), channel_id=1, source_target_pairs={{0,32},{4,36},{8,40},{12,44},{16,48},{20,52},{24,56},{28,60},{32,6... | collective-permute-start | bytes 983048 | tf_op jit(solution)/shard_map/ppermute | solution.py:148
  612.0 13.7 %collective-permute-start.26 = (bf16[2,64,1280]{2,1,0:T(8,128)(2,1)S(1)}, bf16[2,64,1280]{2,1,0:T(8,128)(2,1)S(1)}, u32[]{:S(2)}, u32[]{:S(2)}) collective-permute-start(bf16[2,64,1280]{2,1,0:T(8,128)(2,1)S(1)} %fusion.114), channel_id=1, source_target_pairs={{0,96},{4,100},{8,104},{12,108},{16,112},{20,116},{24,120},{28,124... | collective-permute-start | bytes 983048 | tf_op jit(solution)/shard_map/ppermute | solution.py:148
  623.9 10.1 %collective-permute-start.21 = (bf16[2,64,1280]{2,1,0:T(8,128)(2,1)S(1)}, bf16[2,64,1280]{2,1,0:T(8,128)(2,1)S(1)}, u32[]{:S(2)}, u32[]{:S(2)}) collective-permute-start(bf16[2,64,1280]{2,1,0:T(8,128)(2,1)S(1)} %fusion.117), channel_id=1, source_target_pairs={{0,32},{4,36},{8,40},{12,44},{16,48},{20,52},{24,56},{28,60},{32,6... | collective-permute-start | bytes 983048 | tf_op jit(solution)/shard_map/ppermute | solution.py:148
  625.8 11.3 %copy-start.10 = (f32[128,2048]{1,0:T(8,128)S(1)}, f32[128,2048]{1,0:T(8,128)}, u32[]{:S(2)}) copy-start(f32[128,2048]{1,0:T(8,128)} %get-tuple-element.26) | copy-start | bytes 3145732
  625.8 11.3 %copy-start.12 = (f32[128,2048]{1,0:T(8,128)S(1)}, f32[128,2048]{1,0:T(8,128)}, u32[]{:S(2)}) copy-start(f32[128,2048]{1,0:T(8,128)} %get-tuple-element.24) | copy-start | bytes 3145732
  625.8 11.2 %copy-start.40 = (f32[128]{0:T(128)S(1)}, f32[128]{0:T(128)}, u32[]{:S(2)}) copy-start(f32[128]{0:T(128)} %get-tuple-element.54) | copy-start | bytes 1540
  625.8 8.4 %collective-permute-start.27 = (bf16[2,64,1280]{2,1,0:T(8,128)(2,1)S(1)}, bf16[2,64,1280]{2,1,0:T(8,128)(2,1)S(1)}, u32[]{:S(2)}, u32[]{:S(2)}) collective-permute-start(bf16[2,64,1280]{2,1,0:T(8,128)(2,1)S(1)} %fusion.115), channel_id=1, source_target_pairs={{0,96},{4,100},{8,104},{12,108},{16,112},{20,116},{24,120},{28,124... | collective-permute-start | bytes 983048 | tf_op jit(solution)/shard_map/ppermute | solution.py:148
  634.3 8.7 %collective-permute-start.28 = (bf16[64,2560]{1,0:T(8,128)(2,1)S(1)}, bf16[64,2560]{1,0:T(8,128)(2,1)S(1)}, u32[]{:S(2)}, u32[]{:S(2)}) collective-permute-start(bf16[64,2560]{1,0:T(8,128)(2,1)S(1)} %fusion.130), channel_id=1, source_target_pairs={{0,16},{4,20},{8,24},{12,28},{16,0},{20,4},{24,8},{28,12},{32,48},... | collective-permute-start | bytes 983048 | tf_op jit(solution)/shard_map/ppermute | solution.py:163
  (16 other events, 29.8 us)
Sparse Core Ops, SparseCore 0:
  12.4 121.4 all-gather.2
  136.9 166.7 all-gather.4
  345.3 289.3 reduce-scatter.1

commit v11 on v9

--- a/solution.py
+++ b/solution.py
@@ -123,6 +123,51 @@
     blocks = values.reshape((count, -1) + values.shape[1:])
     got = lax.all_to_all(blocks, axis, 0, 0, tiled=False)
     return got.astype(jnp.float32).sum(axis=0)
+
+
+def ring_pairs(step, stride, size):
+    pairs = []
+    for i in range(32):
+        pos = (i // stride) % size
+        pairs.append((i, i + (((pos + step) % size) - pos) * stride))
+    return pairs
+
+
+def ring_stage(chunks, pos, stride, size, step):
+    pairs = ring_pairs(step, stride, size)
+
+    def pick(k):
+        return lax.dynamic_index_in_dim(chunks, (pos - k * step) % size, 0, keepdims=False).astype(
+            jnp.float32
+        )
+
+    acc = pick(1)
+    for k in range(2, size + 1):
+        got = lax.ppermute(acc.astype(jnp.bfloat16), "dp", pairs)
+        acc = pick(k % size) + got.astype(jnp.float32)
+    return acc
+
+
+def ring_sum(values):
+    index = lax.axis_index("dp")
+    x_pos, y_pos, z_pos = index % 4, (index // 4) % 2, index // 8
+    blocks = values.reshape((4, 2, 4, -1) + values.shape[1:])
+    part_rows = blocks.shape[3] // 4
+    pieces = []
+    for part, (x_first, step) in enumerate(((True, 1), (True, 3), (False, 1), (False, 3))):
+        rows = blocks[:, :, :, part * part_rows : (part + 1) * part_rows]
+        if x_first:
+            once = ring_stage(jnp.moveaxis(rows, 2, 0), x_pos, 1, 4, step)
+            twice = ring_stage(once.astype(jnp.bfloat16), z_pos, 8, 4, step)
+        else:
+            once = ring_stage(rows, z_pos, 8, 4, step)
+            twice = ring_stage(jnp.moveaxis(once, 1, 0).astype(jnp.bfloat16), x_pos, 1, 4, step)
+        pieces.append(twice)
+    both = jnp.concatenate(pieces, axis=1)
+    keep = lax.dynamic_index_in_dim(both, y_pos, 0, keepdims=False)
+    give = lax.dynamic_index_in_dim(both, 1 - y_pos, 0, keepdims=False)
+    pair = [(i, i ^ 4) for i in range(32)]
+    return keep + lax.ppermute(give.astype(jnp.bfloat16), "dp", pair).astype(jnp.float32)
 
 
 def small_gather(vectors):
@@ -219,7 +264,7 @@
     mlp_grads = grad_pack(
         normed2, cot_full, jnp.concatenate([d_gate, d_up, hidden], axis=1), hidden_width
     )
-    mlp_red = lax.psum_scatter(mlp_grads, "dp", scatter_dimension=0, tiled=True).astype(jnp.float32)
+    mlp_red = ring_sum(mlp_grads)
     d_normed2 = row_sum(times_trans(d_gate, wgate_all) + times_trans(d_up, wup_all))
     grad_mlp = jnp.sum(d_normed2 * resid * scale_two, axis=0)
     inner_two = jnp.mean(d_normed2 * mlp_full * resid, axis=-1, keepdims=True)
@@ -242,7 +287,7 @@
         jnp.concatenate([d_query, d_forget, d_value, d_outgate, gated], axis=1),
         local_width,
     )
-    attn_red = spread_sum(attn_grads, "dp", 32)
+    attn_red = ring_sum(attn_grads)
     d_normed = row_sum(
         times_trans(d_query, wq_all)
         + times_trans(d_forget, wf_all)

time: 758 us -> 689 us (0.909)
  waiting for transfers between devices: 513 us -> 345 us
  starting transfers between devices: 36.9 us -> 91.8 us
  local copies, waits for them, and re-layouts: 45.4 us -> 72.4 us
  other arithmetic: 33.1 us -> 51.3 us
    all_to_all x1 -> x0, waiting for transfers between devices: 169 us -> none  [spread_sum(): got = lax.all_to_all(blocks, axis, 0, 0, tiled=False)]
    ppermute x0 -> x50, waiting for transfers between devices: none -> 117 us  [the longest x48 117 us: ring_stage(): got = lax.ppermute(acc.astype(jnp.bfloat16), 'dp', pairs)]
    ppermute x0 -> x50, starting transfers between devices: none -> 67.8 us  [the longest x48 61.9 us: ring_stage(): got = lax.ppermute(acc.astype(jnp.bfloat16), 'dp', pairs)]
    reduce_scatter x1 -> x0, waiting for transfers between devices: 58.3 us -> none  [shards(): lax.psum_scatter(mlp_grads, 'dp', scatter_dimension=0, tiled=True)]
    ppermute x4, waiting for transfers between devices: 57.3 us -> 13.3 us  [row_sum(): lax.ppermute(theirs.astype(jnp.bfloat16), 'tensor', ACROSS)]
    convert_element_type x1 -> x40, other arithmetic: 1.12 us -> 16.1 us  [the longest x32 8.4 us: ring_stage(): got = lax.ppermute(acc.astype(jnp.bfloat16), 'dp', pairs)]
    slice x1 -> x2, local copies, waits for them, and re-layouts: 2.01 us -> 13.6 us  [ring_sum(): rows = blocks[:, :, :, part * part_rows:(part + 1) * part_rows]]
    all_to_all x1 -> x0, starting transfers between devices: 10 us -> none  [spread_sum(): got = lax.all_to_all(blocks, axis, 0, 0, tiled=False)]
  transfers between devices with their start and end apart: 22 -> 70, of which waited for: 19 -> 31; matrix products, arithmetic and copies ran while one was open for 17% -> 23% of each run, Pallas kernels for 1% -> 4%
where the time goes in v11:
time: 689 us; the launch traced here: 683 us
  waiting for transfers between devices  345 us (50%)
  starting transfers between devices  91.8 us (13%)
  matrix products  79.7 us (12%)
  local copies, waits for them, and re-layouts  72.4 us (11%)
  other arithmetic  51.3 us (7%)
  Pallas kernels  26.4 us (4%)
  between operations  16.1 us (2%)
    ppermute x48, waiting for transfers between devices, ring_stage(): got = lax.ppermute(acc.astype(jnp.bfloat16), 'dp', pairs)  117 us
    all_gather x1, waiting for transfers between devices, shards(): attn_all = lax.all_gather(attn_pack, 'dp', axis=0, tiled=True)  71.3 us
    all_gather x1, waiting for transfers between devices, shards(): mlp_all = lax.all_gather(mlp_pack, 'dp', axis=0, tiled=True)  70.2 us
    ppermute x48, starting transfers between devices, ring_stage(): got = lax.ppermute(acc.astype(jnp.bfloat16), 'dp', pairs)  61.9 us
    ppermute x4, waiting for transfers between devices, row_gather(): across = lax.ppermute(values, 'tensor', ACROSS)  46.8 us
    dot_general x8, matrix products, matmul_plain(): return jnp.dot(left, right, preferred_element_type=jnp.float32)  35.3 us
    pallas_call x2, Pallas kernels, grad_pack(): pl.pallas_call(functools.partial(pack_kernel, per), grid=(rows_out // til...  26.4 us
    dot_general x8, matrix products, times_trans(): lax.dot_general(left, right, (((1,), (1,)), ((), ())), preferred_element_...  25.1 us
  transfers between devices with their start and end apart: 70, of which 31 were waited for; matrix products, arithmetic and copies ran while one was open for 23% of the time, Pallas kernels for 4%

profile of v11, /device:TPU:0, one launch (start us, length us, event | category | flops | bytes accessed | tf_op | source)
XLA Modules:
  0.0 683.0 jit_solution(636746505367290780)
XLA Ops:
  15.1 11.1 %all-to-all-start = ((f32[128,3,16]{2,1,0:T(4,128)}), f32[128,3,16]{2,1,0:T(4,128)S(1)}, u32[]{:S(2)}, u32[]{:S(2)}) async-start(f32[128,3,16]{2,1,0:T(4,128)} %broadcast_in_dim.29), calls=%async_computation | async-start | bytes 524288 | tf_op jit(solution)/shard_map/all_to_all | solution.py:176
  27.0 11.6 %all-to-all-done = f32[128,3,16]{2,1,0:T(4,128)S(1)} async-done(((f32[128,3,16]{2,1,0:T(4,128)}), f32[128,3,16]{2,1,0:T(4,128)S(1)}, u32[]{:S(2)}, u32[]{:S(2)}) %all-to-all-start) | async-done | bytes 24608 | tf_op jit(solution)/shard_map/all_to_all | solution.py:176
  40.2 15.5 %collective-permute-done = bf16[128,2048]{1,0:T(8,128)(2,1)S(1)} collective-permute-done((bf16[128,2048]{1,0:T(8,128)(2,1)S(1)}, bf16[128,2048]{1,0:T(8,128)(2,1)S(1)}, u32[]{:S(2)}, u32[]{:S(2)}) %collective-permute-start) | collective-permute-done | bytes 524320 | tf_op jit(solution)/shard_map/ppermute | solution.py:108
  59.8 2.8 pad_maximum_fusion.2
  62.6 71.3 %all-gather.3.cloned.1.call-done = bf16[2048,2560]{1,0:T(8,128)(2,1)} async-done(((bf16[64,2560]{1,0:T(8,128)(2,1)}), bf16[2048,2560]{1,0:T(8,128)(2,1)}) %all-gather.3.cloned.1.call-update) | async-done | bytes 10485776 | tf_op jit(solution)/shard_map/all_gather | solution.py:220
  133.9 5.7 slice_bitcast_fusion
  139.6 4.2 copy.110
  143.7 4.0 copy.112
  147.7 4.0 copy.113
  151.7 3.4 fusion.75
  157.1 2.5 fusion.30
  162.1 2.9 fusion.32
  169.2 4.8 fusion.93
  174.0 3.1 fusion.36
  177.5 4.1 collective-permute-done.2
  184.5 13.3 %collective-permute-done.3 = bf16[128,2048]{1,0:T(8,128)(2,1)} collective-permute-done((bf16[128,2048]{1,0:T(8,128)(2,1)S(1)}, bf16[128,2048]{1,0:T(8,128)(2,1)}, u32[]{:S(2)}, u32[]{:S(2)}) %collective-permute-start.3) | collective-permute-done | bytes 524320 | tf_op jit(solution)/shard_map/ppermute | solution.py:119
  200.6 8.5 %collective-permute-done.8 = bf16[128,2048]{1,0:T(8,128)(2,1)} collective-permute-done((bf16[128,2048]{1,0:T(8,128)(2,1)S(1)}, bf16[128,2048]{1,0:T(8,128)(2,1)}, u32[]{:S(2)}, u32[]{:S(2)}) %collective-permute-start.8) | collective-permute-done | bytes 524320 | tf_op jit(solution)/shard_map/ppermute | solution.py:108
  211.4 14.5 %collective-permute-done.4 = bf16[128,2048]{1,0:T(8,128)(2,1)S(1)} collective-permute-done((bf16[128,2048]{1,0:T(8,128)(2,1)S(1)}, bf16[128,2048]{1,0:T(8,128)(2,1)S(1)}, u32[]{:S(2)}, u32[]{:S(2)}) %collective-permute-start.4) | collective-permute-done | bytes 524320 | tf_op jit(solution)/shard_map/ppermute | solution.py:108
  227.8 3.0 pad_maximum_fusion.4
  230.8 2.8 pad_maximum_fusion.3
  233.5 70.2 %all-gather.5.cloned.1.call-done = bf16[2048,4224]{1,0:T(8,128)(2,1)} async-done(((bf16[64,4224]{1,0:T(8,128)(2,1)}), bf16[2048,4224]{1,0:T(8,128)(2,1)}) %all-gather.5.cloned.1.call-update) | async-done | bytes 17301520 | tf_op jit(solution)/shard_map/all_gather | solution.py:221
  303.7 6.5 fusion
  312.6 3.4 fusion.6
  316.0 7.2 %multiply_convert_fusion.1 = (bf16[512,1408]{1,0:T(8,128)(2,1)S(1)}, bf16[512,1408]{1,0:T(8,128)(2,1)S(1)}, bf16[512,1408]{1,0:T(8,128)(2,1)S(1)}) fusion(f32[512,1408]{1,0:T(8,128)S(1)} %fusion, f32[512,1408]{1,0:T(8,128)S(1)} %fusion.6, bf16[512,2048]{1,0:T(8,128)(2,1)S(1)} %bitcast.529, bf16[2048,4224]{1,0:T(8,128)(2,1)} %all-gather.5.cloned.1.call-done), kind=kOutput, calls=%fused_computation.17 | convolution fusion | flops 2963603456 | bytes 17956864 | tf_op jit(solution)/shard_map/dot_general | solution.py:27
  323.2 5.5 fusion.4
  328.7 5.6 fusion.12
  339.4 5.5 fusion.2
  348.0 15.7 %shard_map.247 = bf16[2048,4224]{1,0:T(8,128)(2,1)} custom-call(bf16[512,2048]{1,0:T(8,128)(2,1)} %bitcast.527, bf16[512,2048]{1,0:T(8,128)(2,1)} %bitcast.526, bf16[512,4224]{1,0:T(8,128)(2,1)} %pad_maximum_fusion.right_ref), custom_call_target="tpu_custom_call" | custom-call | flops 8858370048 | bytes 25821184 | tf_op jit(solution)/shard_map/pallas_call | solution.py:64
  363.7 9.0 %fusion.172 = (bf16[4,2,4,16,4224]{4,3,2,1,0:T(8,128)(2,1)S(1)}, bf16[4,2,4,16,4224]{4,3,2,1,0:T(8,128)(2,1)}, bf16[4,2,4,16,4224]{4,3,2,1,0:T(8,128)(2,1)S(1)}, bf16[4,2,4,16,4224]{4,3,2,1,0:T(8,128)(2,1)S(1)}) fusion(bf16[4,2,4,64,4224]{4,3,2,1,0:T(8,128)(2,1)} %bitcast.506), kind=kLoop, calls=%fused_computation.344 | loop fusion | bytes 34603008 | tf_op jit(solution)/shard_map/slice | solution.py:158
  374.2 2.8 collective-permute-start.59
  380.6 19.6 %collective-permute-done.59 = bf16[2,4,16,4224]{3,2,0,1:T(8,128)(2,1)S(1)} collective-permute-done((bf16[2,4,16,4224]{3,2,0,1:T(8,128)(2,1)S(1)}, bf16[2,4,16,4224]{3,2,0,1:T(8,128)(2,1)S(1)}, u32[]{:S(2)}, u32[]{:S(2)}) %collective-permute-start.59) | collective-permute-done | bytes 1081376 | tf_op jit(solution)/shard_map/ppermute | solution.py:146
  401.8 3.3 collective-permute-done.53
  405.4 2.5 collective-permute-start.54
  408.2 18.2 %collective-permute-done.41 = bf16[4,2,16,4224]{3,2,1,0:T(8,128)(2,1)S(1)} collective-permute-done((bf16[4,2,16,4224]{3,2,1,0:T(8,128)(2,1)S(1)}, bf16[4,2,16,4224]{3,2,1,0:T(8,128)(2,1)S(1)}, u32[]{:S(2)}, u32[]{:S(2)}) %collective-permute-start.41) | collective-permute-done | bytes 1081376 | tf_op jit(solution)/shard_map/ppermute | solution.py:146
  435.2 3.6 collective-permute-start.61
  440.1 10.4 %collective-permute-done.48 = bf16[4,2,16,4224]{3,2,1,0:T(8,128)(2,1)S(1)} collective-permute-done((bf16[4,2,16,4224]{3,2,1,0:T(8,128)(2,1)S(1)}, bf16[4,2,16,4224]{3,2,1,0:T(8,128)(2,1)S(1)}, u32[]{:S(2)}, u32[]{:S(2)}) %collective-permute-start.48) | collective-permute-done | bytes 1081376 | tf_op jit(solution)/shard_map/ppermute | solution.py:146
  456.0 3.0 fusion.169
  461.5 8.3 %collective-permute-done.12 = bf16[128,2048]{1,0:T(8,128)(2,1)S(1)} collective-permute-done((bf16[128,2048]{1,0:T(8,128)(2,1)S(1)}, bf16[128,2048]{1,0:T(8,128)(2,1)S(1)}, u32[]{:S(2)}, u32[]{:S(2)}) %collective-permute-start.12) | collective-permute-done | bytes 524320 | tf_op jit(solution)/shard_map/ppermute | solution.py:108
  472.2 3.7 collective-permute-done.55
  479.4 2.9 collective-permute-start.50
  482.3 5.3 collective-permute-done.43
  495.3 3.9 collective-permute-done.44
  502.2 3.5 collective-permute-start.52
  509.7 6.1 collective-permute-done.46
  519.4 4.6 fusion.161
  530.8 2.6 multiply_convert_fusion.3
  533.4 2.9 convolution_bitcast_fusion
  539.9 4.6 multiply_reduce_fusion.1
  558.1 10.7 %shard_map.246 = bf16[2048,2560]{1,0:T(8,128)(2,1)} custom-call(bf16[512,2048]{1,0:T(8,128)(2,1)} %bitcast.522, bf16[512,2048]{1,0:T(8,128)(2,1)} %bitcast.524, bf16[512,2560]{1,0:T(8,128)(2,1)} %constant_dynamic-update-slice_fusion.4.right_ref), custom_call_target="tpu_custom_call" | custom-call | flops 5368709120 | bytes 17301504 | tf_op jit(solution)/shard_map/pallas_call | solution.py:64
  568.8 4.7 fusion.173
  580.6 10.4 %collective-permute-done.34 = bf16[2,4,16,2560]{3,2,0,1:T(8,128)(2,1)S(1)} collective-permute-done((bf16[2,4,16,2560]{3,2,0,1:T(8,128)(2,1)S(1)}, bf16[2,4,16,2560]{3,2,0,1:T(8,128)(2,1)S(1)}, u32[]{:S(2)}, u32[]{:S(2)}) %collective-permute-start.34) | collective-permute-done | bytes 655392 | tf_op jit(solution)/shard_map/ppermute | solution.py:146
  596.0 11.6 %collective-permute-done.35 = bf16[2,4,16,2560]{3,2,0,1:T(8,128)(2,1)S(1)} collective-permute-done((bf16[2,4,16,2560]{3,2,0,1:T(8,128)(2,1)S(1)}, bf16[2,4,16,2560]{3,2,0,1:T(8,128)(2,1)S(1)}, u32[]{:S(2)}, u32[]{:S(2)}) %collective-permute-start.35) | collective-permute-done | bytes 655392 | tf_op jit(solution)/shard_map/ppermute | solution.py:146
  607.7 3.2 collective-permute-start.36
  613.7 10.4 %collective-permute-done.36 = bf16[2,4,16,2560]{3,2,0,1:T(8,128)(2,1)S(1)} collective-permute-done((bf16[2,4,16,2560]{3,2,0,1:T(8,128)(2,1)S(1)}, bf16[2,4,16,2560]{3,2,0,1:T(8,128)(2,1)S(1)}, u32[]{:S(2)}, u32[]{:S(2)}) %collective-permute-start.36) | collective-permute-done | bytes 655392 | tf_op jit(solution)/shard_map/ppermute | solution.py:146
  624.7 3.1 collective-permute-done.30
  631.8 2.7 collective-permute-start.38
  634.8 2.7 collective-permute-start.26
  637.9 3.7 collective-permute-start.39
  641.8 3.1 collective-permute-start.27
  645.2 3.0 collective-permute-done.33
  648.4 3.3 collective-permute-done.21
  651.9 3.7 collective-permute-start.40
  657.1 5.0 all-to-all-start.1
  663.5 9.4 %all-to-all-done.1 = f32[128,3,16]{2,1,0:T(4,128)S(1)} async-done(((f32[128,3,16]{2,1,0:T(4,128)}), f32[128,3,16]{2,1,0:T(4,128)S(1)}, u32[]{:S(2)}, u32[]{:S(2)}) %all-to-all-start.1) | async-done | bytes 24608 | tf_op jit(solution)/shard_map/all_to_all | solution.py:183
  (382 shorter events, 142.9 us)
Async XLA Ops:
  7.2 126.6 %all-gather.3.cloned.1.call-start = ((), (), s32[]{:S(2)}) async-start(), calls=%async_computation.2 | async-start | bytes 10813440 | tf_op jit(solution)/shard_map/all_gather | solution.py:220
  12.3 291.4 %all-gather.5.cloned.1.call-start = ((), (), s32[]{:S(2)}) async-start(), calls=%async_computation.3 | async-start | bytes 17842176 | tf_op jit(solution)/shard_map/all_gather | solution.py:221
  15.1 23.5 %all-to-all-start = ((f32[128,3,16]{2,1,0:T(4,128)}), f32[128,3,16]{2,1,0:T(4,128)S(1)}, u32[]{:S(2)}, u32[]{:S(2)}) async-start(f32[128,3,16]{2,1,0:T(4,128)} %broadcast_in_dim.29), calls=%async_computation | async-start | bytes 524288 | tf_op jit(solution)/shard_map/all_to_all | solution.py:176
  39.4 16.3 %collective-permute-start = (bf16[128,2048]{1,0:T(8,128)(2,1)S(1)}, bf16[128,2048]{1,0:T(8,128)(2,1)S(1)}, u32[]{:S(2)}, u32[]{:S(2)}) collective-permute-start(bf16[128,2048]{1,0:T(8,128)(2,1)S(1)} %fusion.81), channel_id=1, source_target_pairs={{0,2},{2,0},{1,3},{3,1},{4,6},{6,4},{5,7},{7,5},{8,10},{10,8},{9,1... | collective-permute-start | bytes 1572872 | tf_op jit(solution)/shard_map/ppermute | solution.py:108
  181.8 16.1 %collective-permute-start.3 = (bf16[128,2048]{1,0:T(8,128)(2,1)S(1)}, bf16[128,2048]{1,0:T(8,128)(2,1)}, u32[]{:S(2)}, u32[]{:S(2)}) collective-permute-start(bf16[128,2048]{1,0:T(8,128)(2,1)S(1)} %fusion.111), channel_id=1, source_target_pairs={{0,2},{2,0},{1,3},{3,1},{4,6},{6,4},{5,7},{7,5},{8,10},{10,8},{9,1... | collective-permute-start | bytes 1572872 | tf_op jit(solution)/shard_map/ppermute | solution.py:119
  183.0 26.1 %collective-permute-start.8 = (bf16[128,2048]{1,0:T(8,128)(2,1)S(1)}, bf16[128,2048]{1,0:T(8,128)(2,1)}, u32[]{:S(2)}, u32[]{:S(2)}) collective-permute-start(bf16[128,2048]{1,0:T(8,128)(2,1)S(1)} %bitcast.514), channel_id=1, source_target_pairs={{0,2},{2,0},{1,3},{3,1},{4,6},{6,4},{5,7},{7,5},{8,10},{10,8},{9,1... | collective-permute-start | bytes 1572872 | tf_op jit(solution)/shard_map/ppermute | solution.py:108
  200.1 25.8 %collective-permute-start.4 = (bf16[128,2048]{1,0:T(8,128)(2,1)S(1)}, bf16[128,2048]{1,0:T(8,128)(2,1)S(1)}, u32[]{:S(2)}, u32[]{:S(2)}) collective-permute-start(bf16[128,2048]{1,0:T(8,128)(2,1)S(1)} %multiply_convert_fusion.4), channel_id=1, source_target_pairs={{0,2},{2,0},{1,3},{3,1},{4,6},{6,4},{5,7},{7,5},{8,10},{10,8},{9,1... | collective-permute-start | bytes 1572872 | tf_op jit(solution)/shard_map/ppermute | solution.py:108
  211.2 16.5 %collective-permute-start.9 = (bf16[2,128,2048]{2,1,0:T(8,128)(2,1)}, bf16[2,128,2048]{2,1,0:T(8,128)(2,1)}, u32[]{:S(2)}, u32[]{:S(2)}) collective-permute-start(bf16[2,128,2048]{2,1,0:T(8,128)(2,1)} %pad_maximum_fusion.9), channel_id=1, source_target_pairs={{0,1},{1,0},{2,3},{3,2},{4,5},{5,4},{6,7},{7,6},{8,9},{9,8},{10,11... | collective-permute-start | bytes 3145736 | tf_op jit(solution)/shard_map/ppermute | solution.py:110
  337.0 91.0 %collective-permute-start.10 = (f32[2,128,2048]{2,1,0:T(8,128)}, f32[2,128,2048]{2,1,0:T(8,128)}, u32[]{:S(2)}, u32[]{:S(2)}) collective-permute-start(f32[2,128,2048]{2,1,0:T(8,128)} %bitcast.40), channel_id=1, source_target_pairs={{0,1},{1,0},{2,3},{3,2},{4,5},{5,4},{6,7},{7,6},{8,9},{9,8},{10,11... | collective-permute-start | bytes 6291464 | tf_op jit(solution)/shard_map/ppermute | solution.py:116
  347.5 82.8 %collective-permute-start.6 = (f32[2,128,2048]{2,1,0:T(8,128)}, f32[2,128,2048]{2,1,0:T(8,128)}, u32[]{:S(2)}, u32[]{:S(2)}) collective-permute-start(f32[2,128,2048]{2,1,0:T(8,128)} %bitcast.32), channel_id=1, source_target_pairs={{0,1},{1,0},{2,3},{3,2},{4,5},{5,4},{6,7},{7,6},{8,9},{9,8},{10,11... | collective-permute-start | bytes 6291464 | tf_op jit(solution)/shard_map/ppermute | solution.py:116
  374.2 26.1 %collective-permute-start.59 = (bf16[2,4,16,4224]{3,2,0,1:T(8,128)(2,1)S(1)}, bf16[2,4,16,4224]{3,2,0,1:T(8,128)(2,1)S(1)}, u32[]{:S(2)}, u32[]{:S(2)}) collective-permute-start(bf16[2,4,16,4224]{3,2,0,1:T(8,128)(2,1)S(1)} %bitcast.543), channel_id=1, source_target_pairs={{0,96},{4,100},{8,104},{12,108},{16,112},{20,116},{24,120},{28,124... | collective-permute-start | bytes 3244040 | tf_op jit(solution)/shard_map/ppermute | solution.py:146
  378.3 26.8 %collective-permute-start.53 = (bf16[2,4,16,4224]{3,2,0,1:T(8,128)(2,1)S(1)}, bf16[2,4,16,4224]{3,2,0,1:T(8,128)(2,1)S(1)}, u32[]{:S(2)}, u32[]{:S(2)}) collective-permute-start(bf16[2,4,16,4224]{3,2,0,1:T(8,128)(2,1)S(1)} %bitcast.544), channel_id=1, source_target_pairs={{0,32},{4,36},{8,40},{12,44},{16,48},{20,52},{24,56},{28,60},{32,6... | collective-permute-start | bytes 3244040 | tf_op jit(solution)/shard_map/ppermute | solution.py:146
  378.5 26.9 %collective-permute-start.47 = (bf16[4,2,16,4224]{3,2,1,0:T(8,128)(2,1)S(1)}, bf16[4,2,16,4224]{3,2,1,0:T(8,128)(2,1)S(1)}, u32[]{:S(2)}, u32[]{:S(2)}) collective-permute-start(bf16[4,2,16,4224]{3,2,1,0:T(8,128)(2,1)S(1)} %dynamic-slice_bitcast_fusion), channel_id=1, source_target_pairs={{0,12},{4,0},{8,4},{12,8},{16,28},{20,16},{24,20},{28,24},{32,44},... | collective-permute-start | bytes 3244040 | tf_op jit(solution)/shard_map/ppermute | solution.py:146
  400.3 26.2 %collective-permute-start.41 = (bf16[4,2,16,4224]{3,2,1,0:T(8,128)(2,1)S(1)}, bf16[4,2,16,4224]{3,2,1,0:T(8,128)(2,1)S(1)}, u32[]{:S(2)}, u32[]{:S(2)}) collective-permute-start(bf16[4,2,16,4224]{3,2,1,0:T(8,128)(2,1)S(1)} %dynamic-slice_bitcast_fusion.1), channel_id=1, source_target_pairs={{0,4},{4,8},{8,12},{12,0},{16,20},{20,24},{24,28},{28,16},{32,36},... | collective-permute-start | bytes 3244040 | tf_op jit(solution)/shard_map/ppermute | solution.py:146
  405.1 27.3 %collective-permute-start.60 = (bf16[2,4,16,4224]{3,2,0,1:T(8,128)(2,1)S(1)}, bf16[2,4,16,4224]{3,2,0,1:T(8,128)(2,1)S(1)}, u32[]{:S(2)}, u32[]{:S(2)}) collective-permute-start(bf16[2,4,16,4224]{3,2,0,1:T(8,128)(2,1)S(1)} %fusion.16), channel_id=1, source_target_pairs={{0,96},{4,100},{8,104},{12,108},{16,112},{20,116},{24,120},{28,124... | collective-permute-start | bytes 3244040 | tf_op jit(solution)/shard_map/ppermute | solution.py:146
  405.4 29.8 %collective-permute-start.54 = (bf16[2,4,16,4224]{3,2,0,1:T(8,128)(2,1)S(1)}, bf16[2,4,16,4224]{3,2,0,1:T(8,128)(2,1)S(1)}, u32[]{:S(2)}, u32[]{:S(2)}) collective-permute-start(bf16[2,4,16,4224]{3,2,0,1:T(8,128)(2,1)S(1)} %fusion.19), channel_id=1, source_target_pairs={{0,32},{4,36},{8,40},{12,44},{16,48},{20,52},{24,56},{28,60},{32,6... | collective-permute-start | bytes 3244040 | tf_op jit(solution)/shard_map/ppermute | solution.py:146
  426.4 24.0 %collective-permute-start.48 = (bf16[4,2,16,4224]{3,2,1,0:T(8,128)(2,1)S(1)}, bf16[4,2,16,4224]{3,2,1,0:T(8,128)(2,1)S(1)}, u32[]{:S(2)}, u32[]{:S(2)}) collective-permute-start(bf16[4,2,16,4224]{3,2,1,0:T(8,128)(2,1)S(1)} %fusion.22), channel_id=1, source_target_pairs={{0,12},{4,0},{8,4},{12,8},{16,28},{20,16},{24,20},{28,24},{32,44},... | collective-permute-start | bytes 3244040 | tf_op jit(solution)/shard_map/ppermute | solution.py:146
  428.0 31.6 %collective-permute-start.42 = (bf16[4,2,16,4224]{3,2,1,0:T(8,128)(2,1)S(1)}, bf16[4,2,16,4224]{3,2,1,0:T(8,128)(2,1)S(1)}, u32[]{:S(2)}, u32[]{:S(2)}) collective-permute-start(bf16[4,2,16,4224]{3,2,1,0:T(8,128)(2,1)S(1)} %fusion.25), channel_id=1, source_target_pairs={{0,4},{4,8},{8,12},{12,0},{16,20},{20,24},{24,28},{28,16},{32,36},... | collective-permute-start | bytes 3244040 | tf_op jit(solution)/shard_map/ppermute | solution.py:146
  430.4 22.5 %collective-permute-start.11 = (bf16[128,2048]{1,0:T(8,128)(2,1)S(1)}, bf16[128,2048]{1,0:T(8,128)(2,1)S(1)}, u32[]{:S(2)}, u32[]{:S(2)}) collective-permute-start(bf16[128,2048]{1,0:T(8,128)(2,1)S(1)} %fusion.101), channel_id=1, source_target_pairs={{0,2},{2,0},{1,3},{3,1},{4,6},{6,4},{5,7},{7,5},{8,10},{10,8},{9,1... | collective-permute-start | bytes 1572872 | tf_op jit(solution)/shard_map/ppermute | solution.py:119
  432.4 23.6 %collective-permute-start.7 = (bf16[128,2048]{1,0:T(8,128)(2,1)S(1)}, bf16[128,2048]{1,0:T(8,128)(2,1)S(1)}, u32[]{:S(2)}, u32[]{:S(2)}) collective-permute-start(bf16[128,2048]{1,0:T(8,128)(2,1)S(1)} %fusion.105), channel_id=1, source_target_pairs={{0,2},{2,0},{1,3},{3,1},{4,6},{6,4},{5,7},{7,5},{8,10},{10,8},{9,1... | collective-permute-start | bytes 1572872 | tf_op jit(solution)/shard_map/ppermute | solution.py:119
  435.2 34.7 %collective-permute-start.61 = (bf16[2,4,16,4224]{3,2,0,1:T(8,128)(2,1)}, bf16[2,4,16,4224]{3,2,0,1:T(8,128)(2,1)}, u32[]{:S(2)}, u32[]{:S(2)}) collective-permute-start(bf16[2,4,16,4224]{3,2,0,1:T(8,128)(2,1)} %fusion.17), channel_id=1, source_target_pairs={{0,96},{4,100},{8,104},{12,108},{16,112},{20,116},{24,120},{28,124... | collective-permute-start | bytes 3244040 | tf_op jit(solution)/shard_map/ppermute | solution.py:146
  450.5 25.5 %collective-permute-start.55 = (bf16[2,4,16,4224]{3,2,0,1:T(8,128)(2,1)}, bf16[2,4,16,4224]{3,2,0,1:T(8,128)(2,1)}, u32[]{:S(2)}, u32[]{:S(2)}) collective-permute-start(bf16[2,4,16,4224]{3,2,0,1:T(8,128)(2,1)} %fusion.20), channel_id=1, source_target_pairs={{0,32},{4,36},{8,40},{12,44},{16,48},{20,52},{24,56},{28,60},{32,6... | collective-permute-start | bytes 3244040 | tf_op jit(solution)/shard_map/ppermute | solution.py:146
  452.8 24.8 %collective-permute-start.49 = (bf16[4,2,16,4224]{3,2,1,0:T(8,128)(2,1)}, bf16[4,2,16,4224]{3,2,1,0:T(8,128)(2,1)}, u32[]{:S(2)}, u32[]{:S(2)}) collective-permute-start(bf16[4,2,16,4224]{3,2,1,0:T(8,128)(2,1)} %fusion.23), channel_id=1, source_target_pairs={{0,12},{4,0},{8,4},{12,8},{16,28},{20,16},{24,20},{28,24},{32,44},... | collective-permute-start | bytes 3244040 | tf_op jit(solution)/shard_map/ppermute | solution.py:146
  459.0 10.7 %collective-permute-start.12 = (bf16[128,2048]{1,0:T(8,128)(2,1)S(1)}, bf16[128,2048]{1,0:T(8,128)(2,1)S(1)}, u32[]{:S(2)}, u32[]{:S(2)}) collective-permute-start(bf16[128,2048]{1,0:T(8,128)(2,1)S(1)} %get-tuple-element.25), channel_id=1, source_target_pairs={{0,2},{2,0},{1,3},{3,1},{4,6},{6,4},{5,7},{7,5},{8,10},{10,8},{9,1... | collective-permute-start | bytes 1572872 | tf_op jit(solution)/shard_map/ppermute | solution.py:108
  460.9 26.8 %collective-permute-start.43 = (bf16[4,2,16,4224]{3,2,1,0:T(8,128)(2,1)}, bf16[4,2,16,4224]{3,2,1,0:T(8,128)(2,1)}, u32[]{:S(2)}, u32[]{:S(2)}) collective-permute-start(bf16[4,2,16,4224]{3,2,1,0:T(8,128)(2,1)} %fusion.26), channel_id=1, source_target_pairs={{0,4},{4,8},{8,12},{12,0},{16,20},{20,24},{24,28},{28,16},{32,36},... | collective-permute-start | bytes 3244040 | tf_op jit(solution)/shard_map/ppermute | solution.py:146
  469.9 49.3 %collective-permute-start.13 = (bf16[2,128,2048]{2,1,0:T(8,128)(2,1)S(1)}, bf16[2,128,2048]{2,1,0:T(8,128)(2,1)S(1)}, u32[]{:S(2)}, u32[]{:S(2)}) collective-permute-start(bf16[2,128,2048]{2,1,0:T(8,128)(2,1)S(1)} %pad_maximum_fusion.10), channel_id=1, source_target_pairs={{0,1},{1,0},{2,3},{3,2},{4,5},{5,4},{6,7},{7,6},{8,9},{9,8},{10,11... | collective-permute-start | bytes 3145736 | tf_op jit(solution)/shard_map/ppermute | solution.py:110
  471.9 19.3 %collective-permute-start.62 = (bf16[2,16,4224]{2,1,0:T(8,128)(2,1)S(1)}, bf16[2,16,4224]{2,1,0:T(8,128)(2,1)S(1)}, u32[]{:S(2)}, u32[]{:S(2)}) collective-permute-start(bf16[2,16,4224]{2,1,0:T(8,128)(2,1)S(1)} %dynamic-slice_bitcast_fusion.4), channel_id=1, source_target_pairs={{0,12},{4,0},{8,4},{12,8},{16,28},{20,16},{24,20},{28,24},{32,44},... | collective-permute-start | bytes 811016 | tf_op jit(solution)/shard_map/ppermute | solution.py:146
  477.5 13.9 %collective-permute-start.56 = (bf16[2,16,4224]{2,1,0:T(8,128)(2,1)S(1)}, bf16[2,16,4224]{2,1,0:T(8,128)(2,1)S(1)}, u32[]{:S(2)}, u32[]{:S(2)}) collective-permute-start(bf16[2,16,4224]{2,1,0:T(8,128)(2,1)S(1)} %dynamic-slice_bitcast_fusion.5), channel_id=1, source_target_pairs={{0,4},{4,8},{8,12},{12,0},{16,20},{20,24},{24,28},{28,16},{32,36},... | collective-permute-start | bytes 811016 | tf_op jit(solution)/shard_map/ppermute | solution.py:146
  479.4 14.1 %collective-permute-start.50 = (bf16[2,16,4224]{2,1,0:T(8,128)(2,1)S(1)}, bf16[2,16,4224]{2,1,0:T(8,128)(2,1)S(1)}, u32[]{:S(2)}, u32[]{:S(2)}) collective-permute-start(bf16[2,16,4224]{2,1,0:T(8,128)(2,1)S(1)} %dynamic-slice_bitcast_fusion.6), channel_id=1, source_target_pairs={{0,96},{4,100},{8,104},{12,108},{16,112},{20,116},{24,120},{28,124... | collective-permute-start | bytes 811016 | tf_op jit(solution)/shard_map/ppermute | solution.py:146
  489.5 9.6 %collective-permute-start.44 = (bf16[2,16,4224]{2,1,0:T(8,128)(2,1)S(1)}, bf16[2,16,4224]{2,1,0:T(8,128)(2,1)S(1)}, u32[]{:S(2)}, u32[]{:S(2)}) collective-permute-start(bf16[2,16,4224]{2,1,0:T(8,128)(2,1)S(1)} %dynamic-slice_bitcast_fusion.7), channel_id=1, source_target_pairs={{0,32},{4,36},{8,40},{12,44},{16,48},{20,52},{24,56},{28,60},{32,6... | collective-permute-start | bytes 811016 | tf_op jit(solution)/shard_map/ppermute | solution.py:146
  491.3 8.0 %collective-permute-start.63 = (bf16[2,16,4224]{2,1,0:T(8,128)(2,1)S(1)}, bf16[2,16,4224]{2,1,0:T(8,128)(2,1)S(1)}, u32[]{:S(2)}, u32[]{:S(2)}) collective-permute-start(bf16[2,16,4224]{2,1,0:T(8,128)(2,1)S(1)} %fusion.128), channel_id=1, source_target_pairs={{0,12},{4,0},{8,4},{12,8},{16,28},{20,16},{24,20},{28,24},{32,44},... | collective-permute-start | bytes 811016 | tf_op jit(solution)/shard_map/ppermute | solution.py:146
  491.5 10.3 %collective-permute-start.57 = (bf16[2,16,4224]{2,1,0:T(8,128)(2,1)S(1)}, bf16[2,16,4224]{2,1,0:T(8,128)(2,1)S(1)}, u32[]{:S(2)}, u32[]{:S(2)}) collective-permute-start(bf16[2,16,4224]{2,1,0:T(8,128)(2,1)S(1)} %fusion.130), channel_id=1, source_target_pairs={{0,4},{4,8},{8,12},{12,0},{16,20},{20,24},{24,28},{28,16},{32,36},... | collective-permute-start | bytes 811016 | tf_op jit(solution)/shard_map/ppermute | solution.py:146
  493.6 8.5 %collective-permute-start.51 = (bf16[2,16,4224]{2,1,0:T(8,128)(2,1)S(1)}, bf16[2,16,4224]{2,1,0:T(8,128)(2,1)S(1)}, u32[]{:S(2)}, u32[]{:S(2)}) collective-permute-start(bf16[2,16,4224]{2,1,0:T(8,128)(2,1)S(1)} %fusion.132), channel_id=1, source_target_pairs={{0,96},{4,100},{8,104},{12,108},{16,112},{20,116},{24,120},{28,124... | collective-permute-start | bytes 811016 | tf_op jit(solution)/shard_map/ppermute | solution.py:146
  499.2 8.8 %collective-permute-start.45 = (bf16[2,16,4224]{2,1,0:T(8,128)(2,1)S(1)}, bf16[2,16,4224]{2,1,0:T(8,128)(2,1)S(1)}, u32[]{:S(2)}, u32[]{:S(2)}) collective-permute-start(bf16[2,16,4224]{2,1,0:T(8,128)(2,1)S(1)} %fusion.134), channel_id=1, source_target_pairs={{0,32},{4,36},{8,40},{12,44},{16,48},{20,52},{24,56},{28,60},{32,6... | collective-permute-start | bytes 811016 | tf_op jit(solution)/shard_map/ppermute | solution.py:146
  499.4 8.7 %collective-permute-start.64 = (bf16[2,16,4224]{2,1,0:T(8,128)(2,1)S(1)}, bf16[2,16,4224]{2,1,0:T(8,128)(2,1)S(1)}, u32[]{:S(2)}, u32[]{:S(2)}) collective-permute-start(bf16[2,16,4224]{2,1,0:T(8,128)(2,1)S(1)} %fusion.129), channel_id=1, source_target_pairs={{0,12},{4,0},{8,4},{12,8},{16,28},{20,16},{24,20},{28,24},{32,44},... | collective-permute-start | bytes 811016 | tf_op jit(solution)/shard_map/ppermute | solution.py:146
  501.8 7.7 %collective-permute-start.58 = (bf16[2,16,4224]{2,1,0:T(8,128)(2,1)S(1)}, bf16[2,16,4224]{2,1,0:T(8,128)(2,1)S(1)}, u32[]{:S(2)}, u32[]{:S(2)}) collective-permute-start(bf16[2,16,4224]{2,1,0:T(8,128)(2,1)S(1)} %fusion.131), channel_id=1, source_target_pairs={{0,4},{4,8},{8,12},{12,0},{16,20},{20,24},{24,28},{28,16},{32,36},... | collective-permute-start | bytes 811016 | tf_op jit(solution)/shard_map/ppermute | solution.py:146
  502.2 7.4 %collective-permute-start.52 = (bf16[2,16,4224]{2,1,0:T(8,128)(2,1)S(1)}, bf16[2,16,4224]{2,1,0:T(8,128)(2,1)S(1)}, u32[]{:S(2)}, u32[]{:S(2)}) collective-permute-start(bf16[2,16,4224]{2,1,0:T(8,128)(2,1)S(1)} %fusion.133), channel_id=1, source_target_pairs={{0,96},{4,100},{8,104},{12,108},{16,112},{20,116},{24,120},{28,124... | collective-permute-start | bytes 811016 | tf_op jit(solution)/shard_map/ppermute | solution.py:146
  508.0 7.7 %collective-permute-start.46 = (bf16[2,16,4224]{2,1,0:T(8,128)(2,1)S(1)}, bf16[2,16,4224]{2,1,0:T(8,128)(2,1)S(1)}, u32[]{:S(2)}, u32[]{:S(2)}) collective-permute-start(bf16[2,16,4224]{2,1,0:T(8,128)(2,1)S(1)} %fusion.135), channel_id=1, source_target_pairs={{0,32},{4,36},{8,40},{12,44},{16,48},{20,52},{24,56},{28,60},{32,6... | collective-permute-start | bytes 811016 | tf_op jit(solution)/shard_map/ppermute | solution.py:146
  517.0 59.4 %collective-permute-start.65 = (bf16[64,4224]{1,0:T(8,128)(2,1)}, bf16[64,4224]{1,0:T(8,128)(2,1)}, u32[]{:S(2)}, u32[]{:S(2)}) collective-permute-start(bf16[64,4224]{1,0:T(8,128)(2,1)} %fusion.127), channel_id=1, source_target_pairs={{0,16},{4,20},{8,24},{12,28},{16,0},{20,4},{24,8},{28,12},{32,48},... | collective-permute-start | bytes 1622024 | tf_op jit(solution)/shard_map/ppermute | solution.py:170
  555.9 75.3 %collective-permute-start.14 = (f32[2,128,2048]{2,1,0:T(8,128)}, f32[2,128,2048]{2,1,0:T(8,128)S(1)}, u32[]{:S(2)}, u32[]{:S(2)}) collective-permute-start(f32[2,128,2048]{2,1,0:T(8,128)} %bitcast.54), channel_id=1, source_target_pairs={{0,1},{1,0},{2,3},{3,2},{4,5},{5,4},{6,7},{7,6},{8,9},{9,8},{10,11... | collective-permute-start | bytes 6291464 | tf_op jit(solution)/shard_map/ppermute | solution.py:116
  573.8 17.2 %collective-permute-start.34 = (bf16[2,4,16,2560]{3,2,0,1:T(8,128)(2,1)S(1)}, bf16[2,4,16,2560]{3,2,0,1:T(8,128)(2,1)S(1)}, u32[]{:S(2)}, u32[]{:S(2)}) collective-permute-start(bf16[2,4,16,2560]{3,2,0,1:T(8,128)(2,1)S(1)} %bitcast.546), channel_id=1, source_target_pairs={{0,96},{4,100},{8,104},{12,108},{16,112},{20,116},{24,120},{28,124... | collective-permute-start | bytes 1966088 | tf_op jit(solution)/shard_map/ppermute | solution.py:146
  574.1 18.6 %collective-permute-start.28 = (bf16[2,4,16,2560]{3,2,0,1:T(8,128)(2,1)S(1)}, bf16[2,4,16,2560]{3,2,0,1:T(8,128)(2,1)S(1)}, u32[]{:S(2)}, u32[]{:S(2)}) collective-permute-start(bf16[2,4,16,2560]{3,2,0,1:T(8,128)(2,1)S(1)} %bitcast.547), channel_id=1, source_target_pairs={{0,32},{4,36},{8,40},{12,44},{16,48},{20,52},{24,56},{28,60},{32,6... | collective-permute-start | bytes 1966088 | tf_op jit(solution)/shard_map/ppermute | solution.py:146
  576.2 17.2 %collective-permute-start.22 = (bf16[4,2,16,2560]{3,2,1,0:T(8,128)(2,1)S(1)}, bf16[4,2,16,2560]{3,2,1,0:T(8,128)(2,1)S(1)}, u32[]{:S(2)}, u32[]{:S(2)}) collective-permute-start(bf16[4,2,16,2560]{3,2,1,0:T(8,128)(2,1)S(1)} %dynamic-slice_bitcast_fusion.2), channel_id=1, source_target_pairs={{0,12},{4,0},{8,4},{12,8},{16,28},{20,16},{24,20},{28,24},{32,44},... | collective-permute-start | bytes 1966088 | tf_op jit(solution)/shard_map/ppermute | solution.py:146
  576.4 18.3 %collective-permute-start.16 = (bf16[4,2,16,2560]{3,2,1,0:T(8,128)(2,1)S(1)}, bf16[4,2,16,2560]{3,2,1,0:T(8,128)(2,1)S(1)}, u32[]{:S(2)}, u32[]{:S(2)}) collective-permute-start(bf16[4,2,16,2560]{3,2,1,0:T(8,128)(2,1)S(1)} %dynamic-slice_bitcast_fusion.3), channel_id=1, source_target_pairs={{0,4},{4,8},{8,12},{12,0},{16,20},{20,24},{24,28},{28,16},{32,36},... | collective-permute-start | bytes 1966088 | tf_op jit(solution)/shard_map/ppermute | solution.py:146
  591.1 16.4 %collective-permute-start.35 = (bf16[2,4,16,2560]{3,2,0,1:T(8,128)(2,1)S(1)}, bf16[2,4,16,2560]{3,2,0,1:T(8,128)(2,1)S(1)}, u32[]{:S(2)}, u32[]{:S(2)}) collective-permute-start(bf16[2,4,16,2560]{3,2,0,1:T(8,128)(2,1)S(1)} %fusion.60), channel_id=1, source_target_pairs={{0,96},{4,100},{8,104},{12,108},{16,112},{20,116},{24,120},{28,124... | collective-permute-start | bytes 1966088 | tf_op jit(solution)/shard_map/ppermute | solution.py:146
  592.9 18.1 %collective-permute-start.29 = (bf16[2,4,16,2560]{3,2,0,1:T(8,128)(2,1)S(1)}, bf16[2,4,16,2560]{3,2,0,1:T(8,128)(2,1)S(1)}, u32[]{:S(2)}, u32[]{:S(2)}) collective-permute-start(bf16[2,4,16,2560]{3,2,0,1:T(8,128)(2,1)S(1)} %fusion.63), channel_id=1, source_target_pairs={{0,32},{4,36},{8,40},{12,44},{16,48},{20,52},{24,56},{28,60},{32,6... | collective-permute-start | bytes 1966088 | tf_op jit(solution)/shard_map/ppermute | solution.py:146
  593.6 17.6 %collective-permute-start.23 = (bf16[4,2,16,2560]{3,2,1,0:T(8,128)(2,1)S(1)}, bf16[4,2,16,2560]{3,2,1,0:T(8,128)(2,1)S(1)}, u32[]{:S(2)}, u32[]{:S(2)}) collective-permute-start(bf16[4,2,16,2560]{3,2,1,0:T(8,128)(2,1)S(1)} %fusion.66), channel_id=1, source_target_pairs={{0,12},{4,0},{8,4},{12,8},{16,28},{20,16},{24,20},{28,24},{32,44},... | collective-permute-start | bytes 1966088 | tf_op jit(solution)/shard_map/ppermute | solution.py:146
  594.8 17.3 %collective-permute-start.17 = (bf16[4,2,16,2560]{3,2,1,0:T(8,128)(2,1)S(1)}, bf16[4,2,16,2560]{3,2,1,0:T(8,128)(2,1)S(1)}, u32[]{:S(2)}, u32[]{:S(2)}) collective-permute-start(bf16[4,2,16,2560]{3,2,1,0:T(8,128)(2,1)S(1)} %fusion.69), channel_id=1, source_target_pairs={{0,4},{4,8},{8,12},{12,0},{16,20},{20,24},{24,28},{28,16},{32,36},... | collective-permute-start | bytes 1966088 | tf_op jit(solution)/shard_map/ppermute | solution.py:146
  607.7 16.5 %collective-permute-start.36 = (bf16[2,4,16,2560]{3,2,0,1:T(8,128)(2,1)S(1)}, bf16[2,4,16,2560]{3,2,0,1:T(8,128)(2,1)S(1)}, u32[]{:S(2)}, u32[]{:S(2)}) collective-permute-start(bf16[2,4,16,2560]{3,2,0,1:T(8,128)(2,1)S(1)} %fusion.61), channel_id=1, source_target_pairs={{0,96},{4,100},{8,104},{12,108},{16,112},{20,116},{24,120},{28,124... | collective-permute-start | bytes 1966088 | tf_op jit(solution)/shard_map/ppermute | solution.py:146
  611.1 16.7 %collective-permute-start.30 = (bf16[2,4,16,2560]{3,2,0,1:T(8,128)(2,1)S(1)}, bf16[2,4,16,2560]{3,2,0,1:T(8,128)(2,1)S(1)}, u32[]{:S(2)}, u32[]{:S(2)}) collective-permute-start(bf16[2,4,16,2560]{3,2,0,1:T(8,128)(2,1)S(1)} %fusion.64), channel_id=1, source_target_pairs={{0,32},{4,36},{8,40},{12,44},{16,48},{20,52},{24,56},{28,60},{32,6... | collective-permute-start | bytes 1966088 | tf_op jit(solution)/shard_map/ppermute | solution.py:146
  611.4 17.1 %collective-permute-start.24 = (bf16[4,2,16,2560]{3,2,1,0:T(8,128)(2,1)S(1)}, bf16[4,2,16,2560]{3,2,1,0:T(8,128)(2,1)S(1)}, u32[]{:S(2)}, u32[]{:S(2)}) collective-permute-start(bf16[4,2,16,2560]{3,2,1,0:T(8,128)(2,1)S(1)} %fusion.67), channel_id=1, source_target_pairs={{0,12},{4,0},{8,4},{12,8},{16,28},{20,16},{24,20},{28,24},{32,44},... | collective-permute-start | bytes 1966088 | tf_op jit(solution)/shard_map/ppermute | solution.py:146
  612.3 18.6 %collective-permute-start.18 = (bf16[4,2,16,2560]{3,2,1,0:T(8,128)(2,1)S(1)}, bf16[4,2,16,2560]{3,2,1,0:T(8,128)(2,1)S(1)}, u32[]{:S(2)}, u32[]{:S(2)}) collective-permute-start(bf16[4,2,16,2560]{3,2,1,0:T(8,128)(2,1)S(1)} %fusion.70), channel_id=1, source_target_pairs={{0,4},{4,8},{8,12},{12,0},{16,20},{20,24},{24,28},{28,16},{32,36},... | collective-permute-start | bytes 1966088 | tf_op jit(solution)/shard_map/ppermute | solution.py:146
  624.4 7.4 %collective-permute-start.37 = (bf16[2,16,2560]{2,1,0:T(8,128)(2,1)S(1)}, bf16[2,16,2560]{2,1,0:T(8,128)(2,1)S(1)}, u32[]{:S(2)}, u32[]{:S(2)}) collective-permute-start(bf16[2,16,2560]{2,1,0:T(8,128)(2,1)S(1)} %dynamic-slice_bitcast_fusion.8), channel_id=1, source_target_pairs={{0,12},{4,0},{8,4},{12,8},{16,28},{20,16},{24,20},{28,24},{32,44},... | collective-permute-start | bytes 491528 | tf_op jit(solution)/shard_map/ppermute | solution.py:146
  628.0 6.6 collective-permute-start.31
  631.1 6.6 collective-permute-start.19
  631.4 24.2 %collective-permute-start.15 = (bf16[128,2048]{1,0:T(8,128)(2,1)S(1)}, bf16[128,2048]{1,0:T(8,128)(2,1)S(1)}, u32[]{:S(2)}, u32[]{:S(2)}) collective-permute-start(bf16[128,2048]{1,0:T(8,128)(2,1)S(1)} %fusion.97), channel_id=1, source_target_pairs={{0,2},{2,0},{1,3},{3,1},{4,6},{6,4},{5,7},{7,5},{8,10},{10,8},{9,1... | collective-permute-start | bytes 1572872 | tf_op jit(solution)/shard_map/ppermute | solution.py:119
  634.7 6.9 %collective-permute-start.32 = (bf16[2,16,2560]{2,1,0:T(8,128)(2,1)S(1)}, bf16[2,16,2560]{2,1,0:T(8,128)(2,1)S(1)}, u32[]{:S(2)}, u32[]{:S(2)}) collective-permute-start(bf16[2,16,2560]{2,1,0:T(8,128)(2,1)S(1)} %fusion.151), channel_id=1, source_target_pairs={{0,4},{4,8},{8,12},{12,0},{16,20},{20,24},{24,28},{28,16},{32,36},... | collective-permute-start | bytes 491528 | tf_op jit(solution)/shard_map/ppermute | solution.py:146
  634.8 6.9 %collective-permute-start.26 = (bf16[2,16,2560]{2,1,0:T(8,128)(2,1)S(1)}, bf16[2,16,2560]{2,1,0:T(8,128)(2,1)S(1)}, u32[]{:S(2)}, u32[]{:S(2)}) collective-permute-start(bf16[2,16,2560]{2,1,0:T(8,128)(2,1)S(1)} %fusion.153), channel_id=1, source_target_pairs={{0,96},{4,100},{8,104},{12,108},{16,112},{20,116},{24,120},{28,124... | collective-permute-start | bytes 491528 | tf_op jit(solution)/shard_map/ppermute | solution.py:146
  637.8 7.3 %collective-permute-start.20 = (bf16[2,16,2560]{2,1,0:T(8,128)(2,1)S(1)}, bf16[2,16,2560]{2,1,0:T(8,128)(2,1)S(1)}, u32[]{:S(2)}, u32[]{:S(2)}) collective-permute-start(bf16[2,16,2560]{2,1,0:T(8,128)(2,1)S(1)} %fusion.155), channel_id=1, source_target_pairs={{0,32},{4,36},{8,40},{12,44},{16,48},{20,52},{24,56},{28,60},{32,6... | collective-permute-start | bytes 491528 | tf_op jit(solution)/shard_map/ppermute | solution.py:146
  637.9 7.2 %collective-permute-start.39 = (bf16[2,16,2560]{2,1,0:T(8,128)(2,1)S(1)}, bf16[2,16,2560]{2,1,0:T(8,128)(2,1)S(1)}, u32[]{:S(2)}, u32[]{:S(2)}) collective-permute-start(bf16[2,16,2560]{2,1,0:T(8,128)(2,1)S(1)} %fusion.150), channel_id=1, source_target_pairs={{0,12},{4,0},{8,4},{12,8},{16,28},{20,16},{24,20},{28,24},{32,44},... | collective-permute-start | bytes 491528 | tf_op jit(solution)/shard_map/ppermute | solution.py:146
  641.7 6.6 collective-permute-start.33
  645.1 6.6 collective-permute-start.21
  651.9 21.7 %collective-permute-start.40 = (bf16[64,2560]{1,0:T(8,128)(2,1)S(1)}, bf16[64,2560]{1,0:T(8,128)(2,1)}, u32[]{:S(2)}, u32[]{:S(2)}) collective-permute-start(bf16[64,2560]{1,0:T(8,128)(2,1)S(1)} %fusion.148), channel_id=1, source_target_pairs={{0,16},{4,20},{8,24},{12,28},{16,0},{20,4},{24,8},{28,12},{32,48},... | collective-permute-start | bytes 983048 | tf_op jit(solution)/shard_map/ppermute | solution.py:170
  657.1 15.8 %all-to-all-start.1 = ((f32[128,3,16]{2,1,0:T(4,128)}), f32[128,3,16]{2,1,0:T(4,128)S(1)}, u32[]{:S(2)}, u32[]{:S(2)}) async-start(f32[128,3,16]{2,1,0:T(4,128)} %copy.128), calls=%async_computation.1 | async-start | bytes 524288 | tf_op jit(solution)/shard_map/all_to_all | solution.py:183
  (65 other events, 501.9 us)
Sparse Core Ops, SparseCore 0:
  12.4 121.3 all-gather.2
  136.9 166.7 all-gather.4

commit v12 on v10

--- a/solution.py
+++ b/solution.py
@@ -161,6 +161,40 @@
     give = lax.dynamic_index_in_dim(along_z, 1 - y_pos, 0, keepdims=False)
     pair = [(i, i ^ 4) for i in range(32)]
     return keep + lax.ppermute(give.astype(jnp.bfloat16), "dp", pair).astype(jnp.float32)
+
+
+def ring_collect(chunk, pos, stride, size, step):
+    pairs = ring_pairs(step, stride, size)
+    got = [chunk]
+    for _ in range(size - 1):
+        got.append(lax.ppermute(got[-1], "dp", pairs))
+    relative = jnp.stack(got)
+    if step == 1:
+        where_from = (pos - jnp.arange(size)) % size
+    else:
+        where_from = (jnp.arange(size) - pos) % size
+    return jnp.take(relative, where_from, axis=0)
+
+
+def ring_gather(values):
+    index = lax.axis_index("dp")
+    x_pos, y_pos, z_pos = index % 4, (index // 4) % 2, index // 8
+    pair = [(i, i ^ 4) for i in range(32)]
+    other = lax.ppermute(values, "dp", pair)
+    both = jnp.where(y_pos == 0, jnp.stack([values, other]), jnp.stack([other, values]))
+    part_rows = values.shape[0] // 4
+    pieces = []
+    for part, (x_first, step) in enumerate(((True, 1), (True, 3), (False, 1), (False, 3))):
+        rows = both[:, part * part_rows : (part + 1) * part_rows]
+        if x_first:
+            once = ring_collect(rows, x_pos, 1, 4, step)
+            twice = ring_collect(once, z_pos, 8, 4, step)
+            pieces.append(jnp.moveaxis(twice, 1, 2))
+        else:
+            once = ring_collect(rows, z_pos, 8, 4, step)
+            twice = ring_collect(once, x_pos, 1, 4, step)
+            pieces.append(jnp.moveaxis(twice, 0, 2))
+    return jnp.concatenate(pieces, axis=3).reshape((-1,) + values.shape[1:])
 
 
 def small_gather(vectors):
@@ -210,7 +244,7 @@
     cot_local = cotangent[0].reshape(-1, model_width)
     attn_pack = jnp.concatenate([w_query, w_forget, w_value, w_outgate, w_output.T], axis=1)
     mlp_pack = jnp.concatenate([w_gate, w_up, w_down.T], axis=1)
-    attn_all = lax.all_gather(attn_pack, "dp", axis=0, tiled=True)
+    attn_all = ring_gather(attn_pack)
     mlp_all = lax.all_gather(mlp_pack, "dp", axis=0, tiled=True)
     wq_all = attn_all[:, 0 * local_width : 1 * local_width]
     wf_all = attn_all[:, 1 * local_width : 2 * local_width]

time: 659 us -> 654 us (level)
  waiting for transfers between devices: 355 us -> 243 us
  starting transfers between devices: 51 us -> 89 us
  other arithmetic: 46.8 us -> 79.2 us
  local copies, waits for them, and re-layouts: 70 us -> 101 us
    all_gather x1, waiting for transfers between devices: 73.2 us -> 0.01 us  [shards(): mlp_all = lax.all_gather(mlp_pack, 'dp', axis=0, tiled=True)]
    all_gather x1 -> x0, waiting for transfers between devices: 72.5 us -> none  [shards(): attn_all = lax.all_gather(attn_pack, 'dp', axis=0, tiled=True)]
    ppermute x0 -> x25, waiting for transfers between devices: none -> 64 us  [the longest x24 64 us: ring_collect(): got.append(lax.ppermute(got[-1], 'dp', pairs))]
    ppermute x0 -> x25, starting transfers between devices: none -> 33.6 us  [the longest x24 30.3 us: ring_collect(): got.append(lax.ppermute(got[-1], 'dp', pairs))]
    ppermute x4, waiting for transfers between devices: 56.6 us -> 32 us  [row_gather(): across = lax.ppermute(values, 'tensor', ACROSS)]
    gather x0 -> x8, local copies, waits for them, and re-layouts: none -> 19.4 us  [ring_collect(): return jnp.take(relative, where_from, axis=0)]
    another operation x0 -> x12, other arithmetic: none -> 19.1 us  [ring_collect(): relative = jnp.stack(got)]
    concatenate x0 -> x1, local copies, waits for them, and re-layouts: none -> 8.9 us  [ring_gather(): return jnp.concatenate(pieces, axis=3).reshape((-1,) + values.shape[1:])]
  transfers between devices with their start and end apart: 34 -> 58, of which waited for: 25 -> 32; matrix products, arithmetic and copies ran while one was open for 26% -> 36% of each run, Pallas kernels for 2% -> 2%
where the time goes in v12:
time: 654 us; the launch traced here: 642 us
  waiting for transfers between devices  243 us (37%)
  local copies, waits for them, and re-layouts  101 us (15%)
  starting transfers between devices  89 us (14%)
  matrix products  87.9 us (13%)
  other arithmetic  79.2 us (12%)
  Pallas kernels  26.6 us (4%)
  between operations  15.7 us (2%)
    ppermute x12, waiting for transfers between devices, ring_stage(): got = lax.ppermute(acc.astype(jnp.bfloat16), 'dp', pairs)  82.5 us
    ppermute x24, waiting for transfers between devices, ring_collect(): got.append(lax.ppermute(got[-1], 'dp', pairs))  64 us
    ppermute x4, waiting for transfers between devices, row_sum(): lax.ppermute(theirs.astype(jnp.bfloat16), 'tensor', ACROSS)  41.9 us
    dot_general x8, matrix products, matmul_plain(): return jnp.dot(left, right, preferred_element_type=jnp.float32)  38.8 us
    ppermute x4, waiting for transfers between devices, row_gather(): across = lax.ppermute(values, 'tensor', ACROSS)  32 us
    dot_general x8, matrix products, times_trans(): lax.dot_general(left, right, (((1,), (1,)), ((), ())), preferred_element_...  31.9 us
    ppermute x24, starting transfers between devices, ring_collect(): got.append(lax.ppermute(got[-1], 'dp', pairs))  30.3 us
    pallas_call x2, Pallas kernels, grad_pack(): pl.pallas_call(functools.partial(pack_kernel, per), grid=(rows_out // til...  26.6 us
  transfers between devices with their start and end apart: 58, of which 32 were waited for; matrix products, arithmetic and copies ran while one was open for 36% of the time, Pallas kernels for 2%

profile of v12, /device:TPU:0, one launch (start us, length us, event | category | flops | bytes accessed | tf_op | source)
XLA Modules:
  0.0 642.4 jit_solution(14586021421308018005)
XLA Ops:
  13.5 3.3 collective-permute-start.2
  18.2 8.9 %all-to-all-start = ((f32[128,3,16]{2,1,0:T(4,128)}), f32[128,3,16]{2,1,0:T(4,128)S(1)}, u32[]{:S(2)}, u32[]{:S(2)}) async-start(f32[128,3,16]{2,1,0:T(4,128)} %broadcast_in_dim.65), calls=%async_computation | async-start | bytes 524288 | tf_op jit(solution)/shard_map/all_to_all | solution.py:203
  29.4 9.9 %all-to-all-done = f32[128,3,16]{2,1,0:T(4,128)S(1)} async-done(((f32[128,3,16]{2,1,0:T(4,128)}), f32[128,3,16]{2,1,0:T(4,128)S(1)}, u32[]{:S(2)}, u32[]{:S(2)}) %all-to-all-start) | async-done | bytes 24608 | tf_op jit(solution)/shard_map/all_to_all | solution.py:203
  52.5 4.3 collective-permute-done.22
  56.7 3.7 collective-permute-start.23
  83.2 13.2 %collective-permute-done.24 = bf16[4,2,16,2560]{3,2,1,0:T(8,128)(2,1)} collective-permute-done((bf16[4,2,16,2560]{3,2,1,0:T(8,128)(2,1)}, bf16[4,2,16,2560]{3,2,1,0:T(8,128)(2,1)}, u32[]{:S(2)}, u32[]{:S(2)}) %collective-permute-start.24) | collective-permute-done | bytes 655392 | tf_op jit(solution)/shard_map/ppermute | solution.py:170
  101.7 21.8 %collective-permute-done.25 = bf16[4,2,16,2560]{3,2,1,0:T(8,128)(2,1)S(1)} collective-permute-done((bf16[4,2,16,2560]{3,2,1,0:T(8,128)(2,1)}, bf16[4,2,16,2560]{3,2,1,0:T(8,128)(2,1)S(1)}, u32[]{:S(2)}, u32[]{:S(2)}) %collective-permute-start.25) | collective-permute-done | bytes 655392 | tf_op jit(solution)/shard_map/ppermute | solution.py:170
  123.5 3.6 collective-permute-start.26
  133.4 20.4 %collective-permute-done.26 = bf16[4,2,16,2560]{3,2,1,0:T(8,128)(2,1)S(1)} collective-permute-done((bf16[4,2,16,2560]{3,2,1,0:T(8,128)(2,1)S(1)}, bf16[4,2,16,2560]{3,2,1,0:T(8,128)(2,1)S(1)}, u32[]{:S(2)}, u32[]{:S(2)}) %collective-permute-start.26) | collective-permute-done | bytes 655392 | tf_op jit(solution)/shard_map/ppermute | solution.py:170
  153.8 3.0 pad_maximum_fusion.5
  156.8 4.0 gather_fusion.8
  160.8 3.4 pad_maximum_fusion.4
  164.1 4.0 gather_fusion.6
  168.1 3.4 pad_maximum_fusion.3
  171.5 4.1 gather_fusion.4
  178.4 3.9 gather_fusion.2
  188.7 4.9 pad_maximum_fusion
  193.6 8.9 %copy.114 = bf16[4,2,4,64,2560]{4,3,2,1,0:T(8,128)(2,1)} copy(bf16[4,2,4,64,2560]{4,3,1,2,0:T(8,128)(2,1)} %pad_maximum_fusion) | data formatting | bytes 20971520 | tf_op jit(solution)/shard_map/concatenate | solution.py:197
  202.5 5.3 slice_bitcast_fusion
  207.8 4.0 copy.115
  211.8 4.0 copy.117
  218.6 3.6 fusion.59
  235.5 4.8 fusion.77
  240.3 3.1 fusion.32
  243.7 4.1 collective-permute-done.27
  251.1 11.9 %collective-permute-done.28 = bf16[128,2048]{1,0:T(8,128)(2,1)} collective-permute-done((bf16[128,2048]{1,0:T(8,128)(2,1)S(1)}, bf16[128,2048]{1,0:T(8,128)(2,1)}, u32[]{:S(2)}, u32[]{:S(2)}) %collective-permute-start.28) | collective-permute-done | bytes 524320 | tf_op jit(solution)/shard_map/ppermute | solution.py:119
  267.3 6.9 %collective-permute-done.33 = bf16[128,2048]{1,0:T(8,128)(2,1)} collective-permute-done((bf16[128,2048]{1,0:T(8,128)(2,1)S(1)}, bf16[128,2048]{1,0:T(8,128)(2,1)}, u32[]{:S(2)}, u32[]{:S(2)}) %collective-permute-start.33) | collective-permute-done | bytes 524320 | tf_op jit(solution)/shard_map/ppermute | solution.py:108
  275.6 9.0 %collective-permute-done.29 = bf16[128,2048]{1,0:T(8,128)(2,1)S(1)} collective-permute-done((bf16[128,2048]{1,0:T(8,128)(2,1)S(1)}, bf16[128,2048]{1,0:T(8,128)(2,1)S(1)}, u32[]{:S(2)}, u32[]{:S(2)}) %collective-permute-start.29) | collective-permute-done | bytes 524320 | tf_op jit(solution)/shard_map/ppermute | solution.py:108
  289.0 8.4 %fusion = f32[512,1408]{1,0:T(8,128)} fusion(bf16[512,2048]{1,0:T(8,128)(2,1)} %bitcast.388, bf16[2048,4224]{1,0:T(8,128)(2,1)} %all-gather.2.cloned.1.call-done), kind=kOutput, calls=%fused_computation.11 | convolution fusion | flops 2952790016 | bytes 10747904 | tf_op jit(solution)/shard_map/dot_general | solution.py:27
  298.9 5.0 fusion.6
  303.9 6.6 %multiply_convert_fusion.1 = (bf16[512,1408]{1,0:T(8,128)(2,1)S(1)}, bf16[512,1408]{1,0:T(8,128)(2,1)S(1)}, bf16[512,1408]{1,0:T(8,128)(2,1)S(1)}) fusion(f32[512,1408]{1,0:T(8,128)} %fusion, f32[512,1408]{1,0:T(8,128)} %fusion.6, bf16[512,2048]{1,0:T(8,128)(2,1)S(1)} %bitcast.392, bf16[2048,4224]{1,0:T(8,128)(2,1)S(1)} %copy-done.53), kind=kOutput, calls=%fused_computation.27 | convolution fusion | flops 2963603456 | bytes 17956864 | tf_op jit(solution)/shard_map/dot_general | solution.py:27
  314.7 15.7 %shard_map.247 = bf16[2048,4224]{1,0:T(8,128)(2,1)} custom-call(bf16[512,2048]{1,0:T(8,128)(2,1)} %bitcast.390, bf16[512,2048]{1,0:T(8,128)(2,1)} %bitcast.389, bf16[512,4224]{1,0:T(8,128)(2,1)} %pad_maximum_fusion.1.right_ref), custom_call_target="tpu_custom_call" | custom-call | flops 8858370048 | bytes 25821184 | tf_op jit(solution)/shard_map/pallas_call | solution.py:64
  330.5 6.0 fusion.4
  336.5 5.5 fusion.12
  343.4 5.5 fusion.2
  355.4 13.5 %collective-permute-done.36 = bf16[128,2048]{1,0:T(8,128)(2,1)S(1)} collective-permute-done((bf16[128,2048]{1,0:T(8,128)(2,1)S(1)}, bf16[128,2048]{1,0:T(8,128)(2,1)S(1)}, u32[]{:S(2)}, u32[]{:S(2)}) %collective-permute-start.36) | collective-permute-done | bytes 524320 | tf_op jit(solution)/shard_map/ppermute | solution.py:119
  369.4 13.8 %collective-permute-done.32 = bf16[128,2048]{1,0:T(8,128)(2,1)S(1)} collective-permute-done((bf16[128,2048]{1,0:T(8,128)(2,1)S(1)}, bf16[128,2048]{1,0:T(8,128)(2,1)S(1)}, u32[]{:S(2)}, u32[]{:S(2)}) %collective-permute-start.32) | collective-permute-done | bytes 524320 | tf_op jit(solution)/shard_map/ppermute | solution.py:119
  386.6 15.9 %collective-permute-done.37 = bf16[128,2048]{1,0:T(8,128)(2,1)S(1)} collective-permute-done((bf16[128,2048]{1,0:T(8,128)(2,1)S(1)}, bf16[128,2048]{1,0:T(8,128)(2,1)S(1)}, u32[]{:S(2)}, u32[]{:S(2)}) %collective-permute-start.37) | collective-permute-done | bytes 524320 | tf_op jit(solution)/shard_map/ppermute | solution.py:108
  403.6 3.0 collective-permute-done.38
  408.2 4.9 fusion.137
  416.1 3.2 fusion.62
  420.6 3.2 convolution_select_fusion
  435.5 10.9 %shard_map.246 = bf16[2048,2560]{1,0:T(8,128)(2,1)} custom-call(bf16[512,2048]{1,0:T(8,128)(2,1)} %bitcast.385, bf16[512,2048]{1,0:T(8,128)(2,1)} %bitcast.387, bf16[512,2560]{1,0:T(8,128)(2,1)} %constant_dynamic-update-slice_fusion.4.right_ref), custom_call_target="tpu_custom_call" | custom-call | flops 5368709120 | bytes 17301504 | tf_op jit(solution)/shard_map/pallas_call | solution.py:64
  446.3 9.0 %copy.176 = bf16[4,2,4,64,2560]{4,3,1,0,2:T(8,128)(2,1)} copy(bf16[4,2,4,64,2560]{4,3,2,1,0:T(8,128)(2,1)} %bitcast.370) | data formatting | bytes 20971520 | tf_op jit(solution)/shard_map/reshape | solution.py:157
  455.4 9.5 %fusion.152 = (bf16[4,4,2,64,1280]{4,3,2,1,0:T(8,128)(2,1)}, bf16[4,4,2,64,1280]{4,3,2,1,0:T(8,128)(2,1)}) fusion(bf16[4,4,2,64,2560]{4,3,2,1,0:T(8,128)(2,1)} %bitcast.369), kind=kLoop, calls=%fused_computation.301 | loop fusion | bytes 20971520 | tf_op jit(solution)/shard_map/slice | solution.py:140
  474.7 3.7 collective-permute-start.47
  478.4 2.9 fusion.37
  481.4 3.0 add_add_fusion
  486.0 13.2 %collective-permute-done.41 = bf16[4,2,64,1280]{3,2,1,0:T(8,128)(2,1)S(1)} collective-permute-done((bf16[4,2,64,1280]{3,2,1,0:T(8,128)(2,1)S(1)}, bf16[4,2,64,1280]{3,2,1,0:T(8,128)(2,1)S(1)}, u32[]{:S(2)}, u32[]{:S(2)}) %collective-permute-start.41) | collective-permute-done | bytes 1310752 | tf_op jit(solution)/shard_map/ppermute | solution.py:148
  502.4 4.7 collective-permute-done.47
  507.2 3.1 fusion.16
  510.2 3.7 collective-permute-start.48
  515.2 18.9 %collective-permute-done.42 = bf16[4,2,64,1280]{3,2,1,0:T(8,128)(2,1)} collective-permute-done((bf16[4,2,64,1280]{3,2,1,0:T(8,128)(2,1)}, bf16[4,2,64,1280]{3,2,1,0:T(8,128)(2,1)}, u32[]{:S(2)}, u32[]{:S(2)}) %collective-permute-start.42) | collective-permute-done | bytes 1310752 | tf_op jit(solution)/shard_map/ppermute | solution.py:148
  534.1 3.1 fusion.20
  541.9 3.1 fusion.17
  544.9 3.7 collective-permute-start.49
  555.0 9.3 %all-to-all-start.1 = ((f32[128,3,16]{2,1,0:T(4,128)}), f32[128,3,16]{2,1,0:T(4,128)S(1)}, u32[]{:S(2)}, u32[]{:S(2)}) async-start(f32[128,3,16]{2,1,0:T(4,128)} %copy.133), calls=%async_computation.1 | async-start | bytes 524288 | tf_op jit(solution)/shard_map/all_to_all | solution.py:210
  564.3 17.6 %collective-permute-done.43 = bf16[4,2,64,1280]{3,2,1,0:T(8,128)(2,1)} collective-permute-done((bf16[4,2,64,1280]{3,2,1,0:T(8,128)(2,1)}, bf16[4,2,64,1280]{3,2,1,0:T(8,128)(2,1)}, u32[]{:S(2)}, u32[]{:S(2)}) %collective-permute-start.43) | collective-permute-done | bytes 1310752 | tf_op jit(solution)/shard_map/ppermute | solution.py:148
  584.6 4.7 collective-permute-done.49
  594.0 5.9 collective-permute-done.44
  603.4 7.2 %collective-permute-done.45 = bf16[2,64,1280]{2,1,0:T(8,128)(2,1)S(1)} collective-permute-done((bf16[2,64,1280]{2,1,0:T(8,128)(2,1)S(1)}, bf16[2,64,1280]{2,1,0:T(8,128)(2,1)S(1)}, u32[]{:S(2)}, u32[]{:S(2)}) %collective-permute-start.45) | collective-permute-done | bytes 327712 | tf_op jit(solution)/shard_map/ppermute | solution.py:148
  613.7 3.8 collective-permute-start.52
  617.4 4.1 collective-permute-done.46
  626.8 4.4 collective-permute-done.53
  (335 shorter events, 181.6 us)
Async XLA Ops:
  7.2 20.1 %copy-start = (s32[1,4,128]{2,1,0:T(4,128)S(1)}, s32[1,4,128]{2,1,0:T(4,128)}, u32[]{:S(2)}) copy-start(s32[1,4,128]{2,1,0:T(4,128)} %param.20) | copy-start | bytes 6148
  7.2 20.8 %copy-start.3 = (bf16[1,1,128,2048]{3,2,1,0:T(8,128)(2,1)S(1)}, bf16[1,1,128,2048]{3,2,1,0:T(8,128)(2,1)}, u32[]{:S(2)}) copy-start(bf16[1,1,128,2048]{3,2,1,0:T(8,128)(2,1)} %param.19) | copy-start | bytes 1572868
  7.2 281.7 %all-gather.2.cloned.1.call-start = ((), (), s32[]{:S(2)}) async-start(), calls=%async_computation.3 | async-start | bytes 17842176 | tf_op jit(solution)/shard_map/all_gather | solution.py:248
  13.5 26.8 %collective-permute-start.2 = (bf16[64,2560]{1,0:T(8,128)(2,1)S(1)}, bf16[64,2560]{1,0:T(8,128)(2,1)S(1)}, u32[]{:S(2)}, u32[]{:S(2)}) collective-permute-start(bf16[64,2560]{1,0:T(8,128)(2,1)S(1)} %bitcast_dynamic-update-slice_fusion.3), channel_id=1, source_target_pairs={{0,16},{4,20},{8,24},{12,28},{16,0},{20,4},{24,8},{28,12},{32,48},... | collective-permute-start | bytes 983048 | tf_op jit(solution)/shard_map/ppermute | solution.py:183
  18.2 21.1 %all-to-all-start = ((f32[128,3,16]{2,1,0:T(4,128)}), f32[128,3,16]{2,1,0:T(4,128)S(1)}, u32[]{:S(2)}, u32[]{:S(2)}) async-start(f32[128,3,16]{2,1,0:T(4,128)} %broadcast_in_dim.65), calls=%async_computation | async-start | bytes 524288 | tf_op jit(solution)/shard_map/all_to_all | solution.py:203
  27.2 605.0 %reduce-scatter.2.cloned.1.call-start = ((), (), s32[]{:S(2)}) async-start(), calls=%async_computation.4 | async-start | bytes 17842176 | tf_op jit(solution)/shard_map/reduce_scatter | solution.py:294
  28.8 21.4 %copy-start.49 = (f32[128]{0:T(128)}, f32[128]{0:T(128)S(1)}, u32[]{:S(2)}) copy-start(f32[128]{0:T(128)S(1)} %get-tuple-element.65) | copy-start | bytes 1540
  41.3 6.3 collective-permute-start.21
  42.6 18.0 %collective-permute-start = (bf16[128,2048]{1,0:T(8,128)(2,1)S(1)}, bf16[128,2048]{1,0:T(8,128)(2,1)S(1)}, u32[]{:S(2)}, u32[]{:S(2)}) collective-permute-start(bf16[128,2048]{1,0:T(8,128)(2,1)S(1)} %fusion.65), channel_id=1, source_target_pairs={{0,2},{2,0},{1,3},{3,1},{4,6},{6,4},{5,7},{7,5},{8,10},{10,8},{9,1... | collective-permute-start | bytes 1572872 | tf_op jit(solution)/shard_map/ppermute | solution.py:108
  42.9 7.4 %collective-permute-start.15 = (bf16[2,16,2560]{2,1,0:T(8,128)(2,1)}, bf16[2,16,2560]{2,1,0:T(8,128)(2,1)S(1)}, u32[]{:S(2)}, u32[]{:S(2)}) collective-permute-start(bf16[2,16,2560]{2,1,0:T(8,128)(2,1)} %get-tuple-element.56), channel_id=1, source_target_pairs={{0,32},{4,36},{8,40},{12,44},{16,48},{20,52},{24,56},{28,60},{32,6... | collective-permute-start | bytes 491528 | tf_op jit(solution)/shard_map/ppermute | solution.py:170
  44.1 6.3 collective-permute-start.9
  44.8 7.0 %collective-permute-start.3 = (bf16[2,16,2560]{2,1,0:T(8,128)(2,1)}, bf16[2,16,2560]{2,1,0:T(8,128)(2,1)S(1)}, u32[]{:S(2)}, u32[]{:S(2)}) collective-permute-start(bf16[2,16,2560]{2,1,0:T(8,128)(2,1)} %get-tuple-element.58), channel_id=1, source_target_pairs={{0,4},{4,8},{8,12},{12,0},{16,20},{20,24},{24,28},{28,16},{32,36},... | collective-permute-start | bytes 491528 | tf_op jit(solution)/shard_map/ppermute | solution.py:170
  47.6 9.1 %collective-permute-start.22 = (bf16[2,16,2560]{2,1,0:T(8,128)(2,1)}, bf16[2,16,2560]{2,1,0:T(8,128)(2,1)}, u32[]{:S(2)}, u32[]{:S(2)}) collective-permute-start(bf16[2,16,2560]{2,1,0:T(8,128)(2,1)} %collective-permute-done.21), channel_id=1, source_target_pairs={{0,96},{4,100},{8,104},{12,108},{16,112},{20,116},{24,120},{28,124... | collective-permute-start | bytes 491528 | tf_op jit(solution)/shard_map/ppermute | solution.py:170
  50.3 11.4 %collective-permute-start.16 = (bf16[2,16,2560]{2,1,0:T(8,128)(2,1)S(1)}, bf16[2,16,2560]{2,1,0:T(8,128)(2,1)}, u32[]{:S(2)}, u32[]{:S(2)}) collective-permute-start(bf16[2,16,2560]{2,1,0:T(8,128)(2,1)S(1)} %collective-permute-done.15), channel_id=1, source_target_pairs={{0,32},{4,36},{8,40},{12,44},{16,48},{20,52},{24,56},{28,60},{32,6... | collective-permute-start | bytes 491528 | tf_op jit(solution)/shard_map/ppermute | solution.py:170
  50.4 11.7 %collective-permute-start.10 = (bf16[2,16,2560]{2,1,0:T(8,128)(2,1)S(1)}, bf16[2,16,2560]{2,1,0:T(8,128)(2,1)}, u32[]{:S(2)}, u32[]{:S(2)}) collective-permute-start(bf16[2,16,2560]{2,1,0:T(8,128)(2,1)S(1)} %collective-permute-done.9), channel_id=1, source_target_pairs={{0,12},{4,0},{8,4},{12,8},{16,28},{20,16},{24,20},{28,24},{32,44},... | collective-permute-start | bytes 491528 | tf_op jit(solution)/shard_map/ppermute | solution.py:170
  51.9 10.8 %collective-permute-start.4 = (bf16[2,16,2560]{2,1,0:T(8,128)(2,1)S(1)}, bf16[2,16,2560]{2,1,0:T(8,128)(2,1)}, u32[]{:S(2)}, u32[]{:S(2)}) collective-permute-start(bf16[2,16,2560]{2,1,0:T(8,128)(2,1)S(1)} %collective-permute-done.3), channel_id=1, source_target_pairs={{0,4},{4,8},{8,12},{12,0},{16,20},{20,24},{24,28},{28,16},{32,36},... | collective-permute-start | bytes 491528 | tf_op jit(solution)/shard_map/ppermute | solution.py:170
  56.7 7.4 %collective-permute-start.23 = (bf16[2,16,2560]{2,1,0:T(8,128)(2,1)}, bf16[2,16,2560]{2,1,0:T(8,128)(2,1)S(1)}, u32[]{:S(2)}, u32[]{:S(2)}) collective-permute-start(bf16[2,16,2560]{2,1,0:T(8,128)(2,1)} %collective-permute-done.22), channel_id=1, source_target_pairs={{0,96},{4,100},{8,104},{12,108},{16,112},{20,116},{24,120},{28,124... | collective-permute-start | bytes 491528 | tf_op jit(solution)/shard_map/ppermute | solution.py:170
  61.7 66.0 %collective-permute-start.1 = (bf16[2,128,2048]{2,1,0:T(8,128)(2,1)}, bf16[2,128,2048]{2,1,0:T(8,128)(2,1)}, u32[]{:S(2)}, u32[]{:S(2)}) collective-permute-start(bf16[2,128,2048]{2,1,0:T(8,128)(2,1)} %pad_maximum_fusion.10), channel_id=1, source_target_pairs={{0,1},{1,0},{2,3},{3,2},{4,5},{5,4},{6,7},{7,6},{8,9},{9,8},{10,11... | collective-permute-start | bytes 3145736 | tf_op jit(solution)/shard_map/ppermute | solution.py:110
  61.7 9.2 %collective-permute-start.17 = (bf16[2,16,2560]{2,1,0:T(8,128)(2,1)}, bf16[2,16,2560]{2,1,0:T(8,128)(2,1)S(1)}, u32[]{:S(2)}, u32[]{:S(2)}) collective-permute-start(bf16[2,16,2560]{2,1,0:T(8,128)(2,1)} %collective-permute-done.16), channel_id=1, source_target_pairs={{0,32},{4,36},{8,40},{12,44},{16,48},{20,52},{24,56},{28,60},{32,6... | collective-permute-start | bytes 491528 | tf_op jit(solution)/shard_map/ppermute | solution.py:170
  62.1 11.4 %collective-permute-start.11 = (bf16[2,16,2560]{2,1,0:T(8,128)(2,1)}, bf16[2,16,2560]{2,1,0:T(8,128)(2,1)}, u32[]{:S(2)}, u32[]{:S(2)}) collective-permute-start(bf16[2,16,2560]{2,1,0:T(8,128)(2,1)} %collective-permute-done.10), channel_id=1, source_target_pairs={{0,12},{4,0},{8,4},{12,8},{16,28},{20,16},{24,20},{28,24},{32,44},... | collective-permute-start | bytes 491528 | tf_op jit(solution)/shard_map/ppermute | solution.py:170
  62.6 15.5 %collective-permute-start.5 = (bf16[2,16,2560]{2,1,0:T(8,128)(2,1)}, bf16[2,16,2560]{2,1,0:T(8,128)(2,1)}, u32[]{:S(2)}, u32[]{:S(2)}) collective-permute-start(bf16[2,16,2560]{2,1,0:T(8,128)(2,1)} %collective-permute-done.4), channel_id=1, source_target_pairs={{0,4},{4,8},{8,12},{12,0},{16,20},{20,24},{24,28},{28,16},{32,36},... | collective-permute-start | bytes 491528 | tf_op jit(solution)/shard_map/ppermute | solution.py:170
  66.8 29.5 %collective-permute-start.24 = (bf16[4,2,16,2560]{3,2,1,0:T(8,128)(2,1)}, bf16[4,2,16,2560]{3,2,1,0:T(8,128)(2,1)}, u32[]{:S(2)}, u32[]{:S(2)}) collective-permute-start(bf16[4,2,16,2560]{3,2,1,0:T(8,128)(2,1)} %broadcast_select_fusion), channel_id=1, source_target_pairs={{0,12},{4,0},{8,4},{12,8},{16,28},{20,16},{24,20},{28,24},{32,44},... | collective-permute-start | bytes 1966088 | tf_op jit(solution)/shard_map/ppermute | solution.py:170
  73.5 25.2 %collective-permute-start.18 = (bf16[4,2,16,2560]{3,2,1,0:T(8,128)(2,1)}, bf16[4,2,16,2560]{3,2,1,0:T(8,128)(2,1)}, u32[]{:S(2)}, u32[]{:S(2)}) collective-permute-start(bf16[4,2,16,2560]{3,2,1,0:T(8,128)(2,1)} %broadcast_select_fusion.1), channel_id=1, source_target_pairs={{0,4},{4,8},{8,12},{12,0},{16,20},{20,24},{24,28},{28,16},{32,36},... | collective-permute-start | bytes 1966088 | tf_op jit(solution)/shard_map/ppermute | solution.py:170
  76.2 22.6 %collective-permute-start.12 = (bf16[4,2,16,2560]{3,2,1,0:T(8,128)(2,1)}, bf16[4,2,16,2560]{3,2,1,0:T(8,128)(2,1)}, u32[]{:S(2)}, u32[]{:S(2)}) collective-permute-start(bf16[4,2,16,2560]{3,2,1,0:T(8,128)(2,1)} %broadcast_select_fusion.2), channel_id=1, source_target_pairs={{0,96},{4,100},{8,104},{12,108},{16,112},{20,116},{24,120},{28,124... | collective-permute-start | bytes 1966088 | tf_op jit(solution)/shard_map/ppermute | solution.py:170
  82.0 45.7 %copy-start.14 = (bf16[1,128,2048]{2,1,0:T(8,128)(2,1)S(1)}, bf16[1,128,2048]{2,1,0:T(8,128)(2,1)}, u32[]{:S(2)}) copy-start(bf16[1,128,2048]{2,1,0:T(8,128)(2,1)} %copy-done.13) | copy-start | bytes 1572868
  82.0 45.7 %copy-start.32 = (bf16[128,2048]{1,0:T(8,128)(2,1)S(1)}, bf16[128,2048]{1,0:T(8,128)(2,1)}, u32[]{:S(2)}) copy-start(bf16[128,2048]{1,0:T(8,128)(2,1)} %copy-done.31) | copy-start | bytes 1572868
  82.0 19.7 %collective-permute-start.6 = (bf16[4,2,16,2560]{3,2,1,0:T(8,128)(2,1)S(1)}, bf16[4,2,16,2560]{3,2,1,0:T(8,128)(2,1)S(1)}, u32[]{:S(2)}, u32[]{:S(2)}) collective-permute-start(bf16[4,2,16,2560]{3,2,1,0:T(8,128)(2,1)S(1)} %broadcast_select_fusion.3), channel_id=1, source_target_pairs={{0,32},{4,36},{8,40},{12,44},{16,48},{20,52},{24,56},{28,60},{32,6... | collective-permute-start | bytes 1966088 | tf_op jit(solution)/shard_map/ppermute | solution.py:170
  96.4 27.1 %collective-permute-start.25 = (bf16[4,2,16,2560]{3,2,1,0:T(8,128)(2,1)}, bf16[4,2,16,2560]{3,2,1,0:T(8,128)(2,1)S(1)}, u32[]{:S(2)}, u32[]{:S(2)}) collective-permute-start(bf16[4,2,16,2560]{3,2,1,0:T(8,128)(2,1)} %collective-permute-done.24), channel_id=1, source_target_pairs={{0,12},{4,0},{8,4},{12,8},{16,28},{20,16},{24,20},{28,24},{32,44},... | collective-permute-start | bytes 1966088 | tf_op jit(solution)/shard_map/ppermute | solution.py:170
  98.7 29.0 %collective-permute-start.19 = (bf16[4,2,16,2560]{3,2,1,0:T(8,128)(2,1)}, bf16[4,2,16,2560]{3,2,1,0:T(8,128)(2,1)}, u32[]{:S(2)}, u32[]{:S(2)}) collective-permute-start(bf16[4,2,16,2560]{3,2,1,0:T(8,128)(2,1)} %collective-permute-done.18), channel_id=1, source_target_pairs={{0,4},{4,8},{8,12},{12,0},{16,20},{20,24},{24,28},{28,16},{32,36},... | collective-permute-start | bytes 1966088 | tf_op jit(solution)/shard_map/ppermute | solution.py:170
  98.8 31.6 %collective-permute-start.13 = (bf16[4,2,16,2560]{3,2,1,0:T(8,128)(2,1)}, bf16[4,2,16,2560]{3,2,1,0:T(8,128)(2,1)}, u32[]{:S(2)}, u32[]{:S(2)}) collective-permute-start(bf16[4,2,16,2560]{3,2,1,0:T(8,128)(2,1)} %collective-permute-done.12), channel_id=1, source_target_pairs={{0,96},{4,100},{8,104},{12,108},{16,112},{20,116},{24,120},{28,124... | collective-permute-start | bytes 1966088 | tf_op jit(solution)/shard_map/ppermute | solution.py:170
  101.7 28.8 %copy-start.41 = (bf16[4,2,16,2560]{3,2,1,0:T(8,128)(2,1)}, bf16[4,2,16,2560]{3,2,1,0:T(8,128)(2,1)S(1)}, u32[]{:S(2)}) copy-start(bf16[4,2,16,2560]{3,2,1,0:T(8,128)(2,1)S(1)} %collective-permute-done.6) | copy-start | bytes 1966084
  101.7 31.7 %collective-permute-start.7 = (bf16[4,2,16,2560]{3,2,1,0:T(8,128)(2,1)S(1)}, bf16[4,2,16,2560]{3,2,1,0:T(8,128)(2,1)S(1)}, u32[]{:S(2)}, u32[]{:S(2)}) collective-permute-start(bf16[4,2,16,2560]{3,2,1,0:T(8,128)(2,1)S(1)} %collective-permute-done.6), channel_id=1, source_target_pairs={{0,32},{4,36},{8,40},{12,44},{16,48},{20,52},{24,56},{28,60},{32,6... | collective-permute-start | bytes 1966088 | tf_op jit(solution)/shard_map/ppermute | solution.py:170
  123.5 30.3 %collective-permute-start.26 = (bf16[4,2,16,2560]{3,2,1,0:T(8,128)(2,1)S(1)}, bf16[4,2,16,2560]{3,2,1,0:T(8,128)(2,1)S(1)}, u32[]{:S(2)}, u32[]{:S(2)}) collective-permute-start(bf16[4,2,16,2560]{3,2,1,0:T(8,128)(2,1)S(1)} %collective-permute-done.25), channel_id=1, source_target_pairs={{0,12},{4,0},{8,4},{12,8},{16,28},{20,16},{24,20},{28,24},{32,44},... | collective-permute-start | bytes 1966088 | tf_op jit(solution)/shard_map/ppermute | solution.py:170
  127.7 33.1 %collective-permute-start.20 = (bf16[4,2,16,2560]{3,2,1,0:T(8,128)(2,1)}, bf16[4,2,16,2560]{3,2,1,0:T(8,128)(2,1)}, u32[]{:S(2)}, u32[]{:S(2)}) collective-permute-start(bf16[4,2,16,2560]{3,2,1,0:T(8,128)(2,1)} %collective-permute-done.19), channel_id=1, source_target_pairs={{0,4},{4,8},{8,12},{12,0},{16,20},{20,24},{24,28},{28,16},{32,36},... | collective-permute-start | bytes 1966088 | tf_op jit(solution)/shard_map/ppermute | solution.py:170
  130.5 37.6 %collective-permute-start.14 = (bf16[4,2,16,2560]{3,2,1,0:T(8,128)(2,1)}, bf16[4,2,16,2560]{3,2,1,0:T(8,128)(2,1)}, u32[]{:S(2)}, u32[]{:S(2)}) collective-permute-start(bf16[4,2,16,2560]{3,2,1,0:T(8,128)(2,1)} %collective-permute-done.13), channel_id=1, source_target_pairs={{0,96},{4,100},{8,104},{12,108},{16,112},{20,116},{24,120},{28,124... | collective-permute-start | bytes 1966088 | tf_op jit(solution)/shard_map/ppermute | solution.py:170
  133.4 42.1 %collective-permute-start.8 = (bf16[4,2,16,2560]{3,2,1,0:T(8,128)(2,1)S(1)}, bf16[4,2,16,2560]{3,2,1,0:T(8,128)(2,1)}, u32[]{:S(2)}, u32[]{:S(2)}) collective-permute-start(bf16[4,2,16,2560]{3,2,1,0:T(8,128)(2,1)S(1)} %collective-permute-done.7), channel_id=1, source_target_pairs={{0,32},{4,36},{8,40},{12,44},{16,48},{20,52},{24,56},{28,60},{32,6... | collective-permute-start | bytes 1966088 | tf_op jit(solution)/shard_map/ppermute | solution.py:170
  243.6 4.2 collective-permute-start.27
  248.0 14.9 %collective-permute-start.28 = (bf16[128,2048]{1,0:T(8,128)(2,1)S(1)}, bf16[128,2048]{1,0:T(8,128)(2,1)}, u32[]{:S(2)}, u32[]{:S(2)}) collective-permute-start(bf16[128,2048]{1,0:T(8,128)(2,1)S(1)} %fusion.95), channel_id=1, source_target_pairs={{0,2},{2,0},{1,3},{3,1},{4,6},{6,4},{5,7},{7,5},{8,10},{10,8},{9,1... | collective-permute-start | bytes 1572872 | tf_op jit(solution)/shard_map/ppermute | solution.py:119
  249.9 24.3 %collective-permute-start.33 = (bf16[128,2048]{1,0:T(8,128)(2,1)S(1)}, bf16[128,2048]{1,0:T(8,128)(2,1)}, u32[]{:S(2)}, u32[]{:S(2)}) collective-permute-start(bf16[128,2048]{1,0:T(8,128)(2,1)S(1)} %bitcast.377), channel_id=1, source_target_pairs={{0,2},{2,0},{1,3},{3,1},{4,6},{6,4},{5,7},{7,5},{8,10},{10,8},{9,1... | collective-permute-start | bytes 1572872 | tf_op jit(solution)/shard_map/ppermute | solution.py:108
  265.2 19.4 %collective-permute-start.29 = (bf16[128,2048]{1,0:T(8,128)(2,1)S(1)}, bf16[128,2048]{1,0:T(8,128)(2,1)S(1)}, u32[]{:S(2)}, u32[]{:S(2)}) collective-permute-start(bf16[128,2048]{1,0:T(8,128)(2,1)S(1)} %multiply_convert_fusion.4), channel_id=1, source_target_pairs={{0,2},{2,0},{1,3},{3,1},{4,6},{6,4},{5,7},{7,5},{8,10},{10,8},{9,1... | collective-permute-start | bytes 1572872 | tf_op jit(solution)/shard_map/ppermute | solution.py:108
  275.4 9.4 %collective-permute-start.34 = (bf16[2,128,2048]{2,1,0:T(8,128)(2,1)S(1)}, bf16[2,128,2048]{2,1,0:T(8,128)(2,1)S(1)}, u32[]{:S(2)}, u32[]{:S(2)}) collective-permute-start(bf16[2,128,2048]{2,1,0:T(8,128)(2,1)S(1)} %pad_maximum_fusion.12), channel_id=1, source_target_pairs={{0,1},{1,0},{2,3},{3,2},{4,5},{5,4},{6,7},{7,6},{8,9},{9,8},{10,11... | collective-permute-start | bytes 3145736 | tf_op jit(solution)/shard_map/ppermute | solution.py:110
  284.7 2.7 collective-permute-start.30
  342.3 7.4 %collective-permute-start.35 = (f32[2,128,2048]{2,1,0:T(8,128)S(1)}, f32[2,128,2048]{2,1,0:T(8,128)S(1)}, u32[]{:S(2)}, u32[]{:S(2)}) collective-permute-start(f32[2,128,2048]{2,1,0:T(8,128)S(1)} %bitcast.395), channel_id=1, source_target_pairs={{0,1},{1,0},{2,3},{3,2},{4,5},{5,4},{6,7},{7,6},{8,9},{9,8},{10,11... | collective-permute-start | bytes 6291464 | tf_op jit(solution)/shard_map/ppermute | solution.py:116
  349.1 4.3 collective-permute-start.31
  349.8 19.1 %collective-permute-start.36 = (bf16[128,2048]{1,0:T(8,128)(2,1)S(1)}, bf16[128,2048]{1,0:T(8,128)(2,1)S(1)}, u32[]{:S(2)}, u32[]{:S(2)}) collective-permute-start(bf16[128,2048]{1,0:T(8,128)(2,1)S(1)} %fusion.85), channel_id=1, source_target_pairs={{0,2},{2,0},{1,3},{3,1},{4,6},{6,4},{5,7},{7,5},{8,10},{10,8},{9,1... | collective-permute-start | bytes 1572872 | tf_op jit(solution)/shard_map/ppermute | solution.py:119
  353.6 29.5 %collective-permute-start.32 = (bf16[128,2048]{1,0:T(8,128)(2,1)S(1)}, bf16[128,2048]{1,0:T(8,128)(2,1)S(1)}, u32[]{:S(2)}, u32[]{:S(2)}) collective-permute-start(bf16[128,2048]{1,0:T(8,128)(2,1)S(1)} %fusion.89), channel_id=1, source_target_pairs={{0,2},{2,0},{1,3},{3,1},{4,6},{6,4},{5,7},{7,5},{8,10},{10,8},{9,1... | collective-permute-start | bytes 1572872 | tf_op jit(solution)/shard_map/ppermute | solution.py:119
  384.8 17.7 %collective-permute-start.37 = (bf16[128,2048]{1,0:T(8,128)(2,1)S(1)}, bf16[128,2048]{1,0:T(8,128)(2,1)S(1)}, u32[]{:S(2)}, u32[]{:S(2)}) collective-permute-start(bf16[128,2048]{1,0:T(8,128)(2,1)S(1)} %get-tuple-element.27), channel_id=1, source_target_pairs={{0,2},{2,0},{1,3},{3,1},{4,6},{6,4},{5,7},{7,5},{8,10},{10,8},{9,1... | collective-permute-start | bytes 1572872 | tf_op jit(solution)/shard_map/ppermute | solution.py:108
  403.6 3.0 collective-permute-start.38
  466.3 33.0 %collective-permute-start.41 = (bf16[4,2,64,1280]{3,2,1,0:T(8,128)(2,1)S(1)}, bf16[4,2,64,1280]{3,2,1,0:T(8,128)(2,1)S(1)}, u32[]{:S(2)}, u32[]{:S(2)}) collective-permute-start(bf16[4,2,64,1280]{3,2,1,0:T(8,128)(2,1)S(1)} %dynamic-slice_bitcast_fusion.1), channel_id=1, source_target_pairs={{0,4},{4,8},{8,12},{12,0},{16,20},{20,24},{24,28},{28,16},{32,36},... | collective-permute-start | bytes 3932168 | tf_op jit(solution)/shard_map/ppermute | solution.py:148
  474.7 32.5 %collective-permute-start.47 = (bf16[4,2,64,1280]{3,2,1,0:T(8,128)(2,1)}, bf16[4,2,64,1280]{3,2,1,0:T(8,128)(2,1)}, u32[]{:S(2)}, u32[]{:S(2)}) collective-permute-start(bf16[4,2,64,1280]{3,2,1,0:T(8,128)(2,1)} %dynamic-slice_bitcast_fusion), channel_id=1, source_target_pairs={{0,12},{4,0},{8,4},{12,8},{16,28},{20,16},{24,20},{28,24},{32,44},... | collective-permute-start | bytes 3932168 | tf_op jit(solution)/shard_map/ppermute | solution.py:148
  486.0 51.2 %collective-permute-start.39 = (f32[2,128,2048]{2,1,0:T(8,128)}, f32[2,128,2048]{2,1,0:T(8,128)S(1)}, u32[]{:S(2)}, u32[]{:S(2)}) collective-permute-start(f32[2,128,2048]{2,1,0:T(8,128)} %bitcast.93), channel_id=1, source_target_pairs={{0,1},{1,0},{2,3},{3,2},{4,5},{5,4},{6,7},{7,6},{8,9},{9,8},{10,11... | collective-permute-start | bytes 6291464 | tf_op jit(solution)/shard_map/ppermute | solution.py:116
  502.0 32.1 %collective-permute-start.42 = (bf16[4,2,64,1280]{3,2,1,0:T(8,128)(2,1)}, bf16[4,2,64,1280]{3,2,1,0:T(8,128)(2,1)}, u32[]{:S(2)}, u32[]{:S(2)}) collective-permute-start(bf16[4,2,64,1280]{3,2,1,0:T(8,128)(2,1)} %fusion.19), channel_id=1, source_target_pairs={{0,4},{4,8},{8,12},{12,0},{16,20},{20,24},{24,28},{28,16},{32,36},... | collective-permute-start | bytes 3932168 | tf_op jit(solution)/shard_map/ppermute | solution.py:148
  510.2 31.6 %collective-permute-start.48 = (bf16[4,2,64,1280]{3,2,1,0:T(8,128)(2,1)}, bf16[4,2,64,1280]{3,2,1,0:T(8,128)(2,1)}, u32[]{:S(2)}, u32[]{:S(2)}) collective-permute-start(bf16[4,2,64,1280]{3,2,1,0:T(8,128)(2,1)} %fusion.16), channel_id=1, source_target_pairs={{0,12},{4,0},{8,4},{12,8},{16,28},{20,16},{24,20},{28,24},{32,44},... | collective-permute-start | bytes 3932168 | tf_op jit(solution)/shard_map/ppermute | solution.py:148
  537.2 44.7 %collective-permute-start.43 = (bf16[4,2,64,1280]{3,2,1,0:T(8,128)(2,1)}, bf16[4,2,64,1280]{3,2,1,0:T(8,128)(2,1)}, u32[]{:S(2)}, u32[]{:S(2)}) collective-permute-start(bf16[4,2,64,1280]{3,2,1,0:T(8,128)(2,1)} %fusion.20), channel_id=1, source_target_pairs={{0,4},{4,8},{8,12},{12,0},{16,20},{20,24},{24,28},{28,16},{32,36},... | collective-permute-start | bytes 3932168 | tf_op jit(solution)/shard_map/ppermute | solution.py:148
  538.7 12.7 %collective-permute-start.40 = (bf16[128,2048]{1,0:T(8,128)(2,1)S(1)}, bf16[128,2048]{1,0:T(8,128)(2,1)S(1)}, u32[]{:S(2)}, u32[]{:S(2)}) collective-permute-start(bf16[128,2048]{1,0:T(8,128)(2,1)S(1)} %fusion.81), channel_id=1, source_target_pairs={{0,2},{2,0},{1,3},{3,1},{4,6},{6,4},{5,7},{7,5},{8,10},{10,8},{9,1... | collective-permute-start | bytes 1572872 | tf_op jit(solution)/shard_map/ppermute | solution.py:119
  544.9 44.3 %collective-permute-start.49 = (bf16[4,2,64,1280]{3,2,1,0:T(8,128)(2,1)}, bf16[4,2,64,1280]{3,2,1,0:T(8,128)(2,1)}, u32[]{:S(2)}, u32[]{:S(2)}) collective-permute-start(bf16[4,2,64,1280]{3,2,1,0:T(8,128)(2,1)} %fusion.17), channel_id=1, source_target_pairs={{0,12},{4,0},{8,4},{12,8},{16,28},{20,16},{24,20},{28,24},{32,44},... | collective-permute-start | bytes 3932168 | tf_op jit(solution)/shard_map/ppermute | solution.py:148
  555.0 71.2 %all-to-all-start.1 = ((f32[128,3,16]{2,1,0:T(4,128)}), f32[128,3,16]{2,1,0:T(4,128)S(1)}, u32[]{:S(2)}, u32[]{:S(2)}) async-start(f32[128,3,16]{2,1,0:T(4,128)} %copy.133), calls=%async_computation.1 | async-start | bytes 524288 | tf_op jit(solution)/shard_map/all_to_all | solution.py:210
  584.0 15.9 %collective-permute-start.44 = (bf16[2,64,1280]{2,1,0:T(8,128)(2,1)S(1)}, bf16[2,64,1280]{2,1,0:T(8,128)(2,1)S(1)}, u32[]{:S(2)}, u32[]{:S(2)}) collective-permute-start(bf16[2,64,1280]{2,1,0:T(8,128)(2,1)S(1)} %dynamic-slice_bitcast_fusion.3), channel_id=1, source_target_pairs={{0,32},{4,36},{8,40},{12,44},{16,48},{20,52},{24,56},{28,60},{32,6... | collective-permute-start | bytes 983048 | tf_op jit(solution)/shard_map/ppermute | solution.py:148
  591.4 9.9 %collective-permute-start.50 = (bf16[2,64,1280]{2,1,0:T(8,128)(2,1)S(1)}, bf16[2,64,1280]{2,1,0:T(8,128)(2,1)S(1)}, u32[]{:S(2)}, u32[]{:S(2)}) collective-permute-start(bf16[2,64,1280]{2,1,0:T(8,128)(2,1)S(1)} %dynamic-slice_bitcast_fusion.2), channel_id=1, source_target_pairs={{0,96},{4,100},{8,104},{12,108},{16,112},{20,116},{24,120},{28,124... | collective-permute-start | bytes 983048 | tf_op jit(solution)/shard_map/ppermute | solution.py:148
  600.0 10.6 %collective-permute-start.45 = (bf16[2,64,1280]{2,1,0:T(8,128)(2,1)S(1)}, bf16[2,64,1280]{2,1,0:T(8,128)(2,1)S(1)}, u32[]{:S(2)}, u32[]{:S(2)}) collective-permute-start(bf16[2,64,1280]{2,1,0:T(8,128)(2,1)S(1)} %fusion.118), channel_id=1, source_target_pairs={{0,32},{4,36},{8,40},{12,44},{16,48},{20,52},{24,56},{28,60},{32,6... | collective-permute-start | bytes 983048 | tf_op jit(solution)/shard_map/ppermute | solution.py:148
  601.3 12.2 %collective-permute-start.51 = (bf16[2,64,1280]{2,1,0:T(8,128)(2,1)S(1)}, bf16[2,64,1280]{2,1,0:T(8,128)(2,1)S(1)}, u32[]{:S(2)}, u32[]{:S(2)}) collective-permute-start(bf16[2,64,1280]{2,1,0:T(8,128)(2,1)S(1)} %fusion.116), channel_id=1, source_target_pairs={{0,96},{4,100},{8,104},{12,108},{16,112},{20,116},{24,120},{28,124... | collective-permute-start | bytes 983048 | tf_op jit(solution)/shard_map/ppermute | solution.py:148
  610.7 10.8 %collective-permute-start.46 = (bf16[2,64,1280]{2,1,0:T(8,128)(2,1)S(1)}, bf16[2,64,1280]{2,1,0:T(8,128)(2,1)S(1)}, u32[]{:S(2)}, u32[]{:S(2)}) collective-permute-start(bf16[2,64,1280]{2,1,0:T(8,128)(2,1)S(1)} %fusion.119), channel_id=1, source_target_pairs={{0,32},{4,36},{8,40},{12,44},{16,48},{20,52},{24,56},{28,60},{32,6... | collective-permute-start | bytes 983048 | tf_op jit(solution)/shard_map/ppermute | solution.py:148
  613.7 8.8 %collective-permute-start.52 = (bf16[2,64,1280]{2,1,0:T(8,128)(2,1)S(1)}, bf16[2,64,1280]{2,1,0:T(8,128)(2,1)S(1)}, u32[]{:S(2)}, u32[]{:S(2)}) collective-permute-start(bf16[2,64,1280]{2,1,0:T(8,128)(2,1)S(1)} %fusion.117), channel_id=1, source_target_pairs={{0,96},{4,100},{8,104},{12,108},{16,112},{20,116},{24,120},{28,124... | collective-permute-start | bytes 983048 | tf_op jit(solution)/shard_map/ppermute | solution.py:148
  622.6 8.7 %collective-permute-start.53 = (bf16[64,2560]{1,0:T(8,128)(2,1)S(1)}, bf16[64,2560]{1,0:T(8,128)(2,1)S(1)}, u32[]{:S(2)}, u32[]{:S(2)}) collective-permute-start(bf16[64,2560]{1,0:T(8,128)(2,1)S(1)} %fusion.132), channel_id=1, source_target_pairs={{0,16},{4,20},{8,24},{12,28},{16,0},{20,4},{24,8},{28,12},{32,48},... | collective-permute-start | bytes 983048 | tf_op jit(solution)/shard_map/ppermute | solution.py:163
  (48 other events, 312.9 us)
Sparse Core Ops, SparseCore 0:
  11.1 177.6 all-gather.1
  330.6 293.0 reduce-scatter.1

commit v13 on v10

--- a/solution.py
+++ b/solution.py
@@ -161,6 +161,52 @@
     give = lax.dynamic_index_in_dim(along_z, 1 - y_pos, 0, keepdims=False)
     pair = [(i, i ^ 4) for i in range(32)]
     return keep + lax.ppermute(give.astype(jnp.bfloat16), "dp", pair).astype(jnp.float32)
+
+
+def ring_gather(values):
+    index = lax.axis_index("dp")
+    x_pos, y_pos, z_pos = index % 4, (index // 4) % 2, index // 8
+    zero = jnp.zeros((), jnp.int32)
+    pair = [(i, i ^ 4) for i in range(32)]
+    other = lax.ppermute(values, "dp", pair)
+    both = jnp.zeros((2,) + values.shape, values.dtype)
+    both = lax.dynamic_update_slice(both, values[None], (y_pos, zero, zero))
+    both = lax.dynamic_update_slice(both, other[None], (1 - y_pos, zero, zero))
+    part_rows = values.shape[0] // 4
+    cols = values.shape[1]
+    full = jnp.zeros((4, 2, 4) + values.shape, values.dtype)
+    for part, (x_first, step) in enumerate(((True, 1), (True, 3), (False, 1), (False, 3))):
+        rows = both[:, part * part_rows : (part + 1) * part_rows]
+        row_at = jnp.full((), part * part_rows, jnp.int32)
+        if x_first:
+            pairs = ring_pairs(step, 1, 4)
+            first = jnp.zeros((2, 4, part_rows, cols), values.dtype)
+            cur = rows
+            first = lax.dynamic_update_slice(first, cur[:, None], (zero, x_pos, zero, zero))
+            for k in range(1, 4):
+                cur = lax.ppermute(cur, "dp", pairs)
+                first = lax.dynamic_update_slice(first, cur[:, None], (zero, (x_pos - k * step) % 4, zero, zero))
+            pairs = ring_pairs(step, 8, 4)
+            cur = first
+            full = lax.dynamic_update_slice(full, cur[None], (z_pos, zero, zero, row_at, zero))
+            for k in range(1, 4):
+                cur = lax.ppermute(cur, "dp", pairs)
+                full = lax.dynamic_update_slice(full, cur[None], ((z_pos - k * step) % 4, zero, zero, row_at, zero))
+        else:
+            pairs = ring_pairs(step, 8, 4)
+            first = jnp.zeros((4, 2, part_rows, cols), values.dtype)
+            cur = rows
+            first = lax.dynamic_update_slice(first, cur[None], (z_pos, zero, zero, zero))
+            for k in range(1, 4):
+                cur = lax.ppermute(cur, "dp", pairs)
+                first = lax.dynamic_update_slice(first, cur[None], ((z_pos - k * step) % 4, zero, zero, zero))
+            pairs = ring_pairs(step, 1, 4)
+            cur = first
+            full = lax.dynamic_update_slice(full, cur[:, :, None], (zero, zero, x_pos, row_at, zero))
+            for k in range(1, 4):
+                cur = lax.ppermute(cur, "dp", pairs)
+                full = lax.dynamic_update_slice(full, cur[:, :, None], (zero, zero, (x_pos - k * step) % 4, row_at, zero))
+    return full.reshape((-1, cols))
 
 
 def small_gather(vectors):
@@ -210,7 +256,7 @@
     cot_local = cotangent[0].reshape(-1, model_width)
     attn_pack = jnp.concatenate([w_query, w_forget, w_value, w_outgate, w_output.T], axis=1)
     mlp_pack = jnp.concatenate([w_gate, w_up, w_down.T], axis=1)
-    attn_all = lax.all_gather(attn_pack, "dp", axis=0, tiled=True)
+    attn_all = ring_gather(attn_pack)
     mlp_all = lax.all_gather(mlp_pack, "dp", axis=0, tiled=True)
     wq_all = attn_all[:, 0 * local_width : 1 * local_width]
     wf_all = attn_all[:, 1 * local_width : 2 * local_width]

time: 659 us -> 612 us (0.929)
  waiting for transfers between devices: 355 us -> 233 us
  starting transfers between devices: 51 us -> 111 us
  local copies, waits for them, and re-layouts: 70 us -> 84 us
    all_gather x1, waiting for transfers between devices: 73.2 us -> 0.01 us  [shards(): mlp_all = lax.all_gather(mlp_pack, 'dp', axis=0, tiled=True)]
    all_gather x1 -> x0, waiting for transfers between devices: 72.5 us -> none  [shards(): attn_all = lax.all_gather(attn_pack, 'dp', axis=0, tiled=True)]
    ppermute x0 -> x25, waiting for transfers between devices: none -> 56.2 us  [the longest x24 56.2 us: ring_gather(): cur = lax.ppermute(cur, 'dp', pairs)]
    ppermute x0 -> x25, starting transfers between devices: none -> 43 us  [the longest x24 39.7 us: ring_gather(): cur = lax.ppermute(cur, 'dp', pairs)]
    ppermute x4, waiting for transfers between devices: 56.6 us -> 32.8 us  [row_gather(): across = lax.ppermute(values, 'tensor', ACROSS)]
    ppermute x4, starting transfers between devices: 5.22 us -> 20.1 us  [row_sum(): lax.ppermute(theirs.astype(jnp.bfloat16), 'tensor', ACROSS)]
    dynamic_update_slice x0 -> x34, local copies, waits for them, and re-layouts: none -> 13 us  [the longest x6 2.5 us: ring_gather(): lax.dynamic_update_slice(full, cur[:, :, None], (zero, zero, (x_pos - k *...]
    unnamed x99 -> x85, local copies, waits for them, and re-layouts: 14.7 us -> 13.9 us
  transfers between devices with their start and end apart: 34 -> 58, of which waited for: 25 -> 30; matrix products, arithmetic and copies ran while one was open for 26% -> 30% of each run, Pallas kernels for 2% -> 2%
where the time goes in v13:
time: 612 us; the launch traced here: 606 us
  waiting for transfers between devices  233 us (38%)
  starting transfers between devices  111 us (18%)
  matrix products  89.4 us (15%)
  local copies, waits for them, and re-layouts  84 us (14%)
  other arithmetic  47.1 us (8%)
  Pallas kernels  26.5 us (4%)
  between operations  15.7 us (3%)
    ppermute x12, waiting for transfers between devices, ring_stage(): got = lax.ppermute(acc.astype(jnp.bfloat16), 'dp', pairs)  81.8 us
    ppermute x24, waiting for transfers between devices, ring_gather(): cur = lax.ppermute(cur, 'dp', pairs)  56.2 us
    ppermute x4, waiting for transfers between devices, row_sum(): lax.ppermute(theirs.astype(jnp.bfloat16), 'tensor', ACROSS)  43.2 us
    ppermute x24, starting transfers between devices, ring_gather(): cur = lax.ppermute(cur, 'dp', pairs)  39.7 us
    dot_general x8, matrix products, matmul_plain(): return jnp.dot(left, right, preferred_element_type=jnp.float32)  39.2 us
    ppermute x4, waiting for transfers between devices, row_gather(): across = lax.ppermute(values, 'tensor', ACROSS)  32.8 us
    dot_general x8, matrix products, times_trans(): lax.dot_general(left, right, (((1,), (1,)), ((), ())), preferred_element_...  31.9 us
    pallas_call x2, Pallas kernels, grad_pack(): pl.pallas_call(functools.partial(pack_kernel, per), grid=(rows_out // til...  26.5 us
  transfers between devices with their start and end apart: 58, of which 30 were waited for; matrix products, arithmetic and copies ran while one was open for 30% of the time, Pallas kernels for 2%

profile of v13, /device:TPU:0, one launch (start us, length us, event | category | flops | bytes accessed | tf_op | source)
XLA Modules:
  0.0 606.2 jit_solution(2487148376831124449)
XLA Ops:
  11.5 3.3 collective-permute-start.2
  16.2 8.9 %all-to-all-start = ((f32[128,3,16]{2,1,0:T(4,128)}), f32[128,3,16]{2,1,0:T(4,128)S(1)}, u32[]{:S(2)}, u32[]{:S(2)}) async-start(f32[128,3,16]{2,1,0:T(4,128)} %broadcast_in_dim.155), calls=%async_computation | async-start | bytes 524288 | tf_op jit(solution)/shard_map/all_to_all | solution.py:215
  29.3 6.6 %all-to-all-done = f32[128,3,16]{2,1,0:T(4,128)S(1)} async-done(((f32[128,3,16]{2,1,0:T(4,128)}), f32[128,3,16]{2,1,0:T(4,128)S(1)}, u32[]{:S(2)}, u32[]{:S(2)}) %all-to-all-start) | async-done | bytes 24608 | tf_op jit(solution)/shard_map/all_to_all | solution.py:215
  48.5 3.2 collective-permute-start.10
  51.7 3.2 collective-permute-start.22
  57.7 3.2 collective-permute-start.11
  61.0 3.1 collective-permute-start.23
  66.3 3.2 collective-permute-start.12
  70.3 3.3 collective-permute-start.24
  74.8 15.0 %collective-permute-done.6 = bf16[2,4,16,2560]{3,2,1,0:T(8,128)(2,1)} collective-permute-done((bf16[2,4,16,2560]{3,2,1,0:T(8,128)(2,1)S(1)}, bf16[2,4,16,2560]{3,2,1,0:T(8,128)(2,1)}, u32[]{:S(2)}, u32[]{:S(2)}) %collective-permute-start.6) | collective-permute-done | bytes 655392 | tf_op jit(solution)/shard_map/ppermute | solution.py:193
  89.8 3.8 collective-permute-start.13
  93.6 9.1 %collective-permute-done.18 = bf16[4,2,16,2560]{3,2,1,0:T(8,128)(2,1)} collective-permute-done((bf16[4,2,16,2560]{3,2,1,0:T(8,128)(2,1)}, bf16[4,2,16,2560]{3,2,1,0:T(8,128)(2,1)}, u32[]{:S(2)}, u32[]{:S(2)}) %collective-permute-start.18) | collective-permute-done | bytes 655392 | tf_op jit(solution)/shard_map/ppermute | solution.py:207
  102.7 3.2 collective-permute-start.25
  110.0 3.2 collective-permute-start.14
  113.2 8.7 %collective-permute-done.19 = bf16[4,2,16,2560]{3,2,1,0:T(8,128)(2,1)S(1)} collective-permute-done((bf16[4,2,16,2560]{3,2,1,0:T(8,128)(2,1)}, bf16[4,2,16,2560]{3,2,1,0:T(8,128)(2,1)S(1)}, u32[]{:S(2)}, u32[]{:S(2)}) %collective-permute-start.19) | collective-permute-done | bytes 655392 | tf_op jit(solution)/shard_map/ppermute | solution.py:207
  121.9 3.2 collective-permute-start.26
  132.6 20.7 %collective-permute-done.20 = bf16[4,2,16,2560]{3,2,1,0:T(8,128)(2,1)S(1)} collective-permute-done((bf16[4,2,16,2560]{3,2,1,0:T(8,128)(2,1)S(1)}, bf16[4,2,16,2560]{3,2,1,0:T(8,128)(2,1)S(1)}, u32[]{:S(2)}, u32[]{:S(2)}) %collective-permute-start.20) | collective-permute-done | bytes 655392 | tf_op jit(solution)/shard_map/ppermute | solution.py:207
  154.8 3.1 slice_bitcast_fusion
  160.4 3.9 copy.148
  164.3 4.0 copy.150
  170.8 3.6 fusion.57
  189.2 5.2 fusion.75
  194.4 3.1 fusion.30
  197.9 4.1 collective-permute-done.27
  202.2 14.2 %collective-permute-start.28 = (bf16[128,2048]{1,0:T(8,128)(2,1)S(1)}, bf16[128,2048]{1,0:T(8,128)(2,1)}, u32[]{:S(2)}, u32[]{:S(2)}) collective-permute-start(bf16[128,2048]{1,0:T(8,128)(2,1)S(1)} %fusion.93), channel_id=1, source_target_pairs={{0,2},{2,0},{1,3},{3,1},{4,6},{6,4},{5,7},{7,5},{8,10},{10,8},{9,1... | collective-permute-start | bytes 1572872 | tf_op jit(solution)/shard_map/ppermute | solution.py:119
  217.1 12.8 %collective-permute-done.28 = bf16[128,2048]{1,0:T(8,128)(2,1)} collective-permute-done((bf16[128,2048]{1,0:T(8,128)(2,1)S(1)}, bf16[128,2048]{1,0:T(8,128)(2,1)}, u32[]{:S(2)}, u32[]{:S(2)}) %collective-permute-start.28) | collective-permute-done | bytes 524320 | tf_op jit(solution)/shard_map/ppermute | solution.py:119
  233.6 7.5 %collective-permute-done.33 = bf16[128,2048]{1,0:T(8,128)(2,1)} collective-permute-done((bf16[128,2048]{1,0:T(8,128)(2,1)S(1)}, bf16[128,2048]{1,0:T(8,128)(2,1)}, u32[]{:S(2)}, u32[]{:S(2)}) %collective-permute-start.33) | collective-permute-done | bytes 524320 | tf_op jit(solution)/shard_map/ppermute | solution.py:108
  242.5 8.9 %collective-permute-done.29 = bf16[128,2048]{1,0:T(8,128)(2,1)S(1)} collective-permute-done((bf16[128,2048]{1,0:T(8,128)(2,1)S(1)}, bf16[128,2048]{1,0:T(8,128)(2,1)S(1)}, u32[]{:S(2)}, u32[]{:S(2)}) %collective-permute-start.29) | collective-permute-done | bytes 524320 | tf_op jit(solution)/shard_map/ppermute | solution.py:108
  255.8 8.4 %fusion = f32[512,1408]{1,0:T(8,128)} fusion(bf16[512,2048]{1,0:T(8,128)(2,1)} %bitcast.438, bf16[2048,4224]{1,0:T(8,128)(2,1)} %all-gather.2.cloned.1.call-done), kind=kOutput, calls=%fused_computation.2 | convolution fusion | flops 2952790016 | bytes 10747904 | tf_op jit(solution)/shard_map/dot_general | solution.py:27
  265.7 5.0 fusion.6
  270.7 6.6 %multiply_convert_fusion.1 = (bf16[512,1408]{1,0:T(8,128)(2,1)S(1)}, bf16[512,1408]{1,0:T(8,128)(2,1)S(1)}, bf16[512,1408]{1,0:T(8,128)(2,1)S(1)}) fusion(f32[512,1408]{1,0:T(8,128)} %fusion, f32[512,1408]{1,0:T(8,128)} %fusion.6, bf16[512,2048]{1,0:T(8,128)(2,1)S(1)} %bitcast.442, bf16[2048,4224]{1,0:T(8,128)(2,1)S(1)} %copy-done.38), kind=kOutput, calls=%fused_computation.18 | convolution fusion | flops 2963603456 | bytes 17956864 | tf_op jit(solution)/shard_map/dot_general | solution.py:27
  281.5 15.7 %shard_map.247 = bf16[2048,4224]{1,0:T(8,128)(2,1)} custom-call(bf16[512,2048]{1,0:T(8,128)(2,1)} %bitcast.440, bf16[512,2048]{1,0:T(8,128)(2,1)} %bitcast.439, bf16[512,4224]{1,0:T(8,128)(2,1)} %pad_maximum_fusion.right_ref), custom_call_target="tpu_custom_call" | custom-call | flops 8858370048 | bytes 25821184 | tf_op jit(solution)/shard_map/pallas_call | solution.py:64
  297.2 6.0 fusion.4
  303.3 5.5 fusion.12
  310.2 5.5 fusion.2
  321.9 13.8 %collective-permute-done.36 = bf16[128,2048]{1,0:T(8,128)(2,1)S(1)} collective-permute-done((bf16[128,2048]{1,0:T(8,128)(2,1)S(1)}, bf16[128,2048]{1,0:T(8,128)(2,1)S(1)}, u32[]{:S(2)}, u32[]{:S(2)}) %collective-permute-start.36) | collective-permute-done | bytes 524320 | tf_op jit(solution)/shard_map/ppermute | solution.py:119
  336.2 13.7 %collective-permute-done.32 = bf16[128,2048]{1,0:T(8,128)(2,1)S(1)} collective-permute-done((bf16[128,2048]{1,0:T(8,128)(2,1)S(1)}, bf16[128,2048]{1,0:T(8,128)(2,1)S(1)}, u32[]{:S(2)}, u32[]{:S(2)}) %collective-permute-start.32) | collective-permute-done | bytes 524320 | tf_op jit(solution)/shard_map/ppermute | solution.py:119
  353.1 16.4 %collective-permute-done.37 = bf16[128,2048]{1,0:T(8,128)(2,1)S(1)} collective-permute-done((bf16[128,2048]{1,0:T(8,128)(2,1)S(1)}, bf16[128,2048]{1,0:T(8,128)(2,1)S(1)}, u32[]{:S(2)}, u32[]{:S(2)}) %collective-permute-start.37) | collective-permute-done | bytes 524320 | tf_op jit(solution)/shard_map/ppermute | solution.py:108
  372.6 4.6 fusion.135
  380.1 3.2 fusion.60
  384.6 3.3 convolution_select_fusion
  399.3 10.8 %shard_map.246 = bf16[2048,2560]{1,0:T(8,128)(2,1)} custom-call(bf16[512,2048]{1,0:T(8,128)(2,1)} %bitcast.435, bf16[512,2048]{1,0:T(8,128)(2,1)} %bitcast.437, bf16[512,2560]{1,0:T(8,128)(2,1)} %constant_dynamic-update-slice_fusion.4.right_ref), custom_call_target="tpu_custom_call" | custom-call | flops 5368709120 | bytes 17301504 | tf_op jit(solution)/shard_map/pallas_call | solution.py:64
  410.2 9.1 %copy.203 = bf16[4,2,4,64,2560]{4,3,1,0,2:T(8,128)(2,1)} copy(bf16[4,2,4,64,2560]{4,3,2,1,0:T(8,128)(2,1)} %bitcast.420) | data formatting | bytes 20971520 | tf_op jit(solution)/shard_map/reshape | solution.py:157
  419.2 9.5 %fusion.146 = (bf16[4,4,2,64,1280]{4,3,2,1,0:T(8,128)(2,1)}, bf16[4,4,2,64,1280]{4,3,2,1,0:T(8,128)(2,1)}) fusion(bf16[4,4,2,64,2560]{4,3,2,1,0:T(8,128)(2,1)} %bitcast.419), kind=kLoop, calls=%fused_computation.275 | loop fusion | bytes 20971520 | tf_op jit(solution)/shard_map/slice | solution.py:140
  438.5 3.2 collective-permute-start.47
  444.7 3.0 add_add_fusion
  449.3 13.0 %collective-permute-done.41 = bf16[4,2,64,1280]{3,2,1,0:T(8,128)(2,1)S(1)} collective-permute-done((bf16[4,2,64,1280]{3,2,1,0:T(8,128)(2,1)S(1)}, bf16[4,2,64,1280]{3,2,1,0:T(8,128)(2,1)S(1)}, u32[]{:S(2)}, u32[]{:S(2)}) %collective-permute-start.41) | collective-permute-done | bytes 1310752 | tf_op jit(solution)/shard_map/ppermute | solution.py:148
  465.4 4.8 collective-permute-done.47
  470.2 3.1 fusion.16
  473.3 3.7 collective-permute-start.48
  478.3 18.5 %collective-permute-done.42 = bf16[4,2,64,1280]{3,2,1,0:T(8,128)(2,1)} collective-permute-done((bf16[4,2,64,1280]{3,2,1,0:T(8,128)(2,1)}, bf16[4,2,64,1280]{3,2,1,0:T(8,128)(2,1)}, u32[]{:S(2)}, u32[]{:S(2)}) %collective-permute-start.42) | collective-permute-done | bytes 1310752 | tf_op jit(solution)/shard_map/ppermute | solution.py:148
  496.8 3.1 fusion.20
  504.5 3.1 fusion.17
  507.6 3.7 collective-permute-start.49
  517.9 8.0 %all-to-all-start.1 = ((f32[128,3,16]{2,1,0:T(4,128)}), f32[128,3,16]{2,1,0:T(4,128)S(1)}, u32[]{:S(2)}, u32[]{:S(2)}) async-start(f32[128,3,16]{2,1,0:T(4,128)} %copy.166), calls=%async_computation.1 | async-start | bytes 524288 | tf_op jit(solution)/shard_map/all_to_all | solution.py:222
  525.9 18.3 %collective-permute-done.43 = bf16[4,2,64,1280]{3,2,1,0:T(8,128)(2,1)} collective-permute-done((bf16[4,2,64,1280]{3,2,1,0:T(8,128)(2,1)}, bf16[4,2,64,1280]{3,2,1,0:T(8,128)(2,1)}, u32[]{:S(2)}, u32[]{:S(2)}) %collective-permute-start.43) | collective-permute-done | bytes 1310752 | tf_op jit(solution)/shard_map/ppermute | solution.py:148
  547.8 3.9 collective-permute-done.49
  556.2 4.8 collective-permute-done.44
  562.1 3.6 collective-permute-done.50
  571.1 5.1 collective-permute-done.51
  576.3 3.8 collective-permute-start.52
  580.0 4.1 collective-permute-done.46
  586.5 3.2 collective-permute-start.53
  591.7 3.4 collective-permute-done.53
  (302 shorter events, 160.1 us)
Async XLA Ops:
  7.2 20.3 %copy-start = (s32[1,4,128]{2,1,0:T(4,128)S(1)}, s32[1,4,128]{2,1,0:T(4,128)}, u32[]{:S(2)}) copy-start(s32[1,4,128]{2,1,0:T(4,128)} %param.16) | copy-start | bytes 6148
  7.2 20.3 %copy-start.37 = (s32[4]{0:T(128)S(1)}, s32[4]{0:T(128)}, u32[]{:S(2)}) copy-start(s32[4]{0:T(128)} %constant.282.clone) | copy-start | bytes 52
  7.2 20.1 %copy-start.4 = (bf16[1,1,128,2048]{3,2,1,0:T(8,128)(2,1)S(1)}, bf16[1,1,128,2048]{3,2,1,0:T(8,128)(2,1)}, u32[]{:S(2)}) copy-start(bf16[1,1,128,2048]{3,2,1,0:T(8,128)(2,1)} %param.15) | copy-start | bytes 1572868
  11.5 27.0 %collective-permute-start.2 = (bf16[64,2560]{1,0:T(8,128)(2,1)S(1)}, bf16[64,2560]{1,0:T(8,128)(2,1)S(1)}, u32[]{:S(2)}, u32[]{:S(2)}) collective-permute-start(bf16[64,2560]{1,0:T(8,128)(2,1)S(1)} %bitcast_dynamic-update-slice_fusion.37), channel_id=1, source_target_pairs={{0,16},{4,20},{8,24},{12,28},{16,0},{20,4},{24,8},{28,12},{32,48},... | collective-permute-start | bytes 983048 | tf_op jit(solution)/shard_map/ppermute | solution.py:171
  16.2 19.7 %all-to-all-start = ((f32[128,3,16]{2,1,0:T(4,128)}), f32[128,3,16]{2,1,0:T(4,128)S(1)}, u32[]{:S(2)}, u32[]{:S(2)}) async-start(f32[128,3,16]{2,1,0:T(4,128)} %broadcast_in_dim.155), calls=%async_computation | async-start | bytes 524288 | tf_op jit(solution)/shard_map/all_to_all | solution.py:215
  25.1 230.7 %all-gather.2.cloned.1.call-start = ((), (), s32[]{:S(2)}) async-start(), calls=%async_computation.3 | async-start | bytes 17842176 | tf_op jit(solution)/shard_map/all_gather | solution.py:260
  27.2 568.9 %reduce-scatter.2.cloned.1.call-start = ((), (), s32[]{:S(2)}) async-start(), calls=%async_computation.4 | async-start | bytes 17842176 | tf_op jit(solution)/shard_map/reduce_scatter | solution.py:306
  37.5 18.8 %collective-permute-start = (bf16[128,2048]{1,0:T(8,128)(2,1)}, bf16[128,2048]{1,0:T(8,128)(2,1)}, u32[]{:S(2)}, u32[]{:S(2)}) collective-permute-start(bf16[128,2048]{1,0:T(8,128)(2,1)} %fusion.63), channel_id=1, source_target_pairs={{0,2},{2,0},{1,3},{3,1},{4,6},{6,4},{5,7},{7,5},{8,10},{10,8},{9,1... | collective-permute-start | bytes 1572872 | tf_op jit(solution)/shard_map/ppermute | solution.py:108
  38.6 9.8 %collective-permute-start.3 = (bf16[2,16,2560]{2,1,0:T(8,128)(2,1)S(1)}, bf16[2,16,2560]{2,1,0:T(8,128)(2,1)S(1)}, u32[]{:S(2)}, u32[]{:S(2)}) collective-permute-start(bf16[2,16,2560]{2,1,0:T(8,128)(2,1)S(1)} %get-tuple-element.52), channel_id=1, source_target_pairs={{0,4},{4,8},{8,12},{12,0},{16,20},{20,24},{24,28},{28,16},{32,36},... | collective-permute-start | bytes 491528 | tf_op jit(solution)/shard_map/ppermute | solution.py:187
  39.3 9.2 %collective-permute-start.9 = (bf16[2,16,2560]{2,1,0:T(8,128)(2,1)S(1)}, bf16[2,16,2560]{2,1,0:T(8,128)(2,1)S(1)}, u32[]{:S(2)}, u32[]{:S(2)}) collective-permute-start(bf16[2,16,2560]{2,1,0:T(8,128)(2,1)S(1)} %get-tuple-element.51), channel_id=1, source_target_pairs={{0,12},{4,0},{8,4},{12,8},{16,28},{20,16},{24,20},{28,24},{32,44},... | collective-permute-start | bytes 491528 | tf_op jit(solution)/shard_map/ppermute | solution.py:187
  41.9 9.8 %collective-permute-start.15 = (bf16[2,16,2560]{2,1,0:T(8,128)(2,1)S(1)}, bf16[2,16,2560]{2,1,0:T(8,128)(2,1)S(1)}, u32[]{:S(2)}, u32[]{:S(2)}) collective-permute-start(bf16[2,16,2560]{2,1,0:T(8,128)(2,1)S(1)} %get-tuple-element.50), channel_id=1, source_target_pairs={{0,32},{4,36},{8,40},{12,44},{16,48},{20,52},{24,56},{28,60},{32,6... | collective-permute-start | bytes 491528 | tf_op jit(solution)/shard_map/ppermute | solution.py:201
  42.7 9.0 %collective-permute-start.21 = (bf16[2,16,2560]{2,1,0:T(8,128)(2,1)S(1)}, bf16[2,16,2560]{2,1,0:T(8,128)(2,1)S(1)}, u32[]{:S(2)}, u32[]{:S(2)}) collective-permute-start(bf16[2,16,2560]{2,1,0:T(8,128)(2,1)S(1)} %get-tuple-element.49), channel_id=1, source_target_pairs={{0,96},{4,100},{8,104},{12,108},{16,112},{20,116},{24,120},{28,124... | collective-permute-start | bytes 491528 | tf_op jit(solution)/shard_map/ppermute | solution.py:201
  48.4 9.2 %collective-permute-start.4 = (bf16[2,16,2560]{2,1,0:T(8,128)(2,1)S(1)}, bf16[2,16,2560]{2,1,0:T(8,128)(2,1)S(1)}, u32[]{:S(2)}, u32[]{:S(2)}) collective-permute-start(bf16[2,16,2560]{2,1,0:T(8,128)(2,1)S(1)} %collective-permute-done.3), channel_id=1, source_target_pairs={{0,4},{4,8},{8,12},{12,0},{16,20},{20,24},{24,28},{28,16},{32,36},... | collective-permute-start | bytes 491528 | tf_op jit(solution)/shard_map/ppermute | solution.py:187
  48.5 9.2 %collective-permute-start.10 = (bf16[2,16,2560]{2,1,0:T(8,128)(2,1)S(1)}, bf16[2,16,2560]{2,1,0:T(8,128)(2,1)S(1)}, u32[]{:S(2)}, u32[]{:S(2)}) collective-permute-start(bf16[2,16,2560]{2,1,0:T(8,128)(2,1)S(1)} %collective-permute-done.9), channel_id=1, source_target_pairs={{0,12},{4,0},{8,4},{12,8},{16,28},{20,16},{24,20},{28,24},{32,44},... | collective-permute-start | bytes 491528 | tf_op jit(solution)/shard_map/ppermute | solution.py:187
  51.7 9.2 %collective-permute-start.16 = (bf16[2,16,2560]{2,1,0:T(8,128)(2,1)S(1)}, bf16[2,16,2560]{2,1,0:T(8,128)(2,1)S(1)}, u32[]{:S(2)}, u32[]{:S(2)}) collective-permute-start(bf16[2,16,2560]{2,1,0:T(8,128)(2,1)S(1)} %collective-permute-done.15), channel_id=1, source_target_pairs={{0,32},{4,36},{8,40},{12,44},{16,48},{20,52},{24,56},{28,60},{32,6... | collective-permute-start | bytes 491528 | tf_op jit(solution)/shard_map/ppermute | solution.py:201
  51.7 9.3 %collective-permute-start.22 = (bf16[2,16,2560]{2,1,0:T(8,128)(2,1)S(1)}, bf16[2,16,2560]{2,1,0:T(8,128)(2,1)S(1)}, u32[]{:S(2)}, u32[]{:S(2)}) collective-permute-start(bf16[2,16,2560]{2,1,0:T(8,128)(2,1)S(1)} %collective-permute-done.21), channel_id=1, source_target_pairs={{0,96},{4,100},{8,104},{12,108},{16,112},{20,116},{24,120},{28,124... | collective-permute-start | bytes 491528 | tf_op jit(solution)/shard_map/ppermute | solution.py:201
  57.5 49.6 %collective-permute-start.1 = (bf16[2,128,2048]{2,1,0:T(8,128)(2,1)S(1)}, bf16[2,128,2048]{2,1,0:T(8,128)(2,1)}, u32[]{:S(2)}, u32[]{:S(2)}) collective-permute-start(bf16[2,128,2048]{2,1,0:T(8,128)(2,1)S(1)} %pad_maximum_fusion.5), channel_id=1, source_target_pairs={{0,1},{1,0},{2,3},{3,2},{4,5},{5,4},{6,7},{7,6},{8,9},{9,8},{10,11... | collective-permute-start | bytes 3145736 | tf_op jit(solution)/shard_map/ppermute | solution.py:110
  57.6 8.0 %collective-permute-start.5 = (bf16[2,16,2560]{2,1,0:T(8,128)(2,1)S(1)}, bf16[2,16,2560]{2,1,0:T(8,128)(2,1)S(1)}, u32[]{:S(2)}, u32[]{:S(2)}) collective-permute-start(bf16[2,16,2560]{2,1,0:T(8,128)(2,1)S(1)} %collective-permute-done.4), channel_id=1, source_target_pairs={{0,4},{4,8},{8,12},{12,0},{16,20},{20,24},{24,28},{28,16},{32,36},... | collective-permute-start | bytes 491528 | tf_op jit(solution)/shard_map/ppermute | solution.py:187
  57.7 8.0 %collective-permute-start.11 = (bf16[2,16,2560]{2,1,0:T(8,128)(2,1)S(1)}, bf16[2,16,2560]{2,1,0:T(8,128)(2,1)S(1)}, u32[]{:S(2)}, u32[]{:S(2)}) collective-permute-start(bf16[2,16,2560]{2,1,0:T(8,128)(2,1)S(1)} %collective-permute-done.10), channel_id=1, source_target_pairs={{0,12},{4,0},{8,4},{12,8},{16,28},{20,16},{24,20},{28,24},{32,44},... | collective-permute-start | bytes 491528 | tf_op jit(solution)/shard_map/ppermute | solution.py:187
  60.9 8.7 %collective-permute-start.17 = (bf16[2,16,2560]{2,1,0:T(8,128)(2,1)S(1)}, bf16[2,16,2560]{2,1,0:T(8,128)(2,1)S(1)}, u32[]{:S(2)}, u32[]{:S(2)}) collective-permute-start(bf16[2,16,2560]{2,1,0:T(8,128)(2,1)S(1)} %collective-permute-done.16), channel_id=1, source_target_pairs={{0,32},{4,36},{8,40},{12,44},{16,48},{20,52},{24,56},{28,60},{32,6... | collective-permute-start | bytes 491528 | tf_op jit(solution)/shard_map/ppermute | solution.py:201
  61.0 9.2 %collective-permute-start.23 = (bf16[2,16,2560]{2,1,0:T(8,128)(2,1)S(1)}, bf16[2,16,2560]{2,1,0:T(8,128)(2,1)S(1)}, u32[]{:S(2)}, u32[]{:S(2)}) collective-permute-start(bf16[2,16,2560]{2,1,0:T(8,128)(2,1)S(1)} %collective-permute-done.22), channel_id=1, source_target_pairs={{0,96},{4,100},{8,104},{12,108},{16,112},{20,116},{24,120},{28,124... | collective-permute-start | bytes 491528 | tf_op jit(solution)/shard_map/ppermute | solution.py:201
  65.6 24.3 %collective-permute-start.6 = (bf16[2,4,16,2560]{3,2,1,0:T(8,128)(2,1)S(1)}, bf16[2,4,16,2560]{3,2,1,0:T(8,128)(2,1)}, u32[]{:S(2)}, u32[]{:S(2)}) collective-permute-start(bf16[2,4,16,2560]{3,2,1,0:T(8,128)(2,1)S(1)} %bitcast_dynamic-update-slice_fusion.25), channel_id=1, source_target_pairs={{0,32},{4,36},{8,40},{12,44},{16,48},{20,52},{24,56},{28,60},{32,6... | collective-permute-start | bytes 1966088 | tf_op jit(solution)/shard_map/ppermute | solution.py:193
  66.3 23.5 %collective-permute-start.12 = (bf16[2,4,16,2560]{3,2,1,0:T(8,128)(2,1)}, bf16[2,4,16,2560]{3,2,1,0:T(8,128)(2,1)}, u32[]{:S(2)}, u32[]{:S(2)}) collective-permute-start(bf16[2,4,16,2560]{3,2,1,0:T(8,128)(2,1)} %bitcast_dynamic-update-slice_fusion.21), channel_id=1, source_target_pairs={{0,96},{4,100},{8,104},{12,108},{16,112},{20,116},{24,120},{28,124... | collective-permute-start | bytes 1966088 | tf_op jit(solution)/shard_map/ppermute | solution.py:193
  70.2 32.5 %collective-permute-start.18 = (bf16[4,2,16,2560]{3,2,1,0:T(8,128)(2,1)}, bf16[4,2,16,2560]{3,2,1,0:T(8,128)(2,1)}, u32[]{:S(2)}, u32[]{:S(2)}) collective-permute-start(bf16[4,2,16,2560]{3,2,1,0:T(8,128)(2,1)} %bitcast_dynamic-update-slice_fusion.33), channel_id=1, source_target_pairs={{0,4},{4,8},{8,12},{12,0},{16,20},{20,24},{24,28},{28,16},{32,36},... | collective-permute-start | bytes 1966088 | tf_op jit(solution)/shard_map/ppermute | solution.py:207
  70.3 32.4 %collective-permute-start.24 = (bf16[4,2,16,2560]{3,2,1,0:T(8,128)(2,1)S(1)}, bf16[4,2,16,2560]{3,2,1,0:T(8,128)(2,1)}, u32[]{:S(2)}, u32[]{:S(2)}) collective-permute-start(bf16[4,2,16,2560]{3,2,1,0:T(8,128)(2,1)S(1)} %bitcast_dynamic-update-slice_fusion.29), channel_id=1, source_target_pairs={{0,12},{4,0},{8,4},{12,8},{16,28},{20,16},{24,20},{28,24},{32,44},... | collective-permute-start | bytes 1966088 | tf_op jit(solution)/shard_map/ppermute | solution.py:207
  89.8 20.1 %collective-permute-start.7 = (bf16[2,4,16,2560]{3,2,1,0:T(8,128)(2,1)}, bf16[2,4,16,2560]{3,2,1,0:T(8,128)(2,1)S(1)}, u32[]{:S(2)}, u32[]{:S(2)}) collective-permute-start(bf16[2,4,16,2560]{3,2,1,0:T(8,128)(2,1)} %collective-permute-done.6), channel_id=1, source_target_pairs={{0,32},{4,36},{8,40},{12,44},{16,48},{20,52},{24,56},{28,60},{32,6... | collective-permute-start | bytes 1966088 | tf_op jit(solution)/shard_map/ppermute | solution.py:193
  89.8 20.1 %collective-permute-start.13 = (bf16[2,4,16,2560]{3,2,1,0:T(8,128)(2,1)}, bf16[2,4,16,2560]{3,2,1,0:T(8,128)(2,1)S(1)}, u32[]{:S(2)}, u32[]{:S(2)}) collective-permute-start(bf16[2,4,16,2560]{3,2,1,0:T(8,128)(2,1)} %collective-permute-done.12), channel_id=1, source_target_pairs={{0,96},{4,100},{8,104},{12,108},{16,112},{20,116},{24,120},{28,124... | collective-permute-start | bytes 1966088 | tf_op jit(solution)/shard_map/ppermute | solution.py:193
  102.7 19.2 %collective-permute-start.19 = (bf16[4,2,16,2560]{3,2,1,0:T(8,128)(2,1)}, bf16[4,2,16,2560]{3,2,1,0:T(8,128)(2,1)S(1)}, u32[]{:S(2)}, u32[]{:S(2)}) collective-permute-start(bf16[4,2,16,2560]{3,2,1,0:T(8,128)(2,1)} %collective-permute-done.18), channel_id=1, source_target_pairs={{0,4},{4,8},{8,12},{12,0},{16,20},{20,24},{24,28},{28,16},{32,36},... | collective-permute-start | bytes 1966088 | tf_op jit(solution)/shard_map/ppermute | solution.py:207
  102.7 19.2 %collective-permute-start.25 = (bf16[4,2,16,2560]{3,2,1,0:T(8,128)(2,1)}, bf16[4,2,16,2560]{3,2,1,0:T(8,128)(2,1)S(1)}, u32[]{:S(2)}, u32[]{:S(2)}) collective-permute-start(bf16[4,2,16,2560]{3,2,1,0:T(8,128)(2,1)} %collective-permute-done.24), channel_id=1, source_target_pairs={{0,12},{4,0},{8,4},{12,8},{16,28},{20,16},{24,20},{28,24},{32,44},... | collective-permute-start | bytes 1966088 | tf_op jit(solution)/shard_map/ppermute | solution.py:207
  110.0 15.7 %collective-permute-start.8 = (bf16[2,4,16,2560]{3,2,1,0:T(8,128)(2,1)S(1)}, bf16[2,4,16,2560]{3,2,1,0:T(8,128)(2,1)S(1)}, u32[]{:S(2)}, u32[]{:S(2)}) collective-permute-start(bf16[2,4,16,2560]{3,2,1,0:T(8,128)(2,1)S(1)} %collective-permute-done.7), channel_id=1, source_target_pairs={{0,32},{4,36},{8,40},{12,44},{16,48},{20,52},{24,56},{28,60},{32,6... | collective-permute-start | bytes 1966088 | tf_op jit(solution)/shard_map/ppermute | solution.py:193
  110.0 20.2 %collective-permute-start.14 = (bf16[2,4,16,2560]{3,2,1,0:T(8,128)(2,1)S(1)}, bf16[2,4,16,2560]{3,2,1,0:T(8,128)(2,1)S(1)}, u32[]{:S(2)}, u32[]{:S(2)}) collective-permute-start(bf16[2,4,16,2560]{3,2,1,0:T(8,128)(2,1)S(1)} %collective-permute-done.13), channel_id=1, source_target_pairs={{0,96},{4,100},{8,104},{12,108},{16,112},{20,116},{24,120},{28,124... | collective-permute-start | bytes 1966088 | tf_op jit(solution)/shard_map/ppermute | solution.py:193
  121.9 31.4 %collective-permute-start.20 = (bf16[4,2,16,2560]{3,2,1,0:T(8,128)(2,1)S(1)}, bf16[4,2,16,2560]{3,2,1,0:T(8,128)(2,1)S(1)}, u32[]{:S(2)}, u32[]{:S(2)}) collective-permute-start(bf16[4,2,16,2560]{3,2,1,0:T(8,128)(2,1)S(1)} %collective-permute-done.19), channel_id=1, source_target_pairs={{0,4},{4,8},{8,12},{12,0},{16,20},{20,24},{24,28},{28,16},{32,36},... | collective-permute-start | bytes 1966088 | tf_op jit(solution)/shard_map/ppermute | solution.py:207
  121.9 32.8 %collective-permute-start.26 = (bf16[4,2,16,2560]{3,2,1,0:T(8,128)(2,1)S(1)}, bf16[4,2,16,2560]{3,2,1,0:T(8,128)(2,1)S(1)}, u32[]{:S(2)}, u32[]{:S(2)}) collective-permute-start(bf16[4,2,16,2560]{3,2,1,0:T(8,128)(2,1)S(1)} %collective-permute-done.25), channel_id=1, source_target_pairs={{0,12},{4,0},{8,4},{12,8},{16,28},{20,16},{24,20},{28,24},{32,44},... | collective-permute-start | bytes 1966088 | tf_op jit(solution)/shard_map/ppermute | solution.py:207
  197.5 18.9 %copy-start.9 = (bf16[1,1,128,2048]{3,2,1,0:T(8,128)(2,1)S(1)}, bf16[1,1,128,2048]{3,2,1,0:T(8,128)(2,1)}, u32[]{:S(2)}) copy-start(bf16[1,1,128,2048]{3,2,1,0:T(8,128)(2,1)} %param.28) | copy-start | bytes 1572868
  197.8 4.2 collective-permute-start.27
  202.2 27.7 %collective-permute-start.28 = (bf16[128,2048]{1,0:T(8,128)(2,1)S(1)}, bf16[128,2048]{1,0:T(8,128)(2,1)}, u32[]{:S(2)}, u32[]{:S(2)}) collective-permute-start(bf16[128,2048]{1,0:T(8,128)(2,1)S(1)} %fusion.93), channel_id=1, source_target_pairs={{0,2},{2,0},{1,3},{3,1},{4,6},{6,4},{5,7},{7,5},{8,10},{10,8},{9,1... | collective-permute-start | bytes 1572872 | tf_op jit(solution)/shard_map/ppermute | solution.py:119
  216.4 24.7 %collective-permute-start.33 = (bf16[128,2048]{1,0:T(8,128)(2,1)S(1)}, bf16[128,2048]{1,0:T(8,128)(2,1)}, u32[]{:S(2)}, u32[]{:S(2)}) collective-permute-start(bf16[128,2048]{1,0:T(8,128)(2,1)S(1)} %bitcast.427), channel_id=1, source_target_pairs={{0,2},{2,0},{1,3},{3,1},{4,6},{6,4},{5,7},{7,5},{8,10},{10,8},{9,1... | collective-permute-start | bytes 1572872 | tf_op jit(solution)/shard_map/ppermute | solution.py:108
  232.1 19.3 %collective-permute-start.29 = (bf16[128,2048]{1,0:T(8,128)(2,1)S(1)}, bf16[128,2048]{1,0:T(8,128)(2,1)S(1)}, u32[]{:S(2)}, u32[]{:S(2)}) collective-permute-start(bf16[128,2048]{1,0:T(8,128)(2,1)S(1)} %multiply_convert_fusion.4), channel_id=1, source_target_pairs={{0,2},{2,0},{1,3},{3,1},{4,6},{6,4},{5,7},{7,5},{8,10},{10,8},{9,1... | collective-permute-start | bytes 1572872 | tf_op jit(solution)/shard_map/ppermute | solution.py:108
  242.2 9.4 %collective-permute-start.34 = (bf16[2,128,2048]{2,1,0:T(8,128)(2,1)S(1)}, bf16[2,128,2048]{2,1,0:T(8,128)(2,1)S(1)}, u32[]{:S(2)}, u32[]{:S(2)}) collective-permute-start(bf16[2,128,2048]{2,1,0:T(8,128)(2,1)S(1)} %pad_maximum_fusion.7), channel_id=1, source_target_pairs={{0,1},{1,0},{2,3},{3,2},{4,5},{5,4},{6,7},{7,6},{8,9},{9,8},{10,11... | collective-permute-start | bytes 3145736 | tf_op jit(solution)/shard_map/ppermute | solution.py:110
  251.5 2.7 collective-permute-start.30
  309.1 7.4 %collective-permute-start.35 = (f32[2,128,2048]{2,1,0:T(8,128)S(1)}, f32[2,128,2048]{2,1,0:T(8,128)S(1)}, u32[]{:S(2)}, u32[]{:S(2)}) collective-permute-start(f32[2,128,2048]{2,1,0:T(8,128)S(1)} %bitcast.445), channel_id=1, source_target_pairs={{0,1},{1,0},{2,3},{3,2},{4,5},{5,4},{6,7},{7,6},{8,9},{9,8},{10,11... | collective-permute-start | bytes 6291464 | tf_op jit(solution)/shard_map/ppermute | solution.py:116
  315.9 4.4 collective-permute-start.31
  316.6 19.1 %collective-permute-start.36 = (bf16[128,2048]{1,0:T(8,128)(2,1)S(1)}, bf16[128,2048]{1,0:T(8,128)(2,1)S(1)}, u32[]{:S(2)}, u32[]{:S(2)}) collective-permute-start(bf16[128,2048]{1,0:T(8,128)(2,1)S(1)} %fusion.83), channel_id=1, source_target_pairs={{0,2},{2,0},{1,3},{3,1},{4,6},{6,4},{5,7},{7,5},{8,10},{10,8},{9,1... | collective-permute-start | bytes 1572872 | tf_op jit(solution)/shard_map/ppermute | solution.py:119
  320.4 29.5 %collective-permute-start.32 = (bf16[128,2048]{1,0:T(8,128)(2,1)S(1)}, bf16[128,2048]{1,0:T(8,128)(2,1)S(1)}, u32[]{:S(2)}, u32[]{:S(2)}) collective-permute-start(bf16[128,2048]{1,0:T(8,128)(2,1)S(1)} %fusion.87), channel_id=1, source_target_pairs={{0,2},{2,0},{1,3},{3,1},{4,6},{6,4},{5,7},{7,5},{8,10},{10,8},{9,1... | collective-permute-start | bytes 1572872 | tf_op jit(solution)/shard_map/ppermute | solution.py:119
  351.6 17.9 %collective-permute-start.37 = (bf16[128,2048]{1,0:T(8,128)(2,1)S(1)}, bf16[128,2048]{1,0:T(8,128)(2,1)S(1)}, u32[]{:S(2)}, u32[]{:S(2)}) collective-permute-start(bf16[128,2048]{1,0:T(8,128)(2,1)S(1)} %get-tuple-element.25), channel_id=1, source_target_pairs={{0,2},{2,0},{1,3},{3,1},{4,6},{6,4},{5,7},{7,5},{8,10},{10,8},{9,1... | collective-permute-start | bytes 1572872 | tf_op jit(solution)/shard_map/ppermute | solution.py:108
  369.6 2.7 collective-permute-start.38
  430.2 32.1 %collective-permute-start.41 = (bf16[4,2,64,1280]{3,2,1,0:T(8,128)(2,1)S(1)}, bf16[4,2,64,1280]{3,2,1,0:T(8,128)(2,1)S(1)}, u32[]{:S(2)}, u32[]{:S(2)}) collective-permute-start(bf16[4,2,64,1280]{3,2,1,0:T(8,128)(2,1)S(1)} %dynamic-slice_bitcast_fusion.1), channel_id=1, source_target_pairs={{0,4},{4,8},{8,12},{12,0},{16,20},{20,24},{24,28},{28,16},{32,36},... | collective-permute-start | bytes 3932168 | tf_op jit(solution)/shard_map/ppermute | solution.py:148
  438.5 31.6 %collective-permute-start.47 = (bf16[4,2,64,1280]{3,2,1,0:T(8,128)(2,1)}, bf16[4,2,64,1280]{3,2,1,0:T(8,128)(2,1)}, u32[]{:S(2)}, u32[]{:S(2)}) collective-permute-start(bf16[4,2,64,1280]{3,2,1,0:T(8,128)(2,1)} %dynamic-slice_bitcast_fusion), channel_id=1, source_target_pairs={{0,12},{4,0},{8,4},{12,8},{16,28},{20,16},{24,20},{28,24},{32,44},... | collective-permute-start | bytes 3932168 | tf_op jit(solution)/shard_map/ppermute | solution.py:148
  449.3 50.6 %collective-permute-start.39 = (f32[2,128,2048]{2,1,0:T(8,128)}, f32[2,128,2048]{2,1,0:T(8,128)S(1)}, u32[]{:S(2)}, u32[]{:S(2)}) collective-permute-start(f32[2,128,2048]{2,1,0:T(8,128)} %bitcast.105), channel_id=1, source_target_pairs={{0,1},{1,0},{2,3},{3,2},{4,5},{5,4},{6,7},{7,6},{8,9},{9,8},{10,11... | collective-permute-start | bytes 6291464 | tf_op jit(solution)/shard_map/ppermute | solution.py:116
  465.0 31.8 %collective-permute-start.42 = (bf16[4,2,64,1280]{3,2,1,0:T(8,128)(2,1)}, bf16[4,2,64,1280]{3,2,1,0:T(8,128)(2,1)}, u32[]{:S(2)}, u32[]{:S(2)}) collective-permute-start(bf16[4,2,64,1280]{3,2,1,0:T(8,128)(2,1)} %fusion.19), channel_id=1, source_target_pairs={{0,4},{4,8},{8,12},{12,0},{16,20},{20,24},{24,28},{28,16},{32,36},... | collective-permute-start | bytes 3932168 | tf_op jit(solution)/shard_map/ppermute | solution.py:148
  473.3 31.3 %collective-permute-start.48 = (bf16[4,2,64,1280]{3,2,1,0:T(8,128)(2,1)}, bf16[4,2,64,1280]{3,2,1,0:T(8,128)(2,1)}, u32[]{:S(2)}, u32[]{:S(2)}) collective-permute-start(bf16[4,2,64,1280]{3,2,1,0:T(8,128)(2,1)} %fusion.16), channel_id=1, source_target_pairs={{0,12},{4,0},{8,4},{12,8},{16,28},{20,16},{24,20},{28,24},{32,44},... | collective-permute-start | bytes 3932168 | tf_op jit(solution)/shard_map/ppermute | solution.py:148
  499.9 44.3 %collective-permute-start.43 = (bf16[4,2,64,1280]{3,2,1,0:T(8,128)(2,1)}, bf16[4,2,64,1280]{3,2,1,0:T(8,128)(2,1)}, u32[]{:S(2)}, u32[]{:S(2)}) collective-permute-start(bf16[4,2,64,1280]{3,2,1,0:T(8,128)(2,1)} %fusion.20), channel_id=1, source_target_pairs={{0,4},{4,8},{8,12},{12,0},{16,20},{20,24},{24,28},{28,16},{32,36},... | collective-permute-start | bytes 3932168 | tf_op jit(solution)/shard_map/ppermute | solution.py:148
  501.3 13.0 %collective-permute-start.40 = (bf16[128,2048]{1,0:T(8,128)(2,1)S(1)}, bf16[128,2048]{1,0:T(8,128)(2,1)S(1)}, u32[]{:S(2)}, u32[]{:S(2)}) collective-permute-start(bf16[128,2048]{1,0:T(8,128)(2,1)S(1)} %fusion.79), channel_id=1, source_target_pairs={{0,2},{2,0},{1,3},{3,1},{4,6},{6,4},{5,7},{7,5},{8,10},{10,8},{9,1... | collective-permute-start | bytes 1572872 | tf_op jit(solution)/shard_map/ppermute | solution.py:119
  507.6 44.0 %collective-permute-start.49 = (bf16[4,2,64,1280]{3,2,1,0:T(8,128)(2,1)}, bf16[4,2,64,1280]{3,2,1,0:T(8,128)(2,1)}, u32[]{:S(2)}, u32[]{:S(2)}) collective-permute-start(bf16[4,2,64,1280]{3,2,1,0:T(8,128)(2,1)} %fusion.17), channel_id=1, source_target_pairs={{0,12},{4,0},{8,4},{12,8},{16,28},{20,16},{24,20},{28,24},{32,44},... | collective-permute-start | bytes 3932168 | tf_op jit(solution)/shard_map/ppermute | solution.py:148
  517.9 73.2 %all-to-all-start.1 = ((f32[128,3,16]{2,1,0:T(4,128)}), f32[128,3,16]{2,1,0:T(4,128)S(1)}, u32[]{:S(2)}, u32[]{:S(2)}) async-start(f32[128,3,16]{2,1,0:T(4,128)} %copy.166), calls=%async_computation.1 | async-start | bytes 524288 | tf_op jit(solution)/shard_map/all_to_all | solution.py:222
  546.5 14.5 %collective-permute-start.44 = (bf16[2,64,1280]{2,1,0:T(8,128)(2,1)S(1)}, bf16[2,64,1280]{2,1,0:T(8,128)(2,1)S(1)}, u32[]{:S(2)}, u32[]{:S(2)}) collective-permute-start(bf16[2,64,1280]{2,1,0:T(8,128)(2,1)S(1)} %dynamic-slice_bitcast_fusion.3), channel_id=1, source_target_pairs={{0,32},{4,36},{8,40},{12,44},{16,48},{20,52},{24,56},{28,60},{32,6... | collective-permute-start | bytes 983048 | tf_op jit(solution)/shard_map/ppermute | solution.py:148
  553.7 12.0 %collective-permute-start.50 = (bf16[2,64,1280]{2,1,0:T(8,128)(2,1)S(1)}, bf16[2,64,1280]{2,1,0:T(8,128)(2,1)S(1)}, u32[]{:S(2)}, u32[]{:S(2)}) collective-permute-start(bf16[2,64,1280]{2,1,0:T(8,128)(2,1)S(1)} %dynamic-slice_bitcast_fusion.2), channel_id=1, source_target_pairs={{0,96},{4,100},{8,104},{12,108},{16,112},{20,116},{24,120},{28,124... | collective-permute-start | bytes 983048 | tf_op jit(solution)/shard_map/ppermute | solution.py:148
  561.1 9.8 %collective-permute-start.45 = (bf16[2,64,1280]{2,1,0:T(8,128)(2,1)S(1)}, bf16[2,64,1280]{2,1,0:T(8,128)(2,1)S(1)}, u32[]{:S(2)}, u32[]{:S(2)}) collective-permute-start(bf16[2,64,1280]{2,1,0:T(8,128)(2,1)S(1)} %fusion.116), channel_id=1, source_target_pairs={{0,32},{4,36},{8,40},{12,44},{16,48},{20,52},{24,56},{28,60},{32,6... | collective-permute-start | bytes 983048 | tf_op jit(solution)/shard_map/ppermute | solution.py:148
  565.8 10.4 %collective-permute-start.51 = (bf16[2,64,1280]{2,1,0:T(8,128)(2,1)S(1)}, bf16[2,64,1280]{2,1,0:T(8,128)(2,1)S(1)}, u32[]{:S(2)}, u32[]{:S(2)}) collective-permute-start(bf16[2,64,1280]{2,1,0:T(8,128)(2,1)S(1)} %fusion.114), channel_id=1, source_target_pairs={{0,96},{4,100},{8,104},{12,108},{16,112},{20,116},{24,120},{28,124... | collective-permute-start | bytes 983048 | tf_op jit(solution)/shard_map/ppermute | solution.py:148
  571.0 18.7 %copy-start.10 = (f32[128,2048]{1,0:T(8,128)S(1)}, f32[128,2048]{1,0:T(8,128)}, u32[]{:S(2)}) copy-start(f32[128,2048]{1,0:T(8,128)} %get-tuple-element.26) | copy-start | bytes 3145732
  571.0 18.7 %copy-start.12 = (f32[128,2048]{1,0:T(8,128)S(1)}, f32[128,2048]{1,0:T(8,128)}, u32[]{:S(2)}) copy-start(f32[128,2048]{1,0:T(8,128)} %get-tuple-element.24) | copy-start | bytes 3145732
  571.0 13.2 %collective-permute-start.46 = (bf16[2,64,1280]{2,1,0:T(8,128)(2,1)S(1)}, bf16[2,64,1280]{2,1,0:T(8,128)(2,1)S(1)}, u32[]{:S(2)}, u32[]{:S(2)}) collective-permute-start(bf16[2,64,1280]{2,1,0:T(8,128)(2,1)S(1)} %fusion.117), channel_id=1, source_target_pairs={{0,32},{4,36},{8,40},{12,44},{16,48},{20,52},{24,56},{28,60},{32,6... | collective-permute-start | bytes 983048 | tf_op jit(solution)/shard_map/ppermute | solution.py:148
  576.3 10.0 %collective-permute-start.52 = (bf16[2,64,1280]{2,1,0:T(8,128)(2,1)S(1)}, bf16[2,64,1280]{2,1,0:T(8,128)(2,1)S(1)}, u32[]{:S(2)}, u32[]{:S(2)}) collective-permute-start(bf16[2,64,1280]{2,1,0:T(8,128)(2,1)S(1)} %fusion.115), channel_id=1, source_target_pairs={{0,96},{4,100},{8,104},{12,108},{16,112},{20,116},{24,120},{28,124... | collective-permute-start | bytes 983048 | tf_op jit(solution)/shard_map/ppermute | solution.py:148
  586.5 8.7 %collective-permute-start.53 = (bf16[64,2560]{1,0:T(8,128)(2,1)S(1)}, bf16[64,2560]{1,0:T(8,128)(2,1)S(1)}, u32[]{:S(2)}, u32[]{:S(2)}) collective-permute-start(bf16[64,2560]{1,0:T(8,128)(2,1)S(1)} %fusion.130), channel_id=1, source_target_pairs={{0,16},{4,20},{8,24},{12,28},{16,0},{20,4},{24,8},{28,12},{32,48},... | collective-permute-start | bytes 983048 | tf_op jit(solution)/shard_map/ppermute | solution.py:163
  (33 other events, 194.7 us)
Sparse Core Ops, SparseCore 0:
  29.0 178.8 all-gather.1
  297.3 291.7 reduce-scatter.1

commit v14 on v13

--- a/solution.py
+++ b/solution.py
@@ -133,32 +133,39 @@
     return pairs
 
 
-def ring_stage(chunks, pos, stride, size):
-    half = chunks.shape[-1] // 2
-    result = []
-    for step, cols in ((1, slice(0, half)), (size - 1, slice(half, None))):
-        own = chunks[..., cols]
-        pairs = ring_pairs(step, stride, size)
-
-        def pick(k):
-            return lax.dynamic_index_in_dim(own, (pos - k * step) % size, 0, keepdims=False)
-
-        acc = pick(1).astype(jnp.float32)
-        for k in range(2, size + 1):
-            got = lax.ppermute(acc.astype(jnp.bfloat16), "dp", pairs)
-            acc = pick(k % size).astype(jnp.float32) + got.astype(jnp.float32)
-        result.append(acc)
-    return jnp.concatenate(result, axis=-1)
+def ring_stage(chunks, pos, stride, size, step):
+    pairs = ring_pairs(step, stride, size)
+
+    def pick(k):
+        return lax.dynamic_index_in_dim(chunks, (pos - k * step) % size, 0, keepdims=False).astype(
+            jnp.float32
+        )
+
+    acc = pick(1)
+    for k in range(2, size + 1):
+        got = lax.ppermute(acc.astype(jnp.bfloat16), "dp", pairs)
+        acc = pick(k % size) + got.astype(jnp.float32)
+    return acc
 
 
 def ring_sum(values):
     index = lax.axis_index("dp")
     x_pos, y_pos, z_pos = index % 4, (index // 4) % 2, index // 8
     blocks = values.reshape((4, 2, 4, -1) + values.shape[1:])
-    along_x = ring_stage(jnp.moveaxis(blocks, 2, 0), x_pos, 1, 4)
-    along_z = ring_stage(along_x.astype(jnp.bfloat16), z_pos, 8, 4)
-    keep = lax.dynamic_index_in_dim(along_z, y_pos, 0, keepdims=False)
-    give = lax.dynamic_index_in_dim(along_z, 1 - y_pos, 0, keepdims=False)
+    part_rows = blocks.shape[3] // 4
+    pieces = []
+    for part, (x_first, step) in enumerate(((True, 1), (True, 3), (False, 1), (False, 3))):
+        rows = blocks[:, :, :, part * part_rows : (part + 1) * part_rows]
+        if x_first:
+            once = ring_stage(jnp.moveaxis(rows, 2, 0), x_pos, 1, 4, step)
+            twice = ring_stage(once.astype(jnp.bfloat16), z_pos, 8, 4, step)
+        else:
+            once = ring_stage(rows, z_pos, 8, 4, step)
+            twice = ring_stage(jnp.moveaxis(once, 1, 0).astype(jnp.bfloat16), x_pos, 1, 4, step)
+        pieces.append(twice)
+    both = jnp.concatenate(pieces, axis=1)
+    keep = lax.dynamic_index_in_dim(both, y_pos, 0, keepdims=False)
+    give = lax.dynamic_index_in_dim(both, 1 - y_pos, 0, keepdims=False)
     pair = [(i, i ^ 4) for i in range(32)]
     return keep + lax.ppermute(give.astype(jnp.bfloat16), "dp", pair).astype(jnp.float32)
 

time: 612 us -> 613 us (level)
  waiting for transfers between devices: 233 us -> 257 us
  local copies, waits for them, and re-layouts: 84 us -> 73.2 us
  matrix products: 89.4 us -> 79 us
  other arithmetic: 47.1 us -> 39.4 us
    reduce_scatter x1, waiting for transfers between devices: 0.01 us -> 67.7 us  [shards(): lax.psum_scatter(mlp_grads, 'dp', scatter_dimension=0, tiled=True)]
    ppermute x12 -> x24, waiting for transfers between devices: 81.8 us -> 40.7 us  [ring_stage(): got = lax.ppermute(acc.astype(jnp.bfloat16), 'dp', pairs)]
    ppermute x12 -> x24, starting transfers between devices: 21.9 us -> 40.5 us  [ring_stage(): got = lax.ppermute(acc.astype(jnp.bfloat16), 'dp', pairs)]
    ppermute x4, starting transfers between devices: 20.1 us -> 4.99 us  [row_sum(): lax.ppermute(theirs.astype(jnp.bfloat16), 'tensor', ACROSS)]
    convert_element_type x8 -> x16, other arithmetic: 12.3 us -> 1.58 us  [ring_stage(): got = lax.ppermute(acc.astype(jnp.bfloat16), 'dp', pairs)]
    reshape x1 -> x0, local copies, waits for them, and re-layouts: 9.08 us -> none  [ring_sum(): blocks = values.reshape((4, 2, 4, -1) + values.shape[1:])]
    all_to_all x1, waiting for transfers between devices: 0.01 us -> 8.77 us  [small_sum(): lax.all_to_all(jnp.swapaxes(blocks, 0, 1), ('dp', 'tensor'), 0, 0, tiled=...]
    dot_general x8, matrix products: 31.9 us -> 24.8 us  [times_trans(): lax.dot_general(left, right, (((1,), (1,)), ((), ())), preferred_element_...]
  transfers between devices with their start and end apart: 58 -> 70, of which waited for: 30 -> 28; matrix products, arithmetic and copies ran while one was open for 30% -> 24% of each run, Pallas kernels for 2% -> 4%
where the time goes in v14:
time: 613 us; the launch traced here: 603 us
  waiting for transfers between devices  257 us (42%)
  starting transfers between devices  111 us (18%)
  matrix products  79 us (13%)
  local copies, waits for them, and re-layouts  73.2 us (12%)
  other arithmetic  39.4 us (6%)
  Pallas kernels  26.4 us (4%)
  between operations  16.2 us (3%)
    reduce_scatter x1, waiting for transfers between devices, shards(): lax.psum_scatter(mlp_grads, 'dp', scatter_dimension=0, tiled=True)  67.7 us
    ppermute x24, waiting for transfers between devices, ring_gather(): cur = lax.ppermute(cur, 'dp', pairs)  56.1 us
    ppermute x24, waiting for transfers between devices, ring_stage(): got = lax.ppermute(acc.astype(jnp.bfloat16), 'dp', pairs)  40.7 us
    ppermute x24, starting transfers between devices, ring_stage(): got = lax.ppermute(acc.astype(jnp.bfloat16), 'dp', pairs)  40.5 us
    ppermute x24, starting transfers between devices, ring_gather(): cur = lax.ppermute(cur, 'dp', pairs)  39.7 us
    ppermute x4, waiting for transfers between devices, row_sum(): lax.ppermute(theirs.astype(jnp.bfloat16), 'tensor', ACROSS)  39.4 us
    dot_general x8, matrix products, matmul_plain(): return jnp.dot(left, right, preferred_element_type=jnp.float32)  36.9 us
    ppermute x4, waiting for transfers between devices, row_gather(): across = lax.ppermute(values, 'tensor', ACROSS)  31.9 us
  transfers between devices with their start and end apart: 70, of which 28 were waited for; matrix products, arithmetic and copies ran while one was open for 24% of the time, Pallas kernels for 4%

profile of v14, /device:TPU:0, one launch (start us, length us, event | category | flops | bytes accessed | tf_op | source)
XLA Modules:
  0.0 602.7 jit_solution(1757260686449544045)
XLA Ops:
  11.5 3.3 collective-permute-start.2
  16.2 8.9 %all-to-all-start = ((f32[128,3,16]{2,1,0:T(4,128)}), f32[128,3,16]{2,1,0:T(4,128)S(1)}, u32[]{:S(2)}, u32[]{:S(2)}) async-start(f32[128,3,16]{2,1,0:T(4,128)} %broadcast_in_dim.155), calls=%async_computation | async-start | bytes 524288 | tf_op jit(solution)/shard_map/all_to_all | solution.py:222
  29.3 6.6 %all-to-all-done = f32[128,3,16]{2,1,0:T(4,128)S(1)} async-done(((f32[128,3,16]{2,1,0:T(4,128)}), f32[128,3,16]{2,1,0:T(4,128)S(1)}, u32[]{:S(2)}, u32[]{:S(2)}) %all-to-all-start) | async-done | bytes 24608 | tf_op jit(solution)/shard_map/all_to_all | solution.py:222
  48.5 3.2 collective-permute-start.10
  51.7 3.2 collective-permute-start.22
  57.7 3.2 collective-permute-start.11
  61.0 3.1 collective-permute-start.23
  66.4 3.2 collective-permute-start.12
  70.3 3.3 collective-permute-start.24
  74.8 15.1 %collective-permute-done.6 = bf16[2,4,16,2560]{3,2,1,0:T(8,128)(2,1)} collective-permute-done((bf16[2,4,16,2560]{3,2,1,0:T(8,128)(2,1)S(1)}, bf16[2,4,16,2560]{3,2,1,0:T(8,128)(2,1)}, u32[]{:S(2)}, u32[]{:S(2)}) %collective-permute-start.6) | collective-permute-done | bytes 655392 | tf_op jit(solution)/shard_map/ppermute | solution.py:200
  89.9 3.8 collective-permute-start.13
  93.7 9.0 %collective-permute-done.18 = bf16[4,2,16,2560]{3,2,1,0:T(8,128)(2,1)} collective-permute-done((bf16[4,2,16,2560]{3,2,1,0:T(8,128)(2,1)}, bf16[4,2,16,2560]{3,2,1,0:T(8,128)(2,1)}, u32[]{:S(2)}, u32[]{:S(2)}) %collective-permute-start.18) | collective-permute-done | bytes 655392 | tf_op jit(solution)/shard_map/ppermute | solution.py:214
  102.7 3.2 collective-permute-start.25
  107.1 2.9 pad_maximum_fusion.1
  110.1 3.2 collective-permute-start.14
  113.3 8.6 %collective-permute-done.19 = bf16[4,2,16,2560]{3,2,1,0:T(8,128)(2,1)S(1)} collective-permute-done((bf16[4,2,16,2560]{3,2,1,0:T(8,128)(2,1)}, bf16[4,2,16,2560]{3,2,1,0:T(8,128)(2,1)S(1)}, u32[]{:S(2)}, u32[]{:S(2)}) %collective-permute-start.19) | collective-permute-done | bytes 655392 | tf_op jit(solution)/shard_map/ppermute | solution.py:214
  121.9 3.2 collective-permute-start.26
  132.8 20.6 %collective-permute-done.20 = bf16[4,2,16,2560]{3,2,1,0:T(8,128)(2,1)S(1)} collective-permute-done((bf16[4,2,16,2560]{3,2,1,0:T(8,128)(2,1)S(1)}, bf16[4,2,16,2560]{3,2,1,0:T(8,128)(2,1)S(1)}, u32[]{:S(2)}, u32[]{:S(2)}) %collective-permute-start.20) | collective-permute-done | bytes 655392 | tf_op jit(solution)/shard_map/ppermute | solution.py:214
  154.8 3.1 slice_bitcast_fusion
  160.4 4.3 copy.157
  164.8 4.0 copy.159
  171.2 3.6 fusion.63
  175.8 2.7 fusion.18
  181.1 3.0 fusion.20
  188.3 5.8 fusion.81
  194.1 3.1 fusion.24
  197.5 4.1 collective-permute-done.27
  204.2 12.7 %collective-permute-done.28 = bf16[128,2048]{1,0:T(8,128)(2,1)} collective-permute-done((bf16[128,2048]{1,0:T(8,128)(2,1)S(1)}, bf16[128,2048]{1,0:T(8,128)(2,1)}, u32[]{:S(2)}, u32[]{:S(2)}) %collective-permute-start.28) | collective-permute-done | bytes 524320 | tf_op jit(solution)/shard_map/ppermute | solution.py:119
  220.4 7.8 %collective-permute-done.33 = bf16[128,2048]{1,0:T(8,128)(2,1)} collective-permute-done((bf16[128,2048]{1,0:T(8,128)(2,1)S(1)}, bf16[128,2048]{1,0:T(8,128)(2,1)}, u32[]{:S(2)}, u32[]{:S(2)}) %collective-permute-start.33) | collective-permute-done | bytes 524320 | tf_op jit(solution)/shard_map/ppermute | solution.py:108
  229.6 8.9 %collective-permute-done.29 = bf16[128,2048]{1,0:T(8,128)(2,1)S(1)} collective-permute-done((bf16[128,2048]{1,0:T(8,128)(2,1)S(1)}, bf16[128,2048]{1,0:T(8,128)(2,1)S(1)}, u32[]{:S(2)}, u32[]{:S(2)}) %collective-permute-start.29) | collective-permute-done | bytes 524320 | tf_op jit(solution)/shard_map/ppermute | solution.py:108
  242.9 6.6 %fusion = f32[512,1408]{1,0:T(8,128)S(1)} fusion(bf16[512,2048]{1,0:T(8,128)(2,1)} %bitcast.508, bf16[2048,4224]{1,0:T(8,128)(2,1)} %all-gather.2.cloned.1.call-done), kind=kOutput, calls=%fused_computation.1 | convolution fusion | flops 2952790016 | bytes 10747904 | tf_op jit(solution)/shard_map/dot_general | solution.py:27
  251.8 3.4 fusion.6
  255.2 7.2 %multiply_convert_fusion.1 = (bf16[512,1408]{1,0:T(8,128)(2,1)S(1)}, bf16[512,1408]{1,0:T(8,128)(2,1)S(1)}, bf16[512,1408]{1,0:T(8,128)(2,1)S(1)}) fusion(f32[512,1408]{1,0:T(8,128)S(1)} %fusion, f32[512,1408]{1,0:T(8,128)S(1)} %fusion.6, bf16[512,2048]{1,0:T(8,128)(2,1)S(1)} %bitcast.512, bf16[2048,4224]{1,0:T(8,128)(2,1)} %all-gather.2.cloned.1.call-done), kind=kOutput, calls=%fused_computation.17 | convolution fusion | flops 2963603456 | bytes 17956864 | tf_op jit(solution)/shard_map/dot_general | solution.py:27
  262.4 5.5 fusion.4
  267.9 5.5 fusion.12
  275.7 5.5 fusion.2
  287.0 15.7 %shard_map.247 = bf16[2048,4224]{1,0:T(8,128)(2,1)} custom-call(bf16[512,2048]{1,0:T(8,128)(2,1)} %bitcast.510, bf16[512,2048]{1,0:T(8,128)(2,1)} %bitcast.509, bf16[512,4224]{1,0:T(8,128)(2,1)} %pad_maximum_fusion.right_ref), custom_call_target="tpu_custom_call" | custom-call | flops 8858370048 | bytes 25821184 | tf_op jit(solution)/shard_map/pallas_call | solution.py:64
  308.2 14.8 %collective-permute-done.36 = bf16[128,2048]{1,0:T(8,128)(2,1)S(1)} collective-permute-done((bf16[128,2048]{1,0:T(8,128)(2,1)S(1)}, bf16[128,2048]{1,0:T(8,128)(2,1)S(1)}, u32[]{:S(2)}, u32[]{:S(2)}) %collective-permute-start.36) | collective-permute-done | bytes 524320 | tf_op jit(solution)/shard_map/ppermute | solution.py:119
  325.1 11.8 %collective-permute-done.32 = bf16[128,2048]{1,0:T(8,128)(2,1)S(1)} collective-permute-done((bf16[128,2048]{1,0:T(8,128)(2,1)S(1)}, bf16[128,2048]{1,0:T(8,128)(2,1)S(1)}, u32[]{:S(2)}, u32[]{:S(2)}) %collective-permute-start.32) | collective-permute-done | bytes 524320 | tf_op jit(solution)/shard_map/ppermute | solution.py:119
  336.9 3.3 fusion.148
  341.0 15.2 %collective-permute-done.37 = bf16[128,2048]{1,0:T(8,128)(2,1)S(1)} collective-permute-done((bf16[128,2048]{1,0:T(8,128)(2,1)S(1)}, bf16[128,2048]{1,0:T(8,128)(2,1)S(1)}, u32[]{:S(2)}, u32[]{:S(2)}) %collective-permute-start.37) | collective-permute-done | bytes 524320 | tf_op jit(solution)/shard_map/ppermute | solution.py:108
  361.2 4.6 fusion.140
  368.7 3.2 fusion.66
  373.3 3.3 convolution_select_fusion
  398.8 10.7 %shard_map.246 = bf16[2048,2560]{1,0:T(8,128)(2,1)} custom-call(bf16[512,2048]{1,0:T(8,128)(2,1)} %bitcast.505, bf16[512,2048]{1,0:T(8,128)(2,1)} %bitcast.507, bf16[512,2560]{1,0:T(8,128)(2,1)} %constant_dynamic-update-slice_fusion.4.right_ref), custom_call_target="tpu_custom_call" | custom-call | flops 5368709120 | bytes 17301504 | tf_op jit(solution)/shard_map/pallas_call | solution.py:64
  409.5 4.9 fusion.151
  414.9 3.4 collective-permute-start.59
  418.5 3.7 collective-permute-start.47
  422.3 12.4 %collective-permute-done.59 = bf16[2,4,16,2560]{3,2,0,1:T(8,128)(2,1)S(1)} collective-permute-done((bf16[2,4,16,2560]{3,2,0,1:T(8,128)(2,1)S(1)}, bf16[2,4,16,2560]{3,2,0,1:T(8,128)(2,1)S(1)}, u32[]{:S(2)}, u32[]{:S(2)}) %collective-permute-start.59) | collective-permute-done | bytes 655392 | tf_op jit(solution)/shard_map/ppermute | solution.py:146
  434.9 3.8 collective-permute-start.60
  439.2 3.1 collective-permute-start.48
  442.5 10.1 %collective-permute-done.60 = bf16[2,4,16,2560]{3,2,0,1:T(8,128)(2,1)S(1)} collective-permute-done((bf16[2,4,16,2560]{3,2,0,1:T(8,128)(2,1)S(1)}, bf16[2,4,16,2560]{3,2,0,1:T(8,128)(2,1)S(1)}, u32[]{:S(2)}, u32[]{:S(2)}) %collective-permute-start.60) | collective-permute-done | bytes 655392 | tf_op jit(solution)/shard_map/ppermute | solution.py:146
  452.7 3.8 collective-permute-start.61
  456.9 2.9 collective-permute-start.49
  460.0 9.3 %collective-permute-done.61 = bf16[2,4,16,2560]{3,2,0,1:T(8,128)(2,1)S(1)} collective-permute-done((bf16[2,4,16,2560]{3,2,0,1:T(8,128)(2,1)S(1)}, bf16[2,4,16,2560]{3,2,0,1:T(8,128)(2,1)S(1)}, u32[]{:S(2)}, u32[]{:S(2)}) %collective-permute-start.61) | collective-permute-done | bytes 655392 | tf_op jit(solution)/shard_map/ppermute | solution.py:146
  469.5 2.8 collective-permute-start.62
  479.1 3.0 collective-permute-start.63
  482.3 3.3 collective-permute-start.51
  485.9 3.8 collective-permute-start.64
  490.2 3.6 collective-permute-start.52
  496.7 3.9 collective-permute-done.46
  504.2 7.0 %all-to-all-start.1 = ((f32[128,3,16]{2,1,0:T(4,128)}), f32[128,3,16]{2,1,0:T(4,128)S(1)}, u32[]{:S(2)}, u32[]{:S(2)}) async-start(f32[128,3,16]{2,1,0:T(4,128)} %copy.175), calls=%async_computation.1 | async-start | bytes 524288 | tf_op jit(solution)/shard_map/all_to_all | solution.py:229
  513.1 8.8 %all-to-all-done.1 = f32[128,3,16]{2,1,0:T(4,128)S(1)} async-done(((f32[128,3,16]{2,1,0:T(4,128)}), f32[128,3,16]{2,1,0:T(4,128)S(1)}, u32[]{:S(2)}, u32[]{:S(2)}) %all-to-all-start.1) | async-done | bytes 24608 | tf_op jit(solution)/shard_map/all_to_all | solution.py:229
  524.6 67.7 %reduce-scatter.2.cloned.1.call-done = bf16[64,4224]{1,0:T(8,128)(2,1)} async-done(((bf16[2048,4224]{1,0:T(8,128)(2,1)}), bf16[64,4224]{1,0:T(8,128)(2,1)}) %reduce-scatter.2.cloned.1.call-update) | async-done | bytes 540688 | tf_op jit(solution)/shard_map/reduce_scatter | solution.py:313
  (354 shorter events, 138.2 us)
Async XLA Ops:
  11.5 27.0 %collective-permute-start.2 = (bf16[64,2560]{1,0:T(8,128)(2,1)S(1)}, bf16[64,2560]{1,0:T(8,128)(2,1)S(1)}, u32[]{:S(2)}, u32[]{:S(2)}) collective-permute-start(bf16[64,2560]{1,0:T(8,128)(2,1)S(1)} %bitcast_dynamic-update-slice_fusion.37), channel_id=1, source_target_pairs={{0,16},{4,20},{8,24},{12,28},{16,0},{20,4},{24,8},{28,12},{32,48},... | collective-permute-start | bytes 983048 | tf_op jit(solution)/shard_map/ppermute | solution.py:178
  16.2 19.7 %all-to-all-start = ((f32[128,3,16]{2,1,0:T(4,128)}), f32[128,3,16]{2,1,0:T(4,128)S(1)}, u32[]{:S(2)}, u32[]{:S(2)}) async-start(f32[128,3,16]{2,1,0:T(4,128)} %broadcast_in_dim.155), calls=%async_computation | async-start | bytes 524288 | tf_op jit(solution)/shard_map/all_to_all | solution.py:222
  25.1 217.7 %all-gather.2.cloned.1.call-start = ((), (), s32[]{:S(2)}) async-start(), calls=%async_computation.3 | async-start | bytes 17842176 | tf_op jit(solution)/shard_map/all_gather | solution.py:267
  27.2 565.2 %reduce-scatter.2.cloned.1.call-start = ((), (), s32[]{:S(2)}) async-start(), calls=%async_computation.4 | async-start | bytes 17842176 | tf_op jit(solution)/shard_map/reduce_scatter | solution.py:313
  37.5 18.9 %collective-permute-start = (bf16[128,2048]{1,0:T(8,128)(2,1)}, bf16[128,2048]{1,0:T(8,128)(2,1)}, u32[]{:S(2)}, u32[]{:S(2)}) collective-permute-start(bf16[128,2048]{1,0:T(8,128)(2,1)} %fusion.69), channel_id=1, source_target_pairs={{0,2},{2,0},{1,3},{3,1},{4,6},{6,4},{5,7},{7,5},{8,10},{10,8},{9,1... | collective-permute-start | bytes 1572872 | tf_op jit(solution)/shard_map/ppermute | solution.py:108
  38.6 9.8 %collective-permute-start.3 = (bf16[2,16,2560]{2,1,0:T(8,128)(2,1)S(1)}, bf16[2,16,2560]{2,1,0:T(8,128)(2,1)S(1)}, u32[]{:S(2)}, u32[]{:S(2)}) collective-permute-start(bf16[2,16,2560]{2,1,0:T(8,128)(2,1)S(1)} %get-tuple-element.62), channel_id=1, source_target_pairs={{0,4},{4,8},{8,12},{12,0},{16,20},{20,24},{24,28},{28,16},{32,36},... | collective-permute-start | bytes 491528 | tf_op jit(solution)/shard_map/ppermute | solution.py:194
  39.3 9.2 %collective-permute-start.9 = (bf16[2,16,2560]{2,1,0:T(8,128)(2,1)S(1)}, bf16[2,16,2560]{2,1,0:T(8,128)(2,1)S(1)}, u32[]{:S(2)}, u32[]{:S(2)}) collective-permute-start(bf16[2,16,2560]{2,1,0:T(8,128)(2,1)S(1)} %get-tuple-element.61), channel_id=1, source_target_pairs={{0,12},{4,0},{8,4},{12,8},{16,28},{20,16},{24,20},{28,24},{32,44},... | collective-permute-start | bytes 491528 | tf_op jit(solution)/shard_map/ppermute | solution.py:194
  41.9 9.9 %collective-permute-start.15 = (bf16[2,16,2560]{2,1,0:T(8,128)(2,1)S(1)}, bf16[2,16,2560]{2,1,0:T(8,128)(2,1)S(1)}, u32[]{:S(2)}, u32[]{:S(2)}) collective-permute-start(bf16[2,16,2560]{2,1,0:T(8,128)(2,1)S(1)} %get-tuple-element.60), channel_id=1, source_target_pairs={{0,32},{4,36},{8,40},{12,44},{16,48},{20,52},{24,56},{28,60},{32,6... | collective-permute-start | bytes 491528 | tf_op jit(solution)/shard_map/ppermute | solution.py:208
  42.7 9.0 %collective-permute-start.21 = (bf16[2,16,2560]{2,1,0:T(8,128)(2,1)S(1)}, bf16[2,16,2560]{2,1,0:T(8,128)(2,1)S(1)}, u32[]{:S(2)}, u32[]{:S(2)}) collective-permute-start(bf16[2,16,2560]{2,1,0:T(8,128)(2,1)S(1)} %get-tuple-element.59), channel_id=1, source_target_pairs={{0,96},{4,100},{8,104},{12,108},{16,112},{20,116},{24,120},{28,124... | collective-permute-start | bytes 491528 | tf_op jit(solution)/shard_map/ppermute | solution.py:208
  48.4 9.2 %collective-permute-start.4 = (bf16[2,16,2560]{2,1,0:T(8,128)(2,1)S(1)}, bf16[2,16,2560]{2,1,0:T(8,128)(2,1)S(1)}, u32[]{:S(2)}, u32[]{:S(2)}) collective-permute-start(bf16[2,16,2560]{2,1,0:T(8,128)(2,1)S(1)} %collective-permute-done.3), channel_id=1, source_target_pairs={{0,4},{4,8},{8,12},{12,0},{16,20},{20,24},{24,28},{28,16},{32,36},... | collective-permute-start | bytes 491528 | tf_op jit(solution)/shard_map/ppermute | solution.py:194
  48.5 9.2 %collective-permute-start.10 = (bf16[2,16,2560]{2,1,0:T(8,128)(2,1)S(1)}, bf16[2,16,2560]{2,1,0:T(8,128)(2,1)S(1)}, u32[]{:S(2)}, u32[]{:S(2)}) collective-permute-start(bf16[2,16,2560]{2,1,0:T(8,128)(2,1)S(1)} %collective-permute-done.9), channel_id=1, source_target_pairs={{0,12},{4,0},{8,4},{12,8},{16,28},{20,16},{24,20},{28,24},{32,44},... | collective-permute-start | bytes 491528 | tf_op jit(solution)/shard_map/ppermute | solution.py:194
  51.7 9.2 %collective-permute-start.16 = (bf16[2,16,2560]{2,1,0:T(8,128)(2,1)S(1)}, bf16[2,16,2560]{2,1,0:T(8,128)(2,1)S(1)}, u32[]{:S(2)}, u32[]{:S(2)}) collective-permute-start(bf16[2,16,2560]{2,1,0:T(8,128)(2,1)S(1)} %collective-permute-done.15), channel_id=1, source_target_pairs={{0,32},{4,36},{8,40},{12,44},{16,48},{20,52},{24,56},{28,60},{32,6... | collective-permute-start | bytes 491528 | tf_op jit(solution)/shard_map/ppermute | solution.py:208
  51.7 9.3 %collective-permute-start.22 = (bf16[2,16,2560]{2,1,0:T(8,128)(2,1)S(1)}, bf16[2,16,2560]{2,1,0:T(8,128)(2,1)S(1)}, u32[]{:S(2)}, u32[]{:S(2)}) collective-permute-start(bf16[2,16,2560]{2,1,0:T(8,128)(2,1)S(1)} %collective-permute-done.21), channel_id=1, source_target_pairs={{0,96},{4,100},{8,104},{12,108},{16,112},{20,116},{24,120},{28,124... | collective-permute-start | bytes 491528 | tf_op jit(solution)/shard_map/ppermute | solution.py:208
  57.5 49.6 %collective-permute-start.1 = (bf16[2,128,2048]{2,1,0:T(8,128)(2,1)S(1)}, bf16[2,128,2048]{2,1,0:T(8,128)(2,1)}, u32[]{:S(2)}, u32[]{:S(2)}) collective-permute-start(bf16[2,128,2048]{2,1,0:T(8,128)(2,1)S(1)} %pad_maximum_fusion.6), channel_id=1, source_target_pairs={{0,1},{1,0},{2,3},{3,2},{4,5},{5,4},{6,7},{7,6},{8,9},{9,8},{10,11... | collective-permute-start | bytes 3145736 | tf_op jit(solution)/shard_map/ppermute | solution.py:110
  57.6 7.9 %collective-permute-start.5 = (bf16[2,16,2560]{2,1,0:T(8,128)(2,1)S(1)}, bf16[2,16,2560]{2,1,0:T(8,128)(2,1)S(1)}, u32[]{:S(2)}, u32[]{:S(2)}) collective-permute-start(bf16[2,16,2560]{2,1,0:T(8,128)(2,1)S(1)} %collective-permute-done.4), channel_id=1, source_target_pairs={{0,4},{4,8},{8,12},{12,0},{16,20},{20,24},{24,28},{28,16},{32,36},... | collective-permute-start | bytes 491528 | tf_op jit(solution)/shard_map/ppermute | solution.py:194
  57.7 8.0 %collective-permute-start.11 = (bf16[2,16,2560]{2,1,0:T(8,128)(2,1)S(1)}, bf16[2,16,2560]{2,1,0:T(8,128)(2,1)S(1)}, u32[]{:S(2)}, u32[]{:S(2)}) collective-permute-start(bf16[2,16,2560]{2,1,0:T(8,128)(2,1)S(1)} %collective-permute-done.10), channel_id=1, source_target_pairs={{0,12},{4,0},{8,4},{12,8},{16,28},{20,16},{24,20},{28,24},{32,44},... | collective-permute-start | bytes 491528 | tf_op jit(solution)/shard_map/ppermute | solution.py:194
  60.9 8.7 %collective-permute-start.17 = (bf16[2,16,2560]{2,1,0:T(8,128)(2,1)S(1)}, bf16[2,16,2560]{2,1,0:T(8,128)(2,1)S(1)}, u32[]{:S(2)}, u32[]{:S(2)}) collective-permute-start(bf16[2,16,2560]{2,1,0:T(8,128)(2,1)S(1)} %collective-permute-done.16), channel_id=1, source_target_pairs={{0,32},{4,36},{8,40},{12,44},{16,48},{20,52},{24,56},{28,60},{32,6... | collective-permute-start | bytes 491528 | tf_op jit(solution)/shard_map/ppermute | solution.py:208
  61.0 9.2 %collective-permute-start.23 = (bf16[2,16,2560]{2,1,0:T(8,128)(2,1)S(1)}, bf16[2,16,2560]{2,1,0:T(8,128)(2,1)S(1)}, u32[]{:S(2)}, u32[]{:S(2)}) collective-permute-start(bf16[2,16,2560]{2,1,0:T(8,128)(2,1)S(1)} %collective-permute-done.22), channel_id=1, source_target_pairs={{0,96},{4,100},{8,104},{12,108},{16,112},{20,116},{24,120},{28,124... | collective-permute-start | bytes 491528 | tf_op jit(solution)/shard_map/ppermute | solution.py:208
  65.6 24.3 %collective-permute-start.6 = (bf16[2,4,16,2560]{3,2,1,0:T(8,128)(2,1)S(1)}, bf16[2,4,16,2560]{3,2,1,0:T(8,128)(2,1)}, u32[]{:S(2)}, u32[]{:S(2)}) collective-permute-start(bf16[2,4,16,2560]{3,2,1,0:T(8,128)(2,1)S(1)} %bitcast_dynamic-update-slice_fusion.25), channel_id=1, source_target_pairs={{0,32},{4,36},{8,40},{12,44},{16,48},{20,52},{24,56},{28,60},{32,6... | collective-permute-start | bytes 1966088 | tf_op jit(solution)/shard_map/ppermute | solution.py:200
  66.4 23.5 %collective-permute-start.12 = (bf16[2,4,16,2560]{3,2,1,0:T(8,128)(2,1)}, bf16[2,4,16,2560]{3,2,1,0:T(8,128)(2,1)}, u32[]{:S(2)}, u32[]{:S(2)}) collective-permute-start(bf16[2,4,16,2560]{3,2,1,0:T(8,128)(2,1)} %bitcast_dynamic-update-slice_fusion.21), channel_id=1, source_target_pairs={{0,96},{4,100},{8,104},{12,108},{16,112},{20,116},{24,120},{28,124... | collective-permute-start | bytes 1966088 | tf_op jit(solution)/shard_map/ppermute | solution.py:200
  70.3 32.5 %collective-permute-start.18 = (bf16[4,2,16,2560]{3,2,1,0:T(8,128)(2,1)}, bf16[4,2,16,2560]{3,2,1,0:T(8,128)(2,1)}, u32[]{:S(2)}, u32[]{:S(2)}) collective-permute-start(bf16[4,2,16,2560]{3,2,1,0:T(8,128)(2,1)} %bitcast_dynamic-update-slice_fusion.33), channel_id=1, source_target_pairs={{0,4},{4,8},{8,12},{12,0},{16,20},{20,24},{24,28},{28,16},{32,36},... | collective-permute-start | bytes 1966088 | tf_op jit(solution)/shard_map/ppermute | solution.py:214
  70.3 32.4 %collective-permute-start.24 = (bf16[4,2,16,2560]{3,2,1,0:T(8,128)(2,1)S(1)}, bf16[4,2,16,2560]{3,2,1,0:T(8,128)(2,1)}, u32[]{:S(2)}, u32[]{:S(2)}) collective-permute-start(bf16[4,2,16,2560]{3,2,1,0:T(8,128)(2,1)S(1)} %bitcast_dynamic-update-slice_fusion.29), channel_id=1, source_target_pairs={{0,12},{4,0},{8,4},{12,8},{16,28},{20,16},{24,20},{28,24},{32,44},... | collective-permute-start | bytes 1966088 | tf_op jit(solution)/shard_map/ppermute | solution.py:214
  89.9 20.2 %collective-permute-start.7 = (bf16[2,4,16,2560]{3,2,1,0:T(8,128)(2,1)}, bf16[2,4,16,2560]{3,2,1,0:T(8,128)(2,1)S(1)}, u32[]{:S(2)}, u32[]{:S(2)}) collective-permute-start(bf16[2,4,16,2560]{3,2,1,0:T(8,128)(2,1)} %collective-permute-done.6), channel_id=1, source_target_pairs={{0,32},{4,36},{8,40},{12,44},{16,48},{20,52},{24,56},{28,60},{32,6... | collective-permute-start | bytes 1966088 | tf_op jit(solution)/shard_map/ppermute | solution.py:200
  89.9 20.1 %collective-permute-start.13 = (bf16[2,4,16,2560]{3,2,1,0:T(8,128)(2,1)}, bf16[2,4,16,2560]{3,2,1,0:T(8,128)(2,1)S(1)}, u32[]{:S(2)}, u32[]{:S(2)}) collective-permute-start(bf16[2,4,16,2560]{3,2,1,0:T(8,128)(2,1)} %collective-permute-done.12), channel_id=1, source_target_pairs={{0,96},{4,100},{8,104},{12,108},{16,112},{20,116},{24,120},{28,124... | collective-permute-start | bytes 1966088 | tf_op jit(solution)/shard_map/ppermute | solution.py:200
  102.7 19.2 %collective-permute-start.19 = (bf16[4,2,16,2560]{3,2,1,0:T(8,128)(2,1)}, bf16[4,2,16,2560]{3,2,1,0:T(8,128)(2,1)S(1)}, u32[]{:S(2)}, u32[]{:S(2)}) collective-permute-start(bf16[4,2,16,2560]{3,2,1,0:T(8,128)(2,1)} %collective-permute-done.18), channel_id=1, source_target_pairs={{0,4},{4,8},{8,12},{12,0},{16,20},{20,24},{24,28},{28,16},{32,36},... | collective-permute-start | bytes 1966088 | tf_op jit(solution)/shard_map/ppermute | solution.py:214
  102.7 19.2 %collective-permute-start.25 = (bf16[4,2,16,2560]{3,2,1,0:T(8,128)(2,1)}, bf16[4,2,16,2560]{3,2,1,0:T(8,128)(2,1)S(1)}, u32[]{:S(2)}, u32[]{:S(2)}) collective-permute-start(bf16[4,2,16,2560]{3,2,1,0:T(8,128)(2,1)} %collective-permute-done.24), channel_id=1, source_target_pairs={{0,12},{4,0},{8,4},{12,8},{16,28},{20,16},{24,20},{28,24},{32,44},... | collective-permute-start | bytes 1966088 | tf_op jit(solution)/shard_map/ppermute | solution.py:214
  110.1 15.7 %collective-permute-start.8 = (bf16[2,4,16,2560]{3,2,1,0:T(8,128)(2,1)S(1)}, bf16[2,4,16,2560]{3,2,1,0:T(8,128)(2,1)S(1)}, u32[]{:S(2)}, u32[]{:S(2)}) collective-permute-start(bf16[2,4,16,2560]{3,2,1,0:T(8,128)(2,1)S(1)} %collective-permute-done.7), channel_id=1, source_target_pairs={{0,32},{4,36},{8,40},{12,44},{16,48},{20,52},{24,56},{28,60},{32,6... | collective-permute-start | bytes 1966088 | tf_op jit(solution)/shard_map/ppermute | solution.py:200
  110.1 20.3 %collective-permute-start.14 = (bf16[2,4,16,2560]{3,2,1,0:T(8,128)(2,1)S(1)}, bf16[2,4,16,2560]{3,2,1,0:T(8,128)(2,1)S(1)}, u32[]{:S(2)}, u32[]{:S(2)}) collective-permute-start(bf16[2,4,16,2560]{3,2,1,0:T(8,128)(2,1)S(1)} %collective-permute-done.13), channel_id=1, source_target_pairs={{0,96},{4,100},{8,104},{12,108},{16,112},{20,116},{24,120},{28,124... | collective-permute-start | bytes 1966088 | tf_op jit(solution)/shard_map/ppermute | solution.py:200
  121.9 31.5 %collective-permute-start.20 = (bf16[4,2,16,2560]{3,2,1,0:T(8,128)(2,1)S(1)}, bf16[4,2,16,2560]{3,2,1,0:T(8,128)(2,1)S(1)}, u32[]{:S(2)}, u32[]{:S(2)}) collective-permute-start(bf16[4,2,16,2560]{3,2,1,0:T(8,128)(2,1)S(1)} %collective-permute-done.19), channel_id=1, source_target_pairs={{0,4},{4,8},{8,12},{12,0},{16,20},{20,24},{24,28},{28,16},{32,36},... | collective-permute-start | bytes 1966088 | tf_op jit(solution)/shard_map/ppermute | solution.py:214
  121.9 32.8 %collective-permute-start.26 = (bf16[4,2,16,2560]{3,2,1,0:T(8,128)(2,1)S(1)}, bf16[4,2,16,2560]{3,2,1,0:T(8,128)(2,1)S(1)}, u32[]{:S(2)}, u32[]{:S(2)}) collective-permute-start(bf16[4,2,16,2560]{3,2,1,0:T(8,128)(2,1)S(1)} %collective-permute-done.25), channel_id=1, source_target_pairs={{0,12},{4,0},{8,4},{12,8},{16,28},{20,16},{24,20},{28,24},{32,44},... | collective-permute-start | bytes 1966088 | tf_op jit(solution)/shard_map/ppermute | solution.py:214
  201.8 15.1 %collective-permute-start.28 = (bf16[128,2048]{1,0:T(8,128)(2,1)S(1)}, bf16[128,2048]{1,0:T(8,128)(2,1)}, u32[]{:S(2)}, u32[]{:S(2)}) collective-permute-start(bf16[128,2048]{1,0:T(8,128)(2,1)S(1)} %fusion.99), channel_id=1, source_target_pairs={{0,2},{2,0},{1,3},{3,1},{4,6},{6,4},{5,7},{7,5},{8,10},{10,8},{9,1... | collective-permute-start | bytes 1572872 | tf_op jit(solution)/shard_map/ppermute | solution.py:119
  203.2 25.0 %collective-permute-start.33 = (bf16[128,2048]{1,0:T(8,128)(2,1)S(1)}, bf16[128,2048]{1,0:T(8,128)(2,1)}, u32[]{:S(2)}, u32[]{:S(2)}) collective-permute-start(bf16[128,2048]{1,0:T(8,128)(2,1)S(1)} %bitcast.497), channel_id=1, source_target_pairs={{0,2},{2,0},{1,3},{3,1},{4,6},{6,4},{5,7},{7,5},{8,10},{10,8},{9,1... | collective-permute-start | bytes 1572872 | tf_op jit(solution)/shard_map/ppermute | solution.py:108
  219.2 19.3 %collective-permute-start.29 = (bf16[128,2048]{1,0:T(8,128)(2,1)S(1)}, bf16[128,2048]{1,0:T(8,128)(2,1)S(1)}, u32[]{:S(2)}, u32[]{:S(2)}) collective-permute-start(bf16[128,2048]{1,0:T(8,128)(2,1)S(1)} %multiply_convert_fusion.4), channel_id=1, source_target_pairs={{0,2},{2,0},{1,3},{3,1},{4,6},{6,4},{5,7},{7,5},{8,10},{10,8},{9,1... | collective-permute-start | bytes 1572872 | tf_op jit(solution)/shard_map/ppermute | solution.py:108
  229.3 9.4 %collective-permute-start.34 = (bf16[2,128,2048]{2,1,0:T(8,128)(2,1)S(1)}, bf16[2,128,2048]{2,1,0:T(8,128)(2,1)S(1)}, u32[]{:S(2)}, u32[]{:S(2)}) collective-permute-start(bf16[2,128,2048]{2,1,0:T(8,128)(2,1)S(1)} %pad_maximum_fusion.8), channel_id=1, source_target_pairs={{0,1},{1,0},{2,3},{3,2},{4,5},{5,4},{6,7},{7,6},{8,9},{9,8},{10,11... | collective-permute-start | bytes 3145736 | tf_op jit(solution)/shard_map/ppermute | solution.py:110
  275.1 27.6 %collective-permute-start.35 = (f32[2,128,2048]{2,1,0:T(8,128)}, f32[2,128,2048]{2,1,0:T(8,128)}, u32[]{:S(2)}, u32[]{:S(2)}) collective-permute-start(f32[2,128,2048]{2,1,0:T(8,128)} %bitcast.91), channel_id=1, source_target_pairs={{0,1},{1,0},{2,3},{3,2},{4,5},{5,4},{6,7},{7,6},{8,9},{9,8},{10,11... | collective-permute-start | bytes 6291464 | tf_op jit(solution)/shard_map/ppermute | solution.py:116
  284.7 20.9 %collective-permute-start.31 = (f32[2,128,2048]{2,1,0:T(8,128)}, f32[2,128,2048]{2,1,0:T(8,128)}, u32[]{:S(2)}, u32[]{:S(2)}) collective-permute-start(f32[2,128,2048]{2,1,0:T(8,128)} %bitcast.83), channel_id=1, source_target_pairs={{0,1},{1,0},{2,3},{3,2},{4,5},{5,4},{6,7},{7,6},{8,9},{9,8},{10,11... | collective-permute-start | bytes 6291464 | tf_op jit(solution)/shard_map/ppermute | solution.py:116
  304.4 18.7 %collective-permute-start.36 = (bf16[128,2048]{1,0:T(8,128)(2,1)S(1)}, bf16[128,2048]{1,0:T(8,128)(2,1)S(1)}, u32[]{:S(2)}, u32[]{:S(2)}) collective-permute-start(bf16[128,2048]{1,0:T(8,128)(2,1)S(1)} %fusion.89), channel_id=1, source_target_pairs={{0,2},{2,0},{1,3},{3,1},{4,6},{6,4},{5,7},{7,5},{8,10},{10,8},{9,1... | collective-permute-start | bytes 1572872 | tf_op jit(solution)/shard_map/ppermute | solution.py:119
  307.3 29.6 %collective-permute-start.32 = (bf16[128,2048]{1,0:T(8,128)(2,1)S(1)}, bf16[128,2048]{1,0:T(8,128)(2,1)S(1)}, u32[]{:S(2)}, u32[]{:S(2)}) collective-permute-start(bf16[128,2048]{1,0:T(8,128)(2,1)S(1)} %fusion.93), channel_id=1, source_target_pairs={{0,2},{2,0},{1,3},{3,1},{4,6},{6,4},{5,7},{7,5},{8,10},{10,8},{9,1... | collective-permute-start | bytes 1572872 | tf_op jit(solution)/shard_map/ppermute | solution.py:119
  340.2 16.0 %collective-permute-start.37 = (bf16[128,2048]{1,0:T(8,128)(2,1)S(1)}, bf16[128,2048]{1,0:T(8,128)(2,1)S(1)}, u32[]{:S(2)}, u32[]{:S(2)}) collective-permute-start(bf16[128,2048]{1,0:T(8,128)(2,1)S(1)} %get-tuple-element.25), channel_id=1, source_target_pairs={{0,2},{2,0},{1,3},{3,1},{4,6},{6,4},{5,7},{7,5},{8,10},{10,8},{9,1... | collective-permute-start | bytes 1572872 | tf_op jit(solution)/shard_map/ppermute | solution.py:108
  395.7 81.7 %collective-permute-start.39 = (f32[2,128,2048]{2,1,0:T(8,128)}, f32[2,128,2048]{2,1,0:T(8,128)S(1)}, u32[]{:S(2)}, u32[]{:S(2)}) collective-permute-start(f32[2,128,2048]{2,1,0:T(8,128)} %bitcast.105), channel_id=1, source_target_pairs={{0,1},{1,0},{2,3},{3,2},{4,5},{5,4},{6,7},{7,6},{8,9},{9,8},{10,11... | collective-permute-start | bytes 6291464 | tf_op jit(solution)/shard_map/ppermute | solution.py:116
  414.9 19.9 %collective-permute-start.59 = (bf16[2,4,16,2560]{3,2,0,1:T(8,128)(2,1)S(1)}, bf16[2,4,16,2560]{3,2,0,1:T(8,128)(2,1)S(1)}, u32[]{:S(2)}, u32[]{:S(2)}) collective-permute-start(bf16[2,4,16,2560]{3,2,0,1:T(8,128)(2,1)S(1)} %bitcast.523), channel_id=1, source_target_pairs={{0,96},{4,100},{8,104},{12,108},{16,112},{20,116},{24,120},{28,124... | collective-permute-start | bytes 1966088 | tf_op jit(solution)/shard_map/ppermute | solution.py:146
  418.3 20.4 %collective-permute-start.53 = (bf16[2,4,16,2560]{3,2,0,1:T(8,128)(2,1)S(1)}, bf16[2,4,16,2560]{3,2,0,1:T(8,128)(2,1)S(1)}, u32[]{:S(2)}, u32[]{:S(2)}) collective-permute-start(bf16[2,4,16,2560]{3,2,0,1:T(8,128)(2,1)S(1)} %bitcast.522), channel_id=1, source_target_pairs={{0,32},{4,36},{8,40},{12,44},{16,48},{20,52},{24,56},{28,60},{32,6... | collective-permute-start | bytes 1966088 | tf_op jit(solution)/shard_map/ppermute | solution.py:146
  418.5 20.5 %collective-permute-start.47 = (bf16[4,2,16,2560]{3,2,1,0:T(8,128)(2,1)S(1)}, bf16[4,2,16,2560]{3,2,1,0:T(8,128)(2,1)S(1)}, u32[]{:S(2)}, u32[]{:S(2)}) collective-permute-start(bf16[4,2,16,2560]{3,2,1,0:T(8,128)(2,1)S(1)} %dynamic-slice_bitcast_fusion), channel_id=1, source_target_pairs={{0,12},{4,0},{8,4},{12,8},{16,28},{20,16},{24,20},{28,24},{32,44},... | collective-permute-start | bytes 1966088 | tf_op jit(solution)/shard_map/ppermute | solution.py:146
  422.3 20.0 %collective-permute-start.41 = (bf16[4,2,16,2560]{3,2,1,0:T(8,128)(2,1)S(1)}, bf16[4,2,16,2560]{3,2,1,0:T(8,128)(2,1)S(1)}, u32[]{:S(2)}, u32[]{:S(2)}) collective-permute-start(bf16[4,2,16,2560]{3,2,1,0:T(8,128)(2,1)S(1)} %dynamic-slice_bitcast_fusion.1), channel_id=1, source_target_pairs={{0,4},{4,8},{8,12},{12,0},{16,20},{20,24},{24,28},{28,16},{32,36},... | collective-permute-start | bytes 1966088 | tf_op jit(solution)/shard_map/ppermute | solution.py:146
  434.9 17.6 %collective-permute-start.60 = (bf16[2,4,16,2560]{3,2,0,1:T(8,128)(2,1)S(1)}, bf16[2,4,16,2560]{3,2,0,1:T(8,128)(2,1)S(1)}, u32[]{:S(2)}, u32[]{:S(2)}) collective-permute-start(bf16[2,4,16,2560]{3,2,0,1:T(8,128)(2,1)S(1)} %fusion.48), channel_id=1, source_target_pairs={{0,96},{4,100},{8,104},{12,108},{16,112},{20,116},{24,120},{28,124... | collective-permute-start | bytes 1966088 | tf_op jit(solution)/shard_map/ppermute | solution.py:146
  438.9 17.5 %collective-permute-start.54 = (bf16[2,4,16,2560]{3,2,0,1:T(8,128)(2,1)S(1)}, bf16[2,4,16,2560]{3,2,0,1:T(8,128)(2,1)S(1)}, u32[]{:S(2)}, u32[]{:S(2)}) collective-permute-start(bf16[2,4,16,2560]{3,2,0,1:T(8,128)(2,1)S(1)} %fusion.51), channel_id=1, source_target_pairs={{0,32},{4,36},{8,40},{12,44},{16,48},{20,52},{24,56},{28,60},{32,6... | collective-permute-start | bytes 1966088 | tf_op jit(solution)/shard_map/ppermute | solution.py:146
  439.2 17.5 %collective-permute-start.48 = (bf16[4,2,16,2560]{3,2,1,0:T(8,128)(2,1)S(1)}, bf16[4,2,16,2560]{3,2,1,0:T(8,128)(2,1)S(1)}, u32[]{:S(2)}, u32[]{:S(2)}) collective-permute-start(bf16[4,2,16,2560]{3,2,1,0:T(8,128)(2,1)S(1)} %fusion.54), channel_id=1, source_target_pairs={{0,12},{4,0},{8,4},{12,8},{16,28},{20,16},{24,20},{28,24},{32,44},... | collective-permute-start | bytes 1966088 | tf_op jit(solution)/shard_map/ppermute | solution.py:146
  442.4 17.4 %collective-permute-start.42 = (bf16[4,2,16,2560]{3,2,1,0:T(8,128)(2,1)S(1)}, bf16[4,2,16,2560]{3,2,1,0:T(8,128)(2,1)S(1)}, u32[]{:S(2)}, u32[]{:S(2)}) collective-permute-start(bf16[4,2,16,2560]{3,2,1,0:T(8,128)(2,1)S(1)} %fusion.57), channel_id=1, source_target_pairs={{0,4},{4,8},{8,12},{12,0},{16,20},{20,24},{24,28},{28,16},{32,36},... | collective-permute-start | bytes 1966088 | tf_op jit(solution)/shard_map/ppermute | solution.py:146
  452.7 16.6 %collective-permute-start.61 = (bf16[2,4,16,2560]{3,2,0,1:T(8,128)(2,1)S(1)}, bf16[2,4,16,2560]{3,2,0,1:T(8,128)(2,1)S(1)}, u32[]{:S(2)}, u32[]{:S(2)}) collective-permute-start(bf16[2,4,16,2560]{3,2,0,1:T(8,128)(2,1)S(1)} %fusion.49), channel_id=1, source_target_pairs={{0,96},{4,100},{8,104},{12,108},{16,112},{20,116},{24,120},{28,124... | collective-permute-start | bytes 1966088 | tf_op jit(solution)/shard_map/ppermute | solution.py:146
  456.6 16.3 %collective-permute-start.55 = (bf16[2,4,16,2560]{3,2,0,1:T(8,128)(2,1)S(1)}, bf16[2,4,16,2560]{3,2,0,1:T(8,128)(2,1)S(1)}, u32[]{:S(2)}, u32[]{:S(2)}) collective-permute-start(bf16[2,4,16,2560]{3,2,0,1:T(8,128)(2,1)S(1)} %fusion.52), channel_id=1, source_target_pairs={{0,32},{4,36},{8,40},{12,44},{16,48},{20,52},{24,56},{28,60},{32,6... | collective-permute-start | bytes 1966088 | tf_op jit(solution)/shard_map/ppermute | solution.py:146
  456.9 17.1 %collective-permute-start.49 = (bf16[4,2,16,2560]{3,2,1,0:T(8,128)(2,1)S(1)}, bf16[4,2,16,2560]{3,2,1,0:T(8,128)(2,1)S(1)}, u32[]{:S(2)}, u32[]{:S(2)}) collective-permute-start(bf16[4,2,16,2560]{3,2,1,0:T(8,128)(2,1)S(1)} %fusion.55), channel_id=1, source_target_pairs={{0,12},{4,0},{8,4},{12,8},{16,28},{20,16},{24,20},{28,24},{32,44},... | collective-permute-start | bytes 1966088 | tf_op jit(solution)/shard_map/ppermute | solution.py:146
  459.9 17.3 %collective-permute-start.43 = (bf16[4,2,16,2560]{3,2,1,0:T(8,128)(2,1)S(1)}, bf16[4,2,16,2560]{3,2,1,0:T(8,128)(2,1)S(1)}, u32[]{:S(2)}, u32[]{:S(2)}) collective-permute-start(bf16[4,2,16,2560]{3,2,1,0:T(8,128)(2,1)S(1)} %fusion.58), channel_id=1, source_target_pairs={{0,4},{4,8},{8,12},{12,0},{16,20},{20,24},{24,28},{28,16},{32,36},... | collective-permute-start | bytes 1966088 | tf_op jit(solution)/shard_map/ppermute | solution.py:146
  469.5 9.6 %collective-permute-start.62 = (bf16[2,16,2560]{2,1,0:T(8,128)(2,1)S(1)}, bf16[2,16,2560]{2,1,0:T(8,128)(2,1)S(1)}, u32[]{:S(2)}, u32[]{:S(2)}) collective-permute-start(bf16[2,16,2560]{2,1,0:T(8,128)(2,1)S(1)} %dynamic-slice_bitcast_fusion.2), channel_id=1, source_target_pairs={{0,12},{4,0},{8,4},{12,8},{16,28},{20,16},{24,20},{28,24},{32,44},... | collective-permute-start | bytes 491528 | tf_op jit(solution)/shard_map/ppermute | solution.py:146
  473.2 9.0 %collective-permute-start.56 = (bf16[2,16,2560]{2,1,0:T(8,128)(2,1)S(1)}, bf16[2,16,2560]{2,1,0:T(8,128)(2,1)S(1)}, u32[]{:S(2)}, u32[]{:S(2)}) collective-permute-start(bf16[2,16,2560]{2,1,0:T(8,128)(2,1)S(1)} %dynamic-slice_bitcast_fusion.3), channel_id=1, source_target_pairs={{0,4},{4,8},{8,12},{12,0},{16,20},{20,24},{24,28},{28,16},{32,36},... | collective-permute-start | bytes 491528 | tf_op jit(solution)/shard_map/ppermute | solution.py:146
  474.2 8.1 %collective-permute-start.50 = (bf16[2,16,2560]{2,1,0:T(8,128)(2,1)S(1)}, bf16[2,16,2560]{2,1,0:T(8,128)(2,1)S(1)}, u32[]{:S(2)}, u32[]{:S(2)}) collective-permute-start(bf16[2,16,2560]{2,1,0:T(8,128)(2,1)S(1)} %dynamic-slice_bitcast_fusion.4), channel_id=1, source_target_pairs={{0,96},{4,100},{8,104},{12,108},{16,112},{20,116},{24,120},{28,124... | collective-permute-start | bytes 491528 | tf_op jit(solution)/shard_map/ppermute | solution.py:146
  477.4 8.2 %collective-permute-start.44 = (bf16[2,16,2560]{2,1,0:T(8,128)(2,1)S(1)}, bf16[2,16,2560]{2,1,0:T(8,128)(2,1)S(1)}, u32[]{:S(2)}, u32[]{:S(2)}) collective-permute-start(bf16[2,16,2560]{2,1,0:T(8,128)(2,1)S(1)} %dynamic-slice_bitcast_fusion.5), channel_id=1, source_target_pairs={{0,32},{4,36},{8,40},{12,44},{16,48},{20,52},{24,56},{28,60},{32,6... | collective-permute-start | bytes 491528 | tf_op jit(solution)/shard_map/ppermute | solution.py:146
  477.7 24.6 %collective-permute-start.40 = (bf16[128,2048]{1,0:T(8,128)(2,1)S(1)}, bf16[128,2048]{1,0:T(8,128)(2,1)S(1)}, u32[]{:S(2)}, u32[]{:S(2)}) collective-permute-start(bf16[128,2048]{1,0:T(8,128)(2,1)S(1)} %fusion.85), channel_id=1, source_target_pairs={{0,2},{2,0},{1,3},{3,1},{4,6},{6,4},{5,7},{7,5},{8,10},{10,8},{9,1... | collective-permute-start | bytes 1572872 | tf_op jit(solution)/shard_map/ppermute | solution.py:119
  479.1 6.7 %collective-permute-start.63 = (bf16[2,16,2560]{2,1,0:T(8,128)(2,1)S(1)}, bf16[2,16,2560]{2,1,0:T(8,128)(2,1)S(1)}, u32[]{:S(2)}, u32[]{:S(2)}) collective-permute-start(bf16[2,16,2560]{2,1,0:T(8,128)(2,1)S(1)} %fusion.128), channel_id=1, source_target_pairs={{0,12},{4,0},{8,4},{12,8},{16,28},{20,16},{24,20},{28,24},{32,44},... | collective-permute-start | bytes 491528 | tf_op jit(solution)/shard_map/ppermute | solution.py:146
  482.2 7.8 %collective-permute-start.57 = (bf16[2,16,2560]{2,1,0:T(8,128)(2,1)S(1)}, bf16[2,16,2560]{2,1,0:T(8,128)(2,1)S(1)}, u32[]{:S(2)}, u32[]{:S(2)}) collective-permute-start(bf16[2,16,2560]{2,1,0:T(8,128)(2,1)S(1)} %fusion.130), channel_id=1, source_target_pairs={{0,4},{4,8},{8,12},{12,0},{16,20},{20,24},{24,28},{28,16},{32,36},... | collective-permute-start | bytes 491528 | tf_op jit(solution)/shard_map/ppermute | solution.py:146
  482.3 7.8 %collective-permute-start.51 = (bf16[2,16,2560]{2,1,0:T(8,128)(2,1)S(1)}, bf16[2,16,2560]{2,1,0:T(8,128)(2,1)S(1)}, u32[]{:S(2)}, u32[]{:S(2)}) collective-permute-start(bf16[2,16,2560]{2,1,0:T(8,128)(2,1)S(1)} %fusion.132), channel_id=1, source_target_pairs={{0,96},{4,100},{8,104},{12,108},{16,112},{20,116},{24,120},{28,124... | collective-permute-start | bytes 491528 | tf_op jit(solution)/shard_map/ppermute | solution.py:146
  485.6 8.3 %collective-permute-start.45 = (bf16[2,16,2560]{2,1,0:T(8,128)(2,1)S(1)}, bf16[2,16,2560]{2,1,0:T(8,128)(2,1)S(1)}, u32[]{:S(2)}, u32[]{:S(2)}) collective-permute-start(bf16[2,16,2560]{2,1,0:T(8,128)(2,1)S(1)} %fusion.134), channel_id=1, source_target_pairs={{0,32},{4,36},{8,40},{12,44},{16,48},{20,52},{24,56},{28,60},{32,6... | collective-permute-start | bytes 491528 | tf_op jit(solution)/shard_map/ppermute | solution.py:146
  485.9 8.2 %collective-permute-start.64 = (bf16[2,16,2560]{2,1,0:T(8,128)(2,1)S(1)}, bf16[2,16,2560]{2,1,0:T(8,128)(2,1)S(1)}, u32[]{:S(2)}, u32[]{:S(2)}) collective-permute-start(bf16[2,16,2560]{2,1,0:T(8,128)(2,1)S(1)} %fusion.129), channel_id=1, source_target_pairs={{0,12},{4,0},{8,4},{12,8},{16,28},{20,16},{24,20},{28,24},{32,44},... | collective-permute-start | bytes 491528 | tf_op jit(solution)/shard_map/ppermute | solution.py:146
  500.8 21.8 %collective-permute-start.65 = (bf16[64,2560]{1,0:T(8,128)(2,1)S(1)}, bf16[64,2560]{1,0:T(8,128)(2,1)S(1)}, u32[]{:S(2)}, u32[]{:S(2)}) collective-permute-start(bf16[64,2560]{1,0:T(8,128)(2,1)S(1)} %fusion.127), channel_id=1, source_target_pairs={{0,16},{4,20},{8,24},{12,28},{16,0},{20,4},{24,8},{28,12},{32,48},... | collective-permute-start | bytes 983048 | tf_op jit(solution)/shard_map/ppermute | solution.py:170
  504.2 17.7 %all-to-all-start.1 = ((f32[128,3,16]{2,1,0:T(4,128)}), f32[128,3,16]{2,1,0:T(4,128)S(1)}, u32[]{:S(2)}, u32[]{:S(2)}) async-start(f32[128,3,16]{2,1,0:T(4,128)} %copy.175), calls=%async_computation.1 | async-start | bytes 524288 | tf_op jit(solution)/shard_map/all_to_all | solution.py:229
  (50 other events, 386.1 us)
Sparse Core Ops, SparseCore 0:
  29.0 178.8 all-gather.1
  302.8 289.4 reduce-scatter.1

commit v15 on v13

--- a/solution.py
+++ b/solution.py
@@ -254,7 +254,7 @@
     row_count = doc_all.shape[0]
     resid_in = tokens[0].reshape(-1, model_width).astype(jnp.float32)
     cot_local = cotangent[0].reshape(-1, model_width)
-    attn_pack = jnp.concatenate([w_query, w_forget, w_value, w_outgate, w_output.T], axis=1)
+    attn_pack = jnp.concatenate([w_query, w_forget, w_value, w_outgate], axis=1)
     mlp_pack = jnp.concatenate([w_gate, w_up, w_down.T], axis=1)
     attn_all = ring_gather(attn_pack)
     mlp_all = lax.all_gather(mlp_pack, "dp", axis=0, tiled=True)
@@ -262,7 +262,7 @@
     wf_all = attn_all[:, 1 * local_width : 2 * local_width]
     wv_all = attn_all[:, 2 * local_width : 3 * local_width]
     wg_all = attn_all[:, 3 * local_width : 4 * local_width]
-    wo_t = attn_all[:, 4 * local_width : 5 * local_width]
+    wo_t = ring_gather(w_output.T)
     wgate_all = mlp_all[:, 0:hidden_width]
     wup_all = mlp_all[:, hidden_width : 2 * hidden_width]
     wdown_t = mlp_all[:, 2 * hidden_width : 3 * hidden_width]

time: 612 us -> 648 us (1.059)
  waiting for transfers between devices: 233 us -> 289 us
  local copies, waits for them, and re-layouts: 84 us -> 70.2 us
  matrix products: 89.4 us -> 81.2 us
    ppermute x24 -> x48, waiting for transfers between devices: 56.2 us -> 104 us  [ring_gather(): cur = lax.ppermute(cur, 'dp', pairs)]
    ppermute x24 -> x48, starting transfers between devices: 39.7 us -> 55.3 us  [ring_gather(): cur = lax.ppermute(cur, 'dp', pairs)]
    ppermute x4, starting transfers between devices: 20.1 us -> 5.23 us  [row_sum(): lax.ppermute(theirs.astype(jnp.bfloat16), 'tensor', ACROSS)]
    ppermute x12, waiting for transfers between devices: 81.8 us -> 89 us  [ring_stage(): got = lax.ppermute(acc.astype(jnp.bfloat16), 'dp', pairs)]
    ppermute x12, starting transfers between devices: 21.9 us -> 15.4 us  [ring_stage(): got = lax.ppermute(acc.astype(jnp.bfloat16), 'dp', pairs)]
    unnamed x85 -> x102, local copies, waits for them, and re-layouts: 13.9 us -> 14.2 us
  transfers between devices with their start and end apart: 58 -> 83, of which waited for: 30 -> 46; matrix products, arithmetic and copies ran while one was open for 30% -> 25% of each run, Pallas kernels for 2% -> 2%
where the time goes in v15:
time: 648 us; the launch traced here: 636 us
  waiting for transfers between devices  289 us (45%)
  starting transfers between devices  105 us (16%)
  matrix products  81.2 us (13%)
  local copies, waits for them, and re-layouts  70.2 us (11%)
  other arithmetic  47.3 us (7%)
  Pallas kernels  26.5 us (4%)
  between operations  16.3 us (3%)
    ppermute x48, waiting for transfers between devices, ring_gather(): cur = lax.ppermute(cur, 'dp', pairs)  104 us
    ppermute x12, waiting for transfers between devices, ring_stage(): got = lax.ppermute(acc.astype(jnp.bfloat16), 'dp', pairs)  89 us
    ppermute x48, starting transfers between devices, ring_gather(): cur = lax.ppermute(cur, 'dp', pairs)  55.3 us
    ppermute x4, waiting for transfers between devices, row_sum(): lax.ppermute(theirs.astype(jnp.bfloat16), 'tensor', ACROSS)  44.1 us
    dot_general x8, matrix products, matmul_plain(): return jnp.dot(left, right, preferred_element_type=jnp.float32)  35.7 us
    ppermute x4, waiting for transfers between devices, row_gather(): across = lax.ppermute(values, 'tensor', ACROSS)  34 us
    dot_general x8, matrix products, times_trans(): lax.dot_general(left, right, (((1,), (1,)), ((), ())), preferred_element_...  27.2 us
    pallas_call x2, Pallas kernels, grad_pack(): pl.pallas_call(functools.partial(pack_kernel, per), grid=(rows_out // til...  26.5 us
  transfers between devices with their start and end apart: 83, of which 46 were waited for; matrix products, arithmetic and copies ran while one was open for 25% of the time, Pallas kernels for 2%

profile of v15, /device:TPU:0, one launch (start us, length us, event | category | flops | bytes accessed | tf_op | source)
XLA Modules:
  0.0 636.3 jit_solution(6865675164109281999)
XLA Ops:
  10.7 3.3 collective-permute-start.2
  15.4 8.9 %all-to-all-start = ((f32[128,3,16]{2,1,0:T(4,128)}), f32[128,3,16]{2,1,0:T(4,128)S(1)}, u32[]{:S(2)}, u32[]{:S(2)}) async-start(f32[128,3,16]{2,1,0:T(4,128)} %broadcast_in_dim.263), calls=%async_computation | async-start | bytes 524288 | tf_op jit(solution)/shard_map/all_to_all | solution.py:215
  31.1 4.0 all-to-all-done
  65.7 8.9 %collective-permute-done.3 = bf16[2,16,2048]{2,1,0:T(8,128)(2,1)S(1)} collective-permute-done((bf16[2,16,2048]{2,1,0:T(8,128)(2,1)S(1)}, bf16[2,16,2048]{2,1,0:T(8,128)(2,1)S(1)}, u32[]{:S(2)}, u32[]{:S(2)}) %collective-permute-start.3) | collective-permute-done | bytes 131104 | tf_op jit(solution)/shard_map/ppermute | solution.py:187
  74.6 6.5 %collective-permute-done.9 = bf16[2,16,2048]{2,1,0:T(8,128)(2,1)S(1)} collective-permute-done((bf16[2,16,2048]{2,1,0:T(8,128)(2,1)S(1)}, bf16[2,16,2048]{2,1,0:T(8,128)(2,1)S(1)}, u32[]{:S(2)}, u32[]{:S(2)}) %collective-permute-start.9) | collective-permute-done | bytes 131104 | tf_op jit(solution)/shard_map/ppermute | solution.py:187
  81.6 6.5 %collective-permute-done.15 = bf16[2,16,2048]{2,1,0:T(8,128)(2,1)S(1)} collective-permute-done((bf16[2,16,2048]{2,1,0:T(8,128)(2,1)S(1)}, bf16[2,16,2048]{2,1,0:T(8,128)(2,1)S(1)}, u32[]{:S(2)}, u32[]{:S(2)}) %collective-permute-start.15) | collective-permute-done | bytes 131104 | tf_op jit(solution)/shard_map/ppermute | solution.py:201
  91.8 3.1 collective-permute-done.21
  97.9 6.1 collective-permute-done.4
  104.2 4.8 collective-permute-done.10
  109.1 8.7 %collective-permute-done.16 = bf16[2,16,2048]{2,1,0:T(8,128)(2,1)S(1)} collective-permute-done((bf16[2,16,2048]{2,1,0:T(8,128)(2,1)S(1)}, bf16[2,16,2048]{2,1,0:T(8,128)(2,1)S(1)}, u32[]{:S(2)}, u32[]{:S(2)}) %collective-permute-start.16) | collective-permute-done | bytes 131104 | tf_op jit(solution)/shard_map/ppermute | solution.py:201
  121.2 5.1 collective-permute-done.22
  132.3 3.3 collective-permute-start.23
  142.1 3.3 collective-permute-start.24
  145.4 10.9 %collective-permute-done.6 = bf16[2,4,16,2048]{3,2,1,0:T(8,128)(2,1)S(1)} collective-permute-done((bf16[2,4,16,2048]{3,2,1,0:T(8,128)(2,1)S(1)}, bf16[2,4,16,2048]{3,2,1,0:T(8,128)(2,1)S(1)}, u32[]{:S(2)}, u32[]{:S(2)}) %collective-permute-start.6) | collective-permute-done | bytes 524320 | tf_op jit(solution)/shard_map/ppermute | solution.py:193
  157.4 3.3 collective-permute-start.13
  164.0 9.4 %collective-permute-done.7 = bf16[2,4,16,2048]{3,2,1,0:T(8,128)(2,1)S(1)} collective-permute-done((bf16[2,4,16,2048]{3,2,1,0:T(8,128)(2,1)S(1)}, bf16[2,4,16,2048]{3,2,1,0:T(8,128)(2,1)S(1)}, u32[]{:S(2)}, u32[]{:S(2)}) %collective-permute-start.7) | collective-permute-done | bytes 524320 | tf_op jit(solution)/shard_map/ppermute | solution.py:193
  176.3 3.3 collective-permute-start.14
  183.6 10.7 %collective-permute-done.8 = bf16[2,4,16,2048]{3,2,1,0:T(8,128)(2,1)S(1)} collective-permute-done((bf16[2,4,16,2048]{3,2,1,0:T(8,128)(2,1)S(1)}, bf16[2,4,16,2048]{3,2,1,0:T(8,128)(2,1)S(1)}, u32[]{:S(2)}, u32[]{:S(2)}) %collective-permute-start.8) | collective-permute-done | bytes 524320 | tf_op jit(solution)/shard_map/ppermute | solution.py:193
  194.5 5.7 collective-permute-done.14
  200.5 4.0 collective-permute-done.20
  209.3 4.1 copy.182
  213.4 4.0 copy.184
  219.9 3.6 fusion.53
  238.6 4.9 fusion.71
  245.2 4.1 collective-permute-done.52
  252.0 12.8 %collective-permute-done.53 = bf16[128,2048]{1,0:T(8,128)(2,1)} collective-permute-done((bf16[128,2048]{1,0:T(8,128)(2,1)S(1)}, bf16[128,2048]{1,0:T(8,128)(2,1)}, u32[]{:S(2)}, u32[]{:S(2)}) %collective-permute-start.53) | collective-permute-done | bytes 524320 | tf_op jit(solution)/shard_map/ppermute | solution.py:119
  268.1 7.9 %collective-permute-done.58 = bf16[128,2048]{1,0:T(8,128)(2,1)} collective-permute-done((bf16[128,2048]{1,0:T(8,128)(2,1)S(1)}, bf16[128,2048]{1,0:T(8,128)(2,1)}, u32[]{:S(2)}, u32[]{:S(2)}) %collective-permute-start.58) | collective-permute-done | bytes 524320 | tf_op jit(solution)/shard_map/ppermute | solution.py:108
  277.4 8.9 %collective-permute-done.54 = bf16[128,2048]{1,0:T(8,128)(2,1)S(1)} collective-permute-done((bf16[128,2048]{1,0:T(8,128)(2,1)S(1)}, bf16[128,2048]{1,0:T(8,128)(2,1)S(1)}, u32[]{:S(2)}, u32[]{:S(2)}) %collective-permute-start.54) | collective-permute-done | bytes 524320 | tf_op jit(solution)/shard_map/ppermute | solution.py:108
  290.8 8.4 %fusion = f32[512,1408]{1,0:T(8,128)} fusion(bf16[512,2048]{1,0:T(8,128)(2,1)} %bitcast.541, bf16[2048,4224]{1,0:T(8,128)(2,1)} %all-gather.2.cloned.1.call-done), kind=kOutput, calls=%fused_computation.2 | convolution fusion | flops 2952790016 | bytes 10747904 | tf_op jit(solution)/shard_map/dot_general | solution.py:27
  300.7 5.0 fusion.6
  305.7 6.6 %multiply_convert_fusion.1 = (bf16[512,1408]{1,0:T(8,128)(2,1)S(1)}, bf16[512,1408]{1,0:T(8,128)(2,1)S(1)}, bf16[512,1408]{1,0:T(8,128)(2,1)S(1)}) fusion(f32[512,1408]{1,0:T(8,128)} %fusion, f32[512,1408]{1,0:T(8,128)} %fusion.6, bf16[512,2048]{1,0:T(8,128)(2,1)S(1)} %bitcast.545, bf16[2048,4224]{1,0:T(8,128)(2,1)S(1)} %copy-done.45), kind=kOutput, calls=%fused_computation.18 | convolution fusion | flops 2963603456 | bytes 17956864 | tf_op jit(solution)/shard_map/dot_general | solution.py:27
  316.4 15.7 %shard_map.247 = bf16[2048,4224]{1,0:T(8,128)(2,1)} custom-call(bf16[512,2048]{1,0:T(8,128)(2,1)} %bitcast.543, bf16[512,2048]{1,0:T(8,128)(2,1)} %bitcast.542, bf16[512,4224]{1,0:T(8,128)(2,1)} %pad_maximum_fusion.right_ref), custom_call_target="tpu_custom_call" | custom-call | flops 8858370048 | bytes 25821184 | tf_op jit(solution)/shard_map/pallas_call | solution.py:64
  332.1 6.0 fusion.4
  338.2 5.5 fusion.12
  345.1 5.5 fusion.2
  356.4 14.0 %collective-permute-done.61 = bf16[128,2048]{1,0:T(8,128)(2,1)S(1)} collective-permute-done((bf16[128,2048]{1,0:T(8,128)(2,1)S(1)}, bf16[128,2048]{1,0:T(8,128)(2,1)S(1)}, u32[]{:S(2)}, u32[]{:S(2)}) %collective-permute-start.61) | collective-permute-done | bytes 524320 | tf_op jit(solution)/shard_map/ppermute | solution.py:119
  370.8 14.0 %collective-permute-done.57 = bf16[128,2048]{1,0:T(8,128)(2,1)S(1)} collective-permute-done((bf16[128,2048]{1,0:T(8,128)(2,1)S(1)}, bf16[128,2048]{1,0:T(8,128)(2,1)S(1)}, u32[]{:S(2)}, u32[]{:S(2)}) %collective-permute-start.57) | collective-permute-done | bytes 524320 | tf_op jit(solution)/shard_map/ppermute | solution.py:119
  387.3 17.2 %collective-permute-done.62 = bf16[128,2048]{1,0:T(8,128)(2,1)S(1)} collective-permute-done((bf16[128,2048]{1,0:T(8,128)(2,1)S(1)}, bf16[128,2048]{1,0:T(8,128)(2,1)S(1)}, u32[]{:S(2)}, u32[]{:S(2)}) %collective-permute-start.62) | collective-permute-done | bytes 524320 | tf_op jit(solution)/shard_map/ppermute | solution.py:108
  412.7 3.2 fusion.56
  417.3 3.3 convolution_select_fusion
  432.0 10.8 %shard_map.246 = bf16[2048,2560]{1,0:T(8,128)(2,1)} custom-call(bf16[512,2048]{1,0:T(8,128)(2,1)} %bitcast.538, bf16[512,2048]{1,0:T(8,128)(2,1)} %bitcast.540, bf16[512,2560]{1,0:T(8,128)(2,1)} %constant_dynamic-update-slice_fusion.5.right_ref), custom_call_target="tpu_custom_call" | custom-call | flops 5368709120 | bytes 17301504 | tf_op jit(solution)/shard_map/pallas_call | solution.py:64
  442.8 9.3 %copy.252 = bf16[4,2,4,64,2560]{4,3,1,0,2:T(8,128)(2,1)} copy(bf16[4,2,4,64,2560]{4,3,2,1,0:T(8,128)(2,1)} %bitcast.521) | data formatting | bytes 20971520 | tf_op jit(solution)/shard_map/reshape | solution.py:157
  452.1 9.4 %fusion.142 = (bf16[4,4,2,64,1280]{4,3,2,1,0:T(8,128)(2,1)}, bf16[4,4,2,64,1280]{4,3,2,1,0:T(8,128)(2,1)}) fusion(bf16[4,4,2,64,2560]{4,3,2,1,0:T(8,128)(2,1)} %bitcast.520), kind=kLoop, calls=%fused_computation.304 | loop fusion | bytes 20971520 | tf_op jit(solution)/shard_map/slice | solution.py:140
  463.1 3.0 fusion.35
  466.1 3.1 fusion.33
  471.7 3.1 collective-permute-start.72
  480.2 14.7 %collective-permute-done.66 = bf16[4,2,64,1280]{3,2,1,0:T(8,128)(2,1)S(1)} collective-permute-done((bf16[4,2,64,1280]{3,2,1,0:T(8,128)(2,1)S(1)}, bf16[4,2,64,1280]{3,2,1,0:T(8,128)(2,1)S(1)}, u32[]{:S(2)}, u32[]{:S(2)}) %collective-permute-start.66) | collective-permute-done | bytes 1310752 | tf_op jit(solution)/shard_map/ppermute | solution.py:148
  498.1 5.0 collective-permute-done.72
  503.1 3.0 fusion.16
  506.1 3.7 collective-permute-start.73
  511.1 18.3 %collective-permute-done.67 = bf16[4,2,64,1280]{3,2,1,0:T(8,128)(2,1)} collective-permute-done((bf16[4,2,64,1280]{3,2,1,0:T(8,128)(2,1)}, bf16[4,2,64,1280]{3,2,1,0:T(8,128)(2,1)}, u32[]{:S(2)}, u32[]{:S(2)}) %collective-permute-start.67) | collective-permute-done | bytes 1310752 | tf_op jit(solution)/shard_map/ppermute | solution.py:148
  529.4 3.1 fusion.20
  540.2 3.7 collective-permute-start.74
  543.9 3.4 collective-permute-done.65
  550.9 7.3 %all-to-all-start.1 = ((f32[128,3,16]{2,1,0:T(4,128)}), f32[128,3,16]{2,1,0:T(4,128)S(1)}, u32[]{:S(2)}, u32[]{:S(2)}) async-start(f32[128,3,16]{2,1,0:T(4,128)} %copy.215), calls=%async_computation.1 | async-start | bytes 524288 | tf_op jit(solution)/shard_map/all_to_all | solution.py:222
  558.2 18.6 %collective-permute-done.68 = bf16[4,2,64,1280]{3,2,1,0:T(8,128)(2,1)} collective-permute-done((bf16[4,2,64,1280]{3,2,1,0:T(8,128)(2,1)}, bf16[4,2,64,1280]{3,2,1,0:T(8,128)(2,1)}, u32[]{:S(2)}, u32[]{:S(2)}) %collective-permute-start.68) | collective-permute-done | bytes 1310752 | tf_op jit(solution)/shard_map/ppermute | solution.py:148
  579.0 5.1 collective-permute-done.74
  587.7 6.6 %collective-permute-done.69 = bf16[2,64,1280]{2,1,0:T(8,128)(2,1)S(1)} collective-permute-done((bf16[2,64,1280]{2,1,0:T(8,128)(2,1)S(1)}, bf16[2,64,1280]{2,1,0:T(8,128)(2,1)S(1)}, u32[]{:S(2)}, u32[]{:S(2)}) %collective-permute-start.69) | collective-permute-done | bytes 327712 | tf_op jit(solution)/shard_map/ppermute | solution.py:148
  594.6 3.6 collective-permute-done.75
  599.4 4.4 collective-permute-done.70
  604.0 3.7 collective-permute-done.76
  609.2 3.9 collective-permute-done.71
  613.2 3.9 collective-permute-done.77
  621.1 4.8 collective-permute-done.78
  (411 shorter events, 190.1 us)
Async XLA Ops:
  10.7 52.0 %collective-permute-start.2 = (bf16[64,2048]{1,0:T(8,128)(2,1)S(1)}, bf16[64,2048]{1,0:T(8,128)(2,1)S(1)}, u32[]{:S(2)}, u32[]{:S(2)}) collective-permute-start(bf16[64,2048]{1,0:T(8,128)(2,1)S(1)} %constant_dynamic-update-slice_fusion.1), channel_id=1, source_target_pairs={{0,16},{4,20},{8,24},{12,28},{16,0},{20,4},{24,8},{28,12},{32,48},... | collective-permute-start | bytes 786440 | tf_op jit(solution)/shard_map/ppermute | solution.py:171
  15.4 19.7 %all-to-all-start = ((f32[128,3,16]{2,1,0:T(4,128)}), f32[128,3,16]{2,1,0:T(4,128)S(1)}, u32[]{:S(2)}, u32[]{:S(2)}) async-start(f32[128,3,16]{2,1,0:T(4,128)} %broadcast_in_dim.263), calls=%async_computation | async-start | bytes 524288 | tf_op jit(solution)/shard_map/all_to_all | solution.py:215
  24.3 266.5 %all-gather.2.cloned.1.call-start = ((), (), s32[]{:S(2)}) async-start(), calls=%async_computation.3 | async-start | bytes 17842176 | tf_op jit(solution)/shard_map/all_gather | solution.py:260
  24.3 13.4 %collective-permute-start.27 = (bf16[64,512]{1,0:T(8,128)(2,1)}, bf16[64,512]{1,0:T(8,128)(2,1)S(1)}, u32[]{:S(2)}, u32[]{:S(2)}) collective-permute-start(bf16[64,512]{1,0:T(8,128)(2,1)} %bitcast.558), channel_id=1, source_target_pairs={{0,16},{4,20},{8,24},{12,28},{16,0},{20,4},{24,8},{28,12},{32,48},... | collective-permute-start | bytes 196616 | tf_op jit(solution)/shard_map/ppermute | solution.py:171
  28.9 597.9 %reduce-scatter.2.cloned.1.call-start = ((), (), s32[]{:S(2)}) async-start(), calls=%async_computation.4 | async-start | bytes 17842176 | tf_op jit(solution)/shard_map/reduce_scatter | solution.py:306
  36.9 90.6 %collective-permute-start = (bf16[128,2048]{1,0:T(8,128)(2,1)}, bf16[128,2048]{1,0:T(8,128)(2,1)}, u32[]{:S(2)}, u32[]{:S(2)}) collective-permute-start(bf16[128,2048]{1,0:T(8,128)(2,1)} %fusion.59), channel_id=1, source_target_pairs={{0,2},{2,0},{1,3},{3,1},{4,6},{6,4},{5,7},{7,5},{8,10},{10,8},{9,1... | collective-permute-start | bytes 1572872 | tf_op jit(solution)/shard_map/ppermute | solution.py:108
  58.2 7.4 %collective-permute-start.31 = (bf16[2,4,16,512]{3,2,1,0:T(8,128)(2,1)S(1)}, bf16[2,4,16,512]{3,2,1,0:T(8,128)(2,1)S(1)}, u32[]{:S(2)}, u32[]{:S(2)}) collective-permute-start(bf16[2,4,16,512]{3,2,1,0:T(8,128)(2,1)S(1)} %bitcast_dynamic-update-slice_fusion.59), channel_id=1, source_target_pairs={{0,32},{4,36},{8,40},{12,44},{16,48},{20,52},{24,56},{28,60},{32,6... | collective-permute-start | bytes 393224 | tf_op jit(solution)/shard_map/ppermute | solution.py:193
  60.4 28.1 %collective-permute-start.37 = (bf16[2,4,16,512]{3,2,1,0:T(8,128)(2,1)S(1)}, bf16[2,4,16,512]{3,2,1,0:T(8,128)(2,1)S(1)}, u32[]{:S(2)}, u32[]{:S(2)}) collective-permute-start(bf16[2,4,16,512]{3,2,1,0:T(8,128)(2,1)S(1)} %bitcast_dynamic-update-slice_fusion.55), channel_id=1, source_target_pairs={{0,96},{4,100},{8,104},{12,108},{16,112},{20,116},{24,120},{28,124... | collective-permute-start | bytes 393224 | tf_op jit(solution)/shard_map/ppermute | solution.py:193
  61.6 29.0 %collective-permute-start.43 = (bf16[4,2,16,512]{3,2,1,0:T(8,128)(2,1)S(1)}, bf16[4,2,16,512]{3,2,1,0:T(8,128)(2,1)S(1)}, u32[]{:S(2)}, u32[]{:S(2)}) collective-permute-start(bf16[4,2,16,512]{3,2,1,0:T(8,128)(2,1)S(1)} %bitcast_dynamic-update-slice_fusion.67), channel_id=1, source_target_pairs={{0,4},{4,8},{8,12},{12,0},{16,20},{20,24},{24,28},{28,16},{32,36},... | collective-permute-start | bytes 393224 | tf_op jit(solution)/shard_map/ppermute | solution.py:207
  62.7 29.1 %collective-permute-start.49 = (bf16[4,2,16,512]{3,2,1,0:T(8,128)(2,1)S(1)}, bf16[4,2,16,512]{3,2,1,0:T(8,128)(2,1)S(1)}, u32[]{:S(2)}, u32[]{:S(2)}) collective-permute-start(bf16[4,2,16,512]{3,2,1,0:T(8,128)(2,1)S(1)} %bitcast_dynamic-update-slice_fusion.63), channel_id=1, source_target_pairs={{0,12},{4,0},{8,4},{12,8},{16,28},{20,16},{24,20},{28,24},{32,44},... | collective-permute-start | bytes 393224 | tf_op jit(solution)/shard_map/ppermute | solution.py:207
  65.6 9.0 %collective-permute-start.3 = (bf16[2,16,2048]{2,1,0:T(8,128)(2,1)S(1)}, bf16[2,16,2048]{2,1,0:T(8,128)(2,1)S(1)}, u32[]{:S(2)}, u32[]{:S(2)}) collective-permute-start(bf16[2,16,2048]{2,1,0:T(8,128)(2,1)S(1)} %get-tuple-element.54), channel_id=1, source_target_pairs={{0,4},{4,8},{8,12},{12,0},{16,20},{20,24},{24,28},{28,16},{32,36},... | collective-permute-start | bytes 393224 | tf_op jit(solution)/shard_map/ppermute | solution.py:187
  81.1 7.0 %collective-permute-start.15 = (bf16[2,16,2048]{2,1,0:T(8,128)(2,1)S(1)}, bf16[2,16,2048]{2,1,0:T(8,128)(2,1)S(1)}, u32[]{:S(2)}, u32[]{:S(2)}) collective-permute-start(bf16[2,16,2048]{2,1,0:T(8,128)(2,1)S(1)} %get-tuple-element.52), channel_id=1, source_target_pairs={{0,32},{4,36},{8,40},{12,44},{16,48},{20,52},{24,56},{28,60},{32,6... | collective-permute-start | bytes 393224 | tf_op jit(solution)/shard_map/ppermute | solution.py:201
  88.1 6.8 %collective-permute-start.21 = (bf16[2,16,2048]{2,1,0:T(8,128)(2,1)S(1)}, bf16[2,16,2048]{2,1,0:T(8,128)(2,1)S(1)}, u32[]{:S(2)}, u32[]{:S(2)}) collective-permute-start(bf16[2,16,2048]{2,1,0:T(8,128)(2,1)S(1)} %get-tuple-element.51), channel_id=1, source_target_pairs={{0,96},{4,100},{8,104},{12,108},{16,112},{20,116},{24,120},{28,124... | collective-permute-start | bytes 393224 | tf_op jit(solution)/shard_map/ppermute | solution.py:201
  88.5 9.3 %collective-permute-start.32 = (bf16[2,4,16,512]{3,2,1,0:T(8,128)(2,1)S(1)}, bf16[2,4,16,512]{3,2,1,0:T(8,128)(2,1)S(1)}, u32[]{:S(2)}, u32[]{:S(2)}) collective-permute-start(bf16[2,4,16,512]{3,2,1,0:T(8,128)(2,1)S(1)} %collective-permute-done.31), channel_id=1, source_target_pairs={{0,32},{4,36},{8,40},{12,44},{16,48},{20,52},{24,56},{28,60},{32,6... | collective-permute-start | bytes 393224 | tf_op jit(solution)/shard_map/ppermute | solution.py:193
  90.6 27.4 %collective-permute-start.38 = (bf16[2,4,16,512]{3,2,1,0:T(8,128)(2,1)S(1)}, bf16[2,4,16,512]{3,2,1,0:T(8,128)(2,1)S(1)}, u32[]{:S(2)}, u32[]{:S(2)}) collective-permute-start(bf16[2,4,16,512]{3,2,1,0:T(8,128)(2,1)S(1)} %collective-permute-done.37), channel_id=1, source_target_pairs={{0,96},{4,100},{8,104},{12,108},{16,112},{20,116},{24,120},{28,124... | collective-permute-start | bytes 393224 | tf_op jit(solution)/shard_map/ppermute | solution.py:193
  91.8 28.1 %collective-permute-start.44 = (bf16[4,2,16,512]{3,2,1,0:T(8,128)(2,1)S(1)}, bf16[4,2,16,512]{3,2,1,0:T(8,128)(2,1)S(1)}, u32[]{:S(2)}, u32[]{:S(2)}) collective-permute-start(bf16[4,2,16,512]{3,2,1,0:T(8,128)(2,1)S(1)} %collective-permute-done.43), channel_id=1, source_target_pairs={{0,4},{4,8},{8,12},{12,0},{16,20},{20,24},{24,28},{28,16},{32,36},... | collective-permute-start | bytes 393224 | tf_op jit(solution)/shard_map/ppermute | solution.py:207
  94.9 26.4 %collective-permute-start.50 = (bf16[4,2,16,512]{3,2,1,0:T(8,128)(2,1)S(1)}, bf16[4,2,16,512]{3,2,1,0:T(8,128)(2,1)S(1)}, u32[]{:S(2)}, u32[]{:S(2)}) collective-permute-start(bf16[4,2,16,512]{3,2,1,0:T(8,128)(2,1)S(1)} %collective-permute-done.49), channel_id=1, source_target_pairs={{0,12},{4,0},{8,4},{12,8},{16,28},{20,16},{24,20},{28,24},{32,44},... | collective-permute-start | bytes 393224 | tf_op jit(solution)/shard_map/ppermute | solution.py:207
  109.0 8.8 %collective-permute-start.16 = (bf16[2,16,2048]{2,1,0:T(8,128)(2,1)S(1)}, bf16[2,16,2048]{2,1,0:T(8,128)(2,1)S(1)}, u32[]{:S(2)}, u32[]{:S(2)}) collective-permute-start(bf16[2,16,2048]{2,1,0:T(8,128)(2,1)S(1)} %collective-permute-done.15), channel_id=1, source_target_pairs={{0,32},{4,36},{8,40},{12,44},{16,48},{20,52},{24,56},{28,60},{32,6... | collective-permute-start | bytes 393224 | tf_op jit(solution)/shard_map/ppermute | solution.py:201
  117.8 8.5 %collective-permute-start.22 = (bf16[2,16,2048]{2,1,0:T(8,128)(2,1)S(1)}, bf16[2,16,2048]{2,1,0:T(8,128)(2,1)S(1)}, u32[]{:S(2)}, u32[]{:S(2)}) collective-permute-start(bf16[2,16,2048]{2,1,0:T(8,128)(2,1)S(1)} %collective-permute-done.21), channel_id=1, source_target_pairs={{0,96},{4,100},{8,104},{12,108},{16,112},{20,116},{24,120},{28,124... | collective-permute-start | bytes 393224 | tf_op jit(solution)/shard_map/ppermute | solution.py:201
  117.9 11.6 %collective-permute-start.33 = (bf16[2,4,16,512]{3,2,1,0:T(8,128)(2,1)S(1)}, bf16[2,4,16,512]{3,2,1,0:T(8,128)(2,1)S(1)}, u32[]{:S(2)}, u32[]{:S(2)}) collective-permute-start(bf16[2,4,16,512]{3,2,1,0:T(8,128)(2,1)S(1)} %collective-permute-done.32), channel_id=1, source_target_pairs={{0,32},{4,36},{8,40},{12,44},{16,48},{20,52},{24,56},{28,60},{32,6... | collective-permute-start | bytes 393224 | tf_op jit(solution)/shard_map/ppermute | solution.py:193
  119.9 12.1 %collective-permute-start.39 = (bf16[2,4,16,512]{3,2,1,0:T(8,128)(2,1)S(1)}, bf16[2,4,16,512]{3,2,1,0:T(8,128)(2,1)S(1)}, u32[]{:S(2)}, u32[]{:S(2)}) collective-permute-start(bf16[2,4,16,512]{3,2,1,0:T(8,128)(2,1)S(1)} %collective-permute-done.38), channel_id=1, source_target_pairs={{0,96},{4,100},{8,104},{12,108},{16,112},{20,116},{24,120},{28,124... | collective-permute-start | bytes 393224 | tf_op jit(solution)/shard_map/ppermute | solution.py:193
  121.2 11.0 %collective-permute-start.45 = (bf16[4,2,16,512]{3,2,1,0:T(8,128)(2,1)S(1)}, bf16[4,2,16,512]{3,2,1,0:T(8,128)(2,1)S(1)}, u32[]{:S(2)}, u32[]{:S(2)}) collective-permute-start(bf16[4,2,16,512]{3,2,1,0:T(8,128)(2,1)S(1)} %collective-permute-done.44), channel_id=1, source_target_pairs={{0,4},{4,8},{8,12},{12,0},{16,20},{20,24},{24,28},{28,16},{32,36},... | collective-permute-start | bytes 393224 | tf_op jit(solution)/shard_map/ppermute | solution.py:207
  126.3 15.8 %collective-permute-start.51 = (bf16[4,2,16,512]{3,2,1,0:T(8,128)(2,1)S(1)}, bf16[4,2,16,512]{3,2,1,0:T(8,128)(2,1)S(1)}, u32[]{:S(2)}, u32[]{:S(2)}) collective-permute-start(bf16[4,2,16,512]{3,2,1,0:T(8,128)(2,1)S(1)} %collective-permute-done.50), channel_id=1, source_target_pairs={{0,12},{4,0},{8,4},{12,8},{16,28},{20,16},{24,20},{28,24},{32,44},... | collective-permute-start | bytes 393224 | tf_op jit(solution)/shard_map/ppermute | solution.py:207
  127.5 9.0 %collective-permute-start.5 = (bf16[2,16,2048]{2,1,0:T(8,128)(2,1)S(1)}, bf16[2,16,2048]{2,1,0:T(8,128)(2,1)S(1)}, u32[]{:S(2)}, u32[]{:S(2)}) collective-permute-start(bf16[2,16,2048]{2,1,0:T(8,128)(2,1)S(1)} %collective-permute-done.4), channel_id=1, source_target_pairs={{0,4},{4,8},{8,12},{12,0},{16,20},{20,24},{24,28},{28,16},{32,36},... | collective-permute-start | bytes 393224 | tf_op jit(solution)/shard_map/ppermute | solution.py:187
  129.6 8.7 %collective-permute-start.11 = (bf16[2,16,2048]{2,1,0:T(8,128)(2,1)S(1)}, bf16[2,16,2048]{2,1,0:T(8,128)(2,1)S(1)}, u32[]{:S(2)}, u32[]{:S(2)}) collective-permute-start(bf16[2,16,2048]{2,1,0:T(8,128)(2,1)S(1)} %collective-permute-done.10), channel_id=1, source_target_pairs={{0,12},{4,0},{8,4},{12,8},{16,28},{20,16},{24,20},{28,24},{32,44},... | collective-permute-start | bytes 393224 | tf_op jit(solution)/shard_map/ppermute | solution.py:187
  132.1 9.0 %collective-permute-start.17 = (bf16[2,16,2048]{2,1,0:T(8,128)(2,1)S(1)}, bf16[2,16,2048]{2,1,0:T(8,128)(2,1)S(1)}, u32[]{:S(2)}, u32[]{:S(2)}) collective-permute-start(bf16[2,16,2048]{2,1,0:T(8,128)(2,1)S(1)} %collective-permute-done.16), channel_id=1, source_target_pairs={{0,32},{4,36},{8,40},{12,44},{16,48},{20,52},{24,56},{28,60},{32,6... | collective-permute-start | bytes 393224 | tf_op jit(solution)/shard_map/ppermute | solution.py:201
  132.3 9.7 %collective-permute-start.23 = (bf16[2,16,2048]{2,1,0:T(8,128)(2,1)S(1)}, bf16[2,16,2048]{2,1,0:T(8,128)(2,1)S(1)}, u32[]{:S(2)}, u32[]{:S(2)}) collective-permute-start(bf16[2,16,2048]{2,1,0:T(8,128)(2,1)S(1)} %collective-permute-done.22), channel_id=1, source_target_pairs={{0,96},{4,100},{8,104},{12,108},{16,112},{20,116},{24,120},{28,124... | collective-permute-start | bytes 393224 | tf_op jit(solution)/shard_map/ppermute | solution.py:201
  136.5 36.9 %collective-permute-start.1 = (bf16[2,128,2048]{2,1,0:T(8,128)(2,1)S(1)}, bf16[2,128,2048]{2,1,0:T(8,128)(2,1)S(1)}, u32[]{:S(2)}, u32[]{:S(2)}) collective-permute-start(bf16[2,128,2048]{2,1,0:T(8,128)(2,1)S(1)} %pad_maximum_fusion.5), channel_id=1, source_target_pairs={{0,1},{1,0},{2,3},{3,2},{4,5},{5,4},{6,7},{7,6},{8,9},{9,8},{10,11... | collective-permute-start | bytes 3145736 | tf_op jit(solution)/shard_map/ppermute | solution.py:110
  138.2 18.0 %collective-permute-start.6 = (bf16[2,4,16,2048]{3,2,1,0:T(8,128)(2,1)S(1)}, bf16[2,4,16,2048]{3,2,1,0:T(8,128)(2,1)S(1)}, u32[]{:S(2)}, u32[]{:S(2)}) collective-permute-start(bf16[2,4,16,2048]{3,2,1,0:T(8,128)(2,1)S(1)} %bitcast_dynamic-update-slice_fusion.32), channel_id=1, source_target_pairs={{0,32},{4,36},{8,40},{12,44},{16,48},{20,52},{24,56},{28,60},{32,6... | collective-permute-start | bytes 1572872 | tf_op jit(solution)/shard_map/ppermute | solution.py:193
  141.1 16.3 %collective-permute-start.12 = (bf16[2,4,16,2048]{3,2,1,0:T(8,128)(2,1)S(1)}, bf16[2,4,16,2048]{3,2,1,0:T(8,128)(2,1)S(1)}, u32[]{:S(2)}, u32[]{:S(2)}) collective-permute-start(bf16[2,4,16,2048]{3,2,1,0:T(8,128)(2,1)S(1)} %bitcast_dynamic-update-slice_fusion.28), channel_id=1, source_target_pairs={{0,96},{4,100},{8,104},{12,108},{16,112},{20,116},{24,120},{28,124... | collective-permute-start | bytes 1572872 | tf_op jit(solution)/shard_map/ppermute | solution.py:193
  141.9 18.7 %collective-permute-start.18 = (bf16[4,2,16,2048]{3,2,1,0:T(8,128)(2,1)S(1)}, bf16[4,2,16,2048]{3,2,1,0:T(8,128)(2,1)S(1)}, u32[]{:S(2)}, u32[]{:S(2)}) collective-permute-start(bf16[4,2,16,2048]{3,2,1,0:T(8,128)(2,1)S(1)} %bitcast_dynamic-update-slice_fusion.49), channel_id=1, source_target_pairs={{0,4},{4,8},{8,12},{12,0},{16,20},{20,24},{24,28},{28,16},{32,36},... | collective-permute-start | bytes 1572872 | tf_op jit(solution)/shard_map/ppermute | solution.py:207
  142.1 19.7 %collective-permute-start.24 = (bf16[4,2,16,2048]{3,2,1,0:T(8,128)(2,1)S(1)}, bf16[4,2,16,2048]{3,2,1,0:T(8,128)(2,1)S(1)}, u32[]{:S(2)}, u32[]{:S(2)}) collective-permute-start(bf16[4,2,16,2048]{3,2,1,0:T(8,128)(2,1)S(1)} %bitcast_dynamic-update-slice_fusion.45), channel_id=1, source_target_pairs={{0,12},{4,0},{8,4},{12,8},{16,28},{20,16},{24,20},{28,24},{32,44},... | collective-permute-start | bytes 1572872 | tf_op jit(solution)/shard_map/ppermute | solution.py:207
  156.2 17.1 %collective-permute-start.7 = (bf16[2,4,16,2048]{3,2,1,0:T(8,128)(2,1)S(1)}, bf16[2,4,16,2048]{3,2,1,0:T(8,128)(2,1)S(1)}, u32[]{:S(2)}, u32[]{:S(2)}) collective-permute-start(bf16[2,4,16,2048]{3,2,1,0:T(8,128)(2,1)S(1)} %collective-permute-done.6), channel_id=1, source_target_pairs={{0,32},{4,36},{8,40},{12,44},{16,48},{20,52},{24,56},{28,60},{32,6... | collective-permute-start | bytes 1572872 | tf_op jit(solution)/shard_map/ppermute | solution.py:193
  157.4 19.0 %collective-permute-start.13 = (bf16[2,4,16,2048]{3,2,1,0:T(8,128)(2,1)S(1)}, bf16[2,4,16,2048]{3,2,1,0:T(8,128)(2,1)S(1)}, u32[]{:S(2)}, u32[]{:S(2)}) collective-permute-start(bf16[2,4,16,2048]{3,2,1,0:T(8,128)(2,1)S(1)} %collective-permute-done.12), channel_id=1, source_target_pairs={{0,96},{4,100},{8,104},{12,108},{16,112},{20,116},{24,120},{28,124... | collective-permute-start | bytes 1572872 | tf_op jit(solution)/shard_map/ppermute | solution.py:193
  160.7 18.9 %collective-permute-start.19 = (bf16[4,2,16,2048]{3,2,1,0:T(8,128)(2,1)S(1)}, bf16[4,2,16,2048]{3,2,1,0:T(8,128)(2,1)S(1)}, u32[]{:S(2)}, u32[]{:S(2)}) collective-permute-start(bf16[4,2,16,2048]{3,2,1,0:T(8,128)(2,1)S(1)} %collective-permute-done.18), channel_id=1, source_target_pairs={{0,4},{4,8},{8,12},{12,0},{16,20},{20,24},{24,28},{28,16},{32,36},... | collective-permute-start | bytes 1572872 | tf_op jit(solution)/shard_map/ppermute | solution.py:207
  161.7 19.9 %collective-permute-start.25 = (bf16[4,2,16,2048]{3,2,1,0:T(8,128)(2,1)S(1)}, bf16[4,2,16,2048]{3,2,1,0:T(8,128)(2,1)S(1)}, u32[]{:S(2)}, u32[]{:S(2)}) collective-permute-start(bf16[4,2,16,2048]{3,2,1,0:T(8,128)(2,1)S(1)} %collective-permute-done.24), channel_id=1, source_target_pairs={{0,12},{4,0},{8,4},{12,8},{16,28},{20,16},{24,20},{28,24},{32,44},... | collective-permute-start | bytes 1572872 | tf_op jit(solution)/shard_map/ppermute | solution.py:207
  173.3 21.0 %collective-permute-start.8 = (bf16[2,4,16,2048]{3,2,1,0:T(8,128)(2,1)S(1)}, bf16[2,4,16,2048]{3,2,1,0:T(8,128)(2,1)S(1)}, u32[]{:S(2)}, u32[]{:S(2)}) collective-permute-start(bf16[2,4,16,2048]{3,2,1,0:T(8,128)(2,1)S(1)} %collective-permute-done.7), channel_id=1, source_target_pairs={{0,32},{4,36},{8,40},{12,44},{16,48},{20,52},{24,56},{28,60},{32,6... | collective-permute-start | bytes 1572872 | tf_op jit(solution)/shard_map/ppermute | solution.py:193
  176.3 23.9 %collective-permute-start.14 = (bf16[2,4,16,2048]{3,2,1,0:T(8,128)(2,1)S(1)}, bf16[2,4,16,2048]{3,2,1,0:T(8,128)(2,1)S(1)}, u32[]{:S(2)}, u32[]{:S(2)}) collective-permute-start(bf16[2,4,16,2048]{3,2,1,0:T(8,128)(2,1)S(1)} %collective-permute-done.13), channel_id=1, source_target_pairs={{0,96},{4,100},{8,104},{12,108},{16,112},{20,116},{24,120},{28,124... | collective-permute-start | bytes 1572872 | tf_op jit(solution)/shard_map/ppermute | solution.py:193
  179.6 24.8 %collective-permute-start.20 = (bf16[4,2,16,2048]{3,2,1,0:T(8,128)(2,1)S(1)}, bf16[4,2,16,2048]{3,2,1,0:T(8,128)(2,1)S(1)}, u32[]{:S(2)}, u32[]{:S(2)}) collective-permute-start(bf16[4,2,16,2048]{3,2,1,0:T(8,128)(2,1)S(1)} %collective-permute-done.19), channel_id=1, source_target_pairs={{0,4},{4,8},{8,12},{12,0},{16,20},{20,24},{24,28},{28,16},{32,36},... | collective-permute-start | bytes 1572872 | tf_op jit(solution)/shard_map/ppermute | solution.py:207
  181.6 23.0 %collective-permute-start.26 = (bf16[4,2,16,2048]{3,2,1,0:T(8,128)(2,1)S(1)}, bf16[4,2,16,2048]{3,2,1,0:T(8,128)(2,1)S(1)}, u32[]{:S(2)}, u32[]{:S(2)}) collective-permute-start(bf16[4,2,16,2048]{3,2,1,0:T(8,128)(2,1)S(1)} %collective-permute-done.25), channel_id=1, source_target_pairs={{0,12},{4,0},{8,4},{12,8},{16,28},{20,16},{24,20},{28,24},{32,44},... | collective-permute-start | bytes 1572872 | tf_op jit(solution)/shard_map/ppermute | solution.py:207
  249.4 15.4 %collective-permute-start.53 = (bf16[128,2048]{1,0:T(8,128)(2,1)S(1)}, bf16[128,2048]{1,0:T(8,128)(2,1)}, u32[]{:S(2)}, u32[]{:S(2)}) collective-permute-start(bf16[128,2048]{1,0:T(8,128)(2,1)S(1)} %fusion.89), channel_id=1, source_target_pairs={{0,2},{2,0},{1,3},{3,1},{4,6},{6,4},{5,7},{7,5},{8,10},{10,8},{9,1... | collective-permute-start | bytes 1572872 | tf_op jit(solution)/shard_map/ppermute | solution.py:119
  250.9 25.2 %collective-permute-start.58 = (bf16[128,2048]{1,0:T(8,128)(2,1)S(1)}, bf16[128,2048]{1,0:T(8,128)(2,1)}, u32[]{:S(2)}, u32[]{:S(2)}) collective-permute-start(bf16[128,2048]{1,0:T(8,128)(2,1)S(1)} %bitcast.530), channel_id=1, source_target_pairs={{0,2},{2,0},{1,3},{3,1},{4,6},{6,4},{5,7},{7,5},{8,10},{10,8},{9,1... | collective-permute-start | bytes 1572872 | tf_op jit(solution)/shard_map/ppermute | solution.py:108
  267.1 19.3 %collective-permute-start.54 = (bf16[128,2048]{1,0:T(8,128)(2,1)S(1)}, bf16[128,2048]{1,0:T(8,128)(2,1)S(1)}, u32[]{:S(2)}, u32[]{:S(2)}) collective-permute-start(bf16[128,2048]{1,0:T(8,128)(2,1)S(1)} %multiply_convert_fusion.4), channel_id=1, source_target_pairs={{0,2},{2,0},{1,3},{3,1},{4,6},{6,4},{5,7},{7,5},{8,10},{10,8},{9,1... | collective-permute-start | bytes 1572872 | tf_op jit(solution)/shard_map/ppermute | solution.py:108
  277.2 9.4 %collective-permute-start.59 = (bf16[2,128,2048]{2,1,0:T(8,128)(2,1)S(1)}, bf16[2,128,2048]{2,1,0:T(8,128)(2,1)S(1)}, u32[]{:S(2)}, u32[]{:S(2)}) collective-permute-start(bf16[2,128,2048]{2,1,0:T(8,128)(2,1)S(1)} %pad_maximum_fusion.7), channel_id=1, source_target_pairs={{0,1},{1,0},{2,3},{3,2},{4,5},{5,4},{6,7},{7,6},{8,9},{9,8},{10,11... | collective-permute-start | bytes 3145736 | tf_op jit(solution)/shard_map/ppermute | solution.py:110
  343.9 7.6 %collective-permute-start.60 = (f32[2,128,2048]{2,1,0:T(8,128)S(1)}, f32[2,128,2048]{2,1,0:T(8,128)S(1)}, u32[]{:S(2)}, u32[]{:S(2)}) collective-permute-start(f32[2,128,2048]{2,1,0:T(8,128)S(1)} %bitcast.548), channel_id=1, source_target_pairs={{0,1},{1,0},{2,3},{3,2},{4,5},{5,4},{6,7},{7,6},{8,9},{9,8},{10,11... | collective-permute-start | bytes 6291464 | tf_op jit(solution)/shard_map/ppermute | solution.py:116
  351.7 18.6 %collective-permute-start.61 = (bf16[128,2048]{1,0:T(8,128)(2,1)S(1)}, bf16[128,2048]{1,0:T(8,128)(2,1)S(1)}, u32[]{:S(2)}, u32[]{:S(2)}) collective-permute-start(bf16[128,2048]{1,0:T(8,128)(2,1)S(1)} %fusion.79), channel_id=1, source_target_pairs={{0,2},{2,0},{1,3},{3,1},{4,6},{6,4},{5,7},{7,5},{8,10},{10,8},{9,1... | collective-permute-start | bytes 1572872 | tf_op jit(solution)/shard_map/ppermute | solution.py:119
  355.5 29.3 %collective-permute-start.57 = (bf16[128,2048]{1,0:T(8,128)(2,1)S(1)}, bf16[128,2048]{1,0:T(8,128)(2,1)S(1)}, u32[]{:S(2)}, u32[]{:S(2)}) collective-permute-start(bf16[128,2048]{1,0:T(8,128)(2,1)S(1)} %fusion.83), channel_id=1, source_target_pairs={{0,2},{2,0},{1,3},{3,1},{4,6},{6,4},{5,7},{7,5},{8,10},{10,8},{9,1... | collective-permute-start | bytes 1572872 | tf_op jit(solution)/shard_map/ppermute | solution.py:119
  386.5 17.9 %collective-permute-start.62 = (bf16[128,2048]{1,0:T(8,128)(2,1)S(1)}, bf16[128,2048]{1,0:T(8,128)(2,1)S(1)}, u32[]{:S(2)}, u32[]{:S(2)}) collective-permute-start(bf16[128,2048]{1,0:T(8,128)(2,1)S(1)} %get-tuple-element.25), channel_id=1, source_target_pairs={{0,2},{2,0},{1,3},{3,1},{4,6},{6,4},{5,7},{7,5},{8,10},{10,8},{9,1... | collective-permute-start | bytes 1572872 | tf_op jit(solution)/shard_map/ppermute | solution.py:108
  462.9 32.0 %collective-permute-start.66 = (bf16[4,2,64,1280]{3,2,1,0:T(8,128)(2,1)S(1)}, bf16[4,2,64,1280]{3,2,1,0:T(8,128)(2,1)S(1)}, u32[]{:S(2)}, u32[]{:S(2)}) collective-permute-start(bf16[4,2,64,1280]{3,2,1,0:T(8,128)(2,1)S(1)} %dynamic-slice_bitcast_fusion.1), channel_id=1, source_target_pairs={{0,4},{4,8},{8,12},{12,0},{16,20},{20,24},{24,28},{28,16},{32,36},... | collective-permute-start | bytes 3932168 | tf_op jit(solution)/shard_map/ppermute | solution.py:148
  471.7 31.4 %collective-permute-start.72 = (bf16[4,2,64,1280]{3,2,1,0:T(8,128)(2,1)}, bf16[4,2,64,1280]{3,2,1,0:T(8,128)(2,1)}, u32[]{:S(2)}, u32[]{:S(2)}) collective-permute-start(bf16[4,2,64,1280]{3,2,1,0:T(8,128)(2,1)} %dynamic-slice_bitcast_fusion), channel_id=1, source_target_pairs={{0,12},{4,0},{8,4},{12,8},{16,28},{20,16},{24,20},{28,24},{32,44},... | collective-permute-start | bytes 3932168 | tf_op jit(solution)/shard_map/ppermute | solution.py:148
  480.2 52.3 %collective-permute-start.64 = (f32[2,128,2048]{2,1,0:T(8,128)}, f32[2,128,2048]{2,1,0:T(8,128)S(1)}, u32[]{:S(2)}, u32[]{:S(2)}) collective-permute-start(f32[2,128,2048]{2,1,0:T(8,128)} %bitcast.155), channel_id=1, source_target_pairs={{0,1},{1,0},{2,3},{3,2},{4,5},{5,4},{6,7},{7,6},{8,9},{9,8},{10,11... | collective-permute-start | bytes 6291464 | tf_op jit(solution)/shard_map/ppermute | solution.py:116
  497.7 31.7 %collective-permute-start.67 = (bf16[4,2,64,1280]{3,2,1,0:T(8,128)(2,1)}, bf16[4,2,64,1280]{3,2,1,0:T(8,128)(2,1)}, u32[]{:S(2)}, u32[]{:S(2)}) collective-permute-start(bf16[4,2,64,1280]{3,2,1,0:T(8,128)(2,1)} %fusion.19), channel_id=1, source_target_pairs={{0,4},{4,8},{8,12},{12,0},{16,20},{20,24},{24,28},{28,16},{32,36},... | collective-permute-start | bytes 3932168 | tf_op jit(solution)/shard_map/ppermute | solution.py:148
  506.1 31.1 %collective-permute-start.73 = (bf16[4,2,64,1280]{3,2,1,0:T(8,128)(2,1)}, bf16[4,2,64,1280]{3,2,1,0:T(8,128)(2,1)}, u32[]{:S(2)}, u32[]{:S(2)}) collective-permute-start(bf16[4,2,64,1280]{3,2,1,0:T(8,128)(2,1)} %fusion.16), channel_id=1, source_target_pairs={{0,12},{4,0},{8,4},{12,8},{16,28},{20,16},{24,20},{28,24},{32,44},... | collective-permute-start | bytes 3932168 | tf_op jit(solution)/shard_map/ppermute | solution.py:148
  532.5 44.2 %collective-permute-start.68 = (bf16[4,2,64,1280]{3,2,1,0:T(8,128)(2,1)}, bf16[4,2,64,1280]{3,2,1,0:T(8,128)(2,1)}, u32[]{:S(2)}, u32[]{:S(2)}) collective-permute-start(bf16[4,2,64,1280]{3,2,1,0:T(8,128)(2,1)} %fusion.20), channel_id=1, source_target_pairs={{0,4},{4,8},{8,12},{12,0},{16,20},{20,24},{24,28},{28,16},{32,36},... | collective-permute-start | bytes 3932168 | tf_op jit(solution)/shard_map/ppermute | solution.py:148
  534.0 13.4 %collective-permute-start.65 = (bf16[128,2048]{1,0:T(8,128)(2,1)S(1)}, bf16[128,2048]{1,0:T(8,128)(2,1)S(1)}, u32[]{:S(2)}, u32[]{:S(2)}) collective-permute-start(bf16[128,2048]{1,0:T(8,128)(2,1)S(1)} %fusion.75), channel_id=1, source_target_pairs={{0,2},{2,0},{1,3},{3,1},{4,6},{6,4},{5,7},{7,5},{8,10},{10,8},{9,1... | collective-permute-start | bytes 1572872 | tf_op jit(solution)/shard_map/ppermute | solution.py:119
  540.2 43.9 %collective-permute-start.74 = (bf16[4,2,64,1280]{3,2,1,0:T(8,128)(2,1)}, bf16[4,2,64,1280]{3,2,1,0:T(8,128)(2,1)}, u32[]{:S(2)}, u32[]{:S(2)}) collective-permute-start(bf16[4,2,64,1280]{3,2,1,0:T(8,128)(2,1)} %fusion.17), channel_id=1, source_target_pairs={{0,12},{4,0},{8,4},{12,8},{16,28},{20,16},{24,20},{28,24},{32,44},... | collective-permute-start | bytes 3932168 | tf_op jit(solution)/shard_map/ppermute | solution.py:148
  550.9 69.5 %all-to-all-start.1 = ((f32[128,3,16]{2,1,0:T(4,128)}), f32[128,3,16]{2,1,0:T(4,128)S(1)}, u32[]{:S(2)}, u32[]{:S(2)}) async-start(f32[128,3,16]{2,1,0:T(4,128)} %copy.215), calls=%async_computation.1 | async-start | bytes 524288 | tf_op jit(solution)/shard_map/all_to_all | solution.py:222
  578.9 15.5 %collective-permute-start.69 = (bf16[2,64,1280]{2,1,0:T(8,128)(2,1)S(1)}, bf16[2,64,1280]{2,1,0:T(8,128)(2,1)S(1)}, u32[]{:S(2)}, u32[]{:S(2)}) collective-permute-start(bf16[2,64,1280]{2,1,0:T(8,128)(2,1)S(1)} %dynamic-slice_bitcast_fusion.3), channel_id=1, source_target_pairs={{0,32},{4,36},{8,40},{12,44},{16,48},{20,52},{24,56},{28,60},{32,6... | collective-permute-start | bytes 983048 | tf_op jit(solution)/shard_map/ppermute | solution.py:148
  586.1 12.0 %collective-permute-start.75 = (bf16[2,64,1280]{2,1,0:T(8,128)(2,1)S(1)}, bf16[2,64,1280]{2,1,0:T(8,128)(2,1)S(1)}, u32[]{:S(2)}, u32[]{:S(2)}) collective-permute-start(bf16[2,64,1280]{2,1,0:T(8,128)(2,1)S(1)} %dynamic-slice_bitcast_fusion.2), channel_id=1, source_target_pairs={{0,96},{4,100},{8,104},{12,108},{16,112},{20,116},{24,120},{28,124... | collective-permute-start | bytes 983048 | tf_op jit(solution)/shard_map/ppermute | solution.py:148
  594.5 9.3 %collective-permute-start.70 = (bf16[2,64,1280]{2,1,0:T(8,128)(2,1)S(1)}, bf16[2,64,1280]{2,1,0:T(8,128)(2,1)S(1)}, u32[]{:S(2)}, u32[]{:S(2)}) collective-permute-start(bf16[2,64,1280]{2,1,0:T(8,128)(2,1)S(1)} %fusion.112), channel_id=1, source_target_pairs={{0,32},{4,36},{8,40},{12,44},{16,48},{20,52},{24,56},{28,60},{32,6... | collective-permute-start | bytes 983048 | tf_op jit(solution)/shard_map/ppermute | solution.py:148
  598.2 9.5 %collective-permute-start.76 = (bf16[2,64,1280]{2,1,0:T(8,128)(2,1)S(1)}, bf16[2,64,1280]{2,1,0:T(8,128)(2,1)S(1)}, u32[]{:S(2)}, u32[]{:S(2)}) collective-permute-start(bf16[2,64,1280]{2,1,0:T(8,128)(2,1)S(1)} %fusion.110), channel_id=1, source_target_pairs={{0,96},{4,100},{8,104},{12,108},{16,112},{20,116},{24,120},{28,124... | collective-permute-start | bytes 983048 | tf_op jit(solution)/shard_map/ppermute | solution.py:148
  603.9 9.2 %collective-permute-start.71 = (bf16[2,64,1280]{2,1,0:T(8,128)(2,1)S(1)}, bf16[2,64,1280]{2,1,0:T(8,128)(2,1)S(1)}, u32[]{:S(2)}, u32[]{:S(2)}) collective-permute-start(bf16[2,64,1280]{2,1,0:T(8,128)(2,1)S(1)} %fusion.113), channel_id=1, source_target_pairs={{0,32},{4,36},{8,40},{12,44},{16,48},{20,52},{24,56},{28,60},{32,6... | collective-permute-start | bytes 983048 | tf_op jit(solution)/shard_map/ppermute | solution.py:148
  607.8 9.3 %collective-permute-start.77 = (bf16[2,64,1280]{2,1,0:T(8,128)(2,1)S(1)}, bf16[2,64,1280]{2,1,0:T(8,128)(2,1)S(1)}, u32[]{:S(2)}, u32[]{:S(2)}) collective-permute-start(bf16[2,64,1280]{2,1,0:T(8,128)(2,1)S(1)} %fusion.111), channel_id=1, source_target_pairs={{0,96},{4,100},{8,104},{12,108},{16,112},{20,116},{24,120},{28,124... | collective-permute-start | bytes 983048 | tf_op jit(solution)/shard_map/ppermute | solution.py:148
  617.2 8.7 %collective-permute-start.78 = (bf16[64,2560]{1,0:T(8,128)(2,1)S(1)}, bf16[64,2560]{1,0:T(8,128)(2,1)S(1)}, u32[]{:S(2)}, u32[]{:S(2)}) collective-permute-start(bf16[64,2560]{1,0:T(8,128)(2,1)S(1)} %fusion.126), channel_id=1, source_target_pairs={{0,16},{4,20},{8,24},{12,28},{16,0},{20,4},{24,8},{28,12},{32,48},... | collective-permute-start | bytes 983048 | tf_op jit(solution)/shard_map/ppermute | solution.py:163
  (67 other events, 413.1 us)
Sparse Core Ops, SparseCore 0:
  29.0 176.0 all-gather.1
  332.2 290.2 reduce-scatter.1

commit v16 on v14

--- a/solution.py
+++ b/solution.py
@@ -133,11 +133,11 @@
     return pairs
 
 
-def ring_stage(chunks, pos, stride, size, step):
+def ring_stage(chunks, axis, pos, stride, size, step):
     pairs = ring_pairs(step, stride, size)
 
     def pick(k):
-        return lax.dynamic_index_in_dim(chunks, (pos - k * step) % size, 0, keepdims=False).astype(
+        return lax.dynamic_index_in_dim(chunks, (pos - k * step) % size, axis, keepdims=False).astype(
             jnp.float32
         )
 
@@ -152,20 +152,15 @@
     index = lax.axis_index("dp")
     x_pos, y_pos, z_pos = index % 4, (index // 4) % 2, index // 8
     blocks = values.reshape((4, 2, 4, -1) + values.shape[1:])
-    part_rows = blocks.shape[3] // 4
-    pieces = []
-    for part, (x_first, step) in enumerate(((True, 1), (True, 3), (False, 1), (False, 3))):
-        rows = blocks[:, :, :, part * part_rows : (part + 1) * part_rows]
-        if x_first:
-            once = ring_stage(jnp.moveaxis(rows, 2, 0), x_pos, 1, 4, step)
-            twice = ring_stage(once.astype(jnp.bfloat16), z_pos, 8, 4, step)
-        else:
-            once = ring_stage(rows, z_pos, 8, 4, step)
-            twice = ring_stage(jnp.moveaxis(once, 1, 0).astype(jnp.bfloat16), x_pos, 1, 4, step)
-        pieces.append(twice)
-    both = jnp.concatenate(pieces, axis=1)
-    keep = lax.dynamic_index_in_dim(both, y_pos, 0, keepdims=False)
-    give = lax.dynamic_index_in_dim(both, 1 - y_pos, 0, keepdims=False)
+    half = blocks.shape[3] // 2
+    result = []
+    for step, rows in ((1, slice(0, half)), (3, slice(half, None))):
+        part = blocks[:, :, :, rows]
+        along_x = ring_stage(part, 2, x_pos, 1, 4, step)
+        result.append(ring_stage(along_x.astype(jnp.bfloat16), 0, z_pos, 8, 4, step))
+    along_z = jnp.concatenate(result, axis=1)
+    keep = lax.dynamic_index_in_dim(along_z, y_pos, 0, keepdims=False)
+    give = lax.dynamic_index_in_dim(along_z, 1 - y_pos, 0, keepdims=False)
     pair = [(i, i ^ 4) for i in range(32)]
     return keep + lax.ppermute(give.astype(jnp.bfloat16), "dp", pair).astype(jnp.float32)
 

time: 613 us -> 614 us (level); the launches traced: 603 us -> 610 us
  matrix products: 79 us -> 89.4 us
  waiting for transfers between devices: 257 us -> 250 us
  other arithmetic: 39.4 us -> 46.2 us
    reduce_scatter x1, waiting for transfers between devices: 67.7 us -> 0.01 us  [shards(): lax.psum_scatter(mlp_grads, 'dp', scatter_dimension=0, tiled=True)]
    ppermute x24 -> x12, waiting for transfers between devices: 40.7 us -> 96.6 us  [ring_stage(): got = lax.ppermute(acc.astype(jnp.bfloat16), 'dp', pairs)]
    ppermute x24 -> x12, starting transfers between devices: 40.5 us -> 19 us  [ring_stage(): got = lax.ppermute(acc.astype(jnp.bfloat16), 'dp', pairs)]
    ppermute x4, starting transfers between devices: 4.99 us -> 19.9 us  [row_sum(): lax.ppermute(theirs.astype(jnp.bfloat16), 'tensor', ACROSS)]
    convert_element_type x16 -> x8, other arithmetic: 1.58 us -> 11.9 us  [ring_stage(): got = lax.ppermute(acc.astype(jnp.bfloat16), 'dp', pairs)]
    all_to_all x1, waiting for transfers between devices: 8.77 us -> 0.01 us  [small_sum(): lax.all_to_all(jnp.swapaxes(blocks, 0, 1), ('dp', 'tensor'), 0, 0, tiled=...]
    dot_general x8, matrix products: 24.8 us -> 31.9 us  [times_trans(): lax.dot_general(left, right, (((1,), (1,)), ((), ())), preferred_element_...]
    unnamed x97 -> x85, local copies, waits for them, and re-layouts: 16.1 us -> 14 us
  transfers between devices with their start and end apart: 70 -> 58, of which waited for: 28 -> 26; matrix products, arithmetic and copies ran while one was open for 24% -> 29% of each run, Pallas kernels for 4% -> 2%
where the time goes in v16:
time: 614 us; the launch traced here: 610 us
  waiting for transfers between devices  250 us (41%)
  starting transfers between devices  106 us (17%)
  matrix products  89.4 us (15%)
  local copies, waits for them, and re-layouts  76.2 us (12%)
  other arithmetic  46.2 us (8%)
  Pallas kernels  26.6 us (4%)
  between operations  15.7 us (3%)
    ppermute x12, waiting for transfers between devices, ring_stage(): got = lax.ppermute(acc.astype(jnp.bfloat16), 'dp', pairs)  96.6 us
    ppermute x24, waiting for transfers between devices, ring_gather(): cur = lax.ppermute(cur, 'dp', pairs)  56.2 us
    ppermute x4, waiting for transfers between devices, row_sum(): lax.ppermute(theirs.astype(jnp.bfloat16), 'tensor', ACROSS)  43.6 us
    ppermute x24, starting transfers between devices, ring_gather(): cur = lax.ppermute(cur, 'dp', pairs)  39.7 us
    dot_general x8, matrix products, matmul_plain(): return jnp.dot(left, right, preferred_element_type=jnp.float32)  39.2 us
    ppermute x4, waiting for transfers between devices, row_gather(): across = lax.ppermute(values, 'tensor', ACROSS)  32.9 us
    dot_general x8, matrix products, times_trans(): lax.dot_general(left, right, (((1,), (1,)), ((), ())), preferred_element_...  31.9 us
    pallas_call x2, Pallas kernels, grad_pack(): pl.pallas_call(functools.partial(pack_kernel, per), grid=(rows_out // til...  26.6 us
  transfers between devices with their start and end apart: 58, of which 26 were waited for; matrix products, arithmetic and copies ran while one was open for 29% of the time, Pallas kernels for 2%

profile of v16, /device:TPU:0, one launch (start us, length us, event | category | flops | bytes accessed | tf_op | source)
XLA Modules:
  0.0 610.0 jit_solution(5588349936828394970)
XLA Ops:
  11.5 3.3 collective-permute-start.2
  16.2 8.9 %all-to-all-start = ((f32[128,3,16]{2,1,0:T(4,128)}), f32[128,3,16]{2,1,0:T(4,128)S(1)}, u32[]{:S(2)}, u32[]{:S(2)}) async-start(f32[128,3,16]{2,1,0:T(4,128)} %broadcast_in_dim.155), calls=%async_computation | async-start | bytes 524288 | tf_op jit(solution)/shard_map/all_to_all | solution.py:217
  29.3 6.6 %all-to-all-done = f32[128,3,16]{2,1,0:T(4,128)S(1)} async-done(((f32[128,3,16]{2,1,0:T(4,128)}), f32[128,3,16]{2,1,0:T(4,128)S(1)}, u32[]{:S(2)}, u32[]{:S(2)}) %all-to-all-start) | async-done | bytes 24608 | tf_op jit(solution)/shard_map/all_to_all | solution.py:217
  48.5 3.2 collective-permute-start.10
  51.7 3.2 collective-permute-start.22
  57.7 3.2 collective-permute-start.11
  61.0 3.1 collective-permute-start.23
  66.3 3.2 collective-permute-start.12
  70.3 3.3 collective-permute-start.24
  74.8 15.0 %collective-permute-done.6 = bf16[2,4,16,2560]{3,2,1,0:T(8,128)(2,1)} collective-permute-done((bf16[2,4,16,2560]{3,2,1,0:T(8,128)(2,1)S(1)}, bf16[2,4,16,2560]{3,2,1,0:T(8,128)(2,1)}, u32[]{:S(2)}, u32[]{:S(2)}) %collective-permute-start.6) | collective-permute-done | bytes 655392 | tf_op jit(solution)/shard_map/ppermute | solution.py:195
  89.8 3.8 collective-permute-start.13
  93.6 9.1 %collective-permute-done.18 = bf16[4,2,16,2560]{3,2,1,0:T(8,128)(2,1)} collective-permute-done((bf16[4,2,16,2560]{3,2,1,0:T(8,128)(2,1)}, bf16[4,2,16,2560]{3,2,1,0:T(8,128)(2,1)}, u32[]{:S(2)}, u32[]{:S(2)}) %collective-permute-start.18) | collective-permute-done | bytes 655392 | tf_op jit(solution)/shard_map/ppermute | solution.py:209
  102.7 3.2 collective-permute-start.25
  110.0 3.2 collective-permute-start.14
  113.2 8.7 %collective-permute-done.19 = bf16[4,2,16,2560]{3,2,1,0:T(8,128)(2,1)S(1)} collective-permute-done((bf16[4,2,16,2560]{3,2,1,0:T(8,128)(2,1)}, bf16[4,2,16,2560]{3,2,1,0:T(8,128)(2,1)S(1)}, u32[]{:S(2)}, u32[]{:S(2)}) %collective-permute-start.19) | collective-permute-done | bytes 655392 | tf_op jit(solution)/shard_map/ppermute | solution.py:209
  121.9 3.2 collective-permute-start.26
  132.6 20.7 %collective-permute-done.20 = bf16[4,2,16,2560]{3,2,1,0:T(8,128)(2,1)S(1)} collective-permute-done((bf16[4,2,16,2560]{3,2,1,0:T(8,128)(2,1)S(1)}, bf16[4,2,16,2560]{3,2,1,0:T(8,128)(2,1)S(1)}, u32[]{:S(2)}, u32[]{:S(2)}) %collective-permute-start.20) | collective-permute-done | bytes 655392 | tf_op jit(solution)/shard_map/ppermute | solution.py:209
  154.8 3.0 slice_bitcast_fusion
  160.4 3.9 copy.151
  164.4 4.0 copy.153
  170.9 3.6 fusion.57
  180.7 3.0 fusion.26
  189.2 5.2 fusion.75
  194.5 3.1 fusion.30
  197.9 4.1 collective-permute-done.27
  202.2 14.2 %collective-permute-start.28 = (bf16[128,2048]{1,0:T(8,128)(2,1)S(1)}, bf16[128,2048]{1,0:T(8,128)(2,1)}, u32[]{:S(2)}, u32[]{:S(2)}) collective-permute-start(bf16[128,2048]{1,0:T(8,128)(2,1)S(1)} %fusion.93), channel_id=1, source_target_pairs={{0,2},{2,0},{1,3},{3,1},{4,6},{6,4},{5,7},{7,5},{8,10},{10,8},{9,1... | collective-permute-start | bytes 1572872 | tf_op jit(solution)/shard_map/ppermute | solution.py:119
  217.1 12.8 %collective-permute-done.28 = bf16[128,2048]{1,0:T(8,128)(2,1)} collective-permute-done((bf16[128,2048]{1,0:T(8,128)(2,1)S(1)}, bf16[128,2048]{1,0:T(8,128)(2,1)}, u32[]{:S(2)}, u32[]{:S(2)}) %collective-permute-start.28) | collective-permute-done | bytes 524320 | tf_op jit(solution)/shard_map/ppermute | solution.py:119
  233.6 7.5 %collective-permute-done.33 = bf16[128,2048]{1,0:T(8,128)(2,1)} collective-permute-done((bf16[128,2048]{1,0:T(8,128)(2,1)S(1)}, bf16[128,2048]{1,0:T(8,128)(2,1)}, u32[]{:S(2)}, u32[]{:S(2)}) %collective-permute-start.33) | collective-permute-done | bytes 524320 | tf_op jit(solution)/shard_map/ppermute | solution.py:108
  242.5 8.9 %collective-permute-done.29 = bf16[128,2048]{1,0:T(8,128)(2,1)S(1)} collective-permute-done((bf16[128,2048]{1,0:T(8,128)(2,1)S(1)}, bf16[128,2048]{1,0:T(8,128)(2,1)S(1)}, u32[]{:S(2)}, u32[]{:S(2)}) %collective-permute-start.29) | collective-permute-done | bytes 524320 | tf_op jit(solution)/shard_map/ppermute | solution.py:108
  255.8 8.4 %fusion = f32[512,1408]{1,0:T(8,128)} fusion(bf16[512,2048]{1,0:T(8,128)(2,1)} %bitcast.450, bf16[2048,4224]{1,0:T(8,128)(2,1)} %all-gather.2.cloned.1.call-done), kind=kOutput, calls=%fused_computation.1 | convolution fusion | flops 2952790016 | bytes 10747904 | tf_op jit(solution)/shard_map/dot_general | solution.py:27
  265.7 5.0 fusion.6
  270.7 6.6 %multiply_convert_fusion.1 = (bf16[512,1408]{1,0:T(8,128)(2,1)S(1)}, bf16[512,1408]{1,0:T(8,128)(2,1)S(1)}, bf16[512,1408]{1,0:T(8,128)(2,1)S(1)}) fusion(f32[512,1408]{1,0:T(8,128)} %fusion, f32[512,1408]{1,0:T(8,128)} %fusion.6, bf16[512,2048]{1,0:T(8,128)(2,1)S(1)} %bitcast.454, bf16[2048,4224]{1,0:T(8,128)(2,1)S(1)} %copy-done.38), kind=kOutput, calls=%fused_computation.17 | convolution fusion | flops 2963603456 | bytes 17956864 | tf_op jit(solution)/shard_map/dot_general | solution.py:27
  281.5 15.7 %shard_map.247 = bf16[2048,4224]{1,0:T(8,128)(2,1)} custom-call(bf16[512,2048]{1,0:T(8,128)(2,1)} %bitcast.452, bf16[512,2048]{1,0:T(8,128)(2,1)} %bitcast.451, bf16[512,4224]{1,0:T(8,128)(2,1)} %pad_maximum_fusion.right_ref), custom_call_target="tpu_custom_call" | custom-call | flops 8858370048 | bytes 25821184 | tf_op jit(solution)/shard_map/pallas_call | solution.py:64
  297.3 6.0 fusion.4
  303.3 5.5 fusion.12
  310.2 5.5 fusion.2
  322.0 13.8 %collective-permute-done.36 = bf16[128,2048]{1,0:T(8,128)(2,1)S(1)} collective-permute-done((bf16[128,2048]{1,0:T(8,128)(2,1)S(1)}, bf16[128,2048]{1,0:T(8,128)(2,1)S(1)}, u32[]{:S(2)}, u32[]{:S(2)}) %collective-permute-start.36) | collective-permute-done | bytes 524320 | tf_op jit(solution)/shard_map/ppermute | solution.py:119
  336.3 13.7 %collective-permute-done.32 = bf16[128,2048]{1,0:T(8,128)(2,1)S(1)} collective-permute-done((bf16[128,2048]{1,0:T(8,128)(2,1)S(1)}, bf16[128,2048]{1,0:T(8,128)(2,1)S(1)}, u32[]{:S(2)}, u32[]{:S(2)}) %collective-permute-start.32) | collective-permute-done | bytes 524320 | tf_op jit(solution)/shard_map/ppermute | solution.py:119
  353.1 16.5 %collective-permute-done.37 = bf16[128,2048]{1,0:T(8,128)(2,1)S(1)} collective-permute-done((bf16[128,2048]{1,0:T(8,128)(2,1)S(1)}, bf16[128,2048]{1,0:T(8,128)(2,1)S(1)}, u32[]{:S(2)}, u32[]{:S(2)}) %collective-permute-start.37) | collective-permute-done | bytes 524320 | tf_op jit(solution)/shard_map/ppermute | solution.py:108
  372.6 4.6 fusion.135
  380.2 3.2 fusion.60
  384.7 3.3 convolution_select_fusion
  399.4 10.8 %shard_map.246 = bf16[2048,2560]{1,0:T(8,128)(2,1)} custom-call(bf16[512,2048]{1,0:T(8,128)(2,1)} %bitcast.447, bf16[512,2048]{1,0:T(8,128)(2,1)} %bitcast.449, bf16[512,2560]{1,0:T(8,128)(2,1)} %constant_dynamic-update-slice_fusion.4.right_ref), custom_call_target="tpu_custom_call" | custom-call | flops 5368709120 | bytes 17301504 | tf_op jit(solution)/shard_map/pallas_call | solution.py:64
  410.2 9.5 %fusion.146 = (bf16[4,2,4,32,2560]{4,3,2,1,0:T(8,128)(2,1)}, bf16[4,2,4,32,2560]{4,3,2,1,0:T(8,128)(2,1)}) fusion(bf16[4,2,4,64,2560]{4,3,2,1,0:T(8,128)(2,1)} %bitcast.432), kind=kLoop, calls=%fused_computation.274 | loop fusion | bytes 20971520 | tf_op jit(solution)/shard_map/slice | solution.py:158
  422.3 2.9 fusion.39
  431.0 3.0 add_add_fusion
  438.6 3.2 collective-permute-start.47
  441.9 12.8 %collective-permute-done.41 = bf16[4,2,32,2560]{3,2,1,0:T(8,128)(2,1)} collective-permute-done((bf16[4,2,32,2560]{3,2,1,0:T(8,128)(2,1)}, bf16[4,2,32,2560]{3,2,1,0:T(8,128)(2,1)}, u32[]{:S(2)}, u32[]{:S(2)}) %collective-permute-start.41) | collective-permute-done | bytes 1310752 | tf_op jit(solution)/shard_map/ppermute | solution.py:146
  454.7 3.2 fusion.19
  459.2 11.1 %collective-permute-done.47 = bf16[4,2,32,2560]{3,2,1,0:T(8,128)(2,1)} collective-permute-done((bf16[4,2,32,2560]{3,2,1,0:T(8,128)(2,1)}, bf16[4,2,32,2560]{3,2,1,0:T(8,128)(2,1)}, u32[]{:S(2)}, u32[]{:S(2)}) %collective-permute-start.47) | collective-permute-done | bytes 1310752 | tf_op jit(solution)/shard_map/ppermute | solution.py:146
  470.4 3.1 fusion.16
  473.5 3.9 collective-permute-start.48
  481.2 8.4 %collective-permute-done.42 = bf16[4,2,32,2560]{3,2,1,0:T(8,128)(2,1)} collective-permute-done((bf16[4,2,32,2560]{3,2,1,0:T(8,128)(2,1)}, bf16[4,2,32,2560]{3,2,1,0:T(8,128)(2,1)}, u32[]{:S(2)}, u32[]{:S(2)}) %collective-permute-start.42) | collective-permute-done | bytes 1310752 | tf_op jit(solution)/shard_map/ppermute | solution.py:146
  489.6 3.1 fusion.20
  492.7 3.4 collective-permute-done.40
  499.6 7.0 %all-to-all-start.1 = ((f32[128,3,16]{2,1,0:T(4,128)}), f32[128,3,16]{2,1,0:T(4,128)S(1)}, u32[]{:S(2)}, u32[]{:S(2)}) async-start(f32[128,3,16]{2,1,0:T(4,128)} %copy.169), calls=%async_computation.1 | async-start | bytes 524288 | tf_op jit(solution)/shard_map/all_to_all | solution.py:224
  510.9 17.8 %collective-permute-done.43 = bf16[4,2,32,2560]{3,2,1,0:T(8,128)(2,1)} collective-permute-done((bf16[4,2,32,2560]{3,2,1,0:T(8,128)(2,1)}, bf16[4,2,32,2560]{3,2,1,0:T(8,128)(2,1)}, u32[]{:S(2)}, u32[]{:S(2)}) %collective-permute-start.43) | collective-permute-done | bytes 1310752 | tf_op jit(solution)/shard_map/ppermute | solution.py:146
  531.3 19.6 %collective-permute-done.49 = bf16[4,2,32,2560]{3,2,1,0:T(8,128)(2,1)S(1)} collective-permute-done((bf16[4,2,32,2560]{3,2,1,0:T(8,128)(2,1)S(1)}, bf16[4,2,32,2560]{3,2,1,0:T(8,128)(2,1)S(1)}, u32[]{:S(2)}, u32[]{:S(2)}) %collective-permute-start.49) | collective-permute-done | bytes 1310752 | tf_op jit(solution)/shard_map/ppermute | solution.py:146
  552.6 3.5 collective-permute-start.50
  556.2 10.2 %collective-permute-done.50 = bf16[2,32,2560]{2,1,0:T(8,128)(2,1)S(1)} collective-permute-done((bf16[2,32,2560]{2,1,0:T(8,128)(2,1)S(1)}, bf16[2,32,2560]{2,1,0:T(8,128)(2,1)S(1)}, u32[]{:S(2)}, u32[]{:S(2)}) %collective-permute-start.50) | collective-permute-done | bytes 327712 | tf_op jit(solution)/shard_map/ppermute | solution.py:146
  568.8 8.7 %collective-permute-done.51 = bf16[2,32,2560]{2,1,0:T(8,128)(2,1)S(1)} collective-permute-done((bf16[2,32,2560]{2,1,0:T(8,128)(2,1)S(1)}, bf16[2,32,2560]{2,1,0:T(8,128)(2,1)S(1)}, u32[]{:S(2)}, u32[]{:S(2)}) %collective-permute-start.51) | collective-permute-done | bytes 327712 | tf_op jit(solution)/shard_map/ppermute | solution.py:146
  577.6 3.5 collective-permute-start.52
  581.2 8.0 %collective-permute-done.52 = bf16[2,32,2560]{2,1,0:T(8,128)(2,1)S(1)} collective-permute-done((bf16[2,32,2560]{2,1,0:T(8,128)(2,1)S(1)}, bf16[2,32,2560]{2,1,0:T(8,128)(2,1)S(1)}, u32[]{:S(2)}, u32[]{:S(2)}) %collective-permute-start.52) | collective-permute-done | bytes 327712 | tf_op jit(solution)/shard_map/ppermute | solution.py:146
  593.7 5.1 collective-permute-done.53
  (301 shorter events, 145.9 us)
Async XLA Ops:
  7.2 20.3 %copy-start = (s32[1,4,128]{2,1,0:T(4,128)S(1)}, s32[1,4,128]{2,1,0:T(4,128)}, u32[]{:S(2)}) copy-start(s32[1,4,128]{2,1,0:T(4,128)} %param.16) | copy-start | bytes 6148
  7.2 20.3 %copy-start.37 = (s32[4]{0:T(128)S(1)}, s32[4]{0:T(128)}, u32[]{:S(2)}) copy-start(s32[4]{0:T(128)} %constant.282.clone) | copy-start | bytes 52
  7.2 20.1 %copy-start.4 = (bf16[1,1,128,2048]{3,2,1,0:T(8,128)(2,1)S(1)}, bf16[1,1,128,2048]{3,2,1,0:T(8,128)(2,1)}, u32[]{:S(2)}) copy-start(bf16[1,1,128,2048]{3,2,1,0:T(8,128)(2,1)} %param.15) | copy-start | bytes 1572868
  11.5 27.0 %collective-permute-start.2 = (bf16[64,2560]{1,0:T(8,128)(2,1)S(1)}, bf16[64,2560]{1,0:T(8,128)(2,1)S(1)}, u32[]{:S(2)}, u32[]{:S(2)}) collective-permute-start(bf16[64,2560]{1,0:T(8,128)(2,1)S(1)} %bitcast_dynamic-update-slice_fusion.37), channel_id=1, source_target_pairs={{0,16},{4,20},{8,24},{12,28},{16,0},{20,4},{24,8},{28,12},{32,48},... | collective-permute-start | bytes 983048 | tf_op jit(solution)/shard_map/ppermute | solution.py:173
  16.2 19.7 %all-to-all-start = ((f32[128,3,16]{2,1,0:T(4,128)}), f32[128,3,16]{2,1,0:T(4,128)S(1)}, u32[]{:S(2)}, u32[]{:S(2)}) async-start(f32[128,3,16]{2,1,0:T(4,128)} %broadcast_in_dim.155), calls=%async_computation | async-start | bytes 524288 | tf_op jit(solution)/shard_map/all_to_all | solution.py:217
  25.1 230.7 %all-gather.2.cloned.1.call-start = ((), (), s32[]{:S(2)}) async-start(), calls=%async_computation.3 | async-start | bytes 17842176 | tf_op jit(solution)/shard_map/all_gather | solution.py:262
  27.2 572.6 %reduce-scatter.2.cloned.1.call-start = ((), (), s32[]{:S(2)}) async-start(), calls=%async_computation.4 | async-start | bytes 17842176 | tf_op jit(solution)/shard_map/reduce_scatter | solution.py:308
  37.5 18.8 %collective-permute-start = (bf16[128,2048]{1,0:T(8,128)(2,1)}, bf16[128,2048]{1,0:T(8,128)(2,1)}, u32[]{:S(2)}, u32[]{:S(2)}) collective-permute-start(bf16[128,2048]{1,0:T(8,128)(2,1)} %fusion.63), channel_id=1, source_target_pairs={{0,2},{2,0},{1,3},{3,1},{4,6},{6,4},{5,7},{7,5},{8,10},{10,8},{9,1... | collective-permute-start | bytes 1572872 | tf_op jit(solution)/shard_map/ppermute | solution.py:108
  38.6 9.8 %collective-permute-start.3 = (bf16[2,16,2560]{2,1,0:T(8,128)(2,1)S(1)}, bf16[2,16,2560]{2,1,0:T(8,128)(2,1)S(1)}, u32[]{:S(2)}, u32[]{:S(2)}) collective-permute-start(bf16[2,16,2560]{2,1,0:T(8,128)(2,1)S(1)} %get-tuple-element.52), channel_id=1, source_target_pairs={{0,4},{4,8},{8,12},{12,0},{16,20},{20,24},{24,28},{28,16},{32,36},... | collective-permute-start | bytes 491528 | tf_op jit(solution)/shard_map/ppermute | solution.py:189
  39.3 9.2 %collective-permute-start.9 = (bf16[2,16,2560]{2,1,0:T(8,128)(2,1)S(1)}, bf16[2,16,2560]{2,1,0:T(8,128)(2,1)S(1)}, u32[]{:S(2)}, u32[]{:S(2)}) collective-permute-start(bf16[2,16,2560]{2,1,0:T(8,128)(2,1)S(1)} %get-tuple-element.51), channel_id=1, source_target_pairs={{0,12},{4,0},{8,4},{12,8},{16,28},{20,16},{24,20},{28,24},{32,44},... | collective-permute-start | bytes 491528 | tf_op jit(solution)/shard_map/ppermute | solution.py:189
  41.9 9.8 %collective-permute-start.15 = (bf16[2,16,2560]{2,1,0:T(8,128)(2,1)S(1)}, bf16[2,16,2560]{2,1,0:T(8,128)(2,1)S(1)}, u32[]{:S(2)}, u32[]{:S(2)}) collective-permute-start(bf16[2,16,2560]{2,1,0:T(8,128)(2,1)S(1)} %get-tuple-element.50), channel_id=1, source_target_pairs={{0,32},{4,36},{8,40},{12,44},{16,48},{20,52},{24,56},{28,60},{32,6... | collective-permute-start | bytes 491528 | tf_op jit(solution)/shard_map/ppermute | solution.py:203
  42.7 9.0 %collective-permute-start.21 = (bf16[2,16,2560]{2,1,0:T(8,128)(2,1)S(1)}, bf16[2,16,2560]{2,1,0:T(8,128)(2,1)S(1)}, u32[]{:S(2)}, u32[]{:S(2)}) collective-permute-start(bf16[2,16,2560]{2,1,0:T(8,128)(2,1)S(1)} %get-tuple-element.49), channel_id=1, source_target_pairs={{0,96},{4,100},{8,104},{12,108},{16,112},{20,116},{24,120},{28,124... | collective-permute-start | bytes 491528 | tf_op jit(solution)/shard_map/ppermute | solution.py:203
  48.4 9.2 %collective-permute-start.4 = (bf16[2,16,2560]{2,1,0:T(8,128)(2,1)S(1)}, bf16[2,16,2560]{2,1,0:T(8,128)(2,1)S(1)}, u32[]{:S(2)}, u32[]{:S(2)}) collective-permute-start(bf16[2,16,2560]{2,1,0:T(8,128)(2,1)S(1)} %collective-permute-done.3), channel_id=1, source_target_pairs={{0,4},{4,8},{8,12},{12,0},{16,20},{20,24},{24,28},{28,16},{32,36},... | collective-permute-start | bytes 491528 | tf_op jit(solution)/shard_map/ppermute | solution.py:189
  48.5 9.2 %collective-permute-start.10 = (bf16[2,16,2560]{2,1,0:T(8,128)(2,1)S(1)}, bf16[2,16,2560]{2,1,0:T(8,128)(2,1)S(1)}, u32[]{:S(2)}, u32[]{:S(2)}) collective-permute-start(bf16[2,16,2560]{2,1,0:T(8,128)(2,1)S(1)} %collective-permute-done.9), channel_id=1, source_target_pairs={{0,12},{4,0},{8,4},{12,8},{16,28},{20,16},{24,20},{28,24},{32,44},... | collective-permute-start | bytes 491528 | tf_op jit(solution)/shard_map/ppermute | solution.py:189
  51.7 9.2 %collective-permute-start.16 = (bf16[2,16,2560]{2,1,0:T(8,128)(2,1)S(1)}, bf16[2,16,2560]{2,1,0:T(8,128)(2,1)S(1)}, u32[]{:S(2)}, u32[]{:S(2)}) collective-permute-start(bf16[2,16,2560]{2,1,0:T(8,128)(2,1)S(1)} %collective-permute-done.15), channel_id=1, source_target_pairs={{0,32},{4,36},{8,40},{12,44},{16,48},{20,52},{24,56},{28,60},{32,6... | collective-permute-start | bytes 491528 | tf_op jit(solution)/shard_map/ppermute | solution.py:203
  51.7 9.3 %collective-permute-start.22 = (bf16[2,16,2560]{2,1,0:T(8,128)(2,1)S(1)}, bf16[2,16,2560]{2,1,0:T(8,128)(2,1)S(1)}, u32[]{:S(2)}, u32[]{:S(2)}) collective-permute-start(bf16[2,16,2560]{2,1,0:T(8,128)(2,1)S(1)} %collective-permute-done.21), channel_id=1, source_target_pairs={{0,96},{4,100},{8,104},{12,108},{16,112},{20,116},{24,120},{28,124... | collective-permute-start | bytes 491528 | tf_op jit(solution)/shard_map/ppermute | solution.py:203
  57.5 49.6 %collective-permute-start.1 = (bf16[2,128,2048]{2,1,0:T(8,128)(2,1)S(1)}, bf16[2,128,2048]{2,1,0:T(8,128)(2,1)}, u32[]{:S(2)}, u32[]{:S(2)}) collective-permute-start(bf16[2,128,2048]{2,1,0:T(8,128)(2,1)S(1)} %pad_maximum_fusion.5), channel_id=1, source_target_pairs={{0,1},{1,0},{2,3},{3,2},{4,5},{5,4},{6,7},{7,6},{8,9},{9,8},{10,11... | collective-permute-start | bytes 3145736 | tf_op jit(solution)/shard_map/ppermute | solution.py:110
  57.6 8.0 %collective-permute-start.5 = (bf16[2,16,2560]{2,1,0:T(8,128)(2,1)S(1)}, bf16[2,16,2560]{2,1,0:T(8,128)(2,1)S(1)}, u32[]{:S(2)}, u32[]{:S(2)}) collective-permute-start(bf16[2,16,2560]{2,1,0:T(8,128)(2,1)S(1)} %collective-permute-done.4), channel_id=1, source_target_pairs={{0,4},{4,8},{8,12},{12,0},{16,20},{20,24},{24,28},{28,16},{32,36},... | collective-permute-start | bytes 491528 | tf_op jit(solution)/shard_map/ppermute | solution.py:189
  57.7 8.0 %collective-permute-start.11 = (bf16[2,16,2560]{2,1,0:T(8,128)(2,1)S(1)}, bf16[2,16,2560]{2,1,0:T(8,128)(2,1)S(1)}, u32[]{:S(2)}, u32[]{:S(2)}) collective-permute-start(bf16[2,16,2560]{2,1,0:T(8,128)(2,1)S(1)} %collective-permute-done.10), channel_id=1, source_target_pairs={{0,12},{4,0},{8,4},{12,8},{16,28},{20,16},{24,20},{28,24},{32,44},... | collective-permute-start | bytes 491528 | tf_op jit(solution)/shard_map/ppermute | solution.py:189
  60.9 8.7 %collective-permute-start.17 = (bf16[2,16,2560]{2,1,0:T(8,128)(2,1)S(1)}, bf16[2,16,2560]{2,1,0:T(8,128)(2,1)S(1)}, u32[]{:S(2)}, u32[]{:S(2)}) collective-permute-start(bf16[2,16,2560]{2,1,0:T(8,128)(2,1)S(1)} %collective-permute-done.16), channel_id=1, source_target_pairs={{0,32},{4,36},{8,40},{12,44},{16,48},{20,52},{24,56},{28,60},{32,6... | collective-permute-start | bytes 491528 | tf_op jit(solution)/shard_map/ppermute | solution.py:203
  61.0 9.2 %collective-permute-start.23 = (bf16[2,16,2560]{2,1,0:T(8,128)(2,1)S(1)}, bf16[2,16,2560]{2,1,0:T(8,128)(2,1)S(1)}, u32[]{:S(2)}, u32[]{:S(2)}) collective-permute-start(bf16[2,16,2560]{2,1,0:T(8,128)(2,1)S(1)} %collective-permute-done.22), channel_id=1, source_target_pairs={{0,96},{4,100},{8,104},{12,108},{16,112},{20,116},{24,120},{28,124... | collective-permute-start | bytes 491528 | tf_op jit(solution)/shard_map/ppermute | solution.py:203
  65.6 24.3 %collective-permute-start.6 = (bf16[2,4,16,2560]{3,2,1,0:T(8,128)(2,1)S(1)}, bf16[2,4,16,2560]{3,2,1,0:T(8,128)(2,1)}, u32[]{:S(2)}, u32[]{:S(2)}) collective-permute-start(bf16[2,4,16,2560]{3,2,1,0:T(8,128)(2,1)S(1)} %bitcast_dynamic-update-slice_fusion.25), channel_id=1, source_target_pairs={{0,32},{4,36},{8,40},{12,44},{16,48},{20,52},{24,56},{28,60},{32,6... | collective-permute-start | bytes 1966088 | tf_op jit(solution)/shard_map/ppermute | solution.py:195
  66.3 23.5 %collective-permute-start.12 = (bf16[2,4,16,2560]{3,2,1,0:T(8,128)(2,1)}, bf16[2,4,16,2560]{3,2,1,0:T(8,128)(2,1)}, u32[]{:S(2)}, u32[]{:S(2)}) collective-permute-start(bf16[2,4,16,2560]{3,2,1,0:T(8,128)(2,1)} %bitcast_dynamic-update-slice_fusion.21), channel_id=1, source_target_pairs={{0,96},{4,100},{8,104},{12,108},{16,112},{20,116},{24,120},{28,124... | collective-permute-start | bytes 1966088 | tf_op jit(solution)/shard_map/ppermute | solution.py:195
  70.2 32.5 %collective-permute-start.18 = (bf16[4,2,16,2560]{3,2,1,0:T(8,128)(2,1)}, bf16[4,2,16,2560]{3,2,1,0:T(8,128)(2,1)}, u32[]{:S(2)}, u32[]{:S(2)}) collective-permute-start(bf16[4,2,16,2560]{3,2,1,0:T(8,128)(2,1)} %bitcast_dynamic-update-slice_fusion.33), channel_id=1, source_target_pairs={{0,4},{4,8},{8,12},{12,0},{16,20},{20,24},{24,28},{28,16},{32,36},... | collective-permute-start | bytes 1966088 | tf_op jit(solution)/shard_map/ppermute | solution.py:209
  70.3 32.4 %collective-permute-start.24 = (bf16[4,2,16,2560]{3,2,1,0:T(8,128)(2,1)S(1)}, bf16[4,2,16,2560]{3,2,1,0:T(8,128)(2,1)}, u32[]{:S(2)}, u32[]{:S(2)}) collective-permute-start(bf16[4,2,16,2560]{3,2,1,0:T(8,128)(2,1)S(1)} %bitcast_dynamic-update-slice_fusion.29), channel_id=1, source_target_pairs={{0,12},{4,0},{8,4},{12,8},{16,28},{20,16},{24,20},{28,24},{32,44},... | collective-permute-start | bytes 1966088 | tf_op jit(solution)/shard_map/ppermute | solution.py:209
  89.8 20.1 %collective-permute-start.7 = (bf16[2,4,16,2560]{3,2,1,0:T(8,128)(2,1)}, bf16[2,4,16,2560]{3,2,1,0:T(8,128)(2,1)S(1)}, u32[]{:S(2)}, u32[]{:S(2)}) collective-permute-start(bf16[2,4,16,2560]{3,2,1,0:T(8,128)(2,1)} %collective-permute-done.6), channel_id=1, source_target_pairs={{0,32},{4,36},{8,40},{12,44},{16,48},{20,52},{24,56},{28,60},{32,6... | collective-permute-start | bytes 1966088 | tf_op jit(solution)/shard_map/ppermute | solution.py:195
  89.8 20.1 %collective-permute-start.13 = (bf16[2,4,16,2560]{3,2,1,0:T(8,128)(2,1)}, bf16[2,4,16,2560]{3,2,1,0:T(8,128)(2,1)S(1)}, u32[]{:S(2)}, u32[]{:S(2)}) collective-permute-start(bf16[2,4,16,2560]{3,2,1,0:T(8,128)(2,1)} %collective-permute-done.12), channel_id=1, source_target_pairs={{0,96},{4,100},{8,104},{12,108},{16,112},{20,116},{24,120},{28,124... | collective-permute-start | bytes 1966088 | tf_op jit(solution)/shard_map/ppermute | solution.py:195
  102.7 19.2 %collective-permute-start.19 = (bf16[4,2,16,2560]{3,2,1,0:T(8,128)(2,1)}, bf16[4,2,16,2560]{3,2,1,0:T(8,128)(2,1)S(1)}, u32[]{:S(2)}, u32[]{:S(2)}) collective-permute-start(bf16[4,2,16,2560]{3,2,1,0:T(8,128)(2,1)} %collective-permute-done.18), channel_id=1, source_target_pairs={{0,4},{4,8},{8,12},{12,0},{16,20},{20,24},{24,28},{28,16},{32,36},... | collective-permute-start | bytes 1966088 | tf_op jit(solution)/shard_map/ppermute | solution.py:209
  102.7 19.2 %collective-permute-start.25 = (bf16[4,2,16,2560]{3,2,1,0:T(8,128)(2,1)}, bf16[4,2,16,2560]{3,2,1,0:T(8,128)(2,1)S(1)}, u32[]{:S(2)}, u32[]{:S(2)}) collective-permute-start(bf16[4,2,16,2560]{3,2,1,0:T(8,128)(2,1)} %collective-permute-done.24), channel_id=1, source_target_pairs={{0,12},{4,0},{8,4},{12,8},{16,28},{20,16},{24,20},{28,24},{32,44},... | collective-permute-start | bytes 1966088 | tf_op jit(solution)/shard_map/ppermute | solution.py:209
  110.0 15.7 %collective-permute-start.8 = (bf16[2,4,16,2560]{3,2,1,0:T(8,128)(2,1)S(1)}, bf16[2,4,16,2560]{3,2,1,0:T(8,128)(2,1)S(1)}, u32[]{:S(2)}, u32[]{:S(2)}) collective-permute-start(bf16[2,4,16,2560]{3,2,1,0:T(8,128)(2,1)S(1)} %collective-permute-done.7), channel_id=1, source_target_pairs={{0,32},{4,36},{8,40},{12,44},{16,48},{20,52},{24,56},{28,60},{32,6... | collective-permute-start | bytes 1966088 | tf_op jit(solution)/shard_map/ppermute | solution.py:195
  110.0 20.2 %collective-permute-start.14 = (bf16[2,4,16,2560]{3,2,1,0:T(8,128)(2,1)S(1)}, bf16[2,4,16,2560]{3,2,1,0:T(8,128)(2,1)S(1)}, u32[]{:S(2)}, u32[]{:S(2)}) collective-permute-start(bf16[2,4,16,2560]{3,2,1,0:T(8,128)(2,1)S(1)} %collective-permute-done.13), channel_id=1, source_target_pairs={{0,96},{4,100},{8,104},{12,108},{16,112},{20,116},{24,120},{28,124... | collective-permute-start | bytes 1966088 | tf_op jit(solution)/shard_map/ppermute | solution.py:195
  121.9 31.4 %collective-permute-start.20 = (bf16[4,2,16,2560]{3,2,1,0:T(8,128)(2,1)S(1)}, bf16[4,2,16,2560]{3,2,1,0:T(8,128)(2,1)S(1)}, u32[]{:S(2)}, u32[]{:S(2)}) collective-permute-start(bf16[4,2,16,2560]{3,2,1,0:T(8,128)(2,1)S(1)} %collective-permute-done.19), channel_id=1, source_target_pairs={{0,4},{4,8},{8,12},{12,0},{16,20},{20,24},{24,28},{28,16},{32,36},... | collective-permute-start | bytes 1966088 | tf_op jit(solution)/shard_map/ppermute | solution.py:209
  121.9 32.8 %collective-permute-start.26 = (bf16[4,2,16,2560]{3,2,1,0:T(8,128)(2,1)S(1)}, bf16[4,2,16,2560]{3,2,1,0:T(8,128)(2,1)S(1)}, u32[]{:S(2)}, u32[]{:S(2)}) collective-permute-start(bf16[4,2,16,2560]{3,2,1,0:T(8,128)(2,1)S(1)} %collective-permute-done.25), channel_id=1, source_target_pairs={{0,12},{4,0},{8,4},{12,8},{16,28},{20,16},{24,20},{28,24},{32,44},... | collective-permute-start | bytes 1966088 | tf_op jit(solution)/shard_map/ppermute | solution.py:209
  197.8 4.2 collective-permute-start.27
  202.2 27.7 %collective-permute-start.28 = (bf16[128,2048]{1,0:T(8,128)(2,1)S(1)}, bf16[128,2048]{1,0:T(8,128)(2,1)}, u32[]{:S(2)}, u32[]{:S(2)}) collective-permute-start(bf16[128,2048]{1,0:T(8,128)(2,1)S(1)} %fusion.93), channel_id=1, source_target_pairs={{0,2},{2,0},{1,3},{3,1},{4,6},{6,4},{5,7},{7,5},{8,10},{10,8},{9,1... | collective-permute-start | bytes 1572872 | tf_op jit(solution)/shard_map/ppermute | solution.py:119
  216.4 24.7 %collective-permute-start.33 = (bf16[128,2048]{1,0:T(8,128)(2,1)S(1)}, bf16[128,2048]{1,0:T(8,128)(2,1)}, u32[]{:S(2)}, u32[]{:S(2)}) collective-permute-start(bf16[128,2048]{1,0:T(8,128)(2,1)S(1)} %bitcast.439), channel_id=1, source_target_pairs={{0,2},{2,0},{1,3},{3,1},{4,6},{6,4},{5,7},{7,5},{8,10},{10,8},{9,1... | collective-permute-start | bytes 1572872 | tf_op jit(solution)/shard_map/ppermute | solution.py:108
  232.1 19.3 %collective-permute-start.29 = (bf16[128,2048]{1,0:T(8,128)(2,1)S(1)}, bf16[128,2048]{1,0:T(8,128)(2,1)S(1)}, u32[]{:S(2)}, u32[]{:S(2)}) collective-permute-start(bf16[128,2048]{1,0:T(8,128)(2,1)S(1)} %multiply_convert_fusion.4), channel_id=1, source_target_pairs={{0,2},{2,0},{1,3},{3,1},{4,6},{6,4},{5,7},{7,5},{8,10},{10,8},{9,1... | collective-permute-start | bytes 1572872 | tf_op jit(solution)/shard_map/ppermute | solution.py:108
  242.3 9.4 %collective-permute-start.34 = (bf16[2,128,2048]{2,1,0:T(8,128)(2,1)S(1)}, bf16[2,128,2048]{2,1,0:T(8,128)(2,1)S(1)}, u32[]{:S(2)}, u32[]{:S(2)}) collective-permute-start(bf16[2,128,2048]{2,1,0:T(8,128)(2,1)S(1)} %pad_maximum_fusion.7), channel_id=1, source_target_pairs={{0,1},{1,0},{2,3},{3,2},{4,5},{5,4},{6,7},{7,6},{8,9},{9,8},{10,11... | collective-permute-start | bytes 3145736 | tf_op jit(solution)/shard_map/ppermute | solution.py:110
  251.5 2.7 collective-permute-start.30
  309.1 7.4 %collective-permute-start.35 = (f32[2,128,2048]{2,1,0:T(8,128)S(1)}, f32[2,128,2048]{2,1,0:T(8,128)S(1)}, u32[]{:S(2)}, u32[]{:S(2)}) collective-permute-start(f32[2,128,2048]{2,1,0:T(8,128)S(1)} %bitcast.457), channel_id=1, source_target_pairs={{0,1},{1,0},{2,3},{3,2},{4,5},{5,4},{6,7},{7,6},{8,9},{9,8},{10,11... | collective-permute-start | bytes 6291464 | tf_op jit(solution)/shard_map/ppermute | solution.py:116
  316.0 4.4 collective-permute-start.31
  316.7 19.1 %collective-permute-start.36 = (bf16[128,2048]{1,0:T(8,128)(2,1)S(1)}, bf16[128,2048]{1,0:T(8,128)(2,1)S(1)}, u32[]{:S(2)}, u32[]{:S(2)}) collective-permute-start(bf16[128,2048]{1,0:T(8,128)(2,1)S(1)} %fusion.83), channel_id=1, source_target_pairs={{0,2},{2,0},{1,3},{3,1},{4,6},{6,4},{5,7},{7,5},{8,10},{10,8},{9,1... | collective-permute-start | bytes 1572872 | tf_op jit(solution)/shard_map/ppermute | solution.py:119
  320.5 29.5 %collective-permute-start.32 = (bf16[128,2048]{1,0:T(8,128)(2,1)S(1)}, bf16[128,2048]{1,0:T(8,128)(2,1)S(1)}, u32[]{:S(2)}, u32[]{:S(2)}) collective-permute-start(bf16[128,2048]{1,0:T(8,128)(2,1)S(1)} %fusion.87), channel_id=1, source_target_pairs={{0,2},{2,0},{1,3},{3,1},{4,6},{6,4},{5,7},{7,5},{8,10},{10,8},{9,1... | collective-permute-start | bytes 1572872 | tf_op jit(solution)/shard_map/ppermute | solution.py:119
  351.7 17.9 %collective-permute-start.37 = (bf16[128,2048]{1,0:T(8,128)(2,1)S(1)}, bf16[128,2048]{1,0:T(8,128)(2,1)S(1)}, u32[]{:S(2)}, u32[]{:S(2)}) collective-permute-start(bf16[128,2048]{1,0:T(8,128)(2,1)S(1)} %get-tuple-element.25), channel_id=1, source_target_pairs={{0,2},{2,0},{1,3},{3,1},{4,6},{6,4},{5,7},{7,5},{8,10},{10,8},{9,1... | collective-permute-start | bytes 1572872 | tf_op jit(solution)/shard_map/ppermute | solution.py:108
  369.7 2.7 collective-permute-start.38
  422.3 32.4 %collective-permute-start.41 = (bf16[4,2,32,2560]{3,2,1,0:T(8,128)(2,1)}, bf16[4,2,32,2560]{3,2,1,0:T(8,128)(2,1)}, u32[]{:S(2)}, u32[]{:S(2)}) collective-permute-start(bf16[4,2,32,2560]{3,2,1,0:T(8,128)(2,1)} %dynamic-slice_bitcast_fusion.1), channel_id=1, source_target_pairs={{0,4},{4,8},{8,12},{12,0},{16,20},{20,24},{24,28},{28,16},{32,36},... | collective-permute-start | bytes 3932168 | tf_op jit(solution)/shard_map/ppermute | solution.py:146
  435.7 41.7 %collective-permute-start.39 = (f32[2,128,2048]{2,1,0:T(8,128)}, f32[2,128,2048]{2,1,0:T(8,128)S(1)}, u32[]{:S(2)}, u32[]{:S(2)}) collective-permute-start(f32[2,128,2048]{2,1,0:T(8,128)} %bitcast.105), channel_id=1, source_target_pairs={{0,1},{1,0},{2,3},{3,2},{4,5},{5,4},{6,7},{7,6},{8,9},{9,8},{10,11... | collective-permute-start | bytes 6291464 | tf_op jit(solution)/shard_map/ppermute | solution.py:116
  438.6 31.8 %collective-permute-start.47 = (bf16[4,2,32,2560]{3,2,1,0:T(8,128)(2,1)}, bf16[4,2,32,2560]{3,2,1,0:T(8,128)(2,1)}, u32[]{:S(2)}, u32[]{:S(2)}) collective-permute-start(bf16[4,2,32,2560]{3,2,1,0:T(8,128)(2,1)} %dynamic-slice_bitcast_fusion), channel_id=1, source_target_pairs={{0,12},{4,0},{8,4},{12,8},{16,28},{20,16},{24,20},{28,24},{32,44},... | collective-permute-start | bytes 3932168 | tf_op jit(solution)/shard_map/ppermute | solution.py:146
  457.9 31.6 %collective-permute-start.42 = (bf16[4,2,32,2560]{3,2,1,0:T(8,128)(2,1)}, bf16[4,2,32,2560]{3,2,1,0:T(8,128)(2,1)}, u32[]{:S(2)}, u32[]{:S(2)}) collective-permute-start(bf16[4,2,32,2560]{3,2,1,0:T(8,128)(2,1)} %fusion.19), channel_id=1, source_target_pairs={{0,4},{4,8},{8,12},{12,0},{16,20},{20,24},{24,28},{28,16},{32,36},... | collective-permute-start | bytes 3932168 | tf_op jit(solution)/shard_map/ppermute | solution.py:146
  473.5 33.1 %collective-permute-start.48 = (bf16[4,2,32,2560]{3,2,1,0:T(8,128)(2,1)}, bf16[4,2,32,2560]{3,2,1,0:T(8,128)(2,1)}, u32[]{:S(2)}, u32[]{:S(2)}) collective-permute-start(bf16[4,2,32,2560]{3,2,1,0:T(8,128)(2,1)} %fusion.16), channel_id=1, source_target_pairs={{0,12},{4,0},{8,4},{12,8},{16,28},{20,16},{24,20},{28,24},{32,44},... | collective-permute-start | bytes 3932168 | tf_op jit(solution)/shard_map/ppermute | solution.py:146
  478.9 17.2 %collective-permute-start.40 = (bf16[128,2048]{1,0:T(8,128)(2,1)S(1)}, bf16[128,2048]{1,0:T(8,128)(2,1)S(1)}, u32[]{:S(2)}, u32[]{:S(2)}) collective-permute-start(bf16[128,2048]{1,0:T(8,128)(2,1)S(1)} %fusion.79), channel_id=1, source_target_pairs={{0,2},{2,0},{1,3},{3,1},{4,6},{6,4},{5,7},{7,5},{8,10},{10,8},{9,1... | collective-permute-start | bytes 1572872 | tf_op jit(solution)/shard_map/ppermute | solution.py:119
  492.7 36.0 %collective-permute-start.43 = (bf16[4,2,32,2560]{3,2,1,0:T(8,128)(2,1)}, bf16[4,2,32,2560]{3,2,1,0:T(8,128)(2,1)}, u32[]{:S(2)}, u32[]{:S(2)}) collective-permute-start(bf16[4,2,32,2560]{3,2,1,0:T(8,128)(2,1)} %fusion.20), channel_id=1, source_target_pairs={{0,4},{4,8},{8,12},{12,0},{16,20},{20,24},{24,28},{28,16},{32,36},... | collective-permute-start | bytes 3932168 | tf_op jit(solution)/shard_map/ppermute | solution.py:146
  499.6 93.5 %all-to-all-start.1 = ((f32[128,3,16]{2,1,0:T(4,128)}), f32[128,3,16]{2,1,0:T(4,128)S(1)}, u32[]{:S(2)}, u32[]{:S(2)}) async-start(f32[128,3,16]{2,1,0:T(4,128)} %copy.169), calls=%async_computation.1 | async-start | bytes 524288 | tf_op jit(solution)/shard_map/all_to_all | solution.py:224
  508.7 42.2 %collective-permute-start.49 = (bf16[4,2,32,2560]{3,2,1,0:T(8,128)(2,1)S(1)}, bf16[4,2,32,2560]{3,2,1,0:T(8,128)(2,1)S(1)}, u32[]{:S(2)}, u32[]{:S(2)}) collective-permute-start(bf16[4,2,32,2560]{3,2,1,0:T(8,128)(2,1)S(1)} %fusion.17), channel_id=1, source_target_pairs={{0,12},{4,0},{8,4},{12,8},{16,28},{20,16},{24,20},{28,24},{32,44},... | collective-permute-start | bytes 3932168 | tf_op jit(solution)/shard_map/ppermute | solution.py:146
  530.9 25.2 %collective-permute-start.44 = (bf16[2,32,2560]{2,1,0:T(8,128)(2,1)S(1)}, bf16[2,32,2560]{2,1,0:T(8,128)(2,1)S(1)}, u32[]{:S(2)}, u32[]{:S(2)}) collective-permute-start(bf16[2,32,2560]{2,1,0:T(8,128)(2,1)S(1)} %dynamic-slice_bitcast_fusion.3), channel_id=1, source_target_pairs={{0,32},{4,36},{8,40},{12,44},{16,48},{20,52},{24,56},{28,60},{32,6... | collective-permute-start | bytes 983048 | tf_op jit(solution)/shard_map/ppermute | solution.py:146
  552.6 13.8 %collective-permute-start.50 = (bf16[2,32,2560]{2,1,0:T(8,128)(2,1)S(1)}, bf16[2,32,2560]{2,1,0:T(8,128)(2,1)S(1)}, u32[]{:S(2)}, u32[]{:S(2)}) collective-permute-start(bf16[2,32,2560]{2,1,0:T(8,128)(2,1)S(1)} %dynamic-slice_bitcast_fusion.2), channel_id=1, source_target_pairs={{0,96},{4,100},{8,104},{12,108},{16,112},{20,116},{24,120},{28,124... | collective-permute-start | bytes 983048 | tf_op jit(solution)/shard_map/ppermute | solution.py:146
  556.2 12.4 %collective-permute-start.45 = (bf16[2,32,2560]{2,1,0:T(8,128)(2,1)S(1)}, bf16[2,32,2560]{2,1,0:T(8,128)(2,1)S(1)}, u32[]{:S(2)}, u32[]{:S(2)}) collective-permute-start(bf16[2,32,2560]{2,1,0:T(8,128)(2,1)S(1)} %fusion.116), channel_id=1, source_target_pairs={{0,32},{4,36},{8,40},{12,44},{16,48},{20,52},{24,56},{28,60},{32,6... | collective-permute-start | bytes 983048 | tf_op jit(solution)/shard_map/ppermute | solution.py:146
  566.5 11.0 %collective-permute-start.51 = (bf16[2,32,2560]{2,1,0:T(8,128)(2,1)S(1)}, bf16[2,32,2560]{2,1,0:T(8,128)(2,1)S(1)}, u32[]{:S(2)}, u32[]{:S(2)}) collective-permute-start(bf16[2,32,2560]{2,1,0:T(8,128)(2,1)S(1)} %fusion.114), channel_id=1, source_target_pairs={{0,96},{4,100},{8,104},{12,108},{16,112},{20,116},{24,120},{28,124... | collective-permute-start | bytes 983048 | tf_op jit(solution)/shard_map/ppermute | solution.py:146
  568.6 23.1 %copy-start.10 = (f32[128,2048]{1,0:T(8,128)S(1)}, f32[128,2048]{1,0:T(8,128)}, u32[]{:S(2)}) copy-start(f32[128,2048]{1,0:T(8,128)} %get-tuple-element.26) | copy-start | bytes 3145732
  568.7 23.1 %copy-start.12 = (f32[128,2048]{1,0:T(8,128)S(1)}, f32[128,2048]{1,0:T(8,128)}, u32[]{:S(2)}) copy-start(f32[128,2048]{1,0:T(8,128)} %get-tuple-element.24) | copy-start | bytes 3145732
  568.7 23.1 %copy-start.36 = (f32[128]{0:T(128)S(1)}, f32[128]{0:T(128)}, u32[]{:S(2)}) copy-start(f32[128]{0:T(128)} %get-tuple-element.58) | copy-start | bytes 1540
  568.7 12.4 %collective-permute-start.46 = (bf16[2,32,2560]{2,1,0:T(8,128)(2,1)S(1)}, bf16[2,32,2560]{2,1,0:T(8,128)(2,1)S(1)}, u32[]{:S(2)}, u32[]{:S(2)}) collective-permute-start(bf16[2,32,2560]{2,1,0:T(8,128)(2,1)S(1)} %fusion.117), channel_id=1, source_target_pairs={{0,32},{4,36},{8,40},{12,44},{16,48},{20,52},{24,56},{28,60},{32,6... | collective-permute-start | bytes 983048 | tf_op jit(solution)/shard_map/ppermute | solution.py:146
  577.6 11.6 %collective-permute-start.52 = (bf16[2,32,2560]{2,1,0:T(8,128)(2,1)S(1)}, bf16[2,32,2560]{2,1,0:T(8,128)(2,1)S(1)}, u32[]{:S(2)}, u32[]{:S(2)}) collective-permute-start(bf16[2,32,2560]{2,1,0:T(8,128)(2,1)S(1)} %fusion.115), channel_id=1, source_target_pairs={{0,96},{4,100},{8,104},{12,108},{16,112},{20,116},{24,120},{28,124... | collective-permute-start | bytes 983048 | tf_op jit(solution)/shard_map/ppermute | solution.py:146
  589.3 9.6 %collective-permute-start.53 = (bf16[64,2560]{1,0:T(8,128)(2,1)S(1)}, bf16[64,2560]{1,0:T(8,128)(2,1)S(1)}, u32[]{:S(2)}, u32[]{:S(2)}) collective-permute-start(bf16[64,2560]{1,0:T(8,128)(2,1)S(1)} %fusion.130), channel_id=1, source_target_pairs={{0,16},{4,20},{8,24},{12,28},{16,0},{20,4},{24,8},{28,12},{32,48},... | collective-permute-start | bytes 983048 | tf_op jit(solution)/shard_map/ppermute | solution.py:165
  (33 other events, 190.4 us)
Sparse Core Ops, SparseCore 0:
  29.0 178.8 all-gather.1
  297.4 292.3 reduce-scatter.1

commit v17 on v16

--- a/solution.py
+++ b/solution.py
@@ -156,8 +156,8 @@
     result = []
     for step, rows in ((1, slice(0, half)), (3, slice(half, None))):
         part = blocks[:, :, :, rows]
-        along_x = ring_stage(part, 2, x_pos, 1, 4, step)
-        result.append(ring_stage(along_x.astype(jnp.bfloat16), 0, z_pos, 8, 4, step))
+        along_z = ring_stage(part, 0, z_pos, 8, 4, step)
+        result.append(ring_stage(along_z.astype(jnp.bfloat16), 1, x_pos, 1, 4, step))
     along_z = jnp.concatenate(result, axis=1)
     keep = lax.dynamic_index_in_dim(along_z, y_pos, 0, keepdims=False)
     give = lax.dynamic_index_in_dim(along_z, 1 - y_pos, 0, keepdims=False)

time: 614 us -> 632 us (1.029)
  waiting for transfers between devices: 250 us -> 263 us
  local copies, waits for them, and re-layouts: 76.2 us -> 83 us
    ppermute x12, waiting for transfers between devices: 96.6 us -> 111 us  [ring_stage(): got = lax.ppermute(acc.astype(jnp.bfloat16), 'dp', pairs)]
    dynamic_slice x0 -> x1, local copies, waits for them, and re-layouts: none -> 7.63 us  [pick(): lax.dynamic_index_in_dim(chunks, (pos - k * step) % size, axis, keepdims=...]
    unnamed x85 -> x103, local copies, waits for them, and re-layouts: 14 us -> 18.3 us
  transfers between devices with their start and end apart: 58 -> 58, of which waited for: 26 -> 26; matrix products, arithmetic and copies ran while one was open for 29% -> 28% of each run, Pallas kernels for 2% -> 2%
where the time goes in v17:
time: 632 us; the launch traced here: 626 us
  waiting for transfers between devices  263 us (42%)
  starting transfers between devices  106 us (17%)
  matrix products  84.9 us (13%)
  local copies, waits for them, and re-layouts  83 us (13%)
  other arithmetic  46.9 us (7%)
  Pallas kernels  26.6 us (4%)
  between operations  15.8 us (2%)
    ppermute x12, waiting for transfers between devices, ring_stage(): got = lax.ppermute(acc.astype(jnp.bfloat16), 'dp', pairs)  111 us
    ppermute x24, waiting for transfers between devices, ring_gather(): cur = lax.ppermute(cur, 'dp', pairs)  56.2 us
    ppermute x4, waiting for transfers between devices, row_sum(): lax.ppermute(theirs.astype(jnp.bfloat16), 'tensor', ACROSS)  40.3 us
    ppermute x24, starting transfers between devices, ring_gather(): cur = lax.ppermute(cur, 'dp', pairs)  39.7 us
    dot_general x8, matrix products, matmul_plain(): return jnp.dot(left, right, preferred_element_type=jnp.float32)  39.5 us
    ppermute x4, waiting for transfers between devices, row_gather(): across = lax.ppermute(values, 'tensor', ACROSS)  32.8 us
    dot_general x8, matrix products, times_trans(): lax.dot_general(left, right, (((1,), (1,)), ((), ())), preferred_element_...  27.1 us
    pallas_call x2, Pallas kernels, grad_pack(): pl.pallas_call(functools.partial(pack_kernel, per), grid=(rows_out // til...  26.6 us
  transfers between devices with their start and end apart: 58, of which 26 were waited for; matrix products, arithmetic and copies ran while one was open for 28% of the time, Pallas kernels for 2%

profile of v17, /device:TPU:0, one launch (start us, length us, event | category | flops | bytes accessed | tf_op | source)
XLA Modules:
  0.0 625.9 jit_solution(6686812971326088126)
XLA Ops:
  11.5 3.3 collective-permute-start.2
  16.2 8.9 %all-to-all-start = ((f32[128,3,16]{2,1,0:T(4,128)}), f32[128,3,16]{2,1,0:T(4,128)S(1)}, u32[]{:S(2)}, u32[]{:S(2)}) async-start(f32[128,3,16]{2,1,0:T(4,128)} %broadcast_in_dim.155), calls=%async_computation | async-start | bytes 524288 | tf_op jit(solution)/shard_map/all_to_all | solution.py:217
  29.3 6.6 %all-to-all-done = f32[128,3,16]{2,1,0:T(4,128)S(1)} async-done(((f32[128,3,16]{2,1,0:T(4,128)}), f32[128,3,16]{2,1,0:T(4,128)S(1)}, u32[]{:S(2)}, u32[]{:S(2)}) %all-to-all-start) | async-done | bytes 24608 | tf_op jit(solution)/shard_map/all_to_all | solution.py:217
  48.5 3.2 collective-permute-start.10
  51.7 3.2 collective-permute-start.22
  57.7 3.2 collective-permute-start.11
  61.0 3.1 collective-permute-start.23
  66.4 3.2 collective-permute-start.12
  70.3 3.3 collective-permute-start.24
  74.8 15.0 %collective-permute-done.6 = bf16[2,4,16,2560]{3,2,1,0:T(8,128)(2,1)} collective-permute-done((bf16[2,4,16,2560]{3,2,1,0:T(8,128)(2,1)S(1)}, bf16[2,4,16,2560]{3,2,1,0:T(8,128)(2,1)}, u32[]{:S(2)}, u32[]{:S(2)}) %collective-permute-start.6) | collective-permute-done | bytes 655392 | tf_op jit(solution)/shard_map/ppermute | solution.py:195
  89.9 3.8 collective-permute-start.13
  93.7 9.0 %collective-permute-done.18 = bf16[4,2,16,2560]{3,2,1,0:T(8,128)(2,1)} collective-permute-done((bf16[4,2,16,2560]{3,2,1,0:T(8,128)(2,1)}, bf16[4,2,16,2560]{3,2,1,0:T(8,128)(2,1)}, u32[]{:S(2)}, u32[]{:S(2)}) %collective-permute-start.18) | collective-permute-done | bytes 655392 | tf_op jit(solution)/shard_map/ppermute | solution.py:209
  102.7 3.2 collective-permute-start.25
  110.0 3.2 collective-permute-start.14
  113.2 8.7 %collective-permute-done.19 = bf16[4,2,16,2560]{3,2,1,0:T(8,128)(2,1)S(1)} collective-permute-done((bf16[4,2,16,2560]{3,2,1,0:T(8,128)(2,1)}, bf16[4,2,16,2560]{3,2,1,0:T(8,128)(2,1)S(1)}, u32[]{:S(2)}, u32[]{:S(2)}) %collective-permute-start.19) | collective-permute-done | bytes 655392 | tf_op jit(solution)/shard_map/ppermute | solution.py:209
  121.9 3.2 collective-permute-start.26
  132.8 20.6 %collective-permute-done.20 = bf16[4,2,16,2560]{3,2,1,0:T(8,128)(2,1)S(1)} collective-permute-done((bf16[4,2,16,2560]{3,2,1,0:T(8,128)(2,1)S(1)}, bf16[4,2,16,2560]{3,2,1,0:T(8,128)(2,1)S(1)}, u32[]{:S(2)}, u32[]{:S(2)}) %collective-permute-start.20) | collective-permute-done | bytes 655392 | tf_op jit(solution)/shard_map/ppermute | solution.py:209
  154.8 3.1 slice_bitcast_fusion
  160.4 3.9 copy.151
  164.3 4.0 copy.153
  170.8 3.6 fusion.57
  180.6 3.0 fusion.26
  184.7 2.9 convolution_bitcast_fusion.2
  189.2 5.2 fusion.75
  194.5 3.1 fusion.30
  197.9 4.1 collective-permute-done.27
  202.2 14.3 %collective-permute-start.28 = (bf16[128,2048]{1,0:T(8,128)(2,1)S(1)}, bf16[128,2048]{1,0:T(8,128)(2,1)}, u32[]{:S(2)}, u32[]{:S(2)}) collective-permute-start(bf16[128,2048]{1,0:T(8,128)(2,1)S(1)} %fusion.93), channel_id=1, source_target_pairs={{0,2},{2,0},{1,3},{3,1},{4,6},{6,4},{5,7},{7,5},{8,10},{10,8},{9,1... | collective-permute-start | bytes 1572872 | tf_op jit(solution)/shard_map/ppermute | solution.py:119
  217.1 12.8 %collective-permute-done.28 = bf16[128,2048]{1,0:T(8,128)(2,1)} collective-permute-done((bf16[128,2048]{1,0:T(8,128)(2,1)S(1)}, bf16[128,2048]{1,0:T(8,128)(2,1)}, u32[]{:S(2)}, u32[]{:S(2)}) %collective-permute-start.28) | collective-permute-done | bytes 524320 | tf_op jit(solution)/shard_map/ppermute | solution.py:119
  233.7 7.4 %collective-permute-done.33 = bf16[128,2048]{1,0:T(8,128)(2,1)} collective-permute-done((bf16[128,2048]{1,0:T(8,128)(2,1)S(1)}, bf16[128,2048]{1,0:T(8,128)(2,1)}, u32[]{:S(2)}, u32[]{:S(2)}) %collective-permute-start.33) | collective-permute-done | bytes 524320 | tf_op jit(solution)/shard_map/ppermute | solution.py:108
  242.5 8.9 %collective-permute-done.29 = bf16[128,2048]{1,0:T(8,128)(2,1)S(1)} collective-permute-done((bf16[128,2048]{1,0:T(8,128)(2,1)S(1)}, bf16[128,2048]{1,0:T(8,128)(2,1)S(1)}, u32[]{:S(2)}, u32[]{:S(2)}) %collective-permute-start.29) | collective-permute-done | bytes 524320 | tf_op jit(solution)/shard_map/ppermute | solution.py:108
  255.8 8.4 %fusion = f32[512,1408]{1,0:T(8,128)} fusion(bf16[512,2048]{1,0:T(8,128)(2,1)} %bitcast.450, bf16[2048,4224]{1,0:T(8,128)(2,1)} %all-gather.2.cloned.1.call-done), kind=kOutput, calls=%fused_computation.1 | convolution fusion | flops 2952790016 | bytes 10747904 | tf_op jit(solution)/shard_map/dot_general | solution.py:27
  265.7 5.0 fusion.6
  270.7 6.6 %multiply_convert_fusion.1 = (bf16[512,1408]{1,0:T(8,128)(2,1)S(1)}, bf16[512,1408]{1,0:T(8,128)(2,1)S(1)}, bf16[512,1408]{1,0:T(8,128)(2,1)S(1)}) fusion(f32[512,1408]{1,0:T(8,128)} %fusion, f32[512,1408]{1,0:T(8,128)} %fusion.6, bf16[512,2048]{1,0:T(8,128)(2,1)S(1)} %bitcast.454, bf16[2048,4224]{1,0:T(8,128)(2,1)S(1)} %copy-done.43), kind=kOutput, calls=%fused_computation.17 | convolution fusion | flops 2963603456 | bytes 17956864 | tf_op jit(solution)/shard_map/dot_general | solution.py:27
  281.6 15.7 %shard_map.247 = bf16[2048,4224]{1,0:T(8,128)(2,1)} custom-call(bf16[512,2048]{1,0:T(8,128)(2,1)} %bitcast.452, bf16[512,2048]{1,0:T(8,128)(2,1)} %bitcast.451, bf16[512,4224]{1,0:T(8,128)(2,1)} %pad_maximum_fusion.right_ref), custom_call_target="tpu_custom_call" | custom-call | flops 8858370048 | bytes 25821184 | tf_op jit(solution)/shard_map/pallas_call | solution.py:64
  297.2 6.0 fusion.4
  303.3 5.5 fusion.12
  310.2 5.5 fusion.2
  322.0 13.7 %collective-permute-done.36 = bf16[128,2048]{1,0:T(8,128)(2,1)S(1)} collective-permute-done((bf16[128,2048]{1,0:T(8,128)(2,1)S(1)}, bf16[128,2048]{1,0:T(8,128)(2,1)S(1)}, u32[]{:S(2)}, u32[]{:S(2)}) %collective-permute-start.36) | collective-permute-done | bytes 524320 | tf_op jit(solution)/shard_map/ppermute | solution.py:119
  336.2 13.8 %collective-permute-done.32 = bf16[128,2048]{1,0:T(8,128)(2,1)S(1)} collective-permute-done((bf16[128,2048]{1,0:T(8,128)(2,1)S(1)}, bf16[128,2048]{1,0:T(8,128)(2,1)S(1)}, u32[]{:S(2)}, u32[]{:S(2)}) %collective-permute-start.32) | collective-permute-done | bytes 524320 | tf_op jit(solution)/shard_map/ppermute | solution.py:119
  353.1 16.4 %collective-permute-done.37 = bf16[128,2048]{1,0:T(8,128)(2,1)S(1)} collective-permute-done((bf16[128,2048]{1,0:T(8,128)(2,1)S(1)}, bf16[128,2048]{1,0:T(8,128)(2,1)S(1)}, u32[]{:S(2)}, u32[]{:S(2)}) %collective-permute-start.37) | collective-permute-done | bytes 524320 | tf_op jit(solution)/shard_map/ppermute | solution.py:108
  370.6 3.0 collective-permute-done.38
  375.2 4.9 fusion.135
  383.0 3.3 fusion.60
  387.6 3.3 convolution_select_fusion
  402.4 10.9 %shard_map.246 = bf16[2048,2560]{1,0:T(8,128)(2,1)} custom-call(bf16[512,2048]{1,0:T(8,128)(2,1)} %bitcast.447, bf16[512,2048]{1,0:T(8,128)(2,1)} %bitcast.449, bf16[512,2560]{1,0:T(8,128)(2,1)} %constant_dynamic-update-slice_fusion.4.right_ref), custom_call_target="tpu_custom_call" | custom-call | flops 5368709120 | bytes 17301504 | tf_op jit(solution)/shard_map/pallas_call | solution.py:64
  413.3 9.5 %fusion.146 = (bf16[4,2,4,32,2560]{4,3,2,1,0:T(8,128)(2,1)}, bf16[4,2,4,32,2560]{4,3,2,1,0:T(8,128)(2,1)}) fusion(bf16[4,2,4,64,2560]{4,3,2,1,0:T(8,128)(2,1)} %bitcast.432), kind=kLoop, calls=%fused_computation.288 | loop fusion | bytes 20971520 | tf_op jit(solution)/shard_map/slice | solution.py:158
  422.8 7.6 %constant_dynamic-slice_fusion.3 = (bf16[1,2,4,32,2560]{4,3,2,1,0:T(8,128)(2,1)}, bf16[1,2,4,32,2560]{4,3,2,1,0:T(8,128)(2,1)}, bf16[1,2,4,32,2560]{4,3,2,1,0:T(...) fusion(bf16[4,2,4,32,2560]{4,3,2,1,0:T(8,128)(2,1)} %get-tuple-, ...), kind=kLoop, calls=%fused_computation.260 | loop fusion | bytes 20971544 | tf_op jit(solution)/shard_map/jit(dynamic_index_in_dim)/dynamic_slice | solution.py:140
  432.4 2.9 fusion.39
  446.7 17.3 %collective-permute-done.41 = bf16[2,4,32,2560]{3,2,0,1:T(8,128)(2,1)} collective-permute-done((bf16[2,4,32,2560]{3,2,0,1:T(8,128)(2,1)}, bf16[2,4,32,2560]{3,2,0,1:T(8,128)(2,1)}, u32[]{:S(2)}, u32[]{:S(2)}) %collective-permute-start.41) | collective-permute-done | bytes 1310752 | tf_op jit(solution)/shard_map/ppermute | solution.py:146
  464.0 3.1 fusion.19
  470.1 2.9 fusion.16
  473.0 3.6 collective-permute-start.48
  480.5 18.4 %collective-permute-done.42 = bf16[2,4,32,2560]{3,2,0,1:T(8,128)(2,1)} collective-permute-done((bf16[2,4,32,2560]{3,2,0,1:T(8,128)(2,1)}, bf16[2,4,32,2560]{3,2,0,1:T(8,128)(2,1)}, u32[]{:S(2)}, u32[]{:S(2)}) %collective-permute-start.42) | collective-permute-done | bytes 1310752 | tf_op jit(solution)/shard_map/ppermute | solution.py:146
  501.7 2.9 fusion.69
  505.5 8.3 %all-to-all-start.1 = ((f32[128,3,16]{2,1,0:T(4,128)}), f32[128,3,16]{2,1,0:T(4,128)S(1)}, u32[]{:S(2)}, u32[]{:S(2)}) async-start(f32[128,3,16]{2,1,0:T(4,128)} %copy.169), calls=%async_computation.1 | async-start | bytes 524288 | tf_op jit(solution)/shard_map/all_to_all | solution.py:224
  515.9 2.9 collective-permute-start.49
  518.8 29.6 %collective-permute-done.43 = bf16[2,4,32,2560]{3,2,0,1:T(8,128)(2,1)} collective-permute-done((bf16[2,4,32,2560]{3,2,0,1:T(8,128)(2,1)}, bf16[2,4,32,2560]{3,2,0,1:T(8,128)(2,1)}, u32[]{:S(2)}, u32[]{:S(2)}) %collective-permute-start.43) | collective-permute-done | bytes 1310752 | tf_op jit(solution)/shard_map/ppermute | solution.py:146
  550.2 21.3 %collective-permute-done.49 = bf16[2,4,32,2560]{3,2,0,1:T(8,128)(2,1)S(1)} collective-permute-done((bf16[2,4,32,2560]{3,2,0,1:T(8,128)(2,1)S(1)}, bf16[2,4,32,2560]{3,2,0,1:T(8,128)(2,1)S(1)}, u32[]{:S(2)}, u32[]{:S(2)}) %collective-permute-start.49) | collective-permute-done | bytes 1310752 | tf_op jit(solution)/shard_map/ppermute | solution.py:146
  574.3 8.9 %collective-permute-done.50 = bf16[2,32,2560]{2,1,0:T(8,128)(2,1)S(1)} collective-permute-done((bf16[2,32,2560]{2,1,0:T(8,128)(2,1)S(1)}, bf16[2,32,2560]{2,1,0:T(8,128)(2,1)S(1)}, u32[]{:S(2)}, u32[]{:S(2)}) %collective-permute-start.50) | collective-permute-done | bytes 327712 | tf_op jit(solution)/shard_map/ppermute | solution.py:146
  583.2 3.8 collective-permute-start.51
  587.2 8.7 %collective-permute-done.51 = bf16[2,32,2560]{2,1,0:T(8,128)(2,1)S(1)} collective-permute-done((bf16[2,32,2560]{2,1,0:T(8,128)(2,1)S(1)}, bf16[2,32,2560]{2,1,0:T(8,128)(2,1)S(1)}, u32[]{:S(2)}, u32[]{:S(2)}) %collective-permute-start.51) | collective-permute-done | bytes 327712 | tf_op jit(solution)/shard_map/ppermute | solution.py:146
  595.9 3.8 collective-permute-start.52
  599.8 5.8 collective-permute-done.52
  607.9 7.0 %collective-permute-done.53 = bf16[64,2560]{1,0:T(8,128)(2,1)S(1)} collective-permute-done((bf16[64,2560]{1,0:T(8,128)(2,1)S(1)}, bf16[64,2560]{1,0:T(8,128)(2,1)S(1)}, u32[]{:S(2)}, u32[]{:S(2)}) %collective-permute-start.53) | collective-permute-done | bytes 327712 | tf_op jit(solution)/shard_map/ppermute | solution.py:165
  (319 shorter events, 138.7 us)
Async XLA Ops:
  11.5 27.0 %collective-permute-start.2 = (bf16[64,2560]{1,0:T(8,128)(2,1)S(1)}, bf16[64,2560]{1,0:T(8,128)(2,1)S(1)}, u32[]{:S(2)}, u32[]{:S(2)}) collective-permute-start(bf16[64,2560]{1,0:T(8,128)(2,1)S(1)} %bitcast_dynamic-update-slice_fusion.37), channel_id=1, source_target_pairs={{0,16},{4,20},{8,24},{12,28},{16,0},{20,4},{24,8},{28,12},{32,48},... | collective-permute-start | bytes 983048 | tf_op jit(solution)/shard_map/ppermute | solution.py:173
  16.2 19.7 %all-to-all-start = ((f32[128,3,16]{2,1,0:T(4,128)}), f32[128,3,16]{2,1,0:T(4,128)S(1)}, u32[]{:S(2)}, u32[]{:S(2)}) async-start(f32[128,3,16]{2,1,0:T(4,128)} %broadcast_in_dim.155), calls=%async_computation | async-start | bytes 524288 | tf_op jit(solution)/shard_map/all_to_all | solution.py:217
  25.1 230.6 %all-gather.2.cloned.1.call-start = ((), (), s32[]{:S(2)}) async-start(), calls=%async_computation.3 | async-start | bytes 17842176 | tf_op jit(solution)/shard_map/all_gather | solution.py:262
  27.1 588.6 %reduce-scatter.2.cloned.1.call-start = ((), (), s32[]{:S(2)}) async-start(), calls=%async_computation.4 | async-start | bytes 17842176 | tf_op jit(solution)/shard_map/reduce_scatter | solution.py:308
  37.5 18.8 %collective-permute-start = (bf16[128,2048]{1,0:T(8,128)(2,1)}, bf16[128,2048]{1,0:T(8,128)(2,1)}, u32[]{:S(2)}, u32[]{:S(2)}) collective-permute-start(bf16[128,2048]{1,0:T(8,128)(2,1)} %fusion.63), channel_id=1, source_target_pairs={{0,2},{2,0},{1,3},{3,1},{4,6},{6,4},{5,7},{7,5},{8,10},{10,8},{9,1... | collective-permute-start | bytes 1572872 | tf_op jit(solution)/shard_map/ppermute | solution.py:108
  38.6 9.8 %collective-permute-start.3 = (bf16[2,16,2560]{2,1,0:T(8,128)(2,1)S(1)}, bf16[2,16,2560]{2,1,0:T(8,128)(2,1)S(1)}, u32[]{:S(2)}, u32[]{:S(2)}) collective-permute-start(bf16[2,16,2560]{2,1,0:T(8,128)(2,1)S(1)} %get-tuple-element.60), channel_id=1, source_target_pairs={{0,4},{4,8},{8,12},{12,0},{16,20},{20,24},{24,28},{28,16},{32,36},... | collective-permute-start | bytes 491528 | tf_op jit(solution)/shard_map/ppermute | solution.py:189
  39.3 9.2 %collective-permute-start.9 = (bf16[2,16,2560]{2,1,0:T(8,128)(2,1)S(1)}, bf16[2,16,2560]{2,1,0:T(8,128)(2,1)S(1)}, u32[]{:S(2)}, u32[]{:S(2)}) collective-permute-start(bf16[2,16,2560]{2,1,0:T(8,128)(2,1)S(1)} %get-tuple-element.59), channel_id=1, source_target_pairs={{0,12},{4,0},{8,4},{12,8},{16,28},{20,16},{24,20},{28,24},{32,44},... | collective-permute-start | bytes 491528 | tf_op jit(solution)/shard_map/ppermute | solution.py:189
  41.9 9.8 %collective-permute-start.15 = (bf16[2,16,2560]{2,1,0:T(8,128)(2,1)S(1)}, bf16[2,16,2560]{2,1,0:T(8,128)(2,1)S(1)}, u32[]{:S(2)}, u32[]{:S(2)}) collective-permute-start(bf16[2,16,2560]{2,1,0:T(8,128)(2,1)S(1)} %get-tuple-element.58), channel_id=1, source_target_pairs={{0,32},{4,36},{8,40},{12,44},{16,48},{20,52},{24,56},{28,60},{32,6... | collective-permute-start | bytes 491528 | tf_op jit(solution)/shard_map/ppermute | solution.py:203
  42.7 9.0 %collective-permute-start.21 = (bf16[2,16,2560]{2,1,0:T(8,128)(2,1)S(1)}, bf16[2,16,2560]{2,1,0:T(8,128)(2,1)S(1)}, u32[]{:S(2)}, u32[]{:S(2)}) collective-permute-start(bf16[2,16,2560]{2,1,0:T(8,128)(2,1)S(1)} %get-tuple-element.57), channel_id=1, source_target_pairs={{0,96},{4,100},{8,104},{12,108},{16,112},{20,116},{24,120},{28,124... | collective-permute-start | bytes 491528 | tf_op jit(solution)/shard_map/ppermute | solution.py:203
  48.4 9.2 %collective-permute-start.4 = (bf16[2,16,2560]{2,1,0:T(8,128)(2,1)S(1)}, bf16[2,16,2560]{2,1,0:T(8,128)(2,1)S(1)}, u32[]{:S(2)}, u32[]{:S(2)}) collective-permute-start(bf16[2,16,2560]{2,1,0:T(8,128)(2,1)S(1)} %collective-permute-done.3), channel_id=1, source_target_pairs={{0,4},{4,8},{8,12},{12,0},{16,20},{20,24},{24,28},{28,16},{32,36},... | collective-permute-start | bytes 491528 | tf_op jit(solution)/shard_map/ppermute | solution.py:189
  48.5 9.2 %collective-permute-start.10 = (bf16[2,16,2560]{2,1,0:T(8,128)(2,1)S(1)}, bf16[2,16,2560]{2,1,0:T(8,128)(2,1)S(1)}, u32[]{:S(2)}, u32[]{:S(2)}) collective-permute-start(bf16[2,16,2560]{2,1,0:T(8,128)(2,1)S(1)} %collective-permute-done.9), channel_id=1, source_target_pairs={{0,12},{4,0},{8,4},{12,8},{16,28},{20,16},{24,20},{28,24},{32,44},... | collective-permute-start | bytes 491528 | tf_op jit(solution)/shard_map/ppermute | solution.py:189
  51.7 9.2 %collective-permute-start.16 = (bf16[2,16,2560]{2,1,0:T(8,128)(2,1)S(1)}, bf16[2,16,2560]{2,1,0:T(8,128)(2,1)S(1)}, u32[]{:S(2)}, u32[]{:S(2)}) collective-permute-start(bf16[2,16,2560]{2,1,0:T(8,128)(2,1)S(1)} %collective-permute-done.15), channel_id=1, source_target_pairs={{0,32},{4,36},{8,40},{12,44},{16,48},{20,52},{24,56},{28,60},{32,6... | collective-permute-start | bytes 491528 | tf_op jit(solution)/shard_map/ppermute | solution.py:203
  51.7 9.3 %collective-permute-start.22 = (bf16[2,16,2560]{2,1,0:T(8,128)(2,1)S(1)}, bf16[2,16,2560]{2,1,0:T(8,128)(2,1)S(1)}, u32[]{:S(2)}, u32[]{:S(2)}) collective-permute-start(bf16[2,16,2560]{2,1,0:T(8,128)(2,1)S(1)} %collective-permute-done.21), channel_id=1, source_target_pairs={{0,96},{4,100},{8,104},{12,108},{16,112},{20,116},{24,120},{28,124... | collective-permute-start | bytes 491528 | tf_op jit(solution)/shard_map/ppermute | solution.py:203
  57.5 49.6 %collective-permute-start.1 = (bf16[2,128,2048]{2,1,0:T(8,128)(2,1)S(1)}, bf16[2,128,2048]{2,1,0:T(8,128)(2,1)}, u32[]{:S(2)}, u32[]{:S(2)}) collective-permute-start(bf16[2,128,2048]{2,1,0:T(8,128)(2,1)S(1)} %pad_maximum_fusion.5), channel_id=1, source_target_pairs={{0,1},{1,0},{2,3},{3,2},{4,5},{5,4},{6,7},{7,6},{8,9},{9,8},{10,11... | collective-permute-start | bytes 3145736 | tf_op jit(solution)/shard_map/ppermute | solution.py:110
  57.6 8.0 %collective-permute-start.5 = (bf16[2,16,2560]{2,1,0:T(8,128)(2,1)S(1)}, bf16[2,16,2560]{2,1,0:T(8,128)(2,1)S(1)}, u32[]{:S(2)}, u32[]{:S(2)}) collective-permute-start(bf16[2,16,2560]{2,1,0:T(8,128)(2,1)S(1)} %collective-permute-done.4), channel_id=1, source_target_pairs={{0,4},{4,8},{8,12},{12,0},{16,20},{20,24},{24,28},{28,16},{32,36},... | collective-permute-start | bytes 491528 | tf_op jit(solution)/shard_map/ppermute | solution.py:189
  57.7 8.0 %collective-permute-start.11 = (bf16[2,16,2560]{2,1,0:T(8,128)(2,1)S(1)}, bf16[2,16,2560]{2,1,0:T(8,128)(2,1)S(1)}, u32[]{:S(2)}, u32[]{:S(2)}) collective-permute-start(bf16[2,16,2560]{2,1,0:T(8,128)(2,1)S(1)} %collective-permute-done.10), channel_id=1, source_target_pairs={{0,12},{4,0},{8,4},{12,8},{16,28},{20,16},{24,20},{28,24},{32,44},... | collective-permute-start | bytes 491528 | tf_op jit(solution)/shard_map/ppermute | solution.py:189
  60.9 8.7 %collective-permute-start.17 = (bf16[2,16,2560]{2,1,0:T(8,128)(2,1)S(1)}, bf16[2,16,2560]{2,1,0:T(8,128)(2,1)S(1)}, u32[]{:S(2)}, u32[]{:S(2)}) collective-permute-start(bf16[2,16,2560]{2,1,0:T(8,128)(2,1)S(1)} %collective-permute-done.16), channel_id=1, source_target_pairs={{0,32},{4,36},{8,40},{12,44},{16,48},{20,52},{24,56},{28,60},{32,6... | collective-permute-start | bytes 491528 | tf_op jit(solution)/shard_map/ppermute | solution.py:203
  61.0 9.2 %collective-permute-start.23 = (bf16[2,16,2560]{2,1,0:T(8,128)(2,1)S(1)}, bf16[2,16,2560]{2,1,0:T(8,128)(2,1)S(1)}, u32[]{:S(2)}, u32[]{:S(2)}) collective-permute-start(bf16[2,16,2560]{2,1,0:T(8,128)(2,1)S(1)} %collective-permute-done.22), channel_id=1, source_target_pairs={{0,96},{4,100},{8,104},{12,108},{16,112},{20,116},{24,120},{28,124... | collective-permute-start | bytes 491528 | tf_op jit(solution)/shard_map/ppermute | solution.py:203
  65.6 24.3 %collective-permute-start.6 = (bf16[2,4,16,2560]{3,2,1,0:T(8,128)(2,1)S(1)}, bf16[2,4,16,2560]{3,2,1,0:T(8,128)(2,1)}, u32[]{:S(2)}, u32[]{:S(2)}) collective-permute-start(bf16[2,4,16,2560]{3,2,1,0:T(8,128)(2,1)S(1)} %bitcast_dynamic-update-slice_fusion.25), channel_id=1, source_target_pairs={{0,32},{4,36},{8,40},{12,44},{16,48},{20,52},{24,56},{28,60},{32,6... | collective-permute-start | bytes 1966088 | tf_op jit(solution)/shard_map/ppermute | solution.py:195
  66.4 23.5 %collective-permute-start.12 = (bf16[2,4,16,2560]{3,2,1,0:T(8,128)(2,1)}, bf16[2,4,16,2560]{3,2,1,0:T(8,128)(2,1)}, u32[]{:S(2)}, u32[]{:S(2)}) collective-permute-start(bf16[2,4,16,2560]{3,2,1,0:T(8,128)(2,1)} %bitcast_dynamic-update-slice_fusion.21), channel_id=1, source_target_pairs={{0,96},{4,100},{8,104},{12,108},{16,112},{20,116},{24,120},{28,124... | collective-permute-start | bytes 1966088 | tf_op jit(solution)/shard_map/ppermute | solution.py:195
  70.3 32.5 %collective-permute-start.18 = (bf16[4,2,16,2560]{3,2,1,0:T(8,128)(2,1)}, bf16[4,2,16,2560]{3,2,1,0:T(8,128)(2,1)}, u32[]{:S(2)}, u32[]{:S(2)}) collective-permute-start(bf16[4,2,16,2560]{3,2,1,0:T(8,128)(2,1)} %bitcast_dynamic-update-slice_fusion.33), channel_id=1, source_target_pairs={{0,4},{4,8},{8,12},{12,0},{16,20},{20,24},{24,28},{28,16},{32,36},... | collective-permute-start | bytes 1966088 | tf_op jit(solution)/shard_map/ppermute | solution.py:209
  70.3 32.4 %collective-permute-start.24 = (bf16[4,2,16,2560]{3,2,1,0:T(8,128)(2,1)S(1)}, bf16[4,2,16,2560]{3,2,1,0:T(8,128)(2,1)}, u32[]{:S(2)}, u32[]{:S(2)}) collective-permute-start(bf16[4,2,16,2560]{3,2,1,0:T(8,128)(2,1)S(1)} %bitcast_dynamic-update-slice_fusion.29), channel_id=1, source_target_pairs={{0,12},{4,0},{8,4},{12,8},{16,28},{20,16},{24,20},{28,24},{32,44},... | collective-permute-start | bytes 1966088 | tf_op jit(solution)/shard_map/ppermute | solution.py:209
  89.9 20.1 %collective-permute-start.7 = (bf16[2,4,16,2560]{3,2,1,0:T(8,128)(2,1)}, bf16[2,4,16,2560]{3,2,1,0:T(8,128)(2,1)S(1)}, u32[]{:S(2)}, u32[]{:S(2)}) collective-permute-start(bf16[2,4,16,2560]{3,2,1,0:T(8,128)(2,1)} %collective-permute-done.6), channel_id=1, source_target_pairs={{0,32},{4,36},{8,40},{12,44},{16,48},{20,52},{24,56},{28,60},{32,6... | collective-permute-start | bytes 1966088 | tf_op jit(solution)/shard_map/ppermute | solution.py:195
  89.9 20.1 %collective-permute-start.13 = (bf16[2,4,16,2560]{3,2,1,0:T(8,128)(2,1)}, bf16[2,4,16,2560]{3,2,1,0:T(8,128)(2,1)S(1)}, u32[]{:S(2)}, u32[]{:S(2)}) collective-permute-start(bf16[2,4,16,2560]{3,2,1,0:T(8,128)(2,1)} %collective-permute-done.12), channel_id=1, source_target_pairs={{0,96},{4,100},{8,104},{12,108},{16,112},{20,116},{24,120},{28,124... | collective-permute-start | bytes 1966088 | tf_op jit(solution)/shard_map/ppermute | solution.py:195
  102.7 19.2 %collective-permute-start.19 = (bf16[4,2,16,2560]{3,2,1,0:T(8,128)(2,1)}, bf16[4,2,16,2560]{3,2,1,0:T(8,128)(2,1)S(1)}, u32[]{:S(2)}, u32[]{:S(2)}) collective-permute-start(bf16[4,2,16,2560]{3,2,1,0:T(8,128)(2,1)} %collective-permute-done.18), channel_id=1, source_target_pairs={{0,4},{4,8},{8,12},{12,0},{16,20},{20,24},{24,28},{28,16},{32,36},... | collective-permute-start | bytes 1966088 | tf_op jit(solution)/shard_map/ppermute | solution.py:209
  102.7 19.2 %collective-permute-start.25 = (bf16[4,2,16,2560]{3,2,1,0:T(8,128)(2,1)}, bf16[4,2,16,2560]{3,2,1,0:T(8,128)(2,1)S(1)}, u32[]{:S(2)}, u32[]{:S(2)}) collective-permute-start(bf16[4,2,16,2560]{3,2,1,0:T(8,128)(2,1)} %collective-permute-done.24), channel_id=1, source_target_pairs={{0,12},{4,0},{8,4},{12,8},{16,28},{20,16},{24,20},{28,24},{32,44},... | collective-permute-start | bytes 1966088 | tf_op jit(solution)/shard_map/ppermute | solution.py:209
  110.0 15.8 %collective-permute-start.8 = (bf16[2,4,16,2560]{3,2,1,0:T(8,128)(2,1)S(1)}, bf16[2,4,16,2560]{3,2,1,0:T(8,128)(2,1)S(1)}, u32[]{:S(2)}, u32[]{:S(2)}) collective-permute-start(bf16[2,4,16,2560]{3,2,1,0:T(8,128)(2,1)S(1)} %collective-permute-done.7), channel_id=1, source_target_pairs={{0,32},{4,36},{8,40},{12,44},{16,48},{20,52},{24,56},{28,60},{32,6... | collective-permute-start | bytes 1966088 | tf_op jit(solution)/shard_map/ppermute | solution.py:195
  110.0 20.4 %collective-permute-start.14 = (bf16[2,4,16,2560]{3,2,1,0:T(8,128)(2,1)S(1)}, bf16[2,4,16,2560]{3,2,1,0:T(8,128)(2,1)S(1)}, u32[]{:S(2)}, u32[]{:S(2)}) collective-permute-start(bf16[2,4,16,2560]{3,2,1,0:T(8,128)(2,1)S(1)} %collective-permute-done.13), channel_id=1, source_target_pairs={{0,96},{4,100},{8,104},{12,108},{16,112},{20,116},{24,120},{28,124... | collective-permute-start | bytes 1966088 | tf_op jit(solution)/shard_map/ppermute | solution.py:195
  121.9 31.5 %collective-permute-start.20 = (bf16[4,2,16,2560]{3,2,1,0:T(8,128)(2,1)S(1)}, bf16[4,2,16,2560]{3,2,1,0:T(8,128)(2,1)S(1)}, u32[]{:S(2)}, u32[]{:S(2)}) collective-permute-start(bf16[4,2,16,2560]{3,2,1,0:T(8,128)(2,1)S(1)} %collective-permute-done.19), channel_id=1, source_target_pairs={{0,4},{4,8},{8,12},{12,0},{16,20},{20,24},{24,28},{28,16},{32,36},... | collective-permute-start | bytes 1966088 | tf_op jit(solution)/shard_map/ppermute | solution.py:209
  121.9 32.8 %collective-permute-start.26 = (bf16[4,2,16,2560]{3,2,1,0:T(8,128)(2,1)S(1)}, bf16[4,2,16,2560]{3,2,1,0:T(8,128)(2,1)S(1)}, u32[]{:S(2)}, u32[]{:S(2)}) collective-permute-start(bf16[4,2,16,2560]{3,2,1,0:T(8,128)(2,1)S(1)} %collective-permute-done.25), channel_id=1, source_target_pairs={{0,12},{4,0},{8,4},{12,8},{16,28},{20,16},{24,20},{28,24},{32,44},... | collective-permute-start | bytes 1966088 | tf_op jit(solution)/shard_map/ppermute | solution.py:209
  197.8 4.2 collective-permute-start.27
  202.2 27.7 %collective-permute-start.28 = (bf16[128,2048]{1,0:T(8,128)(2,1)S(1)}, bf16[128,2048]{1,0:T(8,128)(2,1)}, u32[]{:S(2)}, u32[]{:S(2)}) collective-permute-start(bf16[128,2048]{1,0:T(8,128)(2,1)S(1)} %fusion.93), channel_id=1, source_target_pairs={{0,2},{2,0},{1,3},{3,1},{4,6},{6,4},{5,7},{7,5},{8,10},{10,8},{9,1... | collective-permute-start | bytes 1572872 | tf_op jit(solution)/shard_map/ppermute | solution.py:119
  216.5 24.6 %collective-permute-start.33 = (bf16[128,2048]{1,0:T(8,128)(2,1)S(1)}, bf16[128,2048]{1,0:T(8,128)(2,1)}, u32[]{:S(2)}, u32[]{:S(2)}) collective-permute-start(bf16[128,2048]{1,0:T(8,128)(2,1)S(1)} %bitcast.439), channel_id=1, source_target_pairs={{0,2},{2,0},{1,3},{3,1},{4,6},{6,4},{5,7},{7,5},{8,10},{10,8},{9,1... | collective-permute-start | bytes 1572872 | tf_op jit(solution)/shard_map/ppermute | solution.py:108
  232.1 19.3 %collective-permute-start.29 = (bf16[128,2048]{1,0:T(8,128)(2,1)S(1)}, bf16[128,2048]{1,0:T(8,128)(2,1)S(1)}, u32[]{:S(2)}, u32[]{:S(2)}) collective-permute-start(bf16[128,2048]{1,0:T(8,128)(2,1)S(1)} %multiply_convert_fusion.4), channel_id=1, source_target_pairs={{0,2},{2,0},{1,3},{3,1},{4,6},{6,4},{5,7},{7,5},{8,10},{10,8},{9,1... | collective-permute-start | bytes 1572872 | tf_op jit(solution)/shard_map/ppermute | solution.py:108
  242.2 9.4 %collective-permute-start.34 = (bf16[2,128,2048]{2,1,0:T(8,128)(2,1)S(1)}, bf16[2,128,2048]{2,1,0:T(8,128)(2,1)S(1)}, u32[]{:S(2)}, u32[]{:S(2)}) collective-permute-start(bf16[2,128,2048]{2,1,0:T(8,128)(2,1)S(1)} %pad_maximum_fusion.7), channel_id=1, source_target_pairs={{0,1},{1,0},{2,3},{3,2},{4,5},{5,4},{6,7},{7,6},{8,9},{9,8},{10,11... | collective-permute-start | bytes 3145736 | tf_op jit(solution)/shard_map/ppermute | solution.py:110
  251.5 2.7 collective-permute-start.30
  309.1 7.4 %collective-permute-start.35 = (f32[2,128,2048]{2,1,0:T(8,128)S(1)}, f32[2,128,2048]{2,1,0:T(8,128)S(1)}, u32[]{:S(2)}, u32[]{:S(2)}) collective-permute-start(f32[2,128,2048]{2,1,0:T(8,128)S(1)} %bitcast.457), channel_id=1, source_target_pairs={{0,1},{1,0},{2,3},{3,2},{4,5},{5,4},{6,7},{7,6},{8,9},{9,8},{10,11... | collective-permute-start | bytes 6291464 | tf_op jit(solution)/shard_map/ppermute | solution.py:116
  315.9 4.3 collective-permute-start.31
  316.6 19.1 %collective-permute-start.36 = (bf16[128,2048]{1,0:T(8,128)(2,1)S(1)}, bf16[128,2048]{1,0:T(8,128)(2,1)S(1)}, u32[]{:S(2)}, u32[]{:S(2)}) collective-permute-start(bf16[128,2048]{1,0:T(8,128)(2,1)S(1)} %fusion.83), channel_id=1, source_target_pairs={{0,2},{2,0},{1,3},{3,1},{4,6},{6,4},{5,7},{7,5},{8,10},{10,8},{9,1... | collective-permute-start | bytes 1572872 | tf_op jit(solution)/shard_map/ppermute | solution.py:119
  320.4 29.5 %collective-permute-start.32 = (bf16[128,2048]{1,0:T(8,128)(2,1)S(1)}, bf16[128,2048]{1,0:T(8,128)(2,1)S(1)}, u32[]{:S(2)}, u32[]{:S(2)}) collective-permute-start(bf16[128,2048]{1,0:T(8,128)(2,1)S(1)} %fusion.87), channel_id=1, source_target_pairs={{0,2},{2,0},{1,3},{3,1},{4,6},{6,4},{5,7},{7,5},{8,10},{10,8},{9,1... | collective-permute-start | bytes 1572872 | tf_op jit(solution)/shard_map/ppermute | solution.py:119
  351.6 17.9 %collective-permute-start.37 = (bf16[128,2048]{1,0:T(8,128)(2,1)S(1)}, bf16[128,2048]{1,0:T(8,128)(2,1)S(1)}, u32[]{:S(2)}, u32[]{:S(2)}) collective-permute-start(bf16[128,2048]{1,0:T(8,128)(2,1)S(1)} %get-tuple-element.25), channel_id=1, source_target_pairs={{0,2},{2,0},{1,3},{3,1},{4,6},{6,4},{5,7},{7,5},{8,10},{10,8},{9,1... | collective-permute-start | bytes 1572872 | tf_op jit(solution)/shard_map/ppermute | solution.py:108
  370.6 3.0 collective-permute-start.38
  431.6 32.4 %collective-permute-start.41 = (bf16[2,4,32,2560]{3,2,0,1:T(8,128)(2,1)}, bf16[2,4,32,2560]{3,2,0,1:T(8,128)(2,1)}, u32[]{:S(2)}, u32[]{:S(2)}) collective-permute-start(bf16[2,4,32,2560]{3,2,0,1:T(8,128)(2,1)} %bitcast.420), channel_id=1, source_target_pairs={{0,32},{4,36},{8,40},{12,44},{16,48},{20,52},{24,56},{28,60},{32,6... | collective-permute-start | bytes 3932168 | tf_op jit(solution)/shard_map/ppermute | solution.py:146
  439.1 31.0 %collective-permute-start.47 = (bf16[2,4,32,2560]{3,2,0,1:T(8,128)(2,1)}, bf16[2,4,32,2560]{3,2,0,1:T(8,128)(2,1)}, u32[]{:S(2)}, u32[]{:S(2)}) collective-permute-start(bf16[2,4,32,2560]{3,2,0,1:T(8,128)(2,1)} %bitcast.419), channel_id=1, source_target_pairs={{0,96},{4,100},{8,104},{12,108},{16,112},{20,116},{24,120},{28,124... | collective-permute-start | bytes 3932168 | tf_op jit(solution)/shard_map/ppermute | solution.py:146
  446.6 23.5 %copy-start.12 = (bf16[1,2,4,32,2560]{4,3,2,1,0:T(8,128)(2,1)S(1)}, bf16[1,2,4,32,2560]{4,3,2,1,0:T(8,128)(2,1)}, u32[]{:S(2)}) copy-start(bf16[1,2,4,32,2560]{4,3,2,1,0:T(8,128)(2,1)} %get-tuple-element.43) | copy-start | bytes 3932164
  446.6 30.0 %collective-permute-start.39 = (f32[2,128,2048]{2,1,0:T(8,128)}, f32[2,128,2048]{2,1,0:T(8,128)}, u32[]{:S(2)}, u32[]{:S(2)}) collective-permute-start(f32[2,128,2048]{2,1,0:T(8,128)} %bitcast.105), channel_id=1, source_target_pairs={{0,1},{1,0},{2,3},{3,2},{4,5},{5,4},{6,7},{7,6},{8,9},{9,8},{10,11... | collective-permute-start | bytes 6291464 | tf_op jit(solution)/shard_map/ppermute | solution.py:116
  467.1 31.8 %collective-permute-start.42 = (bf16[2,4,32,2560]{3,2,0,1:T(8,128)(2,1)}, bf16[2,4,32,2560]{3,2,0,1:T(8,128)(2,1)}, u32[]{:S(2)}, u32[]{:S(2)}) collective-permute-start(bf16[2,4,32,2560]{3,2,0,1:T(8,128)(2,1)} %fusion.19), channel_id=1, source_target_pairs={{0,32},{4,36},{8,40},{12,44},{16,48},{20,52},{24,56},{28,60},{32,6... | collective-permute-start | bytes 3932168 | tf_op jit(solution)/shard_map/ppermute | solution.py:146
  470.1 28.7 %copy-start.11 = (bf16[1,2,4,32,2560]{4,3,2,1,0:T(8,128)(2,1)S(1)}, bf16[1,2,4,32,2560]{4,3,2,1,0:T(8,128)(2,1)}, u32[]{:S(2)}) copy-start(bf16[1,2,4,32,2560]{4,3,2,1,0:T(8,128)(2,1)} %get-tuple-element.77) | copy-start | bytes 3932164
  473.0 40.8 %collective-permute-start.48 = (bf16[2,4,32,2560]{3,2,0,1:T(8,128)(2,1)}, bf16[2,4,32,2560]{3,2,0,1:T(8,128)(2,1)}, u32[]{:S(2)}, u32[]{:S(2)}) collective-permute-start(bf16[2,4,32,2560]{3,2,0,1:T(8,128)(2,1)} %fusion.16), channel_id=1, source_target_pairs={{0,96},{4,100},{8,104},{12,108},{16,112},{20,116},{24,120},{28,124... | collective-permute-start | bytes 3932168 | tf_op jit(solution)/shard_map/ppermute | solution.py:146
  478.3 23.4 %copy-start.38 = (f32[2048]{0:T(1024)S(1)}, f32[2048]{0:T(1024)}, u32[]{:S(2)}) copy-start(f32[2048]{0:T(1024)} %copy-done.37) | copy-start | bytes 24580
  478.3 23.3 %copy-start.40 = (f32[128]{0:T(128)S(1)}, f32[128]{0:T(128)}, u32[]{:S(2)}) copy-start(f32[128]{0:T(128)} %copy-done.39) | copy-start | bytes 1540
  478.3 23.3 %collective-permute-start.40 = (bf16[128,2048]{1,0:T(8,128)(2,1)S(1)}, bf16[128,2048]{1,0:T(8,128)(2,1)S(1)}, u32[]{:S(2)}, u32[]{:S(2)}) collective-permute-start(bf16[128,2048]{1,0:T(8,128)(2,1)S(1)} %fusion.79), channel_id=1, source_target_pairs={{0,2},{2,0},{1,3},{3,1},{4,6},{6,4},{5,7},{7,5},{8,10},{10,8},{9,1... | collective-permute-start | bytes 1572872 | tf_op jit(solution)/shard_map/ppermute | solution.py:119
  501.6 46.7 %collective-permute-start.43 = (bf16[2,4,32,2560]{3,2,0,1:T(8,128)(2,1)}, bf16[2,4,32,2560]{3,2,0,1:T(8,128)(2,1)}, u32[]{:S(2)}, u32[]{:S(2)}) collective-permute-start(bf16[2,4,32,2560]{3,2,0,1:T(8,128)(2,1)} %fusion.20), channel_id=1, source_target_pairs={{0,32},{4,36},{8,40},{12,44},{16,48},{20,52},{24,56},{28,60},{32,6... | collective-permute-start | bytes 3932168 | tf_op jit(solution)/shard_map/ppermute | solution.py:146
  504.7 43.7 %copy-start.10 = (bf16[1,2,4,32,2560]{4,3,2,1,0:T(8,128)(2,1)S(1)}, bf16[1,2,4,32,2560]{4,3,2,1,0:T(8,128)(2,1)}, u32[]{:S(2)}) copy-start(bf16[1,2,4,32,2560]{4,3,2,1,0:T(8,128)(2,1)} %get-tuple-element.79) | copy-start | bytes 3932164
  505.5 101.6 %all-to-all-start.1 = ((f32[128,3,16]{2,1,0:T(4,128)}), f32[128,3,16]{2,1,0:T(4,128)S(1)}, u32[]{:S(2)}, u32[]{:S(2)}) async-start(f32[128,3,16]{2,1,0:T(4,128)} %copy.169), calls=%async_computation.1 | async-start | bytes 524288 | tf_op jit(solution)/shard_map/all_to_all | solution.py:224
  515.9 55.6 %copy-start.9 = (bf16[1,2,4,32,2560]{4,3,2,1,0:T(8,128)(2,1)S(1)}, bf16[1,2,4,32,2560]{4,3,2,1,0:T(8,128)(2,1)}, u32[]{:S(2)}) copy-start(bf16[1,2,4,32,2560]{4,3,2,1,0:T(8,128)(2,1)} %get-tuple-element.42) | copy-start | bytes 3932164
  515.9 55.6 %collective-permute-start.49 = (bf16[2,4,32,2560]{3,2,0,1:T(8,128)(2,1)S(1)}, bf16[2,4,32,2560]{3,2,0,1:T(8,128)(2,1)S(1)}, u32[]{:S(2)}, u32[]{:S(2)}) collective-permute-start(bf16[2,4,32,2560]{3,2,0,1:T(8,128)(2,1)S(1)} %fusion.17), channel_id=1, source_target_pairs={{0,96},{4,100},{8,104},{12,108},{16,112},{20,116},{24,120},{28,124... | collective-permute-start | bytes 3932168 | tf_op jit(solution)/shard_map/ppermute | solution.py:146
  550.1 24.0 %collective-permute-start.44 = (bf16[2,32,2560]{2,1,0:T(8,128)(2,1)S(1)}, bf16[2,32,2560]{2,1,0:T(8,128)(2,1)S(1)}, u32[]{:S(2)}, u32[]{:S(2)}) collective-permute-start(bf16[2,32,2560]{2,1,0:T(8,128)(2,1)S(1)} %dynamic-slice_bitcast_fusion.1), channel_id=1, source_target_pairs={{0,4},{4,8},{8,12},{12,0},{16,20},{20,24},{24,28},{28,16},{32,36},... | collective-permute-start | bytes 983048 | tf_op jit(solution)/shard_map/ppermute | solution.py:146
  571.8 11.3 %collective-permute-start.50 = (bf16[2,32,2560]{2,1,0:T(8,128)(2,1)S(1)}, bf16[2,32,2560]{2,1,0:T(8,128)(2,1)S(1)}, u32[]{:S(2)}, u32[]{:S(2)}) collective-permute-start(bf16[2,32,2560]{2,1,0:T(8,128)(2,1)S(1)} %dynamic-slice_bitcast_fusion), channel_id=1, source_target_pairs={{0,12},{4,0},{8,4},{12,8},{16,28},{20,16},{24,20},{28,24},{32,44},... | collective-permute-start | bytes 983048 | tf_op jit(solution)/shard_map/ppermute | solution.py:146
  574.2 12.8 %collective-permute-start.45 = (bf16[2,32,2560]{2,1,0:T(8,128)(2,1)S(1)}, bf16[2,32,2560]{2,1,0:T(8,128)(2,1)S(1)}, u32[]{:S(2)}, u32[]{:S(2)}) collective-permute-start(bf16[2,32,2560]{2,1,0:T(8,128)(2,1)S(1)} %fusion.116), channel_id=1, source_target_pairs={{0,4},{4,8},{8,12},{12,0},{16,20},{20,24},{24,28},{28,16},{32,36},... | collective-permute-start | bytes 983048 | tf_op jit(solution)/shard_map/ppermute | solution.py:146
  583.2 12.6 %collective-permute-start.51 = (bf16[2,32,2560]{2,1,0:T(8,128)(2,1)S(1)}, bf16[2,32,2560]{2,1,0:T(8,128)(2,1)S(1)}, u32[]{:S(2)}, u32[]{:S(2)}) collective-permute-start(bf16[2,32,2560]{2,1,0:T(8,128)(2,1)S(1)} %fusion.114), channel_id=1, source_target_pairs={{0,12},{4,0},{8,4},{12,8},{16,28},{20,16},{24,20},{28,24},{32,44},... | collective-permute-start | bytes 983048 | tf_op jit(solution)/shard_map/ppermute | solution.py:146
  587.1 12.6 %collective-permute-start.46 = (bf16[2,32,2560]{2,1,0:T(8,128)(2,1)S(1)}, bf16[2,32,2560]{2,1,0:T(8,128)(2,1)S(1)}, u32[]{:S(2)}, u32[]{:S(2)}) collective-permute-start(bf16[2,32,2560]{2,1,0:T(8,128)(2,1)S(1)} %fusion.117), channel_id=1, source_target_pairs={{0,4},{4,8},{8,12},{12,0},{16,20},{20,24},{24,28},{28,16},{32,36},... | collective-permute-start | bytes 983048 | tf_op jit(solution)/shard_map/ppermute | solution.py:146
  595.9 9.7 %collective-permute-start.52 = (bf16[2,32,2560]{2,1,0:T(8,128)(2,1)S(1)}, bf16[2,32,2560]{2,1,0:T(8,128)(2,1)S(1)}, u32[]{:S(2)}, u32[]{:S(2)}) collective-permute-start(bf16[2,32,2560]{2,1,0:T(8,128)(2,1)S(1)} %fusion.115), channel_id=1, source_target_pairs={{0,12},{4,0},{8,4},{12,8},{16,28},{20,16},{24,20},{28,24},{32,44},... | collective-permute-start | bytes 983048 | tf_op jit(solution)/shard_map/ppermute | solution.py:146
  605.7 9.1 %collective-permute-start.53 = (bf16[64,2560]{1,0:T(8,128)(2,1)S(1)}, bf16[64,2560]{1,0:T(8,128)(2,1)S(1)}, u32[]{:S(2)}, u32[]{:S(2)}) collective-permute-start(bf16[64,2560]{1,0:T(8,128)(2,1)S(1)} %fusion.130), channel_id=1, source_target_pairs={{0,16},{4,20},{8,24},{12,28},{16,0},{20,4},{24,8},{28,12},{32,48},... | collective-permute-start | bytes 983048 | tf_op jit(solution)/shard_map/ppermute | solution.py:165
  (41 other events, 319.4 us)
Sparse Core Ops, SparseCore 0:
  29.0 178.8 all-gather.1
  297.4 300.5 reduce-scatter.1

commit v18 on v13

--- a/solution.py
+++ b/solution.py
@@ -163,12 +163,13 @@
     return keep + lax.ppermute(give.astype(jnp.bfloat16), "dp", pair).astype(jnp.float32)
 
 
-def ring_gather(values):
+def ring_gather(values, rider):
     index = lax.axis_index("dp")
     x_pos, y_pos, z_pos = index % 4, (index // 4) % 2, index // 8
     zero = jnp.zeros((), jnp.int32)
     pair = [(i, i ^ 4) for i in range(32)]
     other = lax.ppermute(values, "dp", pair)
+    rider, other = lax.optimization_barrier((rider, other))
     both = jnp.zeros((2,) + values.shape, values.dtype)
     both = lax.dynamic_update_slice(both, values[None], (y_pos, zero, zero))
     both = lax.dynamic_update_slice(both, other[None], (1 - y_pos, zero, zero))
@@ -206,7 +207,7 @@
             for k in range(1, 4):
                 cur = lax.ppermute(cur, "dp", pairs)
                 full = lax.dynamic_update_slice(full, cur[:, :, None], (zero, zero, (x_pos - k * step) % 4, row_at, zero))
-    return full.reshape((-1, cols))
+    return full.reshape((-1, cols)), rider
 
 
 def small_gather(vectors):
@@ -239,16 +240,11 @@
     w_down,
     cotangent,
 ):
-    gains = small_gather(jnp.stack([attn_gain, forget_floor, mlp_gain]))
-    attn_full, floor_full, mlp_full = gains[0], gains[1], gains[2]
     part_index = lax.axis_index("tensor")
     local_width = w_query.shape[1]
     local_heads = local_width // HK
     hidden_width = w_gate.shape[1]
-    floor_local = lax.dynamic_slice_in_dim(
-        floor_full, part_index * local_width, local_width
-    ).reshape(local_heads, HK)
-    model_width = attn_full.shape[0]
+    model_width = tokens.shape[-1]
     slot_rows = jnp.bitwise_xor(part_index, jnp.array(SLOT_XOR, jnp.int32))
     doc_all = jnp.take(doc_ids[0], slot_rows, axis=0)
     row_count = doc_all.shape[0]
@@ -256,7 +252,12 @@
     cot_local = cotangent[0].reshape(-1, model_width)
     attn_pack = jnp.concatenate([w_query, w_forget, w_value, w_outgate, w_output.T], axis=1)
     mlp_pack = jnp.concatenate([w_gate, w_up, w_down.T], axis=1)
-    attn_all = ring_gather(attn_pack)
+    attn_all, gain_rows = ring_gather(attn_pack, jnp.stack([attn_gain, forget_floor, mlp_gain]))
+    gains = small_gather(gain_rows)
+    attn_full, floor_full, mlp_full = gains[0], gains[1], gains[2]
+    floor_local = lax.dynamic_slice_in_dim(
+        floor_full, part_index * local_width, local_width
+    ).reshape(local_heads, HK)
     mlp_all = lax.all_gather(mlp_pack, "dp", axis=0, tiled=True)
     wq_all = attn_all[:, 0 * local_width : 1 * local_width]
     wf_all = attn_all[:, 1 * local_width : 2 * local_width]

time: 612 us -> 624 us (1.020)
    unnamed x85 -> x99, local copies, waits for them, and re-layouts: 13.9 us -> 15.5 us
  transfers between devices with their start and end apart: 58 -> 58, of which waited for: 30 -> 37; matrix products, arithmetic and copies ran while one was open for 30% -> 29% of each run, Pallas kernels for 2% -> 2%
where the time goes in v18:
time: 624 us; the launch traced here: 616 us
  waiting for transfers between devices  239 us (38%)
  starting transfers between devices  115 us (18%)
  matrix products  89 us (14%)
  local copies, waits for them, and re-layouts  83.3 us (13%)
  other arithmetic  47.6 us (8%)
  Pallas kernels  26.5 us (4%)
  between operations  15.9 us (3%)
    ppermute x12, waiting for transfers between devices, ring_stage(): got = lax.ppermute(acc.astype(jnp.bfloat16), 'dp', pairs)  84.1 us
    ppermute x24, waiting for transfers between devices, ring_gather(): cur = lax.ppermute(cur, 'dp', pairs)  58.2 us
    ppermute x4, waiting for transfers between devices, row_sum(): lax.ppermute(theirs.astype(jnp.bfloat16), 'tensor', ACROSS)  43.4 us
    ppermute x24, starting transfers between devices, ring_gather(): cur = lax.ppermute(cur, 'dp', pairs)  41.5 us
    dot_general x8, matrix products, matmul_plain(): return jnp.dot(left, right, preferred_element_type=jnp.float32)  38.9 us
    ppermute x4, waiting for transfers between devices, row_gather(): across = lax.ppermute(values, 'tensor', ACROSS)  32.2 us
    dot_general x8, matrix products, times_trans(): lax.dot_general(left, right, (((1,), (1,)), ((), ())), preferred_element_...  31.9 us
    pallas_call x2, Pallas kernels, grad_pack(): pl.pallas_call(functools.partial(pack_kernel, per), grid=(rows_out // til...  26.5 us
  transfers between devices with their start and end apart: 58, of which 37 were waited for; matrix products, arithmetic and copies ran while one was open for 29% of the time, Pallas kernels for 2%

profile of v18, /device:TPU:0, one launch (start us, length us, event | category | flops | bytes accessed | tf_op | source)
XLA Modules:
  0.0 616.2 jit_solution(4248461236583476928)
XLA Ops:
  11.6 3.3 collective-permute-start
  19.2 3.4 collective-permute-done
  29.3 9.4 %all-to-all-start = ((f32[128,3,16]{2,1,0:T(4,128)}), f32[128,3,16]{2,1,0:T(4,128)S(1)}, u32[]{:S(2)}, u32[]{:S(2)}) async-start(f32[128,3,16]{2,1,0:T(4,128)} %broadcast_in_dim.155), calls=%async_computation | async-start | bytes 524288 | tf_op jit(solution)/shard_map/all_to_all | solution.py:216
  43.4 6.0 all-to-all-done
  63.8 3.2 collective-permute-start.11
  76.5 3.3 collective-permute-start.24
  83.2 12.7 %collective-permute-done.6 = bf16[2,4,16,2560]{3,2,1,0:T(8,128)(2,1)} collective-permute-done((bf16[2,4,16,2560]{3,2,1,0:T(8,128)(2,1)S(1)}, bf16[2,4,16,2560]{3,2,1,0:T(8,128)(2,1)}, u32[]{:S(2)}, u32[]{:S(2)}) %collective-permute-start.6) | collective-permute-done | bytes 655392 | tf_op jit(solution)/shard_map/ppermute | solution.py:194
  95.9 3.4 collective-permute-start.13
  99.3 5.1 collective-permute-done.18
  104.3 3.2 collective-permute-start.25
  108.7 3.3 pad_maximum_fusion.1
  112.8 6.5 %collective-permute-done.13 = bf16[2,4,16,2560]{3,2,1,0:T(8,128)(2,1)S(1)} collective-permute-done((bf16[2,4,16,2560]{3,2,1,0:T(8,128)(2,1)}, bf16[2,4,16,2560]{3,2,1,0:T(8,128)(2,1)S(1)}, u32[]{:S(2)}, u32[]{:S(2)}) %collective-permute-start.13) | collective-permute-done | bytes 655392 | tf_op jit(solution)/shard_map/ppermute | solution.py:194
  119.2 3.6 collective-permute-start.14
  122.8 10.4 %collective-permute-done.19 = bf16[4,2,16,2560]{3,2,1,0:T(8,128)(2,1)S(1)} collective-permute-done((bf16[4,2,16,2560]{3,2,1,0:T(8,128)(2,1)}, bf16[4,2,16,2560]{3,2,1,0:T(8,128)(2,1)S(1)}, u32[]{:S(2)}, u32[]{:S(2)}) %collective-permute-start.19) | collective-permute-done | bytes 655392 | tf_op jit(solution)/shard_map/ppermute | solution.py:208
  135.7 3.6 collective-permute-start.26
  139.4 5.1 collective-permute-done.8
  145.9 3.2 collective-permute-done.14
  150.4 9.9 %collective-permute-done.20 = bf16[4,2,16,2560]{3,2,1,0:T(8,128)(2,1)S(1)} collective-permute-done((bf16[4,2,16,2560]{3,2,1,0:T(8,128)(2,1)S(1)}, bf16[4,2,16,2560]{3,2,1,0:T(8,128)(2,1)S(1)}, u32[]{:S(2)}, u32[]{:S(2)}) %collective-permute-start.20) | collective-permute-done | bytes 655392 | tf_op jit(solution)/shard_map/ppermute | solution.py:208
  167.6 4.3 copy.148
  171.9 4.0 copy.150
  178.3 3.6 fusion.57
  188.2 3.0 fusion.26
  196.8 4.9 fusion.75
  201.7 3.1 fusion.30
  205.1 4.1 collective-permute-done.27
  209.4 18.4 %collective-permute-start.28 = (bf16[128,2048]{1,0:T(8,128)(2,1)S(1)}, bf16[128,2048]{1,0:T(8,128)(2,1)}, u32[]{:S(2)}, u32[]{:S(2)}) collective-permute-start(bf16[128,2048]{1,0:T(8,128)(2,1)S(1)} %fusion.93), channel_id=1, source_target_pairs={{0,2},{2,0},{1,3},{3,1},{4,6},{6,4},{5,7},{7,5},{8,10},{10,8},{9,1... | collective-permute-start | bytes 1572872 | tf_op jit(solution)/shard_map/ppermute | solution.py:119
  228.0 12.6 %collective-permute-done.28 = bf16[128,2048]{1,0:T(8,128)(2,1)} collective-permute-done((bf16[128,2048]{1,0:T(8,128)(2,1)S(1)}, bf16[128,2048]{1,0:T(8,128)(2,1)}, u32[]{:S(2)}, u32[]{:S(2)}) %collective-permute-start.28) | collective-permute-done | bytes 524320 | tf_op jit(solution)/shard_map/ppermute | solution.py:119
  245.0 6.8 %collective-permute-done.33 = bf16[128,2048]{1,0:T(8,128)(2,1)} collective-permute-done((bf16[128,2048]{1,0:T(8,128)(2,1)S(1)}, bf16[128,2048]{1,0:T(8,128)(2,1)}, u32[]{:S(2)}, u32[]{:S(2)}) %collective-permute-start.33) | collective-permute-done | bytes 524320 | tf_op jit(solution)/shard_map/ppermute | solution.py:108
  253.3 9.3 %collective-permute-done.29 = bf16[128,2048]{1,0:T(8,128)(2,1)S(1)} collective-permute-done((bf16[128,2048]{1,0:T(8,128)(2,1)S(1)}, bf16[128,2048]{1,0:T(8,128)(2,1)S(1)}, u32[]{:S(2)}, u32[]{:S(2)}) %collective-permute-start.29) | collective-permute-done | bytes 524320 | tf_op jit(solution)/shard_map/ppermute | solution.py:108
  266.9 8.4 %fusion = f32[512,1408]{1,0:T(8,128)} fusion(bf16[512,2048]{1,0:T(8,128)(2,1)} %bitcast.438, bf16[2048,4224]{1,0:T(8,128)(2,1)} %all-gather.2.cloned.1.call-done), kind=kOutput, calls=%fused_computation.2 | convolution fusion | flops 2952790016 | bytes 10747904 | tf_op jit(solution)/shard_map/dot_general | solution.py:27
  276.8 5.0 fusion.6
  281.8 6.6 %multiply_convert_fusion.1 = (bf16[512,1408]{1,0:T(8,128)(2,1)S(1)}, bf16[512,1408]{1,0:T(8,128)(2,1)S(1)}, bf16[512,1408]{1,0:T(8,128)(2,1)S(1)}) fusion(f32[512,1408]{1,0:T(8,128)} %fusion, f32[512,1408]{1,0:T(8,128)} %fusion.6, bf16[512,2048]{1,0:T(8,128)(2,1)S(1)} %bitcast.442, bf16[2048,4224]{1,0:T(8,128)(2,1)S(1)} %copy-done.45), kind=kOutput, calls=%fused_computation.18 | convolution fusion | flops 2963603456 | bytes 17956864 | tf_op jit(solution)/shard_map/dot_general | solution.py:27
  292.6 15.7 %shard_map.247 = bf16[2048,4224]{1,0:T(8,128)(2,1)} custom-call(bf16[512,2048]{1,0:T(8,128)(2,1)} %bitcast.440, bf16[512,2048]{1,0:T(8,128)(2,1)} %bitcast.439, bf16[512,4224]{1,0:T(8,128)(2,1)} %pad_maximum_fusion.right_ref), custom_call_target="tpu_custom_call" | custom-call | flops 8858370048 | bytes 25821184 | tf_op jit(solution)/shard_map/pallas_call | solution.py:64
  308.3 6.0 fusion.4
  314.4 5.5 fusion.12
  321.3 5.5 fusion.2
  333.3 13.5 %collective-permute-done.36 = bf16[128,2048]{1,0:T(8,128)(2,1)S(1)} collective-permute-done((bf16[128,2048]{1,0:T(8,128)(2,1)S(1)}, bf16[128,2048]{1,0:T(8,128)(2,1)S(1)}, u32[]{:S(2)}, u32[]{:S(2)}) %collective-permute-start.36) | collective-permute-done | bytes 524320 | tf_op jit(solution)/shard_map/ppermute | solution.py:119
  347.2 13.7 %collective-permute-done.32 = bf16[128,2048]{1,0:T(8,128)(2,1)S(1)} collective-permute-done((bf16[128,2048]{1,0:T(8,128)(2,1)S(1)}, bf16[128,2048]{1,0:T(8,128)(2,1)S(1)}, u32[]{:S(2)}, u32[]{:S(2)}) %collective-permute-start.32) | collective-permute-done | bytes 524320 | tf_op jit(solution)/shard_map/ppermute | solution.py:119
  364.5 16.2 %collective-permute-done.37 = bf16[128,2048]{1,0:T(8,128)(2,1)S(1)} collective-permute-done((bf16[128,2048]{1,0:T(8,128)(2,1)S(1)}, bf16[128,2048]{1,0:T(8,128)(2,1)S(1)}, u32[]{:S(2)}, u32[]{:S(2)}) %collective-permute-start.37) | collective-permute-done | bytes 524320 | tf_op jit(solution)/shard_map/ppermute | solution.py:108
  383.7 4.6 fusion.135
  391.2 3.2 fusion.60
  395.8 3.3 convolution_select_fusion
  410.4 10.8 %shard_map.246 = bf16[2048,2560]{1,0:T(8,128)(2,1)} custom-call(bf16[512,2048]{1,0:T(8,128)(2,1)} %bitcast.435, bf16[512,2048]{1,0:T(8,128)(2,1)} %bitcast.437, bf16[512,2560]{1,0:T(8,128)(2,1)} %constant_dynamic-update-slice_fusion.4.right_ref), custom_call_target="tpu_custom_call" | custom-call | flops 5368709120 | bytes 17301504 | tf_op jit(solution)/shard_map/pallas_call | solution.py:64
  421.2 9.2 %copy.203 = bf16[4,2,4,64,2560]{4,3,1,0,2:T(8,128)(2,1)} copy(bf16[4,2,4,64,2560]{4,3,2,1,0:T(8,128)(2,1)} %bitcast.420) | data formatting | bytes 20971520 | tf_op jit(solution)/shard_map/reshape | solution.py:157
  430.4 9.5 %fusion.146 = (bf16[4,4,2,64,1280]{4,3,2,1,0:T(8,128)(2,1)}, bf16[4,4,2,64,1280]{4,3,2,1,0:T(8,128)(2,1)}) fusion(bf16[4,4,2,64,2560]{4,3,2,1,0:T(8,128)(2,1)} %bitcast.419), kind=kLoop, calls=%fused_computation.275 | loop fusion | bytes 20971520 | tf_op jit(solution)/shard_map/slice | solution.py:140
  449.8 3.7 collective-permute-start.47
  456.4 3.0 add_add_fusion
  461.1 13.2 %collective-permute-done.41 = bf16[4,2,64,1280]{3,2,1,0:T(8,128)(2,1)S(1)} collective-permute-done((bf16[4,2,64,1280]{3,2,1,0:T(8,128)(2,1)S(1)}, bf16[4,2,64,1280]{3,2,1,0:T(8,128)(2,1)S(1)}, u32[]{:S(2)}, u32[]{:S(2)}) %collective-permute-start.41) | collective-permute-done | bytes 1310752 | tf_op jit(solution)/shard_map/ppermute | solution.py:148
  477.3 4.9 collective-permute-done.47
  482.2 3.1 fusion.16
  485.3 3.7 collective-permute-start.48
  490.3 18.8 %collective-permute-done.42 = bf16[4,2,64,1280]{3,2,1,0:T(8,128)(2,1)} collective-permute-done((bf16[4,2,64,1280]{3,2,1,0:T(8,128)(2,1)}, bf16[4,2,64,1280]{3,2,1,0:T(8,128)(2,1)}, u32[]{:S(2)}, u32[]{:S(2)}) %collective-permute-start.42) | collective-permute-done | bytes 1310752 | tf_op jit(solution)/shard_map/ppermute | solution.py:148
  509.1 3.1 fusion.20
  516.9 3.1 fusion.17
  520.0 3.7 collective-permute-start.49
  523.7 3.6 collective-permute-done.40
  530.8 5.5 all-to-all-start.1
  536.3 19.4 %collective-permute-done.43 = bf16[4,2,64,1280]{3,2,1,0:T(8,128)(2,1)} collective-permute-done((bf16[4,2,64,1280]{3,2,1,0:T(8,128)(2,1)}, bf16[4,2,64,1280]{3,2,1,0:T(8,128)(2,1)}, u32[]{:S(2)}, u32[]{:S(2)}) %collective-permute-start.43) | collective-permute-done | bytes 1310752 | tf_op jit(solution)/shard_map/ppermute | solution.py:148
  557.9 6.4 %collective-permute-done.49 = bf16[4,2,64,1280]{3,2,1,0:T(8,128)(2,1)} collective-permute-done((bf16[4,2,64,1280]{3,2,1,0:T(8,128)(2,1)}, bf16[4,2,64,1280]{3,2,1,0:T(8,128)(2,1)}, u32[]{:S(2)}, u32[]{:S(2)}) %collective-permute-start.49) | collective-permute-done | bytes 1310752 | tf_op jit(solution)/shard_map/ppermute | solution.py:148
  566.5 6.0 collective-permute-done.44
  588.0 3.3 collective-permute-done.46
  591.3 4.1 collective-permute-done.52
  595.5 4.5 collective-permute-start.53
  602.0 3.1 collective-permute-done.53
  (316 shorter events, 174.7 us)
Async XLA Ops:
  7.2 259.6 %all-gather.2.cloned.1.call-start = ((), (), s32[]{:S(2)}) async-start(), calls=%async_computation.3 | async-start | bytes 17842176 | tf_op jit(solution)/shard_map/all_gather | solution.py:261
  11.6 11.0 %collective-permute-start = (bf16[64,2560]{1,0:T(8,128)(2,1)S(1)}, bf16[64,2560]{1,0:T(8,128)(2,1)S(1)}, u32[]{:S(2)}, u32[]{:S(2)}) collective-permute-start(bf16[64,2560]{1,0:T(8,128)(2,1)S(1)} %bitcast_dynamic-update-slice_fusion.37), channel_id=1, source_target_pairs={{0,16},{4,20},{8,24},{12,28},{16,0},{20,4},{24,8},{28,12},{32,48},... | collective-permute-start | bytes 983048 | tf_op jit(solution)/shard_map/ppermute | solution.py:171
  19.2 31.9 %copy-start.38 = (f32[128]{0:T(128)}, f32[128]{0:T(128)S(1)}, u32[]{:S(2)}) copy-start(f32[128]{0:T(128)S(1)} %get-tuple-element.63) | copy-start | bytes 1540
  23.4 29.0 %collective-permute-start.3 = (bf16[2,16,2560]{2,1,0:T(8,128)(2,1)}, bf16[2,16,2560]{2,1,0:T(8,128)(2,1)}, u32[]{:S(2)}, u32[]{:S(2)}) collective-permute-start(bf16[2,16,2560]{2,1,0:T(8,128)(2,1)} %get-tuple-element.56), channel_id=1, source_target_pairs={{0,4},{4,8},{8,12},{12,0},{16,20},{20,24},{24,28},{28,16},{32,36},... | collective-permute-start | bytes 491528 | tf_op jit(solution)/shard_map/ppermute | solution.py:188
  24.9 28.1 %collective-permute-start.9 = (bf16[2,16,2560]{2,1,0:T(8,128)(2,1)}, bf16[2,16,2560]{2,1,0:T(8,128)(2,1)}, u32[]{:S(2)}, u32[]{:S(2)}) collective-permute-start(bf16[2,16,2560]{2,1,0:T(8,128)(2,1)} %get-tuple-element.55), channel_id=1, source_target_pairs={{0,12},{4,0},{8,4},{12,8},{16,28},{20,16},{24,20},{28,24},{32,44},... | collective-permute-start | bytes 491528 | tf_op jit(solution)/shard_map/ppermute | solution.py:188
  26.6 29.0 %collective-permute-start.15 = (bf16[2,16,2560]{2,1,0:T(8,128)(2,1)}, bf16[2,16,2560]{2,1,0:T(8,128)(2,1)}, u32[]{:S(2)}, u32[]{:S(2)}) collective-permute-start(bf16[2,16,2560]{2,1,0:T(8,128)(2,1)} %get-tuple-element.54), channel_id=1, source_target_pairs={{0,32},{4,36},{8,40},{12,44},{16,48},{20,52},{24,56},{28,60},{32,6... | collective-permute-start | bytes 491528 | tf_op jit(solution)/shard_map/ppermute | solution.py:202
  29.3 20.2 %all-to-all-start = ((f32[128,3,16]{2,1,0:T(4,128)}), f32[128,3,16]{2,1,0:T(4,128)S(1)}, u32[]{:S(2)}, u32[]{:S(2)}) async-start(f32[128,3,16]{2,1,0:T(4,128)} %broadcast_in_dim.155), calls=%async_computation | async-start | bytes 524288 | tf_op jit(solution)/shard_map/all_to_all | solution.py:216
  38.7 567.3 %reduce-scatter.2.cloned.1.call-start = ((), (), s32[]{:S(2)}) async-start(), calls=%async_computation.4 | async-start | bytes 17842176 | tf_op jit(solution)/shard_map/reduce_scatter | solution.py:307
  40.6 19.2 %copy-start.20 = (bf16[2,4,16,2560]{3,2,1,0:T(8,128)(2,1)S(1)}, bf16[2,4,16,2560]{3,2,1,0:T(8,128)(2,1)}, u32[]{:S(2)}) copy-start(bf16[2,4,16,2560]{3,2,1,0:T(8,128)(2,1)} %copy-done.19) | copy-start | bytes 1966084
  40.6 15.8 %collective-permute-start.21 = (bf16[2,16,2560]{2,1,0:T(8,128)(2,1)S(1)}, bf16[2,16,2560]{2,1,0:T(8,128)(2,1)}, u32[]{:S(2)}, u32[]{:S(2)}) collective-permute-start(bf16[2,16,2560]{2,1,0:T(8,128)(2,1)S(1)} %get-tuple-element.53), channel_id=1, source_target_pairs={{0,96},{4,100},{8,104},{12,108},{16,112},{20,116},{24,120},{28,124... | collective-permute-start | bytes 491528 | tf_op jit(solution)/shard_map/ppermute | solution.py:202
  50.1 23.7 %copy-start.36 = (f32[2048]{0:T(1024)}, f32[2048]{0:T(1024)S(1)}, u32[]{:S(2)}) copy-start(f32[2048]{0:T(1024)S(1)} %mul.250) | copy-start | bytes 24580
  51.3 28.5 %collective-permute-start.1 = (bf16[128,2048]{1,0:T(8,128)(2,1)}, bf16[128,2048]{1,0:T(8,128)(2,1)}, u32[]{:S(2)}, u32[]{:S(2)}) collective-permute-start(bf16[128,2048]{1,0:T(8,128)(2,1)} %fusion.63), channel_id=1, source_target_pairs={{0,2},{2,0},{1,3},{3,1},{4,6},{6,4},{5,7},{7,5},{8,10},{10,8},{9,1... | collective-permute-start | bytes 1572872 | tf_op jit(solution)/shard_map/ppermute | solution.py:108
  52.3 11.4 %collective-permute-start.4 = (bf16[2,16,2560]{2,1,0:T(8,128)(2,1)}, bf16[2,16,2560]{2,1,0:T(8,128)(2,1)S(1)}, u32[]{:S(2)}, u32[]{:S(2)}) collective-permute-start(bf16[2,16,2560]{2,1,0:T(8,128)(2,1)} %collective-permute-done.3), channel_id=1, source_target_pairs={{0,4},{4,8},{8,12},{12,0},{16,20},{20,24},{24,28},{28,16},{32,36},... | collective-permute-start | bytes 491528 | tf_op jit(solution)/shard_map/ppermute | solution.py:188
  53.0 10.8 %collective-permute-start.10 = (bf16[2,16,2560]{2,1,0:T(8,128)(2,1)}, bf16[2,16,2560]{2,1,0:T(8,128)(2,1)S(1)}, u32[]{:S(2)}, u32[]{:S(2)}) collective-permute-start(bf16[2,16,2560]{2,1,0:T(8,128)(2,1)} %collective-permute-done.9), channel_id=1, source_target_pairs={{0,12},{4,0},{8,4},{12,8},{16,28},{20,16},{24,20},{28,24},{32,44},... | collective-permute-start | bytes 491528 | tf_op jit(solution)/shard_map/ppermute | solution.py:188
  55.6 11.4 %collective-permute-start.16 = (bf16[2,16,2560]{2,1,0:T(8,128)(2,1)}, bf16[2,16,2560]{2,1,0:T(8,128)(2,1)S(1)}, u32[]{:S(2)}, u32[]{:S(2)}) collective-permute-start(bf16[2,16,2560]{2,1,0:T(8,128)(2,1)} %collective-permute-done.15), channel_id=1, source_target_pairs={{0,32},{4,36},{8,40},{12,44},{16,48},{20,52},{24,56},{28,60},{32,6... | collective-permute-start | bytes 491528 | tf_op jit(solution)/shard_map/ppermute | solution.py:202
  56.4 11.5 %collective-permute-start.22 = (bf16[2,16,2560]{2,1,0:T(8,128)(2,1)}, bf16[2,16,2560]{2,1,0:T(8,128)(2,1)S(1)}, u32[]{:S(2)}, u32[]{:S(2)}) collective-permute-start(bf16[2,16,2560]{2,1,0:T(8,128)(2,1)} %collective-permute-done.21), channel_id=1, source_target_pairs={{0,96},{4,100},{8,104},{12,108},{16,112},{20,116},{24,120},{28,124... | collective-permute-start | bytes 491528 | tf_op jit(solution)/shard_map/ppermute | solution.py:202
  63.7 8.6 %collective-permute-start.5 = (bf16[2,16,2560]{2,1,0:T(8,128)(2,1)S(1)}, bf16[2,16,2560]{2,1,0:T(8,128)(2,1)S(1)}, u32[]{:S(2)}, u32[]{:S(2)}) collective-permute-start(bf16[2,16,2560]{2,1,0:T(8,128)(2,1)S(1)} %collective-permute-done.4), channel_id=1, source_target_pairs={{0,4},{4,8},{8,12},{12,0},{16,20},{20,24},{24,28},{28,16},{32,36},... | collective-permute-start | bytes 491528 | tf_op jit(solution)/shard_map/ppermute | solution.py:188
  63.8 10.0 %collective-permute-start.11 = (bf16[2,16,2560]{2,1,0:T(8,128)(2,1)S(1)}, bf16[2,16,2560]{2,1,0:T(8,128)(2,1)S(1)}, u32[]{:S(2)}, u32[]{:S(2)}) collective-permute-start(bf16[2,16,2560]{2,1,0:T(8,128)(2,1)S(1)} %collective-permute-done.10), channel_id=1, source_target_pairs={{0,12},{4,0},{8,4},{12,8},{16,28},{20,16},{24,20},{28,24},{32,44},... | collective-permute-start | bytes 491528 | tf_op jit(solution)/shard_map/ppermute | solution.py:188
  67.0 8.8 %collective-permute-start.17 = (bf16[2,16,2560]{2,1,0:T(8,128)(2,1)S(1)}, bf16[2,16,2560]{2,1,0:T(8,128)(2,1)S(1)}, u32[]{:S(2)}, u32[]{:S(2)}) collective-permute-start(bf16[2,16,2560]{2,1,0:T(8,128)(2,1)S(1)} %collective-permute-done.16), channel_id=1, source_target_pairs={{0,32},{4,36},{8,40},{12,44},{16,48},{20,52},{24,56},{28,60},{32,6... | collective-permute-start | bytes 491528 | tf_op jit(solution)/shard_map/ppermute | solution.py:202
  67.9 8.6 %collective-permute-start.23 = (bf16[2,16,2560]{2,1,0:T(8,128)(2,1)S(1)}, bf16[2,16,2560]{2,1,0:T(8,128)(2,1)S(1)}, u32[]{:S(2)}, u32[]{:S(2)}) collective-permute-start(bf16[2,16,2560]{2,1,0:T(8,128)(2,1)S(1)} %collective-permute-done.22), channel_id=1, source_target_pairs={{0,96},{4,100},{8,104},{12,108},{16,112},{20,116},{24,120},{28,124... | collective-permute-start | bytes 491528 | tf_op jit(solution)/shard_map/ppermute | solution.py:202
  72.4 23.5 %collective-permute-start.6 = (bf16[2,4,16,2560]{3,2,1,0:T(8,128)(2,1)S(1)}, bf16[2,4,16,2560]{3,2,1,0:T(8,128)(2,1)}, u32[]{:S(2)}, u32[]{:S(2)}) collective-permute-start(bf16[2,4,16,2560]{3,2,1,0:T(8,128)(2,1)S(1)} %bitcast_dynamic-update-slice_fusion.25), channel_id=1, source_target_pairs={{0,32},{4,36},{8,40},{12,44},{16,48},{20,52},{24,56},{28,60},{32,6... | collective-permute-start | bytes 1966088 | tf_op jit(solution)/shard_map/ppermute | solution.py:194
  73.8 22.0 %collective-permute-start.12 = (bf16[2,4,16,2560]{3,2,1,0:T(8,128)(2,1)S(1)}, bf16[2,4,16,2560]{3,2,1,0:T(8,128)(2,1)}, u32[]{:S(2)}, u32[]{:S(2)}) collective-permute-start(bf16[2,4,16,2560]{3,2,1,0:T(8,128)(2,1)S(1)} %bitcast_dynamic-update-slice_fusion.21), channel_id=1, source_target_pairs={{0,96},{4,100},{8,104},{12,108},{16,112},{20,116},{24,120},{28,124... | collective-permute-start | bytes 1966088 | tf_op jit(solution)/shard_map/ppermute | solution.py:194
  76.5 27.9 %collective-permute-start.18 = (bf16[4,2,16,2560]{3,2,1,0:T(8,128)(2,1)}, bf16[4,2,16,2560]{3,2,1,0:T(8,128)(2,1)}, u32[]{:S(2)}, u32[]{:S(2)}) collective-permute-start(bf16[4,2,16,2560]{3,2,1,0:T(8,128)(2,1)} %bitcast_dynamic-update-slice_fusion.33), channel_id=1, source_target_pairs={{0,4},{4,8},{8,12},{12,0},{16,20},{20,24},{24,28},{28,16},{32,36},... | collective-permute-start | bytes 1966088 | tf_op jit(solution)/shard_map/ppermute | solution.py:208
  76.5 27.8 %collective-permute-start.24 = (bf16[4,2,16,2560]{3,2,1,0:T(8,128)(2,1)S(1)}, bf16[4,2,16,2560]{3,2,1,0:T(8,128)(2,1)}, u32[]{:S(2)}, u32[]{:S(2)}) collective-permute-start(bf16[4,2,16,2560]{3,2,1,0:T(8,128)(2,1)S(1)} %bitcast_dynamic-update-slice_fusion.29), channel_id=1, source_target_pairs={{0,12},{4,0},{8,4},{12,8},{16,28},{20,16},{24,20},{28,24},{32,44},... | collective-permute-start | bytes 1966088 | tf_op jit(solution)/shard_map/ppermute | solution.py:208
  81.9 26.8 %collective-permute-start.2 = (bf16[2,128,2048]{2,1,0:T(8,128)(2,1)}, bf16[2,128,2048]{2,1,0:T(8,128)(2,1)}, u32[]{:S(2)}, u32[]{:S(2)}) collective-permute-start(bf16[2,128,2048]{2,1,0:T(8,128)(2,1)} %pad_maximum_fusion.5), channel_id=1, source_target_pairs={{0,1},{1,0},{2,3},{3,2},{4,5},{5,4},{6,7},{7,6},{8,9},{9,8},{10,11... | collective-permute-start | bytes 3145736 | tf_op jit(solution)/shard_map/ppermute | solution.py:110
  95.9 16.9 %collective-permute-start.7 = (bf16[2,4,16,2560]{3,2,1,0:T(8,128)(2,1)}, bf16[2,4,16,2560]{3,2,1,0:T(8,128)(2,1)S(1)}, u32[]{:S(2)}, u32[]{:S(2)}) collective-permute-start(bf16[2,4,16,2560]{3,2,1,0:T(8,128)(2,1)} %collective-permute-done.6), channel_id=1, source_target_pairs={{0,32},{4,36},{8,40},{12,44},{16,48},{20,52},{24,56},{28,60},{32,6... | collective-permute-start | bytes 1966088 | tf_op jit(solution)/shard_map/ppermute | solution.py:194
  95.9 23.4 %collective-permute-start.13 = (bf16[2,4,16,2560]{3,2,1,0:T(8,128)(2,1)}, bf16[2,4,16,2560]{3,2,1,0:T(8,128)(2,1)S(1)}, u32[]{:S(2)}, u32[]{:S(2)}) collective-permute-start(bf16[2,4,16,2560]{3,2,1,0:T(8,128)(2,1)} %collective-permute-done.12), channel_id=1, source_target_pairs={{0,96},{4,100},{8,104},{12,108},{16,112},{20,116},{24,120},{28,124... | collective-permute-start | bytes 1966088 | tf_op jit(solution)/shard_map/ppermute | solution.py:194
  104.3 28.9 %collective-permute-start.19 = (bf16[4,2,16,2560]{3,2,1,0:T(8,128)(2,1)}, bf16[4,2,16,2560]{3,2,1,0:T(8,128)(2,1)S(1)}, u32[]{:S(2)}, u32[]{:S(2)}) collective-permute-start(bf16[4,2,16,2560]{3,2,1,0:T(8,128)(2,1)} %collective-permute-done.18), channel_id=1, source_target_pairs={{0,4},{4,8},{8,12},{12,0},{16,20},{20,24},{24,28},{28,16},{32,36},... | collective-permute-start | bytes 1966088 | tf_op jit(solution)/shard_map/ppermute | solution.py:208
  104.3 31.4 %collective-permute-start.25 = (bf16[4,2,16,2560]{3,2,1,0:T(8,128)(2,1)}, bf16[4,2,16,2560]{3,2,1,0:T(8,128)(2,1)S(1)}, u32[]{:S(2)}, u32[]{:S(2)}) collective-permute-start(bf16[4,2,16,2560]{3,2,1,0:T(8,128)(2,1)} %collective-permute-done.24), channel_id=1, source_target_pairs={{0,12},{4,0},{8,4},{12,8},{16,28},{20,16},{24,20},{28,24},{32,44},... | collective-permute-start | bytes 1966088 | tf_op jit(solution)/shard_map/ppermute | solution.py:208
  112.8 31.7 %collective-permute-start.8 = (bf16[2,4,16,2560]{3,2,1,0:T(8,128)(2,1)S(1)}, bf16[2,4,16,2560]{3,2,1,0:T(8,128)(2,1)S(1)}, u32[]{:S(2)}, u32[]{:S(2)}) collective-permute-start(bf16[2,4,16,2560]{3,2,1,0:T(8,128)(2,1)S(1)} %collective-permute-done.7), channel_id=1, source_target_pairs={{0,32},{4,36},{8,40},{12,44},{16,48},{20,52},{24,56},{28,60},{32,6... | collective-permute-start | bytes 1966088 | tf_op jit(solution)/shard_map/ppermute | solution.py:194
  119.2 29.9 %collective-permute-start.14 = (bf16[2,4,16,2560]{3,2,1,0:T(8,128)(2,1)S(1)}, bf16[2,4,16,2560]{3,2,1,0:T(8,128)(2,1)S(1)}, u32[]{:S(2)}, u32[]{:S(2)}) collective-permute-start(bf16[2,4,16,2560]{3,2,1,0:T(8,128)(2,1)S(1)} %collective-permute-done.13), channel_id=1, source_target_pairs={{0,96},{4,100},{8,104},{12,108},{16,112},{20,116},{24,120},{28,124... | collective-permute-start | bytes 1966088 | tf_op jit(solution)/shard_map/ppermute | solution.py:194
  133.2 27.1 %collective-permute-start.20 = (bf16[4,2,16,2560]{3,2,1,0:T(8,128)(2,1)S(1)}, bf16[4,2,16,2560]{3,2,1,0:T(8,128)(2,1)S(1)}, u32[]{:S(2)}, u32[]{:S(2)}) collective-permute-start(bf16[4,2,16,2560]{3,2,1,0:T(8,128)(2,1)S(1)} %collective-permute-done.19), channel_id=1, source_target_pairs={{0,4},{4,8},{8,12},{12,0},{16,20},{20,24},{24,28},{28,16},{32,36},... | collective-permute-start | bytes 1966088 | tf_op jit(solution)/shard_map/ppermute | solution.py:208
  135.7 26.2 %collective-permute-start.26 = (bf16[4,2,16,2560]{3,2,1,0:T(8,128)(2,1)S(1)}, bf16[4,2,16,2560]{3,2,1,0:T(8,128)(2,1)S(1)}, u32[]{:S(2)}, u32[]{:S(2)}) collective-permute-start(bf16[4,2,16,2560]{3,2,1,0:T(8,128)(2,1)S(1)} %collective-permute-done.25), channel_id=1, source_target_pairs={{0,12},{4,0},{8,4},{12,8},{16,28},{20,16},{24,20},{28,24},{32,44},... | collective-permute-start | bytes 1966088 | tf_op jit(solution)/shard_map/ppermute | solution.py:208
  204.7 23.1 %copy-start.9 = (bf16[1,1,128,2048]{3,2,1,0:T(8,128)(2,1)S(1)}, bf16[1,1,128,2048]{3,2,1,0:T(8,128)(2,1)}, u32[]{:S(2)}) copy-start(bf16[1,1,128,2048]{3,2,1,0:T(8,128)(2,1)} %param.28) | copy-start | bytes 1572868
  205.0 4.2 collective-permute-start.27
  209.4 31.2 %collective-permute-start.28 = (bf16[128,2048]{1,0:T(8,128)(2,1)S(1)}, bf16[128,2048]{1,0:T(8,128)(2,1)}, u32[]{:S(2)}, u32[]{:S(2)}) collective-permute-start(bf16[128,2048]{1,0:T(8,128)(2,1)S(1)} %fusion.93), channel_id=1, source_target_pairs={{0,2},{2,0},{1,3},{3,1},{4,6},{6,4},{5,7},{7,5},{8,10},{10,8},{9,1... | collective-permute-start | bytes 1572872 | tf_op jit(solution)/shard_map/ppermute | solution.py:119
  227.8 24.0 %collective-permute-start.33 = (bf16[128,2048]{1,0:T(8,128)(2,1)S(1)}, bf16[128,2048]{1,0:T(8,128)(2,1)}, u32[]{:S(2)}, u32[]{:S(2)}) collective-permute-start(bf16[128,2048]{1,0:T(8,128)(2,1)S(1)} %bitcast.427), channel_id=1, source_target_pairs={{0,2},{2,0},{1,3},{3,1},{4,6},{6,4},{5,7},{7,5},{8,10},{10,8},{9,1... | collective-permute-start | bytes 1572872 | tf_op jit(solution)/shard_map/ppermute | solution.py:108
  242.9 19.6 %collective-permute-start.29 = (bf16[128,2048]{1,0:T(8,128)(2,1)S(1)}, bf16[128,2048]{1,0:T(8,128)(2,1)S(1)}, u32[]{:S(2)}, u32[]{:S(2)}) collective-permute-start(bf16[128,2048]{1,0:T(8,128)(2,1)S(1)} %multiply_convert_fusion.4), channel_id=1, source_target_pairs={{0,2},{2,0},{1,3},{3,1},{4,6},{6,4},{5,7},{7,5},{8,10},{10,8},{9,1... | collective-permute-start | bytes 1572872 | tf_op jit(solution)/shard_map/ppermute | solution.py:108
  253.0 9.7 %collective-permute-start.34 = (bf16[2,128,2048]{2,1,0:T(8,128)(2,1)S(1)}, bf16[2,128,2048]{2,1,0:T(8,128)(2,1)S(1)}, u32[]{:S(2)}, u32[]{:S(2)}) collective-permute-start(bf16[2,128,2048]{2,1,0:T(8,128)(2,1)S(1)} %pad_maximum_fusion.7), channel_id=1, source_target_pairs={{0,1},{1,0},{2,3},{3,2},{4,5},{5,4},{6,7},{7,6},{8,9},{9,8},{10,11... | collective-permute-start | bytes 3145736 | tf_op jit(solution)/shard_map/ppermute | solution.py:110
  262.6 2.7 collective-permute-start.30
  320.1 7.4 %collective-permute-start.35 = (f32[2,128,2048]{2,1,0:T(8,128)S(1)}, f32[2,128,2048]{2,1,0:T(8,128)S(1)}, u32[]{:S(2)}, u32[]{:S(2)}) collective-permute-start(f32[2,128,2048]{2,1,0:T(8,128)S(1)} %bitcast.445), channel_id=1, source_target_pairs={{0,1},{1,0},{2,3},{3,2},{4,5},{5,4},{6,7},{7,6},{8,9},{9,8},{10,11... | collective-permute-start | bytes 6291464 | tf_op jit(solution)/shard_map/ppermute | solution.py:116
  327.0 4.3 collective-permute-start.31
  327.7 19.1 %collective-permute-start.36 = (bf16[128,2048]{1,0:T(8,128)(2,1)S(1)}, bf16[128,2048]{1,0:T(8,128)(2,1)S(1)}, u32[]{:S(2)}, u32[]{:S(2)}) collective-permute-start(bf16[128,2048]{1,0:T(8,128)(2,1)S(1)} %fusion.83), channel_id=1, source_target_pairs={{0,2},{2,0},{1,3},{3,1},{4,6},{6,4},{5,7},{7,5},{8,10},{10,8},{9,1... | collective-permute-start | bytes 1572872 | tf_op jit(solution)/shard_map/ppermute | solution.py:119
  331.5 29.5 %collective-permute-start.32 = (bf16[128,2048]{1,0:T(8,128)(2,1)S(1)}, bf16[128,2048]{1,0:T(8,128)(2,1)S(1)}, u32[]{:S(2)}, u32[]{:S(2)}) collective-permute-start(bf16[128,2048]{1,0:T(8,128)(2,1)S(1)} %fusion.87), channel_id=1, source_target_pairs={{0,2},{2,0},{1,3},{3,1},{4,6},{6,4},{5,7},{7,5},{8,10},{10,8},{9,1... | collective-permute-start | bytes 1572872 | tf_op jit(solution)/shard_map/ppermute | solution.py:119
  362.7 17.9 %collective-permute-start.37 = (bf16[128,2048]{1,0:T(8,128)(2,1)S(1)}, bf16[128,2048]{1,0:T(8,128)(2,1)S(1)}, u32[]{:S(2)}, u32[]{:S(2)}) collective-permute-start(bf16[128,2048]{1,0:T(8,128)(2,1)S(1)} %get-tuple-element.29), channel_id=1, source_target_pairs={{0,2},{2,0},{1,3},{3,1},{4,6},{6,4},{5,7},{7,5},{8,10},{10,8},{9,1... | collective-permute-start | bytes 1572872 | tf_op jit(solution)/shard_map/ppermute | solution.py:108
  380.7 2.7 collective-permute-start.38
  441.3 33.0 %collective-permute-start.41 = (bf16[4,2,64,1280]{3,2,1,0:T(8,128)(2,1)S(1)}, bf16[4,2,64,1280]{3,2,1,0:T(8,128)(2,1)S(1)}, u32[]{:S(2)}, u32[]{:S(2)}) collective-permute-start(bf16[4,2,64,1280]{3,2,1,0:T(8,128)(2,1)S(1)} %dynamic-slice_bitcast_fusion.1), channel_id=1, source_target_pairs={{0,4},{4,8},{8,12},{12,0},{16,20},{20,24},{24,28},{28,16},{32,36},... | collective-permute-start | bytes 3932168 | tf_op jit(solution)/shard_map/ppermute | solution.py:148
  449.8 32.5 %collective-permute-start.47 = (bf16[4,2,64,1280]{3,2,1,0:T(8,128)(2,1)}, bf16[4,2,64,1280]{3,2,1,0:T(8,128)(2,1)}, u32[]{:S(2)}, u32[]{:S(2)}) collective-permute-start(bf16[4,2,64,1280]{3,2,1,0:T(8,128)(2,1)} %dynamic-slice_bitcast_fusion), channel_id=1, source_target_pairs={{0,12},{4,0},{8,4},{12,8},{16,28},{20,16},{24,20},{28,24},{32,44},... | collective-permute-start | bytes 3932168 | tf_op jit(solution)/shard_map/ppermute | solution.py:148
  461.1 51.1 %collective-permute-start.39 = (f32[2,128,2048]{2,1,0:T(8,128)}, f32[2,128,2048]{2,1,0:T(8,128)S(1)}, u32[]{:S(2)}, u32[]{:S(2)}) collective-permute-start(f32[2,128,2048]{2,1,0:T(8,128)} %bitcast.105), channel_id=1, source_target_pairs={{0,1},{1,0},{2,3},{3,2},{4,5},{5,4},{6,7},{7,6},{8,9},{9,8},{10,11... | collective-permute-start | bytes 6291464 | tf_op jit(solution)/shard_map/ppermute | solution.py:116
  477.0 32.1 %collective-permute-start.42 = (bf16[4,2,64,1280]{3,2,1,0:T(8,128)(2,1)}, bf16[4,2,64,1280]{3,2,1,0:T(8,128)(2,1)}, u32[]{:S(2)}, u32[]{:S(2)}) collective-permute-start(bf16[4,2,64,1280]{3,2,1,0:T(8,128)(2,1)} %fusion.19), channel_id=1, source_target_pairs={{0,4},{4,8},{8,12},{12,0},{16,20},{20,24},{24,28},{28,16},{32,36},... | collective-permute-start | bytes 3932168 | tf_op jit(solution)/shard_map/ppermute | solution.py:148
  485.3 31.6 %collective-permute-start.48 = (bf16[4,2,64,1280]{3,2,1,0:T(8,128)(2,1)}, bf16[4,2,64,1280]{3,2,1,0:T(8,128)(2,1)}, u32[]{:S(2)}, u32[]{:S(2)}) collective-permute-start(bf16[4,2,64,1280]{3,2,1,0:T(8,128)(2,1)} %fusion.16), channel_id=1, source_target_pairs={{0,12},{4,0},{8,4},{12,8},{16,28},{20,16},{24,20},{28,24},{32,44},... | collective-permute-start | bytes 3932168 | tf_op jit(solution)/shard_map/ppermute | solution.py:148
  512.2 43.5 %collective-permute-start.43 = (bf16[4,2,64,1280]{3,2,1,0:T(8,128)(2,1)}, bf16[4,2,64,1280]{3,2,1,0:T(8,128)(2,1)}, u32[]{:S(2)}, u32[]{:S(2)}) collective-permute-start(bf16[4,2,64,1280]{3,2,1,0:T(8,128)(2,1)} %fusion.20), channel_id=1, source_target_pairs={{0,4},{4,8},{8,12},{12,0},{16,20},{20,24},{24,28},{28,16},{32,36},... | collective-permute-start | bytes 3932168 | tf_op jit(solution)/shard_map/ppermute | solution.py:148
  513.6 13.6 %collective-permute-start.40 = (bf16[128,2048]{1,0:T(8,128)(2,1)S(1)}, bf16[128,2048]{1,0:T(8,128)(2,1)S(1)}, u32[]{:S(2)}, u32[]{:S(2)}) collective-permute-start(bf16[128,2048]{1,0:T(8,128)(2,1)S(1)} %fusion.79), channel_id=1, source_target_pairs={{0,2},{2,0},{1,3},{3,1},{4,6},{6,4},{5,7},{7,5},{8,10},{10,8},{9,1... | collective-permute-start | bytes 1572872 | tf_op jit(solution)/shard_map/ppermute | solution.py:119
  520.0 44.4 %collective-permute-start.49 = (bf16[4,2,64,1280]{3,2,1,0:T(8,128)(2,1)}, bf16[4,2,64,1280]{3,2,1,0:T(8,128)(2,1)}, u32[]{:S(2)}, u32[]{:S(2)}) collective-permute-start(bf16[4,2,64,1280]{3,2,1,0:T(8,128)(2,1)} %fusion.17), channel_id=1, source_target_pairs={{0,12},{4,0},{8,4},{12,8},{16,28},{20,16},{24,20},{28,24},{32,44},... | collective-permute-start | bytes 3932168 | tf_op jit(solution)/shard_map/ppermute | solution.py:148
  530.8 70.6 %all-to-all-start.1 = ((f32[128,3,16]{2,1,0:T(4,128)}), f32[128,3,16]{2,1,0:T(4,128)S(1)}, u32[]{:S(2)}, u32[]{:S(2)}) async-start(f32[128,3,16]{2,1,0:T(4,128)} %copy.166), calls=%async_computation.1 | async-start | bytes 524288 | tf_op jit(solution)/shard_map/all_to_all | solution.py:223
  557.8 14.6 %collective-permute-start.44 = (bf16[2,64,1280]{2,1,0:T(8,128)(2,1)S(1)}, bf16[2,64,1280]{2,1,0:T(8,128)(2,1)S(1)}, u32[]{:S(2)}, u32[]{:S(2)}) collective-permute-start(bf16[2,64,1280]{2,1,0:T(8,128)(2,1)S(1)} %dynamic-slice_bitcast_fusion.3), channel_id=1, source_target_pairs={{0,32},{4,36},{8,40},{12,44},{16,48},{20,52},{24,56},{28,60},{32,6... | collective-permute-start | bytes 983048 | tf_op jit(solution)/shard_map/ppermute | solution.py:148
  566.4 10.9 %collective-permute-start.50 = (bf16[2,64,1280]{2,1,0:T(8,128)(2,1)S(1)}, bf16[2,64,1280]{2,1,0:T(8,128)(2,1)S(1)}, u32[]{:S(2)}, u32[]{:S(2)}) collective-permute-start(bf16[2,64,1280]{2,1,0:T(8,128)(2,1)S(1)} %dynamic-slice_bitcast_fusion.2), channel_id=1, source_target_pairs={{0,96},{4,100},{8,104},{12,108},{16,112},{20,116},{24,120},{28,124... | collective-permute-start | bytes 983048 | tf_op jit(solution)/shard_map/ppermute | solution.py:148
  572.5 8.4 %collective-permute-start.45 = (bf16[2,64,1280]{2,1,0:T(8,128)(2,1)S(1)}, bf16[2,64,1280]{2,1,0:T(8,128)(2,1)S(1)}, u32[]{:S(2)}, u32[]{:S(2)}) collective-permute-start(bf16[2,64,1280]{2,1,0:T(8,128)(2,1)S(1)} %fusion.116), channel_id=1, source_target_pairs={{0,32},{4,36},{8,40},{12,44},{16,48},{20,52},{24,56},{28,60},{32,6... | collective-permute-start | bytes 983048 | tf_op jit(solution)/shard_map/ppermute | solution.py:148
  577.3 7.8 %collective-permute-start.51 = (bf16[2,64,1280]{2,1,0:T(8,128)(2,1)S(1)}, bf16[2,64,1280]{2,1,0:T(8,128)(2,1)S(1)}, u32[]{:S(2)}, u32[]{:S(2)}) collective-permute-start(bf16[2,64,1280]{2,1,0:T(8,128)(2,1)S(1)} %fusion.114), channel_id=1, source_target_pairs={{0,96},{4,100},{8,104},{12,108},{16,112},{20,116},{24,120},{28,124... | collective-permute-start | bytes 983048 | tf_op jit(solution)/shard_map/ppermute | solution.py:148
  580.9 19.1 %copy-start.10 = (f32[128,2048]{1,0:T(8,128)S(1)}, f32[128,2048]{1,0:T(8,128)}, u32[]{:S(2)}) copy-start(f32[128,2048]{1,0:T(8,128)} %get-tuple-element.30) | copy-start | bytes 3145732
  581.0 19.1 %copy-start.12 = (f32[128,2048]{1,0:T(8,128)S(1)}, f32[128,2048]{1,0:T(8,128)}, u32[]{:S(2)}) copy-start(f32[128,2048]{1,0:T(8,128)} %get-tuple-element.28) | copy-start | bytes 3145732
  581.0 10.3 %collective-permute-start.46 = (bf16[2,64,1280]{2,1,0:T(8,128)(2,1)S(1)}, bf16[2,64,1280]{2,1,0:T(8,128)(2,1)S(1)}, u32[]{:S(2)}, u32[]{:S(2)}) collective-permute-start(bf16[2,64,1280]{2,1,0:T(8,128)(2,1)S(1)} %fusion.117), channel_id=1, source_target_pairs={{0,32},{4,36},{8,40},{12,44},{16,48},{20,52},{24,56},{28,60},{32,6... | collective-permute-start | bytes 983048 | tf_op jit(solution)/shard_map/ppermute | solution.py:148
  585.2 10.2 %collective-permute-start.52 = (bf16[2,64,1280]{2,1,0:T(8,128)(2,1)S(1)}, bf16[2,64,1280]{2,1,0:T(8,128)(2,1)S(1)}, u32[]{:S(2)}, u32[]{:S(2)}) collective-permute-start(bf16[2,64,1280]{2,1,0:T(8,128)(2,1)S(1)} %fusion.115), channel_id=1, source_target_pairs={{0,96},{4,100},{8,104},{12,108},{16,112},{20,116},{24,120},{28,124... | collective-permute-start | bytes 983048 | tf_op jit(solution)/shard_map/ppermute | solution.py:148
  595.5 9.6 %collective-permute-start.53 = (bf16[64,2560]{1,0:T(8,128)(2,1)S(1)}, bf16[64,2560]{1,0:T(8,128)(2,1)S(1)}, u32[]{:S(2)}, u32[]{:S(2)}) collective-permute-start(bf16[64,2560]{1,0:T(8,128)(2,1)S(1)} %fusion.130), channel_id=1, source_target_pairs={{0,16},{4,20},{8,24},{12,28},{16,0},{20,4},{24,8},{28,12},{32,48},... | collective-permute-start | bytes 983048 | tf_op jit(solution)/shard_map/ppermute | solution.py:163
  (40 other events, 247.7 us)
Sparse Core Ops, SparseCore 0:
  16.9 177.5 all-gather.1
  308.4 294.5 reduce-scatter.1

commit v19 on v13

--- a/solution.py
+++ b/solution.py
@@ -8,7 +8,7 @@
 from jax.sharding import PartitionSpec as P
 
 HK = 128
-HIGHEST = lax.Precision.HIGHEST
+HIGHEST = lax.Precision.HIGH
 
 
 epsilon = 1e-06

time: 612 us -> 605 us (0.989)
    ppermute x4, starting transfers between devices: 20.1 us -> 7.8 us  [row_sum(): lax.ppermute(theirs.astype(jnp.bfloat16), 'tensor', ACROSS)]
    ppermute x4, starting transfers between devices: 4.14 us -> 16.4 us  [row_gather(): across = lax.ppermute(values, 'tensor', ACROSS)]
    ppermute x4, waiting for transfers between devices: 43.2 us -> 32 us  [row_sum(): lax.ppermute(theirs.astype(jnp.bfloat16), 'tensor', ACROSS)]
  transfers between devices with their start and end apart: 58 -> 58, of which waited for: 30 -> 26; matrix products, arithmetic and copies ran while one was open for 30% -> 30% of each run, Pallas kernels for 2% -> 2%
where the time goes in v19:
time: 605 us; the launch traced here: 595 us
  waiting for transfers between devices  230 us (38%)
  starting transfers between devices  107 us (18%)
  local copies, waits for them, and re-layouts  84.8 us (14%)
  matrix products  83.5 us (14%)
  other arithmetic  47.1 us (8%)
  Pallas kernels  26.7 us (4%)
  between operations  15.6 us (3%)
    ppermute x12, waiting for transfers between devices, ring_stage(): got = lax.ppermute(acc.astype(jnp.bfloat16), 'dp', pairs)  85.2 us
    ppermute x24, waiting for transfers between devices, ring_gather(): cur = lax.ppermute(cur, 'dp', pairs)  55.9 us
    ppermute x24, starting transfers between devices, ring_gather(): cur = lax.ppermute(cur, 'dp', pairs)  39.9 us
    dot_general x8, matrix products, matmul_plain(): return jnp.dot(left, right, preferred_element_type=jnp.float32)  38.9 us
    ppermute x4, waiting for transfers between devices, row_gather(): across = lax.ppermute(values, 'tensor', ACROSS)  35.6 us
    ppermute x4, waiting for transfers between devices, row_sum(): lax.ppermute(theirs.astype(jnp.bfloat16), 'tensor', ACROSS)  32 us
    dot_general x8, matrix products, times_trans(): lax.dot_general(left, right, (((1,), (1,)), ((), ())), preferred_element_...  31.8 us
    pallas_call x2, Pallas kernels, grad_pack(): pl.pallas_call(functools.partial(pack_kernel, per), grid=(rows_out // til...  26.7 us
  transfers between devices with their start and end apart: 58, of which 26 were waited for; matrix products, arithmetic and copies ran while one was open for 30% of the time, Pallas kernels for 2%

profile of v19, /device:TPU:0, one launch (start us, length us, event | category | flops | bytes accessed | tf_op | source)
XLA Modules:
  0.0 595.2 jit_solution(17321185254234558755)
XLA Ops:
  11.5 3.3 collective-permute-start.2
  16.2 8.9 %all-to-all-start = ((f32[128,3,16]{2,1,0:T(4,128)}), f32[128,3,16]{2,1,0:T(4,128)S(1)}, u32[]{:S(2)}, u32[]{:S(2)}) async-start(f32[128,3,16]{2,1,0:T(4,128)} %broadcast_in_dim.155), calls=%async_computation | async-start | bytes 524288 | tf_op jit(solution)/shard_map/all_to_all | solution.py:215
  29.3 6.6 %all-to-all-done = f32[128,3,16]{2,1,0:T(4,128)S(1)} async-done(((f32[128,3,16]{2,1,0:T(4,128)}), f32[128,3,16]{2,1,0:T(4,128)S(1)}, u32[]{:S(2)}, u32[]{:S(2)}) %all-to-all-start) | async-done | bytes 24608 | tf_op jit(solution)/shard_map/all_to_all | solution.py:215
  48.5 3.2 collective-permute-start.10
  51.7 3.2 collective-permute-start.22
  57.7 3.2 collective-permute-start.11
  61.0 3.1 collective-permute-start.23
  66.3 3.2 collective-permute-start.12
  70.3 3.3 collective-permute-start.24
  74.8 15.0 %collective-permute-done.6 = bf16[2,4,16,2560]{3,2,1,0:T(8,128)(2,1)} collective-permute-done((bf16[2,4,16,2560]{3,2,1,0:T(8,128)(2,1)S(1)}, bf16[2,4,16,2560]{3,2,1,0:T(8,128)(2,1)}, u32[]{:S(2)}, u32[]{:S(2)}) %collective-permute-start.6) | collective-permute-done | bytes 655392 | tf_op jit(solution)/shard_map/ppermute | solution.py:193
  89.8 3.7 collective-permute-start.13
  93.6 9.1 %collective-permute-done.18 = bf16[4,2,16,2560]{3,2,1,0:T(8,128)(2,1)} collective-permute-done((bf16[4,2,16,2560]{3,2,1,0:T(8,128)(2,1)}, bf16[4,2,16,2560]{3,2,1,0:T(8,128)(2,1)}, u32[]{:S(2)}, u32[]{:S(2)}) %collective-permute-start.18) | collective-permute-done | bytes 655392 | tf_op jit(solution)/shard_map/ppermute | solution.py:207
  102.7 3.2 collective-permute-start.25
  107.1 2.9 pad_maximum_fusion.1
  110.0 3.2 collective-permute-start.14
  113.2 8.7 %collective-permute-done.19 = bf16[4,2,16,2560]{3,2,1,0:T(8,128)(2,1)S(1)} collective-permute-done((bf16[4,2,16,2560]{3,2,1,0:T(8,128)(2,1)}, bf16[4,2,16,2560]{3,2,1,0:T(8,128)(2,1)S(1)}, u32[]{:S(2)}, u32[]{:S(2)}) %collective-permute-start.19) | collective-permute-done | bytes 655392 | tf_op jit(solution)/shard_map/ppermute | solution.py:207
  121.9 3.5 collective-permute-start.26
  132.6 20.7 %collective-permute-done.20 = bf16[4,2,16,2560]{3,2,1,0:T(8,128)(2,1)S(1)} collective-permute-done((bf16[4,2,16,2560]{3,2,1,0:T(8,128)(2,1)S(1)}, bf16[4,2,16,2560]{3,2,1,0:T(8,128)(2,1)S(1)}, u32[]{:S(2)}, u32[]{:S(2)}) %collective-permute-start.20) | collective-permute-done | bytes 655392 | tf_op jit(solution)/shard_map/ppermute | solution.py:207
  154.8 3.1 slice_bitcast_fusion
  160.4 3.9 copy.148
  164.3 4.0 copy.150
  170.8 3.6 fusion.57
  187.2 5.3 fusion.75
  192.6 3.1 fusion.30
  196.0 4.1 collective-permute-done.27
  202.3 13.4 %collective-permute-start.33 = (bf16[128,2048]{1,0:T(8,128)(2,1)S(1)}, bf16[128,2048]{1,0:T(8,128)(2,1)}, u32[]{:S(2)}, u32[]{:S(2)}) collective-permute-start(bf16[128,2048]{1,0:T(8,128)(2,1)S(1)} %bitcast.427), channel_id=1, source_target_pairs={{0,2},{2,0},{1,3},{3,1},{4,6},{6,4},{5,7},{7,5},{8,10},{10,8},{9,1... | collective-permute-start | bytes 1572872 | tf_op jit(solution)/shard_map/ppermute | solution.py:108
  219.0 10.5 %collective-permute-done.33 = bf16[128,2048]{1,0:T(8,128)(2,1)} collective-permute-done((bf16[128,2048]{1,0:T(8,128)(2,1)S(1)}, bf16[128,2048]{1,0:T(8,128)(2,1)}, u32[]{:S(2)}, u32[]{:S(2)}) %collective-permute-start.33) | collective-permute-done | bytes 524320 | tf_op jit(solution)/shard_map/ppermute | solution.py:108
  230.9 8.6 %collective-permute-done.29 = bf16[128,2048]{1,0:T(8,128)(2,1)S(1)} collective-permute-done((bf16[128,2048]{1,0:T(8,128)(2,1)S(1)}, bf16[128,2048]{1,0:T(8,128)(2,1)S(1)}, u32[]{:S(2)}, u32[]{:S(2)}) %collective-permute-start.29) | collective-permute-done | bytes 524320 | tf_op jit(solution)/shard_map/ppermute | solution.py:108
  243.9 8.4 %fusion = f32[512,1408]{1,0:T(8,128)} fusion(bf16[512,2048]{1,0:T(8,128)(2,1)} %bitcast.438, bf16[2048,4224]{1,0:T(8,128)(2,1)} %all-gather.2.cloned.1.call-done), kind=kOutput, calls=%fused_computation.2 | convolution fusion | flops 2952790016 | bytes 10747904 | tf_op jit(solution)/shard_map/dot_general | solution.py:27
  253.8 5.0 fusion.6
  258.8 6.6 %multiply_convert_fusion.1 = (bf16[512,1408]{1,0:T(8,128)(2,1)S(1)}, bf16[512,1408]{1,0:T(8,128)(2,1)S(1)}, bf16[512,1408]{1,0:T(8,128)(2,1)S(1)}) fusion(f32[512,1408]{1,0:T(8,128)} %fusion, f32[512,1408]{1,0:T(8,128)} %fusion.6, bf16[512,2048]{1,0:T(8,128)(2,1)S(1)} %bitcast.442, bf16[2048,4224]{1,0:T(8,128)(2,1)S(1)} %copy-done.38), kind=kOutput, calls=%fused_computation.18 | convolution fusion | flops 2963603456 | bytes 17956864 | tf_op jit(solution)/shard_map/dot_general | solution.py:27
  269.6 15.7 %shard_map.247 = bf16[2048,4224]{1,0:T(8,128)(2,1)} custom-call(bf16[512,2048]{1,0:T(8,128)(2,1)} %bitcast.440, bf16[512,2048]{1,0:T(8,128)(2,1)} %bitcast.439, bf16[512,4224]{1,0:T(8,128)(2,1)} %pad_maximum_fusion.right_ref), custom_call_target="tpu_custom_call" | custom-call | flops 8858370048 | bytes 25821184 | tf_op jit(solution)/shard_map/pallas_call | solution.py:64
  285.3 6.0 %fusion.4 = f32[512,2048]{1,0:T(8,128)S(1)} fusion(bf16[512,1408]{1,0:T(8,128)(2,1)} %copy-done.28, bf16[2048,4224]{1,0:T(8,128)(2,1)} %all-gather.2.cloned.1.call-done), kind=kOutput, calls=%fused_computation.6 | convolution fusion | flops 2952790016 | bytes 11403264 | tf_op jit(solution)/shard_map/dot_general | solution.py:31
  291.3 5.5 fusion.12
  298.3 5.5 fusion.2
  310.0 13.8 %collective-permute-done.36 = bf16[128,2048]{1,0:T(8,128)(2,1)S(1)} collective-permute-done((bf16[128,2048]{1,0:T(8,128)(2,1)S(1)}, bf16[128,2048]{1,0:T(8,128)(2,1)S(1)}, u32[]{:S(2)}, u32[]{:S(2)}) %collective-permute-start.36) | collective-permute-done | bytes 524320 | tf_op jit(solution)/shard_map/ppermute | solution.py:119
  324.3 13.7 %collective-permute-done.32 = bf16[128,2048]{1,0:T(8,128)(2,1)S(1)} collective-permute-done((bf16[128,2048]{1,0:T(8,128)(2,1)S(1)}, bf16[128,2048]{1,0:T(8,128)(2,1)S(1)}, u32[]{:S(2)}, u32[]{:S(2)}) %collective-permute-start.32) | collective-permute-done | bytes 524320 | tf_op jit(solution)/shard_map/ppermute | solution.py:119
  341.1 16.5 %collective-permute-done.37 = bf16[128,2048]{1,0:T(8,128)(2,1)S(1)} collective-permute-done((bf16[128,2048]{1,0:T(8,128)(2,1)S(1)}, bf16[128,2048]{1,0:T(8,128)(2,1)S(1)}, u32[]{:S(2)}, u32[]{:S(2)}) %collective-permute-start.37) | collective-permute-done | bytes 524320 | tf_op jit(solution)/shard_map/ppermute | solution.py:108
  360.7 4.6 fusion.135
  384.1 11.0 %shard_map.246 = bf16[2048,2560]{1,0:T(8,128)(2,1)} custom-call(bf16[512,2048]{1,0:T(8,128)(2,1)} %bitcast.435, bf16[512,2048]{1,0:T(8,128)(2,1)} %bitcast.437, bf16[512,2560]{1,0:T(8,128)(2,1)} %constant_dynamic-update-slice_fusion.4.right_ref), custom_call_target="tpu_custom_call" | custom-call | flops 5368709120 | bytes 17301504 | tf_op jit(solution)/shard_map/pallas_call | solution.py:64
  395.1 9.3 %copy.203 = bf16[4,2,4,64,2560]{4,3,1,0,2:T(8,128)(2,1)} copy(bf16[4,2,4,64,2560]{4,3,2,1,0:T(8,128)(2,1)} %bitcast.420) | data formatting | bytes 20971520 | tf_op jit(solution)/shard_map/reshape | solution.py:157
  404.4 9.5 %fusion.146 = (bf16[4,4,2,64,1280]{4,3,2,1,0:T(8,128)(2,1)}, bf16[4,4,2,64,1280]{4,3,2,1,0:T(8,128)(2,1)}) fusion(bf16[4,4,2,64,2560]{4,3,2,1,0:T(8,128)(2,1)} %bitcast.419), kind=kLoop, calls=%fused_computation.275 | loop fusion | bytes 20971520 | tf_op jit(solution)/shard_map/slice | solution.py:140
  415.6 2.9 fusion.39
  418.5 2.9 fusion.37
  423.9 3.2 collective-permute-start.47
  427.1 2.9 fusion.35
  430.0 3.0 add_add_fusion
  434.6 12.5 %collective-permute-done.41 = bf16[4,2,64,1280]{3,2,1,0:T(8,128)(2,1)S(1)} collective-permute-done((bf16[4,2,64,1280]{3,2,1,0:T(8,128)(2,1)S(1)}, bf16[4,2,64,1280]{3,2,1,0:T(8,128)(2,1)S(1)}, u32[]{:S(2)}, u32[]{:S(2)}) %collective-permute-start.41) | collective-permute-done | bytes 1310752 | tf_op jit(solution)/shard_map/ppermute | solution.py:148
  449.9 5.1 collective-permute-done.47
  455.0 3.1 fusion.16
  458.2 3.7 collective-permute-start.48
  463.1 17.9 %collective-permute-done.42 = bf16[4,2,64,1280]{3,2,1,0:T(8,128)(2,1)} collective-permute-done((bf16[4,2,64,1280]{3,2,1,0:T(8,128)(2,1)}, bf16[4,2,64,1280]{3,2,1,0:T(8,128)(2,1)}, u32[]{:S(2)}, u32[]{:S(2)}) %collective-permute-start.42) | collective-permute-done | bytes 1310752 | tf_op jit(solution)/shard_map/ppermute | solution.py:148
  481.0 3.1 fusion.20
  488.9 3.1 fusion.17
  492.0 3.7 collective-permute-start.49
  495.6 4.4 collective-permute-done.40
  503.6 7.9 %all-to-all-start.1 = ((f32[128,3,16]{2,1,0:T(4,128)}), f32[128,3,16]{2,1,0:T(4,128)S(1)}, u32[]{:S(2)}, u32[]{:S(2)}) async-start(f32[128,3,16]{2,1,0:T(4,128)} %copy.166), calls=%async_computation.1 | async-start | bytes 524288 | tf_op jit(solution)/shard_map/all_to_all | solution.py:222
  511.5 10.7 %collective-permute-done.43 = bf16[4,2,64,1280]{3,2,1,0:T(8,128)(2,1)} collective-permute-done((bf16[4,2,64,1280]{3,2,1,0:T(8,128)(2,1)}, bf16[4,2,64,1280]{3,2,1,0:T(8,128)(2,1)}, u32[]{:S(2)}, u32[]{:S(2)}) %collective-permute-start.43) | collective-permute-done | bytes 1310752 | tf_op jit(solution)/shard_map/ppermute | solution.py:148
  525.7 9.7 %collective-permute-done.49 = bf16[4,2,64,1280]{3,2,1,0:T(8,128)(2,1)} collective-permute-done((bf16[4,2,64,1280]{3,2,1,0:T(8,128)(2,1)}, bf16[4,2,64,1280]{3,2,1,0:T(8,128)(2,1)}, u32[]{:S(2)}, u32[]{:S(2)}) %collective-permute-start.49) | collective-permute-done | bytes 1310752 | tf_op jit(solution)/shard_map/ppermute | solution.py:148
  540.3 12.4 %collective-permute-done.50 = bf16[2,64,1280]{2,1,0:T(8,128)(2,1)S(1)} collective-permute-done((bf16[2,64,1280]{2,1,0:T(8,128)(2,1)S(1)}, bf16[2,64,1280]{2,1,0:T(8,128)(2,1)S(1)}, u32[]{:S(2)}, u32[]{:S(2)}) %collective-permute-start.50) | collective-permute-done | bytes 327712 | tf_op jit(solution)/shard_map/ppermute | solution.py:148
  555.4 9.2 %collective-permute-done.51 = bf16[2,64,1280]{2,1,0:T(8,128)(2,1)S(1)} collective-permute-done((bf16[2,64,1280]{2,1,0:T(8,128)(2,1)S(1)}, bf16[2,64,1280]{2,1,0:T(8,128)(2,1)S(1)}, u32[]{:S(2)}, u32[]{:S(2)}) %collective-permute-start.51) | collective-permute-done | bytes 327712 | tf_op jit(solution)/shard_map/ppermute | solution.py:148
  564.7 3.8 collective-permute-start.52
  568.6 6.8 %collective-permute-done.52 = bf16[2,64,1280]{2,1,0:T(8,128)(2,1)S(1)} collective-permute-done((bf16[2,64,1280]{2,1,0:T(8,128)(2,1)S(1)}, bf16[2,64,1280]{2,1,0:T(8,128)(2,1)S(1)}, u32[]{:S(2)}, u32[]{:S(2)}) %collective-permute-start.52) | collective-permute-done | bytes 327712 | tf_op jit(solution)/shard_map/ppermute | solution.py:148
  577.8 6.3 %collective-permute-done.53 = bf16[64,2560]{1,0:T(8,128)(2,1)S(1)} collective-permute-done((bf16[64,2560]{1,0:T(8,128)(2,1)S(1)}, bf16[64,2560]{1,0:T(8,128)(2,1)S(1)}, u32[]{:S(2)}, u32[]{:S(2)}) %collective-permute-start.53) | collective-permute-done | bytes 327712 | tf_op jit(solution)/shard_map/ppermute | solution.py:163
  (302 shorter events, 142.2 us)
Async XLA Ops:
  7.2 20.3 %copy-start = (s32[1,4,128]{2,1,0:T(4,128)S(1)}, s32[1,4,128]{2,1,0:T(4,128)}, u32[]{:S(2)}) copy-start(s32[1,4,128]{2,1,0:T(4,128)} %param.16) | copy-start | bytes 6148
  7.2 20.3 %copy-start.37 = (s32[4]{0:T(128)S(1)}, s32[4]{0:T(128)}, u32[]{:S(2)}) copy-start(s32[4]{0:T(128)} %constant.282.clone) | copy-start | bytes 52
  7.2 20.1 %copy-start.4 = (bf16[1,1,128,2048]{3,2,1,0:T(8,128)(2,1)S(1)}, bf16[1,1,128,2048]{3,2,1,0:T(8,128)(2,1)}, u32[]{:S(2)}) copy-start(bf16[1,1,128,2048]{3,2,1,0:T(8,128)(2,1)} %param.15) | copy-start | bytes 1572868
  11.5 27.0 %collective-permute-start.2 = (bf16[64,2560]{1,0:T(8,128)(2,1)S(1)}, bf16[64,2560]{1,0:T(8,128)(2,1)S(1)}, u32[]{:S(2)}, u32[]{:S(2)}) collective-permute-start(bf16[64,2560]{1,0:T(8,128)(2,1)S(1)} %bitcast_dynamic-update-slice_fusion.37), channel_id=1, source_target_pairs={{0,16},{4,20},{8,24},{12,28},{16,0},{20,4},{24,8},{28,12},{32,48},... | collective-permute-start | bytes 983048 | tf_op jit(solution)/shard_map/ppermute | solution.py:171
  16.2 19.7 %all-to-all-start = ((f32[128,3,16]{2,1,0:T(4,128)}), f32[128,3,16]{2,1,0:T(4,128)S(1)}, u32[]{:S(2)}, u32[]{:S(2)}) async-start(f32[128,3,16]{2,1,0:T(4,128)} %broadcast_in_dim.155), calls=%async_computation | async-start | bytes 524288 | tf_op jit(solution)/shard_map/all_to_all | solution.py:215
  25.1 218.7 %all-gather.2.cloned.1.call-start = ((), (), s32[]{:S(2)}) async-start(), calls=%async_computation.3 | async-start | bytes 17842176 | tf_op jit(solution)/shard_map/all_gather | solution.py:260
  27.2 557.8 %reduce-scatter.2.cloned.1.call-start = ((), (), s32[]{:S(2)}) async-start(), calls=%async_computation.4 | async-start | bytes 17842176 | tf_op jit(solution)/shard_map/reduce_scatter | solution.py:306
  37.5 18.8 %collective-permute-start = (bf16[128,2048]{1,0:T(8,128)(2,1)}, bf16[128,2048]{1,0:T(8,128)(2,1)}, u32[]{:S(2)}, u32[]{:S(2)}) collective-permute-start(bf16[128,2048]{1,0:T(8,128)(2,1)} %fusion.63), channel_id=1, source_target_pairs={{0,2},{2,0},{1,3},{3,1},{4,6},{6,4},{5,7},{7,5},{8,10},{10,8},{9,1... | collective-permute-start | bytes 1572872 | tf_op jit(solution)/shard_map/ppermute | solution.py:108
  38.6 9.8 %collective-permute-start.3 = (bf16[2,16,2560]{2,1,0:T(8,128)(2,1)S(1)}, bf16[2,16,2560]{2,1,0:T(8,128)(2,1)S(1)}, u32[]{:S(2)}, u32[]{:S(2)}) collective-permute-start(bf16[2,16,2560]{2,1,0:T(8,128)(2,1)S(1)} %get-tuple-element.52), channel_id=1, source_target_pairs={{0,4},{4,8},{8,12},{12,0},{16,20},{20,24},{24,28},{28,16},{32,36},... | collective-permute-start | bytes 491528 | tf_op jit(solution)/shard_map/ppermute | solution.py:187
  39.3 9.2 %collective-permute-start.9 = (bf16[2,16,2560]{2,1,0:T(8,128)(2,1)S(1)}, bf16[2,16,2560]{2,1,0:T(8,128)(2,1)S(1)}, u32[]{:S(2)}, u32[]{:S(2)}) collective-permute-start(bf16[2,16,2560]{2,1,0:T(8,128)(2,1)S(1)} %get-tuple-element.51), channel_id=1, source_target_pairs={{0,12},{4,0},{8,4},{12,8},{16,28},{20,16},{24,20},{28,24},{32,44},... | collective-permute-start | bytes 491528 | tf_op jit(solution)/shard_map/ppermute | solution.py:187
  41.9 9.8 %collective-permute-start.15 = (bf16[2,16,2560]{2,1,0:T(8,128)(2,1)S(1)}, bf16[2,16,2560]{2,1,0:T(8,128)(2,1)S(1)}, u32[]{:S(2)}, u32[]{:S(2)}) collective-permute-start(bf16[2,16,2560]{2,1,0:T(8,128)(2,1)S(1)} %get-tuple-element.50), channel_id=1, source_target_pairs={{0,32},{4,36},{8,40},{12,44},{16,48},{20,52},{24,56},{28,60},{32,6... | collective-permute-start | bytes 491528 | tf_op jit(solution)/shard_map/ppermute | solution.py:201
  42.7 9.0 %collective-permute-start.21 = (bf16[2,16,2560]{2,1,0:T(8,128)(2,1)S(1)}, bf16[2,16,2560]{2,1,0:T(8,128)(2,1)S(1)}, u32[]{:S(2)}, u32[]{:S(2)}) collective-permute-start(bf16[2,16,2560]{2,1,0:T(8,128)(2,1)S(1)} %get-tuple-element.49), channel_id=1, source_target_pairs={{0,96},{4,100},{8,104},{12,108},{16,112},{20,116},{24,120},{28,124... | collective-permute-start | bytes 491528 | tf_op jit(solution)/shard_map/ppermute | solution.py:201
  48.4 9.2 %collective-permute-start.4 = (bf16[2,16,2560]{2,1,0:T(8,128)(2,1)S(1)}, bf16[2,16,2560]{2,1,0:T(8,128)(2,1)S(1)}, u32[]{:S(2)}, u32[]{:S(2)}) collective-permute-start(bf16[2,16,2560]{2,1,0:T(8,128)(2,1)S(1)} %collective-permute-done.3), channel_id=1, source_target_pairs={{0,4},{4,8},{8,12},{12,0},{16,20},{20,24},{24,28},{28,16},{32,36},... | collective-permute-start | bytes 491528 | tf_op jit(solution)/shard_map/ppermute | solution.py:187
  48.5 9.2 %collective-permute-start.10 = (bf16[2,16,2560]{2,1,0:T(8,128)(2,1)S(1)}, bf16[2,16,2560]{2,1,0:T(8,128)(2,1)S(1)}, u32[]{:S(2)}, u32[]{:S(2)}) collective-permute-start(bf16[2,16,2560]{2,1,0:T(8,128)(2,1)S(1)} %collective-permute-done.9), channel_id=1, source_target_pairs={{0,12},{4,0},{8,4},{12,8},{16,28},{20,16},{24,20},{28,24},{32,44},... | collective-permute-start | bytes 491528 | tf_op jit(solution)/shard_map/ppermute | solution.py:187
  51.7 9.2 %collective-permute-start.16 = (bf16[2,16,2560]{2,1,0:T(8,128)(2,1)S(1)}, bf16[2,16,2560]{2,1,0:T(8,128)(2,1)S(1)}, u32[]{:S(2)}, u32[]{:S(2)}) collective-permute-start(bf16[2,16,2560]{2,1,0:T(8,128)(2,1)S(1)} %collective-permute-done.15), channel_id=1, source_target_pairs={{0,32},{4,36},{8,40},{12,44},{16,48},{20,52},{24,56},{28,60},{32,6... | collective-permute-start | bytes 491528 | tf_op jit(solution)/shard_map/ppermute | solution.py:201
  51.7 9.3 %collective-permute-start.22 = (bf16[2,16,2560]{2,1,0:T(8,128)(2,1)S(1)}, bf16[2,16,2560]{2,1,0:T(8,128)(2,1)S(1)}, u32[]{:S(2)}, u32[]{:S(2)}) collective-permute-start(bf16[2,16,2560]{2,1,0:T(8,128)(2,1)S(1)} %collective-permute-done.21), channel_id=1, source_target_pairs={{0,96},{4,100},{8,104},{12,108},{16,112},{20,116},{24,120},{28,124... | collective-permute-start | bytes 491528 | tf_op jit(solution)/shard_map/ppermute | solution.py:201
  57.5 49.6 %collective-permute-start.1 = (bf16[2,128,2048]{2,1,0:T(8,128)(2,1)S(1)}, bf16[2,128,2048]{2,1,0:T(8,128)(2,1)}, u32[]{:S(2)}, u32[]{:S(2)}) collective-permute-start(bf16[2,128,2048]{2,1,0:T(8,128)(2,1)S(1)} %pad_maximum_fusion.5), channel_id=1, source_target_pairs={{0,1},{1,0},{2,3},{3,2},{4,5},{5,4},{6,7},{7,6},{8,9},{9,8},{10,11... | collective-permute-start | bytes 3145736 | tf_op jit(solution)/shard_map/ppermute | solution.py:110
  57.6 8.0 %collective-permute-start.5 = (bf16[2,16,2560]{2,1,0:T(8,128)(2,1)S(1)}, bf16[2,16,2560]{2,1,0:T(8,128)(2,1)S(1)}, u32[]{:S(2)}, u32[]{:S(2)}) collective-permute-start(bf16[2,16,2560]{2,1,0:T(8,128)(2,1)S(1)} %collective-permute-done.4), channel_id=1, source_target_pairs={{0,4},{4,8},{8,12},{12,0},{16,20},{20,24},{24,28},{28,16},{32,36},... | collective-permute-start | bytes 491528 | tf_op jit(solution)/shard_map/ppermute | solution.py:187
  57.7 8.0 %collective-permute-start.11 = (bf16[2,16,2560]{2,1,0:T(8,128)(2,1)S(1)}, bf16[2,16,2560]{2,1,0:T(8,128)(2,1)S(1)}, u32[]{:S(2)}, u32[]{:S(2)}) collective-permute-start(bf16[2,16,2560]{2,1,0:T(8,128)(2,1)S(1)} %collective-permute-done.10), channel_id=1, source_target_pairs={{0,12},{4,0},{8,4},{12,8},{16,28},{20,16},{24,20},{28,24},{32,44},... | collective-permute-start | bytes 491528 | tf_op jit(solution)/shard_map/ppermute | solution.py:187
  60.9 8.7 %collective-permute-start.17 = (bf16[2,16,2560]{2,1,0:T(8,128)(2,1)S(1)}, bf16[2,16,2560]{2,1,0:T(8,128)(2,1)S(1)}, u32[]{:S(2)}, u32[]{:S(2)}) collective-permute-start(bf16[2,16,2560]{2,1,0:T(8,128)(2,1)S(1)} %collective-permute-done.16), channel_id=1, source_target_pairs={{0,32},{4,36},{8,40},{12,44},{16,48},{20,52},{24,56},{28,60},{32,6... | collective-permute-start | bytes 491528 | tf_op jit(solution)/shard_map/ppermute | solution.py:201
  61.0 9.2 %collective-permute-start.23 = (bf16[2,16,2560]{2,1,0:T(8,128)(2,1)S(1)}, bf16[2,16,2560]{2,1,0:T(8,128)(2,1)S(1)}, u32[]{:S(2)}, u32[]{:S(2)}) collective-permute-start(bf16[2,16,2560]{2,1,0:T(8,128)(2,1)S(1)} %collective-permute-done.22), channel_id=1, source_target_pairs={{0,96},{4,100},{8,104},{12,108},{16,112},{20,116},{24,120},{28,124... | collective-permute-start | bytes 491528 | tf_op jit(solution)/shard_map/ppermute | solution.py:201
  65.6 24.3 %collective-permute-start.6 = (bf16[2,4,16,2560]{3,2,1,0:T(8,128)(2,1)S(1)}, bf16[2,4,16,2560]{3,2,1,0:T(8,128)(2,1)}, u32[]{:S(2)}, u32[]{:S(2)}) collective-permute-start(bf16[2,4,16,2560]{3,2,1,0:T(8,128)(2,1)S(1)} %bitcast_dynamic-update-slice_fusion.25), channel_id=1, source_target_pairs={{0,32},{4,36},{8,40},{12,44},{16,48},{20,52},{24,56},{28,60},{32,6... | collective-permute-start | bytes 1966088 | tf_op jit(solution)/shard_map/ppermute | solution.py:193
  66.3 23.5 %collective-permute-start.12 = (bf16[2,4,16,2560]{3,2,1,0:T(8,128)(2,1)}, bf16[2,4,16,2560]{3,2,1,0:T(8,128)(2,1)}, u32[]{:S(2)}, u32[]{:S(2)}) collective-permute-start(bf16[2,4,16,2560]{3,2,1,0:T(8,128)(2,1)} %bitcast_dynamic-update-slice_fusion.21), channel_id=1, source_target_pairs={{0,96},{4,100},{8,104},{12,108},{16,112},{20,116},{24,120},{28,124... | collective-permute-start | bytes 1966088 | tf_op jit(solution)/shard_map/ppermute | solution.py:193
  70.2 32.5 %collective-permute-start.18 = (bf16[4,2,16,2560]{3,2,1,0:T(8,128)(2,1)}, bf16[4,2,16,2560]{3,2,1,0:T(8,128)(2,1)}, u32[]{:S(2)}, u32[]{:S(2)}) collective-permute-start(bf16[4,2,16,2560]{3,2,1,0:T(8,128)(2,1)} %bitcast_dynamic-update-slice_fusion.33), channel_id=1, source_target_pairs={{0,4},{4,8},{8,12},{12,0},{16,20},{20,24},{24,28},{28,16},{32,36},... | collective-permute-start | bytes 1966088 | tf_op jit(solution)/shard_map/ppermute | solution.py:207
  70.3 32.4 %collective-permute-start.24 = (bf16[4,2,16,2560]{3,2,1,0:T(8,128)(2,1)S(1)}, bf16[4,2,16,2560]{3,2,1,0:T(8,128)(2,1)}, u32[]{:S(2)}, u32[]{:S(2)}) collective-permute-start(bf16[4,2,16,2560]{3,2,1,0:T(8,128)(2,1)S(1)} %bitcast_dynamic-update-slice_fusion.29), channel_id=1, source_target_pairs={{0,12},{4,0},{8,4},{12,8},{16,28},{20,16},{24,20},{28,24},{32,44},... | collective-permute-start | bytes 1966088 | tf_op jit(solution)/shard_map/ppermute | solution.py:207
  89.8 20.1 %collective-permute-start.7 = (bf16[2,4,16,2560]{3,2,1,0:T(8,128)(2,1)}, bf16[2,4,16,2560]{3,2,1,0:T(8,128)(2,1)S(1)}, u32[]{:S(2)}, u32[]{:S(2)}) collective-permute-start(bf16[2,4,16,2560]{3,2,1,0:T(8,128)(2,1)} %collective-permute-done.6), channel_id=1, source_target_pairs={{0,32},{4,36},{8,40},{12,44},{16,48},{20,52},{24,56},{28,60},{32,6... | collective-permute-start | bytes 1966088 | tf_op jit(solution)/shard_map/ppermute | solution.py:193
  89.8 20.1 %collective-permute-start.13 = (bf16[2,4,16,2560]{3,2,1,0:T(8,128)(2,1)}, bf16[2,4,16,2560]{3,2,1,0:T(8,128)(2,1)S(1)}, u32[]{:S(2)}, u32[]{:S(2)}) collective-permute-start(bf16[2,4,16,2560]{3,2,1,0:T(8,128)(2,1)} %collective-permute-done.12), channel_id=1, source_target_pairs={{0,96},{4,100},{8,104},{12,108},{16,112},{20,116},{24,120},{28,124... | collective-permute-start | bytes 1966088 | tf_op jit(solution)/shard_map/ppermute | solution.py:193
  102.7 19.2 %collective-permute-start.19 = (bf16[4,2,16,2560]{3,2,1,0:T(8,128)(2,1)}, bf16[4,2,16,2560]{3,2,1,0:T(8,128)(2,1)S(1)}, u32[]{:S(2)}, u32[]{:S(2)}) collective-permute-start(bf16[4,2,16,2560]{3,2,1,0:T(8,128)(2,1)} %collective-permute-done.18), channel_id=1, source_target_pairs={{0,4},{4,8},{8,12},{12,0},{16,20},{20,24},{24,28},{28,16},{32,36},... | collective-permute-start | bytes 1966088 | tf_op jit(solution)/shard_map/ppermute | solution.py:207
  102.7 19.2 %collective-permute-start.25 = (bf16[4,2,16,2560]{3,2,1,0:T(8,128)(2,1)}, bf16[4,2,16,2560]{3,2,1,0:T(8,128)(2,1)S(1)}, u32[]{:S(2)}, u32[]{:S(2)}) collective-permute-start(bf16[4,2,16,2560]{3,2,1,0:T(8,128)(2,1)} %collective-permute-done.24), channel_id=1, source_target_pairs={{0,12},{4,0},{8,4},{12,8},{16,28},{20,16},{24,20},{28,24},{32,44},... | collective-permute-start | bytes 1966088 | tf_op jit(solution)/shard_map/ppermute | solution.py:207
  110.0 15.7 %collective-permute-start.8 = (bf16[2,4,16,2560]{3,2,1,0:T(8,128)(2,1)S(1)}, bf16[2,4,16,2560]{3,2,1,0:T(8,128)(2,1)S(1)}, u32[]{:S(2)}, u32[]{:S(2)}) collective-permute-start(bf16[2,4,16,2560]{3,2,1,0:T(8,128)(2,1)S(1)} %collective-permute-done.7), channel_id=1, source_target_pairs={{0,32},{4,36},{8,40},{12,44},{16,48},{20,52},{24,56},{28,60},{32,6... | collective-permute-start | bytes 1966088 | tf_op jit(solution)/shard_map/ppermute | solution.py:193
  110.0 20.2 %collective-permute-start.14 = (bf16[2,4,16,2560]{3,2,1,0:T(8,128)(2,1)S(1)}, bf16[2,4,16,2560]{3,2,1,0:T(8,128)(2,1)S(1)}, u32[]{:S(2)}, u32[]{:S(2)}) collective-permute-start(bf16[2,4,16,2560]{3,2,1,0:T(8,128)(2,1)S(1)} %collective-permute-done.13), channel_id=1, source_target_pairs={{0,96},{4,100},{8,104},{12,108},{16,112},{20,116},{24,120},{28,124... | collective-permute-start | bytes 1966088 | tf_op jit(solution)/shard_map/ppermute | solution.py:193
  121.9 31.5 %collective-permute-start.20 = (bf16[4,2,16,2560]{3,2,1,0:T(8,128)(2,1)S(1)}, bf16[4,2,16,2560]{3,2,1,0:T(8,128)(2,1)S(1)}, u32[]{:S(2)}, u32[]{:S(2)}) collective-permute-start(bf16[4,2,16,2560]{3,2,1,0:T(8,128)(2,1)S(1)} %collective-permute-done.19), channel_id=1, source_target_pairs={{0,4},{4,8},{8,12},{12,0},{16,20},{20,24},{24,28},{28,16},{32,36},... | collective-permute-start | bytes 1966088 | tf_op jit(solution)/shard_map/ppermute | solution.py:207
  121.9 32.8 %collective-permute-start.26 = (bf16[4,2,16,2560]{3,2,1,0:T(8,128)(2,1)S(1)}, bf16[4,2,16,2560]{3,2,1,0:T(8,128)(2,1)S(1)}, u32[]{:S(2)}, u32[]{:S(2)}) collective-permute-start(bf16[4,2,16,2560]{3,2,1,0:T(8,128)(2,1)S(1)} %collective-permute-done.25), channel_id=1, source_target_pairs={{0,12},{4,0},{8,4},{12,8},{16,28},{20,16},{24,20},{28,24},{32,44},... | collective-permute-start | bytes 1966088 | tf_op jit(solution)/shard_map/ppermute | solution.py:207
  195.9 4.2 collective-permute-start.27
  200.3 15.5 %collective-permute-start.28 = (bf16[128,2048]{1,0:T(8,128)(2,1)S(1)}, bf16[128,2048]{1,0:T(8,128)(2,1)}, u32[]{:S(2)}, u32[]{:S(2)}) collective-permute-start(bf16[128,2048]{1,0:T(8,128)(2,1)S(1)} %fusion.93), channel_id=1, source_target_pairs={{0,2},{2,0},{1,3},{3,1},{4,6},{6,4},{5,7},{7,5},{8,10},{10,8},{9,1... | collective-permute-start | bytes 1572872 | tf_op jit(solution)/shard_map/ppermute | solution.py:119
  202.3 27.2 %collective-permute-start.33 = (bf16[128,2048]{1,0:T(8,128)(2,1)S(1)}, bf16[128,2048]{1,0:T(8,128)(2,1)}, u32[]{:S(2)}, u32[]{:S(2)}) collective-permute-start(bf16[128,2048]{1,0:T(8,128)(2,1)S(1)} %bitcast.427), channel_id=1, source_target_pairs={{0,2},{2,0},{1,3},{3,1},{4,6},{6,4},{5,7},{7,5},{8,10},{10,8},{9,1... | collective-permute-start | bytes 1572872 | tf_op jit(solution)/shard_map/ppermute | solution.py:108
  218.0 21.5 %collective-permute-start.29 = (bf16[128,2048]{1,0:T(8,128)(2,1)S(1)}, bf16[128,2048]{1,0:T(8,128)(2,1)S(1)}, u32[]{:S(2)}, u32[]{:S(2)}) collective-permute-start(bf16[128,2048]{1,0:T(8,128)(2,1)S(1)} %multiply_convert_fusion.4), channel_id=1, source_target_pairs={{0,2},{2,0},{1,3},{3,1},{4,6},{6,4},{5,7},{7,5},{8,10},{10,8},{9,1... | collective-permute-start | bytes 1572872 | tf_op jit(solution)/shard_map/ppermute | solution.py:108
  230.6 9.1 %collective-permute-start.34 = (bf16[2,128,2048]{2,1,0:T(8,128)(2,1)S(1)}, bf16[2,128,2048]{2,1,0:T(8,128)(2,1)S(1)}, u32[]{:S(2)}, u32[]{:S(2)}) collective-permute-start(bf16[2,128,2048]{2,1,0:T(8,128)(2,1)S(1)} %pad_maximum_fusion.7), channel_id=1, source_target_pairs={{0,1},{1,0},{2,3},{3,2},{4,5},{5,4},{6,7},{7,6},{8,9},{9,8},{10,11... | collective-permute-start | bytes 3145736 | tf_op jit(solution)/shard_map/ppermute | solution.py:110
  239.6 2.7 collective-permute-start.30
  297.1 7.4 %collective-permute-start.35 = (f32[2,128,2048]{2,1,0:T(8,128)S(1)}, f32[2,128,2048]{2,1,0:T(8,128)S(1)}, u32[]{:S(2)}, u32[]{:S(2)}) collective-permute-start(f32[2,128,2048]{2,1,0:T(8,128)S(1)} %bitcast.445), channel_id=1, source_target_pairs={{0,1},{1,0},{2,3},{3,2},{4,5},{5,4},{6,7},{7,6},{8,9},{9,8},{10,11... | collective-permute-start | bytes 6291464 | tf_op jit(solution)/shard_map/ppermute | solution.py:116
  304.0 4.4 collective-permute-start.31
  304.7 19.1 %collective-permute-start.36 = (bf16[128,2048]{1,0:T(8,128)(2,1)S(1)}, bf16[128,2048]{1,0:T(8,128)(2,1)S(1)}, u32[]{:S(2)}, u32[]{:S(2)}) collective-permute-start(bf16[128,2048]{1,0:T(8,128)(2,1)S(1)} %fusion.83), channel_id=1, source_target_pairs={{0,2},{2,0},{1,3},{3,1},{4,6},{6,4},{5,7},{7,5},{8,10},{10,8},{9,1... | collective-permute-start | bytes 1572872 | tf_op jit(solution)/shard_map/ppermute | solution.py:119
  308.5 29.5 %collective-permute-start.32 = (bf16[128,2048]{1,0:T(8,128)(2,1)S(1)}, bf16[128,2048]{1,0:T(8,128)(2,1)S(1)}, u32[]{:S(2)}, u32[]{:S(2)}) collective-permute-start(bf16[128,2048]{1,0:T(8,128)(2,1)S(1)} %fusion.87), channel_id=1, source_target_pairs={{0,2},{2,0},{1,3},{3,1},{4,6},{6,4},{5,7},{7,5},{8,10},{10,8},{9,1... | collective-permute-start | bytes 1572872 | tf_op jit(solution)/shard_map/ppermute | solution.py:119
  339.7 17.9 %collective-permute-start.37 = (bf16[128,2048]{1,0:T(8,128)(2,1)S(1)}, bf16[128,2048]{1,0:T(8,128)(2,1)S(1)}, u32[]{:S(2)}, u32[]{:S(2)}) collective-permute-start(bf16[128,2048]{1,0:T(8,128)(2,1)S(1)} %get-tuple-element.25), channel_id=1, source_target_pairs={{0,2},{2,0},{1,3},{3,1},{4,6},{6,4},{5,7},{7,5},{8,10},{10,8},{9,1... | collective-permute-start | bytes 1572872 | tf_op jit(solution)/shard_map/ppermute | solution.py:108
  357.7 2.7 collective-permute-start.38
  415.3 31.8 %collective-permute-start.41 = (bf16[4,2,64,1280]{3,2,1,0:T(8,128)(2,1)S(1)}, bf16[4,2,64,1280]{3,2,1,0:T(8,128)(2,1)S(1)}, u32[]{:S(2)}, u32[]{:S(2)}) collective-permute-start(bf16[4,2,64,1280]{3,2,1,0:T(8,128)(2,1)S(1)} %dynamic-slice_bitcast_fusion.1), channel_id=1, source_target_pairs={{0,4},{4,8},{8,12},{12,0},{16,20},{20,24},{24,28},{28,16},{32,36},... | collective-permute-start | bytes 3932168 | tf_op jit(solution)/shard_map/ppermute | solution.py:148
  423.9 31.2 %collective-permute-start.47 = (bf16[4,2,64,1280]{3,2,1,0:T(8,128)(2,1)}, bf16[4,2,64,1280]{3,2,1,0:T(8,128)(2,1)}, u32[]{:S(2)}, u32[]{:S(2)}) collective-permute-start(bf16[4,2,64,1280]{3,2,1,0:T(8,128)(2,1)} %dynamic-slice_bitcast_fusion), channel_id=1, source_target_pairs={{0,12},{4,0},{8,4},{12,8},{16,28},{20,16},{24,20},{28,24},{32,44},... | collective-permute-start | bytes 3932168 | tf_op jit(solution)/shard_map/ppermute | solution.py:148
  434.6 49.4 %collective-permute-start.39 = (f32[2,128,2048]{2,1,0:T(8,128)}, f32[2,128,2048]{2,1,0:T(8,128)S(1)}, u32[]{:S(2)}, u32[]{:S(2)}) collective-permute-start(f32[2,128,2048]{2,1,0:T(8,128)} %bitcast.105), channel_id=1, source_target_pairs={{0,1},{1,0},{2,3},{3,2},{4,5},{5,4},{6,7},{7,6},{8,9},{9,8},{10,11... | collective-permute-start | bytes 6291464 | tf_op jit(solution)/shard_map/ppermute | solution.py:116
  449.9 31.1 %collective-permute-start.42 = (bf16[4,2,64,1280]{3,2,1,0:T(8,128)(2,1)}, bf16[4,2,64,1280]{3,2,1,0:T(8,128)(2,1)}, u32[]{:S(2)}, u32[]{:S(2)}) collective-permute-start(bf16[4,2,64,1280]{3,2,1,0:T(8,128)(2,1)} %fusion.19), channel_id=1, source_target_pairs={{0,4},{4,8},{8,12},{12,0},{16,20},{20,24},{24,28},{28,16},{32,36},... | collective-permute-start | bytes 3932168 | tf_op jit(solution)/shard_map/ppermute | solution.py:148
  458.2 30.7 %collective-permute-start.48 = (bf16[4,2,64,1280]{3,2,1,0:T(8,128)(2,1)}, bf16[4,2,64,1280]{3,2,1,0:T(8,128)(2,1)}, u32[]{:S(2)}, u32[]{:S(2)}) collective-permute-start(bf16[4,2,64,1280]{3,2,1,0:T(8,128)(2,1)} %fusion.16), channel_id=1, source_target_pairs={{0,12},{4,0},{8,4},{12,8},{16,28},{20,16},{24,20},{28,24},{32,44},... | collective-permute-start | bytes 3932168 | tf_op jit(solution)/shard_map/ppermute | solution.py:148
  484.1 38.2 %collective-permute-start.43 = (bf16[4,2,64,1280]{3,2,1,0:T(8,128)(2,1)}, bf16[4,2,64,1280]{3,2,1,0:T(8,128)(2,1)}, u32[]{:S(2)}, u32[]{:S(2)}) collective-permute-start(bf16[4,2,64,1280]{3,2,1,0:T(8,128)(2,1)} %fusion.20), channel_id=1, source_target_pairs={{0,4},{4,8},{8,12},{12,0},{16,20},{20,24},{24,28},{28,16},{32,36},... | collective-permute-start | bytes 3932168 | tf_op jit(solution)/shard_map/ppermute | solution.py:148
  485.5 14.6 %collective-permute-start.40 = (bf16[128,2048]{1,0:T(8,128)(2,1)S(1)}, bf16[128,2048]{1,0:T(8,128)(2,1)S(1)}, u32[]{:S(2)}, u32[]{:S(2)}) collective-permute-start(bf16[128,2048]{1,0:T(8,128)(2,1)S(1)} %fusion.79), channel_id=1, source_target_pairs={{0,2},{2,0},{1,3},{3,1},{4,6},{6,4},{5,7},{7,5},{8,10},{10,8},{9,1... | collective-permute-start | bytes 1572872 | tf_op jit(solution)/shard_map/ppermute | solution.py:119
  492.0 43.5 %collective-permute-start.49 = (bf16[4,2,64,1280]{3,2,1,0:T(8,128)(2,1)}, bf16[4,2,64,1280]{3,2,1,0:T(8,128)(2,1)}, u32[]{:S(2)}, u32[]{:S(2)}) collective-permute-start(bf16[4,2,64,1280]{3,2,1,0:T(8,128)(2,1)} %fusion.17), channel_id=1, source_target_pairs={{0,12},{4,0},{8,4},{12,8},{16,28},{20,16},{24,20},{28,24},{32,44},... | collective-permute-start | bytes 3932168 | tf_op jit(solution)/shard_map/ppermute | solution.py:148
  503.6 73.6 %all-to-all-start.1 = ((f32[128,3,16]{2,1,0:T(4,128)}), f32[128,3,16]{2,1,0:T(4,128)S(1)}, u32[]{:S(2)}, u32[]{:S(2)}) async-start(f32[128,3,16]{2,1,0:T(4,128)} %copy.166), calls=%async_computation.1 | async-start | bytes 524288 | tf_op jit(solution)/shard_map/all_to_all | solution.py:222
  524.4 15.8 %collective-permute-start.44 = (bf16[2,64,1280]{2,1,0:T(8,128)(2,1)S(1)}, bf16[2,64,1280]{2,1,0:T(8,128)(2,1)S(1)}, u32[]{:S(2)}, u32[]{:S(2)}) collective-permute-start(bf16[2,64,1280]{2,1,0:T(8,128)(2,1)S(1)} %dynamic-slice_bitcast_fusion.3), channel_id=1, source_target_pairs={{0,32},{4,36},{8,40},{12,44},{16,48},{20,52},{24,56},{28,60},{32,6... | collective-permute-start | bytes 983048 | tf_op jit(solution)/shard_map/ppermute | solution.py:148
  537.5 15.2 %collective-permute-start.50 = (bf16[2,64,1280]{2,1,0:T(8,128)(2,1)S(1)}, bf16[2,64,1280]{2,1,0:T(8,128)(2,1)S(1)}, u32[]{:S(2)}, u32[]{:S(2)}) collective-permute-start(bf16[2,64,1280]{2,1,0:T(8,128)(2,1)S(1)} %dynamic-slice_bitcast_fusion.2), channel_id=1, source_target_pairs={{0,96},{4,100},{8,104},{12,108},{16,112},{20,116},{24,120},{28,124... | collective-permute-start | bytes 983048 | tf_op jit(solution)/shard_map/ppermute | solution.py:148
  540.3 15.0 %collective-permute-start.45 = (bf16[2,64,1280]{2,1,0:T(8,128)(2,1)S(1)}, bf16[2,64,1280]{2,1,0:T(8,128)(2,1)S(1)}, u32[]{:S(2)}, u32[]{:S(2)}) collective-permute-start(bf16[2,64,1280]{2,1,0:T(8,128)(2,1)S(1)} %fusion.116), channel_id=1, source_target_pairs={{0,32},{4,36},{8,40},{12,44},{16,48},{20,52},{24,56},{28,60},{32,6... | collective-permute-start | bytes 983048 | tf_op jit(solution)/shard_map/ppermute | solution.py:148
  552.8 11.8 %collective-permute-start.51 = (bf16[2,64,1280]{2,1,0:T(8,128)(2,1)S(1)}, bf16[2,64,1280]{2,1,0:T(8,128)(2,1)S(1)}, u32[]{:S(2)}, u32[]{:S(2)}) collective-permute-start(bf16[2,64,1280]{2,1,0:T(8,128)(2,1)S(1)} %fusion.114), channel_id=1, source_target_pairs={{0,96},{4,100},{8,104},{12,108},{16,112},{20,116},{24,120},{28,124... | collective-permute-start | bytes 983048 | tf_op jit(solution)/shard_map/ppermute | solution.py:148
  555.3 20.5 %copy-start.10 = (f32[128,2048]{1,0:T(8,128)S(1)}, f32[128,2048]{1,0:T(8,128)}, u32[]{:S(2)}) copy-start(f32[128,2048]{1,0:T(8,128)} %get-tuple-element.26) | copy-start | bytes 3145732
  555.3 20.5 %copy-start.12 = (f32[128,2048]{1,0:T(8,128)S(1)}, f32[128,2048]{1,0:T(8,128)}, u32[]{:S(2)}) copy-start(f32[128,2048]{1,0:T(8,128)} %get-tuple-element.24) | copy-start | bytes 3145732
  555.3 20.5 %copy-start.36 = (f32[128]{0:T(128)S(1)}, f32[128]{0:T(128)}, u32[]{:S(2)}) copy-start(f32[128]{0:T(128)} %get-tuple-element.58) | copy-start | bytes 1540
  555.3 13.1 %collective-permute-start.46 = (bf16[2,64,1280]{2,1,0:T(8,128)(2,1)S(1)}, bf16[2,64,1280]{2,1,0:T(8,128)(2,1)S(1)}, u32[]{:S(2)}, u32[]{:S(2)}) collective-permute-start(bf16[2,64,1280]{2,1,0:T(8,128)(2,1)S(1)} %fusion.117), channel_id=1, source_target_pairs={{0,32},{4,36},{8,40},{12,44},{16,48},{20,52},{24,56},{28,60},{32,6... | collective-permute-start | bytes 983048 | tf_op jit(solution)/shard_map/ppermute | solution.py:148
  564.7 10.6 %collective-permute-start.52 = (bf16[2,64,1280]{2,1,0:T(8,128)(2,1)S(1)}, bf16[2,64,1280]{2,1,0:T(8,128)(2,1)S(1)}, u32[]{:S(2)}, u32[]{:S(2)}) collective-permute-start(bf16[2,64,1280]{2,1,0:T(8,128)(2,1)S(1)} %fusion.115), channel_id=1, source_target_pairs={{0,96},{4,100},{8,104},{12,108},{16,112},{20,116},{24,120},{28,124... | collective-permute-start | bytes 983048 | tf_op jit(solution)/shard_map/ppermute | solution.py:148
  575.4 8.7 %collective-permute-start.53 = (bf16[64,2560]{1,0:T(8,128)(2,1)S(1)}, bf16[64,2560]{1,0:T(8,128)(2,1)S(1)}, u32[]{:S(2)}, u32[]{:S(2)}) collective-permute-start(bf16[64,2560]{1,0:T(8,128)(2,1)S(1)} %fusion.130), channel_id=1, source_target_pairs={{0,16},{4,20},{8,24},{12,28},{16,0},{20,4},{24,8},{28,12},{32,48},... | collective-permute-start | bytes 983048 | tf_op jit(solution)/shard_map/ppermute | solution.py:163
  (33 other events, 169.7 us)
Sparse Core Ops, SparseCore 0:
  29.0 178.8 all-gather.1
  285.4 294.3 reduce-scatter.1

commit v20 on v19

--- a/solution.py
+++ b/solution.py
@@ -172,10 +172,10 @@
     both = jnp.zeros((2,) + values.shape, values.dtype)
     both = lax.dynamic_update_slice(both, values[None], (y_pos, zero, zero))
     both = lax.dynamic_update_slice(both, other[None], (1 - y_pos, zero, zero))
-    part_rows = values.shape[0] // 4
+    part_rows = values.shape[0] // 2
     cols = values.shape[1]
     full = jnp.zeros((4, 2, 4) + values.shape, values.dtype)
-    for part, (x_first, step) in enumerate(((True, 1), (True, 3), (False, 1), (False, 3))):
+    for part, (x_first, step) in enumerate(((True, 1), (True, 3))):
         rows = both[:, part * part_rows : (part + 1) * part_rows]
         row_at = jnp.full((), part * part_rows, jnp.int32)
         if x_first:

time: 605 us -> 672 us (1.11)
  waiting for transfers between devices: 230 us -> 325 us
  starting transfers between devices: 107 us -> 71.3 us
  matrix products: 83.5 us -> 91.3 us
    ppermute x24 -> x12, waiting for transfers between devices: 55.9 us -> 126 us  [ring_gather(): cur = lax.ppermute(cur, 'dp', pairs)]
    ppermute x24 -> x12, starting transfers between devices: 39.9 us -> 20.9 us  [ring_gather(): cur = lax.ppermute(cur, 'dp', pairs)]
    ppermute x4, waiting for transfers between devices: 35.6 us -> 50.9 us  [row_gather(): across = lax.ppermute(values, 'tensor', ACROSS)]
    ppermute x4, starting transfers between devices: 16.4 us -> 2.33 us  [row_gather(): across = lax.ppermute(values, 'tensor', ACROSS)]
    ppermute x4, waiting for transfers between devices: 32 us -> 43.6 us  [row_sum(): lax.ppermute(theirs.astype(jnp.bfloat16), 'tensor', ACROSS)]
    dot_general x8, matrix products: 38.9 us -> 46.7 us  [matmul_plain(): return jnp.dot(left, right, preferred_element_type=jnp.float32)]
    unnamed x85 -> x99, local copies, waits for them, and re-layouts: 14.5 us -> 17.9 us
  transfers between devices with their start and end apart: 58 -> 46, of which waited for: 26 -> 33; matrix products, arithmetic and copies ran while one was open for 30% -> 26% of each run, Pallas kernels for 2% -> 2%
where the time goes in v20:
time: 672 us; the launch traced here: 660 us
  waiting for transfers between devices  325 us (48%)
  matrix products  91.3 us (14%)
  local copies, waits for them, and re-layouts  83.5 us (12%)
  starting transfers between devices  71.3 us (11%)
  other arithmetic  46.4 us (7%)
  Pallas kernels  26.5 us (4%)
  between operations  15.7 us (2%)
    ppermute x12, waiting for transfers between devices, ring_gather(): cur = lax.ppermute(cur, 'dp', pairs)  126 us
    ppermute x12, waiting for transfers between devices, ring_stage(): got = lax.ppermute(acc.astype(jnp.bfloat16), 'dp', pairs)  79.6 us
    ppermute x4, waiting for transfers between devices, row_gather(): across = lax.ppermute(values, 'tensor', ACROSS)  50.9 us
    dot_general x8, matrix products, matmul_plain(): return jnp.dot(left, right, preferred_element_type=jnp.float32)  46.7 us
    ppermute x4, waiting for transfers between devices, row_sum(): lax.ppermute(theirs.astype(jnp.bfloat16), 'tensor', ACROSS)  43.6 us
    dot_general x8, matrix products, times_trans(): lax.dot_general(left, right, (((1,), (1,)), ((), ())), preferred_element_...  31.9 us
    pallas_call x2, Pallas kernels, grad_pack(): pl.pallas_call(functools.partial(pack_kernel, per), grid=(rows_out // til...  26.5 us
    ppermute x12, starting transfers between devices, ring_stage(): got = lax.ppermute(acc.astype(jnp.bfloat16), 'dp', pairs)  22.3 us
  transfers between devices with their start and end apart: 46, of which 33 were waited for; matrix products, arithmetic and copies ran while one was open for 26% of the time, Pallas kernels for 2%

profile of v20, /device:TPU:0, one launch (start us, length us, event | category | flops | bytes accessed | tf_op | source)
XLA Modules:
  0.0 659.5 jit_solution(9786851942672666438)
XLA Ops:
  12.7 3.4 collective-permute-start.2
  16.9 8.9 %all-to-all-start = ((f32[128,3,16]{2,1,0:T(4,128)}), f32[128,3,16]{2,1,0:T(4,128)S(1)}, u32[]{:S(2)}, u32[]{:S(2)}) async-start(f32[128,3,16]{2,1,0:T(4,128)} %broadcast_in_dim.107), calls=%async_computation | async-start | bytes 524288 | tf_op jit(solution)/shard_map/all_to_all | solution.py:215
  27.5 11.0 %all-to-all-done = f32[128,3,16]{2,1,0:T(4,128)S(1)} async-done(((f32[128,3,16]{2,1,0:T(4,128)}), f32[128,3,16]{2,1,0:T(4,128)S(1)}, u32[]{:S(2)}, u32[]{:S(2)}) %all-to-all-start) | async-done | bytes 24608 | tf_op jit(solution)/shard_map/all_to_all | solution.py:215
  44.7 5.9 collective-permute-done.3
  50.6 3.2 collective-permute-start.10
  54.6 14.0 %collective-permute-done.4 = bf16[2,32,2560]{2,1,0:T(8,128)(2,1)S(1)} collective-permute-done((bf16[2,32,2560]{2,1,0:T(8,128)(2,1)S(1)}, bf16[2,32,2560]{2,1,0:T(8,128)(2,1)S(1)}, u32[]{:S(2)}, u32[]{:S(2)}) %collective-permute-start.4) | collective-permute-done | bytes 327712 | tf_op jit(solution)/shard_map/ppermute | solution.py:187
  68.7 3.3 collective-permute-start.11
  72.8 13.9 %collective-permute-done.5 = bf16[2,32,2560]{2,1,0:T(8,128)(2,1)S(1)} collective-permute-done((bf16[2,32,2560]{2,1,0:T(8,128)(2,1)S(1)}, bf16[2,32,2560]{2,1,0:T(8,128)(2,1)S(1)}, u32[]{:S(2)}, u32[]{:S(2)}) %collective-permute-start.5) | collective-permute-done | bytes 327712 | tf_op jit(solution)/shard_map/ppermute | solution.py:187
  87.9 2.8 collective-permute-start.12
  92.4 18.3 %collective-permute-done = bf16[128,2048]{1,0:T(8,128)(2,1)S(1)} collective-permute-done((bf16[128,2048]{1,0:T(8,128)(2,1)}, bf16[128,2048]{1,0:T(8,128)(2,1)S(1)}, u32[]{:S(2)}, u32[]{:S(2)}) %collective-permute-start) | collective-permute-done | bytes 524320 | tf_op jit(solution)/shard_map/ppermute | solution.py:108
  111.8 27.3 %collective-permute-done.6 = bf16[2,4,32,2560]{3,2,1,0:T(8,128)(2,1)} collective-permute-done((bf16[2,4,32,2560]{3,2,1,0:T(8,128)(2,1)}, bf16[2,4,32,2560]{3,2,1,0:T(8,128)(2,1)}, u32[]{:S(2)}, u32[]{:S(2)}) %collective-permute-start.6) | collective-permute-done | bytes 1310752 | tf_op jit(solution)/shard_map/ppermute | solution.py:193
  141.5 3.8 collective-permute-start.13
  148.0 2.8 pad_maximum_fusion.1
  150.8 40.9 %collective-permute-done.7 = bf16[2,4,32,2560]{3,2,1,0:T(8,128)(2,1)} collective-permute-done((bf16[2,4,32,2560]{3,2,1,0:T(8,128)(2,1)}, bf16[2,4,32,2560]{3,2,1,0:T(8,128)(2,1)}, u32[]{:S(2)}, u32[]{:S(2)}) %collective-permute-start.7) | collective-permute-done | bytes 1310752 | tf_op jit(solution)/shard_map/ppermute | solution.py:193
  193.3 3.9 collective-permute-start.14
  198.7 21.2 %collective-permute-done.8 = bf16[2,4,32,2560]{3,2,1,0:T(8,128)(2,1)S(1)} collective-permute-done((bf16[2,4,32,2560]{3,2,1,0:T(8,128)(2,1)}, bf16[2,4,32,2560]{3,2,1,0:T(8,128)(2,1)S(1)}, u32[]{:S(2)}, u32[]{:S(2)}) %collective-permute-start.8) | collective-permute-done | bytes 1310752 | tf_op jit(solution)/shard_map/ppermute | solution.py:193
  223.3 3.1 slice_bitcast_fusion
  228.9 3.9 copy.117
  232.9 4.0 copy.119
  239.3 3.6 fusion.57
  256.6 4.9 fusion.75
  261.5 3.1 fusion.30
  264.9 4.1 collective-permute-done.15
  271.4 12.8 %collective-permute-done.16 = bf16[128,2048]{1,0:T(8,128)(2,1)} collective-permute-done((bf16[128,2048]{1,0:T(8,128)(2,1)S(1)}, bf16[128,2048]{1,0:T(8,128)(2,1)}, u32[]{:S(2)}, u32[]{:S(2)}) %collective-permute-start.16) | collective-permute-done | bytes 524320 | tf_op jit(solution)/shard_map/ppermute | solution.py:119
  286.5 8.9 %collective-permute-done.21 = bf16[128,2048]{1,0:T(8,128)(2,1)} collective-permute-done((bf16[128,2048]{1,0:T(8,128)(2,1)S(1)}, bf16[128,2048]{1,0:T(8,128)(2,1)}, u32[]{:S(2)}, u32[]{:S(2)}) %collective-permute-start.21) | collective-permute-done | bytes 524320 | tf_op jit(solution)/shard_map/ppermute | solution.py:108
  296.8 8.9 %collective-permute-done.17 = bf16[128,2048]{1,0:T(8,128)(2,1)S(1)} collective-permute-done((bf16[128,2048]{1,0:T(8,128)(2,1)S(1)}, bf16[128,2048]{1,0:T(8,128)(2,1)S(1)}, u32[]{:S(2)}, u32[]{:S(2)}) %collective-permute-start.17) | collective-permute-done | bytes 524320 | tf_op jit(solution)/shard_map/ppermute | solution.py:108
  310.1 8.4 %fusion = f32[512,1408]{1,0:T(8,128)} fusion(bf16[512,2048]{1,0:T(8,128)(2,1)} %bitcast.390, bf16[2048,4224]{1,0:T(8,128)(2,1)} %all-gather.2.cloned.1.call-done), kind=kOutput, calls=%fused_computation.2 | convolution fusion | flops 2952790016 | bytes 10747904 | tf_op jit(solution)/shard_map/dot_general | solution.py:27
  320.0 5.0 fusion.6
  325.0 15.2 %multiply_convert_fusion.1 = (bf16[512,1408]{1,0:T(8,128)(2,1)S(1)}, bf16[512,1408]{1,0:T(8,128)(2,1)S(1)}, bf16[512,1408]{1,0:T(8,128)(2,1)S(1)}) fusion(f32[512,1408]{1,0:T(8,128)} %fusion, f32[512,1408]{1,0:T(8,128)} %fusion.6, bf16[512,2048]{1,0:T(8,128)(2,1)S(1)} %bitcast.394, bf16[2048,4224]{1,0:T(8,128)(2,1)S(1)} %copy-done.45), kind=kOutput, calls=%fused_computation.18 | convolution fusion | flops 2963603456 | bytes 17956864 | tf_op jit(solution)/shard_map/dot_general | solution.py:27
  344.4 15.7 %shard_map.247 = bf16[2048,4224]{1,0:T(8,128)(2,1)} custom-call(bf16[512,2048]{1,0:T(8,128)(2,1)} %bitcast.392, bf16[512,2048]{1,0:T(8,128)(2,1)} %bitcast.391, bf16[512,4224]{1,0:T(8,128)(2,1)} %pad_maximum_fusion.right_ref), custom_call_target="tpu_custom_call" | custom-call | flops 8858370048 | bytes 25821184 | tf_op jit(solution)/shard_map/pallas_call | solution.py:64
  360.1 6.0 fusion.4
  366.1 5.5 fusion.12
  373.1 5.5 fusion.2
  380.3 2.9 collective-permute-done.19
  383.7 12.2 %collective-permute-done.24 = bf16[128,2048]{1,0:T(8,128)(2,1)S(1)} collective-permute-done((bf16[128,2048]{1,0:T(8,128)(2,1)S(1)}, bf16[128,2048]{1,0:T(8,128)(2,1)S(1)}, u32[]{:S(2)}, u32[]{:S(2)}) %collective-permute-start.24) | collective-permute-done | bytes 524320 | tf_op jit(solution)/shard_map/ppermute | solution.py:119
  396.4 14.5 %collective-permute-done.20 = bf16[128,2048]{1,0:T(8,128)(2,1)S(1)} collective-permute-done((bf16[128,2048]{1,0:T(8,128)(2,1)S(1)}, bf16[128,2048]{1,0:T(8,128)(2,1)S(1)}, u32[]{:S(2)}, u32[]{:S(2)}) %collective-permute-start.20) | collective-permute-done | bytes 524320 | tf_op jit(solution)/shard_map/ppermute | solution.py:119
  414.0 14.8 %collective-permute-done.25 = bf16[128,2048]{1,0:T(8,128)(2,1)S(1)} collective-permute-done((bf16[128,2048]{1,0:T(8,128)(2,1)S(1)}, bf16[128,2048]{1,0:T(8,128)(2,1)S(1)}, u32[]{:S(2)}, u32[]{:S(2)}) %collective-permute-start.25) | collective-permute-done | bytes 524320 | tf_op jit(solution)/shard_map/ppermute | solution.py:108
  431.9 4.6 fusion.135
  439.4 2.7 fusion.60
  455.4 10.8 %shard_map.246 = bf16[2048,2560]{1,0:T(8,128)(2,1)} custom-call(bf16[512,2048]{1,0:T(8,128)(2,1)} %bitcast.387, bf16[512,2048]{1,0:T(8,128)(2,1)} %bitcast.389, bf16[512,2560]{1,0:T(8,128)(2,1)} %constant_dynamic-update-slice_fusion.4.right_ref), custom_call_target="tpu_custom_call" | custom-call | flops 5368709120 | bytes 17301504 | tf_op jit(solution)/shard_map/pallas_call | solution.py:64
  466.1 9.2 %copy.172 = bf16[4,2,4,64,2560]{4,3,1,0,2:T(8,128)(2,1)} copy(bf16[4,2,4,64,2560]{4,3,2,1,0:T(8,128)(2,1)} %bitcast.372) | data formatting | bytes 20971520 | tf_op jit(solution)/shard_map/reshape | solution.py:157
  475.4 9.4 %fusion.146 = (bf16[4,4,2,64,1280]{4,3,2,1,0:T(8,128)(2,1)}, bf16[4,4,2,64,1280]{4,3,2,1,0:T(8,128)(2,1)}) fusion(bf16[4,4,2,64,2560]{4,3,2,1,0:T(8,128)(2,1)} %bitcast.371), kind=kLoop, calls=%fused_computation.259 | loop fusion | bytes 20971520 | tf_op jit(solution)/shard_map/slice | solution.py:140
  487.6 2.9 fusion.39
  490.5 2.9 fusion.37
  498.0 2.9 fusion.35
  500.9 3.0 add_add_fusion
  506.6 11.8 %collective-permute-done.29 = bf16[4,2,64,1280]{3,2,1,0:T(8,128)(2,1)S(1)} collective-permute-done((bf16[4,2,64,1280]{3,2,1,0:T(8,128)(2,1)S(1)}, bf16[4,2,64,1280]{3,2,1,0:T(8,128)(2,1)S(1)}, u32[]{:S(2)}, u32[]{:S(2)}) %collective-permute-start.29) | collective-permute-done | bytes 1310752 | tf_op jit(solution)/shard_map/ppermute | solution.py:148
  521.1 5.6 collective-permute-done.35
  526.7 3.1 fusion.16
  529.8 3.2 collective-permute-start.36
  534.3 18.1 %collective-permute-done.30 = bf16[4,2,64,1280]{3,2,1,0:T(8,128)(2,1)} collective-permute-done((bf16[4,2,64,1280]{3,2,1,0:T(8,128)(2,1)}, bf16[4,2,64,1280]{3,2,1,0:T(8,128)(2,1)}, u32[]{:S(2)}, u32[]{:S(2)}) %collective-permute-start.30) | collective-permute-done | bytes 1310752 | tf_op jit(solution)/shard_map/ppermute | solution.py:148
  552.4 3.1 fusion.20
  560.4 3.1 fusion.17
  563.5 3.7 collective-permute-start.37
  567.2 4.1 collective-permute-done.28
  574.8 5.7 all-to-all-start.1
  580.6 17.7 %collective-permute-done.31 = bf16[4,2,64,1280]{3,2,1,0:T(8,128)(2,1)} collective-permute-done((bf16[4,2,64,1280]{3,2,1,0:T(8,128)(2,1)}, bf16[4,2,64,1280]{3,2,1,0:T(8,128)(2,1)}, u32[]{:S(2)}, u32[]{:S(2)}) %collective-permute-start.31) | collective-permute-done | bytes 1310752 | tf_op jit(solution)/shard_map/ppermute | solution.py:148
  601.9 5.4 collective-permute-done.37
  612.0 3.7 collective-permute-done.32
  617.1 4.0 collective-permute-done.38
  624.8 4.9 collective-permute-done.39
  629.8 3.9 collective-permute-start.40
  635.1 5.5 collective-permute-done.40
  645.0 4.4 collective-permute-done.41
  (274 shorter events, 136.7 us)
Async XLA Ops:
  7.2 18.7 %copy-start = (s32[1,4,128]{2,1,0:T(4,128)S(1)}, s32[1,4,128]{2,1,0:T(4,128)}, u32[]{:S(2)}) copy-start(s32[1,4,128]{2,1,0:T(4,128)} %param.16) | copy-start | bytes 6148
  7.2 18.7 %copy-start.44 = (s32[4]{0:T(128)S(1)}, s32[4]{0:T(128)}, u32[]{:S(2)}) copy-start(s32[4]{0:T(128)} %constant.253.clone) | copy-start | bytes 52
  7.2 8.9 %copy-start.41 = (f32[16]{0:T(128)S(1)}, f32[16]{0:T(128)}, u32[]{:S(2)}) copy-start(f32[16]{0:T(128)} %param.24) | copy-start | bytes 196
  7.2 8.9 %copy-start.42 = (f32[16]{0:T(128)S(1)}, f32[16]{0:T(128)}, u32[]{:S(2)}) copy-start(f32[16]{0:T(128)} %param.18) | copy-start | bytes 196
  7.2 8.9 %copy-start.43 = (f32[16]{0:T(128)S(1)}, f32[16]{0:T(128)}, u32[]{:S(2)}) copy-start(f32[16]{0:T(128)} %param.17) | copy-start | bytes 196
  7.3 19.2 %copy-start.4 = (bf16[1,1,128,2048]{3,2,1,0:T(8,128)(2,1)S(1)}, bf16[1,1,128,2048]{3,2,1,0:T(8,128)(2,1)}, u32[]{:S(2)}) copy-start(bf16[1,1,128,2048]{3,2,1,0:T(8,128)(2,1)} %param.15) | copy-start | bytes 1572868
  7.3 302.8 %all-gather.2.cloned.1.call-start = ((), (), s32[]{:S(2)}) async-start(), calls=%async_computation.3 | async-start | bytes 17842176 | tf_op jit(solution)/shard_map/all_gather | solution.py:260
  12.7 26.5 %collective-permute-start.2 = (bf16[64,2560]{1,0:T(8,128)(2,1)S(1)}, bf16[64,2560]{1,0:T(8,128)(2,1)S(1)}, u32[]{:S(2)}, u32[]{:S(2)}) collective-permute-start(bf16[64,2560]{1,0:T(8,128)(2,1)S(1)} %bitcast_dynamic-update-slice_fusion.21), channel_id=1, source_target_pairs={{0,16},{4,20},{8,24},{12,28},{16,0},{20,4},{24,8},{28,12},{32,48},... | collective-permute-start | bytes 983048 | tf_op jit(solution)/shard_map/ppermute | solution.py:171
  16.9 21.7 %all-to-all-start = ((f32[128,3,16]{2,1,0:T(4,128)}), f32[128,3,16]{2,1,0:T(4,128)S(1)}, u32[]{:S(2)}, u32[]{:S(2)}) async-start(f32[128,3,16]{2,1,0:T(4,128)} %broadcast_in_dim.107), calls=%async_computation | async-start | bytes 524288 | tf_op jit(solution)/shard_map/all_to_all | solution.py:215
  25.8 624.5 %reduce-scatter.2.cloned.1.call-start = ((), (), s32[]{:S(2)}) async-start(), calls=%async_computation.4 | async-start | bytes 17842176 | tf_op jit(solution)/shard_map/reduce_scatter | solution.py:306
  27.4 64.8 %copy-start.38 = (f32[128]{0:T(128)}, f32[128]{0:T(128)S(1)}, u32[]{:S(2)}) copy-start(f32[128]{0:T(128)S(1)} %get-tuple-element.57) | copy-start | bytes 1540
  39.2 53.0 %copy-start.35 = (f32[2048]{0:T(1024)}, f32[2048]{0:T(1024)S(1)}, u32[]{:S(2)}) copy-start(f32[2048]{0:T(1024)S(1)} %mul.250) | copy-start | bytes 24580
  39.3 11.3 %collective-permute-start.3 = (bf16[2,32,2560]{2,1,0:T(8,128)(2,1)S(1)}, bf16[2,32,2560]{2,1,0:T(8,128)(2,1)S(1)}, u32[]{:S(2)}, u32[]{:S(2)}) collective-permute-start(bf16[2,32,2560]{2,1,0:T(8,128)(2,1)S(1)} %get-tuple-element.50), channel_id=1, source_target_pairs={{0,4},{4,8},{8,12},{12,0},{16,20},{20,24},{24,28},{28,16},{32,36},... | collective-permute-start | bytes 983048 | tf_op jit(solution)/shard_map/ppermute | solution.py:187
  40.1 10.5 %collective-permute-start.9 = (bf16[2,32,2560]{2,1,0:T(8,128)(2,1)S(1)}, bf16[2,32,2560]{2,1,0:T(8,128)(2,1)S(1)}, u32[]{:S(2)}, u32[]{:S(2)}) collective-permute-start(bf16[2,32,2560]{2,1,0:T(8,128)(2,1)S(1)} %get-tuple-element.49), channel_id=1, source_target_pairs={{0,12},{4,0},{8,4},{12,8},{16,28},{20,16},{24,20},{28,24},{32,44},... | collective-permute-start | bytes 983048 | tf_op jit(solution)/shard_map/ppermute | solution.py:187
  50.6 18.1 %collective-permute-start.4 = (bf16[2,32,2560]{2,1,0:T(8,128)(2,1)S(1)}, bf16[2,32,2560]{2,1,0:T(8,128)(2,1)S(1)}, u32[]{:S(2)}, u32[]{:S(2)}) collective-permute-start(bf16[2,32,2560]{2,1,0:T(8,128)(2,1)S(1)} %collective-permute-done.3), channel_id=1, source_target_pairs={{0,4},{4,8},{8,12},{12,0},{16,20},{20,24},{24,28},{28,16},{32,36},... | collective-permute-start | bytes 983048 | tf_op jit(solution)/shard_map/ppermute | solution.py:187
  50.6 18.1 %collective-permute-start.10 = (bf16[2,32,2560]{2,1,0:T(8,128)(2,1)S(1)}, bf16[2,32,2560]{2,1,0:T(8,128)(2,1)S(1)}, u32[]{:S(2)}, u32[]{:S(2)}) collective-permute-start(bf16[2,32,2560]{2,1,0:T(8,128)(2,1)S(1)} %collective-permute-done.9), channel_id=1, source_target_pairs={{0,12},{4,0},{8,4},{12,8},{16,28},{20,16},{24,20},{28,24},{32,44},... | collective-permute-start | bytes 983048 | tf_op jit(solution)/shard_map/ppermute | solution.py:187
  68.6 18.0 %collective-permute-start.5 = (bf16[2,32,2560]{2,1,0:T(8,128)(2,1)S(1)}, bf16[2,32,2560]{2,1,0:T(8,128)(2,1)S(1)}, u32[]{:S(2)}, u32[]{:S(2)}) collective-permute-start(bf16[2,32,2560]{2,1,0:T(8,128)(2,1)S(1)} %collective-permute-done.4), channel_id=1, source_target_pairs={{0,4},{4,8},{8,12},{12,0},{16,20},{20,24},{24,28},{28,16},{32,36},... | collective-permute-start | bytes 983048 | tf_op jit(solution)/shard_map/ppermute | solution.py:187
  68.7 19.2 %collective-permute-start.11 = (bf16[2,32,2560]{2,1,0:T(8,128)(2,1)S(1)}, bf16[2,32,2560]{2,1,0:T(8,128)(2,1)S(1)}, u32[]{:S(2)}, u32[]{:S(2)}) collective-permute-start(bf16[2,32,2560]{2,1,0:T(8,128)(2,1)S(1)} %collective-permute-done.10), channel_id=1, source_target_pairs={{0,12},{4,0},{8,4},{12,8},{16,28},{20,16},{24,20},{28,24},{32,44},... | collective-permute-start | bytes 983048 | tf_op jit(solution)/shard_map/ppermute | solution.py:187
  87.4 51.7 %collective-permute-start.6 = (bf16[2,4,32,2560]{3,2,1,0:T(8,128)(2,1)}, bf16[2,4,32,2560]{3,2,1,0:T(8,128)(2,1)}, u32[]{:S(2)}, u32[]{:S(2)}) collective-permute-start(bf16[2,4,32,2560]{3,2,1,0:T(8,128)(2,1)} %bitcast_dynamic-update-slice_fusion.15), channel_id=1, source_target_pairs={{0,32},{4,36},{8,40},{12,44},{16,48},{20,52},{24,56},{28,60},{32,6... | collective-permute-start | bytes 3932168 | tf_op jit(solution)/shard_map/ppermute | solution.py:193
  87.9 53.7 %collective-permute-start.12 = (bf16[2,4,32,2560]{3,2,1,0:T(8,128)(2,1)S(1)}, bf16[2,4,32,2560]{3,2,1,0:T(8,128)(2,1)}, u32[]{:S(2)}, u32[]{:S(2)}) collective-permute-start(bf16[2,4,32,2560]{3,2,1,0:T(8,128)(2,1)S(1)} %bitcast_dynamic-update-slice_fusion.11), channel_id=1, source_target_pairs={{0,96},{4,100},{8,104},{12,108},{16,112},{20,116},{24,120},{28,124... | collective-permute-start | bytes 3932168 | tf_op jit(solution)/shard_map/ppermute | solution.py:193
  91.7 19.0 %collective-permute-start = (bf16[128,2048]{1,0:T(8,128)(2,1)}, bf16[128,2048]{1,0:T(8,128)(2,1)S(1)}, u32[]{:S(2)}, u32[]{:S(2)}) collective-permute-start(bf16[128,2048]{1,0:T(8,128)(2,1)} %fusion.63), channel_id=1, source_target_pairs={{0,2},{2,0},{1,3},{3,1},{4,6},{6,4},{5,7},{7,5},{8,10},{10,8},{9,1... | collective-permute-start | bytes 1572872 | tf_op jit(solution)/shard_map/ppermute | solution.py:108
  110.7 37.3 %copy-start.25 = (bf16[128,2048]{1,0:T(8,128)(2,1)}, bf16[128,2048]{1,0:T(8,128)(2,1)S(1)}, u32[]{:S(2)}) copy-start(bf16[128,2048]{1,0:T(8,128)(2,1)S(1)} %collective-permute-done) | copy-start | bytes 1572868
  111.8 36.2 %collective-permute-start.1 = (bf16[2,128,2048]{2,1,0:T(8,128)(2,1)}, bf16[2,128,2048]{2,1,0:T(8,128)(2,1)}, u32[]{:S(2)}, u32[]{:S(2)}) collective-permute-start(bf16[2,128,2048]{2,1,0:T(8,128)(2,1)} %pad_maximum_fusion.5), channel_id=1, source_target_pairs={{0,1},{1,0},{2,3},{3,2},{4,5},{5,4},{6,7},{7,6},{8,9},{9,8},{10,11... | collective-permute-start | bytes 3145736 | tf_op jit(solution)/shard_map/ppermute | solution.py:110
  139.1 52.5 %collective-permute-start.7 = (bf16[2,4,32,2560]{3,2,1,0:T(8,128)(2,1)}, bf16[2,4,32,2560]{3,2,1,0:T(8,128)(2,1)}, u32[]{:S(2)}, u32[]{:S(2)}) collective-permute-start(bf16[2,4,32,2560]{3,2,1,0:T(8,128)(2,1)} %collective-permute-done.6), channel_id=1, source_target_pairs={{0,32},{4,36},{8,40},{12,44},{16,48},{20,52},{24,56},{28,60},{32,6... | collective-permute-start | bytes 3932168 | tf_op jit(solution)/shard_map/ppermute | solution.py:193
  141.5 51.8 %collective-permute-start.13 = (bf16[2,4,32,2560]{3,2,1,0:T(8,128)(2,1)}, bf16[2,4,32,2560]{3,2,1,0:T(8,128)(2,1)}, u32[]{:S(2)}, u32[]{:S(2)}) collective-permute-start(bf16[2,4,32,2560]{3,2,1,0:T(8,128)(2,1)} %collective-permute-done.12), channel_id=1, source_target_pairs={{0,96},{4,100},{8,104},{12,108},{16,112},{20,116},{24,120},{28,124... | collective-permute-start | bytes 3932168 | tf_op jit(solution)/shard_map/ppermute | solution.py:193
  191.6 28.3 %collective-permute-start.8 = (bf16[2,4,32,2560]{3,2,1,0:T(8,128)(2,1)}, bf16[2,4,32,2560]{3,2,1,0:T(8,128)(2,1)S(1)}, u32[]{:S(2)}, u32[]{:S(2)}) collective-permute-start(bf16[2,4,32,2560]{3,2,1,0:T(8,128)(2,1)} %collective-permute-done.7), channel_id=1, source_target_pairs={{0,32},{4,36},{8,40},{12,44},{16,48},{20,52},{24,56},{28,60},{32,6... | collective-permute-start | bytes 3932168 | tf_op jit(solution)/shard_map/ppermute | solution.py:193
  193.3 29.8 %collective-permute-start.14 = (bf16[2,4,32,2560]{3,2,1,0:T(8,128)(2,1)}, bf16[2,4,32,2560]{3,2,1,0:T(8,128)(2,1)S(1)}, u32[]{:S(2)}, u32[]{:S(2)}) collective-permute-start(bf16[2,4,32,2560]{3,2,1,0:T(8,128)(2,1)} %collective-permute-done.13), channel_id=1, source_target_pairs={{0,96},{4,100},{8,104},{12,108},{16,112},{20,116},{24,120},{28,124... | collective-permute-start | bytes 3932168 | tf_op jit(solution)/shard_map/ppermute | solution.py:193
  223.3 5.6 copy-start.2
  264.8 4.2 collective-permute-start.15
  269.2 15.0 %collective-permute-start.16 = (bf16[128,2048]{1,0:T(8,128)(2,1)S(1)}, bf16[128,2048]{1,0:T(8,128)(2,1)}, u32[]{:S(2)}, u32[]{:S(2)}) collective-permute-start(bf16[128,2048]{1,0:T(8,128)(2,1)S(1)} %fusion.93), channel_id=1, source_target_pairs={{0,2},{2,0},{1,3},{3,1},{4,6},{6,4},{5,7},{7,5},{8,10},{10,8},{9,1... | collective-permute-start | bytes 1572872 | tf_op jit(solution)/shard_map/ppermute | solution.py:119
  270.4 25.0 %collective-permute-start.21 = (bf16[128,2048]{1,0:T(8,128)(2,1)S(1)}, bf16[128,2048]{1,0:T(8,128)(2,1)}, u32[]{:S(2)}, u32[]{:S(2)}) collective-permute-start(bf16[128,2048]{1,0:T(8,128)(2,1)S(1)} %bitcast.379), channel_id=1, source_target_pairs={{0,2},{2,0},{1,3},{3,1},{4,6},{6,4},{5,7},{7,5},{8,10},{10,8},{9,1... | collective-permute-start | bytes 1572872 | tf_op jit(solution)/shard_map/ppermute | solution.py:108
  286.4 19.3 %collective-permute-start.17 = (bf16[128,2048]{1,0:T(8,128)(2,1)S(1)}, bf16[128,2048]{1,0:T(8,128)(2,1)S(1)}, u32[]{:S(2)}, u32[]{:S(2)}) collective-permute-start(bf16[128,2048]{1,0:T(8,128)(2,1)S(1)} %multiply_convert_fusion.4), channel_id=1, source_target_pairs={{0,2},{2,0},{1,3},{3,1},{4,6},{6,4},{5,7},{7,5},{8,10},{10,8},{9,1... | collective-permute-start | bytes 1572872 | tf_op jit(solution)/shard_map/ppermute | solution.py:108
  296.5 9.4 %collective-permute-start.22 = (bf16[2,128,2048]{2,1,0:T(8,128)(2,1)S(1)}, bf16[2,128,2048]{2,1,0:T(8,128)(2,1)S(1)}, u32[]{:S(2)}, u32[]{:S(2)}) collective-permute-start(bf16[2,128,2048]{2,1,0:T(8,128)(2,1)S(1)} %pad_maximum_fusion.7), channel_id=1, source_target_pairs={{0,1},{1,0},{2,3},{3,2},{4,5},{5,4},{6,7},{7,6},{8,9},{9,8},{10,11... | collective-permute-start | bytes 3145736 | tf_op jit(solution)/shard_map/ppermute | solution.py:110
  305.8 2.7 collective-permute-start.18
  310.1 8.4 %copy-start.22 = (bf16[4,128,2048]{2,1,0:T(8,128)(2,1)S(1)}, bf16[4,128,2048]{2,1,0:T(8,128)(2,1)}, u32[]{:S(2)}) copy-start(bf16[4,128,2048]{2,1,0:T(8,128)(2,1)} %pad_maximum_fusion.2) | copy-start | bytes 6291460
  310.1 9.9 %copy-start.45 = (bf16[2048,4224]{1,0:T(8,128)(2,1)S(1)}, bf16[2048,4224]{1,0:T(8,128)(2,1)}, u32[]{:S(2)}) copy-start(bf16[2048,4224]{1,0:T(8,128)(2,1)} %all-gather.2.cloned.1.call-done) | copy-start | bytes 51904516
  360.1 6.0 copy-start.30
  371.9 7.5 %collective-permute-start.23 = (f32[2,128,2048]{2,1,0:T(8,128)S(1)}, f32[2,128,2048]{2,1,0:T(8,128)S(1)}, u32[]{:S(2)}, u32[]{:S(2)}) collective-permute-start(f32[2,128,2048]{2,1,0:T(8,128)S(1)} %bitcast.397), channel_id=1, source_target_pairs={{0,1},{1,0},{2,3},{3,2},{4,5},{5,4},{6,7},{7,6},{8,9},{9,8},{10,11... | collective-permute-start | bytes 6291464 | tf_op jit(solution)/shard_map/ppermute | solution.py:116
  378.8 4.4 collective-permute-start.19
  379.5 16.4 %collective-permute-start.24 = (bf16[128,2048]{1,0:T(8,128)(2,1)S(1)}, bf16[128,2048]{1,0:T(8,128)(2,1)S(1)}, u32[]{:S(2)}, u32[]{:S(2)}) collective-permute-start(bf16[128,2048]{1,0:T(8,128)(2,1)S(1)} %fusion.83), channel_id=1, source_target_pairs={{0,2},{2,0},{1,3},{3,1},{4,6},{6,4},{5,7},{7,5},{8,10},{10,8},{9,1... | collective-permute-start | bytes 1572872 | tf_op jit(solution)/shard_map/ppermute | solution.py:119
  383.3 27.5 %collective-permute-start.20 = (bf16[128,2048]{1,0:T(8,128)(2,1)S(1)}, bf16[128,2048]{1,0:T(8,128)(2,1)S(1)}, u32[]{:S(2)}, u32[]{:S(2)}) collective-permute-start(bf16[128,2048]{1,0:T(8,128)(2,1)S(1)} %fusion.87), channel_id=1, source_target_pairs={{0,2},{2,0},{1,3},{3,1},{4,6},{6,4},{5,7},{7,5},{8,10},{10,8},{9,1... | collective-permute-start | bytes 1572872 | tf_op jit(solution)/shard_map/ppermute | solution.py:119
  412.6 16.2 %collective-permute-start.25 = (bf16[128,2048]{1,0:T(8,128)(2,1)S(1)}, bf16[128,2048]{1,0:T(8,128)(2,1)S(1)}, u32[]{:S(2)}, u32[]{:S(2)}) collective-permute-start(bf16[128,2048]{1,0:T(8,128)(2,1)S(1)} %get-tuple-element.25), channel_id=1, source_target_pairs={{0,2},{2,0},{1,3},{3,1},{4,6},{6,4},{5,7},{7,5},{8,10},{10,8},{9,1... | collective-permute-start | bytes 1572872 | tf_op jit(solution)/shard_map/ppermute | solution.py:108
  428.9 2.7 collective-permute-start.26
  486.2 32.1 %collective-permute-start.29 = (bf16[4,2,64,1280]{3,2,1,0:T(8,128)(2,1)S(1)}, bf16[4,2,64,1280]{3,2,1,0:T(8,128)(2,1)S(1)}, u32[]{:S(2)}, u32[]{:S(2)}) collective-permute-start(bf16[4,2,64,1280]{3,2,1,0:T(8,128)(2,1)S(1)} %dynamic-slice_bitcast_fusion.1), channel_id=1, source_target_pairs={{0,4},{4,8},{8,12},{12,0},{16,20},{20,24},{24,28},{28,16},{32,36},... | collective-permute-start | bytes 3932168 | tf_op jit(solution)/shard_map/ppermute | solution.py:148
  495.9 30.7 %collective-permute-start.35 = (bf16[4,2,64,1280]{3,2,1,0:T(8,128)(2,1)}, bf16[4,2,64,1280]{3,2,1,0:T(8,128)(2,1)}, u32[]{:S(2)}, u32[]{:S(2)}) collective-permute-start(bf16[4,2,64,1280]{3,2,1,0:T(8,128)(2,1)} %dynamic-slice_bitcast_fusion), channel_id=1, source_target_pairs={{0,12},{4,0},{8,4},{12,8},{16,28},{20,16},{24,20},{28,24},{32,44},... | collective-permute-start | bytes 3932168 | tf_op jit(solution)/shard_map/ppermute | solution.py:148
  506.6 49.0 %collective-permute-start.27 = (f32[2,128,2048]{2,1,0:T(8,128)}, f32[2,128,2048]{2,1,0:T(8,128)S(1)}, u32[]{:S(2)}, u32[]{:S(2)}) collective-permute-start(f32[2,128,2048]{2,1,0:T(8,128)} %bitcast.81), channel_id=1, source_target_pairs={{0,1},{1,0},{2,3},{3,2},{4,5},{5,4},{6,7},{7,6},{8,9},{9,8},{10,11... | collective-permute-start | bytes 6291464 | tf_op jit(solution)/shard_map/ppermute | solution.py:116
  521.0 31.4 %collective-permute-start.30 = (bf16[4,2,64,1280]{3,2,1,0:T(8,128)(2,1)}, bf16[4,2,64,1280]{3,2,1,0:T(8,128)(2,1)}, u32[]{:S(2)}, u32[]{:S(2)}) collective-permute-start(bf16[4,2,64,1280]{3,2,1,0:T(8,128)(2,1)} %fusion.19), channel_id=1, source_target_pairs={{0,4},{4,8},{8,12},{12,0},{16,20},{20,24},{24,28},{28,16},{32,36},... | collective-permute-start | bytes 3932168 | tf_op jit(solution)/shard_map/ppermute | solution.py:148
  529.8 30.6 %collective-permute-start.36 = (bf16[4,2,64,1280]{3,2,1,0:T(8,128)(2,1)}, bf16[4,2,64,1280]{3,2,1,0:T(8,128)(2,1)}, u32[]{:S(2)}, u32[]{:S(2)}) collective-permute-start(bf16[4,2,64,1280]{3,2,1,0:T(8,128)(2,1)} %fusion.16), channel_id=1, source_target_pairs={{0,12},{4,0},{8,4},{12,8},{16,28},{20,16},{24,20},{28,24},{32,44},... | collective-permute-start | bytes 3932168 | tf_op jit(solution)/shard_map/ppermute | solution.py:148
  555.5 42.7 %collective-permute-start.31 = (bf16[4,2,64,1280]{3,2,1,0:T(8,128)(2,1)}, bf16[4,2,64,1280]{3,2,1,0:T(8,128)(2,1)}, u32[]{:S(2)}, u32[]{:S(2)}) collective-permute-start(bf16[4,2,64,1280]{3,2,1,0:T(8,128)(2,1)} %fusion.20), channel_id=1, source_target_pairs={{0,4},{4,8},{8,12},{12,0},{16,20},{20,24},{24,28},{28,16},{32,36},... | collective-permute-start | bytes 3932168 | tf_op jit(solution)/shard_map/ppermute | solution.py:148
  556.9 14.4 %copy-start.36 = (f32[2048]{0:T(1024)S(1)}, f32[2048]{0:T(1024)}, u32[]{:S(2)}) copy-start(f32[2048]{0:T(1024)} %copy-done.35) | copy-start | bytes 24580
  556.9 14.4 %copy-start.39 = (f32[128]{0:T(128)S(1)}, f32[128]{0:T(128)}, u32[]{:S(2)}) copy-start(f32[128]{0:T(128)} %copy-done.38) | copy-start | bytes 1540
  556.9 14.4 %collective-permute-start.28 = (bf16[128,2048]{1,0:T(8,128)(2,1)S(1)}, bf16[128,2048]{1,0:T(8,128)(2,1)S(1)}, u32[]{:S(2)}, u32[]{:S(2)}) collective-permute-start(bf16[128,2048]{1,0:T(8,128)(2,1)S(1)} %fusion.79), channel_id=1, source_target_pairs={{0,2},{2,0},{1,3},{3,1},{4,6},{6,4},{5,7},{7,5},{8,10},{10,8},{9,1... | collective-permute-start | bytes 1572872 | tf_op jit(solution)/shard_map/ppermute | solution.py:119
  563.5 43.8 %collective-permute-start.37 = (bf16[4,2,64,1280]{3,2,1,0:T(8,128)(2,1)}, bf16[4,2,64,1280]{3,2,1,0:T(8,128)(2,1)}, u32[]{:S(2)}, u32[]{:S(2)}) collective-permute-start(bf16[4,2,64,1280]{3,2,1,0:T(8,128)(2,1)} %fusion.17), channel_id=1, source_target_pairs={{0,12},{4,0},{8,4},{12,8},{16,28},{20,16},{24,20},{28,24},{32,44},... | collective-permute-start | bytes 3932168 | tf_op jit(solution)/shard_map/ppermute | solution.py:148
  574.8 69.5 %all-to-all-start.1 = ((f32[128,3,16]{2,1,0:T(4,128)}), f32[128,3,16]{2,1,0:T(4,128)S(1)}, u32[]{:S(2)}, u32[]{:S(2)}) async-start(f32[128,3,16]{2,1,0:T(4,128)} %copy.135), calls=%async_computation.1 | async-start | bytes 524288 | tf_op jit(solution)/shard_map/all_to_all | solution.py:222
  600.4 15.3 %collective-permute-start.32 = (bf16[2,64,1280]{2,1,0:T(8,128)(2,1)S(1)}, bf16[2,64,1280]{2,1,0:T(8,128)(2,1)S(1)}, u32[]{:S(2)}, u32[]{:S(2)}) collective-permute-start(bf16[2,64,1280]{2,1,0:T(8,128)(2,1)S(1)} %dynamic-slice_bitcast_fusion.3), channel_id=1, source_target_pairs={{0,32},{4,36},{8,40},{12,44},{16,48},{20,52},{24,56},{28,60},{32,6... | collective-permute-start | bytes 983048 | tf_op jit(solution)/shard_map/ppermute | solution.py:148
  609.4 11.8 %collective-permute-start.38 = (bf16[2,64,1280]{2,1,0:T(8,128)(2,1)S(1)}, bf16[2,64,1280]{2,1,0:T(8,128)(2,1)S(1)}, u32[]{:S(2)}, u32[]{:S(2)}) collective-permute-start(bf16[2,64,1280]{2,1,0:T(8,128)(2,1)S(1)} %dynamic-slice_bitcast_fusion.2), channel_id=1, source_target_pairs={{0,96},{4,100},{8,104},{12,108},{16,112},{20,116},{24,120},{28,124... | collective-permute-start | bytes 983048 | tf_op jit(solution)/shard_map/ppermute | solution.py:148
  615.8 8.8 %collective-permute-start.33 = (bf16[2,64,1280]{2,1,0:T(8,128)(2,1)S(1)}, bf16[2,64,1280]{2,1,0:T(8,128)(2,1)S(1)}, u32[]{:S(2)}, u32[]{:S(2)}) collective-permute-start(bf16[2,64,1280]{2,1,0:T(8,128)(2,1)S(1)} %fusion.116), channel_id=1, source_target_pairs={{0,32},{4,36},{8,40},{12,44},{16,48},{20,52},{24,56},{28,60},{32,6... | collective-permute-start | bytes 983048 | tf_op jit(solution)/shard_map/ppermute | solution.py:148
  621.3 8.4 %collective-permute-start.39 = (bf16[2,64,1280]{2,1,0:T(8,128)(2,1)S(1)}, bf16[2,64,1280]{2,1,0:T(8,128)(2,1)S(1)}, u32[]{:S(2)}, u32[]{:S(2)}) collective-permute-start(bf16[2,64,1280]{2,1,0:T(8,128)(2,1)S(1)} %fusion.114), channel_id=1, source_target_pairs={{0,96},{4,100},{8,104},{12,108},{16,112},{20,116},{24,120},{28,124... | collective-permute-start | bytes 983048 | tf_op jit(solution)/shard_map/ppermute | solution.py:148
  624.7 10.3 %collective-permute-start.34 = (bf16[2,64,1280]{2,1,0:T(8,128)(2,1)S(1)}, bf16[2,64,1280]{2,1,0:T(8,128)(2,1)S(1)}, u32[]{:S(2)}, u32[]{:S(2)}) collective-permute-start(bf16[2,64,1280]{2,1,0:T(8,128)(2,1)S(1)} %fusion.117), channel_id=1, source_target_pairs={{0,32},{4,36},{8,40},{12,44},{16,48},{20,52},{24,56},{28,60},{32,6... | collective-permute-start | bytes 983048 | tf_op jit(solution)/shard_map/ppermute | solution.py:148
  629.7 13.3 %copy-start.10 = (f32[128,2048]{1,0:T(8,128)S(1)}, f32[128,2048]{1,0:T(8,128)}, u32[]{:S(2)}) copy-start(f32[128,2048]{1,0:T(8,128)} %get-tuple-element.26) | copy-start | bytes 3145732
  629.8 13.3 %copy-start.12 = (f32[128,2048]{1,0:T(8,128)S(1)}, f32[128,2048]{1,0:T(8,128)}, u32[]{:S(2)}) copy-start(f32[128,2048]{1,0:T(8,128)} %get-tuple-element.24) | copy-start | bytes 3145732
  629.8 13.3 %copy-start.40 = (f32[128]{0:T(128)S(1)}, f32[128]{0:T(128)}, u32[]{:S(2)}) copy-start(f32[128]{0:T(128)} %get-tuple-element.56) | copy-start | bytes 1540
  629.8 10.8 %collective-permute-start.40 = (bf16[2,64,1280]{2,1,0:T(8,128)(2,1)S(1)}, bf16[2,64,1280]{2,1,0:T(8,128)(2,1)S(1)}, u32[]{:S(2)}, u32[]{:S(2)}) collective-permute-start(bf16[2,64,1280]{2,1,0:T(8,128)(2,1)S(1)} %fusion.115), channel_id=1, source_target_pairs={{0,96},{4,100},{8,104},{12,108},{16,112},{20,116},{24,120},{28,124... | collective-permute-start | bytes 983048 | tf_op jit(solution)/shard_map/ppermute | solution.py:148
  640.7 8.7 %collective-permute-start.41 = (bf16[64,2560]{1,0:T(8,128)(2,1)S(1)}, bf16[64,2560]{1,0:T(8,128)(2,1)S(1)}, u32[]{:S(2)}, u32[]{:S(2)}) collective-permute-start(bf16[64,2560]{1,0:T(8,128)(2,1)S(1)} %fusion.130), channel_id=1, source_target_pairs={{0,16},{4,20},{8,24},{12,28},{16,0},{20,4},{24,8},{28,12},{32,48},... | collective-permute-start | bytes 983048 | tf_op jit(solution)/shard_map/ppermute | solution.py:163
  (28 other events, 78.5 us)
Sparse Core Ops, SparseCore 0:
  11.2 184.5 all-gather.1
  360.2 286.5 reduce-scatter.1
